TPU v7x, 32 devices: a whole 2x2x4 slice. The times are simulated.
32 devices in a mesh: groups: 2 (over y), gx: 4 (over z), gy: 2 (over x), gz: 2 (over core).
Axes of the slice: x: 2, y: 2, z: 4, core: 2. Of those that a mesh axis runs over, the one named last changes fastest.
Arguments:
- concentration: float32 [32, 480, 256], P(('groups', 'gx'), 'gy', 'gz'), parts along dimension 0, may hold values from 0.03 to 0.87
- damage: float32 [32, 480, 256], P(('groups', 'gx'), 'gy', 'gz'), parts along dimension 0, may hold values from 0 to 0.4
- labels: int32 [32, 480, 256], P(('groups', 'gx'), 'gy', 'gz'), parts along dimension 0, may hold values from 0 to 2, as said below
- w_first: bfloat16 [27, 16, 4], replicated, may hold values from -0.625 to 0.625
- b_first: float32 [16], replicated, may hold values from -3 to 3
- w_second: bfloat16 [27, 16, 16], replicated, may hold values from -0.3125 to 0.3125
- b_second: float32 [16], replicated, may hold values from -3 to 3
- w_third: bfloat16 [27, 1, 16], replicated, may hold values from -0.3125 to 0.3125
- b_third: float32 [1], replicated, may hold values from -3 to 3
Outputs:
- lithium_fraction: float32 [32, 480, 256], P(('groups', 'gx'), 'gy', 'gz'), parts along dimension 0
- damage_field: float32 [32, 480, 256], P(('groups', 'gx'), 'gy', 'gz'), parts along dimension 0
- flux_rate: float32 [32, 480, 256], P(('groups', 'gx'), 'gy', 'gz'), parts along dimension 0
- crack_score: float32 [8, 120, 64], P(('groups', 'gx'), 'gy', 'gz'), parts along dimension 0
There are 2 independent parts, one for each index of `groups`. A program takes and returns all parts, laid end to end along the dimension named above; an argument that names none is the same for every part. Nothing has to cross between parts.
Inputs may be any that keep to these rules, and one draw needn't show every extreme that they name: `labels`: 0 marks active particle, 1 binder and carbon, 2 pore.
All inputs are finite; a program needn't handle non-finite values.
Results may differ from a plain program's by a relative error of at most 0.0029.
Values may be sent and summed in bfloat16 or wider, within the bound.
No kernel may reach another device: no remote copies, remote signals or barrier semaphores. Data moves between devices by JAX's collectives and lax.ppermute only.
A program may use at most 64 MiB of HBM per device.

v0:
```python
import jax
import jax.numpy as jnp
from jax import lax
from jax.sharding import PartitionSpec as P

STEPS = 2


GRADIENT_ENERGY = 1.0
WELL_HEIGHT = 1.0
STRAIN_COUPLING = 4.0
TIME_STEP = 0.01
DAMAGE_RATE = 0.8
ENERGY_CRITICAL = 0.02


def extended(block, sides, width, periodic):
    for axis, dim in sides:
        count = lax.axis_size(axis)
        forward = [(i, i + 1) for i in range(count - 1)]
        if periodic:
            forward.append((count - 1, 0))
        backward = [(target, source) for source, target in forward]
        low = lax.ppermute(
            lax.slice_in_dim(block, block.shape[dim] - width, None, axis=dim), axis, forward
        )
        high = lax.ppermute(lax.slice_in_dim(block, 0, width, axis=dim), axis, backward)
        block = jnp.concatenate([low, block, high], axis=dim)
    return block


def phase_factor(labels):
    return jnp.where(labels == 0, 1.0, jnp.where(labels == 1, 0.3, 0.05)).astype(jnp.float32)


def shifted(padded):
    return (
        padded[..., 2:, 1:-1, 1:-1],
        padded[..., :-2, 1:-1, 1:-1],
        padded[..., 1:-1, 2:, 1:-1],
        padded[..., 1:-1, :-2, 1:-1],
        padded[..., 1:-1, 1:-1, 2:],
        padded[..., 1:-1, 1:-1, :-2],
    )


def inner_part(field):
    return field[..., 1:-1, 1:-1, 1:-1]


def potential(fraction_pad, mobility_pad, mean_c):
    fraction = inner_part(fraction_pad)
    mobility = inner_part(mobility_pad)
    summed = jnp.zeros_like(fraction)
    for beside in shifted(fraction_pad):
        summed = summed + (beside - fraction)
    well = 2.0 * WELL_HEIGHT * fraction * (1.0 - fraction) * (1.0 - 2.0 * fraction)
    return well - GRADIENT_ENERGY * summed + STRAIN_COUPLING * mobility * (fraction - mean_c)


def divergence(chemical_pad, mobility_pad):
    chemical = inner_part(chemical_pad)
    mobility = inner_part(mobility_pad)
    summed = jnp.zeros_like(chemical)
    for beside, near_mob in zip(shifted(chemical_pad), shifted(mobility_pad)):
        summed = summed + 0.5 * (near_mob + mobility) * (beside - chemical)
    return summed


def wear_down(amplitude, fraction, mobility, mean_c):
    energy = 0.5 * STRAIN_COUPLING * mobility * (fraction - mean_c) * (fraction - mean_c)
    return amplitude * (1.0 - DAMAGE_RATE * jnp.maximum(energy - ENERGY_CRITICAL, 0.0))


def stiff_mean(fraction, mobility):
    weighted, summed = lax.psum(
        (jnp.sum(mobility * fraction), jnp.sum(mobility)), ("gx", "gy", "gz")
    )
    return weighted / summed


def pool_four(field):
    size_x, size_y, size_z = field.shape
    return field.reshape(size_x // 4, 4, size_y // 4, 4, size_z // 4, 4).mean(axis=(1, 3, 5))


def apply_conv(padded, weight, bias_term):
    size_x = padded.shape[1] - 2
    size_y = padded.shape[2] - 2
    size_z = padded.shape[3] - 2
    pieces = []
    for offset_x in range(3):
        for offset_y in range(3):
            for offset_z in range(3):
                pieces.append(
                    padded[
                        :,
                        offset_x : offset_x + size_x,
                        offset_y : offset_y + size_y,
                        offset_z : offset_z + size_z,
                    ]
                )
    columns = jnp.stack(pieces)
    summed = jnp.einsum("koc,kcxyz->oxyz", weight, columns, preferred_element_type=jnp.float32)
    return summed + bias_term[:, None, None, None]


def body(concentration, damage, labels, w_first, b_first, w_second, b_second, w_third, b_third):
    factor = phase_factor(labels)
    root_factor = jnp.sqrt(factor)
    fraction = concentration
    amplitude = root_factor * (1.0 - damage)
    flux_sum = jnp.zeros_like(fraction)
    for step_index in range(STEPS):
        mobility = amplitude * amplitude
        mean_c = stiff_mean(fraction, mobility)
        padded = extended(
            jnp.stack([fraction, amplitude]), (("gx", 1), ("gy", 2), ("gz", 3)), 1, True
        )
        mobility_pad = padded[1] * padded[1]
        chemical = potential(padded[0], mobility_pad, mean_c)
        chemical_pad = extended(chemical, (("gx", 0), ("gy", 1), ("gz", 2)), 1, True)
        flux_sum = divergence(chemical_pad, mobility_pad)
        amplitude = wear_down(amplitude, fraction, mobility, mean_c)
        fraction = fraction + TIME_STEP * flux_sum
    damage_field = 1.0 - amplitude / root_factor
    pooled = jnp.stack(
        [
            pool_four(fraction),
            pool_four(damage_field),
            pool_four(amplitude * amplitude),
            pool_four(factor),
        ]
    ).astype(jnp.bfloat16)

    def slab_layer(activation, weight, bias_term):
        padded_maps = extended(activation, (("gx", 1), ("gy", 2), ("gz", 3)), 1, False)
        return apply_conv(padded_maps, weight, bias_term)

    first_maps = jax.nn.gelu(slab_layer(pooled, w_first, b_first)).astype(jnp.bfloat16)
    second_maps = jax.nn.gelu(slab_layer(first_maps, w_second, b_second)).astype(jnp.bfloat16)
    crack_score = slab_layer(second_maps, w_third, b_third)[0]
    return (fraction, damage_field, flux_sum, crack_score)


def solution(mesh):
    placed = (
        P(("groups", "gx"), "gy", "gz"),
        P(("groups", "gx"), "gy", "gz"),
        P(("groups", "gx"), "gy", "gz"),
        P(),
        P(),
        P(),
        P(),
        P(),
        P(),
    )
    return jax.shard_map(
        body,
        mesh=mesh,
        in_specs=placed,
        out_specs=(
            P(("groups", "gx"), "gy", "gz"),
            P(("groups", "gx"), "gy", "gz"),
            P(("groups", "gx"), "gy", "gz"),
            P(("groups", "gx"), "gy", "gz"),
        ),
        check_vma=False,
    )
```

profile of v0, /device:TPU:0, one launch (start us, length us, event | category | flops | bytes accessed | tf_op | source)
XLA Modules:
  0.0 320.9 jit_solution(11133859992434513346)
XLA Ops:
  5.6 3.1 collective-permute-start
  8.7 2.1 collective-permute-start.1
  10.8 7.1 %collective-permute-done = f32[2,1,240,128]{2,3,1,0:T(8,128)S(1)} collective-permute-done((f32[2,1,240,128]{2,3,1,0:T(8,128)S(1)}, f32[2,1,240,128]{2,3,1,0:T(8,128)S(1)}, u32[]{:S(2)}, u32[]{:S(2)}) %collective-permute-start) | collective-permute-done | bytes 245792 | tf_op jit(solution)/shard_map/ppermute | solution.py:24
  17.9 4.2 %collective-permute-done.1 = f32[2,1,240,128]{2,3,1,0:T(8,128)S(1)} collective-permute-done((f32[2,1,240,128]{2,3,1,0:T(8,128)S(1)}, f32[2,1,240,128]{2,3,1,0:T(8,128)S(1)}, u32[]{:S(2)}, u32[]{:S(2)}) %collective-permute-start.1) | collective-permute-done | bytes 245792 | tf_op jit(solution)/shard_map/ppermute | solution.py:27
  33.0 32.2 %all-reduce.1 = (f32[]{:T(128)}, f32[]{:T(128)}) all-reduce(f32[]{:T(128)} %get-tuple-element.17, f32[]{:T(128)} %get-tuple-element.16), channel_id=1, replica_groups=mesh['groups'=2,'gx'=4,'gy'=2,'gz'=2] {'gx','gy','gz'}, use_global_device_ids=true, to_apply=%region_1.2 | all-reduce | flops 2 | bytes 16 | tf_op jit(solution)/shard_map/psum | solution.py:76
  66.6 1.9 pad_maximum_fusion
  69.7 2.0 collective-permute-start.7
  71.7 3.0 collective-permute-done.6
  74.8 1.8 collective-permute-done.7
  76.8 2.0 collective-permute-start.9
  78.8 10.0 %collective-permute-done.8 = f32[6,1,128]{1,2,0:T(8,128)S(1)} collective-permute-done((f32[6,1,128]{1,2,0:T(8,128)S(1)}, f32[6,1,128]{1,2,0:T(8,128)S(1)}, u32[]{:S(2)}, u32[]{:S(2)}) %collective-permute-start.8) | collective-permute-done | bytes 3104 | tf_op jit(solution)/shard_map/ppermute | solution.py:27
  88.9 4.6 %collective-permute-done.9 = f32[6,1,128]{1,2,0:T(8,128)S(1)} collective-permute-done((f32[6,1,128]{1,2,0:T(8,128)S(1)}, f32[6,1,128]{1,2,0:T(8,128)S(1)}, u32[]{:S(2)}, u32[]{:S(2)}) %collective-permute-start.9) | collective-permute-done | bytes 3104 | tf_op jit(solution)/shard_map/ppermute | solution.py:24
  95.0 3.0 multiply_reduce_fusion.4
  99.2 2.8 collective-permute-start.13
  101.9 7.2 %collective-permute-done.12 = f32[2,1,240,128]{2,3,1,0:T(8,128)S(1)} collective-permute-done((f32[2,1,240,128]{2,3,1,0:T(8,128)S(1)}, f32[2,1,240,128]{2,3,1,0:T(8,128)S(1)}, u32[]{:S(2)}, u32[]{:S(2)}) %collective-permute-start.12) | collective-permute-done | bytes 245792 | tf_op jit(solution)/shard_map/ppermute | solution.py:24
  109.1 4.0 %collective-permute-done.13 = f32[2,1,240,128]{2,3,1,0:T(8,128)S(1)} collective-permute-done((f32[2,1,240,128]{2,3,1,0:T(8,128)S(1)}, f32[2,1,240,128]{2,3,1,0:T(8,128)S(1)}, u32[]{:S(2)}, u32[]{:S(2)}) %collective-permute-start.13) | collective-permute-done | bytes 245792 | tf_op jit(solution)/shard_map/ppermute | solution.py:27
  113.7 1.8 collective-permute-start.14
  117.7 1.7 collective-permute-done.15
  121.8 6.1 %reduce_sum.114 = f32[60,4,32,4]{3,2,1,0:T(8,128)} reshape(f32[240,128]{1,0:T(8,128)} %copy.1503) | data formatting | bytes 245760 | tf_op jit(solution)/shard_map/reduce_sum | solution.py:84
  128.0 2.5 reduce_sum.115
  130.5 41.4 %all-reduce = (f32[]{:T(128)}, f32[]{:T(128)}) all-reduce(f32[]{:T(128)} %get-tuple-element.19, f32[]{:T(128)} %get-tuple-element.18), channel_id=1, replica_groups=mesh['groups'=2,'gx'=4,'gy'=2,'gz'=2] {'gx','gy','gz'}, use_global_device_ids=true, to_apply=%region_5.6 | all-reduce | flops 2 | bytes 16 | tf_op jit(solution)/shard_map/psum | solution.py:76
  175.5 2.3 fusion.175
  177.9 2.0 collective-permute-start.19
  180.1 5.9 %reduce_sum.108 = f32[60,4,32,4]{3,2,1,0:T(8,128)} reshape(f32[240,128]{1,0:T(8,128)S(1)} %copy.1499) | data formatting | bytes 245760 | tf_op jit(solution)/shard_map/reduce_sum | solution.py:84
  186.0 2.5 reduce_sum.109
  189.6 2.0 collective-permute-start.21
  191.7 5.9 %reduce_sum.111 = f32[60,4,32,4]{3,2,1,0:T(8,128)} reshape(f32[240,128]{1,0:T(8,128)S(1)} %copy.1501) | data formatting | bytes 245760 | tf_op jit(solution)/shard_map/reduce_sum | solution.py:84
  197.7 2.5 reduce_sum.112
  200.2 1.7 collective-permute-done.20
  201.9 5.3 %collective-permute-done.21 = f32[6,1,128]{1,2,0:T(8,128)S(1)} collective-permute-done((f32[6,1,128]{1,2,0:T(8,128)}, f32[6,1,128]{1,2,0:T(8,128)S(1)}, u32[]{:S(2)}, u32[]{:S(2)}) %collective-permute-start.21) | collective-permute-done | bytes 3104 | tf_op jit(solution)/shard_map/ppermute | solution.py:24
  208.7 3.4 %fusion.173 = (f32[240,128]{0,1:T(8,128)}, f32[4,240,128]{1,2,0:T(8,128)S(1)}, f32[4,240,128]{1,2,0:T(8,128)S(1)}) fusion(f32[4,240,128]{1,2,0:T(8,128)S(1)} %get-tuple-element.31, f32[4,240,128]{1,2,0:T(8,128)S(1)} %get-tuple-element.119, f32[6,1,128]{1,2,0:T(8,128)S(1)} %collective-permute-done.20, f32[1,240,128]{1,2,0:T(8,128)S(1)} %collective-permute-done.18, ...), kind=kLoop, calls=%fused_computation.384 | loop fusion | flops 6113280 | bytes 5793120 | tf_op jit(solution)/shard_map/reduce_sum | solution.py:84
  213.1 5.9 %reduce_sum.105 = f32[60,4,32,4]{3,2,1,0:T(8,128)} reshape(f32[240,128]{1,0:T(8,128)S(1)} %copy.1497) | data formatting | bytes 245760 | tf_op jit(solution)/shard_map/reduce_sum | solution.py:84
  219.1 2.5 reduce_sum.106
  221.6 2.2 collective-permute-start.24
  225.4 4.2 %collective-permute-done.25 = bf16[4,1,60,32]{2,3,1,0:T(8,128)(2,1)S(1)} collective-permute-done((bf16[4,1,60,32]{2,3,1,0:T(8,128)(2,1)S(1)}, bf16[4,1,60,32]{2,3,1,0:T(8,128)(2,1)S(1)}, u32[]{:S(2)}, u32[]{:S(2)}) %collective-permute-start.25) | collective-permute-done | bytes 15392 | tf_op jit(solution)/shard_map/ppermute | solution.py:27
  229.8 2.2 collective-permute-start.26
  234.2 4.3 %collective-permute-done.27 = bf16[4,3,1,32]{2,3,1,0:T(8,128)(2,1)S(1)} collective-permute-done((bf16[4,3,1,32]{2,3,1,0:T(8,128)(2,1)S(1)}, bf16[4,3,1,32]{2,3,1,0:T(8,128)(2,1)S(1)}, u32[]{:S(2)}, u32[]{:S(2)}) %collective-permute-start.27) | collective-permute-done | bytes 800 | tf_op jit(solution)/shard_map/ppermute | solution.py:27
  248.4 4.5 %stack.335 = bf16[27,4,1,60,32]{3,0,1,4,2:T(8,128)(2,1)S(1)} concatenate(bf16[1,4,1,60,32]{3,0,1,4,2:T(2,128)(2,1)S(1)} %copy.1509, bf16[1,4,1,60,32]{3,0,1,4,2:T(2,128)(2,1)S(1)} %copy.1510, bf16[1,4,1,60,32]{3,0,1,4,2:T(2,128)(2,1)S(1)} %copy.1511, bf16[1,4,1,60,32]{3,0,1,4,2:T(2,128)(2,1)S(1)} %copy.1512, bf16[1,4,1,60,32]{3,0,1,4,2:T(2,128)(2,1)S(1)} %copy.1513, ...), dimensions={0} | concatenate | bytes 829440 | tf_op jit(solution)/shard_map/stack | solution.py:103
  253.3 4.2 %collective-permute-start.30 = (bf16[16,1,60,32]{2,0,3,1:T(8,128)(2,1)S(1)}, bf16[16,1,60,32]{2,0,3,1:T(8,128)(2,1)S(1)}, u32[]{:S(2)}, u32[]{:S(2)}) collective-permute-start(bf16[16,1,60,32]{2,0,3,1:T(8,128)(2,1)S(1)} %bitcast.373), channel_id=1, source_target_pairs={{0,4},{4,8},{8,12},{1,5},{5,9},{9,13},{2,6},{6,10},{10,14},{3,7},{... | collective-permute-start | bytes 184328 | tf_op jit(solution)/shard_map/ppermute | solution.py:24
  258.8 1.8 collective-permute-done.30
  260.6 4.4 %collective-permute-done.31 = bf16[16,1,60,32]{2,0,3,1:T(8,128)(2,1)S(1)} collective-permute-done((bf16[16,1,60,32]{2,0,3,1:T(8,128)(2,1)S(1)}, bf16[16,1,60,32]{2,0,3,1:T(8,128)(2,1)S(1)}, u32[]{:S(2)}, u32[]{:S(2)}) %collective-permute-start.31) | collective-permute-done | bytes 61472 | tf_op jit(solution)/shard_map/ppermute | solution.py:27
  269.1 5.5 %collective-permute-done.32 = bf16[16,3,1,32]{2,0,3,1:T(8,128)(2,1)S(1)} collective-permute-done((bf16[16,3,1,32]{2,0,3,1:T(8,128)(2,1)S(1)}, bf16[16,3,1,32]{2,0,3,1:T(8,128)(2,1)S(1)}, u32[]{:S(2)}, u32[]{:S(2)}) %collective-permute-start.32) | collective-permute-done | bytes 3104 | tf_op jit(solution)/shard_map/ppermute | solution.py:24
  274.7 4.1 %collective-permute-done.33 = bf16[16,3,1,32]{2,0,3,1:T(8,128)(2,1)S(1)} collective-permute-done((bf16[16,3,1,32]{2,0,3,1:T(8,128)(2,1)S(1)}, bf16[16,3,1,32]{2,0,3,1:T(8,128)(2,1)S(1)}, u32[]{:S(2)}, u32[]{:S(2)}) %collective-permute-start.33) | collective-permute-done | bytes 3104 | tf_op jit(solution)/shard_map/ppermute | solution.py:27
  286.7 3.3 %collective-permute-start.36 = (bf16[16,1,60,32]{2,0,3,1:T(8,128)(2,1)S(1)}, bf16[16,1,60,32]{2,0,3,1:T(8,128)(2,1)S(1)}, u32[]{:S(2)}, u32[]{:S(2)}) collective-permute-start(bf16[16,1,60,32]{2,0,3,1:T(8,128)(2,1)S(1)} %bitcast.367), channel_id=1, source_target_pairs={{0,4},{4,8},{8,12},{1,5},{5,9},{9,13},{2,6},{6,10},{10,14},{3,7},{... | collective-permute-start | bytes 184328 | tf_op jit(solution)/shard_map/ppermute | solution.py:24
  291.4 1.8 collective-permute-done.36
  293.1 4.1 %collective-permute-done.37 = bf16[16,1,60,32]{2,0,3,1:T(8,128)(2,1)S(1)} collective-permute-done((bf16[16,1,60,32]{2,0,3,1:T(8,128)(2,1)S(1)}, bf16[16,1,60,32]{2,0,3,1:T(8,128)(2,1)S(1)}, u32[]{:S(2)}, u32[]{:S(2)}) %collective-permute-start.37) | collective-permute-done | bytes 61472 | tf_op jit(solution)/shard_map/ppermute | solution.py:27
  304.8 2.9 collective-permute-done.38
  307.7 3.8 %collective-permute-done.39 = bf16[16,3,1,32]{2,0,3,1:T(8,128)(2,1)S(1)} collective-permute-done((bf16[16,3,1,32]{2,0,3,1:T(8,128)(2,1)S(1)}, bf16[16,3,1,32]{2,0,3,1:T(8,128)(2,1)S(1)}, u32[]{:S(2)}, u32[]{:S(2)}) %collective-permute-start.39) | collective-permute-done | bytes 3104 | tf_op jit(solution)/shard_map/ppermute | solution.py:27
  (238 shorter events, 75.4 us)
Async XLA Ops:
  5.6 12.3 %collective-permute-start = (f32[2,1,240,128]{2,3,1,0:T(8,128)S(1)}, f32[2,1,240,128]{2,3,1,0:T(8,128)S(1)}, u32[]{:S(2)}, u32[]{:S(2)}) collective-permute-start(f32[2,1,240,128]{2,3,1,0:T(8,128)S(1)} %get-tuple-element.61), channel_id=1, source_target_pairs={{0,4},{4,8},{8,12},{12,0},{1,5},{5,9},{9,13},{13,1},{2,6},{6,10},{... | collective-permute-start | bytes 737288 | tf_op jit(solution)/shard_map/ppermute | solution.py:24
  8.7 13.4 %collective-permute-start.1 = (f32[2,1,240,128]{2,3,1,0:T(8,128)S(1)}, f32[2,1,240,128]{2,3,1,0:T(8,128)S(1)}, u32[]{:S(2)}, u32[]{:S(2)}) collective-permute-start(f32[2,1,240,128]{2,3,1,0:T(8,128)S(1)} %get-tuple-element.62), channel_id=1, source_target_pairs={{4,0},{8,4},{12,8},{0,12},{5,1},{9,5},{13,9},{1,13},{6,2},{10,6},{... | collective-permute-start | bytes 737288 | tf_op jit(solution)/shard_map/ppermute | solution.py:27
  24.8 3.7 %collective-permute-start.2 = (f32[2,6,1,128]{3,0,2,1:T(2,128)S(1)}, f32[2,6,1,128]{3,0,2,1:T(2,128)S(1)}, u32[]{:S(2)}, u32[]{:S(2)}) collective-permute-start(f32[2,6,1,128]{3,0,2,1:T(2,128)S(1)} %copy.1474), channel_id=1, source_target_pairs={{0,2},{2,0},{1,3},{3,1},{4,6},{6,4},{5,7},{7,5},{8,10},{10,8},{9,1... | collective-permute-start | bytes 18440 | tf_op jit(solution)/shard_map/ppermute | solution.py:24
  26.6 3.7 %collective-permute-start.3 = (f32[2,6,1,128]{3,0,2,1:T(2,128)S(1)}, f32[2,6,1,128]{3,0,2,1:T(2,128)S(1)}, u32[]{:S(2)}, u32[]{:S(2)}) collective-permute-start(f32[2,6,1,128]{3,0,2,1:T(2,128)S(1)} %copy.1475), channel_id=1, source_target_pairs={{2,0},{0,2},{3,1},{1,3},{6,4},{4,6},{7,5},{5,7},{10,8},{8,10},{11,... | collective-permute-start | bytes 18440 | tf_op jit(solution)/shard_map/ppermute | solution.py:27
  32.4 34.1 %collective-permute-start.4 = (f32[2,6,242,1]{2,0,3,1:T(2,128)S(1)}, f32[2,6,242,1]{2,0,3,1:T(2,128)S(1)}, u32[]{:S(2)}, u32[]{:S(2)}) collective-permute-start(f32[2,6,242,1]{2,0,3,1:T(2,128)S(1)} %copy.1478), channel_id=1, source_target_pairs={{0,1},{1,0},{2,3},{3,2},{4,5},{5,4},{6,7},{7,6},{8,9},{9,8},{10,11... | collective-permute-start | bytes 34856 | tf_op jit(solution)/shard_map/ppermute | solution.py:24
  32.5 34.0 %collective-permute-start.5 = (f32[2,6,242,1]{2,0,3,1:T(2,128)S(1)}, f32[2,6,242,1]{2,0,3,1:T(2,128)S(1)}, u32[]{:S(2)}, u32[]{:S(2)}) collective-permute-start(f32[2,6,242,1]{2,0,3,1:T(2,128)S(1)} %copy.1479), channel_id=1, source_target_pairs={{1,0},{0,1},{3,2},{2,3},{5,4},{4,5},{7,6},{6,7},{9,8},{8,9},{11,10... | collective-permute-start | bytes 34856 | tf_op jit(solution)/shard_map/ppermute | solution.py:27
  69.6 5.1 %collective-permute-start.6 = (f32[1,240,128]{1,2,0:T(8,128)S(1)}, f32[1,240,128]{1,2,0:T(8,128)S(1)}, u32[]{:S(2)}, u32[]{:S(2)}) collective-permute-start(f32[1,240,128]{1,2,0:T(8,128)S(1)} %get-tuple-element.70), channel_id=1, source_target_pairs={{4,0},{8,4},{12,8},{0,12},{5,1},{9,5},{13,9},{1,13},{6,2},{10,6},{... | collective-permute-start | bytes 368648 | tf_op jit(solution)/shard_map/ppermute | solution.py:27
  69.7 6.8 %collective-permute-start.7 = (f32[1,240,128]{1,2,0:T(8,128)S(1)}, f32[1,240,128]{1,2,0:T(8,128)S(1)}, u32[]{:S(2)}, u32[]{:S(2)}) collective-permute-start(f32[1,240,128]{1,2,0:T(8,128)S(1)} %get-tuple-element.69), channel_id=1, source_target_pairs={{0,4},{4,8},{8,12},{12,0},{1,5},{5,9},{9,13},{13,1},{2,6},{6,10},{... | collective-permute-start | bytes 368648 | tf_op jit(solution)/shard_map/ppermute | solution.py:24
  76.7 12.1 %collective-permute-start.8 = (f32[6,1,128]{1,2,0:T(8,128)S(1)}, f32[6,1,128]{1,2,0:T(8,128)S(1)}, u32[]{:S(2)}, u32[]{:S(2)}) collective-permute-start(f32[6,1,128]{1,2,0:T(8,128)S(1)} %get-tuple-element.66), channel_id=1, source_target_pairs={{2,0},{0,2},{3,1},{1,3},{6,4},{4,6},{7,5},{5,7},{10,8},{8,10},{11,... | collective-permute-start | bytes 9224 | tf_op jit(solution)/shard_map/ppermute | solution.py:27
  76.8 16.6 %collective-permute-start.9 = (f32[6,1,128]{1,2,0:T(8,128)S(1)}, f32[6,1,128]{1,2,0:T(8,128)S(1)}, u32[]{:S(2)}, u32[]{:S(2)}) collective-permute-start(f32[6,1,128]{1,2,0:T(8,128)S(1)} %get-tuple-element.65), channel_id=1, source_target_pairs={{0,2},{2,0},{1,3},{3,1},{4,6},{6,4},{5,7},{7,5},{8,10},{10,8},{9,1... | collective-permute-start | bytes 9224 | tf_op jit(solution)/shard_map/ppermute | solution.py:24
  93.6 1.2 collective-permute-start.10
  93.7 1.3 collective-permute-start.11
  98.1 11.0 %collective-permute-start.12 = (f32[2,1,240,128]{2,3,1,0:T(8,128)S(1)}, f32[2,1,240,128]{2,3,1,0:T(8,128)S(1)}, u32[]{:S(2)}, u32[]{:S(2)}) collective-permute-start(f32[2,1,240,128]{2,3,1,0:T(8,128)S(1)} %get-tuple-element.59), channel_id=1, source_target_pairs={{0,4},{4,8},{8,12},{12,0},{1,5},{5,9},{9,13},{13,1},{2,6},{6,10},{... | collective-permute-start | bytes 737288 | tf_op jit(solution)/shard_map/ppermute | solution.py:24
  99.2 13.9 %collective-permute-start.13 = (f32[2,1,240,128]{2,3,1,0:T(8,128)S(1)}, f32[2,1,240,128]{2,3,1,0:T(8,128)S(1)}, u32[]{:S(2)}, u32[]{:S(2)}) collective-permute-start(f32[2,1,240,128]{2,3,1,0:T(8,128)S(1)} %get-tuple-element.60), channel_id=1, source_target_pairs={{4,0},{8,4},{12,8},{0,12},{5,1},{9,5},{13,9},{1,13},{6,2},{10,6},{... | collective-permute-start | bytes 737288 | tf_op jit(solution)/shard_map/ppermute | solution.py:27
  113.7 3.7 %collective-permute-start.14 = (f32[2,6,1,128]{3,0,2,1:T(2,128)S(1)}, f32[2,6,1,128]{3,0,2,1:T(2,128)S(1)}, u32[]{:S(2)}, u32[]{:S(2)}) collective-permute-start(f32[2,6,1,128]{3,0,2,1:T(2,128)S(1)} %copy.1485), channel_id=1, source_target_pairs={{0,2},{2,0},{1,3},{3,1},{4,6},{6,4},{5,7},{7,5},{8,10},{10,8},{9,1... | collective-permute-start | bytes 18440 | tf_op jit(solution)/shard_map/ppermute | solution.py:24
  115.8 3.7 %collective-permute-start.15 = (f32[2,6,1,128]{3,0,2,1:T(2,128)S(1)}, f32[2,6,1,128]{3,0,2,1:T(2,128)S(1)}, u32[]{:S(2)}, u32[]{:S(2)}) collective-permute-start(f32[2,6,1,128]{3,0,2,1:T(2,128)S(1)} %copy.1486), channel_id=1, source_target_pairs={{2,0},{0,2},{3,1},{1,3},{6,4},{4,6},{7,5},{5,7},{10,8},{8,10},{11,... | collective-permute-start | bytes 18440 | tf_op jit(solution)/shard_map/ppermute | solution.py:27
  119.9 53.3 %collective-permute-start.16 = (f32[2,6,242,1]{2,0,3,1:T(2,128)S(1)}, f32[2,6,242,1]{2,0,3,1:T(2,128)}, u32[]{:S(2)}, u32[]{:S(2)}) collective-permute-start(f32[2,6,242,1]{2,0,3,1:T(2,128)S(1)} %copy.1489), channel_id=1, source_target_pairs={{0,1},{1,0},{2,3},{3,2},{4,5},{5,4},{6,7},{7,6},{8,9},{9,8},{10,11... | collective-permute-start | bytes 34856 | tf_op jit(solution)/shard_map/ppermute | solution.py:24
  120.6 53.4 %collective-permute-start.17 = (f32[2,6,242,1]{2,0,3,1:T(2,128)}, f32[2,6,242,1]{2,0,3,1:T(2,128)}, u32[]{:S(2)}, u32[]{:S(2)}) collective-permute-start(f32[2,6,242,1]{2,0,3,1:T(2,128)} %copy.1490), channel_id=1, source_target_pairs={{1,0},{0,1},{3,2},{2,3},{5,4},{4,5},{7,6},{6,7},{9,8},{8,9},{11,10... | collective-permute-start | bytes 34856 | tf_op jit(solution)/shard_map/ppermute | solution.py:27
  177.9 10.7 %collective-permute-start.18 = (f32[1,240,128]{1,2,0:T(8,128)S(1)}, f32[1,240,128]{1,2,0:T(8,128)S(1)}, u32[]{:S(2)}, u32[]{:S(2)}) collective-permute-start(f32[1,240,128]{1,2,0:T(8,128)S(1)} %get-tuple-element.68), channel_id=1, source_target_pairs={{4,0},{8,4},{12,8},{0,12},{5,1},{9,5},{13,9},{1,13},{6,2},{10,6},{... | collective-permute-start | bytes 368648 | tf_op jit(solution)/shard_map/ppermute | solution.py:27
  177.9 10.6 %collective-permute-start.19 = (f32[1,240,128]{1,2,0:T(8,128)S(1)}, f32[1,240,128]{1,2,0:T(8,128)S(1)}, u32[]{:S(2)}, u32[]{:S(2)}) collective-permute-start(f32[1,240,128]{1,2,0:T(8,128)S(1)} %get-tuple-element.67), channel_id=1, source_target_pairs={{0,4},{4,8},{8,12},{12,0},{1,5},{5,9},{9,13},{13,1},{2,6},{6,10},{... | collective-permute-start | bytes 368648 | tf_op jit(solution)/shard_map/ppermute | solution.py:24
  188.5 18.6 %copy-start.2 = (f32[1,240,128]{1,2,0:T(8,128)}, f32[1,240,128]{1,2,0:T(8,128)S(1)}, u32[]{:S(2)}) copy-start(f32[1,240,128]{1,2,0:T(8,128)S(1)} %collective-permute-done.19) | copy-start | bytes 368644
  189.6 12.3 %collective-permute-start.20 = (f32[6,1,128]{1,2,0:T(8,128)}, f32[6,1,128]{1,2,0:T(8,128)S(1)}, u32[]{:S(2)}, u32[]{:S(2)}) collective-permute-start(f32[6,1,128]{1,2,0:T(8,128)} %get-tuple-element.64), channel_id=1, source_target_pairs={{2,0},{0,2},{3,1},{1,3},{6,4},{4,6},{7,5},{5,7},{10,8},{8,10},{11,... | collective-permute-start | bytes 9224 | tf_op jit(solution)/shard_map/ppermute | solution.py:27
  189.6 17.5 %collective-permute-start.21 = (f32[6,1,128]{1,2,0:T(8,128)}, f32[6,1,128]{1,2,0:T(8,128)S(1)}, u32[]{:S(2)}, u32[]{:S(2)}) collective-permute-start(f32[6,1,128]{1,2,0:T(8,128)} %get-tuple-element.63), channel_id=1, source_target_pairs={{0,2},{2,0},{1,3},{3,1},{4,6},{6,4},{5,7},{7,5},{8,10},{10,8},{9,1... | collective-permute-start | bytes 9224 | tf_op jit(solution)/shard_map/ppermute | solution.py:24
  207.3 1.2 collective-permute-start.22
  207.4 1.3 collective-permute-start.23
  221.6 3.8 %collective-permute-start.24 = (bf16[4,1,60,32]{2,3,1,0:T(8,128)(2,1)S(1)}, bf16[4,1,60,32]{2,3,1,0:T(8,128)(2,1)S(1)}, u32[]{:S(2)}, u32[]{:S(2)}) collective-permute-start(bf16[4,1,60,32]{2,3,1,0:T(8,128)(2,1)S(1)} %pad_maximum_fusion.57), channel_id=1, source_target_pairs={{0,4},{4,8},{8,12},{1,5},{5,9},{9,13},{2,6},{6,10},{10,14},{3,7},{... | collective-permute-start | bytes 46088 | tf_op jit(solution)/shard_map/ppermute | solution.py:24
  223.8 5.8 %collective-permute-start.25 = (bf16[4,1,60,32]{2,3,1,0:T(8,128)(2,1)S(1)}, bf16[4,1,60,32]{2,3,1,0:T(8,128)(2,1)S(1)}, u32[]{:S(2)}, u32[]{:S(2)}) collective-permute-start(bf16[4,1,60,32]{2,3,1,0:T(8,128)(2,1)S(1)} %pad_maximum_fusion.57), channel_id=1, source_target_pairs={{4,0},{8,4},{12,8},{5,1},{9,5},{13,9},{6,2},{10,6},{14,10},{7,3},{... | collective-permute-start | bytes 46088 | tf_op jit(solution)/shard_map/ppermute | solution.py:27
  229.8 4.4 %collective-permute-start.26 = (bf16[4,3,1,32]{2,3,1,0:T(8,128)(2,1)S(1)}, bf16[4,3,1,32]{2,3,1,0:T(8,128)(2,1)S(1)}, u32[]{:S(2)}, u32[]{:S(2)}) collective-permute-start(bf16[4,3,1,32]{2,3,1,0:T(8,128)(2,1)S(1)} %get-tuple-element.109), channel_id=1, source_target_pairs={{0,2},{1,3},{4,6},{5,7},{8,10},{9,11},{12,14},{13,15},{16,18},{17,... | collective-permute-start | bytes 2312 | tf_op jit(solution)/shard_map/ppermute | solution.py:24
  232.0 6.5 %collective-permute-start.27 = (bf16[4,3,1,32]{2,3,1,0:T(8,128)(2,1)S(1)}, bf16[4,3,1,32]{2,3,1,0:T(8,128)(2,1)S(1)}, u32[]{:S(2)}, u32[]{:S(2)}) collective-permute-start(bf16[4,3,1,32]{2,3,1,0:T(8,128)(2,1)S(1)} %get-tuple-element.110), channel_id=1, source_target_pairs={{2,0},{3,1},{6,4},{7,5},{10,8},{11,9},{14,12},{15,13},{18,16},{19,... | collective-permute-start | bytes 2312 | tf_op jit(solution)/shard_map/ppermute | solution.py:27
  238.8 3.3 %collective-permute-start.28 = (bf16[4,3,62,1]{2,3,1,0:T(2,128)(2,1)S(1)}, bf16[4,3,62,1]{2,3,1,0:T(2,128)(2,1)S(1)}, u32[]{:S(2)}, u32[]{:S(2)}) collective-permute-start(bf16[4,3,62,1]{2,3,1,0:T(2,128)(2,1)S(1)} %get-tuple-element.108), channel_id=1, source_target_pairs={{0,1},{2,3},{4,5},{6,7},{8,9},{10,11},{12,13},{14,15},{16,17},{18,... | collective-permute-start | bytes 4472 | tf_op jit(solution)/shard_map/ppermute | solution.py:24
  240.1 3.1 collective-permute-start.29
  241.6 11.4 %copy-start.4 = (bf16[27,16,4]{0,2,1:T(4,128)(2,1)S(1)}, bf16[27,16,4]{0,2,1:T(4,128)(2,1)}, u32[]{:S(2)}) copy-start(bf16[27,16,4]{0,2,1:T(4,128)(2,1)} %param.12) | copy-start | bytes 10372
  241.6 11.3 %copy-start.5 = (f32[16]{0:T(128)S(1)}, f32[16]{0:T(128)}, u32[]{:S(2)}) copy-start(f32[16]{0:T(128)} %param.13) | copy-start | bytes 196
  253.3 7.3 %collective-permute-start.30 = (bf16[16,1,60,32]{2,0,3,1:T(8,128)(2,1)S(1)}, bf16[16,1,60,32]{2,0,3,1:T(8,128)(2,1)S(1)}, u32[]{:S(2)}, u32[]{:S(2)}) collective-permute-start(bf16[16,1,60,32]{2,0,3,1:T(8,128)(2,1)S(1)} %bitcast.373), channel_id=1, source_target_pairs={{0,4},{4,8},{8,12},{1,5},{5,9},{9,13},{2,6},{6,10},{10,14},{3,7},{... | collective-permute-start | bytes 184328 | tf_op jit(solution)/shard_map/ppermute | solution.py:24
  257.5 7.5 %collective-permute-start.31 = (bf16[16,1,60,32]{2,0,3,1:T(8,128)(2,1)S(1)}, bf16[16,1,60,32]{2,0,3,1:T(8,128)(2,1)S(1)}, u32[]{:S(2)}, u32[]{:S(2)}) collective-permute-start(bf16[16,1,60,32]{2,0,3,1:T(8,128)(2,1)S(1)} %bitcast.374), channel_id=1, source_target_pairs={{4,0},{8,4},{12,8},{5,1},{9,5},{13,9},{6,2},{10,6},{14,10},{7,3},{... | collective-permute-start | bytes 184328 | tf_op jit(solution)/shard_map/ppermute | solution.py:27
  265.2 9.4 %collective-permute-start.32 = (bf16[16,3,1,32]{2,0,3,1:T(8,128)(2,1)S(1)}, bf16[16,3,1,32]{2,0,3,1:T(8,128)(2,1)S(1)}, u32[]{:S(2)}, u32[]{:S(2)}) collective-permute-start(bf16[16,3,1,32]{2,0,3,1:T(8,128)(2,1)S(1)} %get-tuple-element.77), channel_id=1, source_target_pairs={{0,2},{1,3},{4,6},{5,7},{8,10},{9,11},{12,14},{13,15},{16,18},{17,... | collective-permute-start | bytes 9224 | tf_op jit(solution)/shard_map/ppermute | solution.py:24
  266.8 12.0 %collective-permute-start.33 = (bf16[16,3,1,32]{2,0,3,1:T(8,128)(2,1)S(1)}, bf16[16,3,1,32]{2,0,3,1:T(8,128)(2,1)S(1)}, u32[]{:S(2)}, u32[]{:S(2)}) collective-permute-start(bf16[16,3,1,32]{2,0,3,1:T(8,128)(2,1)S(1)} %get-tuple-element.78), channel_id=1, source_target_pairs={{2,0},{3,1},{6,4},{7,5},{10,8},{11,9},{14,12},{15,13},{18,16},{19,... | collective-permute-start | bytes 9224 | tf_op jit(solution)/shard_map/ppermute | solution.py:27
  278.9 3.0 collective-permute-start.34
  280.2 3.1 collective-permute-start.35
  283.8 2.3 copy-start.6
  286.1 15.0 %copy-start.3 = (bf16[27,1,16]{0,2,1:T(8,128)(2,1)S(1)}, bf16[27,1,16]{0,2,1:T(8,128)(2,1)}, u32[]{:S(2)}) copy-start(bf16[27,1,16]{0,2,1:T(8,128)(2,1)} %param.16) | copy-start | bytes 2596
  286.1 15.7 %copy-start = (f32[4,240,128]{1,2,0:T(8,128)S(1)}, f32[4,240,128]{1,2,0:T(8,128)}, u32[]{:S(2)}) copy-start(f32[4,240,128]{1,2,0:T(8,128)} %get-tuple-element.29) | copy-start | bytes 1474564
  286.7 6.4 %collective-permute-start.36 = (bf16[16,1,60,32]{2,0,3,1:T(8,128)(2,1)S(1)}, bf16[16,1,60,32]{2,0,3,1:T(8,128)(2,1)S(1)}, u32[]{:S(2)}, u32[]{:S(2)}) collective-permute-start(bf16[16,1,60,32]{2,0,3,1:T(8,128)(2,1)S(1)} %bitcast.367), channel_id=1, source_target_pairs={{0,4},{4,8},{8,12},{1,5},{5,9},{9,13},{2,6},{6,10},{10,14},{3,7},{... | collective-permute-start | bytes 184328 | tf_op jit(solution)/shard_map/ppermute | solution.py:24
  290.1 7.2 %collective-permute-start.37 = (bf16[16,1,60,32]{2,0,3,1:T(8,128)(2,1)S(1)}, bf16[16,1,60,32]{2,0,3,1:T(8,128)(2,1)S(1)}, u32[]{:S(2)}, u32[]{:S(2)}) collective-permute-start(bf16[16,1,60,32]{2,0,3,1:T(8,128)(2,1)S(1)} %bitcast.368), channel_id=1, source_target_pairs={{4,0},{8,4},{12,8},{5,1},{9,5},{13,9},{6,2},{10,6},{14,10},{7,3},{... | collective-permute-start | bytes 184328 | tf_op jit(solution)/shard_map/ppermute | solution.py:27
  298.3 9.4 %collective-permute-start.38 = (bf16[16,3,1,32]{2,0,3,1:T(8,128)(2,1)}, bf16[16,3,1,32]{2,0,3,1:T(8,128)(2,1)S(1)}, u32[]{:S(2)}, u32[]{:S(2)}) collective-permute-start(bf16[16,3,1,32]{2,0,3,1:T(8,128)(2,1)} %get-tuple-element.73), channel_id=1, source_target_pairs={{0,2},{1,3},{4,6},{5,7},{8,10},{9,11},{12,14},{13,15},{16,18},{17,... | collective-permute-start | bytes 9224 | tf_op jit(solution)/shard_map/ppermute | solution.py:24
  299.8 11.8 %collective-permute-start.39 = (bf16[16,3,1,32]{2,0,3,1:T(8,128)(2,1)S(1)}, bf16[16,3,1,32]{2,0,3,1:T(8,128)(2,1)S(1)}, u32[]{:S(2)}, u32[]{:S(2)}) collective-permute-start(bf16[16,3,1,32]{2,0,3,1:T(8,128)(2,1)S(1)} %get-tuple-element.74), channel_id=1, source_target_pairs={{2,0},{3,1},{6,4},{7,5},{10,8},{11,9},{14,12},{15,13},{18,16},{19,... | collective-permute-start | bytes 9224 | tf_op jit(solution)/shard_map/ppermute | solution.py:27
  311.6 3.3 %collective-permute-start.40 = (bf16[16,3,62,1]{2,0,3,1:T(8,128)(2,1)S(1)}, bf16[16,3,62,1]{2,0,3,1:T(8,128)(2,1)S(1)}, u32[]{:S(2)}, u32[]{:S(2)}) collective-permute-start(bf16[16,3,62,1]{2,0,3,1:T(8,128)(2,1)S(1)} %get-tuple-element.53), channel_id=1, source_target_pairs={{0,1},{2,3},{4,5},{6,7},{8,9},{10,11},{12,13},{14,15},{16,17},{18,... | collective-permute-start | bytes 17864 | tf_op jit(solution)/shard_map/ppermute | solution.py:24
  312.9 3.1 collective-permute-start.41
  (1 other events, 1.5 us)
where the time goes:
time: 325 us; the launch traced here: 321 us
  waiting for transfers between devices  97.6 us (30%)
  blocking collectives  73.6 us (23%)
  local copies, waits for them, and re-layouts  58.2 us (18%)
  starting transfers between devices  54.6 us (17%)
  other arithmetic  30 us (9%)
  between operations  5.8 us (2%)
    psum x2, blocking collectives, stiff_mean(): lax.psum((jnp.sum(mobility * fraction), jnp.sum(mobility)), ('gx', 'gy',...  73.6 us
    ppermute x21, waiting for transfers between devices, extended(): lax.ppermute(lax.slice_in_dim(block, 0, width, axis=dim), axis, backward)  55.9 us
    ppermute x21, waiting for transfers between devices, extended(): lax.ppermute(lax.slice_in_dim(block, block.shape[dim] - width, None, axis...  41.8 us
    ppermute x21, starting transfers between devices, extended(): lax.ppermute(lax.slice_in_dim(block, block.shape[dim] - width, None, axis...  35.5 us
    reduce_sum x12, local copies, waits for them, and re-layouts, pool_four(): field.reshape(size_x // 4, 4, size_y // 4, 4, size_z // 4, 4)  26.2 us
    ppermute x21, starting transfers between devices, extended(): lax.ppermute(lax.slice_in_dim(block, 0, width, axis=dim), axis, backward)  19.1 us
    reduce_sum x6, other arithmetic, pool_four(): field.reshape(size_x // 4, 4, size_y // 4, 4, size_z // 4, 4)  15.6 us
    unnamed x74, local copies, waits for them, and re-layouts  11.6 us
  transfers between devices with their start and end apart: 42, of which 33 were waited for; matrix products, arithmetic and copies ran while one was open for 11% of the time, Pallas kernels for 0%

commit v1 on v0

v1 whole, which is shorter than its diff:
```python
import jax
import jax.numpy as jnp
import numpy as np
from jax import lax
from jax.experimental import pallas as pl
from jax.experimental.pallas import tpu as pltpu
from jax.sharding import PartitionSpec as P

F32 = jnp.float32
WELL_HEIGHT = 1.0
STRAIN_COUPLING = 4.0
TIME_STEP = 0.01
DAMAGE_RATE = 0.8
ENERGY_CRITICAL = 0.02

OFF = 16
A_LOW, A_SPAN = 0.0, 1.0
B_LOW, B_SPAN = -1.1, 3.1


def to_code(x, low, span):
    v = (x - low) * (65535.0 / span) - 32768.0
    v = jnp.clip(jnp.round(v), -32768.0, 32767.0)
    return v.astype(jnp.int32).astype(jnp.int16)


def from_code(q, low, span):
    return (q.astype(jnp.int32).astype(F32) + 32768.0) * (span / 65535.0) + low


def call(kernel, outs, *args):
    return pl.pallas_call(
        kernel,
        out_shape=[jax.ShapeDtypeStruct(s, t) for s, t in outs],
        compiler_params=pltpu.CompilerParams(vmem_limit_bytes=48 * 1024 * 1024),
    )(*args)


def chunks(start, stop, size):
    return [(r, min(size, stop - r)) for r in range(start, stop, size)]


def by_label(labels, values):
    return jnp.where(labels == 0, values[0], jnp.where(labels == 1, values[1], values[2])).astype(F32)


FACTORS = (1.0, 0.3, 0.05)
ROOTS = tuple(float(np.sqrt(np.float32(v))) for v in FACTORS)


def fold(x):
    return x.reshape(x.shape[0] // 8, 8, x.shape[1]).sum(0)


def first_kernel(c_ref, d_ref, l_ref, amp_ref, lo_ref, hi_ref, sum_ref):
    nx, ny, nz = c_ref.shape
    top = jnp.zeros((8, nz), F32)
    bottom = jnp.zeros((8, nz), F32)
    for x in range(nx):
        for r, n in chunks(0, ny, 48):
            f = c_ref[x, r:r + n, :]
            a = by_label(l_ref[x, r:r + n, :], ROOTS) * (1.0 - d_ref[x, r:r + n, :])
            amp_ref[x, r:r + n, :] = a
            m = a * a
            top = top + fold(m * f)
            bottom = bottom + fold(m)
            if x < 2:
                lo_ref[x, r:r + n, :] = to_code(f, A_LOW, A_SPAN)
            if x >= nx - 2:
                hi_ref[nx - 1 - x, r:r + n, :] = to_code(f, A_LOW, A_SPAN)
            if x == 0:
                lo_ref[2, r:r + n, :] = to_code(a, A_LOW, A_SPAN)
            if x == nx - 1:
                hi_ref[2, r:r + n, :] = to_code(a, A_LOW, A_SPAN)
    sum_ref[0:8, :] = top
    sum_ref[8:16, :] = bottom


def edge_rows(f_ref, amp_ref, lo_ref, hi_ref, s_ref, out_ref, low, span):
    nx, ny, nz = f_ref.shape
    low_rows = [from_code(r[0, 0:16, :], low, span)[0:1] for r in (lo_ref, hi_ref)]
    high_rows = [from_code(r[0, ny - 16:ny, :], low, span)[15:16] for r in (lo_ref, hi_ref)]
    for side, first, second, beside in ((0, 0, 1, low_rows), (1, ny - 1, ny - 2, high_rows)):
        for x in range(nx):
            out_ref[side, 2 * x:2 * x + 1, :] = f_ref[x, first:first + 1, :]
            out_ref[side, 2 * x + 1:2 * x + 2, :] = f_ref[x, second:second + 1, :]
            if amp_ref is not None:
                out_ref[side, 10 + x:11 + x, :] = amp_ref[x, first:first + 1, :]
        out_ref[side, 8:9, :] = beside[0]
        out_ref[side, 9:10, :] = beside[1]
        out_ref[side, 16:32, :] = s_ref[...]


def edge_rows_a(f_ref, amp_ref, lo_ref, hi_ref, s_ref, out_ref):
    edge_rows(f_ref, amp_ref, lo_ref, hi_ref, s_ref, out_ref, A_LOW, A_SPAN)


def edge_rows_b(f_ref, lo_ref, hi_ref, s_ref, out_ref):
    edge_rows(f_ref, None, lo_ref, hi_ref, s_ref, out_ref, B_LOW, B_SPAN)


def assemble(f_ref, amp_ref, lo_ref, hi_ref, yr_ref, s_ref, pad_ref, apad_ref, zp_ref, low, span, add):
    nx, ny, nz = f_ref.shape
    end = OFF + ny
    lane = lax.broadcasted_iota(jnp.int32, (1, nz), 1)
    outer = (lane < 16) | (lane >= nz - 16)

    def pack(f, a):
        return f if a is None else jnp.where(outer, f, pltpu.roll(a, nz // 2, 1))

    for p, ref in ((0, lo_ref), (nx + 3, hi_ref)):
        for r, n in chunks(0, ny, 48):
            pad_ref[p, OFF + r:OFF + r + n, :] = from_code(ref[1, r:r + n, :], low, span)
    for p, ref in ((1, lo_ref), (nx + 2, hi_ref)):
        for r, n in chunks(0, ny, 48):
            f = from_code(ref[0, r:r + n, :], low, span)
            pad_ref[p, OFF + r:OFF + r + n, :] = f
            if amp_ref is not None:
                apad_ref[p - 1, OFF + r:OFF + r + n, :] = from_code(ref[2, r:r + n, :], low, span)
            zp_ref[p - 1, OFF + r:OFF + r + n, :] = f
    for p, k in ((1, 8), (nx + 2, 9)):
        pad_ref[p, OFF - 1:OFF, :] = yr_ref[1, k:k + 1, :]
        pad_ref[p, end:end + 1, :] = yr_ref[0, k:k + 1, :]
    for x in range(nx):
        for r, n in chunks(0, ny, 48):
            f = f_ref[x, r:r + n, :]
            a = None
            if amp_ref is not None:
                a = amp_ref[x, r:r + n, :]
                apad_ref[x + 1, OFF + r:OFF + r + n, :] = a
            pad_ref[x + 2, OFF + r:OFF + r + n, :] = f
            zp_ref[x + 1, OFF + r:OFF + r + n, :] = pack(f, a)
        for side, near, far in ((1, OFF - 1, OFF - 2), (0, end, end + 1)):
            f = yr_ref[side, 2 * x:2 * x + 1, :]
            pad_ref[x + 2, near:near + 1, :] = f
            pad_ref[x + 2, far:far + 1, :] = yr_ref[side, 2 * x + 1:2 * x + 2, :]
            if amp_ref is not None:
                apad_ref[x + 1, near:near + 1, :] = yr_ref[side, 10 + x:11 + x, :]
            zp_ref[x + 1, near:near + 1, :] = f
    s = s_ref[...]
    if add:
        s = s + yr_ref[0, 16:32, :]
    zp_ref[0, 0:16, :] = s
    pad_ref[0, 0:16, :] = s


def assemble_a(add):
    def kernel(f_ref, amp_ref, lo_ref, hi_ref, yr_ref, s_ref, pad_ref, apad_ref, zp_ref):
        assemble(f_ref, amp_ref, lo_ref, hi_ref, yr_ref, s_ref, pad_ref, apad_ref, zp_ref, A_LOW, A_SPAN, add)
    return kernel


def assemble_b(add):
    def kernel(f_ref, lo_ref, hi_ref, yr_ref, s_ref, pad_ref, zp_ref):
        assemble(f_ref, None, lo_ref, hi_ref, yr_ref, s_ref, pad_ref, None, zp_ref, B_LOW, B_SPAN, add)
    return kernel


def weighted_mean(pad_ref, zr_ref, add):
    s = pad_ref[0, 0:16, :]
    if add:
        s = s + zr_ref[0, 0:16, :]
    return jnp.sum(s[0:8], keepdims=True) / jnp.sum(s[8:16], keepdims=True)


def chem_of(f, m, around, mean):
    well = 2.0 * WELL_HEIGHT * f * (1.0 - f) * (1.0 - 2.0 * f)
    return well + 6.0 * f - around + STRAIN_COUPLING * m * (f - mean)


def worn(a, m, f, mean):
    e = f - mean
    energy = 0.5 * STRAIN_COUPLING * m * e * e
    return a * (1.0 - DAMAGE_RATE * jnp.maximum(energy - ENERGY_CRITICAL, 0.0))


class Geometry:
    def __init__(self, nx, ny, nz):
        self.nx, self.ny, self.nz = nx, ny, nz
        self.lane = lax.broadcasted_iota(jnp.int32, (1, nz), 1)
        self.first = self.lane == 0
        self.last = self.lane == nz - 1

    def before(self, own, other):
        return pltpu.roll(jnp.where(self.last, other, own), 1, 1)

    def after(self, own, other):
        return pltpu.roll(jnp.where(self.first, other, own), self.nz - 1, 1)


def chemistry(g, pad_ref, mob_ref, mobe_ref, zr_ref, chem_ref, cheme_ref, mean):
    nx, ny = g.nx, g.ny
    for p in range(nx + 2):
        inside = 1 <= p <= nx
        rows = chunks(OFF - 8, OFF + ny + 8, 32) if inside else chunks(OFF, OFF + ny, 48)
        for r, n in rows:
            f = pad_ref[p + 1, r:r + n, :]
            e = zr_ref[p, r:r + n, :]
            around = (pad_ref[p, r:r + n, :] + pad_ref[p + 2, r:r + n, :]
                      + pad_ref[p + 1, r - 1:r - 1 + n, :] + pad_ref[p + 1, r + 1:r + 1 + n, :]
                      + g.before(f, e) + g.after(f, e))
            chem_ref[p, r:r + n, :] = chem_of(f, mob_ref[p, r:r + n, :], around, mean)
        if inside:
            for r, n in chunks(OFF, OFF + ny, 48):
                f = pad_ref[p + 1, r:r + n, :]
                e = zr_ref[p, r:r + n, :]
                around = (zr_ref[p - 1, r:r + n, :] + zr_ref[p + 1, r:r + n, :]
                          + zr_ref[p, r - 1:r - 1 + n, :] + zr_ref[p, r + 1:r + 1 + n, :]
                          + g.before(e, f) + g.after(e, f))
                cheme_ref[p - 1, r - OFF:r - OFF + n, :] = chem_of(
                    e, mobe_ref[p - 1, r - OFF:r - OFF + n, :], around, mean)


def flux_of(g, x, r, n, mob_ref, mobe_ref, chem_ref, cheme_ref):
    p = x + 1
    m = mob_ref[p, r:r + n, :]
    q = chem_ref[p, r:r + n, :]
    me = mobe_ref[x, r - OFF:r - OFF + n, :]
    qe = cheme_ref[x, r - OFF:r - OFF + n, :]
    total = None
    for nm, nq in (
        (mob_ref[p - 1, r:r + n, :], chem_ref[p - 1, r:r + n, :]),
        (mob_ref[p + 1, r:r + n, :], chem_ref[p + 1, r:r + n, :]),
        (mob_ref[p, r - 1:r - 1 + n, :], chem_ref[p, r - 1:r - 1 + n, :]),
        (mob_ref[p, r + 1:r + 1 + n, :], chem_ref[p, r + 1:r + 1 + n, :]),
        (g.before(m, me), g.before(q, qe)),
        (g.after(m, me), g.after(q, qe)),
    ):
        term = (nm + m) * (nq - q)
        total = term if total is None else total + term
    return m, 0.5 * total


def step_a(add):
    def kernel(pad_ref, apad_ref, zr_ref, f2_ref, a2_ref, ae2_ref, lo_ref, hi_ref, sum_ref,
               mob_ref, mobe_ref, chem_ref, cheme_ref):
        nx, ny, nz = f2_ref.shape
        g = Geometry(nx, ny, nz)
        mean = weighted_mean(pad_ref, zr_ref, add)
        for p in range(nx + 2):
            inside = 1 <= p <= nx
            rows = chunks(OFF - 8, OFF + ny + 8, 32) if inside else chunks(OFF, OFF + ny, 48)
            for r, n in rows:
                a = apad_ref[p, r:r + n, :]
                m = a * a
                mob_ref[p, r:r + n, :] = m
                a2_ref[p, r:r + n, :] = worn(a, m, pad_ref[p + 1, r:r + n, :], mean)
            if inside:
                for r, n in chunks(OFF, OFF + ny, 48):
                    e = zr_ref[p, r:r + n, :]
                    a = pltpu.roll(e, nz // 2, 1)
                    m = a * a
                    mobe_ref[p - 1, r - OFF:r - OFF + n, :] = m
                    ae2_ref[p - 1, r - OFF:r - OFF + n, :] = worn(a, m, e, mean)
        chemistry(g, pad_ref, mob_ref, mobe_ref, zr_ref, chem_ref, cheme_ref, mean)
        top = jnp.zeros((8, nz), F32)
        bottom = jnp.zeros((8, nz), F32)
        for x in range(nx):
            for r, n in chunks(OFF, OFF + ny, 48):
                _, flux = flux_of(g, x, r, n, mob_ref, mobe_ref, chem_ref, cheme_ref)
                f = pad_ref[x + 2, r:r + n, :] + TIME_STEP * flux
                s = slice(r - OFF, r - OFF + n)
                f2_ref[x, s, :] = f
                a = a2_ref[x + 1, r:r + n, :]
                m = a * a
                top = top + fold(m * f)
                bottom = bottom + fold(m)
                if x < 2:
                    lo_ref[x, s, :] = to_code(f, B_LOW, B_SPAN)
                if x >= nx - 2:
                    hi_ref[nx - 1 - x, s, :] = to_code(f, B_LOW, B_SPAN)
        sum_ref[0:8, :] = top
        sum_ref[8:16, :] = bottom
    return kernel


def step_b(add):
    def kernel(pad_ref, a2_ref, ae2_ref, zr_ref, l_ref, f3_ref, dmg_ref, flux_ref, pool_ref,
               mob_ref, mobe_ref, chem_ref, cheme_ref, pool_scr):
        nx, ny, nz = f3_ref.shape
        g = Geometry(nx, ny, nz)
        mean = weighted_mean(pad_ref, zr_ref, add)
        for p in range(nx + 2):
            inside = 1 <= p <= nx
            rows = chunks(OFF - 8, OFF + ny + 8, 32) if inside else chunks(OFF, OFF + ny, 48)
            for r, n in rows:
                a = a2_ref[p, r:r + n, :]
                mob_ref[p, r:r + n, :] = a * a
            if inside:
                for r, n in chunks(0, ny, 48):
                    a = ae2_ref[p - 1, r:r + n, :]
                    mobe_ref[p - 1, r:r + n, :] = a * a
        chemistry(g, pad_ref, mob_ref, mobe_ref, zr_ref, chem_ref, cheme_ref, mean)
        for r, n in chunks(OFF, OFF + ny, 48):
            s = slice(r - OFF, r - OFF + n)
            pooled = [None] * 4
            for x in range(nx):
                m, flux = flux_of(g, x, r, n, mob_ref, mobe_ref, chem_ref, cheme_ref)
                f0 = pad_ref[x + 2, r:r + n, :]
                f = f0 + TIME_STEP * flux
                a = worn(a2_ref[x + 1, r:r + n, :], m, f0, mean)
                labels = l_ref[x, s, :]
                k = by_label(labels, FACTORS)
                dmg = 1.0 - a * by_label(labels, tuple(1.0 / v for v in ROOTS))
                f3_ref[x, s, :] = f
                dmg_ref[x, s, :] = dmg
                flux_ref[x, s, :] = flux
                for i, v in enumerate((f, dmg, a * a, k)):
                    pooled[i] = v if pooled[i] is None else pooled[i] + v
            for i in range(4):
                pool_scr[i, s, :] = pooled[i]
        py, pz = ny // 4, nz // 4
        zin = lax.broadcasted_iota(jnp.int32, (nz, 4 * pz), 0)
        out = lax.broadcasted_iota(jnp.int32, (nz, 4 * pz), 1)
        total = jnp.zeros((py, 4 * pz), F32)
        for i in range(4):
            rows = (pool_scr[i, pl.ds(0, py, stride=4), :] + pool_scr[i, pl.ds(1, py, stride=4), :]
                    + pool_scr[i, pl.ds(2, py, stride=4), :] + pool_scr[i, pl.ds(3, py, stride=4), :])
            pick = jnp.where((zin // 4 == out // 4) & (out % 4 == i), 1.0 / 64.0, 0.0).astype(F32)
            total = total + jnp.dot(rows, pick, precision=lax.Precision.HIGHEST, preferred_element_type=F32)
        pool_ref[0:py, :] = total.astype(jnp.bfloat16)
    return kernel


def ring(axis, shift):
    count = lax.axis_size(axis)
    return [(i, (i + shift) % count) for i in range(count)]


def pair_sum(s, axis):
    count = lax.axis_size(axis)
    if count & (count - 1):
        return lax.psum(s, axis)
    bit = 1
    while bit < count:
        s = s + lax.ppermute(s, axis, [(i, i ^ bit) for i in range(count)])
        bit *= 2
    return s


def both_sides(pay, axis):
    if lax.axis_size(axis) == 2:
        return lax.ppermute(pay, axis, ring(axis, 1))
    return jnp.stack([lax.ppermute(pay[0], axis, ring(axis, -1)), lax.ppermute(pay[1], axis, ring(axis, 1))])


def z_neighbour(pay, axis):
    if lax.axis_size(axis) == 2:
        return lax.ppermute(pay, axis, ring(axis, 1))
    above = lax.ppermute(pay, axis, ring(axis, -1))
    below = lax.ppermute(pay, axis, ring(axis, 1))
    lane = lax.broadcasted_iota(jnp.int32, pay.shape, pay.ndim - 1)
    quarter = pay.shape[-1] // 4
    return jnp.where((lane < quarter) | ((lane >= 2 * quarter) & (lane < 3 * quarter)), above, below)


def reduce_ahead(s):
    for axis in ("gx",) + tuple(a for a in ("gy", "gz") if lax.axis_size(a) != 2):
        s = pair_sum(s, axis)
    return s


def body(concentration, damage, labels, w_first, b_first, w_second, b_second, w_third, b_third):
    nx, ny, nz = concentration.shape
    rows = ny + 2 * OFF
    plane = (ny, nz)
    ride_y = lax.axis_size("gy") == 2
    ride_z = lax.axis_size("gz") == 2
    i16 = jnp.int16
    scratch = [
        pltpu.VMEM((nx + 2, rows, nz), F32), pltpu.VMEM((nx,) + plane, F32),
        pltpu.VMEM((nx + 2, rows, nz), F32), pltpu.VMEM((nx,) + plane, F32),
    ]

    def heavy(kernel, outs, extra, *args):
        return pl.pallas_call(
            kernel,
            out_shape=[jax.ShapeDtypeStruct(s, t) for s, t in outs],
            scratch_shapes=scratch + extra,
            compiler_params=pltpu.CompilerParams(vmem_limit_bytes=48 * 1024 * 1024),
        )(*args)

    amp, lo, hi, sums = call(
        first_kernel,
        [((nx,) + plane, F32), ((3,) + plane, i16), ((3,) + plane, i16), ((16, nz), F32)],
        concentration, damage, labels)
    from_lo = lax.ppermute(hi, "gx", ring("gx", 1))
    from_hi = lax.ppermute(lo, "gx", ring("gx", -1))
    sums = reduce_ahead(sums)
    (ypay,) = call(edge_rows_a, [((2, 32, nz), F32)], concentration, amp, from_lo, from_hi, sums)
    yr = both_sides(ypay, "gy")
    pad, apad, zpay = call(
        assemble_a(ride_y),
        [((nx + 4, rows, nz), F32), ((nx + 2, rows, nz), F32), ((nx + 2, rows, nz), F32)],
        concentration, amp, from_lo, from_hi, yr, sums)
    zr = z_neighbour(zpay, "gz")
    f2, a2, ae2, lo, hi, sums = heavy(
        step_a(ride_z),
        [((nx,) + plane, F32), ((nx + 2, rows, nz), F32), ((nx,) + plane, F32),
         ((2,) + plane, i16), ((2,) + plane, i16), ((16, nz), F32)],
        [], pad, apad, zr)

    from_lo = lax.ppermute(hi, "gx", ring("gx", 1))
    from_hi = lax.ppermute(lo, "gx", ring("gx", -1))
    sums = reduce_ahead(sums)
    (ypay,) = call(edge_rows_b, [((2, 32, nz), F32)], f2, from_lo, from_hi, sums)
    yr = both_sides(ypay, "gy")
    pad, zpay = call(
        assemble_b(ride_y),
        [((nx + 4, rows, nz), F32), ((nx + 2, rows, nz), F32)],
        f2, from_lo, from_hi, yr, sums)
    zr = z_neighbour(zpay, "gz")
    fraction, damage_field, flux_sum, pooled = heavy(
        step_b(ride_z),
        [((nx,) + plane, F32), ((nx,) + plane, F32), ((nx,) + plane, F32), ((ny // 4 + 4, nz), jnp.bfloat16)],
        [pltpu.VMEM((4,) + plane, F32)],
        pad, a2, ae2, zr, labels)
    crack_score = detector(pooled, w_first, b_first, w_second, b_second, w_third, b_third, ny // 4, nz // 4)
    return (fraction, damage_field, flux_sum, crack_score)


def extended(block, sides, width):
    for axis, dim in sides:
        count = lax.axis_size(axis)
        forward = [(i, i + 1) for i in range(count - 1)]
        backward = [(target, source) for source, target in forward]
        low = lax.ppermute(
            lax.slice_in_dim(block, block.shape[dim] - width, None, axis=dim), axis, forward)
        high = lax.ppermute(lax.slice_in_dim(block, 0, width, axis=dim), axis, backward)
        block = jnp.concatenate([low, block, high], axis=dim)
    return block


def apply_conv(padded, weight, bias_term):
    size_x = padded.shape[1] - 2
    size_y = padded.shape[2] - 2
    size_z = padded.shape[3] - 2
    pieces = []
    for i in range(3):
        for j in range(3):
            for l in range(3):
                pieces.append(padded[:, i:i + size_x, j:j + size_y, l:l + size_z])
    columns = jnp.stack(pieces)
    summed = jnp.einsum("koc,kcxyz->oxyz", weight, columns, preferred_element_type=F32)
    return summed + bias_term[:, None, None, None]


def detector(pooled, w_first, b_first, w_second, b_second, w_third, b_third, py, pz):
    maps = pooled[:py].reshape(py, pz, 4).transpose(2, 0, 1)[:, None]

    def slab_layer(activation, weight, bias_term):
        return apply_conv(extended(activation, (("gx", 1), ("gy", 2), ("gz", 3)), 1), weight, bias_term)

    maps = jax.nn.gelu(slab_layer(maps, w_first, b_first)).astype(jnp.bfloat16)
    maps = jax.nn.gelu(slab_layer(maps, w_second, b_second)).astype(jnp.bfloat16)
    return slab_layer(maps, w_third, b_third)[0]


def solution(mesh):
    slab = P(("groups", "gx"), "gy", "gz")
    return jax.shard_map(
        body,
        mesh=mesh,
        in_specs=(slab, slab, slab, P(), P(), P(), P(), P(), P()),
        out_specs=(slab, slab, slab, slab),
        check_vma=False,
    )
```

time: 325 us -> 147 us (0.45); the launches traced: 321 us -> 147 us
  blocking collectives: 73.6 us -> 0 us
  local copies, waits for them, and re-layouts: 58.2 us -> 12.9 us
  other arithmetic: 30 us -> 4.73 us
  waiting for transfers between devices: 97.6 us -> 72.4 us
  starting transfers between devices: 54.6 us -> 47.1 us
  Pallas kernels: 0 us -> 6.12 us
  between operations: 5.8 us -> 2.36 us
    psum x2 -> x0, blocking collectives: 73.6 us -> none  [stiff_mean(): lax.psum((jnp.sum(mobility * fraction), jnp.sum(mobility)), ('gx', 'gy',...]
    ppermute x0 -> x12, waiting for transfers between devices: none -> 27.7 us  [the longest x4 18.1 us: pair_sum(): s = s + lax.ppermute(s, axis, [(i, i ^ bit) for i in range(count)])]
    ppermute x21 -> x9, waiting for transfers between devices: 55.9 us -> 28.7 us  [extended(): lax.ppermute(lax.slice_in_dim(block, 0, width, axis=dim), axis, backward)]
    reduce_sum x12 -> x0, local copies, waits for them, and re-layouts: 26.2 us -> none  [pool_four(): field.reshape(size_x // 4, 4, size_y // 4, 4, size_z // 4, 4)]
    ppermute x21 -> x9, waiting for transfers between devices: 41.8 us -> 16 us  [extended(): lax.ppermute(lax.slice_in_dim(block, block.shape[dim] - width, None, axis...]
    reduce_sum x8 -> x0, other arithmetic: 19.6 us -> none  [the longest x6 15.6 us: pool_four(): field.reshape(size_x // 4, 4, size_y // 4, 4, size_z // 4, 4)]
    ppermute x21 -> x9, starting transfers between devices: 35.5 us -> 19.5 us  [extended(): lax.ppermute(lax.slice_in_dim(block, block.shape[dim] - width, None, axis...]
    ppermute x0 -> x12, starting transfers between devices: none -> 15.8 us  [the longest x2 5.59 us: body(): from_hi = lax.ppermute(lo, 'gx', ring('gx', -1))]
  transfers between devices with their start and end apart: 42 -> 30, of which waited for: 33 -> 23; matrix products, arithmetic and copies ran while one was open for 11% -> 1% of each run, Pallas kernels for 0% -> 0%
where the time goes in v1:
time: 147 us
  waiting for transfers between devices  72.4 us (49%)
  starting transfers between devices  47.1 us (32%)
  local copies, waits for them, and re-layouts  12.9 us (9%)
  Pallas kernels  6.12 us (4%)
  other arithmetic  4.73 us (3%)
  between operations  2.36 us (2%)
    ppermute x9, waiting for transfers between devices, extended(): lax.ppermute(lax.slice_in_dim(block, 0, width, axis=dim), axis, backward)  28.7 us
    ppermute x9, starting transfers between devices, extended(): lax.ppermute(lax.slice_in_dim(block, block.shape[dim] - width, None, axis...  19.5 us
    ppermute x4, waiting for transfers between devices, pair_sum(): s = s + lax.ppermute(s, axis, [(i, i ^ bit) for i in range(count)])  18.1 us
    ppermute x9, waiting for transfers between devices, extended(): lax.ppermute(lax.slice_in_dim(block, block.shape[dim] - width, None, axis...  16 us
    ppermute x9, starting transfers between devices, extended(): lax.ppermute(lax.slice_in_dim(block, 0, width, axis=dim), axis, backward)  11.8 us
    unnamed x72, local copies, waits for them, and re-layouts  7.23 us
    ppermute x2, starting transfers between devices, body(): from_hi = lax.ppermute(lo, 'gx', ring('gx', -1))  5.59 us
    pallas_call x2, Pallas kernels, heavy(): pl.pallas_call(kernel, out_shape=[jax.ShapeDtypeStruct(s, t) for s, t in...  5.39 us
  transfers between devices with their start and end apart: 30, of which 23 were waited for; matrix products, arithmetic and copies ran while one was open for 1% of the time, Pallas kernels for 0%

profile of v1, /device:TPU:0, one launch (start us, length us, event | category | flops | bytes accessed | tf_op | source)
XLA Modules:
  0.0 146.5 jit_solution(469426436147267248)
XLA Ops:
  4.0 3.1 %collective-permute-start = (s16[3,240,128]{2,1,0:T(8,128)(2,1)S(1)}, s16[3,240,128]{2,1,0:T(8,128)(2,1)S(1)}, u32[]{:S(2)}, u32[]{:S(2)}) collective-permute-start(s16[3,240,128]{2,1,0:T(8,128)(2,1)S(1)} %get-tuple-element.24), channel_id=1, source_target_pairs={{0,4},{4,8},{8,12},{12,0},{1,5},{5,9},{9,13},{13,1},{2,6},{6,10},{... | collective-permute-start | bytes 552968 | tf_op jit(solution)/shard_map/ppermute | solution.py:387
  7.1 2.1 %collective-permute-start.1 = (s16[3,240,128]{2,1,0:T(8,128)(2,1)S(1)}, s16[3,240,128]{2,1,0:T(8,128)(2,1)S(1)}, u32[]{:S(2)}, u32[]{:S(2)}) collective-permute-start(s16[3,240,128]{2,1,0:T(8,128)(2,1)S(1)} %get-tuple-element.25), channel_id=1, source_target_pairs={{0,12},{4,0},{8,4},{12,8},{1,13},{5,1},{9,5},{13,9},{2,14},{6,2},{... | collective-permute-start | bytes 552968 | tf_op jit(solution)/shard_map/ppermute | solution.py:388
  9.2 8.1 %collective-permute-done.2 = f32[16,128]{1,0:T(8,128)S(1)} collective-permute-done((f32[16,128]{1,0:T(8,128)S(1)}, f32[16,128]{1,0:T(8,128)S(1)}, u32[]{:S(2)}, u32[]{:S(2)}) %collective-permute-start.2) | collective-permute-done | bytes 8224 | tf_op jit(solution)/shard_map/ppermute | solution.py:336
  17.3 1.2 collective-permute-start.3
  18.5 3.4 %collective-permute-done.3 = f32[16,128]{1,0:T(8,128)S(1)} collective-permute-done((f32[16,128]{1,0:T(8,128)S(1)}, f32[16,128]{1,0:T(8,128)S(1)}, u32[]{:S(2)}, u32[]{:S(2)}) %collective-permute-start.3) | collective-permute-done | bytes 8224 | tf_op jit(solution)/shard_map/ppermute | solution.py:336
  21.9 1.6 %collective-permute-start.4 = (f32[2,32,128]{2,1,0:T(8,128)S(1)}, f32[2,32,128]{2,1,0:T(8,128)S(1)}, u32[]{:S(2)}, u32[]{:S(2)}) collective-permute-start(f32[2,32,128]{2,1,0:T(8,128)S(1)} %shard_map.121), channel_id=1, source_target_pairs={{0,2},{2,0},{1,3},{3,1},{4,6},{6,4},{5,7},{7,5},{8,10},{10,8},{9,1... | collective-permute-start | bytes 98312 | tf_op jit(solution)/shard_map/ppermute | solution.py:343
  23.5 2.4 %collective-permute-done.4.yr_ref = f32[2,32,128]{2,1,0:T(8,128)S(1)} collective-permute-done((f32[2,32,128]{2,1,0:T(8,128)S(1)}, f32[2,32,128]{2,1,0:T(8,128)S(1)}, u32[]{:S(2)}, u32[]{:S(2)}) %collective-permute-start.4) | collective-permute-done | bytes 32800 | tf_op jit(solution)/shard_map/ppermute | solution.py:343
  26.2 2.3 %collective-permute-done.5.zr_ref = f32[6,272,128]{2,1,0:T(8,128)S(1)} collective-permute-done((f32[6,272,128]{2,1,0:T(8,128)S(1)}, f32[6,272,128]{2,1,0:T(8,128)S(1)}, u32[]{:S(2)}, u32[]{:S(2)}) %collective-permute-start.5) | collective-permute-done | bytes 835616 | tf_op jit(solution)/shard_map/ppermute | solution.py:349
  28.6 2.1 %shard_map.123 = (f32[4,240,128]{2,1,0:T(8,128)S(1)}, f32[6,272,128]{2,1,0:T(8,128)S(1)}, f32[4,240,128]{2,1,0:T(8,128)S(1)}, s16[2,240,128]{2,1,0:T(8,128)(2,1)...) custom-call(f32[8,272,128]{2,1,0:T(8,128)S(1)} %get-tuple-element.27.pad_ref, ...), custom_call_target="tpu_custom_call" | custom-call | tf_op jit(solution)/shard_map/pallas_call | solution.py:376
  31.1 3.5 %collective-permute-start.7 = (s16[2,240,128]{2,1,0:T(8,128)(2,1)S(1)}, s16[2,240,128]{2,1,0:T(8,128)(2,1)S(1)}, u32[]{:S(2)}, u32[]{:S(2)}) collective-permute-start(s16[2,240,128]{2,1,0:T(8,128)(2,1)S(1)} %get-tuple-element.32), channel_id=1, source_target_pairs={{0,12},{4,0},{8,4},{12,8},{1,13},{5,1},{9,5},{13,9},{2,14},{6,2},{... | collective-permute-start | bytes 368648 | tf_op jit(solution)/shard_map/ppermute | solution.py:404
  34.6 4.4 %collective-permute-done.8 = f32[16,128]{1,0:T(8,128)S(1)} collective-permute-done((f32[16,128]{1,0:T(8,128)S(1)}, f32[16,128]{1,0:T(8,128)S(1)}, u32[]{:S(2)}, u32[]{:S(2)}) %collective-permute-start.8) | collective-permute-done | bytes 8224 | tf_op jit(solution)/shard_map/ppermute | solution.py:336
  39.0 2.3 %collective-permute-start.9 = (f32[16,128]{1,0:T(8,128)S(1)}, f32[16,128]{1,0:T(8,128)S(1)}, u32[]{:S(2)}, u32[]{:S(2)}) collective-permute-start(f32[16,128]{1,0:T(8,128)S(1)} %add.65), channel_id=1, source_target_pairs={{0,8},{4,12},{8,0},{12,4},{1,9},{5,13},{9,1},{13,5},{2,10},{6,14},... | collective-permute-start | bytes 24584 | tf_op jit(solution)/shard_map/ppermute | solution.py:336
  41.4 2.2 %collective-permute-done.9 = f32[16,128]{1,0:T(8,128)S(1)} collective-permute-done((f32[16,128]{1,0:T(8,128)S(1)}, f32[16,128]{1,0:T(8,128)S(1)}, u32[]{:S(2)}, u32[]{:S(2)}) %collective-permute-start.9) | collective-permute-done | bytes 8224 | tf_op jit(solution)/shard_map/ppermute | solution.py:336
  43.6 1.6 %collective-permute-start.10 = (f32[2,32,128]{2,1,0:T(8,128)S(1)}, f32[2,32,128]{2,1,0:T(8,128)S(1)}, u32[]{:S(2)}, u32[]{:S(2)}) collective-permute-start(f32[2,32,128]{2,1,0:T(8,128)S(1)} %shard_map.124), channel_id=1, source_target_pairs={{0,2},{2,0},{1,3},{3,1},{4,6},{6,4},{5,7},{7,5},{8,10},{10,8},{9,1... | collective-permute-start | bytes 98312 | tf_op jit(solution)/shard_map/ppermute | solution.py:343
  45.1 2.4 %collective-permute-done.10.yr_ref = f32[2,32,128]{2,1,0:T(8,128)S(1)} collective-permute-done((f32[2,32,128]{2,1,0:T(8,128)S(1)}, f32[2,32,128]{2,1,0:T(8,128)S(1)}, u32[]{:S(2)}, u32[]{:S(2)}) %collective-permute-start.10) | collective-permute-done | bytes 32800 | tf_op jit(solution)/shard_map/ppermute | solution.py:343
  47.8 2.3 %collective-permute-done.11.zr_ref = f32[6,272,128]{2,1,0:T(8,128)S(1)} collective-permute-done((f32[6,272,128]{2,1,0:T(8,128)S(1)}, f32[6,272,128]{2,1,0:T(8,128)S(1)}, u32[]{:S(2)}, u32[]{:S(2)}) %collective-permute-start.11) | collective-permute-done | bytes 835616 | tf_op jit(solution)/shard_map/ppermute | solution.py:349
  50.1 3.3 %shard_map.126 = (f32[4,240,128]{2,1,0:T(8,128)}, f32[4,240,128]{2,1,0:T(8,128)}, f32[4,240,128]{2,1,0:T(8,128)}, bf16[64,128]{1,0:T(8,128)(2,1)S(1)}) custom-call(f32[8,272,128]{2,1,0:T(8,128)S(1)} %get-tuple-element.34.pad_ref, f32[6,272,128]{2,1,0:T(8,128)S(1)} %get-tuple-element.35.a2_ref, f32[4,240,128]{2,1,0:T(8,128)S(1)} %get-tuple-element.36.ae2_ref, ...), custom_call_target="tpu_custom_call" | custom-call | tf_op jit(solution)/shard_map/pallas_call | solution.py:376
  53.5 2.7 %collective-permute-start.12 = (bf16[4,1,60,32]{2,0,3,1:T(4,128)(2,1)S(1)}, bf16[4,1,60,32]{2,0,3,1:T(4,128)(2,1)S(1)}, u32[]{:S(2)}, u32[]{:S(2)}) collective-permute-start(bf16[4,1,60,32]{2,0,3,1:T(4,128)(2,1)S(1)} %bitcast.347), channel_id=1, source_target_pairs={{0,4},{4,8},{8,12},{1,5},{5,9},{9,13},{2,6},{6,10},{10,14},{3,7},{... | collective-permute-start | bytes 46088 | tf_op jit(solution)/shard_map/ppermute | solution.py:427
  56.3 1.3 collective-permute-start.13
  57.9 4.3 %collective-permute-done.13 = bf16[4,1,60,32]{2,0,3,1:T(4,128)(2,1)S(1)} collective-permute-done((bf16[4,1,60,32]{2,0,3,1:T(4,128)(2,1)S(1)}, bf16[4,1,60,32]{2,0,3,1:T(4,128)(2,1)S(1)}, u32[]{:S(2)}, u32[]{:S(2)}) %collective-permute-start.13) | collective-permute-done | bytes 15392 | tf_op jit(solution)/shard_map/ppermute | solution.py:429
  62.4 3.4 %collective-permute-start.14 = (bf16[4,3,1,32]{2,0,3,1:T(4,128)(2,1)S(1)}, bf16[4,3,1,32]{2,0,3,1:T(4,128)(2,1)S(1)}, u32[]{:S(2)}, u32[]{:S(2)}) collective-permute-start(bf16[4,3,1,32]{2,0,3,1:T(4,128)(2,1)S(1)} %get-tuple-element.88), channel_id=1, source_target_pairs={{0,2},{1,3},{4,6},{5,7},{8,10},{9,11},{12,14},{13,15},{16,18},{17,... | collective-permute-start | bytes 2312 | tf_op jit(solution)/shard_map/ppermute | solution.py:427
  65.8 1.3 collective-permute-start.15
  68.0 4.3 %collective-permute-done.15 = bf16[4,3,1,32]{2,0,3,1:T(4,128)(2,1)S(1)} collective-permute-done((bf16[4,3,1,32]{2,0,3,1:T(4,128)(2,1)S(1)}, bf16[4,3,1,32]{2,0,3,1:T(4,128)(2,1)S(1)}, u32[]{:S(2)}, u32[]{:S(2)}) %collective-permute-start.15) | collective-permute-done | bytes 800 | tf_op jit(solution)/shard_map/ppermute | solution.py:429
  72.4 1.3 collective-permute-start.16
  73.7 1.3 collective-permute-start.17
  78.4 3.0 %stack.275 = bf16[27,4,1,60,32]{3,0,1,4,2:T(8,128)(2,1)S(1)} concatenate(bf16[1,4,1,60,32]{3,0,1,4,2:T(2,128)(2,1)S(1)} %copy.1177, bf16[1,4,1,60,32]{3,0,1,4,2:T(2,128)(2,1)S(1)} %copy.1178, bf16[1,4,1,60,32]{3,0,1,4,2:T(2,128)(2,1)S(1)} %copy.1179, bf16[1,4,1,60,32]{3,0,1,4,2:T(2,128)(2,1)S(1)} %copy.1180, bf16[1,4,1,60,32]{3,0,1,4,2:T(2,128)(2,1)S(1)} %copy.1181, ...), dimensions={0} | concatenate | bytes 829440 | tf_op jit(solution)/shard_map/stack | solution.py:443
  81.8 3.9 %collective-permute-start.18 = (bf16[16,1,60,32]{2,0,3,1:T(8,128)(2,1)S(1)}, bf16[16,1,60,32]{2,0,3,1:T(8,128)(2,1)S(1)}, u32[]{:S(2)}, u32[]{:S(2)}) collective-permute-start(bf16[16,1,60,32]{2,0,3,1:T(8,128)(2,1)S(1)} %bitcast.341), channel_id=1, source_target_pairs={{0,4},{4,8},{8,12},{1,5},{5,9},{9,13},{2,6},{6,10},{10,14},{3,7},{... | collective-permute-start | bytes 184328 | tf_op jit(solution)/shard_map/ppermute | solution.py:427
  85.7 1.3 collective-permute-start.19
  87.0 1.8 %collective-permute-done.18 = bf16[16,1,60,32]{2,0,3,1:T(8,128)(2,1)S(1)} collective-permute-done((bf16[16,1,60,32]{2,0,3,1:T(8,128)(2,1)S(1)}, bf16[16,1,60,32]{2,0,3,1:T(8,128)(2,1)S(1)}, u32[]{:S(2)}, u32[]{:S(2)}) %collective-permute-start.18) | collective-permute-done | bytes 61472 | tf_op jit(solution)/shard_map/ppermute | solution.py:427
  88.8 4.1 %collective-permute-done.19 = bf16[16,1,60,32]{2,0,3,1:T(8,128)(2,1)S(1)} collective-permute-done((bf16[16,1,60,32]{2,0,3,1:T(8,128)(2,1)S(1)}, bf16[16,1,60,32]{2,0,3,1:T(8,128)(2,1)S(1)}, u32[]{:S(2)}, u32[]{:S(2)}) %collective-permute-start.19) | collective-permute-done | bytes 61472 | tf_op jit(solution)/shard_map/ppermute | solution.py:429
  93.2 1.6 %collective-permute-start.20 = (bf16[16,3,1,32]{2,0,3,1:T(8,128)(2,1)S(1)}, bf16[16,3,1,32]{2,0,3,1:T(8,128)(2,1)S(1)}, u32[]{:S(2)}, u32[]{:S(2)}) collective-permute-start(bf16[16,3,1,32]{2,0,3,1:T(8,128)(2,1)S(1)} %get-tuple-element.56), channel_id=1, source_target_pairs={{0,2},{1,3},{4,6},{5,7},{8,10},{9,11},{12,14},{13,15},{16,18},{17,... | collective-permute-start | bytes 9224 | tf_op jit(solution)/shard_map/ppermute | solution.py:427
  94.7 1.5 %collective-permute-start.21 = (bf16[16,3,1,32]{2,0,3,1:T(8,128)(2,1)S(1)}, bf16[16,3,1,32]{2,0,3,1:T(8,128)(2,1)S(1)}, u32[]{:S(2)}, u32[]{:S(2)}) collective-permute-start(bf16[16,3,1,32]{2,0,3,1:T(8,128)(2,1)S(1)} %get-tuple-element.57), channel_id=1, source_target_pairs={{2,0},{3,1},{6,4},{7,5},{10,8},{11,9},{14,12},{15,13},{18,16},{19,... | collective-permute-start | bytes 9224 | tf_op jit(solution)/shard_map/ppermute | solution.py:429
  96.4 5.9 %collective-permute-done.20 = bf16[16,3,1,32]{2,0,3,1:T(8,128)(2,1)S(1)} collective-permute-done((bf16[16,3,1,32]{2,0,3,1:T(8,128)(2,1)S(1)}, bf16[16,3,1,32]{2,0,3,1:T(8,128)(2,1)S(1)}, u32[]{:S(2)}, u32[]{:S(2)}) %collective-permute-start.20) | collective-permute-done | bytes 3104 | tf_op jit(solution)/shard_map/ppermute | solution.py:427
  102.3 4.1 %collective-permute-done.21 = bf16[16,3,1,32]{2,0,3,1:T(8,128)(2,1)S(1)} collective-permute-done((bf16[16,3,1,32]{2,0,3,1:T(8,128)(2,1)S(1)}, bf16[16,3,1,32]{2,0,3,1:T(8,128)(2,1)S(1)}, u32[]{:S(2)}, u32[]{:S(2)}) %collective-permute-start.21) | collective-permute-done | bytes 3104 | tf_op jit(solution)/shard_map/ppermute | solution.py:429
  106.5 1.3 collective-permute-start.22
  107.8 1.3 collective-permute-start.23
  109.6 1.3 collective-permute-done.23
  114.4 2.5 %collective-permute-start.24 = (bf16[16,1,60,32]{2,0,3,1:T(8,128)(2,1)S(1)}, bf16[16,1,60,32]{2,0,3,1:T(8,128)(2,1)S(1)}, u32[]{:S(2)}, u32[]{:S(2)}) collective-permute-start(bf16[16,1,60,32]{2,0,3,1:T(8,128)(2,1)S(1)} %bitcast.335), channel_id=1, source_target_pairs={{0,4},{4,8},{8,12},{1,5},{5,9},{9,13},{2,6},{6,10},{10,14},{3,7},{... | collective-permute-start | bytes 184328 | tf_op jit(solution)/shard_map/ppermute | solution.py:427
  116.9 1.3 collective-permute-start.25
  118.2 1.8 %collective-permute-done.24 = bf16[16,1,60,32]{2,0,3,1:T(8,128)(2,1)S(1)} collective-permute-done((bf16[16,1,60,32]{2,0,3,1:T(8,128)(2,1)S(1)}, bf16[16,1,60,32]{2,0,3,1:T(8,128)(2,1)S(1)}, u32[]{:S(2)}, u32[]{:S(2)}) %collective-permute-start.24) | collective-permute-done | bytes 61472 | tf_op jit(solution)/shard_map/ppermute | solution.py:427
  120.0 4.1 %collective-permute-done.25 = bf16[16,1,60,32]{2,0,3,1:T(8,128)(2,1)S(1)} collective-permute-done((bf16[16,1,60,32]{2,0,3,1:T(8,128)(2,1)S(1)}, bf16[16,1,60,32]{2,0,3,1:T(8,128)(2,1)S(1)}, u32[]{:S(2)}, u32[]{:S(2)}) %collective-permute-start.25) | collective-permute-done | bytes 61472 | tf_op jit(solution)/shard_map/ppermute | solution.py:429
  124.4 1.5 %collective-permute-start.26 = (bf16[16,3,1,32]{2,0,3,1:T(8,128)(2,1)S(1)}, bf16[16,3,1,32]{2,0,3,1:T(8,128)(2,1)S(1)}, u32[]{:S(2)}, u32[]{:S(2)}) collective-permute-start(bf16[16,3,1,32]{2,0,3,1:T(8,128)(2,1)S(1)} %get-tuple-element.52), channel_id=1, source_target_pairs={{0,2},{1,3},{4,6},{5,7},{8,10},{9,11},{12,14},{13,15},{16,18},{17,... | collective-permute-start | bytes 9224 | tf_op jit(solution)/shard_map/ppermute | solution.py:427
  125.9 1.3 collective-permute-start.27
  127.9 5.6 %collective-permute-done.26 = bf16[16,3,1,32]{2,0,3,1:T(8,128)(2,1)S(1)} collective-permute-done((bf16[16,3,1,32]{2,0,3,1:T(8,128)(2,1)S(1)}, bf16[16,3,1,32]{2,0,3,1:T(8,128)(2,1)S(1)}, u32[]{:S(2)}, u32[]{:S(2)}) %collective-permute-start.26) | collective-permute-done | bytes 3104 | tf_op jit(solution)/shard_map/ppermute | solution.py:427
  133.5 4.1 %collective-permute-done.27 = bf16[16,3,1,32]{2,0,3,1:T(8,128)(2,1)S(1)} collective-permute-done((bf16[16,3,1,32]{2,0,3,1:T(8,128)(2,1)S(1)}, bf16[16,3,1,32]{2,0,3,1:T(8,128)(2,1)S(1)}, u32[]{:S(2)}, u32[]{:S(2)}) %collective-permute-start.27) | collective-permute-done | bytes 3104 | tf_op jit(solution)/shard_map/ppermute | solution.py:429
  137.7 1.3 collective-permute-start.28
  139.0 1.3 collective-permute-start.29
  140.8 1.3 collective-permute-done.29
  (148 shorter events, 18.8 us)
Async XLA Ops:
  0.6 1.0 copy-start
  1.7 1.0 copy-start.1
  2.7 1.0 copy-start.3
  4.0 17.9 %collective-permute-start = (s16[3,240,128]{2,1,0:T(8,128)(2,1)S(1)}, s16[3,240,128]{2,1,0:T(8,128)(2,1)S(1)}, u32[]{:S(2)}, u32[]{:S(2)}) collective-permute-start(s16[3,240,128]{2,1,0:T(8,128)(2,1)S(1)} %get-tuple-element.24), channel_id=1, source_target_pairs={{0,4},{4,8},{8,12},{12,0},{1,5},{5,9},{9,13},{13,1},{2,6},{6,10},{... | collective-permute-start | bytes 552968 | tf_op jit(solution)/shard_map/ppermute | solution.py:387
  7.1 14.8 %collective-permute-start.1 = (s16[3,240,128]{2,1,0:T(8,128)(2,1)S(1)}, s16[3,240,128]{2,1,0:T(8,128)(2,1)S(1)}, u32[]{:S(2)}, u32[]{:S(2)}) collective-permute-start(s16[3,240,128]{2,1,0:T(8,128)(2,1)S(1)} %get-tuple-element.25), channel_id=1, source_target_pairs={{0,12},{4,0},{8,4},{12,8},{1,13},{5,1},{9,5},{13,9},{2,14},{6,2},{... | collective-permute-start | bytes 552968 | tf_op jit(solution)/shard_map/ppermute | solution.py:388
  9.2 8.1 %collective-permute-start.2 = (f32[16,128]{1,0:T(8,128)S(1)}, f32[16,128]{1,0:T(8,128)S(1)}, u32[]{:S(2)}, u32[]{:S(2)}) collective-permute-start(f32[16,128]{1,0:T(8,128)S(1)} %get-tuple-element.26), channel_id=1, source_target_pairs={{0,4},{4,0},{8,12},{12,8},{1,5},{5,1},{9,13},{13,9},{2,6},{6,2},{1... | collective-permute-start | bytes 24584 | tf_op jit(solution)/shard_map/ppermute | solution.py:336
  17.3 4.5 %collective-permute-start.3 = (f32[16,128]{1,0:T(8,128)S(1)}, f32[16,128]{1,0:T(8,128)S(1)}, u32[]{:S(2)}, u32[]{:S(2)}) collective-permute-start(f32[16,128]{1,0:T(8,128)S(1)} %add.63), channel_id=1, source_target_pairs={{0,8},{4,12},{8,0},{12,4},{1,9},{5,13},{9,1},{13,5},{2,10},{6,14},... | collective-permute-start | bytes 24584 | tf_op jit(solution)/shard_map/ppermute | solution.py:336
  21.9 28.2 %copy-start.2 = (s32[4,240,128]{2,1,0:T(8,128)S(1)}, s32[4,240,128]{2,1,0:T(8,128)}, u32[]{:S(2)}) copy-start(s32[4,240,128]{2,1,0:T(8,128)} %l_ref.3) | copy-start | bytes 1474564
  21.9 4.0 %collective-permute-start.4 = (f32[2,32,128]{2,1,0:T(8,128)S(1)}, f32[2,32,128]{2,1,0:T(8,128)S(1)}, u32[]{:S(2)}, u32[]{:S(2)}) collective-permute-start(f32[2,32,128]{2,1,0:T(8,128)S(1)} %shard_map.121), channel_id=1, source_target_pairs={{0,2},{2,0},{1,3},{3,1},{4,6},{6,4},{5,7},{7,5},{8,10},{10,8},{9,1... | collective-permute-start | bytes 98312 | tf_op jit(solution)/shard_map/ppermute | solution.py:343
  26.2 2.4 %collective-permute-start.5 = (f32[6,272,128]{2,1,0:T(8,128)S(1)}, f32[6,272,128]{2,1,0:T(8,128)S(1)}, u32[]{:S(2)}, u32[]{:S(2)}) collective-permute-start(f32[6,272,128]{2,1,0:T(8,128)S(1)} %get-tuple-element.29), channel_id=1, source_target_pairs={{0,1},{1,0},{2,3},{3,2},{4,5},{5,4},{6,7},{7,6},{8,9},{9,8},{10,11... | collective-permute-start | bytes 2506760 | tf_op jit(solution)/shard_map/ppermute | solution.py:349
  30.7 12.9 %collective-permute-start.6 = (s16[2,240,128]{2,1,0:T(8,128)(2,1)S(1)}, s16[2,240,128]{2,1,0:T(8,128)(2,1)S(1)}, u32[]{:S(2)}, u32[]{:S(2)}) collective-permute-start(s16[2,240,128]{2,1,0:T(8,128)(2,1)S(1)} %get-tuple-element.31), channel_id=1, source_target_pairs={{0,4},{4,8},{8,12},{12,0},{1,5},{5,9},{9,13},{13,1},{2,6},{6,10},{... | collective-permute-start | bytes 368648 | tf_op jit(solution)/shard_map/ppermute | solution.py:403
  31.1 12.5 %collective-permute-start.7 = (s16[2,240,128]{2,1,0:T(8,128)(2,1)S(1)}, s16[2,240,128]{2,1,0:T(8,128)(2,1)S(1)}, u32[]{:S(2)}, u32[]{:S(2)}) collective-permute-start(s16[2,240,128]{2,1,0:T(8,128)(2,1)S(1)} %get-tuple-element.32), channel_id=1, source_target_pairs={{0,12},{4,0},{8,4},{12,8},{1,13},{5,1},{9,5},{13,9},{2,14},{6,2},{... | collective-permute-start | bytes 368648 | tf_op jit(solution)/shard_map/ppermute | solution.py:404
  34.6 4.4 %collective-permute-start.8 = (f32[16,128]{1,0:T(8,128)S(1)}, f32[16,128]{1,0:T(8,128)S(1)}, u32[]{:S(2)}, u32[]{:S(2)}) collective-permute-start(f32[16,128]{1,0:T(8,128)S(1)} %get-tuple-element.33), channel_id=1, source_target_pairs={{0,4},{4,0},{8,12},{12,8},{1,5},{5,1},{9,13},{13,9},{2,6},{6,2},{1... | collective-permute-start | bytes 24584 | tf_op jit(solution)/shard_map/ppermute | solution.py:336
  39.0 4.5 %collective-permute-start.9 = (f32[16,128]{1,0:T(8,128)S(1)}, f32[16,128]{1,0:T(8,128)S(1)}, u32[]{:S(2)}, u32[]{:S(2)}) collective-permute-start(f32[16,128]{1,0:T(8,128)S(1)} %add.65), channel_id=1, source_target_pairs={{0,8},{4,12},{8,0},{12,4},{1,9},{5,13},{9,1},{13,5},{2,10},{6,14},... | collective-permute-start | bytes 24584 | tf_op jit(solution)/shard_map/ppermute | solution.py:336
  43.6 4.0 %collective-permute-start.10 = (f32[2,32,128]{2,1,0:T(8,128)S(1)}, f32[2,32,128]{2,1,0:T(8,128)S(1)}, u32[]{:S(2)}, u32[]{:S(2)}) collective-permute-start(f32[2,32,128]{2,1,0:T(8,128)S(1)} %shard_map.124), channel_id=1, source_target_pairs={{0,2},{2,0},{1,3},{3,1},{4,6},{6,4},{5,7},{7,5},{8,10},{10,8},{9,1... | collective-permute-start | bytes 98312 | tf_op jit(solution)/shard_map/ppermute | solution.py:343
  47.7 2.4 %collective-permute-start.11 = (f32[6,272,128]{2,1,0:T(8,128)S(1)}, f32[6,272,128]{2,1,0:T(8,128)S(1)}, u32[]{:S(2)}, u32[]{:S(2)}) collective-permute-start(f32[6,272,128]{2,1,0:T(8,128)S(1)} %get-tuple-element.37), channel_id=1, source_target_pairs={{0,1},{1,0},{2,3},{3,2},{4,5},{5,4},{6,7},{7,6},{8,9},{9,8},{10,11... | collective-permute-start | bytes 2506760 | tf_op jit(solution)/shard_map/ppermute | solution.py:349
  53.5 4.3 %collective-permute-start.12 = (bf16[4,1,60,32]{2,0,3,1:T(4,128)(2,1)S(1)}, bf16[4,1,60,32]{2,0,3,1:T(4,128)(2,1)S(1)}, u32[]{:S(2)}, u32[]{:S(2)}) collective-permute-start(bf16[4,1,60,32]{2,0,3,1:T(4,128)(2,1)S(1)} %bitcast.347), channel_id=1, source_target_pairs={{0,4},{4,8},{8,12},{1,5},{5,9},{9,13},{2,6},{6,10},{10,14},{3,7},{... | collective-permute-start | bytes 46088 | tf_op jit(solution)/shard_map/ppermute | solution.py:427
  56.3 5.9 %collective-permute-start.13 = (bf16[4,1,60,32]{2,0,3,1:T(4,128)(2,1)S(1)}, bf16[4,1,60,32]{2,0,3,1:T(4,128)(2,1)S(1)}, u32[]{:S(2)}, u32[]{:S(2)}) collective-permute-start(bf16[4,1,60,32]{2,0,3,1:T(4,128)(2,1)S(1)} %bitcast.348), channel_id=1, source_target_pairs={{4,0},{8,4},{12,8},{5,1},{9,5},{13,9},{6,2},{10,6},{14,10},{7,3},{... | collective-permute-start | bytes 46088 | tf_op jit(solution)/shard_map/ppermute | solution.py:429
  62.4 5.6 %collective-permute-start.14 = (bf16[4,3,1,32]{2,0,3,1:T(4,128)(2,1)S(1)}, bf16[4,3,1,32]{2,0,3,1:T(4,128)(2,1)S(1)}, u32[]{:S(2)}, u32[]{:S(2)}) collective-permute-start(bf16[4,3,1,32]{2,0,3,1:T(4,128)(2,1)S(1)} %get-tuple-element.88), channel_id=1, source_target_pairs={{0,2},{1,3},{4,6},{5,7},{8,10},{9,11},{12,14},{13,15},{16,18},{17,... | collective-permute-start | bytes 2312 | tf_op jit(solution)/shard_map/ppermute | solution.py:427
  65.8 6.5 %collective-permute-start.15 = (bf16[4,3,1,32]{2,0,3,1:T(4,128)(2,1)S(1)}, bf16[4,3,1,32]{2,0,3,1:T(4,128)(2,1)S(1)}, u32[]{:S(2)}, u32[]{:S(2)}) collective-permute-start(bf16[4,3,1,32]{2,0,3,1:T(4,128)(2,1)S(1)} %get-tuple-element.89), channel_id=1, source_target_pairs={{2,0},{3,1},{6,4},{7,5},{10,8},{11,9},{14,12},{15,13},{18,16},{19,... | collective-permute-start | bytes 2312 | tf_op jit(solution)/shard_map/ppermute | solution.py:429
  72.4 3.4 %collective-permute-start.16 = (bf16[4,3,62,1]{2,0,3,1:T(4,128)(2,1)S(1)}, bf16[4,3,62,1]{2,0,3,1:T(4,128)(2,1)S(1)}, u32[]{:S(2)}, u32[]{:S(2)}) collective-permute-start(bf16[4,3,62,1]{2,0,3,1:T(4,128)(2,1)S(1)} %get-tuple-element.61), channel_id=1, source_target_pairs={{0,1},{2,3},{4,5},{6,7},{8,9},{10,11},{12,13},{14,15},{16,17},{18,... | collective-permute-start | bytes 4472 | tf_op jit(solution)/shard_map/ppermute | solution.py:427
  73.7 3.1 %collective-permute-start.17 = (bf16[4,3,62,1]{2,0,3,1:T(4,128)(2,1)S(1)}, bf16[4,3,62,1]{2,0,3,1:T(4,128)(2,1)S(1)}, u32[]{:S(2)}, u32[]{:S(2)}) collective-permute-start(bf16[4,3,62,1]{2,0,3,1:T(4,128)(2,1)S(1)} %get-tuple-element.60), channel_id=1, source_target_pairs={{1,0},{3,2},{5,4},{7,6},{9,8},{11,10},{13,12},{15,14},{17,16},{19,... | collective-permute-start | bytes 4472 | tf_op jit(solution)/shard_map/ppermute | solution.py:429
  75.4 6.1 %copy-start.6 = (bf16[27,16,4]{0,2,1:T(4,128)(2,1)S(1)}, bf16[27,16,4]{0,2,1:T(4,128)(2,1)}, u32[]{:S(2)}) copy-start(bf16[27,16,4]{0,2,1:T(4,128)(2,1)} %param.12) | copy-start | bytes 10372
  75.4 6.1 %copy-start.7 = (f32[16]{0:T(128)S(1)}, f32[16]{0:T(128)}, u32[]{:S(2)}) copy-start(f32[16]{0:T(128)} %param.13) | copy-start | bytes 196
  78.2 18.0 %copy-start.4 = (bf16[27,16,16]{0,2,1:T(8,128)(2,1)S(1)}, bf16[27,16,16]{0,2,1:T(8,128)(2,1)}, u32[]{:S(2)}) copy-start(bf16[27,16,16]{0,2,1:T(8,128)(2,1)} %param.14) | copy-start | bytes 41476
  81.8 7.0 %collective-permute-start.18 = (bf16[16,1,60,32]{2,0,3,1:T(8,128)(2,1)S(1)}, bf16[16,1,60,32]{2,0,3,1:T(8,128)(2,1)S(1)}, u32[]{:S(2)}, u32[]{:S(2)}) collective-permute-start(bf16[16,1,60,32]{2,0,3,1:T(8,128)(2,1)S(1)} %bitcast.341), channel_id=1, source_target_pairs={{0,4},{4,8},{8,12},{1,5},{5,9},{9,13},{2,6},{6,10},{10,14},{3,7},{... | collective-permute-start | bytes 184328 | tf_op jit(solution)/shard_map/ppermute | solution.py:427
  85.7 7.2 %collective-permute-start.19 = (bf16[16,1,60,32]{2,0,3,1:T(8,128)(2,1)S(1)}, bf16[16,1,60,32]{2,0,3,1:T(8,128)(2,1)S(1)}, u32[]{:S(2)}, u32[]{:S(2)}) collective-permute-start(bf16[16,1,60,32]{2,0,3,1:T(8,128)(2,1)S(1)} %bitcast.342), channel_id=1, source_target_pairs={{4,0},{8,4},{12,8},{5,1},{9,5},{13,9},{6,2},{10,6},{14,10},{7,3},{... | collective-permute-start | bytes 184328 | tf_op jit(solution)/shard_map/ppermute | solution.py:429
  93.2 9.1 %collective-permute-start.20 = (bf16[16,3,1,32]{2,0,3,1:T(8,128)(2,1)S(1)}, bf16[16,3,1,32]{2,0,3,1:T(8,128)(2,1)S(1)}, u32[]{:S(2)}, u32[]{:S(2)}) collective-permute-start(bf16[16,3,1,32]{2,0,3,1:T(8,128)(2,1)S(1)} %get-tuple-element.56), channel_id=1, source_target_pairs={{0,2},{1,3},{4,6},{5,7},{8,10},{9,11},{12,14},{13,15},{16,18},{17,... | collective-permute-start | bytes 9224 | tf_op jit(solution)/shard_map/ppermute | solution.py:427
  94.7 11.7 %collective-permute-start.21 = (bf16[16,3,1,32]{2,0,3,1:T(8,128)(2,1)S(1)}, bf16[16,3,1,32]{2,0,3,1:T(8,128)(2,1)S(1)}, u32[]{:S(2)}, u32[]{:S(2)}) collective-permute-start(bf16[16,3,1,32]{2,0,3,1:T(8,128)(2,1)S(1)} %get-tuple-element.57), channel_id=1, source_target_pairs={{2,0},{3,1},{6,4},{7,5},{10,8},{11,9},{14,12},{15,13},{18,16},{19,... | collective-permute-start | bytes 9224 | tf_op jit(solution)/shard_map/ppermute | solution.py:429
  106.5 3.0 %collective-permute-start.22 = (bf16[16,3,62,1]{2,0,3,1:T(8,128)(2,1)S(1)}, bf16[16,3,62,1]{2,0,3,1:T(8,128)(2,1)S(1)}, u32[]{:S(2)}, u32[]{:S(2)}) collective-permute-start(bf16[16,3,62,1]{2,0,3,1:T(8,128)(2,1)S(1)} %get-tuple-element.49), channel_id=1, source_target_pairs={{0,1},{2,3},{4,5},{6,7},{8,9},{10,11},{12,13},{14,15},{16,17},{18,... | collective-permute-start | bytes 17864 | tf_op jit(solution)/shard_map/ppermute | solution.py:427
  107.8 3.1 %collective-permute-start.23 = (bf16[16,3,62,1]{2,0,3,1:T(8,128)(2,1)S(1)}, bf16[16,3,62,1]{2,0,3,1:T(8,128)(2,1)S(1)}, u32[]{:S(2)}, u32[]{:S(2)}) collective-permute-start(bf16[16,3,62,1]{2,0,3,1:T(8,128)(2,1)S(1)} %get-tuple-element.48), channel_id=1, source_target_pairs={{1,0},{3,2},{5,4},{7,6},{9,8},{11,10},{13,12},{15,14},{17,16},{19,... | collective-permute-start | bytes 17864 | tf_op jit(solution)/shard_map/ppermute | solution.py:429
  111.5 2.3 %copy-start.8 = (f32[16]{0:T(128)S(1)}, f32[16]{0:T(128)}, u32[]{:S(2)}) copy-start(f32[16]{0:T(128)} %param.15) | copy-start | bytes 196
  113.7 13.4 %copy-start.5 = (bf16[27,1,16]{0,2,1:T(8,128)(2,1)S(1)}, bf16[27,1,16]{0,2,1:T(8,128)(2,1)}, u32[]{:S(2)}) copy-start(bf16[27,1,16]{0,2,1:T(8,128)(2,1)} %param.16) | copy-start | bytes 2596
  114.4 5.6 %collective-permute-start.24 = (bf16[16,1,60,32]{2,0,3,1:T(8,128)(2,1)S(1)}, bf16[16,1,60,32]{2,0,3,1:T(8,128)(2,1)S(1)}, u32[]{:S(2)}, u32[]{:S(2)}) collective-permute-start(bf16[16,1,60,32]{2,0,3,1:T(8,128)(2,1)S(1)} %bitcast.335), channel_id=1, source_target_pairs={{0,4},{4,8},{8,12},{1,5},{5,9},{9,13},{2,6},{6,10},{10,14},{3,7},{... | collective-permute-start | bytes 184328 | tf_op jit(solution)/shard_map/ppermute | solution.py:427
  116.9 7.2 %collective-permute-start.25 = (bf16[16,1,60,32]{2,0,3,1:T(8,128)(2,1)S(1)}, bf16[16,1,60,32]{2,0,3,1:T(8,128)(2,1)S(1)}, u32[]{:S(2)}, u32[]{:S(2)}) collective-permute-start(bf16[16,1,60,32]{2,0,3,1:T(8,128)(2,1)S(1)} %bitcast.336), channel_id=1, source_target_pairs={{4,0},{8,4},{12,8},{5,1},{9,5},{13,9},{6,2},{10,6},{14,10},{7,3},{... | collective-permute-start | bytes 184328 | tf_op jit(solution)/shard_map/ppermute | solution.py:429
  124.4 9.1 %collective-permute-start.26 = (bf16[16,3,1,32]{2,0,3,1:T(8,128)(2,1)S(1)}, bf16[16,3,1,32]{2,0,3,1:T(8,128)(2,1)S(1)}, u32[]{:S(2)}, u32[]{:S(2)}) collective-permute-start(bf16[16,3,1,32]{2,0,3,1:T(8,128)(2,1)S(1)} %get-tuple-element.52), channel_id=1, source_target_pairs={{0,2},{1,3},{4,6},{5,7},{8,10},{9,11},{12,14},{13,15},{16,18},{17,... | collective-permute-start | bytes 9224 | tf_op jit(solution)/shard_map/ppermute | solution.py:427
  125.9 11.8 %collective-permute-start.27 = (bf16[16,3,1,32]{2,0,3,1:T(8,128)(2,1)S(1)}, bf16[16,3,1,32]{2,0,3,1:T(8,128)(2,1)S(1)}, u32[]{:S(2)}, u32[]{:S(2)}) collective-permute-start(bf16[16,3,1,32]{2,0,3,1:T(8,128)(2,1)S(1)} %get-tuple-element.53), channel_id=1, source_target_pairs={{2,0},{3,1},{6,4},{7,5},{10,8},{11,9},{14,12},{15,13},{18,16},{19,... | collective-permute-start | bytes 9224 | tf_op jit(solution)/shard_map/ppermute | solution.py:429
  137.7 3.0 %collective-permute-start.28 = (bf16[16,3,62,1]{2,0,3,1:T(8,128)(2,1)S(1)}, bf16[16,3,62,1]{2,0,3,1:T(8,128)(2,1)S(1)}, u32[]{:S(2)}, u32[]{:S(2)}) collective-permute-start(bf16[16,3,62,1]{2,0,3,1:T(8,128)(2,1)S(1)} %get-tuple-element.45), channel_id=1, source_target_pairs={{0,1},{2,3},{4,5},{6,7},{8,9},{10,11},{12,13},{14,15},{16,17},{18,... | collective-permute-start | bytes 17864 | tf_op jit(solution)/shard_map/ppermute | solution.py:427
  139.0 3.1 %collective-permute-start.29 = (bf16[16,3,62,1]{2,0,3,1:T(8,128)(2,1)S(1)}, bf16[16,3,62,1]{2,0,3,1:T(8,128)(2,1)S(1)}, u32[]{:S(2)}, u32[]{:S(2)}) collective-permute-start(bf16[16,3,62,1]{2,0,3,1:T(8,128)(2,1)S(1)} %get-tuple-element.44), channel_id=1, source_target_pairs={{1,0},{3,2},{5,4},{7,6},{9,8},{11,10},{13,12},{15,14},{17,16},{19,... | collective-permute-start | bytes 17864 | tf_op jit(solution)/shard_map/ppermute | solution.py:429

commit v2 on v1

--- a/solution.py
+++ b/solution.py
@@ -275,7 +275,7 @@
 
 
 def step_b(add):
-    def kernel(pad_ref, a2_ref, ae2_ref, zr_ref, l_ref, f3_ref, dmg_ref, flux_ref, pool_ref,
+    def kernel(pad_ref, a2_ref, ae2_ref, zr_ref, l_ref, f3_ref, dmg_ref, flux_ref, pool_ref, edge_ref,
                mob_ref, mobe_ref, chem_ref, cheme_ref, pool_scr):
         nx, ny, nz = f3_ref.shape
         g = Geometry(nx, ny, nz)
@@ -318,7 +318,10 @@
                     + pool_scr[i, pl.ds(2, py, stride=4), :] + pool_scr[i, pl.ds(3, py, stride=4), :])
             pick = jnp.where((zin // 4 == out // 4) & (out % 4 == i), 1.0 / 64.0, 0.0).astype(F32)
             total = total + jnp.dot(rows, pick, precision=lax.Precision.HIGHEST, preferred_element_type=F32)
-        pool_ref[0:py, :] = total.astype(jnp.bfloat16)
+        pool_ref[...] = total.astype(BF16)
+        blank = jnp.zeros((13, 4 * pz), F32)
+        edge_ref[0] = jnp.concatenate([total[0:3], blank]).astype(BF16)
+        edge_ref[1] = jnp.concatenate([total[py - 3:py], blank]).astype(BF16)
     return kernel
 
 
@@ -344,14 +347,14 @@
     return jnp.stack([lax.ppermute(pay[0], axis, ring(axis, -1)), lax.ppermute(pay[1], axis, ring(axis, 1))])
 
 
-def z_neighbour(pay, axis):
+def z_neighbour(pay, axis, packed=True):
     if lax.axis_size(axis) == 2:
         return lax.ppermute(pay, axis, ring(axis, 1))
     above = lax.ppermute(pay, axis, ring(axis, -1))
     below = lax.ppermute(pay, axis, ring(axis, 1))
     lane = lax.broadcasted_iota(jnp.int32, pay.shape, pay.ndim - 1)
-    quarter = pay.shape[-1] // 4
-    return jnp.where((lane < quarter) | ((lane >= 2 * quarter) & (lane < 3 * quarter)), above, below)
+    part = pay.shape[-1] // (4 if packed else 2)
+    return jnp.where(lane // part % 2 == 0, above, below)
 
 
 def reduce_ahead(s):
@@ -410,50 +413,222 @@
         [((nx + 4, rows, nz), F32), ((nx + 2, rows, nz), F32)],
         f2, from_lo, from_hi, yr, sums)
     zr = z_neighbour(zpay, "gz")
-    fraction, damage_field, flux_sum, pooled = heavy(
+    fraction, damage_field, flux_sum, pooled, edge = heavy(
         step_b(ride_z),
-        [((nx,) + plane, F32), ((nx,) + plane, F32), ((nx,) + plane, F32), ((ny // 4 + 4, nz), jnp.bfloat16)],
+        [((nx,) + plane, F32), ((nx,) + plane, F32), ((nx,) + plane, F32), ((ny // 4, nz), BF16), ((2, 16, nz), BF16)],
         [pltpu.VMEM((4,) + plane, F32)],
         pad, a2, ae2, zr, labels)
-    crack_score = detector(pooled, w_first, b_first, w_second, b_second, w_third, b_third, ny // 4, nz // 4)
+    ids = jnp.stack([lax.axis_index(a) for a in ("gx", "gy", "gz")])
+    crack_score = detector(pooled, edge, ids, w_first, b_first, w_second, b_second, w_third, b_third, ny // 4, nz // 4)
     return (fraction, damage_field, flux_sum, crack_score)
 
 
-def extended(block, sides, width):
-    for axis, dim in sides:
-        count = lax.axis_size(axis)
-        forward = [(i, i + 1) for i in range(count - 1)]
-        backward = [(target, source) for source, target in forward]
-        low = lax.ppermute(
-            lax.slice_in_dim(block, block.shape[dim] - width, None, axis=dim), axis, forward)
-        high = lax.ppermute(lax.slice_in_dim(block, 0, width, axis=dim), axis, backward)
-        block = jnp.concatenate([low, block, high], axis=dim)
-    return block
-
-
-def apply_conv(padded, weight, bias_term):
-    size_x = padded.shape[1] - 2
-    size_y = padded.shape[2] - 2
-    size_z = padded.shape[3] - 2
-    pieces = []
+CH = 16
+CIN = 4
+TOP = 8
+BF16 = jnp.bfloat16
+
+
+def iota(shape, dim):
+    return lax.broadcasted_iota(jnp.int32, shape, dim)
+
+
+def lanes_for(n):
+    return -(-n // 128) * 128
+
+
+def one_hot(mask):
+    return jnp.where(mask, 1.0, 0.0).astype(BF16)
+
+
+def mm(a, b):
+    return jnp.dot(a, b, preferred_element_type=F32)
+
+
+def mm_nt(a, b):
+    return lax.dot_general(a, b, (((1,), (1,)), ((), ())), preferred_element_type=F32)
+
+
+def weight_kernel(w1_ref, w2_ref, w3_ref, b1_ref, b2_ref, t1_ref, t2_ref, t3_ref, bias_ref):
+    k1 = t1_ref.shape[1] // 3
+    n1 = t1_ref.shape[2]
+    pz = k1 // (2 * CIN)
+    spread = one_hot(iota((CH, n1), 1) % CH == iota((CH, n1), 0))
+    pick_c = one_hot(iota((k1, CIN), 0) % CIN == iota((k1, CIN), 1))
+    slot = iota((k1, n1), 0) // CIN
+    z_in = jnp.where(slot < pz + pz // 2, slot, slot - 2 * pz)
+    offset1 = z_in - iota((k1, n1), 1) // CH + 3
+    k2 = t2_ref.shape[1] // 3
+    n2 = t2_ref.shape[2]
+    pick_o = one_hot(iota((k2, CH), 0) % CH == iota((k2, CH), 1))
+    offset2 = iota((k2, n2), 0) // CH - iota((k2, n2), 1) // CH
+    k3 = t3_ref.shape[1]
+    n3 = t3_ref.shape[2]
+    pick_3 = one_hot(iota((k3, CH), 0) % CH == iota((k3, CH), 1))
+    offset3 = iota((k3, n3), 0) // CH - iota((k3, n3), 1) % pz
+    part3 = iota((k3, n3), 1) // pz
     for i in range(3):
         for j in range(3):
+            one = jnp.zeros((k1, n1), F32)
+            two = jnp.zeros((k2, n2), F32)
             for l in range(3):
-                pieces.append(padded[:, i:i + size_x, j:j + size_y, l:l + size_z])
-    columns = jnp.stack(pieces)
-    summed = jnp.einsum("koc,kcxyz->oxyz", weight, columns, preferred_element_type=F32)
-    return summed + bias_term[:, None, None, None]
-
-
-def detector(pooled, w_first, b_first, w_second, b_second, w_third, b_third, py, pz):
-    maps = pooled[:py].reshape(py, pz, 4).transpose(2, 0, 1)[:, None]
-
-    def slab_layer(activation, weight, bias_term):
-        return apply_conv(extended(activation, (("gx", 1), ("gy", 2), ("gz", 3)), 1), weight, bias_term)
-
-    maps = jax.nn.gelu(slab_layer(maps, w_first, b_first)).astype(jnp.bfloat16)
-    maps = jax.nn.gelu(slab_layer(maps, w_second, b_second)).astype(jnp.bfloat16)
-    return slab_layer(maps, w_third, b_third)[0]
+                tap = 9 * i + 3 * j + l
+                wide = mm(mm_nt(pick_c, w1_ref[tap]).astype(BF16), spread)
+                one = jnp.where(offset1 == l, wide, one)
+                wide = mm(mm_nt(pick_o, w2_ref[tap]).astype(BF16), spread[:, :n2])
+                two = jnp.where(offset2 == l, wide, two)
+            t1_ref[i, j * k1:(j + 1) * k1, :] = one.astype(BF16)
+            t2_ref[i, j * k2:(j + 1) * k2, :] = two.astype(BF16)
+        three = jnp.zeros((k3, n3), F32)
+        for j in range(3):
+            for l in range(3):
+                tap = 9 * i + 3 * j + l
+                column = mm_nt(pick_3, jnp.broadcast_to(w3_ref[tap], (CH, CH)))[:, 0:1]
+                three = jnp.where((offset3 == l) & (part3 == j), column, three)
+        t3_ref[i] = three.astype(BF16)
+    wide = spread.astype(F32)
+    for k, ref in ((0, b1_ref), (1, b2_ref)):
+        bias_ref[k:k + 1, :] = jnp.dot(ref[...], wide, precision=lax.Precision.HIGHEST, preferred_element_type=F32)
+
+
+def gelu(x):
+    return 0.5 * x * (1.0 + jnp.tanh(0.7978845608028654 * (x + 0.044715 * (x * x * x))))
+
+
+def plane_kernel(py, y_count):
+    def kernel(ids_ref, pool_ref, yr_ref, out_ref, scr_ref):
+        iy = ids_ref[1]
+        scr_ref[...] = jnp.zeros(scr_ref.shape, F32)
+        scr_ref[TOP:TOP + py, :] = pool_ref[0:py, :].astype(F32)
+        below = yr_ref[1].astype(F32)[0:3]
+        above = yr_ref[0].astype(F32)[0:3]
+        scr_ref[TOP - 3:TOP, :] = jnp.where(iy > 0, below, 0.0)
+        scr_ref[TOP + py:TOP + py + 3, :] = jnp.where(iy < y_count - 1, above, 0.0)
+        out_ref[...] = scr_ref[...].astype(BF16)
+    return kernel
+
+
+def conv_kernel(py, counts, shifts):
+    x_count, y_count, z_count = counts
+    n = len(shifts)
+
+    def kernel(*refs):
+        ids_ref, b3_ref = refs[:2]
+        own = refs[2:3 + n]
+        other = refs[3 + n:4 + 2 * n]
+        t1_ref, t2_ref, t3_ref, bias_ref, out_ref = refs[4 + 2 * n:9 + 2 * n]
+        in_ref, lhs1_ref, act1_ref, lhs2_ref, act2_ref, tail_ref = refs[9 + 2 * n:]
+        ix, iy, iz = ids_ref[0], ids_ref[1], ids_ref[2]
+        half = own[0].shape[1]
+        pz = half // CIN
+        rows = py + 4
+        z_row = iota((1, half), 1) // CIN
+        z_ok = ((z_row < pz // 2) & (iz < z_count - 1)) | ((z_row >= pz // 2) & (iz > 0))
+        for w in range(7):
+            o = w - 3
+            k = 0 if o == 0 else 1 + shifts.index((-o) % x_count) if (-o) % x_count in shifts else None
+            if k is None:
+                in_ref[w] = jnp.zeros(in_ref.shape[1:], F32)
+                continue
+            inside = (ix + o >= 0) & (ix + o < x_count)
+            in_ref[w, :, 0:half] = jnp.where(inside, own[k][...].astype(F32), 0.0)
+            in_ref[w, :, half:] = jnp.where(z_ok & inside, other[k][...].astype(F32), 0.0)
+        k1 = 2 * half
+        for w in range(7):
+            for j in range(3):
+                start = TOP - 3 + j
+                lhs1_ref[w, :, j * k1:(j + 1) * k1] = in_ref[w, start:start + rows, :].astype(BF16)
+        out = None
+        for i in range(3):
+            part = mm(lhs1_ref[i:i + 5].reshape(5 * rows, 3 * k1), t1_ref[i])
+            out = part if out is None else out + part
+        width = out.shape[1]
+        y = iota((rows, width), 0) - 2
+        z = iota((rows, width), 1) // CH - 2
+        ok = (z < pz + 2) & ((y >= 0) | (iy > 0)) & ((y < py) | (iy < y_count - 1))
+        ok = ok & ((z >= 0) | (iz > 0)) & ((z < pz) | (iz < z_count - 1))
+        for p in range(5):
+            a = gelu(out[p * rows:(p + 1) * rows] + bias_ref[0:1, :])
+            good = ok & (ix + p - 2 >= 0) & (ix + p - 2 < x_count)
+            act1_ref[p, 0:rows, 0:width] = jnp.where(good, a, 0.0)
+            act1_ref[p, rows:, 0:width] = jnp.zeros((act1_ref.shape[1] - rows, width), F32)
+            act1_ref[p, :, width:] = jnp.zeros((act1_ref.shape[1], act1_ref.shape[2] - width), F32)
+        blocks = lhs2_ref.shape[1]
+        for p in range(5):
+            for j in range(3):
+                a = act1_ref[p, j:j + rows, :].astype(BF16)
+                for b in range(blocks):
+                    lhs2_ref[p, b, :, j * 256:(j + 1) * 256] = a[:, b * 128:b * 128 + 256]
+        out = None
+        for i in range(3):
+            part = mm(lhs2_ref[i:i + 3].reshape(3 * blocks * rows, 768), t2_ref[i])
+            out = part if out is None else out + part
+        for b in range(blocks):
+            y = iota((rows, 128), 0) - 1
+            z = (iota((rows, 128), 1) + b * 128) // CH - 1
+            ok = (z < pz + 1) & (y <= py) & ((y >= 0) | (iy > 0)) & ((y < py) | (iy < y_count - 1))
+            ok = ok & ((z >= 0) | (iz > 0)) & ((z < pz) | (iz < z_count - 1))
+            for p in range(3):
+                s = (p * blocks + b) * rows
+                a = gelu(out[s:s + rows] + bias_ref[1:2, 0:128])
+                good = ok & (ix + p - 1 >= 0) & (ix + p - 1 < x_count)
+                act2_ref[p, :, b * 128:(b + 1) * 128] = jnp.where(good, a, 0.0).astype(BF16)
+        out = None
+        for i in range(3):
+            part = mm(act2_ref[i], t3_ref[i])
+            out = part if out is None else out + part
+        tail_ref[0:rows, :] = out
+        score = tail_ref[0:py, :]
+        for j in (1, 2):
+            score = score + pltpu.roll(tail_ref[j:j + py, :], 128 - j * pz, 1)
+        out_ref[0] = score[:, 0:pz] + b3_ref[0]
+    return kernel
+
+
+def detector(pooled, edge, ids, w_first, b_first, w_second, b_second, w_third, b_third, py, pz):
+    vmem = pl.BlockSpec(memory_space=pltpu.VMEM)
+    smem = pl.BlockSpec(memory_space=pltpu.SMEM)
+    limit = pltpu.CompilerParams(vmem_limit_bytes=48 * 1024 * 1024)
+    counts = tuple(lax.axis_size(a) for a in ("gx", "gy", "gz"))
+    half = pooled.shape[1]
+    assert half == 128 and pz * CIN == half and pz * 3 <= 128
+    rows = py + 4
+    width = lanes_for((pz + 4) * CH)
+    blocks = width // 128
+    t1, t2, t3, bias = call(
+        weight_kernel,
+        [((3, 6 * half, width), BF16), ((3, 768, 128), BF16), ((3, width, 128), BF16), ((8, width), F32)],
+        w_first, w_second, w_third, b_first[None], b_second[None])
+    yr = both_sides(edge, "gy")
+    tall = -(-(TOP + py + 3) // 16) * 16
+    plane = pl.pallas_call(
+        plane_kernel(py, counts[1]),
+        in_specs=[smem, vmem, vmem],
+        out_shape=jax.ShapeDtypeStruct((tall, half), BF16),
+        scratch_shapes=[pltpu.VMEM((tall, half), F32)],
+        compiler_params=limit,
+    )(ids, pooled, yr)
+    shifts = []
+    for s in (1, -1, 2, -2, 3, -3):
+        if s % counts[0] and s % counts[0] not in shifts:
+            shifts.append(s % counts[0])
+    own = [plane] + [lax.ppermute(plane, "gx", ring("gx", s)) for s in shifts]
+    other = [z_neighbour(v, "gz", False) for v in own]
+    (score,) = pl.pallas_call(
+        conv_kernel(py, counts, shifts),
+        in_specs=[smem, smem] + [vmem] * (2 * len(own) + 4),
+        out_shape=[jax.ShapeDtypeStruct((1, py, pz), F32)],
+        scratch_shapes=[
+            pltpu.VMEM((7, tall, 2 * half), F32),
+            pltpu.VMEM((7, rows, 6 * half), BF16),
+            pltpu.VMEM((5, rows + 8, width + 128), F32),
+            pltpu.VMEM((5, blocks, rows, 768), BF16),
+            pltpu.VMEM((3, rows, width), BF16),
+            pltpu.VMEM((rows + 8, 128), F32),
+        ],
+        compiler_params=limit,
+    )(ids, b_third, *own, *other, t1, t2, t3, bias)
+    return score
 
 
 def solution(mesh):

time: 147 us -> 82.6 us (0.56)
  waiting for transfers between devices: 72.4 us -> 33.6 us
  starting transfers between devices: 47.1 us -> 22.2 us
  Pallas kernels: 6.12 us -> 19.6 us
  local copies, waits for them, and re-layouts: 12.9 us -> 5.36 us
  other arithmetic: 4.73 us -> 0.09 us
    ppermute x18 -> x3, waiting for transfers between devices: 44.7 us -> 3.62 us  [detector(): own = [plane] + [lax.ppermute(plane, 'gx', ring('gx', s)) for s in shifts]]
    ppermute x18 -> x3, starting transfers between devices: 31.3 us -> 4.42 us  [detector(): own = [plane] + [lax.ppermute(plane, 'gx', ring('gx', s)) for s in shifts]]
    pallas_call x5 -> x6, Pallas kernels: 0.72 us -> 10.2 us  [call(): pl.pallas_call(kernel, out_shape=[jax.ShapeDtypeStruct(s, t) for s, t in...]
    another operation x32 -> x0, local copies, waits for them, and re-layouts: 5.06 us -> none  [apply_conv(): columns = jnp.stack(pieces)]
    pallas_call x0 -> x2, Pallas kernels: none -> 4.25 us  [the longest x1 3.7 us: detector(): pl.pallas_call(conv_kernel(py, counts, shifts), in_specs=[smem, smem] + [...]
    concatenate x12 -> x0, other arithmetic: 3.09 us -> none  [extended(): block = jnp.concatenate([low, block, high], axis=dim)]
    ppermute x2 -> x3, waiting for transfers between devices: 4.85 us -> 6.93 us  [both_sides(): return lax.ppermute(pay, axis, ring(axis, 1))]
    unnamed x72 -> x26, local copies, waits for them, and re-layouts: 7.23 us -> 5.36 us
  transfers between devices with their start and end apart: 30 -> 20, of which waited for: 23 -> 11; matrix products, arithmetic and copies ran while one was open for 1% -> 1% of each run, Pallas kernels for 0% -> 10%
where the time goes in v2:
time: 82.6 us; the launch traced here: 82.3 us
  waiting for transfers between devices  33.6 us (41%)
  starting transfers between devices  22.2 us (27%)
  Pallas kernels  19.6 us (24%)
  local copies, waits for them, and re-layouts  5.36 us (6%)
  between operations  1.45 us (2%)
    ppermute x4, waiting for transfers between devices, pair_sum(): s = s + lax.ppermute(s, axis, [(i, i ^ bit) for i in range(count)])  18.1 us
    pallas_call x6, Pallas kernels, call(): pl.pallas_call(kernel, out_shape=[jax.ShapeDtypeStruct(s, t) for s, t in...  10.2 us
    ppermute x3, waiting for transfers between devices, both_sides(): return lax.ppermute(pay, axis, ring(axis, 1))  6.93 us
    ppermute x2, starting transfers between devices, body(): from_hi = lax.ppermute(lo, 'gx', ring('gx', -1))  5.59 us
    unnamed x26, local copies, waits for them, and re-layouts  5.36 us
    pallas_call x2, Pallas kernels, heavy(): pl.pallas_call(kernel, out_shape=[jax.ShapeDtypeStruct(s, t) for s, t in...  5.19 us
    ppermute x6, waiting for transfers between devices, z_neighbour(): return lax.ppermute(pay, axis, ring(axis, 1))  4.92 us
    ppermute x3, starting transfers between devices, both_sides(): return lax.ppermute(pay, axis, ring(axis, 1))  4.6 us
  transfers between devices with their start and end apart: 20, of which 11 were waited for; matrix products, arithmetic and copies ran while one was open for 1% of the time, Pallas kernels for 10%

profile of v2, /device:TPU:0, one launch (start us, length us, event | category | flops | bytes accessed | tf_op | source)
XLA Modules:
  0.0 82.3 jit_solution(17039361081107497063)
XLA Ops:
  0.6 1.0 %copy-done = f32[4,240,128]{2,1,0:T(8,128)S(1)} copy-done((f32[4,240,128]{2,1,0:T(8,128)S(1)}, f32[4,240,128]{2,1,0:T(8,128)}, u32[]{:S(2)}) %copy-start) | copy-done | bytes 491544
  1.7 1.0 %copy-done.1 = s32[4,240,128]{2,1,0:T(8,128)S(1)} copy-done((s32[4,240,128]{2,1,0:T(8,128)S(1)}, s32[4,240,128]{2,1,0:T(8,128)}, u32[]{:S(2)}) %copy-start.1) | copy-done | bytes 491544
  2.7 1.0 %copy-done.5 = f32[4,240,128]{2,1,0:T(8,128)S(1)} copy-done((f32[4,240,128]{2,1,0:T(8,128)S(1)}, f32[4,240,128]{2,1,0:T(8,128)}, u32[]{:S(2)}) %copy-start.5) | copy-done | bytes 491544
  3.7 0.3 shard_map.120
  4.0 3.1 %collective-permute-start = (s16[3,240,128]{2,1,0:T(8,128)(2,1)S(1)}, s16[3,240,128]{2,1,0:T(8,128)(2,1)S(1)}, u32[]{:S(2)}, u32[]{:S(2)}) collective-permute-start(s16[3,240,128]{2,1,0:T(8,128)(2,1)S(1)} %get-tuple-element.29), channel_id=1, source_target_pairs={{0,4},{4,8},{8,12},{12,0},{1,5},{5,9},{9,13},{13,1},{2,6},{6,10},{... | collective-permute-start | bytes 552968 | tf_op jit(solution)/shard_map/ppermute | solution.py:390
  7.1 2.1 %collective-permute-start.1 = (s16[3,240,128]{2,1,0:T(8,128)(2,1)S(1)}, s16[3,240,128]{2,1,0:T(8,128)(2,1)S(1)}, u32[]{:S(2)}, u32[]{:S(2)}) collective-permute-start(s16[3,240,128]{2,1,0:T(8,128)(2,1)S(1)} %get-tuple-element.30), channel_id=1, source_target_pairs={{0,12},{4,0},{8,4},{12,8},{1,13},{5,1},{9,5},{13,9},{2,14},{6,2},{... | collective-permute-start | bytes 552968 | tf_op jit(solution)/shard_map/ppermute | solution.py:391
  9.2 0.0 collective-permute-start.2
  9.2 8.1 %collective-permute-done.2 = f32[16,128]{1,0:T(8,128)S(1)} collective-permute-done((f32[16,128]{1,0:T(8,128)S(1)}, f32[16,128]{1,0:T(8,128)S(1)}, u32[]{:S(2)}, u32[]{:S(2)}) %collective-permute-start.2) | collective-permute-done | bytes 8224 | tf_op jit(solution)/shard_map/ppermute | solution.py:339
  17.3 1.2 %collective-permute-start.3 = (f32[16,128]{1,0:T(8,128)S(1)}, f32[16,128]{1,0:T(8,128)S(1)}, u32[]{:S(2)}, u32[]{:S(2)}) collective-permute-start(f32[16,128]{1,0:T(8,128)S(1)} %add.12), channel_id=1, source_target_pairs={{0,8},{4,12},{8,0},{12,4},{1,9},{5,13},{9,1},{13,5},{2,10},{6,14},... | collective-permute-start | bytes 24584 | tf_op jit(solution)/shard_map/ppermute | solution.py:339
  18.5 3.4 %collective-permute-done.3 = f32[16,128]{1,0:T(8,128)S(1)} collective-permute-done((f32[16,128]{1,0:T(8,128)S(1)}, f32[16,128]{1,0:T(8,128)S(1)}, u32[]{:S(2)}, u32[]{:S(2)}) %collective-permute-start.3) | collective-permute-done | bytes 8224 | tf_op jit(solution)/shard_map/ppermute | solution.py:339
  21.9 0.0 collective-permute-done.lo_ref
  21.9 1.6 %collective-permute-start.4 = (f32[2,32,128]{2,1,0:T(8,128)S(1)}, f32[2,32,128]{2,1,0:T(8,128)S(1)}, u32[]{:S(2)}, u32[]{:S(2)}) collective-permute-start(f32[2,32,128]{2,1,0:T(8,128)S(1)} %shard_map.121), channel_id=1, source_target_pairs={{0,2},{2,0},{1,3},{3,1},{4,6},{6,4},{5,7},{7,5},{8,10},{10,8},{9,1... | collective-permute-start | bytes 98312 | tf_op jit(solution)/shard_map/ppermute | solution.py:346
  23.5 2.4 %collective-permute-done.4.yr_ref = f32[2,32,128]{2,1,0:T(8,128)S(1)} collective-permute-done((f32[2,32,128]{2,1,0:T(8,128)S(1)}, f32[2,32,128]{2,1,0:T(8,128)S(1)}, u32[]{:S(2)}, u32[]{:S(2)}) %collective-permute-start.4) | collective-permute-done | bytes 32800 | tf_op jit(solution)/shard_map/ppermute | solution.py:346
  25.9 0.2 shard_map.122
  26.2 0.1 collective-permute-start.5
  26.2 2.3 %collective-permute-done.5.zr_ref = f32[6,272,128]{2,1,0:T(8,128)S(1)} collective-permute-done((f32[6,272,128]{2,1,0:T(8,128)S(1)}, f32[6,272,128]{2,1,0:T(8,128)S(1)}, u32[]{:S(2)}, u32[]{:S(2)}) %collective-permute-start.5) | collective-permute-done | bytes 835616 | tf_op jit(solution)/shard_map/ppermute | solution.py:352
  28.6 2.1 %shard_map.123 = (f32[4,240,128]{2,1,0:T(8,128)S(1)}, f32[6,272,128]{2,1,0:T(8,128)S(1)}, f32[4,240,128]{2,1,0:T(8,128)S(1)}, s16[2,240,128]{2,1,0:T(8,128)(2,1)...) custom-call(f32[8,272,128]{2,1,0:T(8,128)S(1)} %get-tuple-element.32.pad_ref, ...), custom_call_target="tpu_custom_call" | custom-call | tf_op jit(solution)/shard_map/pallas_call | solution.py:379
  30.7 0.0 copy-start.3
  30.7 0.0 copy-start.2
  30.7 0.4 collective-permute-start.6
  31.1 3.5 %collective-permute-start.7 = (s16[2,240,128]{2,1,0:T(8,128)(2,1)S(1)}, s16[2,240,128]{2,1,0:T(8,128)(2,1)S(1)}, u32[]{:S(2)}, u32[]{:S(2)}) collective-permute-start(s16[2,240,128]{2,1,0:T(8,128)(2,1)S(1)} %get-tuple-element.37), channel_id=1, source_target_pairs={{0,12},{4,0},{8,4},{12,8},{1,13},{5,1},{9,5},{13,9},{2,14},{6,2},{... | collective-permute-start | bytes 368648 | tf_op jit(solution)/shard_map/ppermute | solution.py:407
  34.6 4.4 %collective-permute-done.8 = f32[16,128]{1,0:T(8,128)S(1)} collective-permute-done((f32[16,128]{1,0:T(8,128)S(1)}, f32[16,128]{1,0:T(8,128)S(1)}, u32[]{:S(2)}, u32[]{:S(2)}) %collective-permute-start.8) | collective-permute-done | bytes 8224 | tf_op jit(solution)/shard_map/ppermute | solution.py:339
  39.0 2.3 %collective-permute-start.9 = (f32[16,128]{1,0:T(8,128)S(1)}, f32[16,128]{1,0:T(8,128)S(1)}, u32[]{:S(2)}, u32[]{:S(2)}) collective-permute-start(f32[16,128]{1,0:T(8,128)S(1)} %add.14), channel_id=1, source_target_pairs={{0,8},{4,12},{8,0},{12,4},{1,9},{5,13},{9,1},{13,5},{2,10},{6,14},... | collective-permute-start | bytes 24584 | tf_op jit(solution)/shard_map/ppermute | solution.py:339
  41.3 2.2 %collective-permute-done.9 = f32[16,128]{1,0:T(8,128)S(1)} collective-permute-done((f32[16,128]{1,0:T(8,128)S(1)}, f32[16,128]{1,0:T(8,128)S(1)}, u32[]{:S(2)}, u32[]{:S(2)}) %collective-permute-start.9) | collective-permute-done | bytes 8224 | tf_op jit(solution)/shard_map/ppermute | solution.py:339
  43.6 1.6 %collective-permute-start.10 = (f32[2,32,128]{2,1,0:T(8,128)S(1)}, f32[2,32,128]{2,1,0:T(8,128)S(1)}, u32[]{:S(2)}, u32[]{:S(2)}) collective-permute-start(f32[2,32,128]{2,1,0:T(8,128)S(1)} %shard_map.124), channel_id=1, source_target_pairs={{0,2},{2,0},{1,3},{3,1},{4,6},{6,4},{5,7},{7,5},{8,10},{10,8},{9,1... | collective-permute-start | bytes 98312 | tf_op jit(solution)/shard_map/ppermute | solution.py:346
  45.1 2.4 %collective-permute-done.10.yr_ref = f32[2,32,128]{2,1,0:T(8,128)S(1)} collective-permute-done((f32[2,32,128]{2,1,0:T(8,128)S(1)}, f32[2,32,128]{2,1,0:T(8,128)S(1)}, u32[]{:S(2)}, u32[]{:S(2)}) %collective-permute-start.10) | collective-permute-done | bytes 32800 | tf_op jit(solution)/shard_map/ppermute | solution.py:346
  47.6 1.0 %shard_map.125 = (f32[8,272,128]{2,1,0:T(8,128)S(1)}, f32[6,272,128]{2,1,0:T(8,128)}) custom-call(f32[4,240,128]{2,1,0:T(8,128)S(1)} %get-tuple-element.35.f_ref, s16[2,240,128]{2,1,0:T(8,128)(2,1)S(1)} %collective-permute-done.6.lo_ref, s16[2,240,128]{2,1,0:T(8,128)(2,1)S(1)} %collective-permute-done.7.hi_ref, ...), custom_call_target="tpu_custom_call" | custom-call | tf_op jit(solution)/shard_map/pallas_call | solution.py:32
  48.6 2.6 %collective-permute-done.11.zr_ref = f32[6,272,128]{2,1,0:T(8,128)S(1)} collective-permute-done((f32[6,272,128]{2,1,0:T(8,128)}, f32[6,272,128]{2,1,0:T(8,128)S(1)}, u32[]{:S(2)}, u32[]{:S(2)}) %collective-permute-start.11) | collective-permute-done | bytes 835616 | tf_op jit(solution)/shard_map/ppermute | solution.py:352
  51.2 1.0 %copy-done.4 = f32[4,240,128]{2,1,0:T(8,128)S(1)} copy-done((f32[4,240,128]{2,1,0:T(8,128)S(1)}, f32[4,240,128]{2,1,0:T(8,128)}, u32[]{:S(2)}) %copy-start.4) | copy-done | bytes 491544
  52.2 0.0 copy-start.7
  52.2 3.1 %shard_map.126 = (f32[4,240,128]{2,1,0:T(8,128)}, f32[4,240,128]{2,1,0:T(8,128)}, f32[4,240,128]{2,1,0:T(8,128)}, bf16[60,128]{1,0:T(8,128)(2,1)S(1)}, bf16[2,16,128]{2,1,0:T(8,128)(2,1)S(1)}) custom-call(f32[8,272,128]{2,1,0:T(8,128)S(1)} %get-tuple-element.39.pad_ref, f32[6,272,128]{2,1,0:T(8,128)S(1)} %get-tuple-element.40.a2_ref, ...), custom_call_target="tpu_custom_call" | custom-call | tf_op jit(solution)/shard_map/pallas_call | solution.py:379
  55.3 1.5 %collective-permute-start.12 = (bf16[2,16,128]{2,1,0:T(8,128)(2,1)S(1)}, bf16[2,16,128]{2,1,0:T(8,128)(2,1)S(1)}, u32[]{:S(2)}, u32[]{:S(2)}) collective-permute-start(bf16[2,16,128]{2,1,0:T(8,128)(2,1)S(1)} %get-tuple-element.47), channel_id=1, source_target_pairs={{0,2},{2,0},{1,3},{3,1},{4,6},{6,4},{5,7},{7,5},{8,10},{10,8},{9,1... | collective-permute-start | bytes 24584 | tf_op jit(solution)/shard_map/ppermute | solution.py:346
  56.8 0.1 pad_add_fusion.ids_ref.refs_0_
  56.9 2.1 %collective-permute-done.12.yr_ref = bf16[2,16,128]{2,1,0:T(8,128)(2,1)S(1)} collective-permute-done((bf16[2,16,128]{2,1,0:T(8,128)(2,1)S(1)}, bf16[2,16,128]{2,1,0:T(8,128)(2,1)S(1)}, u32[]{:S(2)}, u32[]{:S(2)}) %collective-permute-start.12) | collective-permute-done | bytes 8224 | tf_op jit(solution)/shard_map/ppermute | solution.py:346
  59.0 0.6 shard_map.127.refs_2_
  59.5 0.9 %collective-permute-start.13 = (bf16[80,128]{1,0:T(8,128)(2,1)S(1)}, bf16[80,128]{1,0:T(8,128)(2,1)S(1)}, u32[]{:S(2)}, u32[]{:S(2)}) collective-permute-start(bf16[80,128]{1,0:T(8,128)(2,1)S(1)} %shard_map.127.refs_2_), channel_id=1, source_target_pairs={{0,4},{4,8},{8,12},{12,0},{1,5},{5,9},{9,13},{13,1},{2,6},{6,10},{... | collective-permute-start | bytes 61448 | tf_op jit(solution)/shard_map/ppermute | solution.py:615
  60.4 3.0 %collective-permute-start.14 = (bf16[80,128]{1,0:T(8,128)(2,1)S(1)}, bf16[80,128]{1,0:T(8,128)(2,1)S(1)}, u32[]{:S(2)}, u32[]{:S(2)}) collective-permute-start(bf16[80,128]{1,0:T(8,128)(2,1)S(1)} %shard_map.127.refs_2_), channel_id=1, source_target_pairs={{0,12},{4,0},{8,4},{12,8},{1,13},{5,1},{9,5},{13,9},{2,14},{6,2},{... | collective-permute-start | bytes 61448 | tf_op jit(solution)/shard_map/ppermute | solution.py:615
  63.4 0.5 collective-permute-start.15
  63.9 1.2 %collective-permute-done.13.refs_3_ = bf16[80,128]{1,0:T(8,128)(2,1)S(1)} collective-permute-done((bf16[80,128]{1,0:T(8,128)(2,1)S(1)}, bf16[80,128]{1,0:T(8,128)(2,1)S(1)}, u32[]{:S(2)}, u32[]{:S(2)}) %collective-permute-start.13) | collective-permute-done | bytes 20512 | tf_op jit(solution)/shard_map/ppermute | solution.py:615
  65.1 0.5 collective-permute-start.18
  65.7 2.4 %collective-permute-done.15.refs_5_ = bf16[80,128]{1,0:T(8,128)(2,1)S(1)} collective-permute-done((bf16[80,128]{1,0:T(8,128)(2,1)S(1)}, bf16[80,128]{1,0:T(8,128)(2,1)S(1)}, u32[]{:S(2)}, u32[]{:S(2)}) %collective-permute-start.15) | collective-permute-done | bytes 20512 | tf_op jit(solution)/shard_map/ppermute | solution.py:615
  68.1 0.2 copy.13.w1_ref
  68.3 0.2 copy.14.w2_ref
  68.5 0.1 copy.15.w3_ref
  69.3 8.6 %shard_map.128 = (bf16[3,768,640]{2,1,0:T(8,128)(2,1)S(1)}, bf16[3,768,128]{2,1,0:T(8,128)(2,1)S(1)}, bf16[3,640,128]{2,1,0:T(8,128)(2,1)S(1)}, f32[8,640]{1,0:T(8,128)S(1)}) custom-call(bf16[27,16,4]{2,1,0:T(8,128)(2,1)S(1)} %copy.13.w1_ref, bf16[27,16,16]{2,1,0:T(8,128)(2,1)S(1)} %copy.14.w2_ref, bf16[27,1,16]{2,1,0:T(2,128)(2,1)S(1)} %copy.15.w3_ref, ...), custom_call_target="tpu_custom_call" | custom-call | tf_op jit(solution)/shard_map/pallas_call | solution.py:32
  77.9 0.0 collective-permute-done.18.refs_8_
  77.9 3.7 %shard_map.129 = f32[1,60,32]{2,1,0:T(8,128)S(1)} custom-call(s32[3]{0:T(128)S(1)} %pad_add_fusion.ids_ref.refs_0_, f32[1]{0:T(128)S(6)} %copy.17.refs_1_, bf16[80,128]{1,0:T(8,128)(2,1)S(1)} %shard_map.127.refs_2_, bf16[80,128]{1,0:T(8,128)(2,1)S(1)} %collective-permute-done.13.refs_3_, bf16[80,128]{1,0:T(8,128)(2,1)S(1)} %collective-permute-done.14.refs_4_, ...), custom_call_target="tpu_custom_call" | custom-call | tf_op jit(solution)/shard_map/pallas_call | solution.py:617
  81.6 0.7 copy.16
  (33 shorter events, 0.1 us)
Async XLA Ops:
  0.6 1.0 %copy-start = (f32[4,240,128]{2,1,0:T(8,128)S(1)}, f32[4,240,128]{2,1,0:T(8,128)}, u32[]{:S(2)}) copy-start(f32[4,240,128]{2,1,0:T(8,128)} %f_ref.3) | copy-start | bytes 1474564
  1.7 1.0 %copy-start.1 = (s32[4,240,128]{2,1,0:T(8,128)S(1)}, s32[4,240,128]{2,1,0:T(8,128)}, u32[]{:S(2)}) copy-start(s32[4,240,128]{2,1,0:T(8,128)} %l_ref.3) | copy-start | bytes 1474564
  2.7 1.0 %copy-start.5 = (f32[4,240,128]{2,1,0:T(8,128)S(1)}, f32[4,240,128]{2,1,0:T(8,128)}, u32[]{:S(2)}) copy-start(f32[4,240,128]{2,1,0:T(8,128)} %d_ref.1) | copy-start | bytes 1474564
  4.0 17.9 %collective-permute-start = (s16[3,240,128]{2,1,0:T(8,128)(2,1)S(1)}, s16[3,240,128]{2,1,0:T(8,128)(2,1)S(1)}, u32[]{:S(2)}, u32[]{:S(2)}) collective-permute-start(s16[3,240,128]{2,1,0:T(8,128)(2,1)S(1)} %get-tuple-element.29), channel_id=1, source_target_pairs={{0,4},{4,8},{8,12},{12,0},{1,5},{5,9},{9,13},{13,1},{2,6},{6,10},{... | collective-permute-start | bytes 552968 | tf_op jit(solution)/shard_map/ppermute | solution.py:390
  7.1 14.8 %collective-permute-start.1 = (s16[3,240,128]{2,1,0:T(8,128)(2,1)S(1)}, s16[3,240,128]{2,1,0:T(8,128)(2,1)S(1)}, u32[]{:S(2)}, u32[]{:S(2)}) collective-permute-start(s16[3,240,128]{2,1,0:T(8,128)(2,1)S(1)} %get-tuple-element.30), channel_id=1, source_target_pairs={{0,12},{4,0},{8,4},{12,8},{1,13},{5,1},{9,5},{13,9},{2,14},{6,2},{... | collective-permute-start | bytes 552968 | tf_op jit(solution)/shard_map/ppermute | solution.py:391
  9.2 8.1 %collective-permute-start.2 = (f32[16,128]{1,0:T(8,128)S(1)}, f32[16,128]{1,0:T(8,128)S(1)}, u32[]{:S(2)}, u32[]{:S(2)}) collective-permute-start(f32[16,128]{1,0:T(8,128)S(1)} %get-tuple-element.31), channel_id=1, source_target_pairs={{0,4},{4,0},{8,12},{12,8},{1,5},{5,1},{9,13},{13,9},{2,6},{6,2},{1... | collective-permute-start | bytes 24584 | tf_op jit(solution)/shard_map/ppermute | solution.py:339
  17.3 4.5 %collective-permute-start.3 = (f32[16,128]{1,0:T(8,128)S(1)}, f32[16,128]{1,0:T(8,128)S(1)}, u32[]{:S(2)}, u32[]{:S(2)}) collective-permute-start(f32[16,128]{1,0:T(8,128)S(1)} %add.12), channel_id=1, source_target_pairs={{0,8},{4,12},{8,0},{12,4},{1,9},{5,13},{9,1},{13,5},{2,10},{6,14},... | collective-permute-start | bytes 24584 | tf_op jit(solution)/shard_map/ppermute | solution.py:339
  21.9 4.0 %collective-permute-start.4 = (f32[2,32,128]{2,1,0:T(8,128)S(1)}, f32[2,32,128]{2,1,0:T(8,128)S(1)}, u32[]{:S(2)}, u32[]{:S(2)}) collective-permute-start(f32[2,32,128]{2,1,0:T(8,128)S(1)} %shard_map.121), channel_id=1, source_target_pairs={{0,2},{2,0},{1,3},{3,1},{4,6},{6,4},{5,7},{7,5},{8,10},{10,8},{9,1... | collective-permute-start | bytes 98312 | tf_op jit(solution)/shard_map/ppermute | solution.py:346
  26.2 2.4 %collective-permute-start.5 = (f32[6,272,128]{2,1,0:T(8,128)S(1)}, f32[6,272,128]{2,1,0:T(8,128)S(1)}, u32[]{:S(2)}, u32[]{:S(2)}) collective-permute-start(f32[6,272,128]{2,1,0:T(8,128)S(1)} %get-tuple-element.34), channel_id=1, source_target_pairs={{0,1},{1,0},{2,3},{3,2},{4,5},{5,4},{6,7},{7,6},{8,9},{9,8},{10,11... | collective-permute-start | bytes 2506760 | tf_op jit(solution)/shard_map/ppermute | solution.py:352
  30.7 17.9 %copy-start.3 = (f32[4,240,128]{2,1,0:T(8,128)}, f32[4,240,128]{2,1,0:T(8,128)S(1)}, u32[]{:S(2)}) copy-start(f32[4,240,128]{2,1,0:T(8,128)S(1)} %get-tuple-element.41.ae2_ref) | copy-start | bytes 1474564
  30.7 20.5 %copy-start.2 = (s32[4,240,128]{2,1,0:T(8,128)S(1)}, s32[4,240,128]{2,1,0:T(8,128)}, u32[]{:S(2)}) copy-start(s32[4,240,128]{2,1,0:T(8,128)} %l_ref.3) | copy-start | bytes 1474564
  30.7 12.9 %collective-permute-start.6 = (s16[2,240,128]{2,1,0:T(8,128)(2,1)S(1)}, s16[2,240,128]{2,1,0:T(8,128)(2,1)S(1)}, u32[]{:S(2)}, u32[]{:S(2)}) collective-permute-start(s16[2,240,128]{2,1,0:T(8,128)(2,1)S(1)} %get-tuple-element.36), channel_id=1, source_target_pairs={{0,4},{4,8},{8,12},{12,0},{1,5},{5,9},{9,13},{13,1},{2,6},{6,10},{... | collective-permute-start | bytes 368648 | tf_op jit(solution)/shard_map/ppermute | solution.py:406
  31.1 12.5 %collective-permute-start.7 = (s16[2,240,128]{2,1,0:T(8,128)(2,1)S(1)}, s16[2,240,128]{2,1,0:T(8,128)(2,1)S(1)}, u32[]{:S(2)}, u32[]{:S(2)}) collective-permute-start(s16[2,240,128]{2,1,0:T(8,128)(2,1)S(1)} %get-tuple-element.37), channel_id=1, source_target_pairs={{0,12},{4,0},{8,4},{12,8},{1,13},{5,1},{9,5},{13,9},{2,14},{6,2},{... | collective-permute-start | bytes 368648 | tf_op jit(solution)/shard_map/ppermute | solution.py:407
  34.6 4.4 %collective-permute-start.8 = (f32[16,128]{1,0:T(8,128)S(1)}, f32[16,128]{1,0:T(8,128)S(1)}, u32[]{:S(2)}, u32[]{:S(2)}) collective-permute-start(f32[16,128]{1,0:T(8,128)S(1)} %get-tuple-element.38), channel_id=1, source_target_pairs={{0,4},{4,0},{8,12},{12,8},{1,5},{5,1},{9,13},{13,9},{2,6},{6,2},{1... | collective-permute-start | bytes 24584 | tf_op jit(solution)/shard_map/ppermute | solution.py:339
  39.0 4.5 %collective-permute-start.9 = (f32[16,128]{1,0:T(8,128)S(1)}, f32[16,128]{1,0:T(8,128)S(1)}, u32[]{:S(2)}, u32[]{:S(2)}) collective-permute-start(f32[16,128]{1,0:T(8,128)S(1)} %add.14), channel_id=1, source_target_pairs={{0,8},{4,12},{8,0},{12,4},{1,9},{5,13},{9,1},{13,5},{2,10},{6,14},... | collective-permute-start | bytes 24584 | tf_op jit(solution)/shard_map/ppermute | solution.py:339
  43.6 4.0 %collective-permute-start.10 = (f32[2,32,128]{2,1,0:T(8,128)S(1)}, f32[2,32,128]{2,1,0:T(8,128)S(1)}, u32[]{:S(2)}, u32[]{:S(2)}) collective-permute-start(f32[2,32,128]{2,1,0:T(8,128)S(1)} %shard_map.124), channel_id=1, source_target_pairs={{0,2},{2,0},{1,3},{3,1},{4,6},{6,4},{5,7},{7,5},{8,10},{10,8},{9,1... | collective-permute-start | bytes 98312 | tf_op jit(solution)/shard_map/ppermute | solution.py:346
  48.6 2.6 %collective-permute-start.11 = (f32[6,272,128]{2,1,0:T(8,128)}, f32[6,272,128]{2,1,0:T(8,128)S(1)}, u32[]{:S(2)}, u32[]{:S(2)}) collective-permute-start(f32[6,272,128]{2,1,0:T(8,128)} %get-tuple-element.42), channel_id=1, source_target_pairs={{0,1},{1,0},{2,3},{3,2},{4,5},{5,4},{6,7},{7,6},{8,9},{9,8},{10,11... | collective-permute-start | bytes 2506760 | tf_op jit(solution)/shard_map/ppermute | solution.py:352
  51.2 1.0 %copy-start.4 = (f32[4,240,128]{2,1,0:T(8,128)S(1)}, f32[4,240,128]{2,1,0:T(8,128)}, u32[]{:S(2)}) copy-start(f32[4,240,128]{2,1,0:T(8,128)} %copy-done.3) | copy-start | bytes 1474564
  52.2 15.9 %copy-start.9 = (bf16[27,16,4]{0,2,1:T(4,128)(2,1)S(1)}, bf16[27,16,4]{0,2,1:T(4,128)(2,1)}, u32[]{:S(2)}) copy-start(bf16[27,16,4]{0,2,1:T(4,128)(2,1)} %param.12) | copy-start | bytes 10372
  52.2 16.1 %copy-start.8 = (bf16[27,16,16]{0,2,1:T(8,128)(2,1)S(1)}, bf16[27,16,16]{0,2,1:T(8,128)(2,1)}, u32[]{:S(2)}) copy-start(bf16[27,16,16]{0,2,1:T(8,128)(2,1)} %param.14) | copy-start | bytes 41476
  52.2 16.3 %copy-start.10 = (bf16[27,1,16]{0,2,1:T(8,128)(2,1)S(1)}, bf16[27,1,16]{0,2,1:T(8,128)(2,1)}, u32[]{:S(2)}) copy-start(bf16[27,1,16]{0,2,1:T(8,128)(2,1)} %param.16) | copy-start | bytes 2596
  52.2 17.1 %copy-start.6 = (f32[16]{0:T(128)S(1)}, f32[16]{0:T(128)}, u32[]{:S(2)}) copy-start(f32[16]{0:T(128)} %param.13) | copy-start | bytes 196
  52.2 17.1 %copy-start.7 = (f32[16]{0:T(128)S(1)}, f32[16]{0:T(128)}, u32[]{:S(2)}) copy-start(f32[16]{0:T(128)} %param.15) | copy-start | bytes 196
  55.3 3.7 %collective-permute-start.12 = (bf16[2,16,128]{2,1,0:T(8,128)(2,1)S(1)}, bf16[2,16,128]{2,1,0:T(8,128)(2,1)S(1)}, u32[]{:S(2)}, u32[]{:S(2)}) collective-permute-start(bf16[2,16,128]{2,1,0:T(8,128)(2,1)S(1)} %get-tuple-element.47), channel_id=1, source_target_pairs={{0,2},{2,0},{1,3},{3,1},{4,6},{6,4},{5,7},{7,5},{8,10},{10,8},{9,1... | collective-permute-start | bytes 24584 | tf_op jit(solution)/shard_map/ppermute | solution.py:346
  59.5 5.6 %collective-permute-start.13 = (bf16[80,128]{1,0:T(8,128)(2,1)S(1)}, bf16[80,128]{1,0:T(8,128)(2,1)S(1)}, u32[]{:S(2)}, u32[]{:S(2)}) collective-permute-start(bf16[80,128]{1,0:T(8,128)(2,1)S(1)} %shard_map.127.refs_2_), channel_id=1, source_target_pairs={{0,4},{4,8},{8,12},{12,0},{1,5},{5,9},{9,13},{13,1},{2,6},{6,10},{... | collective-permute-start | bytes 61448 | tf_op jit(solution)/shard_map/ppermute | solution.py:615
  60.4 4.7 %collective-permute-start.14 = (bf16[80,128]{1,0:T(8,128)(2,1)S(1)}, bf16[80,128]{1,0:T(8,128)(2,1)S(1)}, u32[]{:S(2)}, u32[]{:S(2)}) collective-permute-start(bf16[80,128]{1,0:T(8,128)(2,1)S(1)} %shard_map.127.refs_2_), channel_id=1, source_target_pairs={{0,12},{4,0},{8,4},{12,8},{1,13},{5,1},{9,5},{13,9},{2,14},{6,2},{... | collective-permute-start | bytes 61448 | tf_op jit(solution)/shard_map/ppermute | solution.py:615
  63.4 4.7 %collective-permute-start.15 = (bf16[80,128]{1,0:T(8,128)(2,1)S(1)}, bf16[80,128]{1,0:T(8,128)(2,1)S(1)}, u32[]{:S(2)}, u32[]{:S(2)}) collective-permute-start(bf16[80,128]{1,0:T(8,128)(2,1)S(1)} %shard_map.127.refs_2_), channel_id=1, source_target_pairs={{0,8},{4,12},{8,0},{12,4},{1,9},{5,13},{9,1},{13,5},{2,10},{6,14},... | collective-permute-start | bytes 61448 | tf_op jit(solution)/shard_map/ppermute | solution.py:615
  63.9 13.9 %collective-permute-start.16 = (bf16[80,128]{1,0:T(8,128)(2,1)S(1)}, bf16[80,128]{1,0:T(8,128)(2,1)S(1)}, u32[]{:S(2)}, u32[]{:S(2)}) collective-permute-start(bf16[80,128]{1,0:T(8,128)(2,1)S(1)} %shard_map.127.refs_2_), channel_id=1, source_target_pairs={{0,1},{1,0},{2,3},{3,2},{4,5},{5,4},{6,7},{7,6},{8,9},{9,8},{10,11... | collective-permute-start | bytes 61448 | tf_op jit(solution)/shard_map/ppermute | solution.py:352
  65.1 12.7 %collective-permute-start.17 = (bf16[80,128]{1,0:T(8,128)(2,1)S(1)}, bf16[80,128]{1,0:T(8,128)(2,1)S(1)}, u32[]{:S(2)}, u32[]{:S(2)}) collective-permute-start(bf16[80,128]{1,0:T(8,128)(2,1)S(1)} %collective-permute-done.13.refs_3_), channel_id=1, source_target_pairs={{0,1},{1,0},{2,3},{3,2},{4,5},{5,4},{6,7},{7,6},{8,9},{9,8},{10,11... | collective-permute-start | bytes 61448 | tf_op jit(solution)/shard_map/ppermute | solution.py:352
  65.1 12.7 %collective-permute-start.18 = (bf16[80,128]{1,0:T(8,128)(2,1)S(1)}, bf16[80,128]{1,0:T(8,128)(2,1)S(1)}, u32[]{:S(2)}, u32[]{:S(2)}) collective-permute-start(bf16[80,128]{1,0:T(8,128)(2,1)S(1)} %collective-permute-done.14.refs_4_), channel_id=1, source_target_pairs={{0,1},{1,0},{2,3},{3,2},{4,5},{5,4},{6,7},{7,6},{8,9},{9,8},{10,11... | collective-permute-start | bytes 61448 | tf_op jit(solution)/shard_map/ppermute | solution.py:352
  68.1 9.8 %collective-permute-start.19 = (bf16[80,128]{1,0:T(8,128)(2,1)S(1)}, bf16[80,128]{1,0:T(8,128)(2,1)S(1)}, u32[]{:S(2)}, u32[]{:S(2)}) collective-permute-start(bf16[80,128]{1,0:T(8,128)(2,1)S(1)} %collective-permute-done.15.refs_5_), channel_id=1, source_target_pairs={{0,1},{1,0},{2,3},{3,2},{4,5},{5,4},{6,7},{7,6},{8,9},{9,8},{10,11... | collective-permute-start | bytes 61448 | tf_op jit(solution)/shard_map/ppermute | solution.py:352

commit v3 on v2

v3 whole, which is shorter than its diff:
```python
import jax
import jax.numpy as jnp
import numpy as np
from jax import lax
from jax.experimental import pallas as pl
from jax.experimental.pallas import tpu as pltpu
from jax.sharding import PartitionSpec as P

F32 = jnp.float32
BF16 = jnp.bfloat16
I16 = jnp.int16
WELL_HEIGHT = 1.0
STRAIN_COUPLING = 4.0
TIME_STEP = 0.01
DAMAGE_RATE = 0.8
ENERGY_CRITICAL = 0.02

OFF = 16
A_CODE = (0.0, 1.0)
B_CODE = (-1.1, 3.1)
SUM_LOW, SUM_SPAN = -1280.0, 4096.0

VMEM = pl.BlockSpec(memory_space=pltpu.VMEM)
SMEM = pl.BlockSpec(memory_space=pltpu.SMEM)
HBM = pl.BlockSpec(memory_space=pltpu.HBM)


def to_code(x, code):
    low, span = code
    v = (x - low) * (65535.0 / span) - 32768.0
    return jnp.clip(jnp.round(v), -32768.0, 32767.0).astype(jnp.int32).astype(I16)


def from_code(q, code):
    low, span = code
    return q.astype(jnp.int32).astype(F32) * (span / 65535.0) + (low + 32768.0 * span / 65535.0)


def sum_digits(s):
    v = (s[0:2] - SUM_LOW) * (65536.0 / SUM_SPAN)
    high = jnp.floor(v)
    low = jnp.minimum(jnp.floor((v - high) * 65536.0), 65535.0)
    rows = jnp.concatenate([high, low, jnp.full((12, s.shape[1]), 32768.0, F32)]) - 32768.0
    return rows.astype(jnp.int32).astype(I16)


def from_digits(tile):
    v = tile.astype(jnp.int32).astype(F32) + 32768.0
    return (v[0:2] + v[2:4] * (1.0 / 65536.0)) * (SUM_SPAN / 65536.0) + SUM_LOW


def by_label(labels, values):
    return jnp.where(labels == 0, values[0], jnp.where(labels == 1, values[1], values[2])).astype(F32)


FACTORS = (1.0, 0.3, 0.05)
ROOTS = tuple(float(np.sqrt(np.float32(v))) for v in FACTORS)


def call(kernel, outs, *args, in_specs=None, out_specs=None, scratch=(), mib=16):
    return pl.pallas_call(
        kernel,
        in_specs=in_specs or [VMEM] * len(args),
        out_specs=out_specs or [VMEM] * len(outs),
        out_shape=[jax.ShapeDtypeStruct(s, t) for s, t in outs],
        scratch_shapes=scratch,
        compiler_params=pltpu.CompilerParams(vmem_limit_bytes=mib * 1024 * 1024),
    )(*args)


def chunks(start, stop, size):
    return [(r, min(size, stop - r)) for r in range(start, stop, size)]


def fold(x):
    return x.reshape(x.shape[0] // 8, 8, x.shape[1]).sum(0)


def to_rows(top, bottom):
    return jnp.concatenate([jnp.sum(top, 0, keepdims=True), jnp.sum(bottom, 0, keepdims=True),
                            jnp.zeros((6, top.shape[1]), F32)])


def first_kernel(c_hbm, d_hbm, l_hbm, f_ref, amp_ref, lo1_ref, hi1_ref, lo2_ref, hi2_ref, sum_ref,
                 d_ref, l_ref, sems):
    nx, ny, nz = f_ref.shape
    order = [0, nx - 1] + list(range(1, nx - 1))
    copies = []
    for x in order:
        copies.append([pltpu.make_async_copy(src.at[x], dst.at[x], sems.at[k, x])
                       for k, (src, dst) in enumerate(((c_hbm, f_ref), (d_hbm, d_ref), (l_hbm, l_ref)))])
        for c in copies[-1]:
            c.start()
    top = jnp.zeros((8, nz), F32)
    bottom = jnp.zeros((8, nz), F32)
    for k, x in enumerate(order):
        for c in copies[k]:
            c.wait()
        for r, n in chunks(0, ny, 48):
            f = f_ref[x, r:r + n, :]
            a = by_label(l_ref[x, r:r + n, :], ROOTS) * (1.0 - d_ref[x, r:r + n, :])
            amp_ref[x, r:r + n, :] = a
            m = a * a
            top = top + fold(m * f)
            bottom = bottom + fold(m)
            for near, far, first, second in ((0, 1, lo1_ref, lo2_ref), (nx - 1, nx - 2, hi1_ref, hi2_ref)):
                if x == near:
                    first[r:r + n, :] = to_code(f, A_CODE)
                    second[1, r:r + n, :] = to_code(a, A_CODE)
                if x == far:
                    second[0, r:r + n, :] = to_code(f, A_CODE)
    s = to_rows(top, bottom)
    sum_ref[...] = s
    lo1_ref[ny:ny + 16, :] = sum_digits(s)
    hi1_ref[ny:ny + 16, :] = sum_digits(s)


def edge_rows(code, ride_x, with_amp):
    def kernel(*refs):
        f_ref = refs[0]
        amp_ref = refs[1] if with_amp else None
        lo_ref, hi_ref, s_ref, far_ref = refs[1 + with_amp:5 + with_amp]
        out_ref = refs[-1]
        nx, ny, nz = f_ref.shape
        low_rows = [from_code(r[0:16, :], code)[0:1] for r in (lo_ref, hi_ref)]
        high_rows = [from_code(r[ny - 16:ny, :], code)[15:16] for r in (lo_ref, hi_ref)]
        s = s_ref[...]
        if ride_x:
            s = s + far_ref[...]
        for side, first, second, beside in ((0, 0, 1, low_rows), (1, ny - 1, ny - 2, high_rows)):
            for x in range(nx):
                out_ref[side, 2 * x:2 * x + 1, :] = f_ref[x, first:first + 1, :]
                out_ref[side, 2 * x + 1:2 * x + 2, :] = f_ref[x, second:second + 1, :]
                if amp_ref is not None:
                    out_ref[side, 10 + x:11 + x, :] = amp_ref[x, first:first + 1, :]
            out_ref[side, 8:9, :] = beside[0]
            out_ref[side, 9:10, :] = beside[1]
            out_ref[side, 16:24, :] = s
            if ride_x:
                out_ref[side, 16:18, :] = (s[0:2] + from_digits(lo_ref[ny:ny + 16, :])
                                           + from_digits(hi_ref[ny:ny + 16, :]))
    return kernel


def assemble(code, ride_y, with_amp):
    def kernel(*refs):
        f_ref = refs[0]
        amp_ref = refs[1] if with_amp else None
        lo_ref, hi_ref, yr_ref, yp_ref, pad_ref = refs[1 + with_amp:6 + with_amp]
        apad_ref = refs[7] if with_amp else None
        zp_ref = refs[-1]
        nx, ny, nz = f_ref.shape
        end = OFF + ny
        lane = lax.broadcasted_iota(jnp.int32, (1, nz), 1)
        outer = (lane < 16) | (lane >= nz - 16)
        for p, ref in ((0, lo_ref), (nx + 1, hi_ref)):
            for r, n in chunks(0, ny, 48):
                f = from_code(ref[r:r + n, :], code)
                pad_ref[p, OFF + r:OFF + r + n, :] = f
                zp_ref[p, OFF + r:OFF + r + n, :] = f
        for p, k in ((0, 8), (nx + 1, 9)):
            pad_ref[p, OFF - 1:OFF, :] = yr_ref[1, k:k + 1, :]
            pad_ref[p, end:end + 1, :] = yr_ref[0, k:k + 1, :]
        for x in range(nx):
            for r, n in chunks(0, ny, 48):
                f = f_ref[x, r:r + n, :]
                pad_ref[x + 1, OFF + r:OFF + r + n, :] = f
                if amp_ref is not None:
                    a = amp_ref[x, r:r + n, :]
                    apad_ref[x, OFF + r:OFF + r + n, :] = a
                    f = jnp.where(outer, f, pltpu.roll(a, nz // 2, 1))
                zp_ref[x + 1, OFF + r:OFF + r + n, :] = f
            for side, near, far in ((1, OFF - 1, OFF - 2), (0, end, end + 1)):
                f = yr_ref[side, 2 * x:2 * x + 1, :]
                pad_ref[x + 1, near:near + 1, :] = f
                pad_ref[x + 1, far:far + 1, :] = yr_ref[side, 2 * x + 1:2 * x + 2, :]
                if amp_ref is not None:
                    apad_ref[x, near:near + 1, :] = yr_ref[side, 10 + x:11 + x, :]
                zp_ref[x + 1, near:near + 1, :] = f
        s = yp_ref[0, 16:24, :]
        if ride_y:
            s = s + yr_ref[0, 16:24, :]
        zp_ref[0, 0:8, :] = s
        pad_ref[0, 0:8, :] = s
    return kernel


def weighted_mean(pad_ref, zr_ref, ride_z):
    s = pad_ref[0, 0:8, :]
    if ride_z:
        s = s + zr_ref[0, 0:8, :]
    return jnp.sum(s[0:1], keepdims=True) / jnp.sum(s[1:2], keepdims=True)


def worn(a, m, f, mean):
    e = f - mean
    energy = 0.5 * STRAIN_COUPLING * m * e * e
    return a * (1.0 - DAMAGE_RATE * jnp.maximum(energy - ENERGY_CRITICAL, 0.0))


class Geometry:
    def __init__(self, nx, ny, nz):
        self.nx, self.ny, self.nz = nx, ny, nz
        self.lane = lax.broadcasted_iota(jnp.int32, (1, nz), 1)
        self.first = self.lane == 0
        self.last = self.lane == nz - 1

    def before(self, own, other):
        return pltpu.roll(jnp.where(self.last, other, own), 1, 1)

    def after(self, own, other):
        return pltpu.roll(jnp.where(self.first, other, own), self.nz - 1, 1)


def chem_of(f, m, around, mean):
    well = 2.0 * WELL_HEIGHT * f * (1.0 - f) * (1.0 - 2.0 * f)
    return well + 6.0 * f - around + STRAIN_COUPLING * m * (f - mean)


def chemistry(g, pad_ref, lo2_ref, hi2_ref, code, mob_ref, mobe_ref, zr_ref, chem_ref, cheme_ref, mean):
    nx, ny = g.nx, g.ny

    def plane(p, r, n):
        if p < 0:
            return from_code(lo2_ref[0, r - OFF:r - OFF + n, :], code)
        if p > nx + 1:
            return from_code(hi2_ref[0, r - OFF:r - OFF + n, :], code)
        return pad_ref[p, r:r + n, :]

    for p in range(nx + 2):
        inside = 1 <= p <= nx
        rows = chunks(OFF - 8, OFF + ny + 8, 32) if inside else chunks(OFF, OFF + ny, 48)
        for r, n in rows:
            f = pad_ref[p, r:r + n, :]
            e = zr_ref[p, r:r + n, :]
            around = (plane(p - 1, r, n) + plane(p + 1, r, n)
                      + pad_ref[p, r - 1:r - 1 + n, :] + pad_ref[p, r + 1:r + 1 + n, :]
                      + g.before(f, e) + g.after(f, e))
            chem_ref[p, r:r + n, :] = chem_of(f, mob_ref[p, r:r + n, :], around, mean)
        if inside:
            for r, n in chunks(OFF, OFF + ny, 48):
                f = pad_ref[p, r:r + n, :]
                e = zr_ref[p, r:r + n, :]
                around = (zr_ref[p - 1, r:r + n, :] + zr_ref[p + 1, r:r + n, :]
                          + zr_ref[p, r - 1:r - 1 + n, :] + zr_ref[p, r + 1:r + 1 + n, :]
                          + g.before(e, f) + g.after(e, f))
                cheme_ref[p - 1, r - OFF:r - OFF + n, :] = chem_of(
                    e, mobe_ref[p - 1, r - OFF:r - OFF + n, :], around, mean)


def flux_of(g, x, r, n, mob_ref, mobe_ref, chem_ref, cheme_ref):
    p = x + 1
    m = mob_ref[p, r:r + n, :]
    q = chem_ref[p, r:r + n, :]
    me = mobe_ref[x, r - OFF:r - OFF + n, :]
    qe = cheme_ref[x, r - OFF:r - OFF + n, :]
    total = None
    for nm, nq in (
        (mob_ref[p - 1, r:r + n, :], chem_ref[p - 1, r:r + n, :]),
        (mob_ref[p + 1, r:r + n, :], chem_ref[p + 1, r:r + n, :]),
        (mob_ref[p, r - 1:r - 1 + n, :], chem_ref[p, r - 1:r - 1 + n, :]),
        (mob_ref[p, r + 1:r + 1 + n, :], chem_ref[p, r + 1:r + 1 + n, :]),
        (g.before(m, me), g.before(q, qe)),
        (g.after(m, me), g.after(q, qe)),
    ):
        term = (nm + m) * (nq - q)
        total = term if total is None else total + term
    return m, 0.5 * total


def step_a(ride_z):
    def kernel(pad_ref, apad_ref, lo2_ref, hi2_ref, zr_ref,
               f2_ref, a2_ref, ae2_ref, lo1_out, hi1_out, lo2_out, hi2_out, sum_ref,
               mob_ref, mobe_ref, chem_ref, cheme_ref):
        nx, ny, nz = f2_ref.shape
        g = Geometry(nx, ny, nz)
        mean = weighted_mean(pad_ref, zr_ref, ride_z)
        for p in range(nx + 2):
            inside = 1 <= p <= nx
            rows = chunks(OFF - 8, OFF + ny + 8, 32) if inside else chunks(OFF, OFF + ny, 48)
            for r, n in rows:
                if inside:
                    a = apad_ref[p - 1, r:r + n, :]
                else:
                    a = from_code((lo2_ref if p == 0 else hi2_ref)[1, r - OFF:r - OFF + n, :], A_CODE)
                m = a * a
                mob_ref[p, r:r + n, :] = m
                a2_ref[p, r:r + n, :] = worn(a, m, pad_ref[p, r:r + n, :], mean)
            if inside:
                for r, n in chunks(OFF, OFF + ny, 48):
                    e = zr_ref[p, r:r + n, :]
                    a = pltpu.roll(e, nz // 2, 1)
                    m = a * a
                    mobe_ref[p - 1, r - OFF:r - OFF + n, :] = m
                    ae2_ref[p - 1, r - OFF:r - OFF + n, :] = worn(a, m, e, mean)
        chemistry(g, pad_ref, lo2_ref, hi2_ref, A_CODE, mob_ref, mobe_ref, zr_ref, chem_ref, cheme_ref, mean)
        top = jnp.zeros((8, nz), F32)
        bottom = jnp.zeros((8, nz), F32)
        for x in range(nx):
            for r, n in chunks(OFF, OFF + ny, 48):
                _, flux = flux_of(g, x, r, n, mob_ref, mobe_ref, chem_ref, cheme_ref)
                f = pad_ref[x + 1, r:r + n, :] + TIME_STEP * flux
                s = slice(r - OFF, r - OFF + n)
                f2_ref[x, s, :] = f
                a = a2_ref[x + 1, r:r + n, :]
                m = a * a
                top = top + fold(m * f)
                bottom = bottom + fold(m)
                for near, far, first, second in ((0, 1, lo1_out, lo2_out), (nx - 1, nx - 2, hi1_out, hi2_out)):
                    if x == near:
                        first[s, :] = to_code(f, B_CODE)
                    if x == far:
                        second[0, s, :] = to_code(f, B_CODE)
        s = to_rows(top, bottom)
        sum_ref[...] = s
        lo1_out[ny:ny + 16, :] = sum_digits(s)
        hi1_out[ny:ny + 16, :] = sum_digits(s)
    return kernel


def step_b(ride_z):
    def kernel(pad_ref, a2_ref, ae2_ref, lo2_ref, hi2_ref, zr_ref, l_hbm,
               f3_hbm, dmg_hbm, flux_hbm, pool_ref, edge_ref,
               mob_ref, mobe_ref, chem_ref, cheme_ref, pool_scr, l_ref, f3_ref, dmg_ref, flux_ref, l_sem, sems):
        nx, ny, nz = f3_ref.shape
        labels_in = pltpu.make_async_copy(l_hbm, l_ref, l_sem)
        labels_in.start()
        g = Geometry(nx, ny, nz)
        mean = weighted_mean(pad_ref, zr_ref, ride_z)
        for p in range(nx + 2):
            inside = 1 <= p <= nx
            rows = chunks(OFF - 8, OFF + ny + 8, 32) if inside else chunks(OFF, OFF + ny, 48)
            for r, n in rows:
                a = a2_ref[p, r:r + n, :]
                mob_ref[p, r:r + n, :] = a * a
            if inside:
                for r, n in chunks(0, ny, 48):
                    a = ae2_ref[p - 1, r:r + n, :]
                    mobe_ref[p - 1, r:r + n, :] = a * a
        chemistry(g, pad_ref, lo2_ref, hi2_ref, B_CODE, mob_ref, mobe_ref, zr_ref, chem_ref, cheme_ref, mean)
        labels_in.wait()
        copies = []
        for k, (r, n) in enumerate(chunks(OFF, OFF + ny, 48)):
            s = slice(r - OFF, r - OFF + n)
            pooled = [None] * 4
            for x in range(nx):
                m, flux = flux_of(g, x, r, n, mob_ref, mobe_ref, chem_ref, cheme_ref)
                f0 = pad_ref[x + 1, r:r + n, :]
                f = f0 + TIME_STEP * flux
                a = worn(a2_ref[x + 1, r:r + n, :], m, f0, mean)
                labels = l_ref[x, s, :]
                factor = by_label(labels, FACTORS)
                dmg = 1.0 - a * by_label(labels, tuple(1.0 / v for v in ROOTS))
                f3_ref[x, s, :] = f
                dmg_ref[x, s, :] = dmg
                flux_ref[x, s, :] = flux
                for i, v in enumerate((f, dmg, a * a, factor)):
                    pooled[i] = v if pooled[i] is None else pooled[i] + v
            for i in range(4):
                pool_scr[i, s, :] = pooled[i]
            for i, (src, dst) in enumerate(((f3_ref, f3_hbm), (dmg_ref, dmg_hbm), (flux_ref, flux_hbm))):
                copies.append(pltpu.make_async_copy(src.at[:, s, :], dst.at[:, s, :], sems.at[i, k]))
                copies[-1].start()
        py, pz = ny // 4, nz // 4
        zin = lax.broadcasted_iota(jnp.int32, (nz, 4 * pz), 0)
        out = lax.broadcasted_iota(jnp.int32, (nz, 4 * pz), 1)
        total = jnp.zeros((py, 4 * pz), F32)
        for i in range(4):
            rows = (pool_scr[i, pl.ds(0, py, stride=4), :] + pool_scr[i, pl.ds(1, py, stride=4), :]
                    + pool_scr[i, pl.ds(2, py, stride=4), :] + pool_scr[i, pl.ds(3, py, stride=4), :])
            pick = jnp.where((zin // 4 == out // 4) & (out % 4 == i), 1.0 / 64.0, 0.0).astype(F32)
            total = total + jnp.dot(rows, pick, precision=lax.Precision.HIGHEST, preferred_element_type=F32)
        pool_ref[...] = total.astype(BF16)
        blank = jnp.zeros((13, 4 * pz), F32)
        edge_ref[0] = jnp.concatenate([total[0:3], blank]).astype(BF16)
        edge_ref[1] = jnp.concatenate([total[py - 3:py], blank]).astype(BF16)
        for c in copies:
            c.wait()
    return kernel


def ring(axis, shift):
    count = lax.axis_size(axis)
    return [(i, (i + shift) % count) for i in range(count)]


def pair_sum(s, axis):
    count = lax.axis_size(axis)
    if count & (count - 1):
        return lax.psum(s, axis)
    bit = 1
    while bit < count:
        s = s + lax.ppermute(s, axis, [(i, i ^ bit) for i in range(count)])
        bit *= 2
    return s


def both_sides(pay, axis):
    if lax.axis_size(axis) == 2:
        return lax.ppermute(pay, axis, ring(axis, 1))
    return jnp.stack([lax.ppermute(pay[0], axis, ring(axis, -1)), lax.ppermute(pay[1], axis, ring(axis, 1))])


def z_neighbour(pay, axis, packed=True):
    if lax.axis_size(axis) == 2:
        return lax.ppermute(pay, axis, ring(axis, 1))
    above = lax.ppermute(pay, axis, ring(axis, -1))
    below = lax.ppermute(pay, axis, ring(axis, 1))
    lane = lax.broadcasted_iota(jnp.int32, pay.shape, pay.ndim - 1)
    part = pay.shape[-1] // (4 if packed else 2)
    return jnp.where(lane // part % 2 == 0, above, below)


def x_sides(lo, hi):
    return lax.ppermute(hi, "gx", ring("gx", 1)), lax.ppermute(lo, "gx", ring("gx", -1))


def body(concentration, damage, labels, w_first, b_first, w_second, b_second, w_third, b_third):
    nx, ny, nz = concentration.shape
    rows = ny + 2 * OFF
    block = (nx, ny, nz)
    padded = (nx + 2, rows, nz)
    ride_x = lax.axis_size("gx") == 4
    ride_y = lax.axis_size("gy") == 2
    ride_z = lax.axis_size("gz") == 2
    scratch = [pltpu.VMEM(padded, F32), pltpu.VMEM(block, F32), pltpu.VMEM(padded, F32), pltpu.VMEM(block, F32)]

    def start(sums):
        if ride_x:
            far = lax.ppermute(sums, "gx", ring("gx", 2))
        else:
            sums = far = pair_sum(sums, "gx")
        for axis, ride in (("gy", ride_y), ("gz", ride_z)):
            if not ride:
                assert not ride_x
                sums = far = pair_sum(sums, axis)
        return sums, far

    f, amp, lo1, hi1, lo2, hi2, sums = call(
        first_kernel,
        [(block, F32), (block, F32), ((ny + 16, nz), I16), ((ny + 16, nz), I16),
         ((2, ny, nz), I16), ((2, ny, nz), I16), ((8, nz), F32)],
        concentration, damage, labels,
        in_specs=[HBM] * 3,
        scratch=[pltpu.VMEM(block, F32), pltpu.VMEM(block, jnp.int32), pltpu.SemaphoreType.DMA((3, nx))])
    matrices = weight_matrices(w_first, b_first, w_second, b_second, w_third, nz, nz // 4)
    sums, far = start(sums)
    lo1, hi1 = x_sides(lo1, hi1)
    lo2, hi2 = x_sides(lo2, hi2)
    (ypay,) = call(edge_rows(A_CODE, ride_x, True), [((2, 24, nz), F32)], f, amp, lo1, hi1, sums, far, matrices[-1])
    yr = both_sides(ypay, "gy")
    pad, apad, zpay = call(
        assemble(A_CODE, ride_y, True), [(padded, F32), ((nx, rows, nz), F32), (padded, F32)],
        f, amp, lo1, hi1, yr, ypay)
    zr = z_neighbour(zpay, "gz")
    f2, a2, ae2, lo1, hi1, lo2, hi2, sums = call(
        step_a(ride_z),
        [(block, F32), (padded, F32), (block, F32), ((ny + 16, nz), I16), ((ny + 16, nz), I16),
         ((1, ny, nz), I16), ((1, ny, nz), I16), ((8, nz), F32)],
        pad, apad, lo2, hi2, zr, scratch=scratch)

    sums, far = start(sums)
    lo1, hi1 = x_sides(lo1, hi1)
    lo2, hi2 = x_sides(lo2, hi2)
    (ypay,) = call(edge_rows(B_CODE, ride_x, False), [((2, 24, nz), F32)], f2, lo1, hi1, sums, far)
    yr = both_sides(ypay, "gy")
    pad, zpay = call(assemble(B_CODE, ride_y, False), [(padded, F32), (padded, F32)], f2, lo1, hi1, yr, ypay)
    zr = z_neighbour(zpay, "gz")
    fraction, damage_field, flux_sum, pooled, edge = call(
        step_b(ride_z),
        [(block, F32), (block, F32), (block, F32), ((ny // 4, nz), BF16), ((2, 16, nz), BF16)],
        pad, a2, ae2, lo2, hi2, zr, labels,
        in_specs=[VMEM] * 6 + [HBM], out_specs=[HBM] * 3 + [VMEM] * 2,
        scratch=scratch + [
            pltpu.VMEM((4, ny, nz), F32), pltpu.VMEM(block, jnp.int32),
            pltpu.VMEM(block, F32), pltpu.VMEM(block, F32), pltpu.VMEM(block, F32),
            pltpu.SemaphoreType.DMA, pltpu.SemaphoreType.DMA((3, len(chunks(OFF, OFF + ny, 48))))])
    ids = jnp.stack([lax.axis_index(a) for a in ("gx", "gy", "gz")])
    crack_score = detector(pooled, edge, ids, matrices, b_third, ny // 4, nz // 4)
    return (fraction, damage_field, flux_sum, crack_score)


CH = 16
CIN = 4
TOP = 8


def iota(shape, dim):
    return lax.broadcasted_iota(jnp.int32, shape, dim)


def lanes_for(n):
    return -(-n // 128) * 128


def one_hot(mask):
    return jnp.where(mask, 1.0, 0.0).astype(BF16)


def mm(a, b):
    return jnp.dot(a, b, preferred_element_type=F32)


def weight_kernel(w1_ref, w2_ref, w3_ref, b1_ref, b2_ref, t1_ref, t2_ref, t3_ref, bias_ref):
    k1 = t1_ref.shape[1] // 3
    n1 = t1_ref.shape[2]
    pz = k1 // (2 * CIN)
    spread = one_hot(iota((CH, 128), 1) % CH == iota((CH, 128), 0))
    tile1 = mm(w1_ref[...], spread)
    tile2 = mm(w2_ref[...], spread)
    tile3 = mm(w3_ref[...], one_hot(iota((3, 128), 1) // pz == iota((3, 128), 0)))
    step1 = iota((16, 128), 0) // CIN - iota((16, 128), 1) // CH
    step2 = -(iota((16, 128), 1) // CH)
    step3 = -(iota((16, 128), 1) % pz)

    def tile(source, base, stride, step, shift):
        out = jnp.zeros((16, 128), F32)
        for l in range(3):
            k = base + stride * l
            out = jnp.where(step + shift == l, source[16 * k:16 * k + 16], out)
        return out.astype(BF16)

    zero = jnp.zeros((16, 128), BF16)
    for i in range(3):
        for j in range(3):
            tap = 9 * i + 3 * j
            known = {}
            for rb in range(k1 // 16):
                z_in = rb * 16 // CIN
                z_in = z_in if z_in < pz + pz // 2 else z_in - 2 * pz
                for cb in range(n1 // 128):
                    shift = z_in - cb * 8 + 3
                    near = -4 < shift < 10
                    if near and shift not in known:
                        known[shift] = tile(tile1, tap, 1, step1, shift)
                    t1_ref[i, j * k1 + rb * 16:j * k1 + rb * 16 + 16, cb * 128:(cb + 1) * 128] = (
                        known[shift] if near else zero)
            for rb in range(16):
                t2_ref[i, j * 256 + rb * 16:j * 256 + rb * 16 + 16, :] = (
                    tile(tile2, tap, 1, step2, rb) if rb < 10 else zero)
        for rb in range(t3_ref.shape[1] // 16):
            t3_ref[i, rb * 16:rb * 16 + 16, :] = tile(tile3, 3 * i, 1, step3, rb) if rb < pz + 2 else zero
    wide = one_hot(iota((CH, n1), 1) % CH == iota((CH, n1), 0)).astype(F32)
    for k, ref in ((0, b1_ref), (1, b2_ref)):
        bias_ref[k:k + 1, :] = jnp.dot(ref[...], wide, precision=lax.Precision.HIGHEST, preferred_element_type=F32)


def weight_matrices(w_first, b_first, w_second, b_second, w_third, half, pz):
    width = lanes_for((pz + 4) * CH)
    rows1 = jnp.tile(jnp.swapaxes(w_first, 1, 2), (1, 16 // CIN, 1)).reshape(27 * 16, CH)
    rows2 = jnp.swapaxes(w_second, 1, 2).reshape(27 * CH, CH)
    rows3 = w_third.reshape(3, 3, 3, CH).transpose(0, 2, 3, 1).reshape(9 * CH, 3)
    return call(
        weight_kernel,
        [((3, 6 * half, width), BF16), ((3, 768, 128), BF16), ((3, width, 128), BF16), ((8, width), F32)],
        rows1, rows2, rows3, b_first[None], b_second[None])


def gelu(x):
    return 0.5 * x * (1.0 + jnp.tanh(0.7978845608028654 * (x + 0.044715 * (x * x * x))))


def plane_kernel(py, y_count):
    def kernel(ids_ref, pool_ref, yr_ref, out_ref, scr_ref):
        iy = ids_ref[1]
        scr_ref[...] = jnp.zeros(scr_ref.shape, F32)
        scr_ref[TOP:TOP + py, :] = pool_ref[0:py, :].astype(F32)
        below = yr_ref[1].astype(F32)[0:3]
        above = yr_ref[0].astype(F32)[0:3]
        scr_ref[TOP - 3:TOP, :] = jnp.where(iy > 0, below, 0.0)
        scr_ref[TOP + py:TOP + py + 3, :] = jnp.where(iy < y_count - 1, above, 0.0)
        out_ref[...] = scr_ref[...].astype(BF16)
    return kernel


def conv_kernel(py, counts, shifts):
    x_count, y_count, z_count = counts
    n = len(shifts)

    def kernel(*refs):
        ids_ref, b3_ref = refs[:2]
        own = refs[2:3 + n]
        other = refs[3 + n:4 + 2 * n]
        t1_ref, t2_ref, t3_ref, bias_ref, out_ref = refs[4 + 2 * n:9 + 2 * n]
        in_ref, lhs1_ref, act1_ref, lhs2_ref, act2_ref, tail_ref = refs[9 + 2 * n:]
        ix, iy, iz = ids_ref[0], ids_ref[1], ids_ref[2]
        half = own[0].shape[1]
        pz = half // CIN
        rows = py + 4
        z_row = iota((1, half), 1) // CIN
        z_ok = ((z_row < pz // 2) & (iz < z_count - 1)) | ((z_row >= pz // 2) & (iz > 0))
        for w in range(7):
            o = w - 3
            k = 0 if o == 0 else 1 + shifts.index((-o) % x_count) if (-o) % x_count in shifts else None
            if k is None:
                in_ref[w] = jnp.zeros(in_ref.shape[1:], F32)
                continue
            inside = (ix + o >= 0) & (ix + o < x_count)
            in_ref[w, :, 0:half] = jnp.where(inside, own[k][...].astype(F32), 0.0)
            in_ref[w, :, half:] = jnp.where(z_ok & inside, other[k][...].astype(F32), 0.0)
        k1 = 2 * half
        for w in range(7):
            for j in range(3):
                start = TOP - 3 + j
                lhs1_ref[w, :, j * k1:(j + 1) * k1] = in_ref[w, start:start + rows, :].astype(BF16)
        out = None
        for i in range(3):
            part = mm(lhs1_ref[i:i + 5].reshape(5 * rows, 3 * k1), t1_ref[i])
            out = part if out is None else out + part
        width = out.shape[1]
        y = iota((rows, width), 0) - 2
        z = iota((rows, width), 1) // CH - 2
        ok = (z < pz + 2) & ((y >= 0) | (iy > 0)) & ((y < py) | (iy < y_count - 1))
        ok = ok & ((z >= 0) | (iz > 0)) & ((z < pz) | (iz < z_count - 1))
        for p in range(5):
            a = gelu(out[p * rows:(p + 1) * rows] + bias_ref[0:1, :])
            good = ok & (ix + p - 2 >= 0) & (ix + p - 2 < x_count)
            act1_ref[p, 0:rows, 0:width] = jnp.where(good, a, 0.0)
            act1_ref[p, rows:, 0:width] = jnp.zeros((act1_ref.shape[1] - rows, width), F32)
            act1_ref[p, :, width:] = jnp.zeros((act1_ref.shape[1], act1_ref.shape[2] - width), F32)
        blocks = lhs2_ref.shape[1]
        for p in range(5):
            for j in range(3):
                a = act1_ref[p, j:j + rows, :].astype(BF16)
                for b in range(blocks):
                    lhs2_ref[p, b, :, j * 256:(j + 1) * 256] = a[:, b * 128:b * 128 + 256]
        out = None
        for i in range(3):
            part = mm(lhs2_ref[i:i + 3].reshape(3 * blocks * rows, 768), t2_ref[i])
            out = part if out is None else out + part
        for b in range(blocks):
            y = iota((rows, 128), 0) - 1
            z = (iota((rows, 128), 1) + b * 128) // CH - 1
            ok = (z < pz + 1) & (y <= py) & ((y >= 0) | (iy > 0)) & ((y < py) | (iy < y_count - 1))
            ok = ok & ((z >= 0) | (iz > 0)) & ((z < pz) | (iz < z_count - 1))
            for p in range(3):
                s = (p * blocks + b) * rows
                a = gelu(out[s:s + rows] + bias_ref[1:2, 0:128])
                good = ok & (ix + p - 1 >= 0) & (ix + p - 1 < x_count)
                act2_ref[p, :, b * 128:(b + 1) * 128] = jnp.where(good, a, 0.0).astype(BF16)
        out = None
        for i in range(3):
            part = mm(act2_ref[i], t3_ref[i])
            out = part if out is None else out + part
        tail_ref[0:rows, :] = out
        score = tail_ref[0:py, :]
        for j in (1, 2):
            score = score + pltpu.roll(tail_ref[j:j + py, :], 128 - j * pz, 1)
        out_ref[0] = jnp.transpose(score)[0:pz, :] + b3_ref[0]
    return kernel


def detector(pooled, edge, ids, matrices, b_third, py, pz):
    counts = tuple(lax.axis_size(a) for a in ("gx", "gy", "gz"))
    half = pooled.shape[1]
    assert half == 128 and pz * CIN == half and pz * 3 <= 128
    rows = py + 4
    width = lanes_for((pz + 4) * CH)
    blocks = width // 128
    yr = both_sides(edge, "gy")
    tall = -(-(TOP + py + 3) // 16) * 16
    (plane,) = call(
        plane_kernel(py, counts[1]), [((tall, half), BF16)], ids, pooled, yr,
        in_specs=[SMEM, VMEM, VMEM], scratch=[pltpu.VMEM((tall, half), F32)])
    shifts = []
    for s in (1, -1, 2, -2, 3, -3):
        if s % counts[0] and s % counts[0] not in shifts:
            shifts.append(s % counts[0])
    own = [plane] + [lax.ppermute(plane, "gx", ring("gx", s)) for s in shifts]
    other = [z_neighbour(v, "gz", False) for v in own]
    args = (ids, b_third, *own, *other, *matrices)
    (score,) = call(
        conv_kernel(py, counts, shifts), [((1, pz, py), F32)], *args,
        in_specs=[SMEM] * 2 + [VMEM] * (len(args) - 2),
        scratch=[
            pltpu.VMEM((7, tall, 2 * half), F32),
            pltpu.VMEM((7, rows, 6 * half), BF16),
            pltpu.VMEM((5, rows + 8, width + 128), F32),
            pltpu.VMEM((5, blocks, rows, 768), BF16),
            pltpu.VMEM((3, rows, width), BF16),
            pltpu.VMEM((rows + 8, 128), F32),
        ], mib=24)
    return jnp.swapaxes(score, 1, 2)


def solution(mesh):
    slab = P(("groups", "gx"), "gy", "gz")
    return jax.shard_map(
        body,
        mesh=mesh,
        in_specs=(slab, slab, slab, P(), P(), P(), P(), P(), P()),
        out_specs=(slab, slab, slab, slab),
        check_vma=False,
    )
```

time: 82.6 us -> 88.7 us (1.074)
  local copies, waits for them, and re-layouts: 5.36 us -> 18.2 us
  waiting for transfers between devices: 33.6 us -> 24.8 us
  starting transfers between devices: 22.2 us -> 26.8 us
  Pallas kernels: 19.6 us -> 16.7 us
    unnamed x26 -> x49, local copies, waits for them, and re-layouts: 5.36 us -> 16.1 us
    ppermute x8 -> x10, starting transfers between devices: 12.6 us -> 17.6 us  [the longest x4 11 us: x_sides(): lax.ppermute(lo, 'gx', ring('gx', -1))]
    ppermute x8 -> x10, waiting for transfers between devices: 18.1 us -> 13.5 us  [the longest x4 7.35 us: x_sides(): lax.ppermute(hi, 'gx', ring('gx', 1))]
    ppermute x6, waiting for transfers between devices: 4.92 us -> 0.52 us  [z_neighbour(): return lax.ppermute(pay, axis, ring(axis, 1))]
    pallas_call x10, Pallas kernels: 19.6 us -> 16.7 us  [call(): pl.pallas_call(kernel, in_specs=in_specs or [VMEM] * len(args), out_specs...]
    transpose x0 -> x3, local copies, waits for them, and re-layouts: none -> 2.01 us  [the longest x1 1.04 us: weight_matrices(): rows2 = jnp.swapaxes(w_second, 1, 2).reshape(27 * CH, CH)]
  transfers between devices with their start and end apart: 20 -> 22, of which waited for: 11 -> 10; matrix products, arithmetic and copies ran while one was open for 1% -> 3% of each run, Pallas kernels for 10% -> 1%
where the time goes in v3:
time: 88.7 us; the launch traced here: 88 us
  starting transfers between devices  26.8 us (30%)
  waiting for transfers between devices  24.8 us (28%)
  local copies, waits for them, and re-layouts  18.2 us (21%)
  Pallas kernels  16.7 us (19%)
  between operations  1.48 us (2%)
    pallas_call x10, Pallas kernels, call(): pl.pallas_call(kernel, in_specs=in_specs or [VMEM] * len(args), out_specs...  16.7 us
    unnamed x49, local copies, waits for them, and re-layouts  16.1 us
    ppermute x4, starting transfers between devices, x_sides(): lax.ppermute(lo, 'gx', ring('gx', -1))  11 us
    ppermute x4, waiting for transfers between devices, x_sides(): lax.ppermute(hi, 'gx', ring('gx', 1))  7.35 us
    ppermute x3, waiting for transfers between devices, both_sides(): return lax.ppermute(pay, axis, ring(axis, 1))  6.75 us
    ppermute x4, starting transfers between devices, x_sides(): lax.ppermute(hi, 'gx', ring('gx', 1))  5.56 us
    ppermute x3, starting transfers between devices, both_sides(): return lax.ppermute(pay, axis, ring(axis, 1))  4.68 us
    ppermute x2, waiting for transfers between devices, start(): far = lax.ppermute(sums, 'gx', ring('gx', 2))  4.51 us
  transfers between devices with their start and end apart: 22, of which 10 were waited for; matrix products, arithmetic and copies ran while one was open for 3% of the time, Pallas kernels for 1%

profile of v3, /device:TPU:0, one launch (start us, length us, event | category | flops | bytes accessed | tf_op | source)
XLA Modules:
  0.0 88.0 jit_solution(10472085111501450673)
XLA Ops:
  0.6 1.0 %copy-done = s32[4,240,128]{2,1,0:T(8,128)S(1)} copy-done((s32[4,240,128]{2,1,0:T(8,128)S(1)}, s32[4,240,128]{2,1,0:T(8,128)}, u32[]{:S(2)}) %copy-start) | copy-done | bytes 491544
  1.7 1.0 %copy-done.14 = f32[4,240,128]{2,1,0:T(8,128)S(1)} copy-done((f32[4,240,128]{2,1,0:T(8,128)S(1)}, f32[4,240,128]{2,1,0:T(8,128)}, u32[]{:S(2)}) %copy-start.14) | copy-done | bytes 491544
  2.7 1.0 %copy-done.15 = f32[4,240,128]{2,1,0:T(8,128)S(1)} copy-done((f32[4,240,128]{2,1,0:T(8,128)S(1)}, f32[4,240,128]{2,1,0:T(8,128)}, u32[]{:S(2)}) %copy-start.15) | copy-done | bytes 491544
  3.7 2.3 %shard_map.120 = (f32[4,240,128]{2,1,0:T(8,128)S(1)}, f32[4,240,128]{2,1,0:T(8,128)S(1)}, s16[256,128]{1,0:T(8,128)(2,1)S(1)}, s16[256,128]{1,0:T(8,128)(2,1)S(1...) custom-call(f32[4,240,128]{2,1,0:T(8,128)S(1)} %copy-done.14, ...), custom_call_target="tpu_custom_call" | custom-call | tf_op jit(solution)/shard_map/pallas_call | solution.py:61
  6.1 0.8 copy-done.2
  6.8 0.8 copy-done.4
  7.6 3.0 %collective-permute-start = (s16[256,128]{1,0:T(8,128)(2,1)S(1)}, s16[256,128]{1,0:T(8,128)(2,1)S(1)}, u32[]{:S(2)}, u32[]{:S(2)}) collective-permute-start(s16[256,128]{1,0:T(8,128)(2,1)S(1)} %get-tuple-element.35), channel_id=1, source_target_pairs={{0,4},{4,8},{8,12},{12,0},{1,5},{5,9},{9,13},{13,1},{2,6},{6,10},{... | collective-permute-start | bytes 196616 | tf_op jit(solution)/shard_map/ppermute | solution.py:415
  10.6 2.0 %collective-permute-start.1 = (s16[256,128]{1,0:T(8,128)(2,1)S(1)}, s16[256,128]{1,0:T(8,128)(2,1)S(1)}, u32[]{:S(2)}, u32[]{:S(2)}) collective-permute-start(s16[256,128]{1,0:T(8,128)(2,1)S(1)} %get-tuple-element.36), channel_id=1, source_target_pairs={{0,12},{4,0},{8,4},{12,8},{1,13},{5,1},{9,5},{13,9},{2,14},{6,2},{... | collective-permute-start | bytes 196616 | tf_op jit(solution)/shard_map/ppermute | solution.py:415
  12.7 1.0 %collective-permute-start.2 = (f32[8,128]{1,0:T(8,128)S(1)}, f32[8,128]{1,0:T(8,128)S(1)}, u32[]{:S(2)}, u32[]{:S(2)}) collective-permute-start(f32[8,128]{1,0:T(8,128)S(1)} %get-tuple-element.37.refs_4_), channel_id=1, source_target_pairs={{0,8},{4,12},{8,0},{12,4},{1,9},{5,13},{9,1},{13,5},{2,10},{6,14},... | collective-permute-start | bytes 12296 | tf_op jit(solution)/shard_map/ppermute | solution.py:430
  13.7 0.8 copy.16
  14.5 1.0 %copy.17 = bf16[27,16,16]{2,1,0:T(8,128)(2,1)S(1)} copy(bf16[27,16,16]{0,1,2:T(8,128)(2,1)} %bitcast.19) | data formatting | bytes 27648 | tf_op jit(solution)/shard_map/transpose | solution.py:551
  15.6 0.8 copy.18
  16.6 0.6 copy-done.20
  17.2 0.7 copy-done.21
  17.9 0.8 shard_map.121
  18.7 0.8 copy-done.10
  19.5 0.8 copy-done.16
  20.3 0.6 copy-done.18
  21.0 1.0 %copy-done.3 = f32[4,240,128]{2,1,0:T(8,128)S(1)} copy-done((f32[4,240,128]{2,1,0:T(8,128)S(1)}, f32[4,240,128]{2,1,0:T(8,128)}, u32[]{:S(2)}) %copy-start.3) | copy-done | bytes 491544
  22.0 1.0 %copy-done.5 = f32[4,240,128]{2,1,0:T(8,128)S(1)} copy-done((f32[4,240,128]{2,1,0:T(8,128)S(1)}, f32[4,240,128]{2,1,0:T(8,128)}, u32[]{:S(2)}) %copy-start.5) | copy-done | bytes 491544
  23.0 0.8 copy-done.19
  23.9 1.6 %collective-permute-start.3 = (f32[2,24,128]{2,1,0:T(8,128)S(1)}, f32[2,24,128]{2,1,0:T(8,128)S(1)}, u32[]{:S(2)}, u32[]{:S(2)}) collective-permute-start(f32[2,24,128]{2,1,0:T(8,128)S(1)} %shard_map.122.refs_5_), channel_id=1, source_target_pairs={{0,2},{2,0},{1,3},{3,1},{4,6},{6,4},{5,7},{7,5},{8,10},{10,8},{9,1... | collective-permute-start | bytes 73736 | tf_op jit(solution)/shard_map/ppermute | solution.py:400
  25.4 2.3 %collective-permute-done.3.refs_4_ = f32[2,24,128]{2,1,0:T(8,128)S(1)} collective-permute-done((f32[2,24,128]{2,1,0:T(8,128)S(1)}, f32[2,24,128]{2,1,0:T(8,128)S(1)}, u32[]{:S(2)}, u32[]{:S(2)}) %collective-permute-start.3) | collective-permute-done | bytes 24608 | tf_op jit(solution)/shard_map/ppermute | solution.py:400
  28.1 1.6 %collective-permute-start.4 = (s16[2,240,128]{2,1,0:T(8,128)(2,1)}, s16[2,240,128]{2,1,0:T(8,128)(2,1)S(1)}, u32[]{:S(2)}, u32[]{:S(2)}) collective-permute-start(s16[2,240,128]{2,1,0:T(8,128)(2,1)} %copy-done.23), channel_id=1, source_target_pairs={{0,4},{4,8},{8,12},{12,0},{1,5},{5,9},{9,13},{13,1},{2,6},{6,10},{... | collective-permute-start | bytes 368648 | tf_op jit(solution)/shard_map/ppermute | solution.py:415
  29.7 2.2 %collective-permute-start.5 = (s16[2,240,128]{2,1,0:T(8,128)(2,1)}, s16[2,240,128]{2,1,0:T(8,128)(2,1)S(1)}, u32[]{:S(2)}, u32[]{:S(2)}) collective-permute-start(s16[2,240,128]{2,1,0:T(8,128)(2,1)} %copy-done.22), channel_id=1, source_target_pairs={{0,12},{4,0},{8,4},{12,8},{1,13},{5,1},{9,5},{13,9},{2,14},{6,2},{... | collective-permute-start | bytes 368648 | tf_op jit(solution)/shard_map/ppermute | solution.py:415
  32.0 4.4 %collective-permute-done.4.lo2_ref = s16[2,240,128]{2,1,0:T(8,128)(2,1)S(1)} collective-permute-done((s16[2,240,128]{2,1,0:T(8,128)(2,1)}, s16[2,240,128]{2,1,0:T(8,128)(2,1)S(1)}, u32[]{:S(2)}, u32[]{:S(2)}) %collective-permute-start.4) | collective-permute-done | bytes 122912 | tf_op jit(solution)/shard_map/ppermute | solution.py:415
  36.3 1.6 %collective-permute-done.5.hi2_ref = s16[2,240,128]{2,1,0:T(8,128)(2,1)S(1)} collective-permute-done((s16[2,240,128]{2,1,0:T(8,128)(2,1)}, s16[2,240,128]{2,1,0:T(8,128)(2,1)S(1)}, u32[]{:S(2)}, u32[]{:S(2)}) %collective-permute-start.5) | collective-permute-done | bytes 122912 | tf_op jit(solution)/shard_map/ppermute | solution.py:415
  37.9 2.6 %shard_map.124 = (f32[4,240,128]{2,1,0:T(8,128)S(1)}, f32[6,272,128]{2,1,0:T(8,128)S(1)}, f32[4,240,128]{2,1,0:T(8,128)S(1)}, s16[256,128]{1,0:T(8,128)(2,1)S(1)...) custom-call(f32[6,272,128]{2,1,0:T(8,128)S(1)} %get-tuple-element.39, ...), custom_call_target="tpu_custom_call" | custom-call | tf_op jit(solution)/shard_map/pallas_call | solution.py:61
  40.6 0.9 %collective-permute-start.7 = (s16[256,128]{1,0:T(8,128)(2,1)S(1)}, s16[256,128]{1,0:T(8,128)(2,1)S(1)}, u32[]{:S(2)}, u32[]{:S(2)}) collective-permute-start(s16[256,128]{1,0:T(8,128)(2,1)S(1)} %get-tuple-element.45), channel_id=1, source_target_pairs={{0,4},{4,8},{8,12},{12,0},{1,5},{5,9},{9,13},{13,1},{2,6},{6,10},{... | collective-permute-start | bytes 196616 | tf_op jit(solution)/shard_map/ppermute | solution.py:415
  41.5 2.9 %collective-permute-start.8 = (s16[256,128]{1,0:T(8,128)(2,1)S(1)}, s16[256,128]{1,0:T(8,128)(2,1)S(1)}, u32[]{:S(2)}, u32[]{:S(2)}) collective-permute-start(s16[256,128]{1,0:T(8,128)(2,1)S(1)} %get-tuple-element.46), channel_id=1, source_target_pairs={{0,12},{4,0},{8,4},{12,8},{1,13},{5,1},{9,5},{13,9},{2,14},{6,2},{... | collective-permute-start | bytes 196616 | tf_op jit(solution)/shard_map/ppermute | solution.py:415
  44.4 4.5 %collective-permute-done.9.refs_4_ = f32[8,128]{1,0:T(8,128)S(1)} collective-permute-done((f32[8,128]{1,0:T(8,128)S(1)}, f32[8,128]{1,0:T(8,128)S(1)}, u32[]{:S(2)}, u32[]{:S(2)}) %collective-permute-start.9) | collective-permute-done | bytes 4128 | tf_op jit(solution)/shard_map/ppermute | solution.py:430
  48.9 1.6 %collective-permute-start.10 = (f32[2,24,128]{2,1,0:T(8,128)S(1)}, f32[2,24,128]{2,1,0:T(8,128)S(1)}, u32[]{:S(2)}, u32[]{:S(2)}) collective-permute-start(f32[2,24,128]{2,1,0:T(8,128)S(1)} %shard_map.125.refs_4_), channel_id=1, source_target_pairs={{0,2},{2,0},{1,3},{3,1},{4,6},{6,4},{5,7},{7,5},{8,10},{10,8},{9,1... | collective-permute-start | bytes 73736 | tf_op jit(solution)/shard_map/ppermute | solution.py:400
  50.5 2.3 %collective-permute-done.10.refs_3_ = f32[2,24,128]{2,1,0:T(8,128)S(1)} collective-permute-done((f32[2,24,128]{2,1,0:T(8,128)S(1)}, f32[2,24,128]{2,1,0:T(8,128)S(1)}, u32[]{:S(2)}, u32[]{:S(2)}) %collective-permute-start.10) | collective-permute-done | bytes 24608 | tf_op jit(solution)/shard_map/ppermute | solution.py:400
  52.8 1.0 %shard_map.126 = (f32[6,272,128]{2,1,0:T(8,128)S(1)}, f32[6,272,128]{2,1,0:T(8,128)}) custom-call(f32[4,240,128]{2,1,0:T(8,128)S(1)} %get-tuple-element.44.refs_0_, s16[256,128]{1,0:T(8,128)(2,1)S(1)} %collective-permute-done.7.refs_1_, s16[256,128]{1,0:T(8,128)(2,1)S(1)} %collective-permute-done.8.refs_2_, ...), custom_call_target="tpu_custom_call" | custom-call | tf_op jit(solution)/shard_map/pallas_call | solution.py:61
  53.8 0.9 %copy-done.8 = f32[6,272,128]{2,1,0:T(8,128)} copy-done((f32[6,272,128]{2,1,0:T(8,128)}, f32[6,272,128]{2,1,0:T(8,128)S(1)}, u32[]{:S(2)}) %copy-start.8) | copy-done | bytes 835608
  54.7 3.8 %collective-permute-start.12 = (s16[1,240,128]{2,1,0:T(8,128)(2,1)}, s16[1,240,128]{2,1,0:T(8,128)(2,1)}, u32[]{:S(2)}, u32[]{:S(2)}) collective-permute-start(s16[1,240,128]{2,1,0:T(8,128)(2,1)} %get-tuple-element.52), channel_id=1, source_target_pairs={{0,12},{4,0},{8,4},{12,8},{1,13},{5,1},{9,5},{13,9},{2,14},{6,2},{... | collective-permute-start | bytes 184328 | tf_op jit(solution)/shard_map/ppermute | solution.py:415
  58.6 3.0 %collective-permute-done.11.lo2_ref = s16[1,240,128]{2,1,0:T(8,128)(2,1)S(1)} collective-permute-done((s16[1,240,128]{2,1,0:T(8,128)(2,1)}, s16[1,240,128]{2,1,0:T(8,128)(2,1)S(1)}, u32[]{:S(2)}, u32[]{:S(2)}) %collective-permute-start.11) | collective-permute-done | bytes 61472 | tf_op jit(solution)/shard_map/ppermute | solution.py:415
  61.6 1.1 %copy-done.7 = f32[6,272,128]{2,1,0:T(8,128)S(1)} copy-done((f32[6,272,128]{2,1,0:T(8,128)S(1)}, f32[6,272,128]{2,1,0:T(8,128)}, u32[]{:S(2)}) %copy-start.7) | copy-done | bytes 835608
  62.7 1.1 %copy-done.9 = f32[6,272,128]{2,1,0:T(8,128)S(1)} copy-done((f32[6,272,128]{2,1,0:T(8,128)S(1)}, f32[6,272,128]{2,1,0:T(8,128)}, u32[]{:S(2)}) %copy-start.9) | copy-done | bytes 835608
  63.9 1.0 %copy-done.13 = f32[4,240,128]{2,1,0:T(8,128)S(1)} copy-done((f32[4,240,128]{2,1,0:T(8,128)S(1)}, f32[4,240,128]{2,1,0:T(8,128)}, u32[]{:S(2)}) %copy-start.13) | copy-done | bytes 491544
  64.9 4.7 %shard_map.127 = (f32[4,240,128]{2,1,0:T(8,128)}, f32[4,240,128]{2,1,0:T(8,128)}, f32[4,240,128]{2,1,0:T(8,128)}, bf16[60,128]{1,0:T(8,128)(2,1)S(1)}, bf16[2,16,128]{2,1,0:T(8,128)(2,1)S(1)}) custom-call(f32[6,272,128]{2,1,0:T(8,128)S(1)} %copy-done.9, f32[6,272,128]{2,1,0:T(8,128)S(1)} %copy-done.7, f32[4,240,128]{2,1,0:T(8,128)S(1)} %copy-done.13, ...), custom_call_target="tpu_custom_call" | custom-call | tf_op jit(solution)/shard_map/pallas_call | solution.py:61
  69.6 1.6 %collective-permute-start.14 = (bf16[2,16,128]{2,1,0:T(8,128)(2,1)S(1)}, bf16[2,16,128]{2,1,0:T(8,128)(2,1)S(1)}, u32[]{:S(2)}, u32[]{:S(2)}) collective-permute-start(bf16[2,16,128]{2,1,0:T(8,128)(2,1)S(1)} %get-tuple-element.58), channel_id=1, source_target_pairs={{0,2},{2,0},{1,3},{3,1},{4,6},{6,4},{5,7},{7,5},{8,10},{10,8},{9,1... | collective-permute-start | bytes 24584 | tf_op jit(solution)/shard_map/ppermute | solution.py:400
  71.3 2.1 %collective-permute-done.14.yr_ref = bf16[2,16,128]{2,1,0:T(8,128)(2,1)S(1)} collective-permute-done((bf16[2,16,128]{2,1,0:T(8,128)(2,1)S(1)}, bf16[2,16,128]{2,1,0:T(8,128)(2,1)S(1)}, u32[]{:S(2)}, u32[]{:S(2)}) %collective-permute-start.14) | collective-permute-done | bytes 8224 | tf_op jit(solution)/shard_map/ppermute | solution.py:400
  73.3 0.6 shard_map.128.refs_2_
  74.0 3.8 %collective-permute-start.16 = (bf16[80,128]{1,0:T(8,128)(2,1)S(1)}, bf16[80,128]{1,0:T(8,128)(2,1)S(1)}, u32[]{:S(2)}, u32[]{:S(2)}) collective-permute-start(bf16[80,128]{1,0:T(8,128)(2,1)S(1)} %shard_map.128.refs_2_), channel_id=1, source_target_pairs={{0,12},{4,0},{8,4},{12,8},{1,13},{5,1},{9,5},{13,9},{2,14},{6,2},{... | collective-permute-start | bytes 61448 | tf_op jit(solution)/shard_map/ppermute | solution.py:669
  77.9 1.7 %collective-permute-done.15.refs_3_ = bf16[80,128]{1,0:T(8,128)(2,1)S(1)} collective-permute-done((bf16[80,128]{1,0:T(8,128)(2,1)S(1)}, bf16[80,128]{1,0:T(8,128)(2,1)S(1)}, u32[]{:S(2)}, u32[]{:S(2)}) %collective-permute-start.15) | collective-permute-done | bytes 20512 | tf_op jit(solution)/shard_map/ppermute | solution.py:669
  80.1 2.4 %collective-permute-done.17.refs_5_ = bf16[80,128]{1,0:T(8,128)(2,1)S(1)} collective-permute-done((bf16[80,128]{1,0:T(8,128)(2,1)S(1)}, bf16[80,128]{1,0:T(8,128)(2,1)S(1)}, u32[]{:S(2)}, u32[]{:S(2)}) %collective-permute-start.17) | collective-permute-done | bytes 20512 | tf_op jit(solution)/shard_map/ppermute | solution.py:669
  83.7 4.4 %shard_map.129 = f32[1,32,60]{2,1,0:T(8,128)} custom-call(s32[3]{0:T(128)S(1)} %pad_add_fusion.ids_ref.refs_0_, f32[1]{0:T(128)S(6)} %copy.20.refs_1_, bf16[80,128]{1,0:T(8,128)(2,1)S(1)} %shard_map.128.refs_2_, bf16[80,128]{1,0:T(8,128)(2,1)S(1)} %collective-permute-done.15.refs_3_, bf16[80,128]{1,0:T(8,128)(2,1)S(1)} %collective-permute-done.16.refs_4_, ...), custom_call_target="tpu_custom_call" | custom-call | tf_op jit(solution)/shard_map/pallas_call | solution.py:61
  (61 shorter events, 1.9 us)
Async XLA Ops:
  0.6 1.0 %copy-start = (s32[4,240,128]{2,1,0:T(8,128)S(1)}, s32[4,240,128]{2,1,0:T(8,128)}, u32[]{:S(2)}) copy-start(s32[4,240,128]{2,1,0:T(8,128)} %l_hbm.3) | copy-start | bytes 1474564
  1.7 1.0 %copy-start.14 = (f32[4,240,128]{2,1,0:T(8,128)S(1)}, f32[4,240,128]{2,1,0:T(8,128)}, u32[]{:S(2)}) copy-start(f32[4,240,128]{2,1,0:T(8,128)} %c_hbm.1) | copy-start | bytes 1474564
  2.7 1.0 %copy-start.15 = (f32[4,240,128]{2,1,0:T(8,128)S(1)}, f32[4,240,128]{2,1,0:T(8,128)}, u32[]{:S(2)}) copy-start(f32[4,240,128]{2,1,0:T(8,128)} %d_hbm.1) | copy-start | bytes 1474564
  6.1 0.8 copy-start.2
  6.8 0.8 copy-start.4
  7.6 8.9 %copy-start.22 = (s16[2,240,128]{2,1,0:T(8,128)(2,1)}, s16[2,240,128]{2,1,0:T(8,128)(2,1)S(1)}, u32[]{:S(2)}) copy-start(s16[2,240,128]{2,1,0:T(8,128)(2,1)S(1)} %get-tuple-element.42) | copy-start | bytes 368644
  7.6 8.9 %copy-start.23 = (s16[2,240,128]{2,1,0:T(8,128)(2,1)}, s16[2,240,128]{2,1,0:T(8,128)(2,1)S(1)}, u32[]{:S(2)}) copy-start(s16[2,240,128]{2,1,0:T(8,128)(2,1)S(1)} %get-tuple-element.41) | copy-start | bytes 368644
  7.6 12.7 %collective-permute-start = (s16[256,128]{1,0:T(8,128)(2,1)S(1)}, s16[256,128]{1,0:T(8,128)(2,1)S(1)}, u32[]{:S(2)}, u32[]{:S(2)}) collective-permute-start(s16[256,128]{1,0:T(8,128)(2,1)S(1)} %get-tuple-element.35), channel_id=1, source_target_pairs={{0,4},{4,8},{8,12},{12,0},{1,5},{5,9},{9,13},{13,1},{2,6},{6,10},{... | collective-permute-start | bytes 196616 | tf_op jit(solution)/shard_map/ppermute | solution.py:415
  10.6 9.7 %collective-permute-start.1 = (s16[256,128]{1,0:T(8,128)(2,1)S(1)}, s16[256,128]{1,0:T(8,128)(2,1)S(1)}, u32[]{:S(2)}, u32[]{:S(2)}) collective-permute-start(s16[256,128]{1,0:T(8,128)(2,1)S(1)} %get-tuple-element.36), channel_id=1, source_target_pairs={{0,12},{4,0},{8,4},{12,8},{1,13},{5,1},{9,5},{13,9},{2,14},{6,2},{... | collective-permute-start | bytes 196616 | tf_op jit(solution)/shard_map/ppermute | solution.py:415
  12.7 7.6 %collective-permute-start.2 = (f32[8,128]{1,0:T(8,128)S(1)}, f32[8,128]{1,0:T(8,128)S(1)}, u32[]{:S(2)}, u32[]{:S(2)}) collective-permute-start(f32[8,128]{1,0:T(8,128)S(1)} %get-tuple-element.37.refs_4_), channel_id=1, source_target_pairs={{0,8},{4,12},{8,0},{12,4},{1,9},{5,13},{9,1},{13,5},{2,10},{6,14},... | collective-permute-start | bytes 12296 | tf_op jit(solution)/shard_map/ppermute | solution.py:430
  16.6 0.7 copy-start.20
  17.2 0.7 copy-start.21
  18.7 0.8 copy-start.10
  19.5 0.8 copy-start.16
  20.3 0.6 copy-start.18
  21.0 1.0 %copy-start.3 = (f32[4,240,128]{2,1,0:T(8,128)S(1)}, f32[4,240,128]{2,1,0:T(8,128)}, u32[]{:S(2)}) copy-start(f32[4,240,128]{2,1,0:T(8,128)} %copy-done.2) | copy-start | bytes 1474564
  22.0 1.0 %copy-start.5 = (f32[4,240,128]{2,1,0:T(8,128)S(1)}, f32[4,240,128]{2,1,0:T(8,128)}, u32[]{:S(2)}) copy-start(f32[4,240,128]{2,1,0:T(8,128)} %copy-done.4) | copy-start | bytes 1474564
  23.0 0.8 copy-start.19
  23.9 37.7 %copy-start.1 = (s32[4,240,128]{2,1,0:T(8,128)S(1)}, s32[4,240,128]{2,1,0:T(8,128)}, u32[]{:S(2)}) copy-start(s32[4,240,128]{2,1,0:T(8,128)} %l_hbm.3) | copy-start | bytes 1474564
  23.9 3.9 %collective-permute-start.3 = (f32[2,24,128]{2,1,0:T(8,128)S(1)}, f32[2,24,128]{2,1,0:T(8,128)S(1)}, u32[]{:S(2)}, u32[]{:S(2)}) collective-permute-start(f32[2,24,128]{2,1,0:T(8,128)S(1)} %shard_map.122.refs_5_), channel_id=1, source_target_pairs={{0,2},{2,0},{1,3},{3,1},{4,6},{6,4},{5,7},{7,5},{8,10},{10,8},{9,1... | collective-permute-start | bytes 73736 | tf_op jit(solution)/shard_map/ppermute | solution.py:400
  28.0 9.9 %collective-permute-start.6 = (f32[6,272,128]{2,1,0:T(8,128)S(1)}, f32[6,272,128]{2,1,0:T(8,128)S(1)}, u32[]{:S(2)}, u32[]{:S(2)}) collective-permute-start(f32[6,272,128]{2,1,0:T(8,128)S(1)} %get-tuple-element.43), channel_id=1, source_target_pairs={{0,1},{1,0},{2,3},{3,2},{4,5},{5,4},{6,7},{7,6},{8,9},{9,8},{10,11... | collective-permute-start | bytes 2506760 | tf_op jit(solution)/shard_map/ppermute | solution.py:406
  28.1 8.2 %collective-permute-start.4 = (s16[2,240,128]{2,1,0:T(8,128)(2,1)}, s16[2,240,128]{2,1,0:T(8,128)(2,1)S(1)}, u32[]{:S(2)}, u32[]{:S(2)}) collective-permute-start(s16[2,240,128]{2,1,0:T(8,128)(2,1)} %copy-done.23), channel_id=1, source_target_pairs={{0,4},{4,8},{8,12},{12,0},{1,5},{5,9},{9,13},{13,1},{2,6},{6,10},{... | collective-permute-start | bytes 368648 | tf_op jit(solution)/shard_map/ppermute | solution.py:415
  29.7 8.2 %collective-permute-start.5 = (s16[2,240,128]{2,1,0:T(8,128)(2,1)}, s16[2,240,128]{2,1,0:T(8,128)(2,1)S(1)}, u32[]{:S(2)}, u32[]{:S(2)}) collective-permute-start(s16[2,240,128]{2,1,0:T(8,128)(2,1)} %copy-done.22), channel_id=1, source_target_pairs={{0,12},{4,0},{8,4},{12,8},{1,13},{5,1},{9,5},{13,9},{2,14},{6,2},{... | collective-permute-start | bytes 368648 | tf_op jit(solution)/shard_map/ppermute | solution.py:415
  40.5 13.3 %copy-start.6 = (f32[6,272,128]{2,1,0:T(8,128)}, f32[6,272,128]{2,1,0:T(8,128)S(1)}, u32[]{:S(2)}) copy-start(f32[6,272,128]{2,1,0:T(8,128)S(1)} %get-tuple-element.49.a2_ref) | copy-start | bytes 2506756
  40.6 14.2 %copy-start.12 = (f32[4,240,128]{2,1,0:T(8,128)}, f32[4,240,128]{2,1,0:T(8,128)S(1)}, u32[]{:S(2)}) copy-start(f32[4,240,128]{2,1,0:T(8,128)S(1)} %get-tuple-element.50.ae2_ref) | copy-start | bytes 1474564
  40.6 8.3 %collective-permute-start.7 = (s16[256,128]{1,0:T(8,128)(2,1)S(1)}, s16[256,128]{1,0:T(8,128)(2,1)S(1)}, u32[]{:S(2)}, u32[]{:S(2)}) collective-permute-start(s16[256,128]{1,0:T(8,128)(2,1)S(1)} %get-tuple-element.45), channel_id=1, source_target_pairs={{0,4},{4,8},{8,12},{12,0},{1,5},{5,9},{9,13},{13,1},{2,6},{6,10},{... | collective-permute-start | bytes 196616 | tf_op jit(solution)/shard_map/ppermute | solution.py:415
  41.5 7.4 %collective-permute-start.8 = (s16[256,128]{1,0:T(8,128)(2,1)S(1)}, s16[256,128]{1,0:T(8,128)(2,1)S(1)}, u32[]{:S(2)}, u32[]{:S(2)}) collective-permute-start(s16[256,128]{1,0:T(8,128)(2,1)S(1)} %get-tuple-element.46), channel_id=1, source_target_pairs={{0,12},{4,0},{8,4},{12,8},{1,13},{5,1},{9,5},{13,9},{2,14},{6,2},{... | collective-permute-start | bytes 196616 | tf_op jit(solution)/shard_map/ppermute | solution.py:415
  44.4 4.5 %collective-permute-start.9 = (f32[8,128]{1,0:T(8,128)S(1)}, f32[8,128]{1,0:T(8,128)S(1)}, u32[]{:S(2)}, u32[]{:S(2)}) collective-permute-start(f32[8,128]{1,0:T(8,128)S(1)} %get-tuple-element.47.refs_3_), channel_id=1, source_target_pairs={{0,8},{4,12},{8,0},{12,4},{1,9},{5,13},{9,1},{13,5},{2,10},{6,14},... | collective-permute-start | bytes 12296 | tf_op jit(solution)/shard_map/ppermute | solution.py:430
  48.9 3.9 %collective-permute-start.10 = (f32[2,24,128]{2,1,0:T(8,128)S(1)}, f32[2,24,128]{2,1,0:T(8,128)S(1)}, u32[]{:S(2)}, u32[]{:S(2)}) collective-permute-start(f32[2,24,128]{2,1,0:T(8,128)S(1)} %shard_map.125.refs_4_), channel_id=1, source_target_pairs={{0,2},{2,0},{1,3},{3,1},{4,6},{6,4},{5,7},{7,5},{8,10},{10,8},{9,1... | collective-permute-start | bytes 73736 | tf_op jit(solution)/shard_map/ppermute | solution.py:400
  53.8 0.9 %copy-start.8 = (f32[6,272,128]{2,1,0:T(8,128)}, f32[6,272,128]{2,1,0:T(8,128)S(1)}, u32[]{:S(2)}) copy-start(f32[6,272,128]{2,1,0:T(8,128)S(1)} %get-tuple-element.48.pad_ref) | copy-start | bytes 2506756
  54.7 6.8 %collective-permute-start.13 = (f32[6,272,128]{2,1,0:T(8,128)}, f32[6,272,128]{2,1,0:T(8,128)}, u32[]{:S(2)}, u32[]{:S(2)}) collective-permute-start(f32[6,272,128]{2,1,0:T(8,128)} %get-tuple-element.53), channel_id=1, source_target_pairs={{0,1},{1,0},{2,3},{3,2},{4,5},{5,4},{6,7},{7,6},{8,9},{9,8},{10,11... | collective-permute-start | bytes 2506760 | tf_op jit(solution)/shard_map/ppermute | solution.py:406
  54.7 6.8 %collective-permute-start.11 = (s16[1,240,128]{2,1,0:T(8,128)(2,1)}, s16[1,240,128]{2,1,0:T(8,128)(2,1)S(1)}, u32[]{:S(2)}, u32[]{:S(2)}) collective-permute-start(s16[1,240,128]{2,1,0:T(8,128)(2,1)} %get-tuple-element.51), channel_id=1, source_target_pairs={{0,4},{4,8},{8,12},{12,0},{1,5},{5,9},{9,13},{13,1},{2,6},{6,10},{... | collective-permute-start | bytes 184328 | tf_op jit(solution)/shard_map/ppermute | solution.py:415
  54.7 6.8 %collective-permute-start.12 = (s16[1,240,128]{2,1,0:T(8,128)(2,1)}, s16[1,240,128]{2,1,0:T(8,128)(2,1)}, u32[]{:S(2)}, u32[]{:S(2)}) collective-permute-start(s16[1,240,128]{2,1,0:T(8,128)(2,1)} %get-tuple-element.52), channel_id=1, source_target_pairs={{0,12},{4,0},{8,4},{12,8},{1,13},{5,1},{9,5},{13,9},{2,14},{6,2},{... | collective-permute-start | bytes 184328 | tf_op jit(solution)/shard_map/ppermute | solution.py:415
  61.6 1.2 %copy-start.7 = (f32[6,272,128]{2,1,0:T(8,128)S(1)}, f32[6,272,128]{2,1,0:T(8,128)}, u32[]{:S(2)}) copy-start(f32[6,272,128]{2,1,0:T(8,128)} %copy-done.6) | copy-start | bytes 2506756
  62.7 1.1 %copy-start.9 = (f32[6,272,128]{2,1,0:T(8,128)S(1)}, f32[6,272,128]{2,1,0:T(8,128)}, u32[]{:S(2)}) copy-start(f32[6,272,128]{2,1,0:T(8,128)} %copy-done.8) | copy-start | bytes 2506756
  63.9 1.0 %copy-start.13 = (f32[4,240,128]{2,1,0:T(8,128)S(1)}, f32[4,240,128]{2,1,0:T(8,128)}, u32[]{:S(2)}) copy-start(f32[4,240,128]{2,1,0:T(8,128)} %copy-done.12) | copy-start | bytes 1474564
  64.9 18.8 %copy-start.11 = (bf16[3,768,128]{2,1,0:T(8,128)(2,1)S(1)}, bf16[3,768,128]{2,1,0:T(8,128)(2,1)}, u32[]{:S(2)}) copy-start(bf16[3,768,128]{2,1,0:T(8,128)(2,1)} %copy-done.10) | copy-start | bytes 1769476
  64.9 18.8 %copy-start.17 = (bf16[3,640,128]{2,1,0:T(8,128)(2,1)S(1)}, bf16[3,640,128]{2,1,0:T(8,128)(2,1)}, u32[]{:S(2)}) copy-start(bf16[3,640,128]{2,1,0:T(8,128)(2,1)} %copy-done.16) | copy-start | bytes 1474564
  69.6 3.7 %collective-permute-start.14 = (bf16[2,16,128]{2,1,0:T(8,128)(2,1)S(1)}, bf16[2,16,128]{2,1,0:T(8,128)(2,1)S(1)}, u32[]{:S(2)}, u32[]{:S(2)}) collective-permute-start(bf16[2,16,128]{2,1,0:T(8,128)(2,1)S(1)} %get-tuple-element.58), channel_id=1, source_target_pairs={{0,2},{2,0},{1,3},{3,1},{4,6},{6,4},{5,7},{7,5},{8,10},{10,8},{9,1... | collective-permute-start | bytes 24584 | tf_op jit(solution)/shard_map/ppermute | solution.py:400
  73.9 5.6 %collective-permute-start.15 = (bf16[80,128]{1,0:T(8,128)(2,1)S(1)}, bf16[80,128]{1,0:T(8,128)(2,1)S(1)}, u32[]{:S(2)}, u32[]{:S(2)}) collective-permute-start(bf16[80,128]{1,0:T(8,128)(2,1)S(1)} %shard_map.128.refs_2_), channel_id=1, source_target_pairs={{0,4},{4,8},{8,12},{12,0},{1,5},{5,9},{9,13},{13,1},{2,6},{6,10},{... | collective-permute-start | bytes 61448 | tf_op jit(solution)/shard_map/ppermute | solution.py:669
  74.0 5.6 %collective-permute-start.16 = (bf16[80,128]{1,0:T(8,128)(2,1)S(1)}, bf16[80,128]{1,0:T(8,128)(2,1)S(1)}, u32[]{:S(2)}, u32[]{:S(2)}) collective-permute-start(bf16[80,128]{1,0:T(8,128)(2,1)S(1)} %shard_map.128.refs_2_), channel_id=1, source_target_pairs={{0,12},{4,0},{8,4},{12,8},{1,13},{5,1},{9,5},{13,9},{2,14},{6,2},{... | collective-permute-start | bytes 61448 | tf_op jit(solution)/shard_map/ppermute | solution.py:669
  77.8 4.7 %collective-permute-start.17 = (bf16[80,128]{1,0:T(8,128)(2,1)S(1)}, bf16[80,128]{1,0:T(8,128)(2,1)S(1)}, u32[]{:S(2)}, u32[]{:S(2)}) collective-permute-start(bf16[80,128]{1,0:T(8,128)(2,1)S(1)} %shard_map.128.refs_2_), channel_id=1, source_target_pairs={{0,8},{4,12},{8,0},{12,4},{1,9},{5,13},{9,1},{13,5},{2,10},{6,14},... | collective-permute-start | bytes 61448 | tf_op jit(solution)/shard_map/ppermute | solution.py:669
  77.9 5.3 %collective-permute-start.18 = (bf16[80,128]{1,0:T(8,128)(2,1)S(1)}, bf16[80,128]{1,0:T(8,128)(2,1)S(1)}, u32[]{:S(2)}, u32[]{:S(2)}) collective-permute-start(bf16[80,128]{1,0:T(8,128)(2,1)S(1)} %shard_map.128.refs_2_), channel_id=1, source_target_pairs={{0,1},{1,0},{2,3},{3,2},{4,5},{5,4},{6,7},{7,6},{8,9},{9,8},{10,11... | collective-permute-start | bytes 61448 | tf_op jit(solution)/shard_map/ppermute | solution.py:406
  79.5 3.6 %collective-permute-start.19 = (bf16[80,128]{1,0:T(8,128)(2,1)S(1)}, bf16[80,128]{1,0:T(8,128)(2,1)S(1)}, u32[]{:S(2)}, u32[]{:S(2)}) collective-permute-start(bf16[80,128]{1,0:T(8,128)(2,1)S(1)} %collective-permute-done.15.refs_3_), channel_id=1, source_target_pairs={{0,1},{1,0},{2,3},{3,2},{4,5},{5,4},{6,7},{7,6},{8,9},{9,8},{10,11... | collective-permute-start | bytes 61448 | tf_op jit(solution)/shard_map/ppermute | solution.py:406
  79.6 3.6 %collective-permute-start.20 = (bf16[80,128]{1,0:T(8,128)(2,1)S(1)}, bf16[80,128]{1,0:T(8,128)(2,1)S(1)}, u32[]{:S(2)}, u32[]{:S(2)}) collective-permute-start(bf16[80,128]{1,0:T(8,128)(2,1)S(1)} %collective-permute-done.16.refs_4_), channel_id=1, source_target_pairs={{0,1},{1,0},{2,3},{3,2},{4,5},{5,4},{6,7},{7,6},{8,9},{9,8},{10,11... | collective-permute-start | bytes 61448 | tf_op jit(solution)/shard_map/ppermute | solution.py:406
  82.5 1.2 %collective-permute-start.21 = (bf16[80,128]{1,0:T(8,128)(2,1)S(1)}, bf16[80,128]{1,0:T(8,128)(2,1)S(1)}, u32[]{:S(2)}, u32[]{:S(2)}) collective-permute-start(bf16[80,128]{1,0:T(8,128)(2,1)S(1)} %collective-permute-done.17.refs_5_), channel_id=1, source_target_pairs={{0,1},{1,0},{2,3},{3,2},{4,5},{5,4},{6,7},{7,6},{8,9},{9,8},{10,11... | collective-permute-start | bytes 61448 | tf_op jit(solution)/shard_map/ppermute | solution.py:406

commit v4 on v3

--- a/solution.py
+++ b/solution.py
@@ -81,8 +81,7 @@
                             jnp.zeros((6, top.shape[1]), F32)])
 
 
-def first_kernel(c_hbm, d_hbm, l_hbm, f_ref, amp_ref, lo1_ref, hi1_ref, lo2_ref, hi2_ref, sum_ref,
-                 d_ref, l_ref, sems):
+def first_kernel(c_hbm, d_hbm, l_hbm, f_ref, amp_ref, lo_ref, hi_ref, sum_ref, d_ref, l_ref, sems):
     nx, ny, nz = f_ref.shape
     order = [0, nx - 1] + list(range(1, nx - 1))
     copies = []
@@ -103,16 +102,16 @@
             m = a * a
             top = top + fold(m * f)
             bottom = bottom + fold(m)
-            for near, far, first, second in ((0, 1, lo1_ref, lo2_ref), (nx - 1, nx - 2, hi1_ref, hi2_ref)):
+            for near, far, out in ((0, 1, lo_ref), (nx - 1, nx - 2, hi_ref)):
                 if x == near:
-                    first[r:r + n, :] = to_code(f, A_CODE)
-                    second[1, r:r + n, :] = to_code(a, A_CODE)
+                    out[r:r + n, :] = to_code(f, A_CODE)
+                    out[2 * ny + r:2 * ny + r + n, :] = to_code(a, A_CODE)
                 if x == far:
-                    second[0, r:r + n, :] = to_code(f, A_CODE)
+                    out[ny + r:ny + r + n, :] = to_code(f, A_CODE)
     s = to_rows(top, bottom)
     sum_ref[...] = s
-    lo1_ref[ny:ny + 16, :] = sum_digits(s)
-    hi1_ref[ny:ny + 16, :] = sum_digits(s)
+    lo_ref[3 * ny:3 * ny + 16, :] = sum_digits(s)
+    hi_ref[3 * ny:3 * ny + 16, :] = sum_digits(s)
 
 
 def edge_rows(code, ride_x, with_amp):
@@ -137,56 +136,86 @@
             out_ref[side, 9:10, :] = beside[1]
             out_ref[side, 16:24, :] = s
             if ride_x:
-                out_ref[side, 16:18, :] = (s[0:2] + from_digits(lo_ref[ny:ny + 16, :])
-                                           + from_digits(hi_ref[ny:ny + 16, :]))
+                out_ref[side, 16:18, :] = (s[0:2] + from_digits(lo_ref[lo_ref.shape[0] - 16:, :])
+                                           + from_digits(hi_ref[hi_ref.shape[0] - 16:, :]))
     return kernel
 
 
-def assemble(code, ride_y, with_amp):
+def group(lane, j, nz, first, count):
+    return (lane - (32 * j + first)) % nz < count
+
+
+def pack_z(code, ride_y, with_amp):
     def kernel(*refs):
         f_ref = refs[0]
         amp_ref = refs[1] if with_amp else None
-        lo_ref, hi_ref, yr_ref, yp_ref, pad_ref = refs[1 + with_amp:6 + with_amp]
-        apad_ref = refs[7] if with_amp else None
-        zp_ref = refs[-1]
+        lo_ref, hi_ref, yr_ref, yp_ref, out_ref = refs[1 + with_amp:]
         nx, ny, nz = f_ref.shape
         end = OFF + ny
         lane = lax.broadcasted_iota(jnp.int32, (1, nz), 1)
-        outer = (lane < 16) | (lane >= nz - 16)
-        for p, ref in ((0, lo_ref), (nx + 1, hi_ref)):
+        for k in range(out_ref.shape[0]):
+            planes = [p for p in range(4 * k, 4 * k + 4) if p < nx + 2]
+
+            def packed(f_of, a_of, ps):
+                out = None
+                for p in ps:
+                    j = p % 4
+                    f = f_of(p)
+                    f = pltpu.roll(f, 32 * j, 1) if j else f
+                    out = f if out is None else jnp.where(group(lane, j, nz, -2, 4), f, out)
+                    a = a_of(p)
+                    if a is not None:
+                        out = jnp.where(group(lane, j, nz, 15, 2), pltpu.roll(a, 32 * j + 16, 1), out)
+                return out
+
             for r, n in chunks(0, ny, 48):
-                f = from_code(ref[r:r + n, :], code)
-                pad_ref[p, OFF + r:OFF + r + n, :] = f
-                zp_ref[p, OFF + r:OFF + r + n, :] = f
-        for p, k in ((0, 8), (nx + 1, 9)):
-            pad_ref[p, OFF - 1:OFF, :] = yr_ref[1, k:k + 1, :]
-            pad_ref[p, end:end + 1, :] = yr_ref[0, k:k + 1, :]
-        for x in range(nx):
-            for r, n in chunks(0, ny, 48):
-                f = f_ref[x, r:r + n, :]
-                pad_ref[x + 1, OFF + r:OFF + r + n, :] = f
-                if amp_ref is not None:
-                    a = amp_ref[x, r:r + n, :]
-                    apad_ref[x, OFF + r:OFF + r + n, :] = a
-                    f = jnp.where(outer, f, pltpu.roll(a, nz // 2, 1))
-                zp_ref[x + 1, OFF + r:OFF + r + n, :] = f
-            for side, near, far in ((1, OFF - 1, OFF - 2), (0, end, end + 1)):
-                f = yr_ref[side, 2 * x:2 * x + 1, :]
-                pad_ref[x + 1, near:near + 1, :] = f
-                pad_ref[x + 1, far:far + 1, :] = yr_ref[side, 2 * x + 1:2 * x + 2, :]
-                if amp_ref is not None:
-                    apad_ref[x, near:near + 1, :] = yr_ref[side, 10 + x:11 + x, :]
-                zp_ref[x + 1, near:near + 1, :] = f
+                def f_of(p):
+                    if p == 0:
+                        return from_code(lo_ref[r:r + n, :], code)
+                    if p == nx + 1:
+                        return from_code(hi_ref[r:r + n, :], code)
+                    return f_ref[p - 1, r:r + n, :]
+
+                def a_of(p):
+                    return amp_ref[p - 1, r:r + n, :] if with_amp and 1 <= p <= nx else None
+
+                out_ref[k, OFF + r:OFF + r + n, :] = packed(f_of, a_of, planes)
+            inner = [p for p in planes if 1 <= p <= nx]
+            if inner:
+                for side, near in ((1, OFF - 1), (0, end)):
+                    out_ref[k, near:near + 1, :] = packed(
+                        lambda p: yr_ref[side, 2 * (p - 1):2 * (p - 1) + 1, :], lambda p: None, inner)
         s = yp_ref[0, 16:24, :]
-        if ride_y:
-            s = s + yr_ref[0, 16:24, :]
-        zp_ref[0, 0:8, :] = s
-        pad_ref[0, 0:8, :] = s
+        out_ref[0, 0:8, :] = s + yr_ref[0, 16:24, :] if ride_y else s
     return kernel
 
 
-def weighted_mean(pad_ref, zr_ref, ride_z):
-    s = pad_ref[0, 0:8, :]
+def fill(code, f_ref, lo_ref, hi_ref, yr_ref, zr_ref, pad_ref, ze_ref):
+    nx, ny, nz = f_ref.shape
+    end = OFF + ny
+    for near, far, ref in ((1, 0, lo_ref), (nx + 2, nx + 3, hi_ref)):
+        for r, n in chunks(0, ny, 48):
+            pad_ref[near, OFF + r:OFF + r + n, :] = from_code(ref[r:r + n, :], code)
+            pad_ref[far, OFF + r:OFF + r + n, :] = from_code(ref[ny + r:ny + r + n, :], code)
+    for p, k in ((1, 8), (nx + 2, 9)):
+        pad_ref[p, OFF - 1:OFF, :] = yr_ref[1, k:k + 1, :]
+        pad_ref[p, end:end + 1, :] = yr_ref[0, k:k + 1, :]
+    for x in range(nx):
+        for r, n in chunks(0, ny, 48):
+            pad_ref[x + 2, OFF + r:OFF + r + n, :] = f_ref[x, r:r + n, :]
+        for side, near, far in ((1, OFF - 1, OFF - 2), (0, end, end + 1)):
+            pad_ref[x + 2, near:near + 1, :] = yr_ref[side, 2 * x:2 * x + 1, :]
+            pad_ref[x + 2, far:far + 1, :] = yr_ref[side, 2 * x + 1:2 * x + 2, :]
+    for p in range(nx + 2):
+        for r, n in chunks(OFF - 8, OFF + ny + 8, 32):
+            e = zr_ref[p // 4, r:r + n, :]
+            ze_ref[p, r:r + n, :] = pltpu.roll(e, nz - 32 * (p % 4), 1) if p % 4 else e
+
+
+def weighted_mean(yp_ref, yr_ref, zr_ref, ride_y, ride_z):
+    s = yp_ref[0, 16:24, :]
+    if ride_y:
+        s = s + yr_ref[0, 16:24, :]
     if ride_z:
         s = s + zr_ref[0, 0:8, :]
     return jnp.sum(s[0:1], keepdims=True) / jnp.sum(s[1:2], keepdims=True)
@@ -217,32 +246,24 @@
     return well + 6.0 * f - around + STRAIN_COUPLING * m * (f - mean)
 
 
-def chemistry(g, pad_ref, lo2_ref, hi2_ref, code, mob_ref, mobe_ref, zr_ref, chem_ref, cheme_ref, mean):
+def chemistry(g, pad_ref, mob_ref, mobe_ref, ze_ref, chem_ref, cheme_ref, mean):
     nx, ny = g.nx, g.ny
-
-    def plane(p, r, n):
-        if p < 0:
-            return from_code(lo2_ref[0, r - OFF:r - OFF + n, :], code)
-        if p > nx + 1:
-            return from_code(hi2_ref[0, r - OFF:r - OFF + n, :], code)
-        return pad_ref[p, r:r + n, :]
-
     for p in range(nx + 2):
         inside = 1 <= p <= nx
         rows = chunks(OFF - 8, OFF + ny + 8, 32) if inside else chunks(OFF, OFF + ny, 48)
         for r, n in rows:
-            f = pad_ref[p, r:r + n, :]
-            e = zr_ref[p, r:r + n, :]
-            around = (plane(p - 1, r, n) + plane(p + 1, r, n)
-                      + pad_ref[p, r - 1:r - 1 + n, :] + pad_ref[p, r + 1:r + 1 + n, :]
+            f = pad_ref[p + 1, r:r + n, :]
+            e = ze_ref[p, r:r + n, :]
+            around = (pad_ref[p, r:r + n, :] + pad_ref[p + 2, r:r + n, :]
+                      + pad_ref[p + 1, r - 1:r - 1 + n, :] + pad_ref[p + 1, r + 1:r + 1 + n, :]
                       + g.before(f, e) + g.after(f, e))
             chem_ref[p, r:r + n, :] = chem_of(f, mob_ref[p, r:r + n, :], around, mean)
         if inside:
             for r, n in chunks(OFF, OFF + ny, 48):
-                f = pad_ref[p, r:r + n, :]
-                e = zr_ref[p, r:r + n, :]
-                around = (zr_ref[p - 1, r:r + n, :] + zr_ref[p + 1, r:r + n, :]
-                          + zr_ref[p, r - 1:r - 1 + n, :] + zr_ref[p, r + 1:r + 1 + n, :]
+                f = pad_ref[p + 1, r:r + n, :]
+                e = ze_ref[p, r:r + n, :]
+                around = (ze_ref[p - 1, r:r + n, :] + ze_ref[p + 1, r:r + n, :]
+                          + ze_ref[p, r - 1:r - 1 + n, :] + ze_ref[p, r + 1:r + 1 + n, :]
                           + g.before(e, f) + g.after(e, f))
                 cheme_ref[p - 1, r - OFF:r - OFF + n, :] = chem_of(
                     e, mobe_ref[p - 1, r - OFF:r - OFF + n, :], around, mean)
@@ -268,76 +289,90 @@
     return m, 0.5 * total
 
 
-def step_a(ride_z):
-    def kernel(pad_ref, apad_ref, lo2_ref, hi2_ref, zr_ref,
-               f2_ref, a2_ref, ae2_ref, lo1_out, hi1_out, lo2_out, hi2_out, sum_ref,
-               mob_ref, mobe_ref, chem_ref, cheme_ref):
+def pack_edges(values, lane, nz):
+    out = values[0]
+    for x, v in enumerate(values[1:], 1):
+        out = jnp.where(group(lane, x, nz, -1, 2), pltpu.roll(v, 32 * x, 1), out)
+    return out
+
+
+def step_a(ride_y, ride_z):
+    def kernel(f_ref, amp_ref, lo_ref, hi_ref, yr_ref, zr_ref, yp_ref,
+               f2_ref, a2_ref, ae2_ref, lo_out, hi_out, sum_ref,
+               pad_ref, ze_ref, mob_ref, mobe_ref, chem_ref, cheme_ref):
         nx, ny, nz = f2_ref.shape
+        end = OFF + ny
         g = Geometry(nx, ny, nz)
-        mean = weighted_mean(pad_ref, zr_ref, ride_z)
-        for p in range(nx + 2):
-            inside = 1 <= p <= nx
-            rows = chunks(OFF - 8, OFF + ny + 8, 32) if inside else chunks(OFF, OFF + ny, 48)
-            for r, n in rows:
-                if inside:
-                    a = apad_ref[p - 1, r:r + n, :]
-                else:
-                    a = from_code((lo2_ref if p == 0 else hi2_ref)[1, r - OFF:r - OFF + n, :], A_CODE)
+        mean = weighted_mean(yp_ref, yr_ref, zr_ref, ride_y, ride_z)
+        fill(A_CODE, f_ref, lo_ref, hi_ref, yr_ref, zr_ref, pad_ref, ze_ref)
+
+        def wear(p, r, n, a):
+            m = a * a
+            mob_ref[p, r:r + n, :] = m
+            a2_ref[p, r:r + n, :] = worn(a, m, pad_ref[p + 1, r:r + n, :], mean)
+
+        for r, n in chunks(0, ny, 48):
+            wear(0, OFF + r, n, from_code(lo_ref[2 * ny + r:2 * ny + r + n, :], A_CODE))
+            wear(nx + 1, OFF + r, n, from_code(hi_ref[2 * ny + r:2 * ny + r + n, :], A_CODE))
+            edges = []
+            for x in range(nx):
+                wear(x + 1, OFF + r, n, amp_ref[x, r:r + n, :])
+                p = x + 1
+                a = pltpu.roll(zr_ref[p // 4, OFF + r:OFF + r + n, :], nz - 32 * (p % 4) - 16, 1)
                 m = a * a
-                mob_ref[p, r:r + n, :] = m
-                a2_ref[p, r:r + n, :] = worn(a, m, pad_ref[p, r:r + n, :], mean)
-            if inside:
-                for r, n in chunks(OFF, OFF + ny, 48):
-                    e = zr_ref[p, r:r + n, :]
-                    a = pltpu.roll(e, nz // 2, 1)
-                    m = a * a
-                    mobe_ref[p - 1, r - OFF:r - OFF + n, :] = m
-                    ae2_ref[p - 1, r - OFF:r - OFF + n, :] = worn(a, m, e, mean)
-        chemistry(g, pad_ref, lo2_ref, hi2_ref, A_CODE, mob_ref, mobe_ref, zr_ref, chem_ref, cheme_ref, mean)
+                mobe_ref[x, r:r + n, :] = m
+                edges.append(worn(a, m, ze_ref[p, OFF + r:OFF + r + n, :], mean))
+            ae2_ref[r:r + n, :] = pack_edges(edges, g.lane, nz)
+        for x in range(nx):
+            wear(x + 1, OFF - 1, 1, yr_ref[1, 10 + x:11 + x, :])
+            wear(x + 1, end, 1, yr_ref[0, 10 + x:11 + x, :])
+        chemistry(g, pad_ref, mob_ref, mobe_ref, ze_ref, chem_ref, cheme_ref, mean)
         top = jnp.zeros((8, nz), F32)
         bottom = jnp.zeros((8, nz), F32)
         for x in range(nx):
-            for r, n in chunks(OFF, OFF + ny, 48):
+            for r, n in chunks(OFF, end, 48):
                 _, flux = flux_of(g, x, r, n, mob_ref, mobe_ref, chem_ref, cheme_ref)
-                f = pad_ref[x + 1, r:r + n, :] + TIME_STEP * flux
+                f = pad_ref[x + 2, r:r + n, :] + TIME_STEP * flux
                 s = slice(r - OFF, r - OFF + n)
                 f2_ref[x, s, :] = f
                 a = a2_ref[x + 1, r:r + n, :]
                 m = a * a
                 top = top + fold(m * f)
                 bottom = bottom + fold(m)
-                for near, far, first, second in ((0, 1, lo1_out, lo2_out), (nx - 1, nx - 2, hi1_out, hi2_out)):
+                for near, far, out in ((0, 1, lo_out), (nx - 1, nx - 2, hi_out)):
                     if x == near:
-                        first[s, :] = to_code(f, B_CODE)
+                        out[s, :] = to_code(f, B_CODE)
                     if x == far:
-                        second[0, s, :] = to_code(f, B_CODE)
+                        out[r - OFF + ny:r - OFF + ny + n, :] = to_code(f, B_CODE)
         s = to_rows(top, bottom)
         sum_ref[...] = s
-        lo1_out[ny:ny + 16, :] = sum_digits(s)
-        hi1_out[ny:ny + 16, :] = sum_digits(s)
+        lo_out[2 * ny:2 * ny + 16, :] = sum_digits(s)
+        hi_out[2 * ny:2 * ny + 16, :] = sum_digits(s)
     return kernel
 
 
-def step_b(ride_z):
-    def kernel(pad_ref, a2_ref, ae2_ref, lo2_ref, hi2_ref, zr_ref, l_hbm,
+def step_b(ride_y, ride_z):
+    def kernel(f_ref, a2_ref, ae2_ref, lo_ref, hi_ref, yr_ref, zr_ref, yp_ref, l_hbm,
                f3_hbm, dmg_hbm, flux_hbm, pool_ref, edge_ref,
-               mob_ref, mobe_ref, chem_ref, cheme_ref, pool_scr, l_ref, f3_ref, dmg_ref, flux_ref, l_sem, sems):
+               pad_ref, ze_ref, mob_ref, mobe_ref, chem_ref, cheme_ref,
+               pool_scr, l_ref, f3_ref, dmg_ref, flux_ref, l_sem, sems):
         nx, ny, nz = f3_ref.shape
         labels_in = pltpu.make_async_copy(l_hbm, l_ref, l_sem)
         labels_in.start()
         g = Geometry(nx, ny, nz)
-        mean = weighted_mean(pad_ref, zr_ref, ride_z)
+        mean = weighted_mean(yp_ref, yr_ref, zr_ref, ride_y, ride_z)
+        fill(B_CODE, f_ref, lo_ref, hi_ref, yr_ref, zr_ref, pad_ref, ze_ref)
         for p in range(nx + 2):
             inside = 1 <= p <= nx
-            rows = chunks(OFF - 8, OFF + ny + 8, 32) if inside else chunks(OFF, OFF + ny, 48)
-            for r, n in rows:
+            for r, n in chunks(OFF - 8, OFF + ny + 8, 32) if inside else chunks(OFF, OFF + ny, 48):
                 a = a2_ref[p, r:r + n, :]
                 mob_ref[p, r:r + n, :] = a * a
-            if inside:
-                for r, n in chunks(0, ny, 48):
-                    a = ae2_ref[p - 1, r:r + n, :]
-                    mobe_ref[p - 1, r:r + n, :] = a * a
-        chemistry(g, pad_ref, lo2_ref, hi2_ref, B_CODE, mob_ref, mobe_ref, zr_ref, chem_ref, cheme_ref, mean)
+        for r, n in chunks(0, ny, 48):
+            a = ae2_ref[r:r + n, :]
+            a = a * a
+            for x in range(nx):
+                mobe_ref[x, r:r + n, :] = pltpu.roll(a, nz - 32 * x, 1) if x else a
+        chemistry(g, pad_ref, mob_ref, mobe_ref, ze_ref, chem_ref, cheme_ref, mean)
         labels_in.wait()
         copies = []
         for k, (r, n) in enumerate(chunks(OFF, OFF + ny, 48)):
@@ -345,7 +380,7 @@
             pooled = [None] * 4
             for x in range(nx):
                 m, flux = flux_of(g, x, r, n, mob_ref, mobe_ref, chem_ref, cheme_ref)
-                f0 = pad_ref[x + 1, r:r + n, :]
+                f0 = pad_ref[x + 2, r:r + n, :]
                 f = f0 + TIME_STEP * flux
                 a = worn(a2_ref[x + 1, r:r + n, :], m, f0, mean)
                 labels = l_ref[x, s, :]
@@ -407,8 +442,11 @@
     above = lax.ppermute(pay, axis, ring(axis, -1))
     below = lax.ppermute(pay, axis, ring(axis, 1))
     lane = lax.broadcasted_iota(jnp.int32, pay.shape, pay.ndim - 1)
-    part = pay.shape[-1] // (4 if packed else 2)
-    return jnp.where(lane // part % 2 == 0, above, below)
+    if packed:
+        low = (lane % 32 < 8) | (lane % 32 == 16)
+    else:
+        low = lane < pay.shape[-1] // 2
+    return jnp.where(low, above, below)
 
 
 def x_sides(lo, hi):
@@ -423,54 +461,53 @@
     ride_x = lax.axis_size("gx") == 4
     ride_y = lax.axis_size("gy") == 2
     ride_z = lax.axis_size("gz") == 2
-    scratch = [pltpu.VMEM(padded, F32), pltpu.VMEM(block, F32), pltpu.VMEM(padded, F32), pltpu.VMEM(block, F32)]
+    packed = (-(-(nx + 2) // 4), rows, nz)
+    assert nz == 128
+    scratch = [pltpu.VMEM((nx + 4, rows, nz), F32), pltpu.VMEM(padded, F32), pltpu.VMEM(padded, F32),
+               pltpu.VMEM(block, F32), pltpu.VMEM(padded, F32), pltpu.VMEM(block, F32)]
 
     def start(sums):
         if ride_x:
-            far = lax.ppermute(sums, "gx", ring("gx", 2))
-        else:
-            sums = far = pair_sum(sums, "gx")
+            return sums, lax.ppermute(sums, "gx", ring("gx", 2))
+        sums = pair_sum(sums, "gx")
         for axis, ride in (("gy", ride_y), ("gz", ride_z)):
             if not ride:
-                assert not ride_x
-                sums = far = pair_sum(sums, axis)
-        return sums, far
-
-    f, amp, lo1, hi1, lo2, hi2, sums = call(
+                sums = pair_sum(sums, axis)
+        return sums, sums
+
+    concentration, damage, labels = (
+        pltpu.with_memory_space_constraint(v, pltpu.HBM) for v in (concentration, damage, labels))
+    tall = 3 * ny + 16
+    f, amp, lo, hi, sums = call(
         first_kernel,
-        [(block, F32), (block, F32), ((ny + 16, nz), I16), ((ny + 16, nz), I16),
-         ((2, ny, nz), I16), ((2, ny, nz), I16), ((8, nz), F32)],
+        [(block, F32), (block, F32), ((tall, nz), I16), ((tall, nz), I16), ((8, nz), F32)],
         concentration, damage, labels,
         in_specs=[HBM] * 3,
         scratch=[pltpu.VMEM(block, F32), pltpu.VMEM(block, jnp.int32), pltpu.SemaphoreType.DMA((3, nx))])
-    matrices = weight_matrices(w_first, b_first, w_second, b_second, w_third, nz, nz // 4)
+    *matrices, order = weight_matrices(w_first, b_first, w_second, b_second, w_third, nz, nz // 4)
     sums, far = start(sums)
-    lo1, hi1 = x_sides(lo1, hi1)
-    lo2, hi2 = x_sides(lo2, hi2)
-    (ypay,) = call(edge_rows(A_CODE, ride_x, True), [((2, 24, nz), F32)], f, amp, lo1, hi1, sums, far, matrices[-1])
+    lo, hi = x_sides(lo, hi)
+    (ypay,) = call(edge_rows(A_CODE, ride_x, True), [((2, 24, nz), F32)], f, amp, lo, hi, sums, far, order)
     yr = both_sides(ypay, "gy")
-    pad, apad, zpay = call(
-        assemble(A_CODE, ride_y, True), [(padded, F32), ((nx, rows, nz), F32), (padded, F32)],
-        f, amp, lo1, hi1, yr, ypay)
+    (zpay,) = call(pack_z(A_CODE, ride_y, True), [(packed, F32)], f, amp, lo, hi, yr, ypay)
     zr = z_neighbour(zpay, "gz")
-    f2, a2, ae2, lo1, hi1, lo2, hi2, sums = call(
-        step_a(ride_z),
-        [(block, F32), (padded, F32), (block, F32), ((ny + 16, nz), I16), ((ny + 16, nz), I16),
-         ((1, ny, nz), I16), ((1, ny, nz), I16), ((8, nz), F32)],
-        pad, apad, lo2, hi2, zr, scratch=scratch)
+    tall = 2 * ny + 16
+    f, a2, ae2, lo, hi, sums = call(
+        step_a(ride_y, ride_z),
+        [(block, F32), (padded, F32), ((ny, nz), F32), ((tall, nz), I16), ((tall, nz), I16), ((8, nz), F32)],
+        f, amp, lo, hi, yr, zr, ypay, scratch=scratch)
 
     sums, far = start(sums)
-    lo1, hi1 = x_sides(lo1, hi1)
-    lo2, hi2 = x_sides(lo2, hi2)
-    (ypay,) = call(edge_rows(B_CODE, ride_x, False), [((2, 24, nz), F32)], f2, lo1, hi1, sums, far)
+    lo, hi = x_sides(lo, hi)
+    (ypay,) = call(edge_rows(B_CODE, ride_x, False), [((2, 24, nz), F32)], f, lo, hi, sums, far)
     yr = both_sides(ypay, "gy")
-    pad, zpay = call(assemble(B_CODE, ride_y, False), [(padded, F32), (padded, F32)], f2, lo1, hi1, yr, ypay)
+    (zpay,) = call(pack_z(B_CODE, ride_y, False), [(packed, F32)], f, lo, hi, yr, ypay)
     zr = z_neighbour(zpay, "gz")
     fraction, damage_field, flux_sum, pooled, edge = call(
-        step_b(ride_z),
+        step_b(ride_y, ride_z),
         [(block, F32), (block, F32), (block, F32), ((ny // 4, nz), BF16), ((2, 16, nz), BF16)],
-        pad, a2, ae2, lo2, hi2, zr, labels,
-        in_specs=[VMEM] * 6 + [HBM], out_specs=[HBM] * 3 + [VMEM] * 2,
+        f, a2, ae2, lo, hi, yr, zr, ypay, labels,
+        in_specs=[VMEM] * 8 + [HBM], out_specs=[HBM] * 3 + [VMEM] * 2,
         scratch=scratch + [
             pltpu.VMEM((4, ny, nz), F32), pltpu.VMEM(block, jnp.int32),
             pltpu.VMEM(block, F32), pltpu.VMEM(block, F32), pltpu.VMEM(block, F32),
@@ -501,10 +538,19 @@
     return jnp.dot(a, b, preferred_element_type=F32)
 
 
-def weight_kernel(w1_ref, w2_ref, w3_ref, b1_ref, b2_ref, t1_ref, t2_ref, t3_ref, bias_ref):
-    k1 = t1_ref.shape[1] // 3
-    n1 = t1_ref.shape[2]
-    pz = k1 // (2 * CIN)
+def tile_shift(rb, cb, pz):
+    z_in = rb * 16 // CIN
+    z_in = z_in if z_in < pz + pz // 2 else z_in - 2 * pz
+    return z_in - cb * 8 + 3
+
+
+SHIFTS = tuple(k for k in range(-3, 10) if k % (16 // CIN) == 3)
+
+
+def weight_kernel(w1_ref, w2_ref, w3_ref, b1_ref, b2_ref, d1_hbm, t2_hbm, t3_hbm, bias_hbm, order_ref,
+                  d1_ref, t2_ref, t3_ref, bias_ref, sems):
+    n1 = bias_ref.shape[1]
+    pz = n1 // CH // 8 * 8 - 8
     spread = one_hot(iota((CH, 128), 1) % CH == iota((CH, 128), 0))
     tile1 = mm(w1_ref[...], spread)
     tile2 = mm(w2_ref[...], spread)
@@ -521,20 +567,12 @@
         return out.astype(BF16)
 
     zero = jnp.zeros((16, 128), BF16)
+    bias_ref[...] = jnp.zeros(bias_ref.shape, F32)
     for i in range(3):
         for j in range(3):
             tap = 9 * i + 3 * j
-            known = {}
-            for rb in range(k1 // 16):
-                z_in = rb * 16 // CIN
-                z_in = z_in if z_in < pz + pz // 2 else z_in - 2 * pz
-                for cb in range(n1 // 128):
-                    shift = z_in - cb * 8 + 3
-                    near = -4 < shift < 10
-                    if near and shift not in known:
-                        known[shift] = tile(tile1, tap, 1, step1, shift)
-                    t1_ref[i, j * k1 + rb * 16:j * k1 + rb * 16 + 16, cb * 128:(cb + 1) * 128] = (
-                        known[shift] if near else zero)
+            for k, shift in enumerate(SHIFTS):
+                d1_ref[3 * i + j, k] = tile(tile1, tap, 1, step1, shift)
             for rb in range(16):
                 t2_ref[i, j * 256 + rb * 16:j * 256 + rb * 16 + 16, :] = (
                     tile(tile2, tap, 1, step2, rb) if rb < 10 else zero)
@@ -543,6 +581,13 @@
     wide = one_hot(iota((CH, n1), 1) % CH == iota((CH, n1), 0)).astype(F32)
     for k, ref in ((0, b1_ref), (1, b2_ref)):
         bias_ref[k:k + 1, :] = jnp.dot(ref[...], wide, precision=lax.Precision.HIGHEST, preferred_element_type=F32)
+    order_ref[...] = jnp.zeros(order_ref.shape, F32)
+    copies = [pltpu.make_async_copy(src, dst, sems.at[k]) for k, (src, dst) in enumerate(
+        ((d1_ref, d1_hbm), (t2_ref, t2_hbm), (t3_ref, t3_hbm), (bias_ref, bias_hbm)))]
+    for c in copies:
+        c.start()
+    for c in copies:
+        c.wait()
 
 
 def weight_matrices(w_first, b_first, w_second, b_second, w_third, half, pz):
@@ -550,10 +595,11 @@
     rows1 = jnp.tile(jnp.swapaxes(w_first, 1, 2), (1, 16 // CIN, 1)).reshape(27 * 16, CH)
     rows2 = jnp.swapaxes(w_second, 1, 2).reshape(27 * CH, CH)
     rows3 = w_third.reshape(3, 3, 3, CH).transpose(0, 2, 3, 1).reshape(9 * CH, 3)
+    outs = [((9, len(SHIFTS), 16, 128), BF16), ((3, 768, 128), BF16), ((3, width, 128), BF16), ((8, width), F32)]
     return call(
-        weight_kernel,
-        [((3, 6 * half, width), BF16), ((3, 768, 128), BF16), ((3, width, 128), BF16), ((8, width), F32)],
-        rows1, rows2, rows3, b_first[None], b_second[None])
+        weight_kernel, outs + [((8, 128), F32)], rows1, rows2, rows3, b_first[None], b_second[None],
+        out_specs=[HBM] * 4 + [VMEM],
+        scratch=[pltpu.VMEM(*v) for v in outs] + [pltpu.SemaphoreType.DMA((4,))])
 
 
 def gelu(x):
@@ -581,8 +627,14 @@
         ids_ref, b3_ref = refs[:2]
         own = refs[2:3 + n]
         other = refs[3 + n:4 + 2 * n]
-        t1_ref, t2_ref, t3_ref, bias_ref, out_ref = refs[4 + 2 * n:9 + 2 * n]
-        in_ref, lhs1_ref, act1_ref, lhs2_ref, act2_ref, tail_ref = refs[9 + 2 * n:]
+        hbm = refs[4 + 2 * n:8 + 2 * n]
+        out_ref = refs[8 + 2 * n]
+        (in_ref, lhs1_ref, act1_ref, lhs2_ref, act2_ref, tail_ref, t1_ref,
+         d1_ref, t2_ref, t3_ref, bias_ref, sems) = refs[9 + 2 * n:]
+        loads = [pltpu.make_async_copy(src, dst, sems.at[k])
+                 for k, (src, dst) in enumerate(zip(hbm, (d1_ref, t2_ref, t3_ref, bias_ref)))]
+        for c in loads:
+            c.start()
         ix, iy, iz = ids_ref[0], ids_ref[1], ids_ref[2]
         half = own[0].shape[1]
         pz = half // CIN
@@ -603,6 +655,16 @@
             for j in range(3):
                 start = TOP - 3 + j
                 lhs1_ref[w, :, j * k1:(j + 1) * k1] = in_ref[w, start:start + rows, :].astype(BF16)
+        loads[0].wait()
+        loads[3].wait()
+        zero = jnp.zeros((16, 128), BF16)
+        for i in range(3):
+            for j in range(3):
+                for rb in range(k1 // 16):
+                    for cb in range(t1_ref.shape[2] // 128):
+                        shift = tile_shift(rb, cb, pz)
+                        t1_ref[i, j * k1 + rb * 16:j * k1 + rb * 16 + 16, cb * 128:(cb + 1) * 128] = (
+                            d1_ref[3 * i + j, SHIFTS.index(shift)] if shift in SHIFTS else zero)
         out = None
         for i in range(3):
             part = mm(lhs1_ref[i:i + 5].reshape(5 * rows, 3 * k1), t1_ref[i])
@@ -618,6 +680,7 @@
             act1_ref[p, 0:rows, 0:width] = jnp.where(good, a, 0.0)
             act1_ref[p, rows:, 0:width] = jnp.zeros((act1_ref.shape[1] - rows, width), F32)
             act1_ref[p, :, width:] = jnp.zeros((act1_ref.shape[1], act1_ref.shape[2] - width), F32)
+        loads[1].wait()
         blocks = lhs2_ref.shape[1]
         for p in range(5):
             for j in range(3):
@@ -638,6 +701,7 @@
                 a = gelu(out[s:s + rows] + bias_ref[1:2, 0:128])
                 good = ok & (ix + p - 1 >= 0) & (ix + p - 1 < x_count)
                 act2_ref[p, :, b * 128:(b + 1) * 128] = jnp.where(good, a, 0.0).astype(BF16)
+        loads[2].wait()
         out = None
         for i in range(3):
             part = mm(act2_ref[i], t3_ref[i])
@@ -668,10 +732,10 @@
             shifts.append(s % counts[0])
     own = [plane] + [lax.ppermute(plane, "gx", ring("gx", s)) for s in shifts]
     other = [z_neighbour(v, "gz", False) for v in own]
-    args = (ids, b_third, *own, *other, *matrices)
+    args = (ids, b_third, *own, *other, *(pltpu.with_memory_space_constraint(v, pltpu.HBM) for v in matrices))
     (score,) = call(
         conv_kernel(py, counts, shifts), [((1, pz, py), F32)], *args,
-        in_specs=[SMEM] * 2 + [VMEM] * (len(args) - 2),
+        in_specs=[SMEM] * 2 + [VMEM] * (len(args) - 6) + [HBM] * 4,
         scratch=[
             pltpu.VMEM((7, tall, 2 * half), F32),
             pltpu.VMEM((7, rows, 6 * half), BF16),
@@ -679,7 +743,8 @@
             pltpu.VMEM((5, blocks, rows, 768), BF16),
             pltpu.VMEM((3, rows, width), BF16),
             pltpu.VMEM((rows + 8, 128), F32),
-        ], mib=24)
+            pltpu.VMEM((3, 6 * half, width), BF16),
+        ] + [pltpu.VMEM(v.shape, v.dtype) for v in matrices] + [pltpu.SemaphoreType.DMA((4,))], mib=32)
     return jnp.swapaxes(score, 1, 2)
 
 

time: 88.7 us -> 62.6 us (0.71)
  local copies, waits for them, and re-layouts: 18.2 us -> 2.56 us
  starting transfers between devices: 26.8 us -> 19.3 us
  waiting for transfers between devices: 24.8 us -> 23.3 us
  Pallas kernels: 16.7 us -> 15.5 us
    unnamed x49 -> x19, local copies, waits for them, and re-layouts: 16.1 us -> 2.04 us
    ppermute x4 -> x2, waiting for transfers between devices: 7.35 us -> 0.01 us  [x_sides(): lax.ppermute(hi, 'gx', ring('gx', 1))]
    ppermute x4 -> x2, starting transfers between devices: 11 us -> 5.32 us  [x_sides(): lax.ppermute(lo, 'gx', ring('gx', -1))]
    ppermute x2, waiting for transfers between devices: 4.51 us -> 8.94 us  [start(): return (sums, lax.ppermute(sums, 'gx', ring('gx', 2)))]
    ppermute x6, waiting for transfers between devices: 0.52 us -> 3.6 us  [z_neighbour(): return lax.ppermute(pay, axis, ring(axis, 1))]
    ppermute x4 -> x2, starting transfers between devices: 5.56 us -> 3.72 us  [x_sides(): lax.ppermute(hi, 'gx', ring('gx', 1))]
    ppermute x4 -> x2, waiting for transfers between devices: 1.64 us -> 0.01 us  [x_sides(): lax.ppermute(lo, 'gx', ring('gx', -1))]
    pallas_call x10, Pallas kernels: 16.7 us -> 15.5 us  [call(): pl.pallas_call(kernel, in_specs=in_specs or [VMEM] * len(args), out_specs...]
  transfers between devices with their start and end apart: 22 -> 18, of which waited for: 10 -> 10; matrix products, arithmetic and copies ran while one was open for 3% -> 1% of each run, Pallas kernels for 1% -> 2%
where the time goes in v4:
time: 62.6 us; the launch traced here: 62.3 us
  waiting for transfers between devices  23.3 us (37%)
  starting transfers between devices  19.3 us (31%)
  Pallas kernels  15.5 us (25%)
  local copies, waits for them, and re-layouts  2.56 us (4%)
  between operations  1.49 us (2%)
    pallas_call x10, Pallas kernels, call(): pl.pallas_call(kernel, in_specs=in_specs or [VMEM] * len(args), out_specs...  15.5 us
    ppermute x2, waiting for transfers between devices, start(): return (sums, lax.ppermute(sums, 'gx', ring('gx', 2)))  8.94 us
    ppermute x3, waiting for transfers between devices, both_sides(): return lax.ppermute(pay, axis, ring(axis, 1))  6.75 us
    ppermute x2, starting transfers between devices, x_sides(): lax.ppermute(lo, 'gx', ring('gx', -1))  5.32 us
    ppermute x3, starting transfers between devices, both_sides(): return lax.ppermute(pay, axis, ring(axis, 1))  4.67 us
    ppermute x3, waiting for transfers between devices, detector(): own = [plane] + [lax.ppermute(plane, 'gx', ring('gx', s)) for s in shifts]  4.04 us
    ppermute x3, starting transfers between devices, detector(): own = [plane] + [lax.ppermute(plane, 'gx', ring('gx', s)) for s in shifts]  4 us
    ppermute x2, starting transfers between devices, x_sides(): lax.ppermute(hi, 'gx', ring('gx', 1))  3.72 us
  transfers between devices with their start and end apart: 18, of which 10 were waited for; matrix products, arithmetic and copies ran while one was open for 1% of the time, Pallas kernels for 2%

profile of v4, /device:TPU:0, one launch (start us, length us, event | category | flops | bytes accessed | tf_op | source)
XLA Modules:
  0.0 62.3 jit_solution(7943599546091896875)
XLA Ops:
  0.7 1.6 %shard_map.120 = (f32[4,240,128]{2,1,0:T(8,128)S(1)}, f32[4,240,128]{2,1,0:T(8,128)S(1)}, s16[736,128]{1,0:T(8,128)(2,1)S(1)}, s16[736,128]{1,0:T(8,128)(2,1)S(1)}, f32[8,128]{1,0:T(8,128)S(1)}) custom-call(f32[4,240,128]{2,1,0:T(8,128)} %c_hbm.1, f32[4,240,128]{2,1,0:T(8,128)} %d_hbm.1, s32[4,240,128]{2,1,0:T(8,128)} %l_hbm.3), custom_call_target="tpu_custom_call" | custom-call | tf_op jit(solution)/shard_map/pallas_call | solution.py:61
  2.3 3.1 %collective-permute-start = (s16[736,128]{1,0:T(8,128)(2,1)S(1)}, s16[736,128]{1,0:T(8,128)(2,1)S(1)}, u32[]{:S(2)}, u32[]{:S(2)}) collective-permute-start(s16[736,128]{1,0:T(8,128)(2,1)S(1)} %get-tuple-element.27), channel_id=1, source_target_pairs={{0,4},{4,8},{8,12},{12,0},{1,5},{5,9},{9,13},{13,1},{2,6},{6,10},{... | collective-permute-start | bytes 565256 | tf_op jit(solution)/shard_map/ppermute | solution.py:453
  5.4 2.1 %collective-permute-start.1 = (s16[736,128]{1,0:T(8,128)(2,1)S(1)}, s16[736,128]{1,0:T(8,128)(2,1)S(1)}, u32[]{:S(2)}, u32[]{:S(2)}) collective-permute-start(s16[736,128]{1,0:T(8,128)(2,1)S(1)} %get-tuple-element.28), channel_id=1, source_target_pairs={{0,12},{4,0},{8,4},{12,8},{1,13},{5,1},{9,5},{13,9},{2,14},{6,2},{... | collective-permute-start | bytes 565256 | tf_op jit(solution)/shard_map/ppermute | solution.py:453
  7.5 0.9 %collective-permute-start.2 = (f32[8,128]{1,0:T(8,128)S(1)}, f32[8,128]{1,0:T(8,128)S(1)}, u32[]{:S(2)}, u32[]{:S(2)}) collective-permute-start(f32[8,128]{1,0:T(8,128)S(1)} %get-tuple-element.29.refs_4_), channel_id=1, source_target_pairs={{0,8},{4,12},{8,0},{12,4},{1,9},{5,13},{9,1},{13,5},{2,10},{6,14},... | collective-permute-start | bytes 12296 | tf_op jit(solution)/shard_map/ppermute | solution.py:471
  8.4 0.1 copy.16
  8.5 0.0 copy-start.8
  8.6 0.2 copy.17
  8.8 0.5 copy-done.8
  9.2 0.1 copy.18
  9.4 0.1 copy.19
  9.5 0.0 copy-start.4
  9.6 0.0 copy-start.5
  9.6 0.6 %copy-done.4 = f32[16]{0:T(128)S(1)} copy-done((f32[16]{0:T(128)S(1)}, f32[16]{0:T(128)}, u32[]{:S(2)}) %copy-start.4) | copy-done | bytes 88
  10.2 0.0 copy-done.5
  10.2 1.2 %shard_map.121 = (bf16[9,3,16,128]{3,2,1,0:T(8,128)(2,1)S(1)}, bf16[3,768,128]{2,1,0:T(8,128)(2,1)S(1)}, bf16[3,640,128]{2,1,0:T(8,128)(2,1)S(1)}, f32[8,640]{1,0:T(8,128)S(1)}, f32[8,128]{1,0:T(8,128)S(1)}) custom-call(bf16[432,16]{1,0:T(8,128)(2,1)S(1)} %bitcast.15, bf16[432,16]{1,0:T(8,128)(2,1)S(1)} %bitcast.14, bf16[144,3]{1,0:T(8,128)(2,1)S(1)} %bitcast.16, ...), custom_call_target="tpu_custom_call" | custom-call | tf_op jit(solution)/shard_map/pallas_call | solution.py:61
  11.4 0.8 %copy-done.1 = bf16[3,640,128]{2,1,0:T(8,128)(2,1)} copy-done((bf16[3,640,128]{2,1,0:T(8,128)(2,1)}, bf16[3,640,128]{2,1,0:T(8,128)(2,1)S(1)}, u32[]{:S(2)}) %copy-start.1) | copy-done | bytes 491544
  12.2 4.1 %collective-permute-done.2.refs_5_ = f32[8,128]{1,0:T(8,128)S(1)} collective-permute-done((f32[8,128]{1,0:T(8,128)S(1)}, f32[8,128]{1,0:T(8,128)S(1)}, u32[]{:S(2)}, u32[]{:S(2)}) %collective-permute-start.2) | collective-permute-done | bytes 4128 | tf_op jit(solution)/shard_map/ppermute | solution.py:471
  16.3 0.0 collective-permute-done.refs_2_.lo_ref
  16.3 0.0 collective-permute-done.1.refs_3_.hi_ref
  16.4 1.6 %collective-permute-start.3 = (f32[2,24,128]{2,1,0:T(8,128)S(1)}, f32[2,24,128]{2,1,0:T(8,128)S(1)}, u32[]{:S(2)}, u32[]{:S(2)}) collective-permute-start(f32[2,24,128]{2,1,0:T(8,128)S(1)} %shard_map.122.refs_5_.yp_ref), channel_id=1, source_target_pairs={{0,2},{2,0},{1,3},{3,1},{4,6},{6,4},{5,7},{7,5},{8,10},{10,8},{9,1... | collective-permute-start | bytes 73736 | tf_op jit(solution)/shard_map/ppermute | solution.py:435
  17.9 2.3 %collective-permute-done.3.refs_4_.yr_ref = f32[2,24,128]{2,1,0:T(8,128)S(1)} collective-permute-done((f32[2,24,128]{2,1,0:T(8,128)S(1)}, f32[2,24,128]{2,1,0:T(8,128)S(1)}, u32[]{:S(2)}, u32[]{:S(2)}) %collective-permute-start.3) | collective-permute-done | bytes 24608 | tf_op jit(solution)/shard_map/ppermute | solution.py:435
  20.3 0.3 shard_map.123
  20.6 0.1 collective-permute-start.4
  20.7 1.5 %collective-permute-done.4.zr_ref = f32[2,272,128]{2,1,0:T(8,128)S(1)} collective-permute-done((f32[2,272,128]{2,1,0:T(8,128)S(1)}, f32[2,272,128]{2,1,0:T(8,128)S(1)}, u32[]{:S(2)}, u32[]{:S(2)}) %collective-permute-start.4) | collective-permute-done | bytes 278560 | tf_op jit(solution)/shard_map/ppermute | solution.py:441
  22.2 2.2 %shard_map.124 = (f32[4,240,128]{2,1,0:T(8,128)S(1)}, f32[6,272,128]{2,1,0:T(8,128)S(1)}, f32[240,128]{1,0:T(8,128)S(1)}, s16[496,128]{1,0:T(8,128)(2,1)S(1)}, s...) custom-call(f32[4,240,128]{2,1,0:T(8,128)S(1)} %get-tuple-element.25.refs_0_.f_ref, ...), custom_call_target="tpu_custom_call" | custom-call | tf_op jit(solution)/shard_map/pallas_call | solution.py:61
  24.4 0.6 %collective-permute-start.5 = (s16[496,128]{1,0:T(8,128)(2,1)S(1)}, s16[496,128]{1,0:T(8,128)(2,1)S(1)}, u32[]{:S(2)}, u32[]{:S(2)}) collective-permute-start(s16[496,128]{1,0:T(8,128)(2,1)S(1)} %get-tuple-element.34), channel_id=1, source_target_pairs={{0,4},{4,8},{8,12},{12,0},{1,5},{5,9},{9,13},{13,1},{2,6},{6,10},{... | collective-permute-start | bytes 380936 | tf_op jit(solution)/shard_map/ppermute | solution.py:453
  25.1 3.2 %collective-permute-start.6 = (s16[496,128]{1,0:T(8,128)(2,1)S(1)}, s16[496,128]{1,0:T(8,128)(2,1)S(1)}, u32[]{:S(2)}, u32[]{:S(2)}) collective-permute-start(s16[496,128]{1,0:T(8,128)(2,1)S(1)} %get-tuple-element.35), channel_id=1, source_target_pairs={{0,12},{4,0},{8,4},{12,8},{1,13},{5,1},{9,5},{13,9},{2,14},{6,2},{... | collective-permute-start | bytes 380936 | tf_op jit(solution)/shard_map/ppermute | solution.py:453
  28.3 4.9 %collective-permute-done.7.refs_4_ = f32[8,128]{1,0:T(8,128)S(1)} collective-permute-done((f32[8,128]{1,0:T(8,128)S(1)}, f32[8,128]{1,0:T(8,128)S(1)}, u32[]{:S(2)}, u32[]{:S(2)}) %collective-permute-start.7) | collective-permute-done | bytes 4128 | tf_op jit(solution)/shard_map/ppermute | solution.py:471
  33.2 0.0 collective-permute-done.5.refs_1_.lo_ref
  33.2 0.0 collective-permute-done.6.refs_2_.hi_ref
  33.2 1.6 %collective-permute-start.8 = (f32[2,24,128]{2,1,0:T(8,128)S(1)}, f32[2,24,128]{2,1,0:T(8,128)S(1)}, u32[]{:S(2)}, u32[]{:S(2)}) collective-permute-start(f32[2,24,128]{2,1,0:T(8,128)S(1)} %shard_map.125.refs_4_.yp_ref), channel_id=1, source_target_pairs={{0,2},{2,0},{1,3},{3,1},{4,6},{6,4},{5,7},{7,5},{8,10},{10,8},{9,1... | collective-permute-start | bytes 73736 | tf_op jit(solution)/shard_map/ppermute | solution.py:435
  34.7 2.3 %collective-permute-done.8.refs_3_.yr_ref = f32[2,24,128]{2,1,0:T(8,128)S(1)} collective-permute-done((f32[2,24,128]{2,1,0:T(8,128)S(1)}, f32[2,24,128]{2,1,0:T(8,128)S(1)}, u32[]{:S(2)}, u32[]{:S(2)}) %collective-permute-start.8) | collective-permute-done | bytes 24608 | tf_op jit(solution)/shard_map/ppermute | solution.py:435
  37.1 0.2 shard_map.126
  37.3 0.1 collective-permute-start.9
  37.4 1.5 %collective-permute-done.9.zr_ref = f32[2,272,128]{2,1,0:T(8,128)S(1)} collective-permute-done((f32[2,272,128]{2,1,0:T(8,128)S(1)}, f32[2,272,128]{2,1,0:T(8,128)S(1)}, u32[]{:S(2)}, u32[]{:S(2)}) %collective-permute-start.9) | collective-permute-done | bytes 278560 | tf_op jit(solution)/shard_map/ppermute | solution.py:441
  38.9 3.3 %shard_map.127 = (f32[4,240,128]{2,1,0:T(8,128)}, f32[4,240,128]{2,1,0:T(8,128)}, f32[4,240,128]{2,1,0:T(8,128)}, bf16[60,128]{1,0:T(8,128)(2,1)S(1)}, bf16[2,16,128]{2,1,0:T(8,128)(2,1)S(1)}) custom-call(f32[4,240,128]{2,1,0:T(8,128)S(1)} %get-tuple-element.31.refs_0_.f_ref, f32[6,272,128]{2,1,0:T(8,128)S(1)} %get-tuple-element.32.a2_ref, ...), custom_call_target="tpu_custom_call" | custom-call | tf_op jit(solution)/shard_map/pallas_call | solution.py:61
  42.2 1.6 %collective-permute-start.10 = (bf16[2,16,128]{2,1,0:T(8,128)(2,1)S(1)}, bf16[2,16,128]{2,1,0:T(8,128)(2,1)S(1)}, u32[]{:S(2)}, u32[]{:S(2)}) collective-permute-start(bf16[2,16,128]{2,1,0:T(8,128)(2,1)S(1)} %get-tuple-element.41), channel_id=1, source_target_pairs={{0,2},{2,0},{1,3},{3,1},{4,6},{6,4},{5,7},{7,5},{8,10},{10,8},{9,1... | collective-permute-start | bytes 24584 | tf_op jit(solution)/shard_map/ppermute | solution.py:435
  43.8 0.1 pad_add_fusion.ids_ref.refs_0_
  43.9 2.1 %collective-permute-done.10.yr_ref = bf16[2,16,128]{2,1,0:T(8,128)(2,1)S(1)} collective-permute-done((bf16[2,16,128]{2,1,0:T(8,128)(2,1)S(1)}, bf16[2,16,128]{2,1,0:T(8,128)(2,1)S(1)}, u32[]{:S(2)}, u32[]{:S(2)}) %collective-permute-start.10) | collective-permute-done | bytes 8224 | tf_op jit(solution)/shard_map/ppermute | solution.py:435
  45.9 0.6 shard_map.128.refs_2_
  46.5 2.0 %collective-permute-start.11 = (bf16[80,128]{1,0:T(8,128)(2,1)S(1)}, bf16[80,128]{1,0:T(8,128)(2,1)S(1)}, u32[]{:S(2)}, u32[]{:S(2)}) collective-permute-start(bf16[80,128]{1,0:T(8,128)(2,1)S(1)} %shard_map.128.refs_2_), channel_id=1, source_target_pairs={{0,4},{4,8},{8,12},{12,0},{1,5},{5,9},{9,13},{13,1},{2,6},{6,10},{... | collective-permute-start | bytes 61448 | tf_op jit(solution)/shard_map/ppermute | solution.py:733
  48.5 1.9 %collective-permute-start.12 = (bf16[80,128]{1,0:T(8,128)(2,1)S(1)}, bf16[80,128]{1,0:T(8,128)(2,1)S(1)}, u32[]{:S(2)}, u32[]{:S(2)}) collective-permute-start(bf16[80,128]{1,0:T(8,128)(2,1)S(1)} %shard_map.128.refs_2_), channel_id=1, source_target_pairs={{0,12},{4,0},{8,4},{12,8},{1,13},{5,1},{9,5},{13,9},{2,14},{6,2},{... | collective-permute-start | bytes 61448 | tf_op jit(solution)/shard_map/ppermute | solution.py:733
  50.4 0.1 collective-permute-start.13
  50.5 1.9 %collective-permute-done.11.refs_3_ = bf16[80,128]{1,0:T(8,128)(2,1)S(1)} collective-permute-done((bf16[80,128]{1,0:T(8,128)(2,1)S(1)}, bf16[80,128]{1,0:T(8,128)(2,1)S(1)}, u32[]{:S(2)}, u32[]{:S(2)}) %collective-permute-start.11) | collective-permute-done | bytes 20512 | tf_op jit(solution)/shard_map/ppermute | solution.py:733
  52.4 0.5 collective-permute-start.16
  53.0 2.1 %collective-permute-done.13.refs_5_ = bf16[80,128]{1,0:T(8,128)(2,1)S(1)} collective-permute-done((bf16[80,128]{1,0:T(8,128)(2,1)S(1)}, bf16[80,128]{1,0:T(8,128)(2,1)S(1)}, u32[]{:S(2)}, u32[]{:S(2)}) %collective-permute-start.13) | collective-permute-done | bytes 20512 | tf_op jit(solution)/shard_map/ppermute | solution.py:733
  55.7 0.5 collective-permute-done.17.refs_9_
  56.2 6.0 %shard_map.129 = f32[1,32,60]{2,1,0:T(8,128)} custom-call(s32[3]{0:T(128)S(1)} %pad_add_fusion.ids_ref.refs_0_, f32[1]{0:T(128)S(6)} %copy.20.refs_1_, bf16[80,128]{1,0:T(8,128)(2,1)S(1)} %shard_map.128.refs_2_, bf16[80,128]{1,0:T(8,128)(2,1)S(1)} %collective-permute-done.11.refs_3_, bf16[80,128]{1,0:T(8,128)(2,1)S(1)} %collective-permute-done.12.refs_4_, ...), custom_call_target="tpu_custom_call" | custom-call | tf_op jit(solution)/shard_map/pallas_call | solution.py:61
  (23 shorter events, 0.1 us)
Async XLA Ops:
  0.6 7.8 %copy-start.7 = (bf16[27,16,4]{0,2,1:T(4,128)(2,1)S(1)}, bf16[27,16,4]{0,2,1:T(4,128)(2,1)}, u32[]{:S(2)}) copy-start(bf16[27,16,4]{0,2,1:T(4,128)(2,1)} %param.12) | copy-start | bytes 10372
  0.6 7.9 %copy-start.6 = (bf16[27,16,16]{0,2,1:T(8,128)(2,1)S(1)}, bf16[27,16,16]{0,2,1:T(8,128)(2,1)}, u32[]{:S(2)}) copy-start(bf16[27,16,16]{0,2,1:T(8,128)(2,1)} %param.14) | copy-start | bytes 41476
  2.3 14.0 %collective-permute-start = (s16[736,128]{1,0:T(8,128)(2,1)S(1)}, s16[736,128]{1,0:T(8,128)(2,1)S(1)}, u32[]{:S(2)}, u32[]{:S(2)}) collective-permute-start(s16[736,128]{1,0:T(8,128)(2,1)S(1)} %get-tuple-element.27), channel_id=1, source_target_pairs={{0,4},{4,8},{8,12},{12,0},{1,5},{5,9},{9,13},{13,1},{2,6},{6,10},{... | collective-permute-start | bytes 565256 | tf_op jit(solution)/shard_map/ppermute | solution.py:453
  5.4 10.9 %collective-permute-start.1 = (s16[736,128]{1,0:T(8,128)(2,1)S(1)}, s16[736,128]{1,0:T(8,128)(2,1)S(1)}, u32[]{:S(2)}, u32[]{:S(2)}) collective-permute-start(s16[736,128]{1,0:T(8,128)(2,1)S(1)} %get-tuple-element.28), channel_id=1, source_target_pairs={{0,12},{4,0},{8,4},{12,8},{1,13},{5,1},{9,5},{13,9},{2,14},{6,2},{... | collective-permute-start | bytes 565256 | tf_op jit(solution)/shard_map/ppermute | solution.py:453
  7.5 8.8 %collective-permute-start.2 = (f32[8,128]{1,0:T(8,128)S(1)}, f32[8,128]{1,0:T(8,128)S(1)}, u32[]{:S(2)}, u32[]{:S(2)}) collective-permute-start(f32[8,128]{1,0:T(8,128)S(1)} %get-tuple-element.29.refs_4_), channel_id=1, source_target_pairs={{0,8},{4,12},{8,0},{12,4},{1,9},{5,13},{9,1},{13,5},{2,10},{6,14},... | collective-permute-start | bytes 12296 | tf_op jit(solution)/shard_map/ppermute | solution.py:471
  8.5 0.7 %copy-start.8 = (bf16[27,1,16]{0,2,1:T(8,128)(2,1)S(1)}, bf16[27,1,16]{0,2,1:T(8,128)(2,1)}, u32[]{:S(2)}) copy-start(bf16[27,1,16]{0,2,1:T(8,128)(2,1)} %param.16) | copy-start | bytes 2596
  9.5 0.7 %copy-start.4 = (f32[16]{0:T(128)S(1)}, f32[16]{0:T(128)}, u32[]{:S(2)}) copy-start(f32[16]{0:T(128)} %param.13) | copy-start | bytes 196
  9.6 0.7 %copy-start.5 = (f32[16]{0:T(128)S(1)}, f32[16]{0:T(128)}, u32[]{:S(2)}) copy-start(f32[16]{0:T(128)} %param.15) | copy-start | bytes 196
  11.4 0.8 %copy-start.1 = (bf16[3,640,128]{2,1,0:T(8,128)(2,1)}, bf16[3,640,128]{2,1,0:T(8,128)(2,1)S(1)}, u32[]{:S(2)}) copy-start(bf16[3,640,128]{2,1,0:T(8,128)(2,1)S(1)} %get-tuple-element.44.refs_12_) | copy-start | bytes 1474564
  12.2 4.1 %copy-start = (bf16[3,768,128]{2,1,0:T(8,128)(2,1)}, bf16[3,768,128]{2,1,0:T(8,128)(2,1)S(1)}, u32[]{:S(2)}) copy-start(bf16[3,768,128]{2,1,0:T(8,128)(2,1)S(1)} %get-tuple-element.43.refs_11_) | copy-start | bytes 1769476
  12.2 4.1 %copy-start.2 = (bf16[9,3,16,128]{3,2,1,0:T(8,128)(2,1)}, bf16[9,3,16,128]{3,2,1,0:T(8,128)(2,1)S(1)}, u32[]{:S(2)}) copy-start(bf16[9,3,16,128]{3,2,1,0:T(8,128)(2,1)S(1)} %get-tuple-element.42.refs_10_) | copy-start | bytes 331780
  12.2 4.1 %copy-start.3 = (f32[8,640]{1,0:T(8,128)}, f32[8,640]{1,0:T(8,128)S(1)}, u32[]{:S(2)}) copy-start(f32[8,640]{1,0:T(8,128)S(1)} %get-tuple-element.45.refs_13_) | copy-start | bytes 61444
  16.4 3.9 %collective-permute-start.3 = (f32[2,24,128]{2,1,0:T(8,128)S(1)}, f32[2,24,128]{2,1,0:T(8,128)S(1)}, u32[]{:S(2)}, u32[]{:S(2)}) collective-permute-start(f32[2,24,128]{2,1,0:T(8,128)S(1)} %shard_map.122.refs_5_.yp_ref), channel_id=1, source_target_pairs={{0,2},{2,0},{1,3},{3,1},{4,6},{6,4},{5,7},{7,5},{8,10},{10,8},{9,1... | collective-permute-start | bytes 73736 | tf_op jit(solution)/shard_map/ppermute | solution.py:435
  20.6 1.6 %collective-permute-start.4 = (f32[2,272,128]{2,1,0:T(8,128)S(1)}, f32[2,272,128]{2,1,0:T(8,128)S(1)}, u32[]{:S(2)}, u32[]{:S(2)}) collective-permute-start(f32[2,272,128]{2,1,0:T(8,128)S(1)} %shard_map.123), channel_id=1, source_target_pairs={{0,1},{1,0},{2,3},{3,2},{4,5},{5,4},{6,7},{7,6},{8,9},{9,8},{10,11... | collective-permute-start | bytes 835592 | tf_op jit(solution)/shard_map/ppermute | solution.py:441
  24.4 8.7 %collective-permute-start.5 = (s16[496,128]{1,0:T(8,128)(2,1)S(1)}, s16[496,128]{1,0:T(8,128)(2,1)S(1)}, u32[]{:S(2)}, u32[]{:S(2)}) collective-permute-start(s16[496,128]{1,0:T(8,128)(2,1)S(1)} %get-tuple-element.34), channel_id=1, source_target_pairs={{0,4},{4,8},{8,12},{12,0},{1,5},{5,9},{9,13},{13,1},{2,6},{6,10},{... | collective-permute-start | bytes 380936 | tf_op jit(solution)/shard_map/ppermute | solution.py:453
  25.1 8.1 %collective-permute-start.6 = (s16[496,128]{1,0:T(8,128)(2,1)S(1)}, s16[496,128]{1,0:T(8,128)(2,1)S(1)}, u32[]{:S(2)}, u32[]{:S(2)}) collective-permute-start(s16[496,128]{1,0:T(8,128)(2,1)S(1)} %get-tuple-element.35), channel_id=1, source_target_pairs={{0,12},{4,0},{8,4},{12,8},{1,13},{5,1},{9,5},{13,9},{2,14},{6,2},{... | collective-permute-start | bytes 380936 | tf_op jit(solution)/shard_map/ppermute | solution.py:453
  28.3 4.9 %collective-permute-start.7 = (f32[8,128]{1,0:T(8,128)S(1)}, f32[8,128]{1,0:T(8,128)S(1)}, u32[]{:S(2)}, u32[]{:S(2)}) collective-permute-start(f32[8,128]{1,0:T(8,128)S(1)} %get-tuple-element.36.refs_3_), channel_id=1, source_target_pairs={{0,8},{4,12},{8,0},{12,4},{1,9},{5,13},{9,1},{13,5},{2,10},{6,14},... | collective-permute-start | bytes 12296 | tf_op jit(solution)/shard_map/ppermute | solution.py:471
  33.2 3.9 %collective-permute-start.8 = (f32[2,24,128]{2,1,0:T(8,128)S(1)}, f32[2,24,128]{2,1,0:T(8,128)S(1)}, u32[]{:S(2)}, u32[]{:S(2)}) collective-permute-start(f32[2,24,128]{2,1,0:T(8,128)S(1)} %shard_map.125.refs_4_.yp_ref), channel_id=1, source_target_pairs={{0,2},{2,0},{1,3},{3,1},{4,6},{6,4},{5,7},{7,5},{8,10},{10,8},{9,1... | collective-permute-start | bytes 73736 | tf_op jit(solution)/shard_map/ppermute | solution.py:435
  37.3 1.6 %collective-permute-start.9 = (f32[2,272,128]{2,1,0:T(8,128)S(1)}, f32[2,272,128]{2,1,0:T(8,128)S(1)}, u32[]{:S(2)}, u32[]{:S(2)}) collective-permute-start(f32[2,272,128]{2,1,0:T(8,128)S(1)} %shard_map.126), channel_id=1, source_target_pairs={{0,1},{1,0},{2,3},{3,2},{4,5},{5,4},{6,7},{7,6},{8,9},{9,8},{10,11... | collective-permute-start | bytes 835592 | tf_op jit(solution)/shard_map/ppermute | solution.py:441
  42.2 3.7 %collective-permute-start.10 = (bf16[2,16,128]{2,1,0:T(8,128)(2,1)S(1)}, bf16[2,16,128]{2,1,0:T(8,128)(2,1)S(1)}, u32[]{:S(2)}, u32[]{:S(2)}) collective-permute-start(bf16[2,16,128]{2,1,0:T(8,128)(2,1)S(1)} %get-tuple-element.41), channel_id=1, source_target_pairs={{0,2},{2,0},{1,3},{3,1},{4,6},{6,4},{5,7},{7,5},{8,10},{10,8},{9,1... | collective-permute-start | bytes 24584 | tf_op jit(solution)/shard_map/ppermute | solution.py:435
  46.5 5.9 %collective-permute-start.11 = (bf16[80,128]{1,0:T(8,128)(2,1)S(1)}, bf16[80,128]{1,0:T(8,128)(2,1)S(1)}, u32[]{:S(2)}, u32[]{:S(2)}) collective-permute-start(bf16[80,128]{1,0:T(8,128)(2,1)S(1)} %shard_map.128.refs_2_), channel_id=1, source_target_pairs={{0,4},{4,8},{8,12},{12,0},{1,5},{5,9},{9,13},{13,1},{2,6},{6,10},{... | collective-permute-start | bytes 61448 | tf_op jit(solution)/shard_map/ppermute | solution.py:733
  48.5 3.9 %collective-permute-start.12 = (bf16[80,128]{1,0:T(8,128)(2,1)S(1)}, bf16[80,128]{1,0:T(8,128)(2,1)S(1)}, u32[]{:S(2)}, u32[]{:S(2)}) collective-permute-start(bf16[80,128]{1,0:T(8,128)(2,1)S(1)} %shard_map.128.refs_2_), channel_id=1, source_target_pairs={{0,12},{4,0},{8,4},{12,8},{1,13},{5,1},{9,5},{13,9},{2,14},{6,2},{... | collective-permute-start | bytes 61448 | tf_op jit(solution)/shard_map/ppermute | solution.py:733
  50.4 4.7 %collective-permute-start.13 = (bf16[80,128]{1,0:T(8,128)(2,1)S(1)}, bf16[80,128]{1,0:T(8,128)(2,1)S(1)}, u32[]{:S(2)}, u32[]{:S(2)}) collective-permute-start(bf16[80,128]{1,0:T(8,128)(2,1)S(1)} %shard_map.128.refs_2_), channel_id=1, source_target_pairs={{0,8},{4,12},{8,0},{12,4},{1,9},{5,13},{9,1},{13,5},{2,10},{6,14},... | collective-permute-start | bytes 61448 | tf_op jit(solution)/shard_map/ppermute | solution.py:733
  50.5 5.2 %collective-permute-start.14 = (bf16[80,128]{1,0:T(8,128)(2,1)S(1)}, bf16[80,128]{1,0:T(8,128)(2,1)S(1)}, u32[]{:S(2)}, u32[]{:S(2)}) collective-permute-start(bf16[80,128]{1,0:T(8,128)(2,1)S(1)} %shard_map.128.refs_2_), channel_id=1, source_target_pairs={{0,1},{1,0},{2,3},{3,2},{4,5},{5,4},{6,7},{7,6},{8,9},{9,8},{10,11... | collective-permute-start | bytes 61448 | tf_op jit(solution)/shard_map/ppermute | solution.py:441
  52.4 3.3 %collective-permute-start.15 = (bf16[80,128]{1,0:T(8,128)(2,1)S(1)}, bf16[80,128]{1,0:T(8,128)(2,1)S(1)}, u32[]{:S(2)}, u32[]{:S(2)}) collective-permute-start(bf16[80,128]{1,0:T(8,128)(2,1)S(1)} %collective-permute-done.11.refs_3_), channel_id=1, source_target_pairs={{0,1},{1,0},{2,3},{3,2},{4,5},{5,4},{6,7},{7,6},{8,9},{9,8},{10,11... | collective-permute-start | bytes 61448 | tf_op jit(solution)/shard_map/ppermute | solution.py:441
  52.4 3.3 %collective-permute-start.16 = (bf16[80,128]{1,0:T(8,128)(2,1)S(1)}, bf16[80,128]{1,0:T(8,128)(2,1)S(1)}, u32[]{:S(2)}, u32[]{:S(2)}) collective-permute-start(bf16[80,128]{1,0:T(8,128)(2,1)S(1)} %collective-permute-done.12.refs_4_), channel_id=1, source_target_pairs={{0,1},{1,0},{2,3},{3,2},{4,5},{5,4},{6,7},{7,6},{8,9},{9,8},{10,11... | collective-permute-start | bytes 61448 | tf_op jit(solution)/shard_map/ppermute | solution.py:441
  55.1 1.2 %collective-permute-start.17 = (bf16[80,128]{1,0:T(8,128)(2,1)S(1)}, bf16[80,128]{1,0:T(8,128)(2,1)S(1)}, u32[]{:S(2)}, u32[]{:S(2)}) collective-permute-start(bf16[80,128]{1,0:T(8,128)(2,1)S(1)} %collective-permute-done.13.refs_5_), channel_id=1, source_target_pairs={{0,1},{1,0},{2,3},{3,2},{4,5},{5,4},{6,7},{7,6},{8,9},{9,8},{10,11... | collective-permute-start | bytes 61448 | tf_op jit(solution)/shard_map/ppermute | solution.py:441

commit v5 on v4

--- a/solution.py
+++ b/solution.py
@@ -547,10 +547,11 @@
 SHIFTS = tuple(k for k in range(-3, 10) if k % (16 // CIN) == 3)
 
 
-def weight_kernel(w1_ref, w2_ref, w3_ref, b1_ref, b2_ref, d1_hbm, t2_hbm, t3_hbm, bias_hbm, order_ref,
-                  d1_ref, t2_ref, t3_ref, bias_ref, sems):
+def weight_kernel(w1_ref, w2_ref, w3_ref, b1_ref, b2_ref, t1_hbm, t2_hbm, t3_hbm, bias_hbm, order_ref,
+                  t1_ref, t2_ref, t3_ref, bias_ref, sems):
     n1 = bias_ref.shape[1]
-    pz = n1 // CH // 8 * 8 - 8
+    k1 = t1_ref.shape[1] // 3
+    pz = k1 // (2 * CIN)
     spread = one_hot(iota((CH, 128), 1) % CH == iota((CH, 128), 0))
     tile1 = mm(w1_ref[...], spread)
     tile2 = mm(w2_ref[...], spread)
@@ -571,8 +572,11 @@
     for i in range(3):
         for j in range(3):
             tap = 9 * i + 3 * j
-            for k, shift in enumerate(SHIFTS):
-                d1_ref[3 * i + j, k] = tile(tile1, tap, 1, step1, shift)
+            known = {k: tile(tile1, tap, 1, step1, k) for k in SHIFTS}
+            for rb in range(k1 // 16):
+                for cb in range(n1 // 128):
+                    t1_ref[i, j * k1 + rb * 16:j * k1 + rb * 16 + 16, cb * 128:(cb + 1) * 128] = known.get(
+                        tile_shift(rb, cb, pz), zero)
             for rb in range(16):
                 t2_ref[i, j * 256 + rb * 16:j * 256 + rb * 16 + 16, :] = (
                     tile(tile2, tap, 1, step2, rb) if rb < 10 else zero)
@@ -583,7 +587,7 @@
         bias_ref[k:k + 1, :] = jnp.dot(ref[...], wide, precision=lax.Precision.HIGHEST, preferred_element_type=F32)
     order_ref[...] = jnp.zeros(order_ref.shape, F32)
     copies = [pltpu.make_async_copy(src, dst, sems.at[k]) for k, (src, dst) in enumerate(
-        ((d1_ref, d1_hbm), (t2_ref, t2_hbm), (t3_ref, t3_hbm), (bias_ref, bias_hbm)))]
+        ((t1_ref, t1_hbm), (t2_ref, t2_hbm), (t3_ref, t3_hbm), (bias_ref, bias_hbm)))]
     for c in copies:
         c.start()
     for c in copies:
@@ -595,11 +599,15 @@
     rows1 = jnp.tile(jnp.swapaxes(w_first, 1, 2), (1, 16 // CIN, 1)).reshape(27 * 16, CH)
     rows2 = jnp.swapaxes(w_second, 1, 2).reshape(27 * CH, CH)
     rows3 = w_third.reshape(3, 3, 3, CH).transpose(0, 2, 3, 1).reshape(9 * CH, 3)
-    outs = [((9, len(SHIFTS), 16, 128), BF16), ((3, 768, 128), BF16), ((3, width, 128), BF16), ((8, width), F32)]
-    return call(
-        weight_kernel, outs + [((8, 128), F32)], rows1, rows2, rows3, b_first[None], b_second[None],
+    outs = [((3, 6 * half, width), BF16), ((3, 768, 128), BF16), ((3, width, 128), BF16), ((8, width), F32)]
+    return pl.pallas_call(
+        weight_kernel,
+        in_specs=[VMEM] * 5,
         out_specs=[HBM] * 4 + [VMEM],
-        scratch=[pltpu.VMEM(*v) for v in outs] + [pltpu.SemaphoreType.DMA((4,))])
+        out_shape=[pltpu.HBM(*v) for v in outs] + [jax.ShapeDtypeStruct((8, 128), F32)],
+        scratch_shapes=[pltpu.VMEM(*v) for v in outs] + [pltpu.SemaphoreType.DMA((4,))],
+        compiler_params=pltpu.CompilerParams(vmem_limit_bytes=16 * 1024 * 1024),
+    )(rows1, rows2, rows3, b_first[None], b_second[None])
 
 
 def gelu(x):
@@ -627,14 +635,8 @@
         ids_ref, b3_ref = refs[:2]
         own = refs[2:3 + n]
         other = refs[3 + n:4 + 2 * n]
-        hbm = refs[4 + 2 * n:8 + 2 * n]
-        out_ref = refs[8 + 2 * n]
-        (in_ref, lhs1_ref, act1_ref, lhs2_ref, act2_ref, tail_ref, t1_ref,
-         d1_ref, t2_ref, t3_ref, bias_ref, sems) = refs[9 + 2 * n:]
-        loads = [pltpu.make_async_copy(src, dst, sems.at[k])
-                 for k, (src, dst) in enumerate(zip(hbm, (d1_ref, t2_ref, t3_ref, bias_ref)))]
-        for c in loads:
-            c.start()
+        t1_ref, t2_ref, t3_ref, bias_ref, out_ref = refs[4 + 2 * n:9 + 2 * n]
+        in_ref, lhs1_ref, act1_ref, lhs2_ref, act2_ref, tail_ref = refs[9 + 2 * n:]
         ix, iy, iz = ids_ref[0], ids_ref[1], ids_ref[2]
         half = own[0].shape[1]
         pz = half // CIN
@@ -655,16 +657,6 @@
             for j in range(3):
                 start = TOP - 3 + j
                 lhs1_ref[w, :, j * k1:(j + 1) * k1] = in_ref[w, start:start + rows, :].astype(BF16)
-        loads[0].wait()
-        loads[3].wait()
-        zero = jnp.zeros((16, 128), BF16)
-        for i in range(3):
-            for j in range(3):
-                for rb in range(k1 // 16):
-                    for cb in range(t1_ref.shape[2] // 128):
-                        shift = tile_shift(rb, cb, pz)
-                        t1_ref[i, j * k1 + rb * 16:j * k1 + rb * 16 + 16, cb * 128:(cb + 1) * 128] = (
-                            d1_ref[3 * i + j, SHIFTS.index(shift)] if shift in SHIFTS else zero)
         out = None
         for i in range(3):
             part = mm(lhs1_ref[i:i + 5].reshape(5 * rows, 3 * k1), t1_ref[i])
@@ -680,7 +672,6 @@
             act1_ref[p, 0:rows, 0:width] = jnp.where(good, a, 0.0)
             act1_ref[p, rows:, 0:width] = jnp.zeros((act1_ref.shape[1] - rows, width), F32)
             act1_ref[p, :, width:] = jnp.zeros((act1_ref.shape[1], act1_ref.shape[2] - width), F32)
-        loads[1].wait()
         blocks = lhs2_ref.shape[1]
         for p in range(5):
             for j in range(3):
@@ -701,7 +692,6 @@
                 a = gelu(out[s:s + rows] + bias_ref[1:2, 0:128])
                 good = ok & (ix + p - 1 >= 0) & (ix + p - 1 < x_count)
                 act2_ref[p, :, b * 128:(b + 1) * 128] = jnp.where(good, a, 0.0).astype(BF16)
-        loads[2].wait()
         out = None
         for i in range(3):
             part = mm(act2_ref[i], t3_ref[i])
@@ -732,10 +722,10 @@
             shifts.append(s % counts[0])
     own = [plane] + [lax.ppermute(plane, "gx", ring("gx", s)) for s in shifts]
     other = [z_neighbour(v, "gz", False) for v in own]
-    args = (ids, b_third, *own, *other, *(pltpu.with_memory_space_constraint(v, pltpu.HBM) for v in matrices))
+    args = (ids, b_third, *own, *other, *matrices)
     (score,) = call(
         conv_kernel(py, counts, shifts), [((1, pz, py), F32)], *args,
-        in_specs=[SMEM] * 2 + [VMEM] * (len(args) - 6) + [HBM] * 4,
+        in_specs=[SMEM] * 2 + [VMEM] * (len(args) - 2),
         scratch=[
             pltpu.VMEM((7, tall, 2 * half), F32),
             pltpu.VMEM((7, rows, 6 * half), BF16),
@@ -743,8 +733,7 @@
             pltpu.VMEM((5, blocks, rows, 768), BF16),
             pltpu.VMEM((3, rows, width), BF16),
             pltpu.VMEM((rows + 8, 128), F32),
-            pltpu.VMEM((3, 6 * half, width), BF16),
-        ] + [pltpu.VMEM(v.shape, v.dtype) for v in matrices] + [pltpu.SemaphoreType.DMA((4,))], mib=32)
+        ], mib=32)
     return jnp.swapaxes(score, 1, 2)
 
 

time: 62.6 us -> 64.2 us (1.026)
  local copies, waits for them, and re-layouts: 2.56 us -> 7.03 us
  waiting for transfers between devices: 23.3 us -> 20.3 us
    pallas_call x10 -> x9, Pallas kernels: 15.5 us -> 12.6 us  [call(): pl.pallas_call(kernel, in_specs=in_specs or [VMEM] * len(args), out_specs...]
    unnamed x19 -> x13, local copies, waits for them, and re-layouts: 2.04 us -> 4.96 us
    pallas_call x0 -> x1, Pallas kernels: none -> 2.79 us  [weight_matrices(): pl.pallas_call(weight_kernel, in_specs=[VMEM] * 5, out_specs=[HBM] * 4 +...]
    ppermute x2, waiting for transfers between devices: 8.94 us -> 6.16 us  [start(): return (sums, lax.ppermute(sums, 'gx', ring('gx', 2)))]
    transpose x1, local copies, waits for them, and re-layouts: 0.2 us -> 1.04 us  [weight_matrices(): rows2 = jnp.swapaxes(w_second, 1, 2).reshape(27 * CH, CH)]
    transpose x1, local copies, waits for them, and re-layouts: 0.12 us -> 0.83 us  [weight_matrices(): jnp.swapaxes(w_first, 1, 2)]
  transfers between devices with their start and end apart: 18 -> 18, of which waited for: 10 -> 10; matrix products, arithmetic and copies ran while one was open for 1% -> 5% of each run, Pallas kernels for 2% -> 4%
where the time goes in v5:
time: 64.2 us; the launch traced here: 63.8 us
  waiting for transfers between devices  20.3 us (32%)
  starting transfers between devices  19.5 us (30%)
  Pallas kernels  15.4 us (24%)
  local copies, waits for them, and re-layouts  7.03 us (11%)
  between operations  1.43 us (2%)
    pallas_call x9, Pallas kernels, call(): pl.pallas_call(kernel, in_specs=in_specs or [VMEM] * len(args), out_specs...  12.6 us
    ppermute x3, waiting for transfers between devices, both_sides(): return lax.ppermute(pay, axis, ring(axis, 1))  6.4 us
    ppermute x2, waiting for transfers between devices, start(): return (sums, lax.ppermute(sums, 'gx', ring('gx', 2)))  6.16 us
    ppermute x2, starting transfers between devices, x_sides(): lax.ppermute(lo, 'gx', ring('gx', -1))  5.21 us
    ppermute x3, starting transfers between devices, both_sides(): return lax.ppermute(pay, axis, ring(axis, 1))  5.02 us
    unnamed x13, local copies, waits for them, and re-layouts  4.96 us
    ppermute x3, waiting for transfers between devices, detector(): own = [plane] + [lax.ppermute(plane, 'gx', ring('gx', s)) for s in shifts]  4.16 us
    ppermute x3, starting transfers between devices, detector(): own = [plane] + [lax.ppermute(plane, 'gx', ring('gx', s)) for s in shifts]  3.88 us
  transfers between devices with their start and end apart: 18, of which 10 were waited for; matrix products, arithmetic and copies ran while one was open for 5% of the time, Pallas kernels for 4%

profile of v5, /device:TPU:0, one launch (start us, length us, event | category | flops | bytes accessed | tf_op | source)
XLA Modules:
  0.0 63.8 jit_solution(2152856812456148562)
XLA Ops:
  0.6 1.6 %shard_map.120 = (f32[4,240,128]{2,1,0:T(8,128)S(1)}, f32[4,240,128]{2,1,0:T(8,128)S(1)}, s16[736,128]{1,0:T(8,128)(2,1)S(1)}, s16[736,128]{1,0:T(8,128)(2,1)S(1)}, f32[8,128]{1,0:T(8,128)S(1)}) custom-call(f32[4,240,128]{2,1,0:T(8,128)} %c_hbm.1, f32[4,240,128]{2,1,0:T(8,128)} %d_hbm.1, s32[4,240,128]{2,1,0:T(8,128)} %l_hbm.3), custom_call_target="tpu_custom_call" | custom-call | tf_op jit(solution)/shard_map/pallas_call | solution.py:61
  2.3 3.1 %collective-permute-start = (s16[736,128]{1,0:T(8,128)(2,1)S(1)}, s16[736,128]{1,0:T(8,128)(2,1)S(1)}, u32[]{:S(2)}, u32[]{:S(2)}) collective-permute-start(s16[736,128]{1,0:T(8,128)(2,1)S(1)} %get-tuple-element.27), channel_id=1, source_target_pairs={{0,4},{4,8},{8,12},{12,0},{1,5},{5,9},{9,13},{13,1},{2,6},{6,10},{... | collective-permute-start | bytes 565256 | tf_op jit(solution)/shard_map/ppermute | solution.py:453
  5.3 2.1 %collective-permute-start.1 = (s16[736,128]{1,0:T(8,128)(2,1)S(1)}, s16[736,128]{1,0:T(8,128)(2,1)S(1)}, u32[]{:S(2)}, u32[]{:S(2)}) collective-permute-start(s16[736,128]{1,0:T(8,128)(2,1)S(1)} %get-tuple-element.28), channel_id=1, source_target_pairs={{0,12},{4,0},{8,4},{12,8},{1,13},{5,1},{9,5},{13,9},{2,14},{6,2},{... | collective-permute-start | bytes 565256 | tf_op jit(solution)/shard_map/ppermute | solution.py:453
  7.4 0.9 %collective-permute-start.2 = (f32[8,128]{1,0:T(8,128)S(1)}, f32[8,128]{1,0:T(8,128)S(1)}, u32[]{:S(2)}, u32[]{:S(2)}) collective-permute-start(f32[8,128]{1,0:T(8,128)S(1)} %get-tuple-element.29.refs_4_), channel_id=1, source_target_pairs={{0,8},{4,12},{8,0},{12,4},{1,9},{5,13},{9,1},{13,5},{2,10},{6,14},... | collective-permute-start | bytes 12296 | tf_op jit(solution)/shard_map/ppermute | solution.py:471
  8.4 0.8 %copy.16 = bf16[27,4,16]{2,1,0:T(4,128)(2,1)S(1)} copy(bf16[27,4,16]{0,1,2:T(4,128)(2,1)} %bitcast.22) | data formatting | bytes 6912 | tf_op jit(solution)/shard_map/transpose | solution.py:599
  9.2 1.0 %copy.17 = bf16[27,16,16]{2,1,0:T(8,128)(2,1)S(1)} copy(bf16[27,16,16]{0,1,2:T(8,128)(2,1)} %bitcast.19) | data formatting | bytes 27648 | tf_op jit(solution)/shard_map/transpose | solution.py:600
  10.2 0.8 %copy.18 = bf16[27,1,16]{2,0,1:T(8,128)(2,1)S(1)} copy(bf16[27,1,16]{0,2,1:T(8,128)(2,1)} %param.16) | data formatting | bytes 1728 | tf_op args[7]
  11.0 0.1 copy.19
  11.2 0.0 copy-start.4
  11.2 0.6 %copy-done.4 = f32[16]{0:T(128)S(1)} copy-done((f32[16]{0:T(128)S(1)}, f32[16]{0:T(128)}, u32[]{:S(2)}) %copy-start.4) | copy-done | bytes 88
  11.9 0.7 %copy-done.5 = f32[16]{0:T(128)S(1)} copy-done((f32[16]{0:T(128)S(1)}, f32[16]{0:T(128)}, u32[]{:S(2)}) %copy-start.5) | copy-done | bytes 88
  12.5 2.8 %shard_map.121 = (bf16[3,768,640]{2,1,0:T(8,128)(2,1)}, bf16[3,768,128]{2,1,0:T(8,128)(2,1)}, bf16[3,640,128]{2,1,0:T(8,128)(2,1)}, f32[8,640]{1,0:T(8,128)}, f32[8,128]{1,0:T(8,128)S(1)}) custom-call(bf16[432,16]{1,0:T(8,128)(2,1)S(1)} %bitcast.15, bf16[432,16]{1,0:T(8,128)(2,1)S(1)} %bitcast.14, bf16[144,3]{1,0:T(8,128)(2,1)S(1)} %bitcast.16, ...), custom_call_target="tpu_custom_call" | custom-call | tf_op jit(solution)/shard_map/pallas_call | solution.py:603
  15.4 0.9 %collective-permute-done.2.refs_5_ = f32[8,128]{1,0:T(8,128)S(1)} collective-permute-done((f32[8,128]{1,0:T(8,128)S(1)}, f32[8,128]{1,0:T(8,128)S(1)}, u32[]{:S(2)}, u32[]{:S(2)}) %collective-permute-start.2) | collective-permute-done | bytes 4128 | tf_op jit(solution)/shard_map/ppermute | solution.py:471
  16.3 0.0 collective-permute-done.refs_2_.lo_ref
  16.3 0.0 collective-permute-done.1.refs_3_.hi_ref
  16.3 1.6 %collective-permute-start.3 = (f32[2,24,128]{2,1,0:T(8,128)S(1)}, f32[2,24,128]{2,1,0:T(8,128)S(1)}, u32[]{:S(2)}, u32[]{:S(2)}) collective-permute-start(f32[2,24,128]{2,1,0:T(8,128)S(1)} %shard_map.122.refs_5_.yp_ref), channel_id=1, source_target_pairs={{0,2},{2,0},{1,3},{3,1},{4,6},{6,4},{5,7},{7,5},{8,10},{10,8},{9,1... | collective-permute-start | bytes 73736 | tf_op jit(solution)/shard_map/ppermute | solution.py:435
  17.8 2.3 %collective-permute-done.3.refs_4_.yr_ref = f32[2,24,128]{2,1,0:T(8,128)S(1)} collective-permute-done((f32[2,24,128]{2,1,0:T(8,128)S(1)}, f32[2,24,128]{2,1,0:T(8,128)S(1)}, u32[]{:S(2)}, u32[]{:S(2)}) %collective-permute-start.3) | collective-permute-done | bytes 24608 | tf_op jit(solution)/shard_map/ppermute | solution.py:435
  20.2 0.3 shard_map.123
  20.5 0.1 collective-permute-start.4
  20.6 1.5 %collective-permute-done.4.zr_ref = f32[2,272,128]{2,1,0:T(8,128)S(1)} collective-permute-done((f32[2,272,128]{2,1,0:T(8,128)S(1)}, f32[2,272,128]{2,1,0:T(8,128)S(1)}, u32[]{:S(2)}, u32[]{:S(2)}) %collective-permute-start.4) | collective-permute-done | bytes 278560 | tf_op jit(solution)/shard_map/ppermute | solution.py:441
  22.2 2.2 %shard_map.124 = (f32[4,240,128]{2,1,0:T(8,128)S(1)}, f32[6,272,128]{2,1,0:T(8,128)S(1)}, f32[240,128]{1,0:T(8,128)S(1)}, s16[496,128]{1,0:T(8,128)(2,1)S(1)}, s...) custom-call(f32[4,240,128]{2,1,0:T(8,128)S(1)} %get-tuple-element.25.refs_0_.f_ref, ...), custom_call_target="tpu_custom_call" | custom-call | tf_op jit(solution)/shard_map/pallas_call | solution.py:61
  24.4 0.8 %collective-permute-start.5 = (s16[496,128]{1,0:T(8,128)(2,1)S(1)}, s16[496,128]{1,0:T(8,128)(2,1)S(1)}, u32[]{:S(2)}, u32[]{:S(2)}) collective-permute-start(s16[496,128]{1,0:T(8,128)(2,1)S(1)} %get-tuple-element.34), channel_id=1, source_target_pairs={{0,4},{4,8},{8,12},{12,0},{1,5},{5,9},{9,13},{13,1},{2,6},{6,10},{... | collective-permute-start | bytes 380936 | tf_op jit(solution)/shard_map/ppermute | solution.py:453
  25.1 3.1 %collective-permute-start.6 = (s16[496,128]{1,0:T(8,128)(2,1)S(1)}, s16[496,128]{1,0:T(8,128)(2,1)S(1)}, u32[]{:S(2)}, u32[]{:S(2)}) collective-permute-start(s16[496,128]{1,0:T(8,128)(2,1)S(1)} %get-tuple-element.35), channel_id=1, source_target_pairs={{0,12},{4,0},{8,4},{12,8},{1,13},{5,1},{9,5},{13,9},{2,14},{6,2},{... | collective-permute-start | bytes 380936 | tf_op jit(solution)/shard_map/ppermute | solution.py:453
  28.2 5.2 %collective-permute-done.7.refs_4_ = f32[8,128]{1,0:T(8,128)S(1)} collective-permute-done((f32[8,128]{1,0:T(8,128)S(1)}, f32[8,128]{1,0:T(8,128)S(1)}, u32[]{:S(2)}, u32[]{:S(2)}) %collective-permute-start.7) | collective-permute-done | bytes 4128 | tf_op jit(solution)/shard_map/ppermute | solution.py:471
  33.5 0.0 collective-permute-done.5.refs_1_.lo_ref
  33.5 0.0 collective-permute-done.6.refs_2_.hi_ref
  33.5 1.7 %collective-permute-start.8 = (f32[2,24,128]{2,1,0:T(8,128)S(1)}, f32[2,24,128]{2,1,0:T(8,128)S(1)}, u32[]{:S(2)}, u32[]{:S(2)}) collective-permute-start(f32[2,24,128]{2,1,0:T(8,128)S(1)} %shard_map.125.refs_4_.yp_ref), channel_id=1, source_target_pairs={{0,2},{2,0},{1,3},{3,1},{4,6},{6,4},{5,7},{7,5},{8,10},{10,8},{9,1... | collective-permute-start | bytes 73736 | tf_op jit(solution)/shard_map/ppermute | solution.py:435
  35.2 2.2 %collective-permute-done.8.refs_3_.yr_ref = f32[2,24,128]{2,1,0:T(8,128)S(1)} collective-permute-done((f32[2,24,128]{2,1,0:T(8,128)S(1)}, f32[2,24,128]{2,1,0:T(8,128)S(1)}, u32[]{:S(2)}, u32[]{:S(2)}) %collective-permute-start.8) | collective-permute-done | bytes 24608 | tf_op jit(solution)/shard_map/ppermute | solution.py:435
  37.4 0.2 shard_map.126
  37.6 0.1 collective-permute-start.9
  37.7 1.5 %collective-permute-done.9.zr_ref = f32[2,272,128]{2,1,0:T(8,128)S(1)} collective-permute-done((f32[2,272,128]{2,1,0:T(8,128)S(1)}, f32[2,272,128]{2,1,0:T(8,128)S(1)}, u32[]{:S(2)}, u32[]{:S(2)}) %collective-permute-start.9) | collective-permute-done | bytes 278560 | tf_op jit(solution)/shard_map/ppermute | solution.py:441
  39.2 3.3 %shard_map.127 = (f32[4,240,128]{2,1,0:T(8,128)}, f32[4,240,128]{2,1,0:T(8,128)}, f32[4,240,128]{2,1,0:T(8,128)}, bf16[60,128]{1,0:T(8,128)(2,1)S(1)}, bf16[2,16,128]{2,1,0:T(8,128)(2,1)S(1)}) custom-call(f32[4,240,128]{2,1,0:T(8,128)S(1)} %get-tuple-element.31.refs_0_.f_ref, f32[6,272,128]{2,1,0:T(8,128)S(1)} %get-tuple-element.32.a2_ref, ...), custom_call_target="tpu_custom_call" | custom-call | tf_op jit(solution)/shard_map/pallas_call | solution.py:61
  42.5 1.7 %collective-permute-start.10 = (bf16[2,16,128]{2,1,0:T(8,128)(2,1)S(1)}, bf16[2,16,128]{2,1,0:T(8,128)(2,1)S(1)}, u32[]{:S(2)}, u32[]{:S(2)}) collective-permute-start(bf16[2,16,128]{2,1,0:T(8,128)(2,1)S(1)} %get-tuple-element.41), channel_id=1, source_target_pairs={{0,2},{2,0},{1,3},{3,1},{4,6},{6,4},{5,7},{7,5},{8,10},{10,8},{9,1... | collective-permute-start | bytes 24584 | tf_op jit(solution)/shard_map/ppermute | solution.py:435
  44.3 0.1 pad_add_fusion.ids_ref.refs_0_
  44.4 1.9 %collective-permute-done.10.yr_ref = bf16[2,16,128]{2,1,0:T(8,128)(2,1)S(1)} collective-permute-done((bf16[2,16,128]{2,1,0:T(8,128)(2,1)S(1)}, bf16[2,16,128]{2,1,0:T(8,128)(2,1)S(1)}, u32[]{:S(2)}, u32[]{:S(2)}) %collective-permute-start.10) | collective-permute-done | bytes 8224 | tf_op jit(solution)/shard_map/ppermute | solution.py:435
  46.3 0.6 shard_map.128.refs_2_
  46.8 1.6 %collective-permute-start.11 = (bf16[80,128]{1,0:T(8,128)(2,1)S(1)}, bf16[80,128]{1,0:T(8,128)(2,1)S(1)}, u32[]{:S(2)}, u32[]{:S(2)}) collective-permute-start(bf16[80,128]{1,0:T(8,128)(2,1)S(1)} %shard_map.128.refs_2_), channel_id=1, source_target_pairs={{0,4},{4,8},{8,12},{12,0},{1,5},{5,9},{9,13},{13,1},{2,6},{6,10},{... | collective-permute-start | bytes 61448 | tf_op jit(solution)/shard_map/ppermute | solution.py:723
  48.5 2.2 %collective-permute-start.12 = (bf16[80,128]{1,0:T(8,128)(2,1)S(1)}, bf16[80,128]{1,0:T(8,128)(2,1)S(1)}, u32[]{:S(2)}, u32[]{:S(2)}) collective-permute-start(bf16[80,128]{1,0:T(8,128)(2,1)S(1)} %shard_map.128.refs_2_), channel_id=1, source_target_pairs={{0,12},{4,0},{8,4},{12,8},{1,13},{5,1},{9,5},{13,9},{2,14},{6,2},{... | collective-permute-start | bytes 61448 | tf_op jit(solution)/shard_map/ppermute | solution.py:723
  50.7 0.0 collective-permute-start.14
  50.7 1.8 %collective-permute-done.11.refs_3_ = bf16[80,128]{1,0:T(8,128)(2,1)S(1)} collective-permute-done((bf16[80,128]{1,0:T(8,128)(2,1)S(1)}, bf16[80,128]{1,0:T(8,128)(2,1)S(1)}, u32[]{:S(2)}, u32[]{:S(2)}) %collective-permute-start.11) | collective-permute-done | bytes 20512 | tf_op jit(solution)/shard_map/ppermute | solution.py:723
  52.5 0.5 collective-permute-start.16
  53.0 2.4 %collective-permute-done.13.refs_5_ = bf16[80,128]{1,0:T(8,128)(2,1)S(1)} collective-permute-done((bf16[80,128]{1,0:T(8,128)(2,1)S(1)}, bf16[80,128]{1,0:T(8,128)(2,1)S(1)}, u32[]{:S(2)}, u32[]{:S(2)}) %collective-permute-start.13) | collective-permute-done | bytes 20512 | tf_op jit(solution)/shard_map/ppermute | solution.py:723
  56.0 0.0 collective-permute-done.14.refs_6_
  56.0 0.0 collective-permute-done.15.refs_7_
  56.1 0.5 collective-permute-done.17.refs_9_
  56.6 1.8 %copy-done = bf16[3,768,640]{2,1,0:T(8,128)(2,1)S(1)} copy-done((bf16[3,768,640]{2,1,0:T(8,128)(2,1)S(1)}, bf16[3,768,640]{2,1,0:T(8,128)(2,1)}, u32[]{:S(2)}) %copy-start) | copy-done | bytes 2949144
  58.4 1.0 %copy-done.2 = bf16[3,640,128]{2,1,0:T(8,128)(2,1)S(1)} copy-done((bf16[3,640,128]{2,1,0:T(8,128)(2,1)S(1)}, bf16[3,640,128]{2,1,0:T(8,128)(2,1)}, u32[]{:S(2)}) %copy-start.2) | copy-done | bytes 491544
  59.4 4.3 %shard_map.129 = f32[1,32,60]{2,1,0:T(8,128)} custom-call(s32[3]{0:T(128)S(1)} %pad_add_fusion.ids_ref.refs_0_, f32[1]{0:T(128)S(6)} %copy.20.refs_1_, bf16[80,128]{1,0:T(8,128)(2,1)S(1)} %shard_map.128.refs_2_, bf16[80,128]{1,0:T(8,128)(2,1)S(1)} %collective-permute-done.11.refs_3_, bf16[80,128]{1,0:T(8,128)(2,1)S(1)} %collective-permute-done.12.refs_4_, ...), custom_call_target="tpu_custom_call" | custom-call | tf_op jit(solution)/shard_map/pallas_call | solution.py:61
  (17 shorter events, 0.1 us)
Async XLA Ops:
  2.3 14.0 %collective-permute-start = (s16[736,128]{1,0:T(8,128)(2,1)S(1)}, s16[736,128]{1,0:T(8,128)(2,1)S(1)}, u32[]{:S(2)}, u32[]{:S(2)}) collective-permute-start(s16[736,128]{1,0:T(8,128)(2,1)S(1)} %get-tuple-element.27), channel_id=1, source_target_pairs={{0,4},{4,8},{8,12},{12,0},{1,5},{5,9},{9,13},{13,1},{2,6},{6,10},{... | collective-permute-start | bytes 565256 | tf_op jit(solution)/shard_map/ppermute | solution.py:453
  5.3 10.9 %collective-permute-start.1 = (s16[736,128]{1,0:T(8,128)(2,1)S(1)}, s16[736,128]{1,0:T(8,128)(2,1)S(1)}, u32[]{:S(2)}, u32[]{:S(2)}) collective-permute-start(s16[736,128]{1,0:T(8,128)(2,1)S(1)} %get-tuple-element.28), channel_id=1, source_target_pairs={{0,12},{4,0},{8,4},{12,8},{1,13},{5,1},{9,5},{13,9},{2,14},{6,2},{... | collective-permute-start | bytes 565256 | tf_op jit(solution)/shard_map/ppermute | solution.py:453
  7.4 8.8 %collective-permute-start.2 = (f32[8,128]{1,0:T(8,128)S(1)}, f32[8,128]{1,0:T(8,128)S(1)}, u32[]{:S(2)}, u32[]{:S(2)}) collective-permute-start(f32[8,128]{1,0:T(8,128)S(1)} %get-tuple-element.29.refs_4_), channel_id=1, source_target_pairs={{0,8},{4,12},{8,0},{12,4},{1,9},{5,13},{9,1},{13,5},{2,10},{6,14},... | collective-permute-start | bytes 12296 | tf_op jit(solution)/shard_map/ppermute | solution.py:471
  11.2 0.7 %copy-start.4 = (f32[16]{0:T(128)S(1)}, f32[16]{0:T(128)}, u32[]{:S(2)}) copy-start(f32[16]{0:T(128)} %param.13) | copy-start | bytes 196
  11.9 0.7 %copy-start.5 = (f32[16]{0:T(128)S(1)}, f32[16]{0:T(128)}, u32[]{:S(2)}) copy-start(f32[16]{0:T(128)} %param.15) | copy-start | bytes 196
  16.3 3.9 %collective-permute-start.3 = (f32[2,24,128]{2,1,0:T(8,128)S(1)}, f32[2,24,128]{2,1,0:T(8,128)S(1)}, u32[]{:S(2)}, u32[]{:S(2)}) collective-permute-start(f32[2,24,128]{2,1,0:T(8,128)S(1)} %shard_map.122.refs_5_.yp_ref), channel_id=1, source_target_pairs={{0,2},{2,0},{1,3},{3,1},{4,6},{6,4},{5,7},{7,5},{8,10},{10,8},{9,1... | collective-permute-start | bytes 73736 | tf_op jit(solution)/shard_map/ppermute | solution.py:435
  20.5 36.1 %copy-start.1 = (bf16[3,768,128]{2,1,0:T(8,128)(2,1)S(1)}, bf16[3,768,128]{2,1,0:T(8,128)(2,1)}, u32[]{:S(2)}) copy-start(bf16[3,768,128]{2,1,0:T(8,128)(2,1)} %get-tuple-element.43.refs_11_) | copy-start | bytes 1769476
  20.5 36.1 %copy-start.3 = (f32[8,640]{1,0:T(8,128)S(1)}, f32[8,640]{1,0:T(8,128)}, u32[]{:S(2)}) copy-start(f32[8,640]{1,0:T(8,128)} %get-tuple-element.45.refs_13_) | copy-start | bytes 61444
  20.5 1.6 %collective-permute-start.4 = (f32[2,272,128]{2,1,0:T(8,128)S(1)}, f32[2,272,128]{2,1,0:T(8,128)S(1)}, u32[]{:S(2)}, u32[]{:S(2)}) collective-permute-start(f32[2,272,128]{2,1,0:T(8,128)S(1)} %shard_map.123), channel_id=1, source_target_pairs={{0,1},{1,0},{2,3},{3,2},{4,5},{5,4},{6,7},{7,6},{8,9},{9,8},{10,11... | collective-permute-start | bytes 835592 | tf_op jit(solution)/shard_map/ppermute | solution.py:441
  24.4 9.1 %collective-permute-start.5 = (s16[496,128]{1,0:T(8,128)(2,1)S(1)}, s16[496,128]{1,0:T(8,128)(2,1)S(1)}, u32[]{:S(2)}, u32[]{:S(2)}) collective-permute-start(s16[496,128]{1,0:T(8,128)(2,1)S(1)} %get-tuple-element.34), channel_id=1, source_target_pairs={{0,4},{4,8},{8,12},{12,0},{1,5},{5,9},{9,13},{13,1},{2,6},{6,10},{... | collective-permute-start | bytes 380936 | tf_op jit(solution)/shard_map/ppermute | solution.py:453
  25.1 8.4 %collective-permute-start.6 = (s16[496,128]{1,0:T(8,128)(2,1)S(1)}, s16[496,128]{1,0:T(8,128)(2,1)S(1)}, u32[]{:S(2)}, u32[]{:S(2)}) collective-permute-start(s16[496,128]{1,0:T(8,128)(2,1)S(1)} %get-tuple-element.35), channel_id=1, source_target_pairs={{0,12},{4,0},{8,4},{12,8},{1,13},{5,1},{9,5},{13,9},{2,14},{6,2},{... | collective-permute-start | bytes 380936 | tf_op jit(solution)/shard_map/ppermute | solution.py:453
  28.2 5.3 %collective-permute-start.7 = (f32[8,128]{1,0:T(8,128)S(1)}, f32[8,128]{1,0:T(8,128)S(1)}, u32[]{:S(2)}, u32[]{:S(2)}) collective-permute-start(f32[8,128]{1,0:T(8,128)S(1)} %get-tuple-element.36.refs_3_), channel_id=1, source_target_pairs={{0,8},{4,12},{8,0},{12,4},{1,9},{5,13},{9,1},{13,5},{2,10},{6,14},... | collective-permute-start | bytes 12296 | tf_op jit(solution)/shard_map/ppermute | solution.py:471
  33.5 3.9 %collective-permute-start.8 = (f32[2,24,128]{2,1,0:T(8,128)S(1)}, f32[2,24,128]{2,1,0:T(8,128)S(1)}, u32[]{:S(2)}, u32[]{:S(2)}) collective-permute-start(f32[2,24,128]{2,1,0:T(8,128)S(1)} %shard_map.125.refs_4_.yp_ref), channel_id=1, source_target_pairs={{0,2},{2,0},{1,3},{3,1},{4,6},{6,4},{5,7},{7,5},{8,10},{10,8},{9,1... | collective-permute-start | bytes 73736 | tf_op jit(solution)/shard_map/ppermute | solution.py:435
  37.6 1.6 %collective-permute-start.9 = (f32[2,272,128]{2,1,0:T(8,128)S(1)}, f32[2,272,128]{2,1,0:T(8,128)S(1)}, u32[]{:S(2)}, u32[]{:S(2)}) collective-permute-start(f32[2,272,128]{2,1,0:T(8,128)S(1)} %shard_map.126), channel_id=1, source_target_pairs={{0,1},{1,0},{2,3},{3,2},{4,5},{5,4},{6,7},{7,6},{8,9},{9,8},{10,11... | collective-permute-start | bytes 835592 | tf_op jit(solution)/shard_map/ppermute | solution.py:441
  42.5 3.7 %collective-permute-start.10 = (bf16[2,16,128]{2,1,0:T(8,128)(2,1)S(1)}, bf16[2,16,128]{2,1,0:T(8,128)(2,1)S(1)}, u32[]{:S(2)}, u32[]{:S(2)}) collective-permute-start(bf16[2,16,128]{2,1,0:T(8,128)(2,1)S(1)} %get-tuple-element.41), channel_id=1, source_target_pairs={{0,2},{2,0},{1,3},{3,1},{4,6},{6,4},{5,7},{7,5},{8,10},{10,8},{9,1... | collective-permute-start | bytes 24584 | tf_op jit(solution)/shard_map/ppermute | solution.py:435
  46.8 5.7 %collective-permute-start.11 = (bf16[80,128]{1,0:T(8,128)(2,1)S(1)}, bf16[80,128]{1,0:T(8,128)(2,1)S(1)}, u32[]{:S(2)}, u32[]{:S(2)}) collective-permute-start(bf16[80,128]{1,0:T(8,128)(2,1)S(1)} %shard_map.128.refs_2_), channel_id=1, source_target_pairs={{0,4},{4,8},{8,12},{12,0},{1,5},{5,9},{9,13},{13,1},{2,6},{6,10},{... | collective-permute-start | bytes 61448 | tf_op jit(solution)/shard_map/ppermute | solution.py:723
  48.5 4.0 %collective-permute-start.12 = (bf16[80,128]{1,0:T(8,128)(2,1)S(1)}, bf16[80,128]{1,0:T(8,128)(2,1)S(1)}, u32[]{:S(2)}, u32[]{:S(2)}) collective-permute-start(bf16[80,128]{1,0:T(8,128)(2,1)S(1)} %shard_map.128.refs_2_), channel_id=1, source_target_pairs={{0,12},{4,0},{8,4},{12,8},{1,13},{5,1},{9,5},{13,9},{2,14},{6,2},{... | collective-permute-start | bytes 61448 | tf_op jit(solution)/shard_map/ppermute | solution.py:723
  50.7 4.7 %collective-permute-start.13 = (bf16[80,128]{1,0:T(8,128)(2,1)S(1)}, bf16[80,128]{1,0:T(8,128)(2,1)S(1)}, u32[]{:S(2)}, u32[]{:S(2)}) collective-permute-start(bf16[80,128]{1,0:T(8,128)(2,1)S(1)} %shard_map.128.refs_2_), channel_id=1, source_target_pairs={{0,8},{4,12},{8,0},{12,4},{1,9},{5,13},{9,1},{13,5},{2,10},{6,14},... | collective-permute-start | bytes 61448 | tf_op jit(solution)/shard_map/ppermute | solution.py:723
  50.7 5.3 %collective-permute-start.14 = (bf16[80,128]{1,0:T(8,128)(2,1)S(1)}, bf16[80,128]{1,0:T(8,128)(2,1)S(1)}, u32[]{:S(2)}, u32[]{:S(2)}) collective-permute-start(bf16[80,128]{1,0:T(8,128)(2,1)S(1)} %shard_map.128.refs_2_), channel_id=1, source_target_pairs={{0,1},{1,0},{2,3},{3,2},{4,5},{5,4},{6,7},{7,6},{8,9},{9,8},{10,11... | collective-permute-start | bytes 61448 | tf_op jit(solution)/shard_map/ppermute | solution.py:441
  52.5 3.6 %collective-permute-start.15 = (bf16[80,128]{1,0:T(8,128)(2,1)S(1)}, bf16[80,128]{1,0:T(8,128)(2,1)S(1)}, u32[]{:S(2)}, u32[]{:S(2)}) collective-permute-start(bf16[80,128]{1,0:T(8,128)(2,1)S(1)} %collective-permute-done.11.refs_3_), channel_id=1, source_target_pairs={{0,1},{1,0},{2,3},{3,2},{4,5},{5,4},{6,7},{7,6},{8,9},{9,8},{10,11... | collective-permute-start | bytes 61448 | tf_op jit(solution)/shard_map/ppermute | solution.py:441
  52.5 3.6 %collective-permute-start.16 = (bf16[80,128]{1,0:T(8,128)(2,1)S(1)}, bf16[80,128]{1,0:T(8,128)(2,1)S(1)}, u32[]{:S(2)}, u32[]{:S(2)}) collective-permute-start(bf16[80,128]{1,0:T(8,128)(2,1)S(1)} %collective-permute-done.12.refs_4_), channel_id=1, source_target_pairs={{0,1},{1,0},{2,3},{3,2},{4,5},{5,4},{6,7},{7,6},{8,9},{9,8},{10,11... | collective-permute-start | bytes 61448 | tf_op jit(solution)/shard_map/ppermute | solution.py:441
  55.4 1.2 %collective-permute-start.17 = (bf16[80,128]{1,0:T(8,128)(2,1)S(1)}, bf16[80,128]{1,0:T(8,128)(2,1)S(1)}, u32[]{:S(2)}, u32[]{:S(2)}) collective-permute-start(bf16[80,128]{1,0:T(8,128)(2,1)S(1)} %collective-permute-done.13.refs_5_), channel_id=1, source_target_pairs={{0,1},{1,0},{2,3},{3,2},{4,5},{5,4},{6,7},{7,6},{8,9},{9,8},{10,11... | collective-permute-start | bytes 61448 | tf_op jit(solution)/shard_map/ppermute | solution.py:441
  56.6 1.8 %copy-start = (bf16[3,768,640]{2,1,0:T(8,128)(2,1)S(1)}, bf16[3,768,640]{2,1,0:T(8,128)(2,1)}, u32[]{:S(2)}) copy-start(bf16[3,768,640]{2,1,0:T(8,128)(2,1)} %get-tuple-element.42.refs_10_) | copy-start | bytes 8847364
  58.4 1.0 %copy-start.2 = (bf16[3,640,128]{2,1,0:T(8,128)(2,1)S(1)}, bf16[3,640,128]{2,1,0:T(8,128)(2,1)}, u32[]{:S(2)}) copy-start(bf16[3,640,128]{2,1,0:T(8,128)(2,1)} %get-tuple-element.44.refs_12_) | copy-start | bytes 1474564

commit v6 on v5

--- a/solution.py
+++ b/solution.py
@@ -484,10 +484,10 @@
         concentration, damage, labels,
         in_specs=[HBM] * 3,
         scratch=[pltpu.VMEM(block, F32), pltpu.VMEM(block, jnp.int32), pltpu.SemaphoreType.DMA((3, nx))])
-    *matrices, order = weight_matrices(w_first, b_first, w_second, b_second, w_third, nz, nz // 4)
+    weights = weight_rows(w_first, w_second, w_third)
     sums, far = start(sums)
     lo, hi = x_sides(lo, hi)
-    (ypay,) = call(edge_rows(A_CODE, ride_x, True), [((2, 24, nz), F32)], f, amp, lo, hi, sums, far, order)
+    (ypay,) = call(edge_rows(A_CODE, ride_x, True), [((2, 24, nz), F32)], f, amp, lo, hi, sums, far, *weights)
     yr = both_sides(ypay, "gy")
     (zpay,) = call(pack_z(A_CODE, ride_y, True), [(packed, F32)], f, amp, lo, hi, yr, ypay)
     zr = z_neighbour(zpay, "gz")
@@ -513,7 +513,7 @@
             pltpu.VMEM(block, F32), pltpu.VMEM(block, F32), pltpu.VMEM(block, F32),
             pltpu.SemaphoreType.DMA, pltpu.SemaphoreType.DMA((3, len(chunks(OFF, OFF + ny, 48))))])
     ids = jnp.stack([lax.axis_index(a) for a in ("gx", "gy", "gz")])
-    crack_score = detector(pooled, edge, ids, matrices, b_third, ny // 4, nz // 4)
+    crack_score = detector(pooled, edge, ids, weights + (b_first[None], b_second[None]), b_third, ny // 4, nz // 4)
     return (fraction, damage_field, flux_sum, crack_score)
 
 
@@ -547,8 +547,7 @@
 SHIFTS = tuple(k for k in range(-3, 10) if k % (16 // CIN) == 3)
 
 
-def weight_kernel(w1_ref, w2_ref, w3_ref, b1_ref, b2_ref, t1_hbm, t2_hbm, t3_hbm, bias_hbm, order_ref,
-                  t1_ref, t2_ref, t3_ref, bias_ref, sems):
+def weight_kernel(w1_ref, w2_ref, w3_ref, b1_ref, b2_ref, plane_ref, t1_ref, t2_ref, t3_ref, bias_ref):
     n1 = bias_ref.shape[1]
     k1 = t1_ref.shape[1] // 3
     pz = k1 // (2 * CIN)
@@ -585,29 +584,12 @@
     wide = one_hot(iota((CH, n1), 1) % CH == iota((CH, n1), 0)).astype(F32)
     for k, ref in ((0, b1_ref), (1, b2_ref)):
         bias_ref[k:k + 1, :] = jnp.dot(ref[...], wide, precision=lax.Precision.HIGHEST, preferred_element_type=F32)
-    order_ref[...] = jnp.zeros(order_ref.shape, F32)
-    copies = [pltpu.make_async_copy(src, dst, sems.at[k]) for k, (src, dst) in enumerate(
-        ((t1_ref, t1_hbm), (t2_ref, t2_hbm), (t3_ref, t3_hbm), (bias_ref, bias_hbm)))]
-    for c in copies:
-        c.start()
-    for c in copies:
-        c.wait()
-
-
-def weight_matrices(w_first, b_first, w_second, b_second, w_third, half, pz):
-    width = lanes_for((pz + 4) * CH)
-    rows1 = jnp.tile(jnp.swapaxes(w_first, 1, 2), (1, 16 // CIN, 1)).reshape(27 * 16, CH)
-    rows2 = jnp.swapaxes(w_second, 1, 2).reshape(27 * CH, CH)
-    rows3 = w_third.reshape(3, 3, 3, CH).transpose(0, 2, 3, 1).reshape(9 * CH, 3)
-    outs = [((3, 6 * half, width), BF16), ((3, 768, 128), BF16), ((3, width, 128), BF16), ((8, width), F32)]
-    return pl.pallas_call(
-        weight_kernel,
-        in_specs=[VMEM] * 5,
-        out_specs=[HBM] * 4 + [VMEM],
-        out_shape=[pltpu.HBM(*v) for v in outs] + [jax.ShapeDtypeStruct((8, 128), F32)],
-        scratch_shapes=[pltpu.VMEM(*v) for v in outs] + [pltpu.SemaphoreType.DMA((4,))],
-        compiler_params=pltpu.CompilerParams(vmem_limit_bytes=16 * 1024 * 1024),
-    )(rows1, rows2, rows3, b_first[None], b_second[None])
+
+
+def weight_rows(w_first, w_second, w_third):
+    return (jnp.tile(jnp.swapaxes(w_first, 1, 2), (1, 16 // CIN, 1)).reshape(27 * 16, CH),
+            jnp.swapaxes(w_second, 1, 2).reshape(27 * CH, CH),
+            w_third.reshape(3, 3, 3, CH).transpose(0, 2, 3, 1).reshape(9 * CH, 3))
 
 
 def gelu(x):
@@ -704,7 +686,7 @@
     return kernel
 
 
-def detector(pooled, edge, ids, matrices, b_third, py, pz):
+def detector(pooled, edge, ids, weights, b_third, py, pz):
     counts = tuple(lax.axis_size(a) for a in ("gx", "gy", "gz"))
     half = pooled.shape[1]
     assert half == 128 and pz * CIN == half and pz * 3 <= 128
@@ -721,6 +703,11 @@
         if s % counts[0] and s % counts[0] not in shifts:
             shifts.append(s % counts[0])
     own = [plane] + [lax.ppermute(plane, "gx", ring("gx", s)) for s in shifts]
+    matrices = call(
+        weight_kernel,
+        [((3, 6 * half, width), BF16), ((3, 768, 128), BF16), ((3, width, 128), BF16), ((8, width), F32)],
+        *weights, plane)
+    own[1], *matrices = lax.optimization_barrier((own[1], *matrices))
     other = [z_neighbour(v, "gz", False) for v in own]
     args = (ids, b_third, *own, *other, *matrices)
     (score,) = call(

time: 64.2 us -> 61 us (0.950)
  local copies, waits for them, and re-layouts: 7.03 us -> 2.86 us
  waiting for transfers between devices: 20.3 us -> 23.5 us
  Pallas kernels: 15.4 us -> 13.5 us
    unnamed x13 -> x5, local copies, waits for them, and re-layouts: 4.96 us -> 0.8 us
    ppermute x2, waiting for transfers between devices: 6.16 us -> 9.93 us  [start(): return (sums, lax.ppermute(sums, 'gx', ring('gx', 2)))]
    pallas_call x1 -> x0, Pallas kernels: 2.79 us -> none  [weight_matrices(): pl.pallas_call(weight_kernel, in_specs=[VMEM] * 5, out_specs=[HBM] * 4 +...]
    ppermute x3, waiting for transfers between devices: 4.16 us -> 3.22 us  [detector(): own = [plane] + [lax.ppermute(plane, 'gx', ring('gx', s)) for s in shifts]]
    pallas_call x9 -> x10, Pallas kernels: 12.6 us -> 13.5 us  [call(): pl.pallas_call(kernel, in_specs=in_specs or [VMEM] * len(args), out_specs...]
  transfers between devices with their start and end apart: 18 -> 18, of which waited for: 10 -> 10; matrix products, arithmetic and copies ran while one was open for 5% -> 5% of each run, Pallas kernels for 4% -> 1%
where the time goes in v6:
time: 61 us; the launch traced here: 60.6 us
  waiting for transfers between devices  23.5 us (39%)
  starting transfers between devices  19.3 us (32%)
  Pallas kernels  13.5 us (22%)
  local copies, waits for them, and re-layouts  2.86 us (5%)
  between operations  1.42 us (2%)
    pallas_call x10, Pallas kernels, call(): pl.pallas_call(kernel, in_specs=in_specs or [VMEM] * len(args), out_specs...  13.5 us
    ppermute x2, waiting for transfers between devices, start(): return (sums, lax.ppermute(sums, 'gx', ring('gx', 2)))  9.93 us
    ppermute x3, waiting for transfers between devices, both_sides(): return lax.ppermute(pay, axis, ring(axis, 1))  6.75 us
    ppermute x2, starting transfers between devices, x_sides(): lax.ppermute(lo, 'gx', ring('gx', -1))  5.32 us
    ppermute x3, starting transfers between devices, both_sides(): return lax.ppermute(pay, axis, ring(axis, 1))  4.67 us
    ppermute x3, starting transfers between devices, detector(): own = [plane] + [lax.ppermute(plane, 'gx', ring('gx', s)) for s in shifts]  4 us
    ppermute x2, starting transfers between devices, x_sides(): lax.ppermute(hi, 'gx', ring('gx', 1))  3.72 us
    ppermute x6, waiting for transfers between devices, z_neighbour(): return lax.ppermute(pay, axis, ring(axis, 1))  3.6 us
  transfers between devices with their start and end apart: 18, of which 10 were waited for; matrix products, arithmetic and copies ran while one was open for 5% of the time, Pallas kernels for 1%

profile of v6, /device:TPU:0, one launch (start us, length us, event | category | flops | bytes accessed | tf_op | source)
XLA Modules:
  0.0 60.6 jit_solution(15496496811300934247)
XLA Ops:
  0.6 1.6 %shard_map.120 = (f32[4,240,128]{2,1,0:T(8,128)S(1)}, f32[4,240,128]{2,1,0:T(8,128)S(1)}, s16[736,128]{1,0:T(8,128)(2,1)S(1)}, s16[736,128]{1,0:T(8,128)(2,1)S(1)}, f32[8,128]{1,0:T(8,128)S(1)}) custom-call(f32[4,240,128]{2,1,0:T(8,128)} %c_hbm.1, f32[4,240,128]{2,1,0:T(8,128)} %d_hbm.1, s32[4,240,128]{2,1,0:T(8,128)} %l_hbm.3), custom_call_target="tpu_custom_call" | custom-call | tf_op jit(solution)/shard_map/pallas_call | solution.py:61
  2.3 3.1 %collective-permute-start = (s16[736,128]{1,0:T(8,128)(2,1)S(1)}, s16[736,128]{1,0:T(8,128)(2,1)S(1)}, u32[]{:S(2)}, u32[]{:S(2)}) collective-permute-start(s16[736,128]{1,0:T(8,128)(2,1)S(1)} %get-tuple-element.31), channel_id=1, source_target_pairs={{0,4},{4,8},{8,12},{12,0},{1,5},{5,9},{9,13},{13,1},{2,6},{6,10},{... | collective-permute-start | bytes 565256 | tf_op jit(solution)/shard_map/ppermute | solution.py:453
  5.3 2.1 %collective-permute-start.1 = (s16[736,128]{1,0:T(8,128)(2,1)S(1)}, s16[736,128]{1,0:T(8,128)(2,1)S(1)}, u32[]{:S(2)}, u32[]{:S(2)}) collective-permute-start(s16[736,128]{1,0:T(8,128)(2,1)S(1)} %get-tuple-element.32), channel_id=1, source_target_pairs={{0,12},{4,0},{8,4},{12,8},{1,13},{5,1},{9,5},{13,9},{2,14},{6,2},{... | collective-permute-start | bytes 565256 | tf_op jit(solution)/shard_map/ppermute | solution.py:453
  7.4 0.9 %collective-permute-start.2 = (f32[8,128]{1,0:T(8,128)S(1)}, f32[8,128]{1,0:T(8,128)S(1)}, u32[]{:S(2)}, u32[]{:S(2)}) collective-permute-start(f32[8,128]{1,0:T(8,128)S(1)} %get-tuple-element.33.refs_4_), channel_id=1, source_target_pairs={{0,8},{4,12},{8,0},{12,4},{1,9},{5,13},{9,1},{13,5},{2,10},{6,14},... | collective-permute-start | bytes 12296 | tf_op jit(solution)/shard_map/ppermute | solution.py:471
  8.4 0.8 %copy.16 = bf16[27,4,16]{2,1,0:T(4,128)(2,1)S(1)} copy(bf16[27,4,16]{0,1,2:T(4,128)(2,1)} %bitcast.25) | data formatting | bytes 6912 | tf_op jit(solution)/shard_map/transpose | solution.py:590
  9.2 1.0 %copy.17 = bf16[27,16,16]{2,1,0:T(8,128)(2,1)S(1)} copy(bf16[27,16,16]{0,1,2:T(8,128)(2,1)} %bitcast.22) | data formatting | bytes 27648 | tf_op jit(solution)/shard_map/transpose | solution.py:591
  10.2 0.8 %copy.18 = bf16[27,1,16]{2,0,1:T(8,128)(2,1)S(1)} copy(bf16[27,1,16]{0,2,1:T(8,128)(2,1)} %param.16) | data formatting | bytes 1728 | tf_op args[7]
  11.0 0.1 copy.19
  11.2 5.1 %collective-permute-done.2.refs_5_ = f32[8,128]{1,0:T(8,128)S(1)} collective-permute-done((f32[8,128]{1,0:T(8,128)S(1)}, f32[8,128]{1,0:T(8,128)S(1)}, u32[]{:S(2)}, u32[]{:S(2)}) %collective-permute-start.2) | collective-permute-done | bytes 4128 | tf_op jit(solution)/shard_map/ppermute | solution.py:471
  16.3 0.0 collective-permute-done.refs_2_.lo_ref
  16.3 0.0 collective-permute-done.1.refs_3_.hi_ref
  16.3 1.6 %collective-permute-start.3 = (f32[2,24,128]{2,1,0:T(8,128)S(1)}, f32[2,24,128]{2,1,0:T(8,128)S(1)}, u32[]{:S(2)}, u32[]{:S(2)}) collective-permute-start(f32[2,24,128]{2,1,0:T(8,128)S(1)} %shard_map.121.refs_5_.yp_ref), channel_id=1, source_target_pairs={{0,2},{2,0},{1,3},{3,1},{4,6},{6,4},{5,7},{7,5},{8,10},{10,8},{9,1... | collective-permute-start | bytes 73736 | tf_op jit(solution)/shard_map/ppermute | solution.py:435
  17.9 2.3 %collective-permute-done.3.refs_4_.yr_ref = f32[2,24,128]{2,1,0:T(8,128)S(1)} collective-permute-done((f32[2,24,128]{2,1,0:T(8,128)S(1)}, f32[2,24,128]{2,1,0:T(8,128)S(1)}, u32[]{:S(2)}, u32[]{:S(2)}) %collective-permute-start.3) | collective-permute-done | bytes 24608 | tf_op jit(solution)/shard_map/ppermute | solution.py:435
  20.2 0.3 shard_map.122
  20.6 0.0 copy-start
  20.6 0.0 copy-start.1
  20.6 0.1 collective-permute-start.4
  20.7 1.5 %collective-permute-done.4.zr_ref = f32[2,272,128]{2,1,0:T(8,128)S(1)} collective-permute-done((f32[2,272,128]{2,1,0:T(8,128)S(1)}, f32[2,272,128]{2,1,0:T(8,128)S(1)}, u32[]{:S(2)}, u32[]{:S(2)}) %collective-permute-start.4) | collective-permute-done | bytes 278560 | tf_op jit(solution)/shard_map/ppermute | solution.py:441
  22.2 2.2 %shard_map.123 = (f32[4,240,128]{2,1,0:T(8,128)S(1)}, f32[6,272,128]{2,1,0:T(8,128)S(1)}, f32[240,128]{1,0:T(8,128)S(1)}, s16[496,128]{1,0:T(8,128)(2,1)S(1)}, s...) custom-call(f32[4,240,128]{2,1,0:T(8,128)S(1)} %get-tuple-element.29.refs_0_.f_ref, ...), custom_call_target="tpu_custom_call" | custom-call | tf_op jit(solution)/shard_map/pallas_call | solution.py:61
  24.4 0.6 %collective-permute-start.5 = (s16[496,128]{1,0:T(8,128)(2,1)S(1)}, s16[496,128]{1,0:T(8,128)(2,1)S(1)}, u32[]{:S(2)}, u32[]{:S(2)}) collective-permute-start(s16[496,128]{1,0:T(8,128)(2,1)S(1)} %get-tuple-element.37), channel_id=1, source_target_pairs={{0,4},{4,8},{8,12},{12,0},{1,5},{5,9},{9,13},{13,1},{2,6},{6,10},{... | collective-permute-start | bytes 380936 | tf_op jit(solution)/shard_map/ppermute | solution.py:453
  25.1 3.2 %collective-permute-start.6 = (s16[496,128]{1,0:T(8,128)(2,1)S(1)}, s16[496,128]{1,0:T(8,128)(2,1)S(1)}, u32[]{:S(2)}, u32[]{:S(2)}) collective-permute-start(s16[496,128]{1,0:T(8,128)(2,1)S(1)} %get-tuple-element.38), channel_id=1, source_target_pairs={{0,12},{4,0},{8,4},{12,8},{1,13},{5,1},{9,5},{13,9},{2,14},{6,2},{... | collective-permute-start | bytes 380936 | tf_op jit(solution)/shard_map/ppermute | solution.py:453
  28.3 0.0 collective-permute-start.7
  28.3 4.9 %collective-permute-done.7.refs_4_ = f32[8,128]{1,0:T(8,128)S(1)} collective-permute-done((f32[8,128]{1,0:T(8,128)S(1)}, f32[8,128]{1,0:T(8,128)S(1)}, u32[]{:S(2)}, u32[]{:S(2)}) %collective-permute-start.7) | collective-permute-done | bytes 4128 | tf_op jit(solution)/shard_map/ppermute | solution.py:471
  33.2 0.0 collective-permute-done.5.refs_1_.lo_ref
  33.2 1.6 %collective-permute-start.8 = (f32[2,24,128]{2,1,0:T(8,128)S(1)}, f32[2,24,128]{2,1,0:T(8,128)S(1)}, u32[]{:S(2)}, u32[]{:S(2)}) collective-permute-start(f32[2,24,128]{2,1,0:T(8,128)S(1)} %shard_map.124.refs_4_.yp_ref), channel_id=1, source_target_pairs={{0,2},{2,0},{1,3},{3,1},{4,6},{6,4},{5,7},{7,5},{8,10},{10,8},{9,1... | collective-permute-start | bytes 73736 | tf_op jit(solution)/shard_map/ppermute | solution.py:435
  34.8 2.3 %collective-permute-done.8.refs_3_.yr_ref = f32[2,24,128]{2,1,0:T(8,128)S(1)} collective-permute-done((f32[2,24,128]{2,1,0:T(8,128)S(1)}, f32[2,24,128]{2,1,0:T(8,128)S(1)}, u32[]{:S(2)}, u32[]{:S(2)}) %collective-permute-start.8) | collective-permute-done | bytes 24608 | tf_op jit(solution)/shard_map/ppermute | solution.py:435
  37.1 0.2 shard_map.125
  37.3 0.1 collective-permute-start.9
  37.4 1.5 %collective-permute-done.9.zr_ref = f32[2,272,128]{2,1,0:T(8,128)S(1)} collective-permute-done((f32[2,272,128]{2,1,0:T(8,128)S(1)}, f32[2,272,128]{2,1,0:T(8,128)S(1)}, u32[]{:S(2)}, u32[]{:S(2)}) %collective-permute-start.9) | collective-permute-done | bytes 278560 | tf_op jit(solution)/shard_map/ppermute | solution.py:441
  38.9 3.3 %shard_map.126 = (f32[4,240,128]{2,1,0:T(8,128)}, f32[4,240,128]{2,1,0:T(8,128)}, f32[4,240,128]{2,1,0:T(8,128)}, bf16[60,128]{1,0:T(8,128)(2,1)S(1)}, bf16[2,16,128]{2,1,0:T(8,128)(2,1)S(1)}) custom-call(f32[4,240,128]{2,1,0:T(8,128)S(1)} %get-tuple-element.34.refs_0_.f_ref, f32[6,272,128]{2,1,0:T(8,128)S(1)} %get-tuple-element.35.a2_ref, ...), custom_call_target="tpu_custom_call" | custom-call | tf_op jit(solution)/shard_map/pallas_call | solution.py:61
  42.2 1.6 %collective-permute-start.10 = (bf16[2,16,128]{2,1,0:T(8,128)(2,1)S(1)}, bf16[2,16,128]{2,1,0:T(8,128)(2,1)S(1)}, u32[]{:S(2)}, u32[]{:S(2)}) collective-permute-start(bf16[2,16,128]{2,1,0:T(8,128)(2,1)S(1)} %get-tuple-element.44), channel_id=1, source_target_pairs={{0,2},{2,0},{1,3},{3,1},{4,6},{6,4},{5,7},{7,5},{8,10},{10,8},{9,1... | collective-permute-start | bytes 24584 | tf_op jit(solution)/shard_map/ppermute | solution.py:435
  43.8 0.1 pad_add_fusion.ids_ref.refs_0_
  43.9 2.1 %collective-permute-done.10.yr_ref = bf16[2,16,128]{2,1,0:T(8,128)(2,1)S(1)} collective-permute-done((bf16[2,16,128]{2,1,0:T(8,128)(2,1)S(1)}, bf16[2,16,128]{2,1,0:T(8,128)(2,1)S(1)}, u32[]{:S(2)}, u32[]{:S(2)}) %collective-permute-start.10) | collective-permute-done | bytes 8224 | tf_op jit(solution)/shard_map/ppermute | solution.py:435
  46.0 0.6 shard_map.127.plane_ref.refs_2_
  46.5 2.0 %collective-permute-start.11 = (bf16[80,128]{1,0:T(8,128)(2,1)S(1)}, bf16[80,128]{1,0:T(8,128)(2,1)S(1)}, u32[]{:S(2)}, u32[]{:S(2)}) collective-permute-start(bf16[80,128]{1,0:T(8,128)(2,1)S(1)} %shard_map.127.plane_ref.refs_2_), channel_id=1, source_target_pairs={{0,4},{4,8},{8,12},{12,0},{1,5},{5,9},{9,13},{13,1},{2,6},{6,10},{... | collective-permute-start | bytes 61448 | tf_op jit(solution)/shard_map/ppermute | solution.py:705
  48.6 1.9 %collective-permute-start.12 = (bf16[80,128]{1,0:T(8,128)(2,1)S(1)}, bf16[80,128]{1,0:T(8,128)(2,1)S(1)}, u32[]{:S(2)}, u32[]{:S(2)}) collective-permute-start(bf16[80,128]{1,0:T(8,128)(2,1)S(1)} %shard_map.127.plane_ref.refs_2_), channel_id=1, source_target_pairs={{0,12},{4,0},{8,4},{12,8},{1,13},{5,1},{9,5},{13,9},{2,14},{6,2},{... | collective-permute-start | bytes 61448 | tf_op jit(solution)/shard_map/ppermute | solution.py:705
  50.4 0.1 collective-permute-start.13
  50.5 0.0 collective-permute-start.14
  50.5 0.8 %shard_map.128 = (bf16[3,768,640]{2,1,0:T(8,128)(2,1)S(1)}, bf16[3,768,128]{2,1,0:T(8,128)(2,1)S(1)}, bf16[3,640,128]{2,1,0:T(8,128)(2,1)S(1)}, f32[8,640]{1,0:T(8,128)S(1)}) custom-call(bf16[432,16]{1,0:T(8,128)(2,1)S(1)} %bitcast.17, bf16[432,16]{1,0:T(8,128)(2,1)S(1)} %bitcast.15, bf16[144,3]{1,0:T(8,128)(2,1)S(1)} %bitcast.19, f32[1,16]{1,0:T(1,128)S(1)} %bitcast.20, ...), custom_call_target="tpu_custom_call" | custom-call | tf_op jit(solution)/shard_map/pallas_call | solution.py:61
  51.3 1.1 %collective-permute-done.11.refs_3_ = bf16[80,128]{1,0:T(8,128)(2,1)S(1)} collective-permute-done((bf16[80,128]{1,0:T(8,128)(2,1)S(1)}, bf16[80,128]{1,0:T(8,128)(2,1)S(1)}, u32[]{:S(2)}, u32[]{:S(2)}) %collective-permute-start.11) | collective-permute-done | bytes 20512 | tf_op jit(solution)/shard_map/ppermute | solution.py:705
  52.5 0.0 collective-permute-start.15
  52.5 0.0 collective-permute-done.12.refs_4_
  52.5 0.5 collective-permute-start.16
  53.0 2.1 %collective-permute-done.13.refs_5_ = bf16[80,128]{1,0:T(8,128)(2,1)S(1)} collective-permute-done((bf16[80,128]{1,0:T(8,128)(2,1)S(1)}, bf16[80,128]{1,0:T(8,128)(2,1)S(1)}, u32[]{:S(2)}, u32[]{:S(2)}) %collective-permute-start.13) | collective-permute-done | bytes 20512 | tf_op jit(solution)/shard_map/ppermute | solution.py:705
  55.7 0.0 collective-permute-done.14.refs_6_
  55.7 0.0 collective-permute-done.15.refs_7_
  55.8 0.5 collective-permute-done.17.refs_9_
  56.3 4.4 %shard_map.129 = f32[1,32,60]{2,1,0:T(8,128)} custom-call(s32[3]{0:T(128)S(1)} %pad_add_fusion.ids_ref.refs_0_, f32[1]{0:T(128)S(6)} %copy.20.refs_1_, bf16[80,128]{1,0:T(8,128)(2,1)S(1)} %shard_map.127.plane_ref.refs_2_, bf16[80,128]{1,0:T(8,128)(2,1)S(1)} %collective-permute-done.11.refs_3_, bf16[80,128]{1,0:T(8,128)(2,1)S(1)} %collective-permute-done.12.refs_4_, ...), custom_call_target="tpu_custom_call" | custom-call | tf_op jit(solution)/shard_map/pallas_call | solution.py:61
  (9 shorter events, 0.1 us)
Async XLA Ops:
  2.3 14.0 %collective-permute-start = (s16[736,128]{1,0:T(8,128)(2,1)S(1)}, s16[736,128]{1,0:T(8,128)(2,1)S(1)}, u32[]{:S(2)}, u32[]{:S(2)}) collective-permute-start(s16[736,128]{1,0:T(8,128)(2,1)S(1)} %get-tuple-element.31), channel_id=1, source_target_pairs={{0,4},{4,8},{8,12},{12,0},{1,5},{5,9},{9,13},{13,1},{2,6},{6,10},{... | collective-permute-start | bytes 565256 | tf_op jit(solution)/shard_map/ppermute | solution.py:453
  5.3 10.9 %collective-permute-start.1 = (s16[736,128]{1,0:T(8,128)(2,1)S(1)}, s16[736,128]{1,0:T(8,128)(2,1)S(1)}, u32[]{:S(2)}, u32[]{:S(2)}) collective-permute-start(s16[736,128]{1,0:T(8,128)(2,1)S(1)} %get-tuple-element.32), channel_id=1, source_target_pairs={{0,12},{4,0},{8,4},{12,8},{1,13},{5,1},{9,5},{13,9},{2,14},{6,2},{... | collective-permute-start | bytes 565256 | tf_op jit(solution)/shard_map/ppermute | solution.py:453
  7.4 8.8 %collective-permute-start.2 = (f32[8,128]{1,0:T(8,128)S(1)}, f32[8,128]{1,0:T(8,128)S(1)}, u32[]{:S(2)}, u32[]{:S(2)}) collective-permute-start(f32[8,128]{1,0:T(8,128)S(1)} %get-tuple-element.33.refs_4_), channel_id=1, source_target_pairs={{0,8},{4,12},{8,0},{12,4},{1,9},{5,13},{9,1},{13,5},{2,10},{6,14},... | collective-permute-start | bytes 12296 | tf_op jit(solution)/shard_map/ppermute | solution.py:471
  16.3 3.9 %collective-permute-start.3 = (f32[2,24,128]{2,1,0:T(8,128)S(1)}, f32[2,24,128]{2,1,0:T(8,128)S(1)}, u32[]{:S(2)}, u32[]{:S(2)}) collective-permute-start(f32[2,24,128]{2,1,0:T(8,128)S(1)} %shard_map.121.refs_5_.yp_ref), channel_id=1, source_target_pairs={{0,2},{2,0},{1,3},{3,1},{4,6},{6,4},{5,7},{7,5},{8,10},{10,8},{9,1... | collective-permute-start | bytes 73736 | tf_op jit(solution)/shard_map/ppermute | solution.py:435
  20.6 30.0 %copy-start = (f32[16]{0:T(128)S(1)}, f32[16]{0:T(128)}, u32[]{:S(2)}) copy-start(f32[16]{0:T(128)} %param.13) | copy-start | bytes 196
  20.6 30.0 %copy-start.1 = (f32[16]{0:T(128)S(1)}, f32[16]{0:T(128)}, u32[]{:S(2)}) copy-start(f32[16]{0:T(128)} %param.15) | copy-start | bytes 196
  20.6 1.6 %collective-permute-start.4 = (f32[2,272,128]{2,1,0:T(8,128)S(1)}, f32[2,272,128]{2,1,0:T(8,128)S(1)}, u32[]{:S(2)}, u32[]{:S(2)}) collective-permute-start(f32[2,272,128]{2,1,0:T(8,128)S(1)} %shard_map.122), channel_id=1, source_target_pairs={{0,1},{1,0},{2,3},{3,2},{4,5},{5,4},{6,7},{7,6},{8,9},{9,8},{10,11... | collective-permute-start | bytes 835592 | tf_op jit(solution)/shard_map/ppermute | solution.py:441
  24.4 8.7 %collective-permute-start.5 = (s16[496,128]{1,0:T(8,128)(2,1)S(1)}, s16[496,128]{1,0:T(8,128)(2,1)S(1)}, u32[]{:S(2)}, u32[]{:S(2)}) collective-permute-start(s16[496,128]{1,0:T(8,128)(2,1)S(1)} %get-tuple-element.37), channel_id=1, source_target_pairs={{0,4},{4,8},{8,12},{12,0},{1,5},{5,9},{9,13},{13,1},{2,6},{6,10},{... | collective-permute-start | bytes 380936 | tf_op jit(solution)/shard_map/ppermute | solution.py:453
  25.1 8.1 %collective-permute-start.6 = (s16[496,128]{1,0:T(8,128)(2,1)S(1)}, s16[496,128]{1,0:T(8,128)(2,1)S(1)}, u32[]{:S(2)}, u32[]{:S(2)}) collective-permute-start(s16[496,128]{1,0:T(8,128)(2,1)S(1)} %get-tuple-element.38), channel_id=1, source_target_pairs={{0,12},{4,0},{8,4},{12,8},{1,13},{5,1},{9,5},{13,9},{2,14},{6,2},{... | collective-permute-start | bytes 380936 | tf_op jit(solution)/shard_map/ppermute | solution.py:453
  28.3 4.9 %collective-permute-start.7 = (f32[8,128]{1,0:T(8,128)S(1)}, f32[8,128]{1,0:T(8,128)S(1)}, u32[]{:S(2)}, u32[]{:S(2)}) collective-permute-start(f32[8,128]{1,0:T(8,128)S(1)} %get-tuple-element.39.refs_3_), channel_id=1, source_target_pairs={{0,8},{4,12},{8,0},{12,4},{1,9},{5,13},{9,1},{13,5},{2,10},{6,14},... | collective-permute-start | bytes 12296 | tf_op jit(solution)/shard_map/ppermute | solution.py:471
  33.2 3.9 %collective-permute-start.8 = (f32[2,24,128]{2,1,0:T(8,128)S(1)}, f32[2,24,128]{2,1,0:T(8,128)S(1)}, u32[]{:S(2)}, u32[]{:S(2)}) collective-permute-start(f32[2,24,128]{2,1,0:T(8,128)S(1)} %shard_map.124.refs_4_.yp_ref), channel_id=1, source_target_pairs={{0,2},{2,0},{1,3},{3,1},{4,6},{6,4},{5,7},{7,5},{8,10},{10,8},{9,1... | collective-permute-start | bytes 73736 | tf_op jit(solution)/shard_map/ppermute | solution.py:435
  37.3 1.6 %collective-permute-start.9 = (f32[2,272,128]{2,1,0:T(8,128)S(1)}, f32[2,272,128]{2,1,0:T(8,128)S(1)}, u32[]{:S(2)}, u32[]{:S(2)}) collective-permute-start(f32[2,272,128]{2,1,0:T(8,128)S(1)} %shard_map.125), channel_id=1, source_target_pairs={{0,1},{1,0},{2,3},{3,2},{4,5},{5,4},{6,7},{7,6},{8,9},{9,8},{10,11... | collective-permute-start | bytes 835592 | tf_op jit(solution)/shard_map/ppermute | solution.py:441
  42.2 3.7 %collective-permute-start.10 = (bf16[2,16,128]{2,1,0:T(8,128)(2,1)S(1)}, bf16[2,16,128]{2,1,0:T(8,128)(2,1)S(1)}, u32[]{:S(2)}, u32[]{:S(2)}) collective-permute-start(bf16[2,16,128]{2,1,0:T(8,128)(2,1)S(1)} %get-tuple-element.44), channel_id=1, source_target_pairs={{0,2},{2,0},{1,3},{3,1},{4,6},{6,4},{5,7},{7,5},{8,10},{10,8},{9,1... | collective-permute-start | bytes 24584 | tf_op jit(solution)/shard_map/ppermute | solution.py:435
  46.5 5.9 %collective-permute-start.11 = (bf16[80,128]{1,0:T(8,128)(2,1)S(1)}, bf16[80,128]{1,0:T(8,128)(2,1)S(1)}, u32[]{:S(2)}, u32[]{:S(2)}) collective-permute-start(bf16[80,128]{1,0:T(8,128)(2,1)S(1)} %shard_map.127.plane_ref.refs_2_), channel_id=1, source_target_pairs={{0,4},{4,8},{8,12},{12,0},{1,5},{5,9},{9,13},{13,1},{2,6},{6,10},{... | collective-permute-start | bytes 61448 | tf_op jit(solution)/shard_map/ppermute | solution.py:705
  48.6 3.9 %collective-permute-start.12 = (bf16[80,128]{1,0:T(8,128)(2,1)S(1)}, bf16[80,128]{1,0:T(8,128)(2,1)S(1)}, u32[]{:S(2)}, u32[]{:S(2)}) collective-permute-start(bf16[80,128]{1,0:T(8,128)(2,1)S(1)} %shard_map.127.plane_ref.refs_2_), channel_id=1, source_target_pairs={{0,12},{4,0},{8,4},{12,8},{1,13},{5,1},{9,5},{13,9},{2,14},{6,2},{... | collective-permute-start | bytes 61448 | tf_op jit(solution)/shard_map/ppermute | solution.py:705
  50.4 4.7 %collective-permute-start.13 = (bf16[80,128]{1,0:T(8,128)(2,1)S(1)}, bf16[80,128]{1,0:T(8,128)(2,1)S(1)}, u32[]{:S(2)}, u32[]{:S(2)}) collective-permute-start(bf16[80,128]{1,0:T(8,128)(2,1)S(1)} %shard_map.127.plane_ref.refs_2_), channel_id=1, source_target_pairs={{0,8},{4,12},{8,0},{12,4},{1,9},{5,13},{9,1},{13,5},{2,10},{6,14},... | collective-permute-start | bytes 61448 | tf_op jit(solution)/shard_map/ppermute | solution.py:705
  50.5 5.2 %collective-permute-start.14 = (bf16[80,128]{1,0:T(8,128)(2,1)S(1)}, bf16[80,128]{1,0:T(8,128)(2,1)S(1)}, u32[]{:S(2)}, u32[]{:S(2)}) collective-permute-start(bf16[80,128]{1,0:T(8,128)(2,1)S(1)} %shard_map.127.plane_ref.refs_2_), channel_id=1, source_target_pairs={{0,1},{1,0},{2,3},{3,2},{4,5},{5,4},{6,7},{7,6},{8,9},{9,8},{10,11... | collective-permute-start | bytes 61448 | tf_op jit(solution)/shard_map/ppermute | solution.py:441
  52.5 3.3 %collective-permute-start.15 = (bf16[80,128]{1,0:T(8,128)(2,1)S(1)}, bf16[80,128]{1,0:T(8,128)(2,1)S(1)}, u32[]{:S(2)}, u32[]{:S(2)}) collective-permute-start(bf16[80,128]{1,0:T(8,128)(2,1)S(1)} %collective-permute-done.11.refs_3_), channel_id=1, source_target_pairs={{0,1},{1,0},{2,3},{3,2},{4,5},{5,4},{6,7},{7,6},{8,9},{9,8},{10,11... | collective-permute-start | bytes 61448 | tf_op jit(solution)/shard_map/ppermute | solution.py:441
  52.5 3.3 %collective-permute-start.16 = (bf16[80,128]{1,0:T(8,128)(2,1)S(1)}, bf16[80,128]{1,0:T(8,128)(2,1)S(1)}, u32[]{:S(2)}, u32[]{:S(2)}) collective-permute-start(bf16[80,128]{1,0:T(8,128)(2,1)S(1)} %collective-permute-done.12.refs_4_), channel_id=1, source_target_pairs={{0,1},{1,0},{2,3},{3,2},{4,5},{5,4},{6,7},{7,6},{8,9},{9,8},{10,11... | collective-permute-start | bytes 61448 | tf_op jit(solution)/shard_map/ppermute | solution.py:441
  55.1 1.2 %collective-permute-start.17 = (bf16[80,128]{1,0:T(8,128)(2,1)S(1)}, bf16[80,128]{1,0:T(8,128)(2,1)S(1)}, u32[]{:S(2)}, u32[]{:S(2)}) collective-permute-start(bf16[80,128]{1,0:T(8,128)(2,1)S(1)} %collective-permute-done.13.refs_5_), channel_id=1, source_target_pairs={{0,1},{1,0},{2,3},{3,2},{4,5},{5,4},{6,7},{7,6},{8,9},{9,8},{10,11... | collective-permute-start | bytes 61448 | tf_op jit(solution)/shard_map/ppermute | solution.py:441

commit v7 on v6

--- a/solution.py
+++ b/solution.py
@@ -21,7 +21,6 @@
 SUM_LOW, SUM_SPAN = -1280.0, 4096.0
 
 VMEM = pl.BlockSpec(memory_space=pltpu.VMEM)
-SMEM = pl.BlockSpec(memory_space=pltpu.SMEM)
 HBM = pl.BlockSpec(memory_space=pltpu.HBM)
 
 
@@ -190,24 +189,29 @@
     return kernel
 
 
-def fill(code, f_ref, lo_ref, hi_ref, yr_ref, zr_ref, pad_ref, ze_ref):
+def spread(spans, extra, size):
+    return [v for a, b in spans for v in chunks(OFF + a - extra, OFF + b + extra, size)]
+
+
+def fill(code, f_ref, lo_ref, hi_ref, yr_ref, zr_ref, pad_ref, ze_ref, spans):
     nx, ny, nz = f_ref.shape
     end = OFF + ny
+    wide = [v for a, b in spans for v in chunks(max(a - 16, 0), min(b + 16, ny), 48)]
     for near, far, ref in ((1, 0, lo_ref), (nx + 2, nx + 3, hi_ref)):
-        for r, n in chunks(0, ny, 48):
+        for r, n in wide:
             pad_ref[near, OFF + r:OFF + r + n, :] = from_code(ref[r:r + n, :], code)
             pad_ref[far, OFF + r:OFF + r + n, :] = from_code(ref[ny + r:ny + r + n, :], code)
     for p, k in ((1, 8), (nx + 2, 9)):
         pad_ref[p, OFF - 1:OFF, :] = yr_ref[1, k:k + 1, :]
         pad_ref[p, end:end + 1, :] = yr_ref[0, k:k + 1, :]
     for x in range(nx):
-        for r, n in chunks(0, ny, 48):
+        for r, n in wide:
             pad_ref[x + 2, OFF + r:OFF + r + n, :] = f_ref[x, r:r + n, :]
         for side, near, far in ((1, OFF - 1, OFF - 2), (0, end, end + 1)):
             pad_ref[x + 2, near:near + 1, :] = yr_ref[side, 2 * x:2 * x + 1, :]
             pad_ref[x + 2, far:far + 1, :] = yr_ref[side, 2 * x + 1:2 * x + 2, :]
     for p in range(nx + 2):
-        for r, n in chunks(OFF - 8, OFF + ny + 8, 32):
+        for r, n in spread(spans, 8, 32):
             e = zr_ref[p // 4, r:r + n, :]
             ze_ref[p, r:r + n, :] = pltpu.roll(e, nz - 32 * (p % 4), 1) if p % 4 else e
 
@@ -246,11 +250,11 @@
     return well + 6.0 * f - around + STRAIN_COUPLING * m * (f - mean)
 
 
-def chemistry(g, pad_ref, mob_ref, mobe_ref, ze_ref, chem_ref, cheme_ref, mean):
-    nx, ny = g.nx, g.ny
+def chemistry(g, pad_ref, mob_ref, mobe_ref, ze_ref, chem_ref, cheme_ref, mean, spans):
+    nx = g.nx
     for p in range(nx + 2):
         inside = 1 <= p <= nx
-        rows = chunks(OFF - 8, OFF + ny + 8, 32) if inside else chunks(OFF, OFF + ny, 48)
+        rows = spread(spans, 8, 32) if inside else spread(spans, 0, 48)
         for r, n in rows:
             f = pad_ref[p + 1, r:r + n, :]
             e = ze_ref[p, r:r + n, :]
@@ -259,7 +263,7 @@
                       + g.before(f, e) + g.after(f, e))
             chem_ref[p, r:r + n, :] = chem_of(f, mob_ref[p, r:r + n, :], around, mean)
         if inside:
-            for r, n in chunks(OFF, OFF + ny, 48):
+            for r, n in spread(spans, 0, 48):
                 f = pad_ref[p + 1, r:r + n, :]
                 e = ze_ref[p, r:r + n, :]
                 around = (ze_ref[p - 1, r:r + n, :] + ze_ref[p + 1, r:r + n, :]
@@ -304,7 +308,7 @@
         end = OFF + ny
         g = Geometry(nx, ny, nz)
         mean = weighted_mean(yp_ref, yr_ref, zr_ref, ride_y, ride_z)
-        fill(A_CODE, f_ref, lo_ref, hi_ref, yr_ref, zr_ref, pad_ref, ze_ref)
+        fill(A_CODE, f_ref, lo_ref, hi_ref, yr_ref, zr_ref, pad_ref, ze_ref, [(0, ny)])
 
         def wear(p, r, n, a):
             m = a * a
@@ -326,7 +330,7 @@
         for x in range(nx):
             wear(x + 1, OFF - 1, 1, yr_ref[1, 10 + x:11 + x, :])
             wear(x + 1, end, 1, yr_ref[0, 10 + x:11 + x, :])
-        chemistry(g, pad_ref, mob_ref, mobe_ref, ze_ref, chem_ref, cheme_ref, mean)
+        chemistry(g, pad_ref, mob_ref, mobe_ref, ze_ref, chem_ref, cheme_ref, mean, [(0, ny)])
         top = jnp.zeros((8, nz), F32)
         bottom = jnp.zeros((8, nz), F32)
         for x in range(nx):
@@ -351,64 +355,101 @@
     return kernel
 
 
+def potentials_b(g, mean, a2_ref, ae2_ref, others, scratch, spans):
+    f_ref, lo_ref, hi_ref, yr_ref, zr_ref = others
+    pad_ref, ze_ref, mob_ref, mobe_ref, chem_ref, cheme_ref = scratch
+    nx, nz = g.nx, g.nz
+    fill(B_CODE, f_ref, lo_ref, hi_ref, yr_ref, zr_ref, pad_ref, ze_ref, spans)
+    for p in range(nx + 2):
+        for r, n in spread(spans, 8, 32) if 1 <= p <= nx else spread(spans, 0, 48):
+            a = a2_ref[p, r:r + n, :]
+            mob_ref[p, r:r + n, :] = a * a
+    for r, n in spread(spans, 0, 48):
+        a = ae2_ref[r - OFF:r - OFF + n, :]
+        a = a * a
+        for x in range(nx):
+            mobe_ref[x, r - OFF:r - OFF + n, :] = pltpu.roll(a, nz - 32 * x, 1) if x else a
+    chemistry(g, pad_ref, mob_ref, mobe_ref, ze_ref, chem_ref, cheme_ref, mean, spans)
+
+
+def finish_b(g, mean, x, r, n, labels, a2_ref, scratch):
+    pad_ref, ze_ref, mob_ref, mobe_ref, chem_ref, cheme_ref = scratch
+    m, flux = flux_of(g, x, r, n, mob_ref, mobe_ref, chem_ref, cheme_ref)
+    f0 = pad_ref[x + 2, r:r + n, :]
+    f = f0 + TIME_STEP * flux
+    a = worn(a2_ref[x + 1, r:r + n, :], m, f0, mean)
+    dmg = 1.0 - a * by_label(labels, tuple(1.0 / v for v in ROOTS))
+    return flux, (f, dmg, a * a, by_label(labels, FACTORS))
+
+
+def pool_rows(scr_ref, count, nz):
+    zin = lax.broadcasted_iota(jnp.int32, (nz, nz), 0)
+    out = lax.broadcasted_iota(jnp.int32, (nz, nz), 1)
+    total = jnp.zeros((count, nz), F32)
+    for i in range(4):
+        rows = (scr_ref[i, pl.ds(0, count, stride=4), :] + scr_ref[i, pl.ds(1, count, stride=4), :]
+                + scr_ref[i, pl.ds(2, count, stride=4), :] + scr_ref[i, pl.ds(3, count, stride=4), :])
+        pick = jnp.where((zin // 4 == out // 4) & (out % 4 == i), 1.0 / 64.0, 0.0).astype(F32)
+        total = total + jnp.dot(rows, pick, precision=lax.Precision.HIGHEST, preferred_element_type=F32)
+    return total
+
+
+def edge_b(ride_y, ride_z):
+    def kernel(f_ref, a2_ref, ae2_ref, lo_ref, hi_ref, yr_ref, zr_ref, yp_ref, l_hbm, edge_ref, *rest):
+        *scratch, pool_scr, l_ref, l_sem = rest
+        nx, ny, nz = f_ref.shape
+        spans = [(0, 16), (ny - 16, ny)]
+        loads = [pltpu.make_async_copy(l_hbm.at[:, a:b, :], l_ref.at[:, 16 * k:16 * k + 16, :], l_sem.at[k])
+                 for k, (a, b) in enumerate(spans)]
+        for c in loads:
+            c.start()
+        g = Geometry(nx, ny, nz)
+        mean = weighted_mean(yp_ref, yr_ref, zr_ref, ride_y, ride_z)
+        potentials_b(g, mean, a2_ref, ae2_ref, (f_ref, lo_ref, hi_ref, yr_ref, zr_ref), scratch, spans)
+        for c in loads:
+            c.wait()
+        for k, (a, b) in enumerate(spans):
+            s = slice(16 * k, 16 * k + 16)
+            pooled = [None] * 4
+            for x in range(nx):
+                _, values = finish_b(g, mean, x, OFF + a, 16, l_ref[x, s, :], a2_ref, scratch)
+                pooled = [v if p is None else p + v for p, v in zip(pooled, values)]
+            for i in range(4):
+                pool_scr[i, s, :] = pooled[i]
+        total = pool_rows(pool_scr, 8, nz)
+        blank = jnp.zeros((13, nz), F32)
+        edge_ref[0] = jnp.concatenate([total[0:3], blank]).astype(BF16)
+        edge_ref[1] = jnp.concatenate([total[5:8], blank]).astype(BF16)
+    return kernel
+
+
 def step_b(ride_y, ride_z):
     def kernel(f_ref, a2_ref, ae2_ref, lo_ref, hi_ref, yr_ref, zr_ref, yp_ref, l_hbm,
-               f3_hbm, dmg_hbm, flux_hbm, pool_ref, edge_ref,
-               pad_ref, ze_ref, mob_ref, mobe_ref, chem_ref, cheme_ref,
-               pool_scr, l_ref, f3_ref, dmg_ref, flux_ref, l_sem, sems):
-        nx, ny, nz = f3_ref.shape
+               f3_hbm, dmg_hbm, flux_hbm, pool_ref, *rest):
+        *scratch, pool_scr, l_ref, f3_ref, dmg_ref, flux_ref, l_sem, sems = rest
+        nx, ny, nz = f_ref.shape
         labels_in = pltpu.make_async_copy(l_hbm, l_ref, l_sem)
         labels_in.start()
         g = Geometry(nx, ny, nz)
         mean = weighted_mean(yp_ref, yr_ref, zr_ref, ride_y, ride_z)
-        fill(B_CODE, f_ref, lo_ref, hi_ref, yr_ref, zr_ref, pad_ref, ze_ref)
-        for p in range(nx + 2):
-            inside = 1 <= p <= nx
-            for r, n in chunks(OFF - 8, OFF + ny + 8, 32) if inside else chunks(OFF, OFF + ny, 48):
-                a = a2_ref[p, r:r + n, :]
-                mob_ref[p, r:r + n, :] = a * a
-        for r, n in chunks(0, ny, 48):
-            a = ae2_ref[r:r + n, :]
-            a = a * a
-            for x in range(nx):
-                mobe_ref[x, r:r + n, :] = pltpu.roll(a, nz - 32 * x, 1) if x else a
-        chemistry(g, pad_ref, mob_ref, mobe_ref, ze_ref, chem_ref, cheme_ref, mean)
+        potentials_b(g, mean, a2_ref, ae2_ref, (f_ref, lo_ref, hi_ref, yr_ref, zr_ref), scratch, [(0, ny)])
         labels_in.wait()
         copies = []
         for k, (r, n) in enumerate(chunks(OFF, OFF + ny, 48)):
             s = slice(r - OFF, r - OFF + n)
             pooled = [None] * 4
             for x in range(nx):
-                m, flux = flux_of(g, x, r, n, mob_ref, mobe_ref, chem_ref, cheme_ref)
-                f0 = pad_ref[x + 2, r:r + n, :]
-                f = f0 + TIME_STEP * flux
-                a = worn(a2_ref[x + 1, r:r + n, :], m, f0, mean)
-                labels = l_ref[x, s, :]
-                factor = by_label(labels, FACTORS)
-                dmg = 1.0 - a * by_label(labels, tuple(1.0 / v for v in ROOTS))
-                f3_ref[x, s, :] = f
-                dmg_ref[x, s, :] = dmg
+                flux, values = finish_b(g, mean, x, r, n, l_ref[x, s, :], a2_ref, scratch)
+                f3_ref[x, s, :] = values[0]
+                dmg_ref[x, s, :] = values[1]
                 flux_ref[x, s, :] = flux
-                for i, v in enumerate((f, dmg, a * a, factor)):
-                    pooled[i] = v if pooled[i] is None else pooled[i] + v
+                pooled = [v if p is None else p + v for p, v in zip(pooled, values)]
             for i in range(4):
                 pool_scr[i, s, :] = pooled[i]
             for i, (src, dst) in enumerate(((f3_ref, f3_hbm), (dmg_ref, dmg_hbm), (flux_ref, flux_hbm))):
                 copies.append(pltpu.make_async_copy(src.at[:, s, :], dst.at[:, s, :], sems.at[i, k]))
                 copies[-1].start()
-        py, pz = ny // 4, nz // 4
-        zin = lax.broadcasted_iota(jnp.int32, (nz, 4 * pz), 0)
-        out = lax.broadcasted_iota(jnp.int32, (nz, 4 * pz), 1)
-        total = jnp.zeros((py, 4 * pz), F32)
-        for i in range(4):
-            rows = (pool_scr[i, pl.ds(0, py, stride=4), :] + pool_scr[i, pl.ds(1, py, stride=4), :]
-                    + pool_scr[i, pl.ds(2, py, stride=4), :] + pool_scr[i, pl.ds(3, py, stride=4), :])
-            pick = jnp.where((zin // 4 == out // 4) & (out % 4 == i), 1.0 / 64.0, 0.0).astype(F32)
-            total = total + jnp.dot(rows, pick, precision=lax.Precision.HIGHEST, preferred_element_type=F32)
-        pool_ref[...] = total.astype(BF16)
-        blank = jnp.zeros((13, 4 * pz), F32)
-        edge_ref[0] = jnp.concatenate([total[0:3], blank]).astype(BF16)
-        edge_ref[1] = jnp.concatenate([total[py - 3:py], blank]).astype(BF16)
+        pool_ref[...] = pool_rows(pool_scr, ny // 4, nz).astype(BF16)
         for c in copies:
             c.wait()
     return kernel
@@ -503,17 +544,21 @@
     yr = both_sides(ypay, "gy")
     (zpay,) = call(pack_z(B_CODE, ride_y, False), [(packed, F32)], f, lo, hi, yr, ypay)
     zr = z_neighbour(zpay, "gz")
-    fraction, damage_field, flux_sum, pooled, edge = call(
+    last = (f, a2, ae2, lo, hi, yr, zr, ypay, labels)
+    (edge,) = call(
+        edge_b(ride_y, ride_z), [((2, 16, nz), BF16)], *last, in_specs=[VMEM] * 8 + [HBM],
+        scratch=scratch + [
+            pltpu.VMEM((4, 32, nz), F32), pltpu.VMEM((nx, 32, nz), jnp.int32), pltpu.SemaphoreType.DMA((2,))])
+    fraction, damage_field, flux_sum, pooled = call(
         step_b(ride_y, ride_z),
-        [(block, F32), (block, F32), (block, F32), ((ny // 4, nz), BF16), ((2, 16, nz), BF16)],
-        f, a2, ae2, lo, hi, yr, zr, ypay, labels,
-        in_specs=[VMEM] * 8 + [HBM], out_specs=[HBM] * 3 + [VMEM] * 2,
+        [(block, F32), (block, F32), (block, F32), ((ny // 4, nz), BF16)], *last,
+        in_specs=[VMEM] * 8 + [HBM], out_specs=[HBM] * 3 + [VMEM],
         scratch=scratch + [
             pltpu.VMEM((4, ny, nz), F32), pltpu.VMEM(block, jnp.int32),
             pltpu.VMEM(block, F32), pltpu.VMEM(block, F32), pltpu.VMEM(block, F32),
             pltpu.SemaphoreType.DMA, pltpu.SemaphoreType.DMA((3, len(chunks(OFF, OFF + ny, 48))))])
-    ids = jnp.stack([lax.axis_index(a) for a in ("gx", "gy", "gz")])
-    crack_score = detector(pooled, edge, ids, weights + (b_first[None], b_second[None]), b_third, ny // 4, nz // 4)
+    ids = jnp.broadcast_to(jnp.stack([lax.axis_index(a) for a in ("gx", "gy", "gz")])[:, None], (3, nz))
+    crack_score = detector(pooled, edge, ids, weights + (b_first[None], b_second[None], b_third[None]), ny // 4, nz // 4)
     return (fraction, damage_field, flux_sum, crack_score)
 
 
@@ -547,7 +592,7 @@
 SHIFTS = tuple(k for k in range(-3, 10) if k % (16 // CIN) == 3)
 
 
-def weight_kernel(w1_ref, w2_ref, w3_ref, b1_ref, b2_ref, plane_ref, t1_ref, t2_ref, t3_ref, bias_ref):
+def weight_kernel(w1_ref, w2_ref, w3_ref, b1_ref, b2_ref, b3_ref, plane_ref, t1_ref, t2_ref, t3_ref, bias_ref):
     n1 = bias_ref.shape[1]
     k1 = t1_ref.shape[1] // 3
     pz = k1 // (2 * CIN)
@@ -567,7 +612,7 @@
         return out.astype(BF16)
 
     zero = jnp.zeros((16, 128), BF16)
-    bias_ref[...] = jnp.zeros(bias_ref.shape, F32)
+    bias_ref[...] = jnp.broadcast_to(b3_ref[...], bias_ref.shape)
     for i in range(3):
         for j in range(3):
             tap = 9 * i + 3 * j
@@ -598,7 +643,7 @@
 
 def plane_kernel(py, y_count):
     def kernel(ids_ref, pool_ref, yr_ref, out_ref, scr_ref):
-        iy = ids_ref[1]
+        iy = ids_ref[1:2, 0:1]
         scr_ref[...] = jnp.zeros(scr_ref.shape, F32)
         scr_ref[TOP:TOP + py, :] = pool_ref[0:py, :].astype(F32)
         below = yr_ref[1].astype(F32)[0:3]
@@ -614,12 +659,12 @@
     n = len(shifts)
 
     def kernel(*refs):
-        ids_ref, b3_ref = refs[:2]
-        own = refs[2:3 + n]
-        other = refs[3 + n:4 + 2 * n]
-        t1_ref, t2_ref, t3_ref, bias_ref, out_ref = refs[4 + 2 * n:9 + 2 * n]
-        in_ref, lhs1_ref, act1_ref, lhs2_ref, act2_ref, tail_ref = refs[9 + 2 * n:]
-        ix, iy, iz = ids_ref[0], ids_ref[1], ids_ref[2]
+        ids_ref = refs[0]
+        own = refs[1:2 + n]
+        other = refs[2 + n:3 + 2 * n]
+        t1_ref, t2_ref, t3_ref, bias_ref, out_ref = refs[3 + 2 * n:8 + 2 * n]
+        in_ref, lhs1_ref, act1_ref, lhs2_ref, act2_ref, tail_ref = refs[8 + 2 * n:]
+        ix, iy, iz = ids_ref[0:1, 0:1], ids_ref[1:2, 0:1], ids_ref[2:3, 0:1]
         half = own[0].shape[1]
         pz = half // CIN
         rows = py + 4
@@ -682,11 +727,11 @@
         score = tail_ref[0:py, :]
         for j in (1, 2):
             score = score + pltpu.roll(tail_ref[j:j + py, :], 128 - j * pz, 1)
-        out_ref[0] = jnp.transpose(score)[0:pz, :] + b3_ref[0]
+        out_ref[0] = jnp.transpose(score)[0:pz, :] + bias_ref[2:3, 0:1]
     return kernel
 
 
-def detector(pooled, edge, ids, weights, b_third, py, pz):
+def detector(pooled, edge, ids, weights, py, pz):
     counts = tuple(lax.axis_size(a) for a in ("gx", "gy", "gz"))
     half = pooled.shape[1]
     assert half == 128 and pz * CIN == half and pz * 3 <= 128
@@ -697,7 +742,7 @@
     tall = -(-(TOP + py + 3) // 16) * 16
     (plane,) = call(
         plane_kernel(py, counts[1]), [((tall, half), BF16)], ids, pooled, yr,
-        in_specs=[SMEM, VMEM, VMEM], scratch=[pltpu.VMEM((tall, half), F32)])
+        scratch=[pltpu.VMEM((tall, half), F32)])
     shifts = []
     for s in (1, -1, 2, -2, 3, -3):
         if s % counts[0] and s % counts[0] not in shifts:
@@ -709,10 +754,9 @@
         *weights, plane)
     own[1], *matrices = lax.optimization_barrier((own[1], *matrices))
     other = [z_neighbour(v, "gz", False) for v in own]
-    args = (ids, b_third, *own, *other, *matrices)
+    args = (ids, *own, *other, *matrices)
     (score,) = call(
         conv_kernel(py, counts, shifts), [((1, pz, py), F32)], *args,
-        in_specs=[SMEM] * 2 + [VMEM] * (len(args) - 2),
         scratch=[
             pltpu.VMEM((7, tall, 2 * half), F32),
             pltpu.VMEM((7, rows, 6 * half), BF16),

time: 61 us -> 60 us (0.984)
  waiting for transfers between devices: 23.5 us -> 21.2 us
  Pallas kernels: 13.5 us -> 14.5 us
    ppermute x3, waiting for transfers between devices: 6.75 us -> 4.67 us  [both_sides(): return lax.ppermute(pay, axis, ring(axis, 1))]
    pallas_call x10 -> x11, Pallas kernels: 13.5 us -> 14.5 us  [call(): pl.pallas_call(kernel, in_specs=in_specs or [VMEM] * len(args), out_specs...]
    ppermute x3, waiting for transfers between devices: 3.22 us -> 2.34 us  [detector(): own = [plane] + [lax.ppermute(plane, 'gx', ring('gx', s)) for s in shifts]]
    ppermute x6, waiting for transfers between devices: 3.6 us -> 4.26 us  [z_neighbour(): return lax.ppermute(pay, axis, ring(axis, 1))]
  transfers between devices with their start and end apart: 18 -> 18, of which waited for: 10 -> 9; matrix products, arithmetic and copies ran while one was open for 5% -> 5% of each run, Pallas kernels for 1% -> 8%
where the time goes in v7:
time: 60 us; the launch traced here: 59.6 us
  waiting for transfers between devices  21.2 us (35%)
  starting transfers between devices  19.4 us (32%)
  Pallas kernels  14.5 us (24%)
  local copies, waits for them, and re-layouts  2.93 us (5%)
  between operations  1.45 us (2%)
    pallas_call x11, Pallas kernels, call(): pl.pallas_call(kernel, in_specs=in_specs or [VMEM] * len(args), out_specs...  14.5 us
    ppermute x2, waiting for transfers between devices, start(): return (sums, lax.ppermute(sums, 'gx', ring('gx', 2)))  9.93 us
    ppermute x2, starting transfers between devices, x_sides(): lax.ppermute(lo, 'gx', ring('gx', -1))  5.32 us
    ppermute x3, waiting for transfers between devices, both_sides(): return lax.ppermute(pay, axis, ring(axis, 1))  4.67 us
    ppermute x3, starting transfers between devices, both_sides(): return lax.ppermute(pay, axis, ring(axis, 1))  4.67 us
    ppermute x6, waiting for transfers between devices, z_neighbour(): return lax.ppermute(pay, axis, ring(axis, 1))  4.26 us
    ppermute x3, starting transfers between devices, detector(): own = [plane] + [lax.ppermute(plane, 'gx', ring('gx', s)) for s in shifts]  4 us
    ppermute x2, starting transfers between devices, x_sides(): lax.ppermute(hi, 'gx', ring('gx', 1))  3.72 us
  transfers between devices with their start and end apart: 18, of which 9 were waited for; matrix products, arithmetic and copies ran while one was open for 5% of the time, Pallas kernels for 8%

profile of v7, /device:TPU:0, one launch (start us, length us, event | category | flops | bytes accessed | tf_op | source)
XLA Modules:
  0.0 59.6 jit_solution(6824513505394224480)
XLA Ops:
  0.6 1.6 %shard_map.120 = (f32[4,240,128]{2,1,0:T(8,128)S(1)}, f32[4,240,128]{2,1,0:T(8,128)S(1)}, s16[736,128]{1,0:T(8,128)(2,1)S(1)}, s16[736,128]{1,0:T(8,128)(2,1)S(1)}, f32[8,128]{1,0:T(8,128)S(1)}) custom-call(f32[4,240,128]{2,1,0:T(8,128)} %c_hbm.1, f32[4,240,128]{2,1,0:T(8,128)} %d_hbm.1, s32[4,240,128]{2,1,0:T(8,128)} %l_hbm.5), custom_call_target="tpu_custom_call" | custom-call | tf_op jit(solution)/shard_map/pallas_call | solution.py:60
  2.3 3.1 %collective-permute-start = (s16[736,128]{1,0:T(8,128)(2,1)S(1)}, s16[736,128]{1,0:T(8,128)(2,1)S(1)}, u32[]{:S(2)}, u32[]{:S(2)}) collective-permute-start(s16[736,128]{1,0:T(8,128)(2,1)S(1)} %get-tuple-element.30), channel_id=1, source_target_pairs={{0,4},{4,8},{8,12},{12,0},{1,5},{5,9},{9,13},{13,1},{2,6},{6,10},{... | collective-permute-start | bytes 565256 | tf_op jit(solution)/shard_map/ppermute | solution.py:494
  5.3 2.1 %collective-permute-start.1 = (s16[736,128]{1,0:T(8,128)(2,1)S(1)}, s16[736,128]{1,0:T(8,128)(2,1)S(1)}, u32[]{:S(2)}, u32[]{:S(2)}) collective-permute-start(s16[736,128]{1,0:T(8,128)(2,1)S(1)} %get-tuple-element.31), channel_id=1, source_target_pairs={{0,12},{4,0},{8,4},{12,8},{1,13},{5,1},{9,5},{13,9},{2,14},{6,2},{... | collective-permute-start | bytes 565256 | tf_op jit(solution)/shard_map/ppermute | solution.py:494
  7.4 0.9 %collective-permute-start.2 = (f32[8,128]{1,0:T(8,128)S(1)}, f32[8,128]{1,0:T(8,128)S(1)}, u32[]{:S(2)}, u32[]{:S(2)}) collective-permute-start(f32[8,128]{1,0:T(8,128)S(1)} %get-tuple-element.32.refs_4_), channel_id=1, source_target_pairs={{0,8},{4,12},{8,0},{12,4},{1,9},{5,13},{9,1},{13,5},{2,10},{6,14},... | collective-permute-start | bytes 12296 | tf_op jit(solution)/shard_map/ppermute | solution.py:512
  8.4 0.8 %copy.16 = bf16[27,4,16]{2,1,0:T(4,128)(2,1)S(1)} copy(bf16[27,4,16]{0,1,2:T(4,128)(2,1)} %bitcast.27) | data formatting | bytes 6912 | tf_op jit(solution)/shard_map/transpose | solution.py:635
  9.2 1.0 %copy.17 = bf16[27,16,16]{2,1,0:T(8,128)(2,1)S(1)} copy(bf16[27,16,16]{0,1,2:T(8,128)(2,1)} %bitcast.24) | data formatting | bytes 27648 | tf_op jit(solution)/shard_map/transpose | solution.py:636
  10.2 0.8 %copy.18 = bf16[27,1,16]{2,0,1:T(8,128)(2,1)S(1)} copy(bf16[27,1,16]{0,2,1:T(8,128)(2,1)} %param.16) | data formatting | bytes 1728 | tf_op args[7]
  11.0 0.1 copy.19
  11.2 5.1 %collective-permute-done.2.refs_5_ = f32[8,128]{1,0:T(8,128)S(1)} collective-permute-done((f32[8,128]{1,0:T(8,128)S(1)}, f32[8,128]{1,0:T(8,128)S(1)}, u32[]{:S(2)}, u32[]{:S(2)}) %collective-permute-start.2) | collective-permute-done | bytes 4128 | tf_op jit(solution)/shard_map/ppermute | solution.py:512
  16.3 0.0 collective-permute-done.refs_2_.lo_ref
  16.3 0.0 collective-permute-done.1.refs_3_.hi_ref
  16.3 1.6 %collective-permute-start.3 = (f32[2,24,128]{2,1,0:T(8,128)S(1)}, f32[2,24,128]{2,1,0:T(8,128)S(1)}, u32[]{:S(2)}, u32[]{:S(2)}) collective-permute-start(f32[2,24,128]{2,1,0:T(8,128)S(1)} %shard_map.121.refs_5_.yp_ref), channel_id=1, source_target_pairs={{0,2},{2,0},{1,3},{3,1},{4,6},{6,4},{5,7},{7,5},{8,10},{10,8},{9,1... | collective-permute-start | bytes 73736 | tf_op jit(solution)/shard_map/ppermute | solution.py:476
  17.9 2.3 %collective-permute-done.3.refs_4_.yr_ref = f32[2,24,128]{2,1,0:T(8,128)S(1)} collective-permute-done((f32[2,24,128]{2,1,0:T(8,128)S(1)}, f32[2,24,128]{2,1,0:T(8,128)S(1)}, u32[]{:S(2)}, u32[]{:S(2)}) %collective-permute-start.3) | collective-permute-done | bytes 24608 | tf_op jit(solution)/shard_map/ppermute | solution.py:476
  20.2 0.3 shard_map.122
  20.6 0.1 collective-permute-start.4
  20.6 1.5 %collective-permute-done.4.zr_ref = f32[2,272,128]{2,1,0:T(8,128)S(1)} collective-permute-done((f32[2,272,128]{2,1,0:T(8,128)S(1)}, f32[2,272,128]{2,1,0:T(8,128)S(1)}, u32[]{:S(2)}, u32[]{:S(2)}) %collective-permute-start.4) | collective-permute-done | bytes 278560 | tf_op jit(solution)/shard_map/ppermute | solution.py:482
  22.2 2.2 %shard_map.123 = (f32[4,240,128]{2,1,0:T(8,128)S(1)}, f32[6,272,128]{2,1,0:T(8,128)S(1)}, f32[240,128]{1,0:T(8,128)S(1)}, s16[496,128]{1,0:T(8,128)(2,1)S(1)}, s...) custom-call(f32[4,240,128]{2,1,0:T(8,128)S(1)} %get-tuple-element.28.refs_0_.f_ref, ...), custom_call_target="tpu_custom_call" | custom-call | tf_op jit(solution)/shard_map/pallas_call | solution.py:60
  24.4 0.6 %collective-permute-start.5 = (s16[496,128]{1,0:T(8,128)(2,1)S(1)}, s16[496,128]{1,0:T(8,128)(2,1)S(1)}, u32[]{:S(2)}, u32[]{:S(2)}) collective-permute-start(s16[496,128]{1,0:T(8,128)(2,1)S(1)} %get-tuple-element.36), channel_id=1, source_target_pairs={{0,4},{4,8},{8,12},{12,0},{1,5},{5,9},{9,13},{13,1},{2,6},{6,10},{... | collective-permute-start | bytes 380936 | tf_op jit(solution)/shard_map/ppermute | solution.py:494
  25.0 3.2 %collective-permute-start.6 = (s16[496,128]{1,0:T(8,128)(2,1)S(1)}, s16[496,128]{1,0:T(8,128)(2,1)S(1)}, u32[]{:S(2)}, u32[]{:S(2)}) collective-permute-start(s16[496,128]{1,0:T(8,128)(2,1)S(1)} %get-tuple-element.37), channel_id=1, source_target_pairs={{0,12},{4,0},{8,4},{12,8},{1,13},{5,1},{9,5},{13,9},{2,14},{6,2},{... | collective-permute-start | bytes 380936 | tf_op jit(solution)/shard_map/ppermute | solution.py:494
  28.3 0.0 collective-permute-start.7
  28.3 4.9 %collective-permute-done.7.refs_4_ = f32[8,128]{1,0:T(8,128)S(1)} collective-permute-done((f32[8,128]{1,0:T(8,128)S(1)}, f32[8,128]{1,0:T(8,128)S(1)}, u32[]{:S(2)}, u32[]{:S(2)}) %collective-permute-start.7) | collective-permute-done | bytes 4128 | tf_op jit(solution)/shard_map/ppermute | solution.py:512
  33.2 0.0 copy-start
  33.2 0.0 copy-start.1
  33.2 1.6 %collective-permute-start.8 = (f32[2,24,128]{2,1,0:T(8,128)S(1)}, f32[2,24,128]{2,1,0:T(8,128)S(1)}, u32[]{:S(2)}, u32[]{:S(2)}) collective-permute-start(f32[2,24,128]{2,1,0:T(8,128)S(1)} %shard_map.124.refs_4_.yp_ref), channel_id=1, source_target_pairs={{0,2},{2,0},{1,3},{3,1},{4,6},{6,4},{5,7},{7,5},{8,10},{10,8},{9,1... | collective-permute-start | bytes 73736 | tf_op jit(solution)/shard_map/ppermute | solution.py:476
  34.7 2.3 %collective-permute-done.8.refs_3_.yr_ref = f32[2,24,128]{2,1,0:T(8,128)S(1)} collective-permute-done((f32[2,24,128]{2,1,0:T(8,128)S(1)}, f32[2,24,128]{2,1,0:T(8,128)S(1)}, u32[]{:S(2)}, u32[]{:S(2)}) %collective-permute-start.8) | collective-permute-done | bytes 24608 | tf_op jit(solution)/shard_map/ppermute | solution.py:476
  37.1 0.2 shard_map.125
  37.3 0.1 collective-permute-start.9
  37.4 1.5 %collective-permute-done.9.zr_ref = f32[2,272,128]{2,1,0:T(8,128)S(1)} collective-permute-done((f32[2,272,128]{2,1,0:T(8,128)S(1)}, f32[2,272,128]{2,1,0:T(8,128)S(1)}, u32[]{:S(2)}, u32[]{:S(2)}) %collective-permute-start.9) | collective-permute-done | bytes 278560 | tf_op jit(solution)/shard_map/ppermute | solution.py:482
  38.9 1.4 %shard_map.127 = bf16[2,16,128]{2,1,0:T(8,128)(2,1)S(1)} custom-call(f32[4,240,128]{2,1,0:T(8,128)S(1)} %get-tuple-element.33.refs_0_.f_ref, f32[6,272,128]{2,1,0:T(8,128)S(1)} %get-tuple-element.34.a2_ref, f32[240,128]{1,0:T(8,128)S(1)} %get-tuple-element.35.ae2_ref, s16[496,128]{1,0:T(8,128)(2,1)S(1)} %collective-permute-done.5.refs_1_.lo_ref, ...), custom_call_target="tpu_custom_call" | custom-call | tf_op jit(solution)/shard_map/pallas_call | solution.py:60
  40.3 1.6 %collective-permute-start.10 = (bf16[2,16,128]{2,1,0:T(8,128)(2,1)S(1)}, bf16[2,16,128]{2,1,0:T(8,128)(2,1)S(1)}, u32[]{:S(2)}, u32[]{:S(2)}) collective-permute-start(bf16[2,16,128]{2,1,0:T(8,128)(2,1)S(1)} %shard_map.127), channel_id=1, source_target_pairs={{0,2},{2,0},{1,3},{3,1},{4,6},{6,4},{5,7},{7,5},{8,10},{10,8},{9,1... | collective-permute-start | bytes 24584 | tf_op jit(solution)/shard_map/ppermute | solution.py:476
  41.9 0.1 pad_add_fusion
  41.9 3.9 %shard_map.126 = (f32[4,240,128]{2,1,0:T(8,128)}, f32[4,240,128]{2,1,0:T(8,128)}, f32[4,240,128]{2,1,0:T(8,128)}, bf16[60,128]{1,0:T(8,128)(2,1)S(1)}) custom-call(f32[4,240,128]{2,1,0:T(8,128)S(1)} %get-tuple-element.33.refs_0_.f_ref, f32[6,272,128]{2,1,0:T(8,128)S(1)} %get-tuple-element.34.a2_ref, f32[240,128]{1,0:T(8,128)S(1)} %get-tuple-element.35.ae2_ref, ...), custom_call_target="tpu_custom_call" | custom-call | tf_op jit(solution)/shard_map/pallas_call | solution.py:60
  45.8 0.1 broadcast_in_dim.15.ids_ref.refs_0_
  45.9 2.0 %collective-permute-start.11 = (bf16[80,128]{1,0:T(8,128)(2,1)S(1)}, bf16[80,128]{1,0:T(8,128)(2,1)S(1)}, u32[]{:S(2)}, u32[]{:S(2)}) collective-permute-start(bf16[80,128]{1,0:T(8,128)(2,1)S(1)} %shard_map.128.plane_ref.refs_1_), channel_id=1, source_target_pairs={{0,4},{4,8},{8,12},{12,0},{1,5},{5,9},{9,13},{13,1},{2,6},{6,10},{... | collective-permute-start | bytes 61448 | tf_op jit(solution)/shard_map/ppermute | solution.py:750
  48.0 1.9 %collective-permute-start.12 = (bf16[80,128]{1,0:T(8,128)(2,1)S(1)}, bf16[80,128]{1,0:T(8,128)(2,1)S(1)}, u32[]{:S(2)}, u32[]{:S(2)}) collective-permute-start(bf16[80,128]{1,0:T(8,128)(2,1)S(1)} %shard_map.128.plane_ref.refs_1_), channel_id=1, source_target_pairs={{0,12},{4,0},{8,4},{12,8},{1,13},{5,1},{9,5},{13,9},{2,14},{6,2},{... | collective-permute-start | bytes 61448 | tf_op jit(solution)/shard_map/ppermute | solution.py:750
  49.8 0.1 collective-permute-start.13
  50.6 0.1 collective-permute-start.14
  50.7 0.9 %shard_map.129 = (bf16[3,768,640]{2,1,0:T(8,128)(2,1)S(1)}, bf16[3,768,128]{2,1,0:T(8,128)(2,1)S(1)}, bf16[3,640,128]{2,1,0:T(8,128)(2,1)S(1)}, f32[8,640]{1,0:T(8,128)S(1)}) custom-call(bf16[432,16]{1,0:T(8,128)(2,1)S(1)} %bitcast.19, bf16[432,16]{1,0:T(8,128)(2,1)S(1)} %bitcast.17, bf16[144,3]{1,0:T(8,128)(2,1)S(1)} %bitcast.21, f32[1,16]{1,0:T(1,128)S(1)} %bitcast.22, ...), custom_call_target="tpu_custom_call" | custom-call | tf_op jit(solution)/shard_map/pallas_call | solution.py:60
  51.6 0.1 collective-permute-done.11.refs_2_
  51.7 0.5 collective-permute-start.15
  52.2 0.0 collective-permute-done.12.refs_3_
  52.2 0.1 collective-permute-start.16
  52.2 2.3 %collective-permute-done.13.refs_4_ = bf16[80,128]{1,0:T(8,128)(2,1)S(1)} collective-permute-done((bf16[80,128]{1,0:T(8,128)(2,1)S(1)}, bf16[80,128]{1,0:T(8,128)(2,1)S(1)}, u32[]{:S(2)}, u32[]{:S(2)}) %collective-permute-start.13) | collective-permute-done | bytes 20512 | tf_op jit(solution)/shard_map/ppermute | solution.py:750
  54.5 0.0 collective-permute-done.14.refs_5_
  54.5 0.0 collective-permute-done.15.refs_6_
  54.5 0.0 collective-permute-done.16.refs_7_
  54.5 1.2 %collective-permute-done.17.refs_8_ = bf16[80,128]{1,0:T(8,128)(2,1)S(1)} collective-permute-done((bf16[80,128]{1,0:T(8,128)(2,1)S(1)}, bf16[80,128]{1,0:T(8,128)(2,1)S(1)}, u32[]{:S(2)}, u32[]{:S(2)}) %collective-permute-start.17) | collective-permute-done | bytes 20512 | tf_op jit(solution)/shard_map/ppermute | solution.py:482
  55.7 3.9 %shard_map.130 = f32[1,32,60]{2,1,0:T(8,128)} custom-call(s32[3,128]{1,0:T(4,128)S(1)} %broadcast_in_dim.15.ids_ref.refs_0_, bf16[80,128]{1,0:T(8,128)(2,1)S(1)} %shard_map.128.plane_ref.refs_1_, bf16[80,128]{1,0:T(8,128)(2,1)S(1)} %collective-permute-done.11.refs_2_, bf16[80,128]{1,0:T(8,128)(2,1)S(1)} %collective-permute-done.12.refs_3_, ...), custom_call_target="tpu_custom_call" | custom-call | tf_op jit(solution)/shard_map/pallas_call | solution.py:60
  (11 shorter events, 0.1 us)
Async XLA Ops:
  2.3 14.0 %collective-permute-start = (s16[736,128]{1,0:T(8,128)(2,1)S(1)}, s16[736,128]{1,0:T(8,128)(2,1)S(1)}, u32[]{:S(2)}, u32[]{:S(2)}) collective-permute-start(s16[736,128]{1,0:T(8,128)(2,1)S(1)} %get-tuple-element.30), channel_id=1, source_target_pairs={{0,4},{4,8},{8,12},{12,0},{1,5},{5,9},{9,13},{13,1},{2,6},{6,10},{... | collective-permute-start | bytes 565256 | tf_op jit(solution)/shard_map/ppermute | solution.py:494
  5.3 10.9 %collective-permute-start.1 = (s16[736,128]{1,0:T(8,128)(2,1)S(1)}, s16[736,128]{1,0:T(8,128)(2,1)S(1)}, u32[]{:S(2)}, u32[]{:S(2)}) collective-permute-start(s16[736,128]{1,0:T(8,128)(2,1)S(1)} %get-tuple-element.31), channel_id=1, source_target_pairs={{0,12},{4,0},{8,4},{12,8},{1,13},{5,1},{9,5},{13,9},{2,14},{6,2},{... | collective-permute-start | bytes 565256 | tf_op jit(solution)/shard_map/ppermute | solution.py:494
  7.4 8.8 %collective-permute-start.2 = (f32[8,128]{1,0:T(8,128)S(1)}, f32[8,128]{1,0:T(8,128)S(1)}, u32[]{:S(2)}, u32[]{:S(2)}) collective-permute-start(f32[8,128]{1,0:T(8,128)S(1)} %get-tuple-element.32.refs_4_), channel_id=1, source_target_pairs={{0,8},{4,12},{8,0},{12,4},{1,9},{5,13},{9,1},{13,5},{2,10},{6,14},... | collective-permute-start | bytes 12296 | tf_op jit(solution)/shard_map/ppermute | solution.py:512
  16.3 3.9 %collective-permute-start.3 = (f32[2,24,128]{2,1,0:T(8,128)S(1)}, f32[2,24,128]{2,1,0:T(8,128)S(1)}, u32[]{:S(2)}, u32[]{:S(2)}) collective-permute-start(f32[2,24,128]{2,1,0:T(8,128)S(1)} %shard_map.121.refs_5_.yp_ref), channel_id=1, source_target_pairs={{0,2},{2,0},{1,3},{3,1},{4,6},{6,4},{5,7},{7,5},{8,10},{10,8},{9,1... | collective-permute-start | bytes 73736 | tf_op jit(solution)/shard_map/ppermute | solution.py:476
  20.6 1.6 %collective-permute-start.4 = (f32[2,272,128]{2,1,0:T(8,128)S(1)}, f32[2,272,128]{2,1,0:T(8,128)S(1)}, u32[]{:S(2)}, u32[]{:S(2)}) collective-permute-start(f32[2,272,128]{2,1,0:T(8,128)S(1)} %shard_map.122), channel_id=1, source_target_pairs={{0,1},{1,0},{2,3},{3,2},{4,5},{5,4},{6,7},{7,6},{8,9},{9,8},{10,11... | collective-permute-start | bytes 835592 | tf_op jit(solution)/shard_map/ppermute | solution.py:482
  24.4 8.7 %collective-permute-start.5 = (s16[496,128]{1,0:T(8,128)(2,1)S(1)}, s16[496,128]{1,0:T(8,128)(2,1)S(1)}, u32[]{:S(2)}, u32[]{:S(2)}) collective-permute-start(s16[496,128]{1,0:T(8,128)(2,1)S(1)} %get-tuple-element.36), channel_id=1, source_target_pairs={{0,4},{4,8},{8,12},{12,0},{1,5},{5,9},{9,13},{13,1},{2,6},{6,10},{... | collective-permute-start | bytes 380936 | tf_op jit(solution)/shard_map/ppermute | solution.py:494
  25.0 8.1 %collective-permute-start.6 = (s16[496,128]{1,0:T(8,128)(2,1)S(1)}, s16[496,128]{1,0:T(8,128)(2,1)S(1)}, u32[]{:S(2)}, u32[]{:S(2)}) collective-permute-start(s16[496,128]{1,0:T(8,128)(2,1)S(1)} %get-tuple-element.37), channel_id=1, source_target_pairs={{0,12},{4,0},{8,4},{12,8},{1,13},{5,1},{9,5},{13,9},{2,14},{6,2},{... | collective-permute-start | bytes 380936 | tf_op jit(solution)/shard_map/ppermute | solution.py:494
  28.3 4.9 %collective-permute-start.7 = (f32[8,128]{1,0:T(8,128)S(1)}, f32[8,128]{1,0:T(8,128)S(1)}, u32[]{:S(2)}, u32[]{:S(2)}) collective-permute-start(f32[8,128]{1,0:T(8,128)S(1)} %get-tuple-element.38.refs_3_), channel_id=1, source_target_pairs={{0,8},{4,12},{8,0},{12,4},{1,9},{5,13},{9,1},{13,5},{2,10},{6,14},... | collective-permute-start | bytes 12296 | tf_op jit(solution)/shard_map/ppermute | solution.py:512
  33.2 17.5 %copy-start = (f32[16]{0:T(128)S(1)}, f32[16]{0:T(128)}, u32[]{:S(2)}) copy-start(f32[16]{0:T(128)} %param.13) | copy-start | bytes 196
  33.2 17.5 %copy-start.1 = (f32[16]{0:T(128)S(1)}, f32[16]{0:T(128)}, u32[]{:S(2)}) copy-start(f32[16]{0:T(128)} %param.15) | copy-start | bytes 196
  33.2 3.9 %collective-permute-start.8 = (f32[2,24,128]{2,1,0:T(8,128)S(1)}, f32[2,24,128]{2,1,0:T(8,128)S(1)}, u32[]{:S(2)}, u32[]{:S(2)}) collective-permute-start(f32[2,24,128]{2,1,0:T(8,128)S(1)} %shard_map.124.refs_4_.yp_ref), channel_id=1, source_target_pairs={{0,2},{2,0},{1,3},{3,1},{4,6},{6,4},{5,7},{7,5},{8,10},{10,8},{9,1... | collective-permute-start | bytes 73736 | tf_op jit(solution)/shard_map/ppermute | solution.py:476
  37.3 1.6 %collective-permute-start.9 = (f32[2,272,128]{2,1,0:T(8,128)S(1)}, f32[2,272,128]{2,1,0:T(8,128)S(1)}, u32[]{:S(2)}, u32[]{:S(2)}) collective-permute-start(f32[2,272,128]{2,1,0:T(8,128)S(1)} %shard_map.125), channel_id=1, source_target_pairs={{0,1},{1,0},{2,3},{3,2},{4,5},{5,4},{6,7},{7,6},{8,9},{9,8},{10,11... | collective-permute-start | bytes 835592 | tf_op jit(solution)/shard_map/ppermute | solution.py:482
  40.3 5.5 %collective-permute-start.10 = (bf16[2,16,128]{2,1,0:T(8,128)(2,1)S(1)}, bf16[2,16,128]{2,1,0:T(8,128)(2,1)S(1)}, u32[]{:S(2)}, u32[]{:S(2)}) collective-permute-start(bf16[2,16,128]{2,1,0:T(8,128)(2,1)S(1)} %shard_map.127), channel_id=1, source_target_pairs={{0,2},{2,0},{1,3},{3,1},{4,6},{6,4},{5,7},{7,5},{8,10},{10,8},{9,1... | collective-permute-start | bytes 24584 | tf_op jit(solution)/shard_map/ppermute | solution.py:476
  45.9 5.7 %collective-permute-start.11 = (bf16[80,128]{1,0:T(8,128)(2,1)S(1)}, bf16[80,128]{1,0:T(8,128)(2,1)S(1)}, u32[]{:S(2)}, u32[]{:S(2)}) collective-permute-start(bf16[80,128]{1,0:T(8,128)(2,1)S(1)} %shard_map.128.plane_ref.refs_1_), channel_id=1, source_target_pairs={{0,4},{4,8},{8,12},{12,0},{1,5},{5,9},{9,13},{13,1},{2,6},{6,10},{... | collective-permute-start | bytes 61448 | tf_op jit(solution)/shard_map/ppermute | solution.py:750
  48.0 4.2 %collective-permute-start.12 = (bf16[80,128]{1,0:T(8,128)(2,1)S(1)}, bf16[80,128]{1,0:T(8,128)(2,1)S(1)}, u32[]{:S(2)}, u32[]{:S(2)}) collective-permute-start(bf16[80,128]{1,0:T(8,128)(2,1)S(1)} %shard_map.128.plane_ref.refs_1_), channel_id=1, source_target_pairs={{0,12},{4,0},{8,4},{12,8},{1,13},{5,1},{9,5},{13,9},{2,14},{6,2},{... | collective-permute-start | bytes 61448 | tf_op jit(solution)/shard_map/ppermute | solution.py:750
  49.8 4.7 %collective-permute-start.13 = (bf16[80,128]{1,0:T(8,128)(2,1)S(1)}, bf16[80,128]{1,0:T(8,128)(2,1)S(1)}, u32[]{:S(2)}, u32[]{:S(2)}) collective-permute-start(bf16[80,128]{1,0:T(8,128)(2,1)S(1)} %shard_map.128.plane_ref.refs_1_), channel_id=1, source_target_pairs={{0,8},{4,12},{8,0},{12,4},{1,9},{5,13},{9,1},{13,5},{2,10},{6,14},... | collective-permute-start | bytes 61448 | tf_op jit(solution)/shard_map/ppermute | solution.py:750
  50.6 3.9 %collective-permute-start.14 = (bf16[80,128]{1,0:T(8,128)(2,1)S(1)}, bf16[80,128]{1,0:T(8,128)(2,1)S(1)}, u32[]{:S(2)}, u32[]{:S(2)}) collective-permute-start(bf16[80,128]{1,0:T(8,128)(2,1)S(1)} %shard_map.128.plane_ref.refs_1_), channel_id=1, source_target_pairs={{0,1},{1,0},{2,3},{3,2},{4,5},{5,4},{6,7},{7,6},{8,9},{9,8},{10,11... | collective-permute-start | bytes 61448 | tf_op jit(solution)/shard_map/ppermute | solution.py:482
  51.7 2.8 %collective-permute-start.15 = (bf16[80,128]{1,0:T(8,128)(2,1)S(1)}, bf16[80,128]{1,0:T(8,128)(2,1)S(1)}, u32[]{:S(2)}, u32[]{:S(2)}) collective-permute-start(bf16[80,128]{1,0:T(8,128)(2,1)S(1)} %collective-permute-done.11.refs_2_), channel_id=1, source_target_pairs={{0,1},{1,0},{2,3},{3,2},{4,5},{5,4},{6,7},{7,6},{8,9},{9,8},{10,11... | collective-permute-start | bytes 61448 | tf_op jit(solution)/shard_map/ppermute | solution.py:482
  52.2 2.4 %collective-permute-start.16 = (bf16[80,128]{1,0:T(8,128)(2,1)S(1)}, bf16[80,128]{1,0:T(8,128)(2,1)S(1)}, u32[]{:S(2)}, u32[]{:S(2)}) collective-permute-start(bf16[80,128]{1,0:T(8,128)(2,1)S(1)} %collective-permute-done.12.refs_3_), channel_id=1, source_target_pairs={{0,1},{1,0},{2,3},{3,2},{4,5},{5,4},{6,7},{7,6},{8,9},{9,8},{10,11... | collective-permute-start | bytes 61448 | tf_op jit(solution)/shard_map/ppermute | solution.py:482
  54.5 1.2 %collective-permute-start.17 = (bf16[80,128]{1,0:T(8,128)(2,1)S(1)}, bf16[80,128]{1,0:T(8,128)(2,1)S(1)}, u32[]{:S(2)}, u32[]{:S(2)}) collective-permute-start(bf16[80,128]{1,0:T(8,128)(2,1)S(1)} %collective-permute-done.13.refs_4_), channel_id=1, source_target_pairs={{0,1},{1,0},{2,3},{3,2},{4,5},{5,4},{6,7},{7,6},{8,9},{9,8},{10,11... | collective-permute-start | bytes 61448 | tf_op jit(solution)/shard_map/ppermute | solution.py:482

commit v8 on v7

--- a/solution.py
+++ b/solution.py
@@ -80,7 +80,7 @@
                             jnp.zeros((6, top.shape[1]), F32)])
 
 
-def first_kernel(c_hbm, d_hbm, l_hbm, f_ref, amp_ref, lo_ref, hi_ref, sum_ref, d_ref, l_ref, sems):
+def first_kernel(c_hbm, d_hbm, l_hbm, f_ref, amp_ref, lo_ref, hi_ref, sum_ref, le_ref, d_ref, l_ref, sems):
     nx, ny, nz = f_ref.shape
     order = [0, nx - 1] + list(range(1, nx - 1))
     copies = []
@@ -94,6 +94,8 @@
     for k, x in enumerate(order):
         for c in copies[k]:
             c.wait()
+        le_ref[x, 0:16, :] = l_ref[x, 0:16, :]
+        le_ref[x, 16:32, :] = l_ref[x, ny - 16:ny, :]
         for r, n in chunks(0, ny, 48):
             f = f_ref[x, r:r + n, :]
             a = by_label(l_ref[x, r:r + n, :], ROOTS) * (1.0 - d_ref[x, r:r + n, :])
@@ -193,7 +195,7 @@
     return [v for a, b in spans for v in chunks(OFF + a - extra, OFF + b + extra, size)]
 
 
-def fill(code, f_ref, lo_ref, hi_ref, yr_ref, zr_ref, pad_ref, ze_ref, spans):
+def fill(code, f_ref, lo_ref, hi_ref, yr_ref, zr_ref, pad_ref, ec_ref, spans):
     nx, ny, nz = f_ref.shape
     end = OFF + ny
     wide = [v for a, b in spans for v in chunks(max(a - 16, 0), min(b + 16, ny), 48)]
@@ -210,10 +212,17 @@
         for side, near, far in ((1, OFF - 1, OFF - 2), (0, end, end + 1)):
             pad_ref[x + 2, near:near + 1, :] = yr_ref[side, 2 * x:2 * x + 1, :]
             pad_ref[x + 2, far:far + 1, :] = yr_ref[side, 2 * x + 1:2 * x + 2, :]
-    for p in range(nx + 2):
-        for r, n in spread(spans, 8, 32):
-            e = zr_ref[p // 4, r:r + n, :]
-            ze_ref[p, r:r + n, :] = pltpu.roll(e, nz - 32 * (p % 4), 1) if p % 4 else e
+    lane = lax.broadcasted_iota(jnp.int32, (1, nz), 1)
+    for r, n in spread(spans, 8, 32):
+        ec_ref[r:r + n, :] = regroup(zr_ref, r, n, lane, 1)
+
+
+def regroup(z_ref, r, n, lane, first):
+    here = z_ref[0, r:r + n, :]
+    if not first:
+        return here
+    next_four = z_ref[1, r:r + n, :]
+    return pltpu.roll(jnp.where(group(lane, 0, 128, -8, 32 * first), next_four, here), 128 - 32 * first, 1)
 
 
 def weighted_mean(yp_ref, yr_ref, zr_ref, ride_y, ride_z):
@@ -227,8 +236,8 @@
 
 def worn(a, m, f, mean):
     e = f - mean
-    energy = 0.5 * STRAIN_COUPLING * m * e * e
-    return a * (1.0 - DAMAGE_RATE * jnp.maximum(energy - ENERGY_CRITICAL, 0.0))
+    loss = DAMAGE_RATE * 0.5 * STRAIN_COUPLING * (m * (e * e)) - DAMAGE_RATE * ENERGY_CRITICAL
+    return a * (1.0 - jnp.maximum(loss, 0.0))
 
 
 class Geometry:
@@ -244,41 +253,42 @@
     def after(self, own, other):
         return pltpu.roll(jnp.where(self.first, other, own), self.nz - 1, 1)
 
+    def unpack(self, packed, j):
+        return pltpu.roll(packed, self.nz - 32 * j, 1) if j else packed
+
 
 def chem_of(f, m, around, mean):
-    well = 2.0 * WELL_HEIGHT * f * (1.0 - f) * (1.0 - 2.0 * f)
-    return well + 6.0 * f - around + STRAIN_COUPLING * m * (f - mean)
-
-
-def chemistry(g, pad_ref, mob_ref, mobe_ref, ze_ref, chem_ref, cheme_ref, mean, spans):
+    w = 2.0 * WELL_HEIGHT
+    return ((2.0 * w * f - 3.0 * w) * f + (w + 6.0)) * f - around + STRAIN_COUPLING * (m * (f - mean))
+
+
+def chemistry(g, pad_ref, mob_ref, mobe_ref, zr_ref, zo_ref, ec_ref, chem_ref, cheme_ref, mean, spans):
     nx = g.nx
     for p in range(nx + 2):
-        inside = 1 <= p <= nx
-        rows = spread(spans, 8, 32) if inside else spread(spans, 0, 48)
-        for r, n in rows:
+        for r, n in spread(spans, 8, 32) if 1 <= p <= nx else spread(spans, 0, 48):
             f = pad_ref[p + 1, r:r + n, :]
-            e = ze_ref[p, r:r + n, :]
+            e = g.unpack(zr_ref[p // 4, r:r + n, :], p % 4)
             around = (pad_ref[p, r:r + n, :] + pad_ref[p + 2, r:r + n, :]
                       + pad_ref[p + 1, r - 1:r - 1 + n, :] + pad_ref[p + 1, r + 1:r + 1 + n, :]
                       + g.before(f, e) + g.after(f, e))
             chem_ref[p, r:r + n, :] = chem_of(f, mob_ref[p, r:r + n, :], around, mean)
-        if inside:
-            for r, n in spread(spans, 0, 48):
-                f = pad_ref[p + 1, r:r + n, :]
-                e = ze_ref[p, r:r + n, :]
-                around = (ze_ref[p - 1, r:r + n, :] + ze_ref[p + 1, r:r + n, :]
-                          + ze_ref[p, r - 1:r - 1 + n, :] + ze_ref[p, r + 1:r + 1 + n, :]
-                          + g.before(e, f) + g.after(e, f))
-                cheme_ref[p - 1, r - OFF:r - OFF + n, :] = chem_of(
-                    e, mobe_ref[p - 1, r - OFF:r - OFF + n, :], around, mean)
+    firsts, lasts = g.lane % 32 == 0, g.lane % 32 == 31
+    for r, n in spread(spans, 0, 48):
+        e = ec_ref[r:r + n, :]
+        own = regroup(zo_ref, r, n, g.lane, 1)
+        around = (regroup(zr_ref, r, n, g.lane, 0) + regroup(zr_ref, r, n, g.lane, 2)
+                  + ec_ref[r - 1:r - 1 + n, :] + ec_ref[r + 1:r + 1 + n, :]
+                  + pltpu.roll(jnp.where(lasts, own, e), 1, 1)
+                  + pltpu.roll(jnp.where(firsts, own, e), g.nz - 1, 1))
+        cheme_ref[r - OFF:r - OFF + n, :] = chem_of(e, mobe_ref[r - OFF:r - OFF + n, :], around, mean)
 
 
 def flux_of(g, x, r, n, mob_ref, mobe_ref, chem_ref, cheme_ref):
     p = x + 1
     m = mob_ref[p, r:r + n, :]
     q = chem_ref[p, r:r + n, :]
-    me = mobe_ref[x, r - OFF:r - OFF + n, :]
-    qe = cheme_ref[x, r - OFF:r - OFF + n, :]
+    me = g.unpack(mobe_ref[r - OFF:r - OFF + n, :], x)
+    qe = g.unpack(cheme_ref[r - OFF:r - OFF + n, :], x)
     total = None
     for nm, nq in (
         (mob_ref[p - 1, r:r + n, :], chem_ref[p - 1, r:r + n, :]),
@@ -293,22 +303,15 @@
     return m, 0.5 * total
 
 
-def pack_edges(values, lane, nz):
-    out = values[0]
-    for x, v in enumerate(values[1:], 1):
-        out = jnp.where(group(lane, x, nz, -1, 2), pltpu.roll(v, 32 * x, 1), out)
-    return out
-
-
 def step_a(ride_y, ride_z):
-    def kernel(f_ref, amp_ref, lo_ref, hi_ref, yr_ref, zr_ref, yp_ref,
+    def kernel(f_ref, amp_ref, lo_ref, hi_ref, yr_ref, zr_ref, zo_ref, yp_ref,
                f2_ref, a2_ref, ae2_ref, lo_out, hi_out, sum_ref,
-               pad_ref, ze_ref, mob_ref, mobe_ref, chem_ref, cheme_ref):
+               pad_ref, ec_ref, mob_ref, mobe_ref, chem_ref, cheme_ref):
         nx, ny, nz = f2_ref.shape
         end = OFF + ny
         g = Geometry(nx, ny, nz)
         mean = weighted_mean(yp_ref, yr_ref, zr_ref, ride_y, ride_z)
-        fill(A_CODE, f_ref, lo_ref, hi_ref, yr_ref, zr_ref, pad_ref, ze_ref, [(0, ny)])
+        fill(A_CODE, f_ref, lo_ref, hi_ref, yr_ref, zr_ref, pad_ref, ec_ref, [(0, ny)])
 
         def wear(p, r, n, a):
             m = a * a
@@ -318,19 +321,17 @@
         for r, n in chunks(0, ny, 48):
             wear(0, OFF + r, n, from_code(lo_ref[2 * ny + r:2 * ny + r + n, :], A_CODE))
             wear(nx + 1, OFF + r, n, from_code(hi_ref[2 * ny + r:2 * ny + r + n, :], A_CODE))
-            edges = []
             for x in range(nx):
                 wear(x + 1, OFF + r, n, amp_ref[x, r:r + n, :])
-                p = x + 1
-                a = pltpu.roll(zr_ref[p // 4, OFF + r:OFF + r + n, :], nz - 32 * (p % 4) - 16, 1)
-                m = a * a
-                mobe_ref[x, r:r + n, :] = m
-                edges.append(worn(a, m, ze_ref[p, OFF + r:OFF + r + n, :], mean))
-            ae2_ref[r:r + n, :] = pack_edges(edges, g.lane, nz)
+            e = ec_ref[OFF + r:OFF + r + n, :]
+            a = pltpu.roll(e, nz - 16, 1)
+            m = a * a
+            mobe_ref[r:r + n, :] = m
+            ae2_ref[r:r + n, :] = worn(a, m, e, mean)
         for x in range(nx):
             wear(x + 1, OFF - 1, 1, yr_ref[1, 10 + x:11 + x, :])
             wear(x + 1, end, 1, yr_ref[0, 10 + x:11 + x, :])
-        chemistry(g, pad_ref, mob_ref, mobe_ref, ze_ref, chem_ref, cheme_ref, mean, [(0, ny)])
+        chemistry(g, pad_ref, mob_ref, mobe_ref, zr_ref, zo_ref, ec_ref, chem_ref, cheme_ref, mean, [(0, ny)])
         top = jnp.zeros((8, nz), F32)
         bottom = jnp.zeros((8, nz), F32)
         for x in range(nx):
@@ -356,24 +357,22 @@
 
 
 def potentials_b(g, mean, a2_ref, ae2_ref, others, scratch, spans):
-    f_ref, lo_ref, hi_ref, yr_ref, zr_ref = others
-    pad_ref, ze_ref, mob_ref, mobe_ref, chem_ref, cheme_ref = scratch
-    nx, nz = g.nx, g.nz
-    fill(B_CODE, f_ref, lo_ref, hi_ref, yr_ref, zr_ref, pad_ref, ze_ref, spans)
+    f_ref, lo_ref, hi_ref, yr_ref, zr_ref, zo_ref = others
+    pad_ref, ec_ref, mob_ref, mobe_ref, chem_ref, cheme_ref = scratch
+    nx = g.nx
+    fill(B_CODE, f_ref, lo_ref, hi_ref, yr_ref, zr_ref, pad_ref, ec_ref, spans)
     for p in range(nx + 2):
         for r, n in spread(spans, 8, 32) if 1 <= p <= nx else spread(spans, 0, 48):
             a = a2_ref[p, r:r + n, :]
             mob_ref[p, r:r + n, :] = a * a
     for r, n in spread(spans, 0, 48):
         a = ae2_ref[r - OFF:r - OFF + n, :]
-        a = a * a
-        for x in range(nx):
-            mobe_ref[x, r - OFF:r - OFF + n, :] = pltpu.roll(a, nz - 32 * x, 1) if x else a
-    chemistry(g, pad_ref, mob_ref, mobe_ref, ze_ref, chem_ref, cheme_ref, mean, spans)
+        mobe_ref[r - OFF:r - OFF + n, :] = a * a
+    chemistry(g, pad_ref, mob_ref, mobe_ref, zr_ref, zo_ref, ec_ref, chem_ref, cheme_ref, mean, spans)
 
 
 def finish_b(g, mean, x, r, n, labels, a2_ref, scratch):
-    pad_ref, ze_ref, mob_ref, mobe_ref, chem_ref, cheme_ref = scratch
+    pad_ref, ec_ref, mob_ref, mobe_ref, chem_ref, cheme_ref = scratch
     m, flux = flux_of(g, x, r, n, mob_ref, mobe_ref, chem_ref, cheme_ref)
     f0 = pad_ref[x + 2, r:r + n, :]
     f = f0 + TIME_STEP * flux
@@ -395,19 +394,13 @@
 
 
 def edge_b(ride_y, ride_z):
-    def kernel(f_ref, a2_ref, ae2_ref, lo_ref, hi_ref, yr_ref, zr_ref, yp_ref, l_hbm, edge_ref, *rest):
-        *scratch, pool_scr, l_ref, l_sem = rest
+    def kernel(f_ref, a2_ref, ae2_ref, lo_ref, hi_ref, yr_ref, zr_ref, zo_ref, yp_ref, l_ref, edge_ref, *rest):
+        *scratch, pool_scr = rest
         nx, ny, nz = f_ref.shape
         spans = [(0, 16), (ny - 16, ny)]
-        loads = [pltpu.make_async_copy(l_hbm.at[:, a:b, :], l_ref.at[:, 16 * k:16 * k + 16, :], l_sem.at[k])
-                 for k, (a, b) in enumerate(spans)]
-        for c in loads:
-            c.start()
         g = Geometry(nx, ny, nz)
         mean = weighted_mean(yp_ref, yr_ref, zr_ref, ride_y, ride_z)
-        potentials_b(g, mean, a2_ref, ae2_ref, (f_ref, lo_ref, hi_ref, yr_ref, zr_ref), scratch, spans)
-        for c in loads:
-            c.wait()
+        potentials_b(g, mean, a2_ref, ae2_ref, (f_ref, lo_ref, hi_ref, yr_ref, zr_ref, zo_ref), scratch, spans)
         for k, (a, b) in enumerate(spans):
             s = slice(16 * k, 16 * k + 16)
             pooled = [None] * 4
@@ -424,7 +417,7 @@
 
 
 def step_b(ride_y, ride_z):
-    def kernel(f_ref, a2_ref, ae2_ref, lo_ref, hi_ref, yr_ref, zr_ref, yp_ref, l_hbm,
+    def kernel(f_ref, a2_ref, ae2_ref, lo_ref, hi_ref, yr_ref, zr_ref, zo_ref, yp_ref, l_hbm,
                f3_hbm, dmg_hbm, flux_hbm, pool_ref, *rest):
         *scratch, pool_scr, l_ref, f3_ref, dmg_ref, flux_ref, l_sem, sems = rest
         nx, ny, nz = f_ref.shape
@@ -432,7 +425,7 @@
         labels_in.start()
         g = Geometry(nx, ny, nz)
         mean = weighted_mean(yp_ref, yr_ref, zr_ref, ride_y, ride_z)
-        potentials_b(g, mean, a2_ref, ae2_ref, (f_ref, lo_ref, hi_ref, yr_ref, zr_ref), scratch, [(0, ny)])
+        potentials_b(g, mean, a2_ref, ae2_ref, (f_ref, lo_ref, hi_ref, yr_ref, zr_ref, zo_ref), scratch, [(0, ny)])
         labels_in.wait()
         copies = []
         for k, (r, n) in enumerate(chunks(OFF, OFF + ny, 48)):
@@ -503,9 +496,9 @@
     ride_y = lax.axis_size("gy") == 2
     ride_z = lax.axis_size("gz") == 2
     packed = (-(-(nx + 2) // 4), rows, nz)
-    assert nz == 128
-    scratch = [pltpu.VMEM((nx + 4, rows, nz), F32), pltpu.VMEM(padded, F32), pltpu.VMEM(padded, F32),
-               pltpu.VMEM(block, F32), pltpu.VMEM(padded, F32), pltpu.VMEM(block, F32)]
+    assert nz == 128 and nx == 4
+    scratch = [pltpu.VMEM((nx + 4, rows, nz), F32), pltpu.VMEM((rows, nz), F32), pltpu.VMEM(padded, F32),
+               pltpu.VMEM((ny, nz), F32), pltpu.VMEM(padded, F32), pltpu.VMEM((ny, nz), F32)]
 
     def start(sums):
         if ride_x:
@@ -519,9 +512,10 @@
     concentration, damage, labels = (
         pltpu.with_memory_space_constraint(v, pltpu.HBM) for v in (concentration, damage, labels))
     tall = 3 * ny + 16
-    f, amp, lo, hi, sums = call(
+    f, amp, lo, hi, sums, edge_labels = call(
         first_kernel,
-        [(block, F32), (block, F32), ((tall, nz), I16), ((tall, nz), I16), ((8, nz), F32)],
+        [(block, F32), (block, F32), ((tall, nz), I16), ((tall, nz), I16), ((8, nz), F32),
+         ((nx, 32, nz), jnp.int32)],
         concentration, damage, labels,
         in_specs=[HBM] * 3,
         scratch=[pltpu.VMEM(block, F32), pltpu.VMEM(block, jnp.int32), pltpu.SemaphoreType.DMA((3, nx))])
@@ -536,7 +530,7 @@
     f, a2, ae2, lo, hi, sums = call(
         step_a(ride_y, ride_z),
         [(block, F32), (padded, F32), ((ny, nz), F32), ((tall, nz), I16), ((tall, nz), I16), ((8, nz), F32)],
-        f, amp, lo, hi, yr, zr, ypay, scratch=scratch)
+        f, amp, lo, hi, yr, zr, zpay, ypay, scratch=scratch)
 
     sums, far = start(sums)
     lo, hi = x_sides(lo, hi)
@@ -544,15 +538,14 @@
     yr = both_sides(ypay, "gy")
     (zpay,) = call(pack_z(B_CODE, ride_y, False), [(packed, F32)], f, lo, hi, yr, ypay)
     zr = z_neighbour(zpay, "gz")
-    last = (f, a2, ae2, lo, hi, yr, zr, ypay, labels)
+    last = (f, a2, ae2, lo, hi, yr, zr, zpay, ypay)
     (edge,) = call(
-        edge_b(ride_y, ride_z), [((2, 16, nz), BF16)], *last, in_specs=[VMEM] * 8 + [HBM],
-        scratch=scratch + [
-            pltpu.VMEM((4, 32, nz), F32), pltpu.VMEM((nx, 32, nz), jnp.int32), pltpu.SemaphoreType.DMA((2,))])
+        edge_b(ride_y, ride_z), [((2, 16, nz), BF16)], *last, edge_labels,
+        scratch=scratch + [pltpu.VMEM((4, 32, nz), F32)])
     fraction, damage_field, flux_sum, pooled = call(
         step_b(ride_y, ride_z),
-        [(block, F32), (block, F32), (block, F32), ((ny // 4, nz), BF16)], *last,
-        in_specs=[VMEM] * 8 + [HBM], out_specs=[HBM] * 3 + [VMEM],
+        [(block, F32), (block, F32), (block, F32), ((ny // 4, nz), BF16)], *last, labels,
+        in_specs=[VMEM] * 9 + [HBM], out_specs=[HBM] * 3 + [VMEM],
         scratch=scratch + [
             pltpu.VMEM((4, ny, nz), F32), pltpu.VMEM(block, jnp.int32),
             pltpu.VMEM(block, F32), pltpu.VMEM(block, F32), pltpu.VMEM(block, F32),

time: 60 us -> 63.8 us (1.063)
  Pallas kernels: 14.5 us -> 18.4 us
    pallas_call x11, Pallas kernels: 14.5 us -> 18.4 us  [call(): pl.pallas_call(kernel, in_specs=in_specs or [VMEM] * len(args), out_specs...]
  transfers between devices with their start and end apart: 18 -> 18, of which waited for: 9 -> 9; matrix products, arithmetic and copies ran while one was open for 5% -> 5% of each run, Pallas kernels for 8% -> 11%
where the time goes in v8:
time: 63.8 us; the launch traced here: 63.5 us
  waiting for transfers between devices  21.2 us (33%)
  starting transfers between devices  19.4 us (30%)
  Pallas kernels  18.4 us (29%)
  local copies, waits for them, and re-layouts  2.93 us (5%)
  between operations  1.44 us (2%)
    pallas_call x11, Pallas kernels, call(): pl.pallas_call(kernel, in_specs=in_specs or [VMEM] * len(args), out_specs...  18.4 us
    ppermute x2, waiting for transfers between devices, start(): return (sums, lax.ppermute(sums, 'gx', ring('gx', 2)))  9.93 us
    ppermute x2, starting transfers between devices, x_sides(): lax.ppermute(lo, 'gx', ring('gx', -1))  5.32 us
    ppermute x3, waiting for transfers between devices, both_sides(): return lax.ppermute(pay, axis, ring(axis, 1))  4.67 us
    ppermute x3, starting transfers between devices, both_sides(): return lax.ppermute(pay, axis, ring(axis, 1))  4.62 us
    ppermute x6, waiting for transfers between devices, z_neighbour(): return lax.ppermute(pay, axis, ring(axis, 1))  4.26 us
    ppermute x3, starting transfers between devices, detector(): own = [plane] + [lax.ppermute(plane, 'gx', ring('gx', s)) for s in shifts]  4 us
    ppermute x2, starting transfers between devices, x_sides(): lax.ppermute(hi, 'gx', ring('gx', 1))  3.73 us
  transfers between devices with their start and end apart: 18, of which 9 were waited for; matrix products, arithmetic and copies ran while one was open for 5% of the time, Pallas kernels for 11%

profile of v8, /device:TPU:0, one launch (start us, length us, event | category | flops | bytes accessed | tf_op | source)
XLA Modules:
  0.0 63.5 jit_solution(17068040279905727829)
XLA Ops:
  0.6 1.6 %shard_map.120 = (f32[4,240,128]{2,1,0:T(8,128)S(1)}, f32[4,240,128]{2,1,0:T(8,128)S(1)}, s16[736,128]{1,0:T(8,128)(2,1)S(1)}, s16[736,128]{1,0:T(8,128)(2,1)S(1...) custom-call(f32[4,240,128]{2,1,0:T(8,128)} %c_hbm.1, f32[4,240,128]{2,1,0:T(8,128)} %d_hbm.1, s32[4,240,128]{2,1,0:T(8,128)} %l_hbm.3), custom_call_target="tpu_custom_call" | custom-call | tf_op jit(solution)/shard_map/pallas_call | solution.py:60
  2.3 3.1 %collective-permute-start = (s16[736,128]{1,0:T(8,128)(2,1)S(1)}, s16[736,128]{1,0:T(8,128)(2,1)S(1)}, u32[]{:S(2)}, u32[]{:S(2)}) collective-permute-start(s16[736,128]{1,0:T(8,128)(2,1)S(1)} %get-tuple-element.31), channel_id=1, source_target_pairs={{0,4},{4,8},{8,12},{12,0},{1,5},{5,9},{9,13},{13,1},{2,6},{6,10},{... | collective-permute-start | bytes 565256 | tf_op jit(solution)/shard_map/ppermute | solution.py:487
  5.3 2.1 %collective-permute-start.1 = (s16[736,128]{1,0:T(8,128)(2,1)S(1)}, s16[736,128]{1,0:T(8,128)(2,1)S(1)}, u32[]{:S(2)}, u32[]{:S(2)}) collective-permute-start(s16[736,128]{1,0:T(8,128)(2,1)S(1)} %get-tuple-element.32), channel_id=1, source_target_pairs={{0,12},{4,0},{8,4},{12,8},{1,13},{5,1},{9,5},{13,9},{2,14},{6,2},{... | collective-permute-start | bytes 565256 | tf_op jit(solution)/shard_map/ppermute | solution.py:487
  7.4 0.9 %collective-permute-start.2 = (f32[8,128]{1,0:T(8,128)S(1)}, f32[8,128]{1,0:T(8,128)S(1)}, u32[]{:S(2)}, u32[]{:S(2)}) collective-permute-start(f32[8,128]{1,0:T(8,128)S(1)} %get-tuple-element.33.refs_4_), channel_id=1, source_target_pairs={{0,8},{4,12},{8,0},{12,4},{1,9},{5,13},{9,1},{13,5},{2,10},{6,14},... | collective-permute-start | bytes 12296 | tf_op jit(solution)/shard_map/ppermute | solution.py:505
  8.4 0.8 %copy.16 = bf16[27,4,16]{2,1,0:T(4,128)(2,1)S(1)} copy(bf16[27,4,16]{0,1,2:T(4,128)(2,1)} %bitcast.27) | data formatting | bytes 6912 | tf_op jit(solution)/shard_map/transpose | solution.py:628
  9.2 1.0 %copy.17 = bf16[27,16,16]{2,1,0:T(8,128)(2,1)S(1)} copy(bf16[27,16,16]{0,1,2:T(8,128)(2,1)} %bitcast.24) | data formatting | bytes 27648 | tf_op jit(solution)/shard_map/transpose | solution.py:629
  10.2 0.8 %copy.18 = bf16[27,1,16]{2,0,1:T(8,128)(2,1)S(1)} copy(bf16[27,1,16]{0,2,1:T(8,128)(2,1)} %param.16) | data formatting | bytes 1728 | tf_op args[7]
  11.1 0.1 copy.19
  11.2 5.1 %collective-permute-done.2.refs_5_ = f32[8,128]{1,0:T(8,128)S(1)} collective-permute-done((f32[8,128]{1,0:T(8,128)S(1)}, f32[8,128]{1,0:T(8,128)S(1)}, u32[]{:S(2)}, u32[]{:S(2)}) %collective-permute-start.2) | collective-permute-done | bytes 4128 | tf_op jit(solution)/shard_map/ppermute | solution.py:505
  16.3 0.0 collective-permute-done.refs_2_.lo_ref
  16.3 0.0 collective-permute-done.1.refs_3_.hi_ref
  16.3 1.6 %collective-permute-start.3 = (f32[2,24,128]{2,1,0:T(8,128)S(1)}, f32[2,24,128]{2,1,0:T(8,128)S(1)}, u32[]{:S(2)}, u32[]{:S(2)}) collective-permute-start(f32[2,24,128]{2,1,0:T(8,128)S(1)} %shard_map.121.refs_5_.yp_ref), channel_id=1, source_target_pairs={{0,2},{2,0},{1,3},{3,1},{4,6},{6,4},{5,7},{7,5},{8,10},{10,8},{9,1... | collective-permute-start | bytes 73736 | tf_op jit(solution)/shard_map/ppermute | solution.py:469
  17.9 2.3 %collective-permute-done.3.refs_4_.yr_ref = f32[2,24,128]{2,1,0:T(8,128)S(1)} collective-permute-done((f32[2,24,128]{2,1,0:T(8,128)S(1)}, f32[2,24,128]{2,1,0:T(8,128)S(1)}, u32[]{:S(2)}, u32[]{:S(2)}) %collective-permute-start.3) | collective-permute-done | bytes 24608 | tf_op jit(solution)/shard_map/ppermute | solution.py:469
  20.2 0.3 shard_map.122.zo_ref
  20.6 0.1 collective-permute-start.4
  20.6 1.5 %collective-permute-done.4.zr_ref = f32[2,272,128]{2,1,0:T(8,128)S(1)} collective-permute-done((f32[2,272,128]{2,1,0:T(8,128)S(1)}, f32[2,272,128]{2,1,0:T(8,128)S(1)}, u32[]{:S(2)}, u32[]{:S(2)}) %collective-permute-start.4) | collective-permute-done | bytes 278560 | tf_op jit(solution)/shard_map/ppermute | solution.py:475
  22.2 4.5 %shard_map.123 = (f32[4,240,128]{2,1,0:T(8,128)S(1)}, f32[6,272,128]{2,1,0:T(8,128)S(1)}, f32[240,128]{1,0:T(8,128)S(1)}, s16[496,128]{1,0:T(8,128)(2,1)S(1)}, s...) custom-call(f32[4,240,128]{2,1,0:T(8,128)S(1)} %get-tuple-element.29.refs_0_.f_ref, ...), custom_call_target="tpu_custom_call" | custom-call | tf_op jit(solution)/shard_map/pallas_call | solution.py:60
  26.7 0.6 %collective-permute-start.5 = (s16[496,128]{1,0:T(8,128)(2,1)S(1)}, s16[496,128]{1,0:T(8,128)(2,1)S(1)}, u32[]{:S(2)}, u32[]{:S(2)}) collective-permute-start(s16[496,128]{1,0:T(8,128)(2,1)S(1)} %get-tuple-element.37), channel_id=1, source_target_pairs={{0,4},{4,8},{8,12},{12,0},{1,5},{5,9},{9,13},{13,1},{2,6},{6,10},{... | collective-permute-start | bytes 380936 | tf_op jit(solution)/shard_map/ppermute | solution.py:487
  27.3 3.2 %collective-permute-start.6 = (s16[496,128]{1,0:T(8,128)(2,1)S(1)}, s16[496,128]{1,0:T(8,128)(2,1)S(1)}, u32[]{:S(2)}, u32[]{:S(2)}) collective-permute-start(s16[496,128]{1,0:T(8,128)(2,1)S(1)} %get-tuple-element.38), channel_id=1, source_target_pairs={{0,12},{4,0},{8,4},{12,8},{1,13},{5,1},{9,5},{13,9},{2,14},{6,2},{... | collective-permute-start | bytes 380936 | tf_op jit(solution)/shard_map/ppermute | solution.py:487
  30.5 0.0 collective-permute-start.7
  30.5 4.9 %collective-permute-done.7.refs_4_ = f32[8,128]{1,0:T(8,128)S(1)} collective-permute-done((f32[8,128]{1,0:T(8,128)S(1)}, f32[8,128]{1,0:T(8,128)S(1)}, u32[]{:S(2)}, u32[]{:S(2)}) %collective-permute-start.7) | collective-permute-done | bytes 4128 | tf_op jit(solution)/shard_map/ppermute | solution.py:505
  35.4 0.0 collective-permute-done.5.refs_1_.lo_ref
  35.4 0.0 copy-start
  35.4 0.0 copy-start.1
  35.5 1.6 %collective-permute-start.8 = (f32[2,24,128]{2,1,0:T(8,128)S(1)}, f32[2,24,128]{2,1,0:T(8,128)S(1)}, u32[]{:S(2)}, u32[]{:S(2)}) collective-permute-start(f32[2,24,128]{2,1,0:T(8,128)S(1)} %shard_map.124.refs_4_.yp_ref), channel_id=1, source_target_pairs={{0,2},{2,0},{1,3},{3,1},{4,6},{6,4},{5,7},{7,5},{8,10},{10,8},{9,1... | collective-permute-start | bytes 73736 | tf_op jit(solution)/shard_map/ppermute | solution.py:469
  37.0 2.3 %collective-permute-done.8.refs_3_.yr_ref = f32[2,24,128]{2,1,0:T(8,128)S(1)} collective-permute-done((f32[2,24,128]{2,1,0:T(8,128)S(1)}, f32[2,24,128]{2,1,0:T(8,128)S(1)}, u32[]{:S(2)}, u32[]{:S(2)}) %collective-permute-start.8) | collective-permute-done | bytes 24608 | tf_op jit(solution)/shard_map/ppermute | solution.py:469
  39.3 0.2 shard_map.125.zo_ref
  39.5 0.1 collective-permute-start.9
  39.6 1.5 %collective-permute-done.9.zr_ref = f32[2,272,128]{2,1,0:T(8,128)S(1)} collective-permute-done((f32[2,272,128]{2,1,0:T(8,128)S(1)}, f32[2,272,128]{2,1,0:T(8,128)S(1)}, u32[]{:S(2)}, u32[]{:S(2)}) %collective-permute-start.9) | collective-permute-done | bytes 278560 | tf_op jit(solution)/shard_map/ppermute | solution.py:475
  41.2 0.6 shard_map.127
  41.8 1.5 %collective-permute-start.10 = (bf16[2,16,128]{2,1,0:T(8,128)(2,1)S(1)}, bf16[2,16,128]{2,1,0:T(8,128)(2,1)S(1)}, u32[]{:S(2)}, u32[]{:S(2)}) collective-permute-start(bf16[2,16,128]{2,1,0:T(8,128)(2,1)S(1)} %shard_map.127), channel_id=1, source_target_pairs={{0,2},{2,0},{1,3},{3,1},{4,6},{6,4},{5,7},{7,5},{8,10},{10,8},{9,1... | collective-permute-start | bytes 24584 | tf_op jit(solution)/shard_map/ppermute | solution.py:469
  43.3 0.1 pad_add_fusion
  43.4 6.3 %shard_map.126 = (f32[4,240,128]{2,1,0:T(8,128)}, f32[4,240,128]{2,1,0:T(8,128)}, f32[4,240,128]{2,1,0:T(8,128)}, bf16[60,128]{1,0:T(8,128)(2,1)S(1)}) custom-call(f32[4,240,128]{2,1,0:T(8,128)S(1)} %get-tuple-element.34.refs_0_.f_ref, f32[6,272,128]{2,1,0:T(8,128)S(1)} %get-tuple-element.35.a2_ref, f32[240,128]{1,0:T(8,128)S(1)} %get-tuple-element.36.ae2_ref, ...), custom_call_target="tpu_custom_call" | custom-call | tf_op jit(solution)/shard_map/pallas_call | solution.py:60
  49.7 0.0 collective-permute-done.10.yr_ref
  49.7 0.1 broadcast_in_dim.15.ids_ref.refs_0_
  49.8 2.0 %collective-permute-start.11 = (bf16[80,128]{1,0:T(8,128)(2,1)S(1)}, bf16[80,128]{1,0:T(8,128)(2,1)S(1)}, u32[]{:S(2)}, u32[]{:S(2)}) collective-permute-start(bf16[80,128]{1,0:T(8,128)(2,1)S(1)} %shard_map.128.plane_ref.refs_1_), channel_id=1, source_target_pairs={{0,4},{4,8},{8,12},{12,0},{1,5},{5,9},{9,13},{13,1},{2,6},{6,10},{... | collective-permute-start | bytes 61448 | tf_op jit(solution)/shard_map/ppermute | solution.py:743
  51.8 1.9 %collective-permute-start.12 = (bf16[80,128]{1,0:T(8,128)(2,1)S(1)}, bf16[80,128]{1,0:T(8,128)(2,1)S(1)}, u32[]{:S(2)}, u32[]{:S(2)}) collective-permute-start(bf16[80,128]{1,0:T(8,128)(2,1)S(1)} %shard_map.128.plane_ref.refs_1_), channel_id=1, source_target_pairs={{0,12},{4,0},{8,4},{12,8},{1,13},{5,1},{9,5},{13,9},{2,14},{6,2},{... | collective-permute-start | bytes 61448 | tf_op jit(solution)/shard_map/ppermute | solution.py:743
  53.7 0.1 collective-permute-start.13
  54.4 0.1 collective-permute-start.14
  54.5 0.9 %shard_map.129 = (bf16[3,768,640]{2,1,0:T(8,128)(2,1)S(1)}, bf16[3,768,128]{2,1,0:T(8,128)(2,1)S(1)}, bf16[3,640,128]{2,1,0:T(8,128)(2,1)S(1)}, f32[8,640]{1,0:T(8,128)S(1)}) custom-call(bf16[432,16]{1,0:T(8,128)(2,1)S(1)} %bitcast.19, bf16[432,16]{1,0:T(8,128)(2,1)S(1)} %bitcast.17, bf16[144,3]{1,0:T(8,128)(2,1)S(1)} %bitcast.21, f32[1,16]{1,0:T(1,128)S(1)} %bitcast.22, ...), custom_call_target="tpu_custom_call" | custom-call | tf_op jit(solution)/shard_map/pallas_call | solution.py:60
  55.4 0.1 collective-permute-done.11.refs_2_
  55.5 0.5 collective-permute-start.15
  56.0 0.0 collective-permute-done.12.refs_3_
  56.0 0.1 collective-permute-start.16
  56.1 2.3 %collective-permute-done.13.refs_4_ = bf16[80,128]{1,0:T(8,128)(2,1)S(1)} collective-permute-done((bf16[80,128]{1,0:T(8,128)(2,1)S(1)}, bf16[80,128]{1,0:T(8,128)(2,1)S(1)}, u32[]{:S(2)}, u32[]{:S(2)}) %collective-permute-start.13) | collective-permute-done | bytes 20512 | tf_op jit(solution)/shard_map/ppermute | solution.py:743
  58.4 0.0 collective-permute-done.16.refs_7_
  58.4 1.2 %collective-permute-done.17.refs_8_ = bf16[80,128]{1,0:T(8,128)(2,1)S(1)} collective-permute-done((bf16[80,128]{1,0:T(8,128)(2,1)S(1)}, bf16[80,128]{1,0:T(8,128)(2,1)S(1)}, u32[]{:S(2)}, u32[]{:S(2)}) %collective-permute-start.17) | collective-permute-done | bytes 20512 | tf_op jit(solution)/shard_map/ppermute | solution.py:475
  59.5 3.9 %shard_map.130 = f32[1,32,60]{2,1,0:T(8,128)} custom-call(s32[3,128]{1,0:T(4,128)S(1)} %broadcast_in_dim.15.ids_ref.refs_0_, bf16[80,128]{1,0:T(8,128)(2,1)S(1)} %shard_map.128.plane_ref.refs_1_, bf16[80,128]{1,0:T(8,128)(2,1)S(1)} %collective-permute-done.11.refs_2_, bf16[80,128]{1,0:T(8,128)(2,1)S(1)} %collective-permute-done.12.refs_3_, ...), custom_call_target="tpu_custom_call" | custom-call | tf_op jit(solution)/shard_map/pallas_call | solution.py:60
  (11 shorter events, 0.1 us)
Async XLA Ops:
  2.3 14.0 %collective-permute-start = (s16[736,128]{1,0:T(8,128)(2,1)S(1)}, s16[736,128]{1,0:T(8,128)(2,1)S(1)}, u32[]{:S(2)}, u32[]{:S(2)}) collective-permute-start(s16[736,128]{1,0:T(8,128)(2,1)S(1)} %get-tuple-element.31), channel_id=1, source_target_pairs={{0,4},{4,8},{8,12},{12,0},{1,5},{5,9},{9,13},{13,1},{2,6},{6,10},{... | collective-permute-start | bytes 565256 | tf_op jit(solution)/shard_map/ppermute | solution.py:487
  5.3 10.9 %collective-permute-start.1 = (s16[736,128]{1,0:T(8,128)(2,1)S(1)}, s16[736,128]{1,0:T(8,128)(2,1)S(1)}, u32[]{:S(2)}, u32[]{:S(2)}) collective-permute-start(s16[736,128]{1,0:T(8,128)(2,1)S(1)} %get-tuple-element.32), channel_id=1, source_target_pairs={{0,12},{4,0},{8,4},{12,8},{1,13},{5,1},{9,5},{13,9},{2,14},{6,2},{... | collective-permute-start | bytes 565256 | tf_op jit(solution)/shard_map/ppermute | solution.py:487
  7.4 8.8 %collective-permute-start.2 = (f32[8,128]{1,0:T(8,128)S(1)}, f32[8,128]{1,0:T(8,128)S(1)}, u32[]{:S(2)}, u32[]{:S(2)}) collective-permute-start(f32[8,128]{1,0:T(8,128)S(1)} %get-tuple-element.33.refs_4_), channel_id=1, source_target_pairs={{0,8},{4,12},{8,0},{12,4},{1,9},{5,13},{9,1},{13,5},{2,10},{6,14},... | collective-permute-start | bytes 12296 | tf_op jit(solution)/shard_map/ppermute | solution.py:505
  16.3 3.9 %collective-permute-start.3 = (f32[2,24,128]{2,1,0:T(8,128)S(1)}, f32[2,24,128]{2,1,0:T(8,128)S(1)}, u32[]{:S(2)}, u32[]{:S(2)}) collective-permute-start(f32[2,24,128]{2,1,0:T(8,128)S(1)} %shard_map.121.refs_5_.yp_ref), channel_id=1, source_target_pairs={{0,2},{2,0},{1,3},{3,1},{4,6},{6,4},{5,7},{7,5},{8,10},{10,8},{9,1... | collective-permute-start | bytes 73736 | tf_op jit(solution)/shard_map/ppermute | solution.py:469
  20.6 1.6 %collective-permute-start.4 = (f32[2,272,128]{2,1,0:T(8,128)S(1)}, f32[2,272,128]{2,1,0:T(8,128)S(1)}, u32[]{:S(2)}, u32[]{:S(2)}) collective-permute-start(f32[2,272,128]{2,1,0:T(8,128)S(1)} %shard_map.122.zo_ref), channel_id=1, source_target_pairs={{0,1},{1,0},{2,3},{3,2},{4,5},{5,4},{6,7},{7,6},{8,9},{9,8},{10,11... | collective-permute-start | bytes 835592 | tf_op jit(solution)/shard_map/ppermute | solution.py:475
  26.7 8.7 %collective-permute-start.5 = (s16[496,128]{1,0:T(8,128)(2,1)S(1)}, s16[496,128]{1,0:T(8,128)(2,1)S(1)}, u32[]{:S(2)}, u32[]{:S(2)}) collective-permute-start(s16[496,128]{1,0:T(8,128)(2,1)S(1)} %get-tuple-element.37), channel_id=1, source_target_pairs={{0,4},{4,8},{8,12},{12,0},{1,5},{5,9},{9,13},{13,1},{2,6},{6,10},{... | collective-permute-start | bytes 380936 | tf_op jit(solution)/shard_map/ppermute | solution.py:487
  27.3 8.1 %collective-permute-start.6 = (s16[496,128]{1,0:T(8,128)(2,1)S(1)}, s16[496,128]{1,0:T(8,128)(2,1)S(1)}, u32[]{:S(2)}, u32[]{:S(2)}) collective-permute-start(s16[496,128]{1,0:T(8,128)(2,1)S(1)} %get-tuple-element.38), channel_id=1, source_target_pairs={{0,12},{4,0},{8,4},{12,8},{1,13},{5,1},{9,5},{13,9},{2,14},{6,2},{... | collective-permute-start | bytes 380936 | tf_op jit(solution)/shard_map/ppermute | solution.py:487
  30.5 4.9 %collective-permute-start.7 = (f32[8,128]{1,0:T(8,128)S(1)}, f32[8,128]{1,0:T(8,128)S(1)}, u32[]{:S(2)}, u32[]{:S(2)}) collective-permute-start(f32[8,128]{1,0:T(8,128)S(1)} %get-tuple-element.39.refs_3_), channel_id=1, source_target_pairs={{0,8},{4,12},{8,0},{12,4},{1,9},{5,13},{9,1},{13,5},{2,10},{6,14},... | collective-permute-start | bytes 12296 | tf_op jit(solution)/shard_map/ppermute | solution.py:505
  35.4 19.1 %copy-start = (f32[16]{0:T(128)S(1)}, f32[16]{0:T(128)}, u32[]{:S(2)}) copy-start(f32[16]{0:T(128)} %param.13) | copy-start | bytes 196
  35.4 19.1 %copy-start.1 = (f32[16]{0:T(128)S(1)}, f32[16]{0:T(128)}, u32[]{:S(2)}) copy-start(f32[16]{0:T(128)} %param.15) | copy-start | bytes 196
  35.5 3.9 %collective-permute-start.8 = (f32[2,24,128]{2,1,0:T(8,128)S(1)}, f32[2,24,128]{2,1,0:T(8,128)S(1)}, u32[]{:S(2)}, u32[]{:S(2)}) collective-permute-start(f32[2,24,128]{2,1,0:T(8,128)S(1)} %shard_map.124.refs_4_.yp_ref), channel_id=1, source_target_pairs={{0,2},{2,0},{1,3},{3,1},{4,6},{6,4},{5,7},{7,5},{8,10},{10,8},{9,1... | collective-permute-start | bytes 73736 | tf_op jit(solution)/shard_map/ppermute | solution.py:469
  39.5 1.6 %collective-permute-start.9 = (f32[2,272,128]{2,1,0:T(8,128)S(1)}, f32[2,272,128]{2,1,0:T(8,128)S(1)}, u32[]{:S(2)}, u32[]{:S(2)}) collective-permute-start(f32[2,272,128]{2,1,0:T(8,128)S(1)} %shard_map.125.zo_ref), channel_id=1, source_target_pairs={{0,1},{1,0},{2,3},{3,2},{4,5},{5,4},{6,7},{7,6},{8,9},{9,8},{10,11... | collective-permute-start | bytes 835592 | tf_op jit(solution)/shard_map/ppermute | solution.py:475
  41.8 7.9 %collective-permute-start.10 = (bf16[2,16,128]{2,1,0:T(8,128)(2,1)S(1)}, bf16[2,16,128]{2,1,0:T(8,128)(2,1)S(1)}, u32[]{:S(2)}, u32[]{:S(2)}) collective-permute-start(bf16[2,16,128]{2,1,0:T(8,128)(2,1)S(1)} %shard_map.127), channel_id=1, source_target_pairs={{0,2},{2,0},{1,3},{3,1},{4,6},{6,4},{5,7},{7,5},{8,10},{10,8},{9,1... | collective-permute-start | bytes 24584 | tf_op jit(solution)/shard_map/ppermute | solution.py:469
  49.8 5.7 %collective-permute-start.11 = (bf16[80,128]{1,0:T(8,128)(2,1)S(1)}, bf16[80,128]{1,0:T(8,128)(2,1)S(1)}, u32[]{:S(2)}, u32[]{:S(2)}) collective-permute-start(bf16[80,128]{1,0:T(8,128)(2,1)S(1)} %shard_map.128.plane_ref.refs_1_), channel_id=1, source_target_pairs={{0,4},{4,8},{8,12},{12,0},{1,5},{5,9},{9,13},{13,1},{2,6},{6,10},{... | collective-permute-start | bytes 61448 | tf_op jit(solution)/shard_map/ppermute | solution.py:743
  51.8 4.2 %collective-permute-start.12 = (bf16[80,128]{1,0:T(8,128)(2,1)S(1)}, bf16[80,128]{1,0:T(8,128)(2,1)S(1)}, u32[]{:S(2)}, u32[]{:S(2)}) collective-permute-start(bf16[80,128]{1,0:T(8,128)(2,1)S(1)} %shard_map.128.plane_ref.refs_1_), channel_id=1, source_target_pairs={{0,12},{4,0},{8,4},{12,8},{1,13},{5,1},{9,5},{13,9},{2,14},{6,2},{... | collective-permute-start | bytes 61448 | tf_op jit(solution)/shard_map/ppermute | solution.py:743
  53.7 4.7 %collective-permute-start.13 = (bf16[80,128]{1,0:T(8,128)(2,1)S(1)}, bf16[80,128]{1,0:T(8,128)(2,1)S(1)}, u32[]{:S(2)}, u32[]{:S(2)}) collective-permute-start(bf16[80,128]{1,0:T(8,128)(2,1)S(1)} %shard_map.128.plane_ref.refs_1_), channel_id=1, source_target_pairs={{0,8},{4,12},{8,0},{12,4},{1,9},{5,13},{9,1},{13,5},{2,10},{6,14},... | collective-permute-start | bytes 61448 | tf_op jit(solution)/shard_map/ppermute | solution.py:743
  54.4 3.9 %collective-permute-start.14 = (bf16[80,128]{1,0:T(8,128)(2,1)S(1)}, bf16[80,128]{1,0:T(8,128)(2,1)S(1)}, u32[]{:S(2)}, u32[]{:S(2)}) collective-permute-start(bf16[80,128]{1,0:T(8,128)(2,1)S(1)} %shard_map.128.plane_ref.refs_1_), channel_id=1, source_target_pairs={{0,1},{1,0},{2,3},{3,2},{4,5},{5,4},{6,7},{7,6},{8,9},{9,8},{10,11... | collective-permute-start | bytes 61448 | tf_op jit(solution)/shard_map/ppermute | solution.py:475
  55.5 2.8 %collective-permute-start.15 = (bf16[80,128]{1,0:T(8,128)(2,1)S(1)}, bf16[80,128]{1,0:T(8,128)(2,1)S(1)}, u32[]{:S(2)}, u32[]{:S(2)}) collective-permute-start(bf16[80,128]{1,0:T(8,128)(2,1)S(1)} %collective-permute-done.11.refs_2_), channel_id=1, source_target_pairs={{0,1},{1,0},{2,3},{3,2},{4,5},{5,4},{6,7},{7,6},{8,9},{9,8},{10,11... | collective-permute-start | bytes 61448 | tf_op jit(solution)/shard_map/ppermute | solution.py:475
  56.0 2.4 %collective-permute-start.16 = (bf16[80,128]{1,0:T(8,128)(2,1)S(1)}, bf16[80,128]{1,0:T(8,128)(2,1)S(1)}, u32[]{:S(2)}, u32[]{:S(2)}) collective-permute-start(bf16[80,128]{1,0:T(8,128)(2,1)S(1)} %collective-permute-done.12.refs_3_), channel_id=1, source_target_pairs={{0,1},{1,0},{2,3},{3,2},{4,5},{5,4},{6,7},{7,6},{8,9},{9,8},{10,11... | collective-permute-start | bytes 61448 | tf_op jit(solution)/shard_map/ppermute | solution.py:475
  58.4 1.2 %collective-permute-start.17 = (bf16[80,128]{1,0:T(8,128)(2,1)S(1)}, bf16[80,128]{1,0:T(8,128)(2,1)S(1)}, u32[]{:S(2)}, u32[]{:S(2)}) collective-permute-start(bf16[80,128]{1,0:T(8,128)(2,1)S(1)} %collective-permute-done.13.refs_4_), channel_id=1, source_target_pairs={{0,1},{1,0},{2,3},{3,2},{4,5},{5,4},{6,7},{7,6},{8,9},{9,8},{10,11... | collective-permute-start | bytes 61448 | tf_op jit(solution)/shard_map/ppermute | solution.py:475

commit v9 on v8

--- a/solution.py
+++ b/solution.py
@@ -195,7 +195,7 @@
     return [v for a, b in spans for v in chunks(OFF + a - extra, OFF + b + extra, size)]
 
 
-def fill(code, f_ref, lo_ref, hi_ref, yr_ref, zr_ref, pad_ref, ec_ref, spans):
+def fill(code, f_ref, lo_ref, hi_ref, yr_ref, zr_ref, pad_ref, ze_ref, ec_ref, spans):
     nx, ny, nz = f_ref.shape
     end = OFF + ny
     wide = [v for a, b in spans for v in chunks(max(a - 16, 0), min(b + 16, ny), 48)]
@@ -215,6 +215,9 @@
     lane = lax.broadcasted_iota(jnp.int32, (1, nz), 1)
     for r, n in spread(spans, 8, 32):
         ec_ref[r:r + n, :] = regroup(zr_ref, r, n, lane, 1)
+        for p in range(nx + 2):
+            e = zr_ref[p // 4, r:r + n, :]
+            ze_ref[p, r:r + n, :] = pltpu.roll(e, nz - 32 * (p % 4), 1) if p % 4 else e
 
 
 def regroup(z_ref, r, n, lane, first):
@@ -262,12 +265,12 @@
     return ((2.0 * w * f - 3.0 * w) * f + (w + 6.0)) * f - around + STRAIN_COUPLING * (m * (f - mean))
 
 
-def chemistry(g, pad_ref, mob_ref, mobe_ref, zr_ref, zo_ref, ec_ref, chem_ref, cheme_ref, mean, spans):
+def chemistry(g, pad_ref, mob_ref, ae_ref, zr_ref, zo_ref, ze_ref, ec_ref, chem_ref, cheme_ref, mean, spans):
     nx = g.nx
     for p in range(nx + 2):
         for r, n in spread(spans, 8, 32) if 1 <= p <= nx else spread(spans, 0, 48):
             f = pad_ref[p + 1, r:r + n, :]
-            e = g.unpack(zr_ref[p // 4, r:r + n, :], p % 4)
+            e = ze_ref[p, r:r + n, :]
             around = (pad_ref[p, r:r + n, :] + pad_ref[p + 2, r:r + n, :]
                       + pad_ref[p + 1, r - 1:r - 1 + n, :] + pad_ref[p + 1, r + 1:r + 1 + n, :]
                       + g.before(f, e) + g.after(f, e))
@@ -280,15 +283,17 @@
                   + ec_ref[r - 1:r - 1 + n, :] + ec_ref[r + 1:r + 1 + n, :]
                   + pltpu.roll(jnp.where(lasts, own, e), 1, 1)
                   + pltpu.roll(jnp.where(firsts, own, e), g.nz - 1, 1))
-        cheme_ref[r - OFF:r - OFF + n, :] = chem_of(e, mobe_ref[r - OFF:r - OFF + n, :], around, mean)
+        packed = chem_of(e, ae_ref[r - OFF:r - OFF + n, :], around, mean)
+        for x in range(nx):
+            cheme_ref[x, r - OFF:r - OFF + n, :] = g.unpack(packed, x)
 
 
 def flux_of(g, x, r, n, mob_ref, mobe_ref, chem_ref, cheme_ref):
     p = x + 1
     m = mob_ref[p, r:r + n, :]
     q = chem_ref[p, r:r + n, :]
-    me = g.unpack(mobe_ref[r - OFF:r - OFF + n, :], x)
-    qe = g.unpack(cheme_ref[r - OFF:r - OFF + n, :], x)
+    me = mobe_ref[x, r - OFF:r - OFF + n, :]
+    qe = cheme_ref[x, r - OFF:r - OFF + n, :]
     total = None
     for nm, nq in (
         (mob_ref[p - 1, r:r + n, :], chem_ref[p - 1, r:r + n, :]),
@@ -306,12 +311,12 @@
 def step_a(ride_y, ride_z):
     def kernel(f_ref, amp_ref, lo_ref, hi_ref, yr_ref, zr_ref, zo_ref, yp_ref,
                f2_ref, a2_ref, ae2_ref, lo_out, hi_out, sum_ref,
-               pad_ref, ec_ref, mob_ref, mobe_ref, chem_ref, cheme_ref):
+               pad_ref, ze_ref, ec_ref, ae_ref, mob_ref, mobe_ref, chem_ref, cheme_ref):
         nx, ny, nz = f2_ref.shape
         end = OFF + ny
         g = Geometry(nx, ny, nz)
         mean = weighted_mean(yp_ref, yr_ref, zr_ref, ride_y, ride_z)
-        fill(A_CODE, f_ref, lo_ref, hi_ref, yr_ref, zr_ref, pad_ref, ec_ref, [(0, ny)])
+        fill(A_CODE, f_ref, lo_ref, hi_ref, yr_ref, zr_ref, pad_ref, ze_ref, ec_ref, [(0, ny)])
 
         def wear(p, r, n, a):
             m = a * a
@@ -326,12 +331,14 @@
             e = ec_ref[OFF + r:OFF + r + n, :]
             a = pltpu.roll(e, nz - 16, 1)
             m = a * a
-            mobe_ref[r:r + n, :] = m
+            ae_ref[r:r + n, :] = m
+            for x in range(nx):
+                mobe_ref[x, r:r + n, :] = g.unpack(m, x)
             ae2_ref[r:r + n, :] = worn(a, m, e, mean)
         for x in range(nx):
             wear(x + 1, OFF - 1, 1, yr_ref[1, 10 + x:11 + x, :])
             wear(x + 1, end, 1, yr_ref[0, 10 + x:11 + x, :])
-        chemistry(g, pad_ref, mob_ref, mobe_ref, zr_ref, zo_ref, ec_ref, chem_ref, cheme_ref, mean, [(0, ny)])
+        chemistry(g, pad_ref, mob_ref, ae_ref, zr_ref, zo_ref, ze_ref, ec_ref, chem_ref, cheme_ref, mean, [(0, ny)])
         top = jnp.zeros((8, nz), F32)
         bottom = jnp.zeros((8, nz), F32)
         for x in range(nx):
@@ -358,21 +365,24 @@
 
 def potentials_b(g, mean, a2_ref, ae2_ref, others, scratch, spans):
     f_ref, lo_ref, hi_ref, yr_ref, zr_ref, zo_ref = others
-    pad_ref, ec_ref, mob_ref, mobe_ref, chem_ref, cheme_ref = scratch
+    pad_ref, ze_ref, ec_ref, ae_ref, mob_ref, mobe_ref, chem_ref, cheme_ref = scratch
     nx = g.nx
-    fill(B_CODE, f_ref, lo_ref, hi_ref, yr_ref, zr_ref, pad_ref, ec_ref, spans)
+    fill(B_CODE, f_ref, lo_ref, hi_ref, yr_ref, zr_ref, pad_ref, ze_ref, ec_ref, spans)
     for p in range(nx + 2):
         for r, n in spread(spans, 8, 32) if 1 <= p <= nx else spread(spans, 0, 48):
             a = a2_ref[p, r:r + n, :]
             mob_ref[p, r:r + n, :] = a * a
     for r, n in spread(spans, 0, 48):
         a = ae2_ref[r - OFF:r - OFF + n, :]
-        mobe_ref[r - OFF:r - OFF + n, :] = a * a
-    chemistry(g, pad_ref, mob_ref, mobe_ref, zr_ref, zo_ref, ec_ref, chem_ref, cheme_ref, mean, spans)
+        m = a * a
+        ae_ref[r - OFF:r - OFF + n, :] = m
+        for x in range(nx):
+            mobe_ref[x, r - OFF:r - OFF + n, :] = g.unpack(m, x)
+    chemistry(g, pad_ref, mob_ref, ae_ref, zr_ref, zo_ref, ze_ref, ec_ref, chem_ref, cheme_ref, mean, spans)
 
 
 def finish_b(g, mean, x, r, n, labels, a2_ref, scratch):
-    pad_ref, ec_ref, mob_ref, mobe_ref, chem_ref, cheme_ref = scratch
+    pad_ref, ze_ref, ec_ref, ae_ref, mob_ref, mobe_ref, chem_ref, cheme_ref = scratch
     m, flux = flux_of(g, x, r, n, mob_ref, mobe_ref, chem_ref, cheme_ref)
     f0 = pad_ref[x + 2, r:r + n, :]
     f = f0 + TIME_STEP * flux
@@ -497,8 +507,9 @@
     ride_z = lax.axis_size("gz") == 2
     packed = (-(-(nx + 2) // 4), rows, nz)
     assert nz == 128 and nx == 4
-    scratch = [pltpu.VMEM((nx + 4, rows, nz), F32), pltpu.VMEM((rows, nz), F32), pltpu.VMEM(padded, F32),
-               pltpu.VMEM((ny, nz), F32), pltpu.VMEM(padded, F32), pltpu.VMEM((ny, nz), F32)]
+    scratch = [pltpu.VMEM((nx + 4, rows, nz), F32), pltpu.VMEM(padded, F32), pltpu.VMEM((rows, nz), F32),
+               pltpu.VMEM((ny, nz), F32), pltpu.VMEM(padded, F32), pltpu.VMEM(block, F32),
+               pltpu.VMEM(padded, F32), pltpu.VMEM(block, F32)]
 
     def start(sums):
         if ride_x:

time: 63.8 us -> 60 us (0.940)
  Pallas kernels: 18.4 us -> 14.7 us
    pallas_call x11, Pallas kernels: 18.4 us -> 14.7 us  [call(): pl.pallas_call(kernel, in_specs=in_specs or [VMEM] * len(args), out_specs...]
  transfers between devices with their start and end apart: 18 -> 18, of which waited for: 9 -> 9; matrix products, arithmetic and copies ran while one was open for 5% -> 5% of each run, Pallas kernels for 11% -> 9%
where the time goes in v9:
time: 60 us; the launch traced here: 59.7 us
  waiting for transfers between devices  21.2 us (35%)
  starting transfers between devices  19.4 us (32%)
  Pallas kernels  14.7 us (24%)
  local copies, waits for them, and re-layouts  2.93 us (5%)
  between operations  1.44 us (2%)
    pallas_call x11, Pallas kernels, call(): pl.pallas_call(kernel, in_specs=in_specs or [VMEM] * len(args), out_specs...  14.7 us
    ppermute x2, waiting for transfers between devices, start(): return (sums, lax.ppermute(sums, 'gx', ring('gx', 2)))  9.93 us
    ppermute x2, starting transfers between devices, x_sides(): lax.ppermute(lo, 'gx', ring('gx', -1))  5.32 us
    ppermute x3, waiting for transfers between devices, both_sides(): return lax.ppermute(pay, axis, ring(axis, 1))  4.67 us
    ppermute x3, starting transfers between devices, both_sides(): return lax.ppermute(pay, axis, ring(axis, 1))  4.62 us
    ppermute x6, waiting for transfers between devices, z_neighbour(): return lax.ppermute(pay, axis, ring(axis, 1))  4.26 us
    ppermute x3, starting transfers between devices, detector(): own = [plane] + [lax.ppermute(plane, 'gx', ring('gx', s)) for s in shifts]  4 us
    ppermute x2, starting transfers between devices, x_sides(): lax.ppermute(hi, 'gx', ring('gx', 1))  3.73 us
  transfers between devices with their start and end apart: 18, of which 9 were waited for; matrix products, arithmetic and copies ran while one was open for 5% of the time, Pallas kernels for 9%

profile of v9, /device:TPU:0, one launch (start us, length us, event | category | flops | bytes accessed | tf_op | source)
XLA Modules:
  0.0 59.7 jit_solution(4873765018011053992)
XLA Ops:
  0.6 1.6 %shard_map.120 = (f32[4,240,128]{2,1,0:T(8,128)S(1)}, f32[4,240,128]{2,1,0:T(8,128)S(1)}, s16[736,128]{1,0:T(8,128)(2,1)S(1)}, s16[736,128]{1,0:T(8,128)(2,1)S(1...) custom-call(f32[4,240,128]{2,1,0:T(8,128)} %c_hbm.1, f32[4,240,128]{2,1,0:T(8,128)} %d_hbm.1, s32[4,240,128]{2,1,0:T(8,128)} %l_hbm.3), custom_call_target="tpu_custom_call" | custom-call | tf_op jit(solution)/shard_map/pallas_call | solution.py:60
  2.3 3.1 %collective-permute-start = (s16[736,128]{1,0:T(8,128)(2,1)S(1)}, s16[736,128]{1,0:T(8,128)(2,1)S(1)}, u32[]{:S(2)}, u32[]{:S(2)}) collective-permute-start(s16[736,128]{1,0:T(8,128)(2,1)S(1)} %get-tuple-element.31), channel_id=1, source_target_pairs={{0,4},{4,8},{8,12},{12,0},{1,5},{5,9},{9,13},{13,1},{2,6},{6,10},{... | collective-permute-start | bytes 565256 | tf_op jit(solution)/shard_map/ppermute | solution.py:497
  5.3 2.1 %collective-permute-start.1 = (s16[736,128]{1,0:T(8,128)(2,1)S(1)}, s16[736,128]{1,0:T(8,128)(2,1)S(1)}, u32[]{:S(2)}, u32[]{:S(2)}) collective-permute-start(s16[736,128]{1,0:T(8,128)(2,1)S(1)} %get-tuple-element.32), channel_id=1, source_target_pairs={{0,12},{4,0},{8,4},{12,8},{1,13},{5,1},{9,5},{13,9},{2,14},{6,2},{... | collective-permute-start | bytes 565256 | tf_op jit(solution)/shard_map/ppermute | solution.py:497
  7.4 0.9 %collective-permute-start.2 = (f32[8,128]{1,0:T(8,128)S(1)}, f32[8,128]{1,0:T(8,128)S(1)}, u32[]{:S(2)}, u32[]{:S(2)}) collective-permute-start(f32[8,128]{1,0:T(8,128)S(1)} %get-tuple-element.33.refs_4_), channel_id=1, source_target_pairs={{0,8},{4,12},{8,0},{12,4},{1,9},{5,13},{9,1},{13,5},{2,10},{6,14},... | collective-permute-start | bytes 12296 | tf_op jit(solution)/shard_map/ppermute | solution.py:516
  8.4 0.8 %copy.16 = bf16[27,4,16]{2,1,0:T(4,128)(2,1)S(1)} copy(bf16[27,4,16]{0,1,2:T(4,128)(2,1)} %bitcast.27) | data formatting | bytes 6912 | tf_op jit(solution)/shard_map/transpose | solution.py:639
  9.2 1.0 %copy.17 = bf16[27,16,16]{2,1,0:T(8,128)(2,1)S(1)} copy(bf16[27,16,16]{0,1,2:T(8,128)(2,1)} %bitcast.24) | data formatting | bytes 27648 | tf_op jit(solution)/shard_map/transpose | solution.py:640
  10.2 0.8 %copy.18 = bf16[27,1,16]{2,0,1:T(8,128)(2,1)S(1)} copy(bf16[27,1,16]{0,2,1:T(8,128)(2,1)} %param.16) | data formatting | bytes 1728 | tf_op args[7]
  11.1 0.1 copy.19
  11.2 5.1 %collective-permute-done.2.refs_5_ = f32[8,128]{1,0:T(8,128)S(1)} collective-permute-done((f32[8,128]{1,0:T(8,128)S(1)}, f32[8,128]{1,0:T(8,128)S(1)}, u32[]{:S(2)}, u32[]{:S(2)}) %collective-permute-start.2) | collective-permute-done | bytes 4128 | tf_op jit(solution)/shard_map/ppermute | solution.py:516
  16.3 0.0 collective-permute-done.refs_2_.lo_ref
  16.3 1.6 %collective-permute-start.3 = (f32[2,24,128]{2,1,0:T(8,128)S(1)}, f32[2,24,128]{2,1,0:T(8,128)S(1)}, u32[]{:S(2)}, u32[]{:S(2)}) collective-permute-start(f32[2,24,128]{2,1,0:T(8,128)S(1)} %shard_map.121.refs_5_.yp_ref), channel_id=1, source_target_pairs={{0,2},{2,0},{1,3},{3,1},{4,6},{6,4},{5,7},{7,5},{8,10},{10,8},{9,1... | collective-permute-start | bytes 73736 | tf_op jit(solution)/shard_map/ppermute | solution.py:479
  17.9 2.3 %collective-permute-done.3.refs_4_.yr_ref = f32[2,24,128]{2,1,0:T(8,128)S(1)} collective-permute-done((f32[2,24,128]{2,1,0:T(8,128)S(1)}, f32[2,24,128]{2,1,0:T(8,128)S(1)}, u32[]{:S(2)}, u32[]{:S(2)}) %collective-permute-start.3) | collective-permute-done | bytes 24608 | tf_op jit(solution)/shard_map/ppermute | solution.py:479
  20.2 0.3 shard_map.122.zo_ref
  20.6 0.1 collective-permute-start.4
  20.6 1.5 %collective-permute-done.4.zr_ref = f32[2,272,128]{2,1,0:T(8,128)S(1)} collective-permute-done((f32[2,272,128]{2,1,0:T(8,128)S(1)}, f32[2,272,128]{2,1,0:T(8,128)S(1)}, u32[]{:S(2)}, u32[]{:S(2)}) %collective-permute-start.4) | collective-permute-done | bytes 278560 | tf_op jit(solution)/shard_map/ppermute | solution.py:485
  22.2 2.6 %shard_map.123 = (f32[4,240,128]{2,1,0:T(8,128)S(1)}, f32[6,272,128]{2,1,0:T(8,128)S(1)}, f32[240,128]{1,0:T(8,128)S(1)}, s16[496,128]{1,0:T(8,128)(2,1)S(1)}, s...) custom-call(f32[4,240,128]{2,1,0:T(8,128)S(1)} %get-tuple-element.29.refs_0_.f_ref, ...), custom_call_target="tpu_custom_call" | custom-call | tf_op jit(solution)/shard_map/pallas_call | solution.py:60
  24.8 0.6 %collective-permute-start.5 = (s16[496,128]{1,0:T(8,128)(2,1)S(1)}, s16[496,128]{1,0:T(8,128)(2,1)S(1)}, u32[]{:S(2)}, u32[]{:S(2)}) collective-permute-start(s16[496,128]{1,0:T(8,128)(2,1)S(1)} %get-tuple-element.37), channel_id=1, source_target_pairs={{0,4},{4,8},{8,12},{12,0},{1,5},{5,9},{9,13},{13,1},{2,6},{6,10},{... | collective-permute-start | bytes 380936 | tf_op jit(solution)/shard_map/ppermute | solution.py:497
  25.5 3.2 %collective-permute-start.6 = (s16[496,128]{1,0:T(8,128)(2,1)S(1)}, s16[496,128]{1,0:T(8,128)(2,1)S(1)}, u32[]{:S(2)}, u32[]{:S(2)}) collective-permute-start(s16[496,128]{1,0:T(8,128)(2,1)S(1)} %get-tuple-element.38), channel_id=1, source_target_pairs={{0,12},{4,0},{8,4},{12,8},{1,13},{5,1},{9,5},{13,9},{2,14},{6,2},{... | collective-permute-start | bytes 380936 | tf_op jit(solution)/shard_map/ppermute | solution.py:497
  28.7 4.9 %collective-permute-done.7.refs_4_ = f32[8,128]{1,0:T(8,128)S(1)} collective-permute-done((f32[8,128]{1,0:T(8,128)S(1)}, f32[8,128]{1,0:T(8,128)S(1)}, u32[]{:S(2)}, u32[]{:S(2)}) %collective-permute-start.7) | collective-permute-done | bytes 4128 | tf_op jit(solution)/shard_map/ppermute | solution.py:516
  33.6 0.0 collective-permute-done.5.refs_1_.lo_ref
  33.6 0.0 collective-permute-done.6.refs_2_.hi_ref
  33.6 0.0 copy-start
  33.6 0.0 copy-start.1
  33.6 1.6 %collective-permute-start.8 = (f32[2,24,128]{2,1,0:T(8,128)S(1)}, f32[2,24,128]{2,1,0:T(8,128)S(1)}, u32[]{:S(2)}, u32[]{:S(2)}) collective-permute-start(f32[2,24,128]{2,1,0:T(8,128)S(1)} %shard_map.124.refs_4_.yp_ref), channel_id=1, source_target_pairs={{0,2},{2,0},{1,3},{3,1},{4,6},{6,4},{5,7},{7,5},{8,10},{10,8},{9,1... | collective-permute-start | bytes 73736 | tf_op jit(solution)/shard_map/ppermute | solution.py:479
  35.2 2.3 %collective-permute-done.8.refs_3_.yr_ref = f32[2,24,128]{2,1,0:T(8,128)S(1)} collective-permute-done((f32[2,24,128]{2,1,0:T(8,128)S(1)}, f32[2,24,128]{2,1,0:T(8,128)S(1)}, u32[]{:S(2)}, u32[]{:S(2)}) %collective-permute-start.8) | collective-permute-done | bytes 24608 | tf_op jit(solution)/shard_map/ppermute | solution.py:479
  37.5 0.2 shard_map.125.zo_ref
  37.7 0.1 collective-permute-start.9
  37.8 1.5 %collective-permute-done.9.zr_ref = f32[2,272,128]{2,1,0:T(8,128)S(1)} collective-permute-done((f32[2,272,128]{2,1,0:T(8,128)S(1)}, f32[2,272,128]{2,1,0:T(8,128)S(1)}, u32[]{:S(2)}, u32[]{:S(2)}) %collective-permute-start.9) | collective-permute-done | bytes 278560 | tf_op jit(solution)/shard_map/ppermute | solution.py:485
  39.3 0.6 %shard_map.127 = bf16[2,16,128]{2,1,0:T(8,128)(2,1)S(1)} custom-call(f32[4,240,128]{2,1,0:T(8,128)S(1)} %get-tuple-element.34.refs_0_.f_ref, f32[6,272,128]{2,1,0:T(8,128)S(1)} %get-tuple-element.35.a2_ref, f32[240,128]{1,0:T(8,128)S(1)} %get-tuple-element.36.ae2_ref, s16[496,128]{1,0:T(8,128)(2,1)S(1)} %collective-permute-done.5.refs_1_.lo_ref, ...), custom_call_target="tpu_custom_call" | custom-call | tf_op jit(solution)/shard_map/pallas_call | solution.py:60
  39.9 1.5 %collective-permute-start.10 = (bf16[2,16,128]{2,1,0:T(8,128)(2,1)S(1)}, bf16[2,16,128]{2,1,0:T(8,128)(2,1)S(1)}, u32[]{:S(2)}, u32[]{:S(2)}) collective-permute-start(bf16[2,16,128]{2,1,0:T(8,128)(2,1)S(1)} %shard_map.127), channel_id=1, source_target_pairs={{0,2},{2,0},{1,3},{3,1},{4,6},{6,4},{5,7},{7,5},{8,10},{10,8},{9,1... | collective-permute-start | bytes 24584 | tf_op jit(solution)/shard_map/ppermute | solution.py:479
  41.4 0.1 pad_add_fusion
  41.5 4.4 %shard_map.126 = (f32[4,240,128]{2,1,0:T(8,128)}, f32[4,240,128]{2,1,0:T(8,128)}, f32[4,240,128]{2,1,0:T(8,128)}, bf16[60,128]{1,0:T(8,128)(2,1)S(1)}) custom-call(f32[4,240,128]{2,1,0:T(8,128)S(1)} %get-tuple-element.34.refs_0_.f_ref, f32[6,272,128]{2,1,0:T(8,128)S(1)} %get-tuple-element.35.a2_ref, f32[240,128]{1,0:T(8,128)S(1)} %get-tuple-element.36.ae2_ref, ...), custom_call_target="tpu_custom_call" | custom-call | tf_op jit(solution)/shard_map/pallas_call | solution.py:60
  45.9 0.0 collective-permute-done.10.yr_ref
  45.9 0.1 broadcast_in_dim.15.ids_ref.refs_0_
  46.0 2.0 %collective-permute-start.11 = (bf16[80,128]{1,0:T(8,128)(2,1)S(1)}, bf16[80,128]{1,0:T(8,128)(2,1)S(1)}, u32[]{:S(2)}, u32[]{:S(2)}) collective-permute-start(bf16[80,128]{1,0:T(8,128)(2,1)S(1)} %shard_map.128.plane_ref.refs_1_), channel_id=1, source_target_pairs={{0,4},{4,8},{8,12},{12,0},{1,5},{5,9},{9,13},{13,1},{2,6},{6,10},{... | collective-permute-start | bytes 61448 | tf_op jit(solution)/shard_map/ppermute | solution.py:754
  48.0 1.9 %collective-permute-start.12 = (bf16[80,128]{1,0:T(8,128)(2,1)S(1)}, bf16[80,128]{1,0:T(8,128)(2,1)S(1)}, u32[]{:S(2)}, u32[]{:S(2)}) collective-permute-start(bf16[80,128]{1,0:T(8,128)(2,1)S(1)} %shard_map.128.plane_ref.refs_1_), channel_id=1, source_target_pairs={{0,12},{4,0},{8,4},{12,8},{1,13},{5,1},{9,5},{13,9},{2,14},{6,2},{... | collective-permute-start | bytes 61448 | tf_op jit(solution)/shard_map/ppermute | solution.py:754
  49.9 0.1 collective-permute-start.13
  50.7 0.1 collective-permute-start.14
  50.8 0.9 %shard_map.129 = (bf16[3,768,640]{2,1,0:T(8,128)(2,1)S(1)}, bf16[3,768,128]{2,1,0:T(8,128)(2,1)S(1)}, bf16[3,640,128]{2,1,0:T(8,128)(2,1)S(1)}, f32[8,640]{1,0:T(8,128)S(1)}) custom-call(bf16[432,16]{1,0:T(8,128)(2,1)S(1)} %bitcast.19, bf16[432,16]{1,0:T(8,128)(2,1)S(1)} %bitcast.17, bf16[144,3]{1,0:T(8,128)(2,1)S(1)} %bitcast.21, f32[1,16]{1,0:T(1,128)S(1)} %bitcast.22, ...), custom_call_target="tpu_custom_call" | custom-call | tf_op jit(solution)/shard_map/pallas_call | solution.py:60
  51.7 0.1 collective-permute-done.11.refs_2_
  51.7 0.5 collective-permute-start.15
  52.2 0.0 collective-permute-done.12.refs_3_
  52.2 0.1 collective-permute-start.16
  52.3 2.3 %collective-permute-done.13.refs_4_ = bf16[80,128]{1,0:T(8,128)(2,1)S(1)} collective-permute-done((bf16[80,128]{1,0:T(8,128)(2,1)S(1)}, bf16[80,128]{1,0:T(8,128)(2,1)S(1)}, u32[]{:S(2)}, u32[]{:S(2)}) %collective-permute-start.13) | collective-permute-done | bytes 20512 | tf_op jit(solution)/shard_map/ppermute | solution.py:754
  54.6 0.0 collective-permute-done.15.refs_6_
  54.6 0.0 collective-permute-done.16.refs_7_
  54.6 1.2 %collective-permute-done.17.refs_8_ = bf16[80,128]{1,0:T(8,128)(2,1)S(1)} collective-permute-done((bf16[80,128]{1,0:T(8,128)(2,1)S(1)}, bf16[80,128]{1,0:T(8,128)(2,1)S(1)}, u32[]{:S(2)}, u32[]{:S(2)}) %collective-permute-start.17) | collective-permute-done | bytes 20512 | tf_op jit(solution)/shard_map/ppermute | solution.py:485
  55.8 3.9 %shard_map.130 = f32[1,32,60]{2,1,0:T(8,128)} custom-call(s32[3,128]{1,0:T(4,128)S(1)} %broadcast_in_dim.15.ids_ref.refs_0_, bf16[80,128]{1,0:T(8,128)(2,1)S(1)} %shard_map.128.plane_ref.refs_1_, bf16[80,128]{1,0:T(8,128)(2,1)S(1)} %collective-permute-done.11.refs_2_, bf16[80,128]{1,0:T(8,128)(2,1)S(1)} %collective-permute-done.12.refs_3_, ...), custom_call_target="tpu_custom_call" | custom-call | tf_op jit(solution)/shard_map/pallas_call | solution.py:60
  (11 shorter events, 0.1 us)
Async XLA Ops:
  2.3 14.0 %collective-permute-start = (s16[736,128]{1,0:T(8,128)(2,1)S(1)}, s16[736,128]{1,0:T(8,128)(2,1)S(1)}, u32[]{:S(2)}, u32[]{:S(2)}) collective-permute-start(s16[736,128]{1,0:T(8,128)(2,1)S(1)} %get-tuple-element.31), channel_id=1, source_target_pairs={{0,4},{4,8},{8,12},{12,0},{1,5},{5,9},{9,13},{13,1},{2,6},{6,10},{... | collective-permute-start | bytes 565256 | tf_op jit(solution)/shard_map/ppermute | solution.py:497
  5.3 10.9 %collective-permute-start.1 = (s16[736,128]{1,0:T(8,128)(2,1)S(1)}, s16[736,128]{1,0:T(8,128)(2,1)S(1)}, u32[]{:S(2)}, u32[]{:S(2)}) collective-permute-start(s16[736,128]{1,0:T(8,128)(2,1)S(1)} %get-tuple-element.32), channel_id=1, source_target_pairs={{0,12},{4,0},{8,4},{12,8},{1,13},{5,1},{9,5},{13,9},{2,14},{6,2},{... | collective-permute-start | bytes 565256 | tf_op jit(solution)/shard_map/ppermute | solution.py:497
  7.4 8.8 %collective-permute-start.2 = (f32[8,128]{1,0:T(8,128)S(1)}, f32[8,128]{1,0:T(8,128)S(1)}, u32[]{:S(2)}, u32[]{:S(2)}) collective-permute-start(f32[8,128]{1,0:T(8,128)S(1)} %get-tuple-element.33.refs_4_), channel_id=1, source_target_pairs={{0,8},{4,12},{8,0},{12,4},{1,9},{5,13},{9,1},{13,5},{2,10},{6,14},... | collective-permute-start | bytes 12296 | tf_op jit(solution)/shard_map/ppermute | solution.py:516
  16.3 3.9 %collective-permute-start.3 = (f32[2,24,128]{2,1,0:T(8,128)S(1)}, f32[2,24,128]{2,1,0:T(8,128)S(1)}, u32[]{:S(2)}, u32[]{:S(2)}) collective-permute-start(f32[2,24,128]{2,1,0:T(8,128)S(1)} %shard_map.121.refs_5_.yp_ref), channel_id=1, source_target_pairs={{0,2},{2,0},{1,3},{3,1},{4,6},{6,4},{5,7},{7,5},{8,10},{10,8},{9,1... | collective-permute-start | bytes 73736 | tf_op jit(solution)/shard_map/ppermute | solution.py:479
  20.6 1.6 %collective-permute-start.4 = (f32[2,272,128]{2,1,0:T(8,128)S(1)}, f32[2,272,128]{2,1,0:T(8,128)S(1)}, u32[]{:S(2)}, u32[]{:S(2)}) collective-permute-start(f32[2,272,128]{2,1,0:T(8,128)S(1)} %shard_map.122.zo_ref), channel_id=1, source_target_pairs={{0,1},{1,0},{2,3},{3,2},{4,5},{5,4},{6,7},{7,6},{8,9},{9,8},{10,11... | collective-permute-start | bytes 835592 | tf_op jit(solution)/shard_map/ppermute | solution.py:485
  24.8 8.7 %collective-permute-start.5 = (s16[496,128]{1,0:T(8,128)(2,1)S(1)}, s16[496,128]{1,0:T(8,128)(2,1)S(1)}, u32[]{:S(2)}, u32[]{:S(2)}) collective-permute-start(s16[496,128]{1,0:T(8,128)(2,1)S(1)} %get-tuple-element.37), channel_id=1, source_target_pairs={{0,4},{4,8},{8,12},{12,0},{1,5},{5,9},{9,13},{13,1},{2,6},{6,10},{... | collective-permute-start | bytes 380936 | tf_op jit(solution)/shard_map/ppermute | solution.py:497
  25.5 8.1 %collective-permute-start.6 = (s16[496,128]{1,0:T(8,128)(2,1)S(1)}, s16[496,128]{1,0:T(8,128)(2,1)S(1)}, u32[]{:S(2)}, u32[]{:S(2)}) collective-permute-start(s16[496,128]{1,0:T(8,128)(2,1)S(1)} %get-tuple-element.38), channel_id=1, source_target_pairs={{0,12},{4,0},{8,4},{12,8},{1,13},{5,1},{9,5},{13,9},{2,14},{6,2},{... | collective-permute-start | bytes 380936 | tf_op jit(solution)/shard_map/ppermute | solution.py:497
  28.7 4.9 %collective-permute-start.7 = (f32[8,128]{1,0:T(8,128)S(1)}, f32[8,128]{1,0:T(8,128)S(1)}, u32[]{:S(2)}, u32[]{:S(2)}) collective-permute-start(f32[8,128]{1,0:T(8,128)S(1)} %get-tuple-element.39.refs_3_), channel_id=1, source_target_pairs={{0,8},{4,12},{8,0},{12,4},{1,9},{5,13},{9,1},{13,5},{2,10},{6,14},... | collective-permute-start | bytes 12296 | tf_op jit(solution)/shard_map/ppermute | solution.py:516
  33.6 17.2 %copy-start = (f32[16]{0:T(128)S(1)}, f32[16]{0:T(128)}, u32[]{:S(2)}) copy-start(f32[16]{0:T(128)} %param.13) | copy-start | bytes 196
  33.6 17.2 %copy-start.1 = (f32[16]{0:T(128)S(1)}, f32[16]{0:T(128)}, u32[]{:S(2)}) copy-start(f32[16]{0:T(128)} %param.15) | copy-start | bytes 196
  33.6 3.9 %collective-permute-start.8 = (f32[2,24,128]{2,1,0:T(8,128)S(1)}, f32[2,24,128]{2,1,0:T(8,128)S(1)}, u32[]{:S(2)}, u32[]{:S(2)}) collective-permute-start(f32[2,24,128]{2,1,0:T(8,128)S(1)} %shard_map.124.refs_4_.yp_ref), channel_id=1, source_target_pairs={{0,2},{2,0},{1,3},{3,1},{4,6},{6,4},{5,7},{7,5},{8,10},{10,8},{9,1... | collective-permute-start | bytes 73736 | tf_op jit(solution)/shard_map/ppermute | solution.py:479
  37.7 1.6 %collective-permute-start.9 = (f32[2,272,128]{2,1,0:T(8,128)S(1)}, f32[2,272,128]{2,1,0:T(8,128)S(1)}, u32[]{:S(2)}, u32[]{:S(2)}) collective-permute-start(f32[2,272,128]{2,1,0:T(8,128)S(1)} %shard_map.125.zo_ref), channel_id=1, source_target_pairs={{0,1},{1,0},{2,3},{3,2},{4,5},{5,4},{6,7},{7,6},{8,9},{9,8},{10,11... | collective-permute-start | bytes 835592 | tf_op jit(solution)/shard_map/ppermute | solution.py:485
  39.9 5.9 %collective-permute-start.10 = (bf16[2,16,128]{2,1,0:T(8,128)(2,1)S(1)}, bf16[2,16,128]{2,1,0:T(8,128)(2,1)S(1)}, u32[]{:S(2)}, u32[]{:S(2)}) collective-permute-start(bf16[2,16,128]{2,1,0:T(8,128)(2,1)S(1)} %shard_map.127), channel_id=1, source_target_pairs={{0,2},{2,0},{1,3},{3,1},{4,6},{6,4},{5,7},{7,5},{8,10},{10,8},{9,1... | collective-permute-start | bytes 24584 | tf_op jit(solution)/shard_map/ppermute | solution.py:479
  46.0 5.7 %collective-permute-start.11 = (bf16[80,128]{1,0:T(8,128)(2,1)S(1)}, bf16[80,128]{1,0:T(8,128)(2,1)S(1)}, u32[]{:S(2)}, u32[]{:S(2)}) collective-permute-start(bf16[80,128]{1,0:T(8,128)(2,1)S(1)} %shard_map.128.plane_ref.refs_1_), channel_id=1, source_target_pairs={{0,4},{4,8},{8,12},{12,0},{1,5},{5,9},{9,13},{13,1},{2,6},{6,10},{... | collective-permute-start | bytes 61448 | tf_op jit(solution)/shard_map/ppermute | solution.py:754
  48.0 4.2 %collective-permute-start.12 = (bf16[80,128]{1,0:T(8,128)(2,1)S(1)}, bf16[80,128]{1,0:T(8,128)(2,1)S(1)}, u32[]{:S(2)}, u32[]{:S(2)}) collective-permute-start(bf16[80,128]{1,0:T(8,128)(2,1)S(1)} %shard_map.128.plane_ref.refs_1_), channel_id=1, source_target_pairs={{0,12},{4,0},{8,4},{12,8},{1,13},{5,1},{9,5},{13,9},{2,14},{6,2},{... | collective-permute-start | bytes 61448 | tf_op jit(solution)/shard_map/ppermute | solution.py:754
  49.9 4.7 %collective-permute-start.13 = (bf16[80,128]{1,0:T(8,128)(2,1)S(1)}, bf16[80,128]{1,0:T(8,128)(2,1)S(1)}, u32[]{:S(2)}, u32[]{:S(2)}) collective-permute-start(bf16[80,128]{1,0:T(8,128)(2,1)S(1)} %shard_map.128.plane_ref.refs_1_), channel_id=1, source_target_pairs={{0,8},{4,12},{8,0},{12,4},{1,9},{5,13},{9,1},{13,5},{2,10},{6,14},... | collective-permute-start | bytes 61448 | tf_op jit(solution)/shard_map/ppermute | solution.py:754
  50.7 3.9 %collective-permute-start.14 = (bf16[80,128]{1,0:T(8,128)(2,1)S(1)}, bf16[80,128]{1,0:T(8,128)(2,1)S(1)}, u32[]{:S(2)}, u32[]{:S(2)}) collective-permute-start(bf16[80,128]{1,0:T(8,128)(2,1)S(1)} %shard_map.128.plane_ref.refs_1_), channel_id=1, source_target_pairs={{0,1},{1,0},{2,3},{3,2},{4,5},{5,4},{6,7},{7,6},{8,9},{9,8},{10,11... | collective-permute-start | bytes 61448 | tf_op jit(solution)/shard_map/ppermute | solution.py:485
  51.7 2.8 %collective-permute-start.15 = (bf16[80,128]{1,0:T(8,128)(2,1)S(1)}, bf16[80,128]{1,0:T(8,128)(2,1)S(1)}, u32[]{:S(2)}, u32[]{:S(2)}) collective-permute-start(bf16[80,128]{1,0:T(8,128)(2,1)S(1)} %collective-permute-done.11.refs_2_), channel_id=1, source_target_pairs={{0,1},{1,0},{2,3},{3,2},{4,5},{5,4},{6,7},{7,6},{8,9},{9,8},{10,11... | collective-permute-start | bytes 61448 | tf_op jit(solution)/shard_map/ppermute | solution.py:485
  52.2 2.4 %collective-permute-start.16 = (bf16[80,128]{1,0:T(8,128)(2,1)S(1)}, bf16[80,128]{1,0:T(8,128)(2,1)S(1)}, u32[]{:S(2)}, u32[]{:S(2)}) collective-permute-start(bf16[80,128]{1,0:T(8,128)(2,1)S(1)} %collective-permute-done.12.refs_3_), channel_id=1, source_target_pairs={{0,1},{1,0},{2,3},{3,2},{4,5},{5,4},{6,7},{7,6},{8,9},{9,8},{10,11... | collective-permute-start | bytes 61448 | tf_op jit(solution)/shard_map/ppermute | solution.py:485
  54.6 1.2 %collective-permute-start.17 = (bf16[80,128]{1,0:T(8,128)(2,1)S(1)}, bf16[80,128]{1,0:T(8,128)(2,1)S(1)}, u32[]{:S(2)}, u32[]{:S(2)}) collective-permute-start(bf16[80,128]{1,0:T(8,128)(2,1)S(1)} %collective-permute-done.13.refs_4_), channel_id=1, source_target_pairs={{0,1},{1,0},{2,3},{3,2},{4,5},{5,4},{6,7},{7,6},{8,9},{9,8},{10,11... | collective-permute-start | bytes 61448 | tf_op jit(solution)/shard_map/ppermute | solution.py:485

commit v10 on v9

--- a/solution.py
+++ b/solution.py
@@ -1,3 +1,5 @@
+import functools
+
 import jax
 import jax.numpy as jnp
 import numpy as np
@@ -46,6 +48,13 @@
 def from_digits(tile):
     v = tile.astype(jnp.int32).astype(F32) + 32768.0
     return (v[0:2] + v[2:4] * (1.0 / 65536.0)) * (SUM_SPAN / 65536.0) + SUM_LOW
+
+
+def each(count, body):
+    def step(i, carry):
+        body(i)
+        return carry
+    lax.fori_loop(0, count, step, 0)
 
 
 def by_label(labels, values):
@@ -206,9 +215,12 @@
     for p, k in ((1, 8), (nx + 2, 9)):
         pad_ref[p, OFF - 1:OFF, :] = yr_ref[1, k:k + 1, :]
         pad_ref[p, end:end + 1, :] = yr_ref[0, k:k + 1, :]
-    for x in range(nx):
+    @functools.partial(each, nx)
+    def _(x):
         for r, n in wide:
             pad_ref[x + 2, OFF + r:OFF + r + n, :] = f_ref[x, r:r + n, :]
+
+    for x in range(nx):
         for side, near, far in ((1, OFF - 1, OFF - 2), (0, end, end + 1)):
             pad_ref[x + 2, near:near + 1, :] = yr_ref[side, 2 * x:2 * x + 1, :]
             pad_ref[x + 2, far:far + 1, :] = yr_ref[side, 2 * x + 1:2 * x + 2, :]
@@ -267,14 +279,16 @@
 
 def chemistry(g, pad_ref, mob_ref, ae_ref, zr_ref, zo_ref, ze_ref, ec_ref, chem_ref, cheme_ref, mean, spans):
     nx = g.nx
-    for p in range(nx + 2):
-        for r, n in spread(spans, 8, 32) if 1 <= p <= nx else spread(spans, 0, 48):
+    @functools.partial(each, nx + 2)
+    def _(p):
+        for r, n in spread(spans, 8, 32):
             f = pad_ref[p + 1, r:r + n, :]
             e = ze_ref[p, r:r + n, :]
             around = (pad_ref[p, r:r + n, :] + pad_ref[p + 2, r:r + n, :]
                       + pad_ref[p + 1, r - 1:r - 1 + n, :] + pad_ref[p + 1, r + 1:r + 1 + n, :]
                       + g.before(f, e) + g.after(f, e))
             chem_ref[p, r:r + n, :] = chem_of(f, mob_ref[p, r:r + n, :], around, mean)
+
     firsts, lasts = g.lane % 32 == 0, g.lane % 32 == 31
     for r, n in spread(spans, 0, 48):
         e = ec_ref[r:r + n, :]
@@ -326,8 +340,6 @@
         for r, n in chunks(0, ny, 48):
             wear(0, OFF + r, n, from_code(lo_ref[2 * ny + r:2 * ny + r + n, :], A_CODE))
             wear(nx + 1, OFF + r, n, from_code(hi_ref[2 * ny + r:2 * ny + r + n, :], A_CODE))
-            for x in range(nx):
-                wear(x + 1, OFF + r, n, amp_ref[x, r:r + n, :])
             e = ec_ref[OFF + r:OFF + r + n, :]
             a = pltpu.roll(e, nz - 16, 1)
             m = a * a
@@ -335,27 +347,35 @@
             for x in range(nx):
                 mobe_ref[x, r:r + n, :] = g.unpack(m, x)
             ae2_ref[r:r + n, :] = worn(a, m, e, mean)
+
+        @functools.partial(each, nx)
+        def _(x):
+            for r, n in chunks(0, ny, 48):
+                wear(x + 1, OFF + r, n, amp_ref[x, r:r + n, :])
+
         for x in range(nx):
             wear(x + 1, OFF - 1, 1, yr_ref[1, 10 + x:11 + x, :])
             wear(x + 1, end, 1, yr_ref[0, 10 + x:11 + x, :])
         chemistry(g, pad_ref, mob_ref, ae_ref, zr_ref, zo_ref, ze_ref, ec_ref, chem_ref, cheme_ref, mean, [(0, ny)])
-        top = jnp.zeros((8, nz), F32)
-        bottom = jnp.zeros((8, nz), F32)
-        for x in range(nx):
+
+        def advance(x, carry):
+            top, bottom = carry
             for r, n in chunks(OFF, end, 48):
                 _, flux = flux_of(g, x, r, n, mob_ref, mobe_ref, chem_ref, cheme_ref)
                 f = pad_ref[x + 2, r:r + n, :] + TIME_STEP * flux
-                s = slice(r - OFF, r - OFF + n)
-                f2_ref[x, s, :] = f
+                f2_ref[x, r - OFF:r - OFF + n, :] = f
                 a = a2_ref[x + 1, r:r + n, :]
                 m = a * a
                 top = top + fold(m * f)
                 bottom = bottom + fold(m)
-                for near, far, out in ((0, 1, lo_out), (nx - 1, nx - 2, hi_out)):
-                    if x == near:
-                        out[s, :] = to_code(f, B_CODE)
-                    if x == far:
-                        out[r - OFF + ny:r - OFF + ny + n, :] = to_code(f, B_CODE)
+            return top, bottom
+
+        zero = jnp.zeros((8, nz), F32)
+        top, bottom = lax.fori_loop(0, nx, advance, (zero, zero))
+        for near, far, out in ((0, 1, lo_out), (nx - 1, nx - 2, hi_out)):
+            for r, n in chunks(0, ny, 48):
+                out[r:r + n, :] = to_code(f2_ref[near, r:r + n, :], B_CODE)
+                out[ny + r:ny + r + n, :] = to_code(f2_ref[far, r:r + n, :], B_CODE)
         s = to_rows(top, bottom)
         sum_ref[...] = s
         lo_out[2 * ny:2 * ny + 16, :] = sum_digits(s)
@@ -368,10 +388,13 @@
     pad_ref, ze_ref, ec_ref, ae_ref, mob_ref, mobe_ref, chem_ref, cheme_ref = scratch
     nx = g.nx
     fill(B_CODE, f_ref, lo_ref, hi_ref, yr_ref, zr_ref, pad_ref, ze_ref, ec_ref, spans)
-    for p in range(nx + 2):
-        for r, n in spread(spans, 8, 32) if 1 <= p <= nx else spread(spans, 0, 48):
+
+    @functools.partial(each, nx + 2)
+    def _(p):
+        for r, n in spread(spans, 8, 32):
             a = a2_ref[p, r:r + n, :]
             mob_ref[p, r:r + n, :] = a * a
+
     for r, n in spread(spans, 0, 48):
         a = ae2_ref[r - OFF:r - OFF + n, :]
         m = a * a
@@ -437,24 +460,30 @@
         mean = weighted_mean(yp_ref, yr_ref, zr_ref, ride_y, ride_z)
         potentials_b(g, mean, a2_ref, ae2_ref, (f_ref, lo_ref, hi_ref, yr_ref, zr_ref, zo_ref), scratch, [(0, ny)])
         labels_in.wait()
-        copies = []
-        for k, (r, n) in enumerate(chunks(OFF, OFF + ny, 48)):
-            s = slice(r - OFF, r - OFF + n)
-            pooled = [None] * 4
-            for x in range(nx):
+        outs = ((f3_ref, f3_hbm), (dmg_ref, dmg_hbm), (flux_ref, flux_hbm))
+
+        def out_copy(i, x):
+            return pltpu.make_async_copy(outs[i][0].at[x], outs[i][1].at[x], sems.at[i, x])
+
+        pool_scr[...] = jnp.zeros(pool_scr.shape, F32)
+
+        @functools.partial(each, nx)
+        def _(x):
+            for r, n in chunks(OFF, OFF + ny, 48):
+                s = slice(r - OFF, r - OFF + n)
                 flux, values = finish_b(g, mean, x, r, n, l_ref[x, s, :], a2_ref, scratch)
                 f3_ref[x, s, :] = values[0]
                 dmg_ref[x, s, :] = values[1]
                 flux_ref[x, s, :] = flux
-                pooled = [v if p is None else p + v for p, v in zip(pooled, values)]
-            for i in range(4):
-                pool_scr[i, s, :] = pooled[i]
-            for i, (src, dst) in enumerate(((f3_ref, f3_hbm), (dmg_ref, dmg_hbm), (flux_ref, flux_hbm))):
-                copies.append(pltpu.make_async_copy(src.at[:, s, :], dst.at[:, s, :], sems.at[i, k]))
-                copies[-1].start()
+                for i in range(4):
+                    pool_scr[i, s, :] = pool_scr[i, s, :] + values[i]
+            for i in range(3):
+                out_copy(i, x).start()
+
         pool_ref[...] = pool_rows(pool_scr, ny // 4, nz).astype(BF16)
-        for c in copies:
-            c.wait()
+        for x in range(nx):
+            for i in range(3):
+                out_copy(i, x).wait()
     return kernel
 
 
@@ -560,7 +589,7 @@
         scratch=scratch + [
             pltpu.VMEM((4, ny, nz), F32), pltpu.VMEM(block, jnp.int32),
             pltpu.VMEM(block, F32), pltpu.VMEM(block, F32), pltpu.VMEM(block, F32),
-            pltpu.SemaphoreType.DMA, pltpu.SemaphoreType.DMA((3, len(chunks(OFF, OFF + ny, 48))))])
+            pltpu.SemaphoreType.DMA, pltpu.SemaphoreType.DMA((3, nx))])
     ids = jnp.broadcast_to(jnp.stack([lax.axis_index(a) for a in ("gx", "gy", "gz")])[:, None], (3, nz))
     crack_score = detector(pooled, edge, ids, weights + (b_first[None], b_second[None], b_third[None]), ny // 4, nz // 4)
     return (fraction, damage_field, flux_sum, crack_score)

time: 60 us -> 60.6 us (1.010)
    pallas_call x11, Pallas kernels: 14.7 us -> 15.3 us  [call(): pl.pallas_call(kernel, in_specs=in_specs or [VMEM] * len(args), out_specs...]
  transfers between devices with their start and end apart: 18 -> 18, of which waited for: 9 -> 9; matrix products, arithmetic and copies ran while one was open for 5% -> 5% of each run, Pallas kernels for 9% -> 8%
where the time goes in v10:
time: 60.6 us; the launch traced here: 60.3 us
  waiting for transfers between devices  21.2 us (35%)
  starting transfers between devices  19.4 us (32%)
  Pallas kernels  15.3 us (25%)
  local copies, waits for them, and re-layouts  2.93 us (5%)
  between operations  1.44 us (2%)
    pallas_call x11, Pallas kernels, call(): pl.pallas_call(kernel, in_specs=in_specs or [VMEM] * len(args), out_specs...  15.3 us
    ppermute x2, waiting for transfers between devices, start(): return (sums, lax.ppermute(sums, 'gx', ring('gx', 2)))  9.93 us
    ppermute x2, starting transfers between devices, x_sides(): lax.ppermute(lo, 'gx', ring('gx', -1))  5.32 us
    ppermute x3, waiting for transfers between devices, both_sides(): return lax.ppermute(pay, axis, ring(axis, 1))  4.67 us
    ppermute x3, starting transfers between devices, both_sides(): return lax.ppermute(pay, axis, ring(axis, 1))  4.62 us
    ppermute x6, waiting for transfers between devices, z_neighbour(): return lax.ppermute(pay, axis, ring(axis, 1))  4.26 us
    ppermute x3, starting transfers between devices, detector(): own = [plane] + [lax.ppermute(plane, 'gx', ring('gx', s)) for s in shifts]  4 us
    ppermute x2, starting transfers between devices, x_sides(): lax.ppermute(hi, 'gx', ring('gx', 1))  3.73 us
  transfers between devices with their start and end apart: 18, of which 9 were waited for; matrix products, arithmetic and copies ran while one was open for 5% of the time, Pallas kernels for 8%

profile of v10, /device:TPU:0, one launch (start us, length us, event | category | flops | bytes accessed | tf_op | source)
XLA Modules:
  0.0 60.3 jit_solution(6163376998277290550)
XLA Ops:
  0.6 1.6 %shard_map.120 = (f32[4,240,128]{2,1,0:T(8,128)S(1)}, f32[4,240,128]{2,1,0:T(8,128)S(1)}, s16[736,128]{1,0:T(8,128)(2,1)S(1)}, s16[736,128]{1,0:T(8,128)(2,1)S(1...) custom-call(f32[4,240,128]{2,1,0:T(8,128)} %c_hbm.1, f32[4,240,128]{2,1,0:T(8,128)} %d_hbm.1, s32[4,240,128]{2,1,0:T(8,128)} %l_hbm.3), custom_call_target="tpu_custom_call" | custom-call | tf_op jit(solution)/shard_map/pallas_call | solution.py:69
  2.3 3.1 %collective-permute-start = (s16[736,128]{1,0:T(8,128)(2,1)S(1)}, s16[736,128]{1,0:T(8,128)(2,1)S(1)}, u32[]{:S(2)}, u32[]{:S(2)}) collective-permute-start(s16[736,128]{1,0:T(8,128)(2,1)S(1)} %get-tuple-element.31), channel_id=1, source_target_pairs={{0,4},{4,8},{8,12},{12,0},{1,5},{5,9},{9,13},{13,1},{2,6},{6,10},{... | collective-permute-start | bytes 565256 | tf_op jit(solution)/shard_map/ppermute | solution.py:526
  5.3 2.1 %collective-permute-start.1 = (s16[736,128]{1,0:T(8,128)(2,1)S(1)}, s16[736,128]{1,0:T(8,128)(2,1)S(1)}, u32[]{:S(2)}, u32[]{:S(2)}) collective-permute-start(s16[736,128]{1,0:T(8,128)(2,1)S(1)} %get-tuple-element.32), channel_id=1, source_target_pairs={{0,12},{4,0},{8,4},{12,8},{1,13},{5,1},{9,5},{13,9},{2,14},{6,2},{... | collective-permute-start | bytes 565256 | tf_op jit(solution)/shard_map/ppermute | solution.py:526
  7.4 0.9 %collective-permute-start.2 = (f32[8,128]{1,0:T(8,128)S(1)}, f32[8,128]{1,0:T(8,128)S(1)}, u32[]{:S(2)}, u32[]{:S(2)}) collective-permute-start(f32[8,128]{1,0:T(8,128)S(1)} %get-tuple-element.33.refs_4_), channel_id=1, source_target_pairs={{0,8},{4,12},{8,0},{12,4},{1,9},{5,13},{9,1},{13,5},{2,10},{6,14},... | collective-permute-start | bytes 12296 | tf_op jit(solution)/shard_map/ppermute | solution.py:545
  8.4 0.8 %copy.16 = bf16[27,4,16]{2,1,0:T(4,128)(2,1)S(1)} copy(bf16[27,4,16]{0,1,2:T(4,128)(2,1)} %bitcast.27) | data formatting | bytes 6912 | tf_op jit(solution)/shard_map/transpose | solution.py:668
  9.2 1.0 %copy.17 = bf16[27,16,16]{2,1,0:T(8,128)(2,1)S(1)} copy(bf16[27,16,16]{0,1,2:T(8,128)(2,1)} %bitcast.24) | data formatting | bytes 27648 | tf_op jit(solution)/shard_map/transpose | solution.py:669
  10.2 0.8 %copy.18 = bf16[27,1,16]{2,0,1:T(8,128)(2,1)S(1)} copy(bf16[27,1,16]{0,2,1:T(8,128)(2,1)} %param.16) | data formatting | bytes 1728 | tf_op args[7]
  11.1 0.1 copy.19
  11.2 5.1 %collective-permute-done.2.refs_5_ = f32[8,128]{1,0:T(8,128)S(1)} collective-permute-done((f32[8,128]{1,0:T(8,128)S(1)}, f32[8,128]{1,0:T(8,128)S(1)}, u32[]{:S(2)}, u32[]{:S(2)}) %collective-permute-start.2) | collective-permute-done | bytes 4128 | tf_op jit(solution)/shard_map/ppermute | solution.py:545
  16.3 1.6 %collective-permute-start.3 = (f32[2,24,128]{2,1,0:T(8,128)S(1)}, f32[2,24,128]{2,1,0:T(8,128)S(1)}, u32[]{:S(2)}, u32[]{:S(2)}) collective-permute-start(f32[2,24,128]{2,1,0:T(8,128)S(1)} %shard_map.121.refs_5_.yp_ref), channel_id=1, source_target_pairs={{0,2},{2,0},{1,3},{3,1},{4,6},{6,4},{5,7},{7,5},{8,10},{10,8},{9,1... | collective-permute-start | bytes 73736 | tf_op jit(solution)/shard_map/ppermute | solution.py:508
  17.9 2.3 %collective-permute-done.3.refs_4_.yr_ref = f32[2,24,128]{2,1,0:T(8,128)S(1)} collective-permute-done((f32[2,24,128]{2,1,0:T(8,128)S(1)}, f32[2,24,128]{2,1,0:T(8,128)S(1)}, u32[]{:S(2)}, u32[]{:S(2)}) %collective-permute-start.3) | collective-permute-done | bytes 24608 | tf_op jit(solution)/shard_map/ppermute | solution.py:508
  20.2 0.3 shard_map.122.zo_ref
  20.6 0.1 collective-permute-start.4
  20.6 1.5 %collective-permute-done.4.zr_ref = f32[2,272,128]{2,1,0:T(8,128)S(1)} collective-permute-done((f32[2,272,128]{2,1,0:T(8,128)S(1)}, f32[2,272,128]{2,1,0:T(8,128)S(1)}, u32[]{:S(2)}, u32[]{:S(2)}) %collective-permute-start.4) | collective-permute-done | bytes 278560 | tf_op jit(solution)/shard_map/ppermute | solution.py:514
  22.2 3.2 %shard_map.123 = (f32[4,240,128]{2,1,0:T(8,128)S(1)}, f32[6,272,128]{2,1,0:T(8,128)S(1)}, f32[240,128]{1,0:T(8,128)S(1)}, s16[496,128]{1,0:T(8,128)(2,1)S(1)}, s...) custom-call(f32[4,240,128]{2,1,0:T(8,128)S(1)} %get-tuple-element.29.refs_0_.f_ref, ...), custom_call_target="tpu_custom_call" | custom-call | tf_op jit(solution)/shard_map/pallas_call | solution.py:69
  25.3 0.6 %collective-permute-start.5 = (s16[496,128]{1,0:T(8,128)(2,1)S(1)}, s16[496,128]{1,0:T(8,128)(2,1)S(1)}, u32[]{:S(2)}, u32[]{:S(2)}) collective-permute-start(s16[496,128]{1,0:T(8,128)(2,1)S(1)} %get-tuple-element.37), channel_id=1, source_target_pairs={{0,4},{4,8},{8,12},{12,0},{1,5},{5,9},{9,13},{13,1},{2,6},{6,10},{... | collective-permute-start | bytes 380936 | tf_op jit(solution)/shard_map/ppermute | solution.py:526
  26.0 3.2 %collective-permute-start.6 = (s16[496,128]{1,0:T(8,128)(2,1)S(1)}, s16[496,128]{1,0:T(8,128)(2,1)S(1)}, u32[]{:S(2)}, u32[]{:S(2)}) collective-permute-start(s16[496,128]{1,0:T(8,128)(2,1)S(1)} %get-tuple-element.38), channel_id=1, source_target_pairs={{0,12},{4,0},{8,4},{12,8},{1,13},{5,1},{9,5},{13,9},{2,14},{6,2},{... | collective-permute-start | bytes 380936 | tf_op jit(solution)/shard_map/ppermute | solution.py:526
  29.2 4.9 %collective-permute-done.7.refs_4_ = f32[8,128]{1,0:T(8,128)S(1)} collective-permute-done((f32[8,128]{1,0:T(8,128)S(1)}, f32[8,128]{1,0:T(8,128)S(1)}, u32[]{:S(2)}, u32[]{:S(2)}) %collective-permute-start.7) | collective-permute-done | bytes 4128 | tf_op jit(solution)/shard_map/ppermute | solution.py:545
  34.1 0.0 collective-permute-done.5.refs_1_.lo_ref
  34.1 0.0 collective-permute-done.6.refs_2_.hi_ref
  34.1 0.0 copy-start
  34.1 0.0 copy-start.1
  34.1 1.6 %collective-permute-start.8 = (f32[2,24,128]{2,1,0:T(8,128)S(1)}, f32[2,24,128]{2,1,0:T(8,128)S(1)}, u32[]{:S(2)}, u32[]{:S(2)}) collective-permute-start(f32[2,24,128]{2,1,0:T(8,128)S(1)} %shard_map.124.refs_4_.yp_ref), channel_id=1, source_target_pairs={{0,2},{2,0},{1,3},{3,1},{4,6},{6,4},{5,7},{7,5},{8,10},{10,8},{9,1... | collective-permute-start | bytes 73736 | tf_op jit(solution)/shard_map/ppermute | solution.py:508
  35.7 2.3 %collective-permute-done.8.refs_3_.yr_ref = f32[2,24,128]{2,1,0:T(8,128)S(1)} collective-permute-done((f32[2,24,128]{2,1,0:T(8,128)S(1)}, f32[2,24,128]{2,1,0:T(8,128)S(1)}, u32[]{:S(2)}, u32[]{:S(2)}) %collective-permute-start.8) | collective-permute-done | bytes 24608 | tf_op jit(solution)/shard_map/ppermute | solution.py:508
  38.0 0.2 shard_map.125.zo_ref
  38.2 0.1 collective-permute-start.9
  38.3 1.5 %collective-permute-done.9.zr_ref = f32[2,272,128]{2,1,0:T(8,128)S(1)} collective-permute-done((f32[2,272,128]{2,1,0:T(8,128)S(1)}, f32[2,272,128]{2,1,0:T(8,128)S(1)}, u32[]{:S(2)}, u32[]{:S(2)}) %collective-permute-start.9) | collective-permute-done | bytes 278560 | tf_op jit(solution)/shard_map/ppermute | solution.py:514
  39.9 1.4 %shard_map.127 = bf16[2,16,128]{2,1,0:T(8,128)(2,1)S(1)} custom-call(f32[4,240,128]{2,1,0:T(8,128)S(1)} %get-tuple-element.34.refs_0_.f_ref, f32[6,272,128]{2,1,0:T(8,128)S(1)} %get-tuple-element.35.a2_ref, f32[240,128]{1,0:T(8,128)S(1)} %get-tuple-element.36.ae2_ref, s16[496,128]{1,0:T(8,128)(2,1)S(1)} %collective-permute-done.5.refs_1_.lo_ref, ...), custom_call_target="tpu_custom_call" | custom-call | tf_op jit(solution)/shard_map/pallas_call | solution.py:69
  41.3 1.5 %collective-permute-start.10 = (bf16[2,16,128]{2,1,0:T(8,128)(2,1)S(1)}, bf16[2,16,128]{2,1,0:T(8,128)(2,1)S(1)}, u32[]{:S(2)}, u32[]{:S(2)}) collective-permute-start(bf16[2,16,128]{2,1,0:T(8,128)(2,1)S(1)} %shard_map.127), channel_id=1, source_target_pairs={{0,2},{2,0},{1,3},{3,1},{4,6},{6,4},{5,7},{7,5},{8,10},{10,8},{9,1... | collective-permute-start | bytes 24584 | tf_op jit(solution)/shard_map/ppermute | solution.py:508
  42.8 0.1 pad_add_fusion
  42.8 3.7 %shard_map.126 = (f32[4,240,128]{2,1,0:T(8,128)}, f32[4,240,128]{2,1,0:T(8,128)}, f32[4,240,128]{2,1,0:T(8,128)}, bf16[60,128]{1,0:T(8,128)(2,1)S(1)}) custom-call(f32[4,240,128]{2,1,0:T(8,128)S(1)} %get-tuple-element.34.refs_0_.f_ref, f32[6,272,128]{2,1,0:T(8,128)S(1)} %get-tuple-element.35.a2_ref, f32[240,128]{1,0:T(8,128)S(1)} %get-tuple-element.36.ae2_ref, ...), custom_call_target="tpu_custom_call" | custom-call | tf_op jit(solution)/shard_map/pallas_call | solution.py:69
  46.5 0.1 broadcast_in_dim.15.ids_ref.refs_0_
  46.7 2.0 %collective-permute-start.11 = (bf16[80,128]{1,0:T(8,128)(2,1)S(1)}, bf16[80,128]{1,0:T(8,128)(2,1)S(1)}, u32[]{:S(2)}, u32[]{:S(2)}) collective-permute-start(bf16[80,128]{1,0:T(8,128)(2,1)S(1)} %shard_map.128.plane_ref.refs_1_), channel_id=1, source_target_pairs={{0,4},{4,8},{8,12},{12,0},{1,5},{5,9},{9,13},{13,1},{2,6},{6,10},{... | collective-permute-start | bytes 61448 | tf_op jit(solution)/shard_map/ppermute | solution.py:783
  48.7 1.9 %collective-permute-start.12 = (bf16[80,128]{1,0:T(8,128)(2,1)S(1)}, bf16[80,128]{1,0:T(8,128)(2,1)S(1)}, u32[]{:S(2)}, u32[]{:S(2)}) collective-permute-start(bf16[80,128]{1,0:T(8,128)(2,1)S(1)} %shard_map.128.plane_ref.refs_1_), channel_id=1, source_target_pairs={{0,12},{4,0},{8,4},{12,8},{1,13},{5,1},{9,5},{13,9},{2,14},{6,2},{... | collective-permute-start | bytes 61448 | tf_op jit(solution)/shard_map/ppermute | solution.py:783
  50.5 0.1 collective-permute-start.13
  51.3 0.1 collective-permute-start.14
  51.4 0.9 %shard_map.129 = (bf16[3,768,640]{2,1,0:T(8,128)(2,1)S(1)}, bf16[3,768,128]{2,1,0:T(8,128)(2,1)S(1)}, bf16[3,640,128]{2,1,0:T(8,128)(2,1)S(1)}, f32[8,640]{1,0:T(8,128)S(1)}) custom-call(bf16[432,16]{1,0:T(8,128)(2,1)S(1)} %bitcast.19, bf16[432,16]{1,0:T(8,128)(2,1)S(1)} %bitcast.17, bf16[144,3]{1,0:T(8,128)(2,1)S(1)} %bitcast.21, f32[1,16]{1,0:T(1,128)S(1)} %bitcast.22, ...), custom_call_target="tpu_custom_call" | custom-call | tf_op jit(solution)/shard_map/pallas_call | solution.py:69
  52.3 0.1 collective-permute-done.11.refs_2_
  52.4 0.5 collective-permute-start.15
  52.9 0.0 collective-permute-done.12.refs_3_
  52.9 0.1 collective-permute-start.16
  53.0 2.3 %collective-permute-done.13.refs_4_ = bf16[80,128]{1,0:T(8,128)(2,1)S(1)} collective-permute-done((bf16[80,128]{1,0:T(8,128)(2,1)S(1)}, bf16[80,128]{1,0:T(8,128)(2,1)S(1)}, u32[]{:S(2)}, u32[]{:S(2)}) %collective-permute-start.13) | collective-permute-done | bytes 20512 | tf_op jit(solution)/shard_map/ppermute | solution.py:783
  55.2 0.0 collective-permute-start.17
  55.2 0.0 collective-permute-done.14.refs_5_
  55.2 0.0 collective-permute-done.15.refs_6_
  55.2 0.0 collective-permute-done.16.refs_7_
  55.2 1.2 %collective-permute-done.17.refs_8_ = bf16[80,128]{1,0:T(8,128)(2,1)S(1)} collective-permute-done((bf16[80,128]{1,0:T(8,128)(2,1)S(1)}, bf16[80,128]{1,0:T(8,128)(2,1)S(1)}, u32[]{:S(2)}, u32[]{:S(2)}) %collective-permute-start.17) | collective-permute-done | bytes 20512 | tf_op jit(solution)/shard_map/ppermute | solution.py:514
  56.4 3.9 %shard_map.130 = f32[1,32,60]{2,1,0:T(8,128)} custom-call(s32[3,128]{1,0:T(4,128)S(1)} %broadcast_in_dim.15.ids_ref.refs_0_, bf16[80,128]{1,0:T(8,128)(2,1)S(1)} %shard_map.128.plane_ref.refs_1_, bf16[80,128]{1,0:T(8,128)(2,1)S(1)} %collective-permute-done.11.refs_2_, bf16[80,128]{1,0:T(8,128)(2,1)S(1)} %collective-permute-done.12.refs_3_, ...), custom_call_target="tpu_custom_call" | custom-call | tf_op jit(solution)/shard_map/pallas_call | solution.py:69
  (11 shorter events, 0.1 us)
Async XLA Ops:
  2.3 14.0 %collective-permute-start = (s16[736,128]{1,0:T(8,128)(2,1)S(1)}, s16[736,128]{1,0:T(8,128)(2,1)S(1)}, u32[]{:S(2)}, u32[]{:S(2)}) collective-permute-start(s16[736,128]{1,0:T(8,128)(2,1)S(1)} %get-tuple-element.31), channel_id=1, source_target_pairs={{0,4},{4,8},{8,12},{12,0},{1,5},{5,9},{9,13},{13,1},{2,6},{6,10},{... | collective-permute-start | bytes 565256 | tf_op jit(solution)/shard_map/ppermute | solution.py:526
  5.3 10.9 %collective-permute-start.1 = (s16[736,128]{1,0:T(8,128)(2,1)S(1)}, s16[736,128]{1,0:T(8,128)(2,1)S(1)}, u32[]{:S(2)}, u32[]{:S(2)}) collective-permute-start(s16[736,128]{1,0:T(8,128)(2,1)S(1)} %get-tuple-element.32), channel_id=1, source_target_pairs={{0,12},{4,0},{8,4},{12,8},{1,13},{5,1},{9,5},{13,9},{2,14},{6,2},{... | collective-permute-start | bytes 565256 | tf_op jit(solution)/shard_map/ppermute | solution.py:526
  7.4 8.8 %collective-permute-start.2 = (f32[8,128]{1,0:T(8,128)S(1)}, f32[8,128]{1,0:T(8,128)S(1)}, u32[]{:S(2)}, u32[]{:S(2)}) collective-permute-start(f32[8,128]{1,0:T(8,128)S(1)} %get-tuple-element.33.refs_4_), channel_id=1, source_target_pairs={{0,8},{4,12},{8,0},{12,4},{1,9},{5,13},{9,1},{13,5},{2,10},{6,14},... | collective-permute-start | bytes 12296 | tf_op jit(solution)/shard_map/ppermute | solution.py:545
  16.3 3.9 %collective-permute-start.3 = (f32[2,24,128]{2,1,0:T(8,128)S(1)}, f32[2,24,128]{2,1,0:T(8,128)S(1)}, u32[]{:S(2)}, u32[]{:S(2)}) collective-permute-start(f32[2,24,128]{2,1,0:T(8,128)S(1)} %shard_map.121.refs_5_.yp_ref), channel_id=1, source_target_pairs={{0,2},{2,0},{1,3},{3,1},{4,6},{6,4},{5,7},{7,5},{8,10},{10,8},{9,1... | collective-permute-start | bytes 73736 | tf_op jit(solution)/shard_map/ppermute | solution.py:508
  20.6 1.6 %collective-permute-start.4 = (f32[2,272,128]{2,1,0:T(8,128)S(1)}, f32[2,272,128]{2,1,0:T(8,128)S(1)}, u32[]{:S(2)}, u32[]{:S(2)}) collective-permute-start(f32[2,272,128]{2,1,0:T(8,128)S(1)} %shard_map.122.zo_ref), channel_id=1, source_target_pairs={{0,1},{1,0},{2,3},{3,2},{4,5},{5,4},{6,7},{7,6},{8,9},{9,8},{10,11... | collective-permute-start | bytes 835592 | tf_op jit(solution)/shard_map/ppermute | solution.py:514
  25.3 8.7 %collective-permute-start.5 = (s16[496,128]{1,0:T(8,128)(2,1)S(1)}, s16[496,128]{1,0:T(8,128)(2,1)S(1)}, u32[]{:S(2)}, u32[]{:S(2)}) collective-permute-start(s16[496,128]{1,0:T(8,128)(2,1)S(1)} %get-tuple-element.37), channel_id=1, source_target_pairs={{0,4},{4,8},{8,12},{12,0},{1,5},{5,9},{9,13},{13,1},{2,6},{6,10},{... | collective-permute-start | bytes 380936 | tf_op jit(solution)/shard_map/ppermute | solution.py:526
  26.0 8.1 %collective-permute-start.6 = (s16[496,128]{1,0:T(8,128)(2,1)S(1)}, s16[496,128]{1,0:T(8,128)(2,1)S(1)}, u32[]{:S(2)}, u32[]{:S(2)}) collective-permute-start(s16[496,128]{1,0:T(8,128)(2,1)S(1)} %get-tuple-element.38), channel_id=1, source_target_pairs={{0,12},{4,0},{8,4},{12,8},{1,13},{5,1},{9,5},{13,9},{2,14},{6,2},{... | collective-permute-start | bytes 380936 | tf_op jit(solution)/shard_map/ppermute | solution.py:526
  29.2 4.9 %collective-permute-start.7 = (f32[8,128]{1,0:T(8,128)S(1)}, f32[8,128]{1,0:T(8,128)S(1)}, u32[]{:S(2)}, u32[]{:S(2)}) collective-permute-start(f32[8,128]{1,0:T(8,128)S(1)} %get-tuple-element.39.refs_3_), channel_id=1, source_target_pairs={{0,8},{4,12},{8,0},{12,4},{1,9},{5,13},{9,1},{13,5},{2,10},{6,14},... | collective-permute-start | bytes 12296 | tf_op jit(solution)/shard_map/ppermute | solution.py:545
  34.1 17.3 %copy-start = (f32[16]{0:T(128)S(1)}, f32[16]{0:T(128)}, u32[]{:S(2)}) copy-start(f32[16]{0:T(128)} %param.13) | copy-start | bytes 196
  34.1 17.3 %copy-start.1 = (f32[16]{0:T(128)S(1)}, f32[16]{0:T(128)}, u32[]{:S(2)}) copy-start(f32[16]{0:T(128)} %param.15) | copy-start | bytes 196
  34.1 3.9 %collective-permute-start.8 = (f32[2,24,128]{2,1,0:T(8,128)S(1)}, f32[2,24,128]{2,1,0:T(8,128)S(1)}, u32[]{:S(2)}, u32[]{:S(2)}) collective-permute-start(f32[2,24,128]{2,1,0:T(8,128)S(1)} %shard_map.124.refs_4_.yp_ref), channel_id=1, source_target_pairs={{0,2},{2,0},{1,3},{3,1},{4,6},{6,4},{5,7},{7,5},{8,10},{10,8},{9,1... | collective-permute-start | bytes 73736 | tf_op jit(solution)/shard_map/ppermute | solution.py:508
  38.2 1.6 %collective-permute-start.9 = (f32[2,272,128]{2,1,0:T(8,128)S(1)}, f32[2,272,128]{2,1,0:T(8,128)S(1)}, u32[]{:S(2)}, u32[]{:S(2)}) collective-permute-start(f32[2,272,128]{2,1,0:T(8,128)S(1)} %shard_map.125.zo_ref), channel_id=1, source_target_pairs={{0,1},{1,0},{2,3},{3,2},{4,5},{5,4},{6,7},{7,6},{8,9},{9,8},{10,11... | collective-permute-start | bytes 835592 | tf_op jit(solution)/shard_map/ppermute | solution.py:514
  41.3 5.3 %collective-permute-start.10 = (bf16[2,16,128]{2,1,0:T(8,128)(2,1)S(1)}, bf16[2,16,128]{2,1,0:T(8,128)(2,1)S(1)}, u32[]{:S(2)}, u32[]{:S(2)}) collective-permute-start(bf16[2,16,128]{2,1,0:T(8,128)(2,1)S(1)} %shard_map.127), channel_id=1, source_target_pairs={{0,2},{2,0},{1,3},{3,1},{4,6},{6,4},{5,7},{7,5},{8,10},{10,8},{9,1... | collective-permute-start | bytes 24584 | tf_op jit(solution)/shard_map/ppermute | solution.py:508
  46.7 5.7 %collective-permute-start.11 = (bf16[80,128]{1,0:T(8,128)(2,1)S(1)}, bf16[80,128]{1,0:T(8,128)(2,1)S(1)}, u32[]{:S(2)}, u32[]{:S(2)}) collective-permute-start(bf16[80,128]{1,0:T(8,128)(2,1)S(1)} %shard_map.128.plane_ref.refs_1_), channel_id=1, source_target_pairs={{0,4},{4,8},{8,12},{12,0},{1,5},{5,9},{9,13},{13,1},{2,6},{6,10},{... | collective-permute-start | bytes 61448 | tf_op jit(solution)/shard_map/ppermute | solution.py:783
  48.7 4.2 %collective-permute-start.12 = (bf16[80,128]{1,0:T(8,128)(2,1)S(1)}, bf16[80,128]{1,0:T(8,128)(2,1)S(1)}, u32[]{:S(2)}, u32[]{:S(2)}) collective-permute-start(bf16[80,128]{1,0:T(8,128)(2,1)S(1)} %shard_map.128.plane_ref.refs_1_), channel_id=1, source_target_pairs={{0,12},{4,0},{8,4},{12,8},{1,13},{5,1},{9,5},{13,9},{2,14},{6,2},{... | collective-permute-start | bytes 61448 | tf_op jit(solution)/shard_map/ppermute | solution.py:783
  50.5 4.7 %collective-permute-start.13 = (bf16[80,128]{1,0:T(8,128)(2,1)S(1)}, bf16[80,128]{1,0:T(8,128)(2,1)S(1)}, u32[]{:S(2)}, u32[]{:S(2)}) collective-permute-start(bf16[80,128]{1,0:T(8,128)(2,1)S(1)} %shard_map.128.plane_ref.refs_1_), channel_id=1, source_target_pairs={{0,8},{4,12},{8,0},{12,4},{1,9},{5,13},{9,1},{13,5},{2,10},{6,14},... | collective-permute-start | bytes 61448 | tf_op jit(solution)/shard_map/ppermute | solution.py:783
  51.3 3.9 %collective-permute-start.14 = (bf16[80,128]{1,0:T(8,128)(2,1)S(1)}, bf16[80,128]{1,0:T(8,128)(2,1)S(1)}, u32[]{:S(2)}, u32[]{:S(2)}) collective-permute-start(bf16[80,128]{1,0:T(8,128)(2,1)S(1)} %shard_map.128.plane_ref.refs_1_), channel_id=1, source_target_pairs={{0,1},{1,0},{2,3},{3,2},{4,5},{5,4},{6,7},{7,6},{8,9},{9,8},{10,11... | collective-permute-start | bytes 61448 | tf_op jit(solution)/shard_map/ppermute | solution.py:514
  52.4 2.8 %collective-permute-start.15 = (bf16[80,128]{1,0:T(8,128)(2,1)S(1)}, bf16[80,128]{1,0:T(8,128)(2,1)S(1)}, u32[]{:S(2)}, u32[]{:S(2)}) collective-permute-start(bf16[80,128]{1,0:T(8,128)(2,1)S(1)} %collective-permute-done.11.refs_2_), channel_id=1, source_target_pairs={{0,1},{1,0},{2,3},{3,2},{4,5},{5,4},{6,7},{7,6},{8,9},{9,8},{10,11... | collective-permute-start | bytes 61448 | tf_op jit(solution)/shard_map/ppermute | solution.py:514
  52.9 2.4 %collective-permute-start.16 = (bf16[80,128]{1,0:T(8,128)(2,1)S(1)}, bf16[80,128]{1,0:T(8,128)(2,1)S(1)}, u32[]{:S(2)}, u32[]{:S(2)}) collective-permute-start(bf16[80,128]{1,0:T(8,128)(2,1)S(1)} %collective-permute-done.12.refs_3_), channel_id=1, source_target_pairs={{0,1},{1,0},{2,3},{3,2},{4,5},{5,4},{6,7},{7,6},{8,9},{9,8},{10,11... | collective-permute-start | bytes 61448 | tf_op jit(solution)/shard_map/ppermute | solution.py:514
  55.2 1.2 %collective-permute-start.17 = (bf16[80,128]{1,0:T(8,128)(2,1)S(1)}, bf16[80,128]{1,0:T(8,128)(2,1)S(1)}, u32[]{:S(2)}, u32[]{:S(2)}) collective-permute-start(bf16[80,128]{1,0:T(8,128)(2,1)S(1)} %collective-permute-done.13.refs_4_), channel_id=1, source_target_pairs={{0,1},{1,0},{2,3},{3,2},{4,5},{5,4},{6,7},{7,6},{8,9},{9,8},{10,11... | collective-permute-start | bytes 61448 | tf_op jit(solution)/shard_map/ppermute | solution.py:514

commit v11 on v7

--- a/solution.py
+++ b/solution.py
@@ -1,3 +1,5 @@
+import functools
+
 import jax
 import jax.numpy as jnp
 import numpy as np
@@ -46,6 +48,17 @@
 def from_digits(tile):
     v = tile.astype(jnp.int32).astype(F32) + 32768.0
     return (v[0:2] + v[2:4] * (1.0 / 65536.0)) * (SUM_SPAN / 65536.0) + SUM_LOW
+
+
+def each(count, looped, body):
+    def step(i, carry):
+        body(i)
+        return carry
+    if looped:
+        lax.fori_loop(0, count, step, 0)
+    else:
+        for i in range(count):
+            body(i)
 
 
 def by_label(labels, values):
@@ -80,7 +93,7 @@
                             jnp.zeros((6, top.shape[1]), F32)])
 
 
-def first_kernel(c_hbm, d_hbm, l_hbm, f_ref, amp_ref, lo_ref, hi_ref, sum_ref, d_ref, l_ref, sems):
+def first_kernel(c_hbm, d_hbm, l_hbm, f_ref, amp_ref, lo_ref, hi_ref, sum_ref, le_ref, d_ref, l_ref, sems):
     nx, ny, nz = f_ref.shape
     order = [0, nx - 1] + list(range(1, nx - 1))
     copies = []
@@ -94,6 +107,8 @@
     for k, x in enumerate(order):
         for c in copies[k]:
             c.wait()
+        le_ref[x, 0:16, :] = l_ref[x, 0:16, :]
+        le_ref[x, 16:32, :] = l_ref[x, ny - 16:ny, :]
         for r, n in chunks(0, ny, 48):
             f = f_ref[x, r:r + n, :]
             a = by_label(l_ref[x, r:r + n, :], ROOTS) * (1.0 - d_ref[x, r:r + n, :])
@@ -227,8 +242,8 @@
 
 def worn(a, m, f, mean):
     e = f - mean
-    energy = 0.5 * STRAIN_COUPLING * m * e * e
-    return a * (1.0 - DAMAGE_RATE * jnp.maximum(energy - ENERGY_CRITICAL, 0.0))
+    loss = DAMAGE_RATE * 0.5 * STRAIN_COUPLING * (m * (e * e)) - DAMAGE_RATE * ENERGY_CRITICAL
+    return a * (1.0 - jnp.maximum(loss, 0.0))
 
 
 class Geometry:
@@ -246,31 +261,34 @@
 
 
 def chem_of(f, m, around, mean):
-    well = 2.0 * WELL_HEIGHT * f * (1.0 - f) * (1.0 - 2.0 * f)
-    return well + 6.0 * f - around + STRAIN_COUPLING * m * (f - mean)
-
-
-def chemistry(g, pad_ref, mob_ref, mobe_ref, ze_ref, chem_ref, cheme_ref, mean, spans):
+    w = 2.0 * WELL_HEIGHT
+    return ((2.0 * w * f - 3.0 * w) * f + (w + 6.0)) * f - around + STRAIN_COUPLING * (m * (f - mean))
+
+
+def chemistry(g, pad_ref, mob_ref, mobe_ref, ze_ref, chem_ref, cheme_ref, mean, spans, looped=False):
     nx = g.nx
-    for p in range(nx + 2):
-        inside = 1 <= p <= nx
-        rows = spread(spans, 8, 32) if inside else spread(spans, 0, 48)
-        for r, n in rows:
+
+    @functools.partial(each, nx + 2, looped)
+    def _(p):
+        for r, n in spread(spans, 0, 48) if not looped and p in (0, nx + 1) else spread(spans, 8, 32):
             f = pad_ref[p + 1, r:r + n, :]
             e = ze_ref[p, r:r + n, :]
             around = (pad_ref[p, r:r + n, :] + pad_ref[p + 2, r:r + n, :]
                       + pad_ref[p + 1, r - 1:r - 1 + n, :] + pad_ref[p + 1, r + 1:r + 1 + n, :]
                       + g.before(f, e) + g.after(f, e))
             chem_ref[p, r:r + n, :] = chem_of(f, mob_ref[p, r:r + n, :], around, mean)
-        if inside:
-            for r, n in spread(spans, 0, 48):
-                f = pad_ref[p + 1, r:r + n, :]
-                e = ze_ref[p, r:r + n, :]
-                around = (ze_ref[p - 1, r:r + n, :] + ze_ref[p + 1, r:r + n, :]
-                          + ze_ref[p, r - 1:r - 1 + n, :] + ze_ref[p, r + 1:r + 1 + n, :]
-                          + g.before(e, f) + g.after(e, f))
-                cheme_ref[p - 1, r - OFF:r - OFF + n, :] = chem_of(
-                    e, mobe_ref[p - 1, r - OFF:r - OFF + n, :], around, mean)
+
+    @functools.partial(each, nx, looped)
+    def _(x):
+        p = x + 1
+        for r, n in spread(spans, 0, 48):
+            f = pad_ref[p + 1, r:r + n, :]
+            e = ze_ref[p, r:r + n, :]
+            around = (ze_ref[p - 1, r:r + n, :] + ze_ref[p + 1, r:r + n, :]
+                      + ze_ref[p, r - 1:r - 1 + n, :] + ze_ref[p, r + 1:r + 1 + n, :]
+                      + g.before(e, f) + g.after(e, f))
+            cheme_ref[x, r - OFF:r - OFF + n, :] = chem_of(
+                e, mobe_ref[x, r - OFF:r - OFF + n, :], around, mean)
 
 
 def flux_of(g, x, r, n, mob_ref, mobe_ref, chem_ref, cheme_ref):
@@ -355,21 +373,24 @@
     return kernel
 
 
-def potentials_b(g, mean, a2_ref, ae2_ref, others, scratch, spans):
+def potentials_b(g, mean, a2_ref, ae2_ref, others, scratch, spans, looped):
     f_ref, lo_ref, hi_ref, yr_ref, zr_ref = others
     pad_ref, ze_ref, mob_ref, mobe_ref, chem_ref, cheme_ref = scratch
     nx, nz = g.nx, g.nz
     fill(B_CODE, f_ref, lo_ref, hi_ref, yr_ref, zr_ref, pad_ref, ze_ref, spans)
-    for p in range(nx + 2):
-        for r, n in spread(spans, 8, 32) if 1 <= p <= nx else spread(spans, 0, 48):
+
+    @functools.partial(each, nx + 2, looped)
+    def _(p):
+        for r, n in spread(spans, 8, 32):
             a = a2_ref[p, r:r + n, :]
             mob_ref[p, r:r + n, :] = a * a
+
     for r, n in spread(spans, 0, 48):
         a = ae2_ref[r - OFF:r - OFF + n, :]
         a = a * a
         for x in range(nx):
             mobe_ref[x, r - OFF:r - OFF + n, :] = pltpu.roll(a, nz - 32 * x, 1) if x else a
-    chemistry(g, pad_ref, mob_ref, mobe_ref, ze_ref, chem_ref, cheme_ref, mean, spans)
+    chemistry(g, pad_ref, mob_ref, mobe_ref, ze_ref, chem_ref, cheme_ref, mean, spans, looped)
 
 
 def finish_b(g, mean, x, r, n, labels, a2_ref, scratch):
@@ -395,19 +416,13 @@
 
 
 def edge_b(ride_y, ride_z):
-    def kernel(f_ref, a2_ref, ae2_ref, lo_ref, hi_ref, yr_ref, zr_ref, yp_ref, l_hbm, edge_ref, *rest):
-        *scratch, pool_scr, l_ref, l_sem = rest
+    def kernel(f_ref, a2_ref, ae2_ref, lo_ref, hi_ref, yr_ref, zr_ref, yp_ref, l_ref, edge_ref, *rest):
+        *scratch, pool_scr = rest
         nx, ny, nz = f_ref.shape
         spans = [(0, 16), (ny - 16, ny)]
-        loads = [pltpu.make_async_copy(l_hbm.at[:, a:b, :], l_ref.at[:, 16 * k:16 * k + 16, :], l_sem.at[k])
-                 for k, (a, b) in enumerate(spans)]
-        for c in loads:
-            c.start()
         g = Geometry(nx, ny, nz)
         mean = weighted_mean(yp_ref, yr_ref, zr_ref, ride_y, ride_z)
-        potentials_b(g, mean, a2_ref, ae2_ref, (f_ref, lo_ref, hi_ref, yr_ref, zr_ref), scratch, spans)
-        for c in loads:
-            c.wait()
+        potentials_b(g, mean, a2_ref, ae2_ref, (f_ref, lo_ref, hi_ref, yr_ref, zr_ref), scratch, spans, False)
         for k, (a, b) in enumerate(spans):
             s = slice(16 * k, 16 * k + 16)
             pooled = [None] * 4
@@ -432,26 +447,32 @@
         labels_in.start()
         g = Geometry(nx, ny, nz)
         mean = weighted_mean(yp_ref, yr_ref, zr_ref, ride_y, ride_z)
-        potentials_b(g, mean, a2_ref, ae2_ref, (f_ref, lo_ref, hi_ref, yr_ref, zr_ref), scratch, [(0, ny)])
+        potentials_b(g, mean, a2_ref, ae2_ref, (f_ref, lo_ref, hi_ref, yr_ref, zr_ref), scratch, [(0, ny)], True)
         labels_in.wait()
-        copies = []
-        for k, (r, n) in enumerate(chunks(OFF, OFF + ny, 48)):
-            s = slice(r - OFF, r - OFF + n)
-            pooled = [None] * 4
-            for x in range(nx):
+        outs = ((f3_ref, f3_hbm), (dmg_ref, dmg_hbm), (flux_ref, flux_hbm))
+
+        def out_copy(i, x):
+            return pltpu.make_async_copy(outs[i][0].at[x], outs[i][1].at[x], sems.at[i, x])
+
+        pool_scr[...] = jnp.zeros(pool_scr.shape, F32)
+
+        @functools.partial(each, nx, True)
+        def _(x):
+            for r, n in chunks(OFF, OFF + ny, 48):
+                s = slice(r - OFF, r - OFF + n)
                 flux, values = finish_b(g, mean, x, r, n, l_ref[x, s, :], a2_ref, scratch)
                 f3_ref[x, s, :] = values[0]
                 dmg_ref[x, s, :] = values[1]
                 flux_ref[x, s, :] = flux
-                pooled = [v if p is None else p + v for p, v in zip(pooled, values)]
-            for i in range(4):
-                pool_scr[i, s, :] = pooled[i]
-            for i, (src, dst) in enumerate(((f3_ref, f3_hbm), (dmg_ref, dmg_hbm), (flux_ref, flux_hbm))):
-                copies.append(pltpu.make_async_copy(src.at[:, s, :], dst.at[:, s, :], sems.at[i, k]))
-                copies[-1].start()
+                for i in range(4):
+                    pool_scr[i, s, :] = pool_scr[i, s, :] + values[i]
+            for i in range(3):
+                out_copy(i, x).start()
+
         pool_ref[...] = pool_rows(pool_scr, ny // 4, nz).astype(BF16)
-        for c in copies:
-            c.wait()
+        for x in range(nx):
+            for i in range(3):
+                out_copy(i, x).wait()
     return kernel
 
 
@@ -519,9 +540,10 @@
     concentration, damage, labels = (
         pltpu.with_memory_space_constraint(v, pltpu.HBM) for v in (concentration, damage, labels))
     tall = 3 * ny + 16
-    f, amp, lo, hi, sums = call(
+    f, amp, lo, hi, sums, edge_labels = call(
         first_kernel,
-        [(block, F32), (block, F32), ((tall, nz), I16), ((tall, nz), I16), ((8, nz), F32)],
+        [(block, F32), (block, F32), ((tall, nz), I16), ((tall, nz), I16), ((8, nz), F32),
+         ((nx, 32, nz), jnp.int32)],
         concentration, damage, labels,
         in_specs=[HBM] * 3,
         scratch=[pltpu.VMEM(block, F32), pltpu.VMEM(block, jnp.int32), pltpu.SemaphoreType.DMA((3, nx))])
@@ -544,19 +566,18 @@
     yr = both_sides(ypay, "gy")
     (zpay,) = call(pack_z(B_CODE, ride_y, False), [(packed, F32)], f, lo, hi, yr, ypay)
     zr = z_neighbour(zpay, "gz")
-    last = (f, a2, ae2, lo, hi, yr, zr, ypay, labels)
+    last = (f, a2, ae2, lo, hi, yr, zr, ypay)
     (edge,) = call(
-        edge_b(ride_y, ride_z), [((2, 16, nz), BF16)], *last, in_specs=[VMEM] * 8 + [HBM],
-        scratch=scratch + [
-            pltpu.VMEM((4, 32, nz), F32), pltpu.VMEM((nx, 32, nz), jnp.int32), pltpu.SemaphoreType.DMA((2,))])
+        edge_b(ride_y, ride_z), [((2, 16, nz), BF16)], *last, edge_labels,
+        scratch=scratch + [pltpu.VMEM((4, 32, nz), F32)])
     fraction, damage_field, flux_sum, pooled = call(
         step_b(ride_y, ride_z),
-        [(block, F32), (block, F32), (block, F32), ((ny // 4, nz), BF16)], *last,
+        [(block, F32), (block, F32), (block, F32), ((ny // 4, nz), BF16)], *last, labels,
         in_specs=[VMEM] * 8 + [HBM], out_specs=[HBM] * 3 + [VMEM],
         scratch=scratch + [
             pltpu.VMEM((4, ny, nz), F32), pltpu.VMEM(block, jnp.int32),
             pltpu.VMEM(block, F32), pltpu.VMEM(block, F32), pltpu.VMEM(block, F32),
-            pltpu.SemaphoreType.DMA, pltpu.SemaphoreType.DMA((3, len(chunks(OFF, OFF + ny, 48))))])
+            pltpu.SemaphoreType.DMA, pltpu.SemaphoreType.DMA((3, nx))])
     ids = jnp.broadcast_to(jnp.stack([lax.axis_index(a) for a in ("gx", "gy", "gz")])[:, None], (3, nz))
     crack_score = detector(pooled, edge, ids, weights + (b_first[None], b_second[None], b_third[None]), ny // 4, nz // 4)
     return (fraction, damage_field, flux_sum, crack_score)

time: 60 us -> 58.9 us (0.982)
  Pallas kernels: 14.5 us -> 13.6 us
    pallas_call x11, Pallas kernels: 14.5 us -> 13.6 us  [call(): pl.pallas_call(kernel, in_specs=in_specs or [VMEM] * len(args), out_specs...]
where the time goes in v11:
time: 58.9 us; the launch traced here: 58.6 us
  waiting for transfers between devices  21.2 us (36%)
  starting transfers between devices  19.4 us (33%)
  Pallas kernels  13.6 us (23%)
  local copies, waits for them, and re-layouts  2.93 us (5%)
  between operations  1.44 us (2%)
    pallas_call x11, Pallas kernels, call(): pl.pallas_call(kernel, in_specs=in_specs or [VMEM] * len(args), out_specs...  13.6 us
    ppermute x2, waiting for transfers between devices, start(): return (sums, lax.ppermute(sums, 'gx', ring('gx', 2)))  9.93 us
    ppermute x2, starting transfers between devices, x_sides(): lax.ppermute(lo, 'gx', ring('gx', -1))  5.32 us
    ppermute x3, waiting for transfers between devices, both_sides(): return lax.ppermute(pay, axis, ring(axis, 1))  4.67 us
    ppermute x3, starting transfers between devices, both_sides(): return lax.ppermute(pay, axis, ring(axis, 1))  4.62 us
    ppermute x6, waiting for transfers between devices, z_neighbour(): return lax.ppermute(pay, axis, ring(axis, 1))  4.26 us
    ppermute x3, starting transfers between devices, detector(): own = [plane] + [lax.ppermute(plane, 'gx', ring('gx', s)) for s in shifts]  4 us
    ppermute x2, starting transfers between devices, x_sides(): lax.ppermute(hi, 'gx', ring('gx', 1))  3.72 us
  transfers between devices with their start and end apart: 18, of which 9 were waited for; matrix products, arithmetic and copies ran while one was open for 5% of the time, Pallas kernels for 8%

profile of v11, /device:TPU:0, one launch (start us, length us, event | category | flops | bytes accessed | tf_op | source)
XLA Modules:
  0.0 58.6 jit_solution(2595794411216150804)
XLA Ops:
  0.6 1.6 %shard_map.120 = (f32[4,240,128]{2,1,0:T(8,128)S(1)}, f32[4,240,128]{2,1,0:T(8,128)S(1)}, s16[736,128]{1,0:T(8,128)(2,1)S(1)}, s16[736,128]{1,0:T(8,128)(2,1)S(1...) custom-call(f32[4,240,128]{2,1,0:T(8,128)} %c_hbm.1, f32[4,240,128]{2,1,0:T(8,128)} %d_hbm.1, s32[4,240,128]{2,1,0:T(8,128)} %l_hbm.3), custom_call_target="tpu_custom_call" | custom-call | tf_op jit(solution)/shard_map/pallas_call | solution.py:73
  2.3 3.1 %collective-permute-start = (s16[736,128]{1,0:T(8,128)(2,1)S(1)}, s16[736,128]{1,0:T(8,128)(2,1)S(1)}, u32[]{:S(2)}, u32[]{:S(2)}) collective-permute-start(s16[736,128]{1,0:T(8,128)(2,1)S(1)} %get-tuple-element.31), channel_id=1, source_target_pairs={{0,4},{4,8},{8,12},{12,0},{1,5},{5,9},{9,13},{13,1},{2,6},{6,10},{... | collective-permute-start | bytes 565256 | tf_op jit(solution)/shard_map/ppermute | solution.py:515
  5.3 2.1 %collective-permute-start.1 = (s16[736,128]{1,0:T(8,128)(2,1)S(1)}, s16[736,128]{1,0:T(8,128)(2,1)S(1)}, u32[]{:S(2)}, u32[]{:S(2)}) collective-permute-start(s16[736,128]{1,0:T(8,128)(2,1)S(1)} %get-tuple-element.32), channel_id=1, source_target_pairs={{0,12},{4,0},{8,4},{12,8},{1,13},{5,1},{9,5},{13,9},{2,14},{6,2},{... | collective-permute-start | bytes 565256 | tf_op jit(solution)/shard_map/ppermute | solution.py:515
  7.4 0.9 %collective-permute-start.2 = (f32[8,128]{1,0:T(8,128)S(1)}, f32[8,128]{1,0:T(8,128)S(1)}, u32[]{:S(2)}, u32[]{:S(2)}) collective-permute-start(f32[8,128]{1,0:T(8,128)S(1)} %get-tuple-element.33.refs_4_), channel_id=1, source_target_pairs={{0,8},{4,12},{8,0},{12,4},{1,9},{5,13},{9,1},{13,5},{2,10},{6,14},... | collective-permute-start | bytes 12296 | tf_op jit(solution)/shard_map/ppermute | solution.py:533
  8.4 0.8 %copy.16 = bf16[27,4,16]{2,1,0:T(4,128)(2,1)S(1)} copy(bf16[27,4,16]{0,1,2:T(4,128)(2,1)} %bitcast.27) | data formatting | bytes 6912 | tf_op jit(solution)/shard_map/transpose | solution.py:656
  9.2 1.0 %copy.17 = bf16[27,16,16]{2,1,0:T(8,128)(2,1)S(1)} copy(bf16[27,16,16]{0,1,2:T(8,128)(2,1)} %bitcast.24) | data formatting | bytes 27648 | tf_op jit(solution)/shard_map/transpose | solution.py:657
  10.2 0.8 %copy.18 = bf16[27,1,16]{2,0,1:T(8,128)(2,1)S(1)} copy(bf16[27,1,16]{0,2,1:T(8,128)(2,1)} %param.16) | data formatting | bytes 1728 | tf_op args[7]
  11.1 0.1 copy.19
  11.2 5.1 %collective-permute-done.2.refs_5_ = f32[8,128]{1,0:T(8,128)S(1)} collective-permute-done((f32[8,128]{1,0:T(8,128)S(1)}, f32[8,128]{1,0:T(8,128)S(1)}, u32[]{:S(2)}, u32[]{:S(2)}) %collective-permute-start.2) | collective-permute-done | bytes 4128 | tf_op jit(solution)/shard_map/ppermute | solution.py:533
  16.3 0.0 collective-permute-done.refs_2_.lo_ref
  16.3 1.6 %collective-permute-start.3 = (f32[2,24,128]{2,1,0:T(8,128)S(1)}, f32[2,24,128]{2,1,0:T(8,128)S(1)}, u32[]{:S(2)}, u32[]{:S(2)}) collective-permute-start(f32[2,24,128]{2,1,0:T(8,128)S(1)} %shard_map.121.refs_5_.yp_ref), channel_id=1, source_target_pairs={{0,2},{2,0},{1,3},{3,1},{4,6},{6,4},{5,7},{7,5},{8,10},{10,8},{9,1... | collective-permute-start | bytes 73736 | tf_op jit(solution)/shard_map/ppermute | solution.py:497
  17.9 2.3 %collective-permute-done.3.refs_4_.yr_ref = f32[2,24,128]{2,1,0:T(8,128)S(1)} collective-permute-done((f32[2,24,128]{2,1,0:T(8,128)S(1)}, f32[2,24,128]{2,1,0:T(8,128)S(1)}, u32[]{:S(2)}, u32[]{:S(2)}) %collective-permute-start.3) | collective-permute-done | bytes 24608 | tf_op jit(solution)/shard_map/ppermute | solution.py:497
  20.2 0.3 shard_map.122
  20.6 0.1 collective-permute-start.4
  20.6 1.5 %collective-permute-done.4.zr_ref = f32[2,272,128]{2,1,0:T(8,128)S(1)} collective-permute-done((f32[2,272,128]{2,1,0:T(8,128)S(1)}, f32[2,272,128]{2,1,0:T(8,128)S(1)}, u32[]{:S(2)}, u32[]{:S(2)}) %collective-permute-start.4) | collective-permute-done | bytes 278560 | tf_op jit(solution)/shard_map/ppermute | solution.py:503
  22.2 2.2 %shard_map.123 = (f32[4,240,128]{2,1,0:T(8,128)S(1)}, f32[6,272,128]{2,1,0:T(8,128)S(1)}, f32[240,128]{1,0:T(8,128)S(1)}, s16[496,128]{1,0:T(8,128)(2,1)S(1)}, s...) custom-call(f32[4,240,128]{2,1,0:T(8,128)S(1)} %get-tuple-element.29.refs_0_.f_ref, ...), custom_call_target="tpu_custom_call" | custom-call | tf_op jit(solution)/shard_map/pallas_call | solution.py:73
  24.4 0.6 %collective-permute-start.5 = (s16[496,128]{1,0:T(8,128)(2,1)S(1)}, s16[496,128]{1,0:T(8,128)(2,1)S(1)}, u32[]{:S(2)}, u32[]{:S(2)}) collective-permute-start(s16[496,128]{1,0:T(8,128)(2,1)S(1)} %get-tuple-element.37), channel_id=1, source_target_pairs={{0,4},{4,8},{8,12},{12,0},{1,5},{5,9},{9,13},{13,1},{2,6},{6,10},{... | collective-permute-start | bytes 380936 | tf_op jit(solution)/shard_map/ppermute | solution.py:515
  25.1 3.2 %collective-permute-start.6 = (s16[496,128]{1,0:T(8,128)(2,1)S(1)}, s16[496,128]{1,0:T(8,128)(2,1)S(1)}, u32[]{:S(2)}, u32[]{:S(2)}) collective-permute-start(s16[496,128]{1,0:T(8,128)(2,1)S(1)} %get-tuple-element.38), channel_id=1, source_target_pairs={{0,12},{4,0},{8,4},{12,8},{1,13},{5,1},{9,5},{13,9},{2,14},{6,2},{... | collective-permute-start | bytes 380936 | tf_op jit(solution)/shard_map/ppermute | solution.py:515
  28.3 0.0 collective-permute-start.7
  28.3 4.9 %collective-permute-done.7.refs_4_ = f32[8,128]{1,0:T(8,128)S(1)} collective-permute-done((f32[8,128]{1,0:T(8,128)S(1)}, f32[8,128]{1,0:T(8,128)S(1)}, u32[]{:S(2)}, u32[]{:S(2)}) %collective-permute-start.7) | collective-permute-done | bytes 4128 | tf_op jit(solution)/shard_map/ppermute | solution.py:533
  33.2 0.0 collective-permute-done.5.refs_1_.lo_ref
  33.2 0.0 collective-permute-done.6.refs_2_.hi_ref
  33.2 0.0 copy-start
  33.2 0.0 copy-start.1
  33.2 1.6 %collective-permute-start.8 = (f32[2,24,128]{2,1,0:T(8,128)S(1)}, f32[2,24,128]{2,1,0:T(8,128)S(1)}, u32[]{:S(2)}, u32[]{:S(2)}) collective-permute-start(f32[2,24,128]{2,1,0:T(8,128)S(1)} %shard_map.124.refs_4_.yp_ref), channel_id=1, source_target_pairs={{0,2},{2,0},{1,3},{3,1},{4,6},{6,4},{5,7},{7,5},{8,10},{10,8},{9,1... | collective-permute-start | bytes 73736 | tf_op jit(solution)/shard_map/ppermute | solution.py:497
  34.8 2.3 %collective-permute-done.8.refs_3_.yr_ref = f32[2,24,128]{2,1,0:T(8,128)S(1)} collective-permute-done((f32[2,24,128]{2,1,0:T(8,128)S(1)}, f32[2,24,128]{2,1,0:T(8,128)S(1)}, u32[]{:S(2)}, u32[]{:S(2)}) %collective-permute-start.8) | collective-permute-done | bytes 24608 | tf_op jit(solution)/shard_map/ppermute | solution.py:497
  37.1 0.2 shard_map.125
  37.3 0.1 collective-permute-start.9
  37.4 1.5 %collective-permute-done.9.zr_ref = f32[2,272,128]{2,1,0:T(8,128)S(1)} collective-permute-done((f32[2,272,128]{2,1,0:T(8,128)S(1)}, f32[2,272,128]{2,1,0:T(8,128)S(1)}, u32[]{:S(2)}, u32[]{:S(2)}) %collective-permute-start.9) | collective-permute-done | bytes 278560 | tf_op jit(solution)/shard_map/ppermute | solution.py:503
  38.9 0.6 %shard_map.127 = bf16[2,16,128]{2,1,0:T(8,128)(2,1)S(1)} custom-call(f32[4,240,128]{2,1,0:T(8,128)S(1)} %get-tuple-element.34.refs_0_.f_ref, f32[6,272,128]{2,1,0:T(8,128)S(1)} %get-tuple-element.35.a2_ref, f32[240,128]{1,0:T(8,128)S(1)} %get-tuple-element.36.ae2_ref, s16[496,128]{1,0:T(8,128)(2,1)S(1)} %collective-permute-done.5.refs_1_.lo_ref, ...), custom_call_target="tpu_custom_call" | custom-call | tf_op jit(solution)/shard_map/pallas_call | solution.py:73
  39.6 1.5 %collective-permute-start.10 = (bf16[2,16,128]{2,1,0:T(8,128)(2,1)S(1)}, bf16[2,16,128]{2,1,0:T(8,128)(2,1)S(1)}, u32[]{:S(2)}, u32[]{:S(2)}) collective-permute-start(bf16[2,16,128]{2,1,0:T(8,128)(2,1)S(1)} %shard_map.127), channel_id=1, source_target_pairs={{0,2},{2,0},{1,3},{3,1},{4,6},{6,4},{5,7},{7,5},{8,10},{10,8},{9,1... | collective-permute-start | bytes 24584 | tf_op jit(solution)/shard_map/ppermute | solution.py:497
  41.1 0.1 pad_add_fusion
  41.1 3.7 %shard_map.126 = (f32[4,240,128]{2,1,0:T(8,128)}, f32[4,240,128]{2,1,0:T(8,128)}, f32[4,240,128]{2,1,0:T(8,128)}, bf16[60,128]{1,0:T(8,128)(2,1)S(1)}) custom-call(f32[4,240,128]{2,1,0:T(8,128)S(1)} %get-tuple-element.34.refs_0_.f_ref, f32[6,272,128]{2,1,0:T(8,128)S(1)} %get-tuple-element.35.a2_ref, f32[240,128]{1,0:T(8,128)S(1)} %get-tuple-element.36.ae2_ref, ...), custom_call_target="tpu_custom_call" | custom-call | tf_op jit(solution)/shard_map/pallas_call | solution.py:73
  44.8 0.0 collective-permute-done.10.yr_ref
  44.8 0.1 broadcast_in_dim.15.ids_ref.refs_0_
  45.0 2.0 %collective-permute-start.11 = (bf16[80,128]{1,0:T(8,128)(2,1)S(1)}, bf16[80,128]{1,0:T(8,128)(2,1)S(1)}, u32[]{:S(2)}, u32[]{:S(2)}) collective-permute-start(bf16[80,128]{1,0:T(8,128)(2,1)S(1)} %shard_map.128.plane_ref.refs_1_), channel_id=1, source_target_pairs={{0,4},{4,8},{8,12},{12,0},{1,5},{5,9},{9,13},{13,1},{2,6},{6,10},{... | collective-permute-start | bytes 61448 | tf_op jit(solution)/shard_map/ppermute | solution.py:771
  47.0 1.9 %collective-permute-start.12 = (bf16[80,128]{1,0:T(8,128)(2,1)S(1)}, bf16[80,128]{1,0:T(8,128)(2,1)S(1)}, u32[]{:S(2)}, u32[]{:S(2)}) collective-permute-start(bf16[80,128]{1,0:T(8,128)(2,1)S(1)} %shard_map.128.plane_ref.refs_1_), channel_id=1, source_target_pairs={{0,12},{4,0},{8,4},{12,8},{1,13},{5,1},{9,5},{13,9},{2,14},{6,2},{... | collective-permute-start | bytes 61448 | tf_op jit(solution)/shard_map/ppermute | solution.py:771
  48.8 0.1 collective-permute-start.13
  49.6 0.1 collective-permute-start.14
  49.7 0.9 %shard_map.129 = (bf16[3,768,640]{2,1,0:T(8,128)(2,1)S(1)}, bf16[3,768,128]{2,1,0:T(8,128)(2,1)S(1)}, bf16[3,640,128]{2,1,0:T(8,128)(2,1)S(1)}, f32[8,640]{1,0:T(8,128)S(1)}) custom-call(bf16[432,16]{1,0:T(8,128)(2,1)S(1)} %bitcast.19, bf16[432,16]{1,0:T(8,128)(2,1)S(1)} %bitcast.17, bf16[144,3]{1,0:T(8,128)(2,1)S(1)} %bitcast.21, f32[1,16]{1,0:T(1,128)S(1)} %bitcast.22, ...), custom_call_target="tpu_custom_call" | custom-call | tf_op jit(solution)/shard_map/pallas_call | solution.py:73
  50.6 0.1 collective-permute-done.11.refs_2_
  50.7 0.5 collective-permute-start.15
  51.2 0.0 collective-permute-done.12.refs_3_
  51.2 0.1 collective-permute-start.16
  51.3 2.2 %collective-permute-done.13.refs_4_ = bf16[80,128]{1,0:T(8,128)(2,1)S(1)} collective-permute-done((bf16[80,128]{1,0:T(8,128)(2,1)S(1)}, bf16[80,128]{1,0:T(8,128)(2,1)S(1)}, u32[]{:S(2)}, u32[]{:S(2)}) %collective-permute-start.13) | collective-permute-done | bytes 20512 | tf_op jit(solution)/shard_map/ppermute | solution.py:771
  53.5 0.0 collective-permute-start.17
  53.5 1.2 %collective-permute-done.17.refs_8_ = bf16[80,128]{1,0:T(8,128)(2,1)S(1)} collective-permute-done((bf16[80,128]{1,0:T(8,128)(2,1)S(1)}, bf16[80,128]{1,0:T(8,128)(2,1)S(1)}, u32[]{:S(2)}, u32[]{:S(2)}) %collective-permute-start.17) | collective-permute-done | bytes 20512 | tf_op jit(solution)/shard_map/ppermute | solution.py:503
  54.7 3.9 %shard_map.130 = f32[1,32,60]{2,1,0:T(8,128)} custom-call(s32[3,128]{1,0:T(4,128)S(1)} %broadcast_in_dim.15.ids_ref.refs_0_, bf16[80,128]{1,0:T(8,128)(2,1)S(1)} %shard_map.128.plane_ref.refs_1_, bf16[80,128]{1,0:T(8,128)(2,1)S(1)} %collective-permute-done.11.refs_2_, bf16[80,128]{1,0:T(8,128)(2,1)S(1)} %collective-permute-done.12.refs_3_, ...), custom_call_target="tpu_custom_call" | custom-call | tf_op jit(solution)/shard_map/pallas_call | solution.py:73
  (11 shorter events, 0.1 us)
Async XLA Ops:
  2.3 14.0 %collective-permute-start = (s16[736,128]{1,0:T(8,128)(2,1)S(1)}, s16[736,128]{1,0:T(8,128)(2,1)S(1)}, u32[]{:S(2)}, u32[]{:S(2)}) collective-permute-start(s16[736,128]{1,0:T(8,128)(2,1)S(1)} %get-tuple-element.31), channel_id=1, source_target_pairs={{0,4},{4,8},{8,12},{12,0},{1,5},{5,9},{9,13},{13,1},{2,6},{6,10},{... | collective-permute-start | bytes 565256 | tf_op jit(solution)/shard_map/ppermute | solution.py:515
  5.3 10.9 %collective-permute-start.1 = (s16[736,128]{1,0:T(8,128)(2,1)S(1)}, s16[736,128]{1,0:T(8,128)(2,1)S(1)}, u32[]{:S(2)}, u32[]{:S(2)}) collective-permute-start(s16[736,128]{1,0:T(8,128)(2,1)S(1)} %get-tuple-element.32), channel_id=1, source_target_pairs={{0,12},{4,0},{8,4},{12,8},{1,13},{5,1},{9,5},{13,9},{2,14},{6,2},{... | collective-permute-start | bytes 565256 | tf_op jit(solution)/shard_map/ppermute | solution.py:515
  7.4 8.8 %collective-permute-start.2 = (f32[8,128]{1,0:T(8,128)S(1)}, f32[8,128]{1,0:T(8,128)S(1)}, u32[]{:S(2)}, u32[]{:S(2)}) collective-permute-start(f32[8,128]{1,0:T(8,128)S(1)} %get-tuple-element.33.refs_4_), channel_id=1, source_target_pairs={{0,8},{4,12},{8,0},{12,4},{1,9},{5,13},{9,1},{13,5},{2,10},{6,14},... | collective-permute-start | bytes 12296 | tf_op jit(solution)/shard_map/ppermute | solution.py:533
  16.3 3.9 %collective-permute-start.3 = (f32[2,24,128]{2,1,0:T(8,128)S(1)}, f32[2,24,128]{2,1,0:T(8,128)S(1)}, u32[]{:S(2)}, u32[]{:S(2)}) collective-permute-start(f32[2,24,128]{2,1,0:T(8,128)S(1)} %shard_map.121.refs_5_.yp_ref), channel_id=1, source_target_pairs={{0,2},{2,0},{1,3},{3,1},{4,6},{6,4},{5,7},{7,5},{8,10},{10,8},{9,1... | collective-permute-start | bytes 73736 | tf_op jit(solution)/shard_map/ppermute | solution.py:497
  20.6 1.6 %collective-permute-start.4 = (f32[2,272,128]{2,1,0:T(8,128)S(1)}, f32[2,272,128]{2,1,0:T(8,128)S(1)}, u32[]{:S(2)}, u32[]{:S(2)}) collective-permute-start(f32[2,272,128]{2,1,0:T(8,128)S(1)} %shard_map.122), channel_id=1, source_target_pairs={{0,1},{1,0},{2,3},{3,2},{4,5},{5,4},{6,7},{7,6},{8,9},{9,8},{10,11... | collective-permute-start | bytes 835592 | tf_op jit(solution)/shard_map/ppermute | solution.py:503
  24.4 8.7 %collective-permute-start.5 = (s16[496,128]{1,0:T(8,128)(2,1)S(1)}, s16[496,128]{1,0:T(8,128)(2,1)S(1)}, u32[]{:S(2)}, u32[]{:S(2)}) collective-permute-start(s16[496,128]{1,0:T(8,128)(2,1)S(1)} %get-tuple-element.37), channel_id=1, source_target_pairs={{0,4},{4,8},{8,12},{12,0},{1,5},{5,9},{9,13},{13,1},{2,6},{6,10},{... | collective-permute-start | bytes 380936 | tf_op jit(solution)/shard_map/ppermute | solution.py:515
  25.1 8.1 %collective-permute-start.6 = (s16[496,128]{1,0:T(8,128)(2,1)S(1)}, s16[496,128]{1,0:T(8,128)(2,1)S(1)}, u32[]{:S(2)}, u32[]{:S(2)}) collective-permute-start(s16[496,128]{1,0:T(8,128)(2,1)S(1)} %get-tuple-element.38), channel_id=1, source_target_pairs={{0,12},{4,0},{8,4},{12,8},{1,13},{5,1},{9,5},{13,9},{2,14},{6,2},{... | collective-permute-start | bytes 380936 | tf_op jit(solution)/shard_map/ppermute | solution.py:515
  28.3 4.9 %collective-permute-start.7 = (f32[8,128]{1,0:T(8,128)S(1)}, f32[8,128]{1,0:T(8,128)S(1)}, u32[]{:S(2)}, u32[]{:S(2)}) collective-permute-start(f32[8,128]{1,0:T(8,128)S(1)} %get-tuple-element.39.refs_3_), channel_id=1, source_target_pairs={{0,8},{4,12},{8,0},{12,4},{1,9},{5,13},{9,1},{13,5},{2,10},{6,14},... | collective-permute-start | bytes 12296 | tf_op jit(solution)/shard_map/ppermute | solution.py:533
  33.2 16.5 %copy-start = (f32[16]{0:T(128)S(1)}, f32[16]{0:T(128)}, u32[]{:S(2)}) copy-start(f32[16]{0:T(128)} %param.13) | copy-start | bytes 196
  33.2 16.5 %copy-start.1 = (f32[16]{0:T(128)S(1)}, f32[16]{0:T(128)}, u32[]{:S(2)}) copy-start(f32[16]{0:T(128)} %param.15) | copy-start | bytes 196
  33.2 3.9 %collective-permute-start.8 = (f32[2,24,128]{2,1,0:T(8,128)S(1)}, f32[2,24,128]{2,1,0:T(8,128)S(1)}, u32[]{:S(2)}, u32[]{:S(2)}) collective-permute-start(f32[2,24,128]{2,1,0:T(8,128)S(1)} %shard_map.124.refs_4_.yp_ref), channel_id=1, source_target_pairs={{0,2},{2,0},{1,3},{3,1},{4,6},{6,4},{5,7},{7,5},{8,10},{10,8},{9,1... | collective-permute-start | bytes 73736 | tf_op jit(solution)/shard_map/ppermute | solution.py:497
  37.3 1.6 %collective-permute-start.9 = (f32[2,272,128]{2,1,0:T(8,128)S(1)}, f32[2,272,128]{2,1,0:T(8,128)S(1)}, u32[]{:S(2)}, u32[]{:S(2)}) collective-permute-start(f32[2,272,128]{2,1,0:T(8,128)S(1)} %shard_map.125), channel_id=1, source_target_pairs={{0,1},{1,0},{2,3},{3,2},{4,5},{5,4},{6,7},{7,6},{8,9},{9,8},{10,11... | collective-permute-start | bytes 835592 | tf_op jit(solution)/shard_map/ppermute | solution.py:503
  39.6 5.3 %collective-permute-start.10 = (bf16[2,16,128]{2,1,0:T(8,128)(2,1)S(1)}, bf16[2,16,128]{2,1,0:T(8,128)(2,1)S(1)}, u32[]{:S(2)}, u32[]{:S(2)}) collective-permute-start(bf16[2,16,128]{2,1,0:T(8,128)(2,1)S(1)} %shard_map.127), channel_id=1, source_target_pairs={{0,2},{2,0},{1,3},{3,1},{4,6},{6,4},{5,7},{7,5},{8,10},{10,8},{9,1... | collective-permute-start | bytes 24584 | tf_op jit(solution)/shard_map/ppermute | solution.py:497
  45.0 5.7 %collective-permute-start.11 = (bf16[80,128]{1,0:T(8,128)(2,1)S(1)}, bf16[80,128]{1,0:T(8,128)(2,1)S(1)}, u32[]{:S(2)}, u32[]{:S(2)}) collective-permute-start(bf16[80,128]{1,0:T(8,128)(2,1)S(1)} %shard_map.128.plane_ref.refs_1_), channel_id=1, source_target_pairs={{0,4},{4,8},{8,12},{12,0},{1,5},{5,9},{9,13},{13,1},{2,6},{6,10},{... | collective-permute-start | bytes 61448 | tf_op jit(solution)/shard_map/ppermute | solution.py:771
  47.0 4.2 %collective-permute-start.12 = (bf16[80,128]{1,0:T(8,128)(2,1)S(1)}, bf16[80,128]{1,0:T(8,128)(2,1)S(1)}, u32[]{:S(2)}, u32[]{:S(2)}) collective-permute-start(bf16[80,128]{1,0:T(8,128)(2,1)S(1)} %shard_map.128.plane_ref.refs_1_), channel_id=1, source_target_pairs={{0,12},{4,0},{8,4},{12,8},{1,13},{5,1},{9,5},{13,9},{2,14},{6,2},{... | collective-permute-start | bytes 61448 | tf_op jit(solution)/shard_map/ppermute | solution.py:771
  48.8 4.7 %collective-permute-start.13 = (bf16[80,128]{1,0:T(8,128)(2,1)S(1)}, bf16[80,128]{1,0:T(8,128)(2,1)S(1)}, u32[]{:S(2)}, u32[]{:S(2)}) collective-permute-start(bf16[80,128]{1,0:T(8,128)(2,1)S(1)} %shard_map.128.plane_ref.refs_1_), channel_id=1, source_target_pairs={{0,8},{4,12},{8,0},{12,4},{1,9},{5,13},{9,1},{13,5},{2,10},{6,14},... | collective-permute-start | bytes 61448 | tf_op jit(solution)/shard_map/ppermute | solution.py:771
  49.6 3.9 %collective-permute-start.14 = (bf16[80,128]{1,0:T(8,128)(2,1)S(1)}, bf16[80,128]{1,0:T(8,128)(2,1)S(1)}, u32[]{:S(2)}, u32[]{:S(2)}) collective-permute-start(bf16[80,128]{1,0:T(8,128)(2,1)S(1)} %shard_map.128.plane_ref.refs_1_), channel_id=1, source_target_pairs={{0,1},{1,0},{2,3},{3,2},{4,5},{5,4},{6,7},{7,6},{8,9},{9,8},{10,11... | collective-permute-start | bytes 61448 | tf_op jit(solution)/shard_map/ppermute | solution.py:503
  50.7 2.8 %collective-permute-start.15 = (bf16[80,128]{1,0:T(8,128)(2,1)S(1)}, bf16[80,128]{1,0:T(8,128)(2,1)S(1)}, u32[]{:S(2)}, u32[]{:S(2)}) collective-permute-start(bf16[80,128]{1,0:T(8,128)(2,1)S(1)} %collective-permute-done.11.refs_2_), channel_id=1, source_target_pairs={{0,1},{1,0},{2,3},{3,2},{4,5},{5,4},{6,7},{7,6},{8,9},{9,8},{10,11... | collective-permute-start | bytes 61448 | tf_op jit(solution)/shard_map/ppermute | solution.py:503
  51.2 2.4 %collective-permute-start.16 = (bf16[80,128]{1,0:T(8,128)(2,1)S(1)}, bf16[80,128]{1,0:T(8,128)(2,1)S(1)}, u32[]{:S(2)}, u32[]{:S(2)}) collective-permute-start(bf16[80,128]{1,0:T(8,128)(2,1)S(1)} %collective-permute-done.12.refs_3_), channel_id=1, source_target_pairs={{0,1},{1,0},{2,3},{3,2},{4,5},{5,4},{6,7},{7,6},{8,9},{9,8},{10,11... | collective-permute-start | bytes 61448 | tf_op jit(solution)/shard_map/ppermute | solution.py:503
  53.5 1.2 %collective-permute-start.17 = (bf16[80,128]{1,0:T(8,128)(2,1)S(1)}, bf16[80,128]{1,0:T(8,128)(2,1)S(1)}, u32[]{:S(2)}, u32[]{:S(2)}) collective-permute-start(bf16[80,128]{1,0:T(8,128)(2,1)S(1)} %collective-permute-done.13.refs_4_), channel_id=1, source_target_pairs={{0,1},{1,0},{2,3},{3,2},{4,5},{5,4},{6,7},{7,6},{8,9},{9,8},{10,11... | collective-permute-start | bytes 61448 | tf_op jit(solution)/shard_map/ppermute | solution.py:503

commit v12 on v11

--- a/solution.py
+++ b/solution.py
@@ -604,19 +604,12 @@
     return jnp.dot(a, b, preferred_element_type=F32)
 
 
-def tile_shift(rb, cb, pz):
-    z_in = rb * 16 // CIN
-    z_in = z_in if z_in < pz + pz // 2 else z_in - 2 * pz
-    return z_in - cb * 8 + 3
-
-
 SHIFTS = tuple(k for k in range(-3, 10) if k % (16 // CIN) == 3)
 
 
 def weight_kernel(w1_ref, w2_ref, w3_ref, b1_ref, b2_ref, b3_ref, plane_ref, t1_ref, t2_ref, t3_ref, bias_ref):
     n1 = bias_ref.shape[1]
-    k1 = t1_ref.shape[1] // 3
-    pz = k1 // (2 * CIN)
+    pz = 128 // CIN
     spread = one_hot(iota((CH, 128), 1) % CH == iota((CH, 128), 0))
     tile1 = mm(w1_ref[...], spread)
     tile2 = mm(w2_ref[...], spread)
@@ -638,13 +631,19 @@
         for j in range(3):
             tap = 9 * i + 3 * j
             known = {k: tile(tile1, tap, 1, step1, k) for k in SHIFTS}
-            for rb in range(k1 // 16):
+            places = [(j * 128 + rb * 16, rb * 16 // CIN) for rb in range(8)]
+            places += [(384 + 32 * j, pz), (384 + (32 * j - 16) % 128, -16 // CIN)]
+            for row, z_in in places:
                 for cb in range(n1 // 128):
-                    t1_ref[i, j * k1 + rb * 16:j * k1 + rb * 16 + 16, cb * 128:(cb + 1) * 128] = known.get(
-                        tile_shift(rb, cb, pz), zero)
-            for rb in range(16):
-                t2_ref[i, j * 256 + rb * 16:j * 256 + rb * 16 + 16, :] = (
-                    tile(tile2, tap, 1, step2, rb) if rb < 10 else zero)
+                    t1_ref[i, row:row + 16, cb * 128:(cb + 1) * 128] = known.get(z_in - cb * 8 + 3, zero)
+            for rb in range(10):
+                row = j * 128 + rb * 16 if rb < 8 else 384 + 32 * j + (rb - 8) * 16
+                t2_ref[i, row:row + 16, :] = tile(tile2, tap, 1, step2, rb)
+        for row in (464, 480):
+            for cb in range(n1 // 128):
+                t1_ref[i, row:row + 16, cb * 128:(cb + 1) * 128] = zero
+        for row in (480, 496):
+            t2_ref[i, row:row + 16, :] = zero
         for rb in range(t3_ref.shape[1] // 16):
             t3_ref[i, rb * 16:rb * 16 + 16, :] = tile(tile3, 3 * i, 1, step3, rb) if rb < pz + 2 else zero
     wide = one_hot(iota((CH, n1), 1) % CH == iota((CH, n1), 0)).astype(F32)
@@ -684,7 +683,7 @@
         own = refs[1:2 + n]
         other = refs[2 + n:3 + 2 * n]
         t1_ref, t2_ref, t3_ref, bias_ref, out_ref = refs[3 + 2 * n:8 + 2 * n]
-        in_ref, lhs1_ref, act1_ref, lhs2_ref, act2_ref, tail_ref = refs[8 + 2 * n:]
+        in_ref, beside_ref, lhs1_ref, act1_ref, lhs2_ref, act2_ref, tail_ref = refs[8 + 2 * n:]
         ix, iy, iz = ids_ref[0:1, 0:1], ids_ref[1:2, 0:1], ids_ref[2:3, 0:1]
         half = own[0].shape[1]
         pz = half // CIN
@@ -696,18 +695,27 @@
             k = 0 if o == 0 else 1 + shifts.index((-o) % x_count) if (-o) % x_count in shifts else None
             if k is None:
                 in_ref[w] = jnp.zeros(in_ref.shape[1:], F32)
+                beside_ref[w] = jnp.zeros(in_ref.shape[1:], F32)
                 continue
             inside = (ix + o >= 0) & (ix + o < x_count)
-            in_ref[w, :, 0:half] = jnp.where(inside, own[k][...].astype(F32), 0.0)
-            in_ref[w, :, half:] = jnp.where(z_ok & inside, other[k][...].astype(F32), 0.0)
-        k1 = 2 * half
+            in_ref[w] = jnp.where(inside, own[k][...].astype(F32), 0.0)
+            beside_ref[w] = jnp.where(z_ok & inside, other[k][...].astype(F32), 0.0)
+        lane = iota((1, 128), 1)
+
+        def shared(parts, first, count):
+            out = parts[0]
+            for j in (1, 2):
+                out = jnp.where(group(lane, j, 128, first, count), pltpu.roll(parts[j], 32 * j, 1), out)
+            return out.astype(BF16)
+
         for w in range(7):
-            for j in range(3):
-                start = TOP - 3 + j
-                lhs1_ref[w, :, j * k1:(j + 1) * k1] = in_ref[w, start:start + rows, :].astype(BF16)
+            starts = [TOP - 3 + j for j in range(3)]
+            for j, r in enumerate(starts):
+                lhs1_ref[w, :, j * 128:(j + 1) * 128] = in_ref[w, r:r + rows, :].astype(BF16)
+            lhs1_ref[w, :, 384:512] = shared([beside_ref[w, r:r + rows, :] for r in starts], -3 * CIN, 6 * CIN)
         out = None
         for i in range(3):
-            part = mm(lhs1_ref[i:i + 5].reshape(5 * rows, 3 * k1), t1_ref[i])
+            part = mm(lhs1_ref[i:i + 5].reshape(5 * rows, 512), t1_ref[i])
             out = part if out is None else out + part
         width = out.shape[1]
         y = iota((rows, width), 0) - 2
@@ -722,13 +730,15 @@
             act1_ref[p, :, width:] = jnp.zeros((act1_ref.shape[1], act1_ref.shape[2] - width), F32)
         blocks = lhs2_ref.shape[1]
         for p in range(5):
-            for j in range(3):
-                a = act1_ref[p, j:j + rows, :].astype(BF16)
-                for b in range(blocks):
-                    lhs2_ref[p, b, :, j * 256:(j + 1) * 256] = a[:, b * 128:b * 128 + 256]
+            for b in range(blocks):
+                for j in range(3):
+                    lhs2_ref[p, b, :, j * 128:(j + 1) * 128] = (
+                        act1_ref[p, j:j + rows, b * 128:(b + 1) * 128].astype(BF16))
+                following = slice((b + 1) * 128, (b + 2) * 128)
+                lhs2_ref[p, b, :, 384:512] = shared([act1_ref[p, j:j + rows, following] for j in range(3)], 0, 32)
         out = None
         for i in range(3):
-            part = mm(lhs2_ref[i:i + 3].reshape(3 * blocks * rows, 768), t2_ref[i])
+            part = mm(lhs2_ref[i:i + 3].reshape(3 * blocks * rows, 512), t2_ref[i])
             out = part if out is None else out + part
         for b in range(blocks):
             y = iota((rows, 128), 0) - 1
@@ -771,7 +781,7 @@
     own = [plane] + [lax.ppermute(plane, "gx", ring("gx", s)) for s in shifts]
     matrices = call(
         weight_kernel,
-        [((3, 6 * half, width), BF16), ((3, 768, 128), BF16), ((3, width, 128), BF16), ((8, width), F32)],
+        [((3, 512, width), BF16), ((3, 512, 128), BF16), ((3, width, 128), BF16), ((8, width), F32)],
         *weights, plane)
     own[1], *matrices = lax.optimization_barrier((own[1], *matrices))
     other = [z_neighbour(v, "gz", False) for v in own]
@@ -779,10 +789,11 @@
     (score,) = call(
         conv_kernel(py, counts, shifts), [((1, pz, py), F32)], *args,
         scratch=[
-            pltpu.VMEM((7, tall, 2 * half), F32),
-            pltpu.VMEM((7, rows, 6 * half), BF16),
+            pltpu.VMEM((7, tall, half), F32),
+            pltpu.VMEM((7, tall, half), F32),
+            pltpu.VMEM((7, rows, 512), BF16),
             pltpu.VMEM((5, rows + 8, width + 128), F32),
-            pltpu.VMEM((5, blocks, rows, 768), BF16),
+            pltpu.VMEM((5, blocks, rows, 512), BF16),
             pltpu.VMEM((3, rows, width), BF16),
             pltpu.VMEM((rows + 8, 128), F32),
         ], mib=32)

time: 58.9 us -> 58.6 us (level)
  no operation moved by 1% of the time
where the time goes in v12:
time: 58.6 us; the launch traced here: 58.3 us
  waiting for transfers between devices  21.4 us (37%)
  starting transfers between devices  19.3 us (33%)
  Pallas kernels  13.1 us (22%)
  local copies, waits for them, and re-layouts  2.93 us (5%)
  between operations  1.42 us (2%)
    pallas_call x11, Pallas kernels, call(): pl.pallas_call(kernel, in_specs=in_specs or [VMEM] * len(args), out_specs...  13.1 us
    ppermute x2, waiting for transfers between devices, start(): return (sums, lax.ppermute(sums, 'gx', ring('gx', 2)))  9.93 us
    ppermute x2, starting transfers between devices, x_sides(): lax.ppermute(lo, 'gx', ring('gx', -1))  5.32 us
    ppermute x3, waiting for transfers between devices, both_sides(): return lax.ppermute(pay, axis, ring(axis, 1))  4.67 us
    ppermute x3, starting transfers between devices, both_sides(): return lax.ppermute(pay, axis, ring(axis, 1))  4.62 us
    ppermute x6, waiting for transfers between devices, z_neighbour(): return lax.ppermute(pay, axis, ring(axis, 1))  4.26 us
    ppermute x3, starting transfers between devices, detector(): own = [plane] + [lax.ppermute(plane, 'gx', ring('gx', s)) for s in shifts]  4 us
    ppermute x2, starting transfers between devices, x_sides(): lax.ppermute(hi, 'gx', ring('gx', 1))  3.72 us
  transfers between devices with their start and end apart: 18, of which 9 were waited for; matrix products, arithmetic and copies ran while one was open for 5% of the time, Pallas kernels for 8%

profile of v12, /device:TPU:0, one launch (start us, length us, event | category | flops | bytes accessed | tf_op | source)
XLA Modules:
  0.0 58.3 jit_solution(16295399993982064571)
XLA Ops:
  0.6 1.6 %shard_map.120 = (f32[4,240,128]{2,1,0:T(8,128)S(1)}, f32[4,240,128]{2,1,0:T(8,128)S(1)}, s16[736,128]{1,0:T(8,128)(2,1)S(1)}, s16[736,128]{1,0:T(8,128)(2,1)S(1...) custom-call(f32[4,240,128]{2,1,0:T(8,128)} %c_hbm.1, f32[4,240,128]{2,1,0:T(8,128)} %d_hbm.1, s32[4,240,128]{2,1,0:T(8,128)} %l_hbm.3), custom_call_target="tpu_custom_call" | custom-call | tf_op jit(solution)/shard_map/pallas_call | solution.py:73
  2.3 3.1 %collective-permute-start = (s16[736,128]{1,0:T(8,128)(2,1)S(1)}, s16[736,128]{1,0:T(8,128)(2,1)S(1)}, u32[]{:S(2)}, u32[]{:S(2)}) collective-permute-start(s16[736,128]{1,0:T(8,128)(2,1)S(1)} %get-tuple-element.31), channel_id=1, source_target_pairs={{0,4},{4,8},{8,12},{12,0},{1,5},{5,9},{9,13},{13,1},{2,6},{6,10},{... | collective-permute-start | bytes 565256 | tf_op jit(solution)/shard_map/ppermute | solution.py:515
  5.3 2.1 %collective-permute-start.1 = (s16[736,128]{1,0:T(8,128)(2,1)S(1)}, s16[736,128]{1,0:T(8,128)(2,1)S(1)}, u32[]{:S(2)}, u32[]{:S(2)}) collective-permute-start(s16[736,128]{1,0:T(8,128)(2,1)S(1)} %get-tuple-element.32), channel_id=1, source_target_pairs={{0,12},{4,0},{8,4},{12,8},{1,13},{5,1},{9,5},{13,9},{2,14},{6,2},{... | collective-permute-start | bytes 565256 | tf_op jit(solution)/shard_map/ppermute | solution.py:515
  7.4 0.9 %collective-permute-start.2 = (f32[8,128]{1,0:T(8,128)S(1)}, f32[8,128]{1,0:T(8,128)S(1)}, u32[]{:S(2)}, u32[]{:S(2)}) collective-permute-start(f32[8,128]{1,0:T(8,128)S(1)} %get-tuple-element.33.refs_4_), channel_id=1, source_target_pairs={{0,8},{4,12},{8,0},{12,4},{1,9},{5,13},{9,1},{13,5},{2,10},{6,14},... | collective-permute-start | bytes 12296 | tf_op jit(solution)/shard_map/ppermute | solution.py:533
  8.4 0.8 %copy.16 = bf16[27,4,16]{2,1,0:T(4,128)(2,1)S(1)} copy(bf16[27,4,16]{0,1,2:T(4,128)(2,1)} %bitcast.27) | data formatting | bytes 6912 | tf_op jit(solution)/shard_map/transpose | solution.py:655
  9.2 1.0 %copy.17 = bf16[27,16,16]{2,1,0:T(8,128)(2,1)S(1)} copy(bf16[27,16,16]{0,1,2:T(8,128)(2,1)} %bitcast.24) | data formatting | bytes 27648 | tf_op jit(solution)/shard_map/transpose | solution.py:656
  10.2 0.8 %copy.18 = bf16[27,1,16]{2,0,1:T(8,128)(2,1)S(1)} copy(bf16[27,1,16]{0,2,1:T(8,128)(2,1)} %param.16) | data formatting | bytes 1728 | tf_op args[7]
  11.1 0.1 copy.19
  11.2 5.1 %collective-permute-done.2.refs_5_ = f32[8,128]{1,0:T(8,128)S(1)} collective-permute-done((f32[8,128]{1,0:T(8,128)S(1)}, f32[8,128]{1,0:T(8,128)S(1)}, u32[]{:S(2)}, u32[]{:S(2)}) %collective-permute-start.2) | collective-permute-done | bytes 4128 | tf_op jit(solution)/shard_map/ppermute | solution.py:533
  16.3 0.0 collective-permute-done.refs_2_.lo_ref
  16.3 0.0 collective-permute-done.1.refs_3_.hi_ref
  16.3 1.6 %collective-permute-start.3 = (f32[2,24,128]{2,1,0:T(8,128)S(1)}, f32[2,24,128]{2,1,0:T(8,128)S(1)}, u32[]{:S(2)}, u32[]{:S(2)}) collective-permute-start(f32[2,24,128]{2,1,0:T(8,128)S(1)} %shard_map.121.refs_5_.yp_ref), channel_id=1, source_target_pairs={{0,2},{2,0},{1,3},{3,1},{4,6},{6,4},{5,7},{7,5},{8,10},{10,8},{9,1... | collective-permute-start | bytes 73736 | tf_op jit(solution)/shard_map/ppermute | solution.py:497
  17.9 2.3 %collective-permute-done.3.refs_4_.yr_ref = f32[2,24,128]{2,1,0:T(8,128)S(1)} collective-permute-done((f32[2,24,128]{2,1,0:T(8,128)S(1)}, f32[2,24,128]{2,1,0:T(8,128)S(1)}, u32[]{:S(2)}, u32[]{:S(2)}) %collective-permute-start.3) | collective-permute-done | bytes 24608 | tf_op jit(solution)/shard_map/ppermute | solution.py:497
  20.2 0.3 shard_map.122
  20.6 0.1 collective-permute-start.4
  20.6 1.5 %collective-permute-done.4.zr_ref = f32[2,272,128]{2,1,0:T(8,128)S(1)} collective-permute-done((f32[2,272,128]{2,1,0:T(8,128)S(1)}, f32[2,272,128]{2,1,0:T(8,128)S(1)}, u32[]{:S(2)}, u32[]{:S(2)}) %collective-permute-start.4) | collective-permute-done | bytes 278560 | tf_op jit(solution)/shard_map/ppermute | solution.py:503
  22.2 2.2 %shard_map.123 = (f32[4,240,128]{2,1,0:T(8,128)S(1)}, f32[6,272,128]{2,1,0:T(8,128)S(1)}, f32[240,128]{1,0:T(8,128)S(1)}, s16[496,128]{1,0:T(8,128)(2,1)S(1)}, s...) custom-call(f32[4,240,128]{2,1,0:T(8,128)S(1)} %get-tuple-element.29.refs_0_.f_ref, ...), custom_call_target="tpu_custom_call" | custom-call | tf_op jit(solution)/shard_map/pallas_call | solution.py:73
  24.4 0.6 %collective-permute-start.5 = (s16[496,128]{1,0:T(8,128)(2,1)S(1)}, s16[496,128]{1,0:T(8,128)(2,1)S(1)}, u32[]{:S(2)}, u32[]{:S(2)}) collective-permute-start(s16[496,128]{1,0:T(8,128)(2,1)S(1)} %get-tuple-element.37), channel_id=1, source_target_pairs={{0,4},{4,8},{8,12},{12,0},{1,5},{5,9},{9,13},{13,1},{2,6},{6,10},{... | collective-permute-start | bytes 380936 | tf_op jit(solution)/shard_map/ppermute | solution.py:515
  25.1 3.2 %collective-permute-start.6 = (s16[496,128]{1,0:T(8,128)(2,1)S(1)}, s16[496,128]{1,0:T(8,128)(2,1)S(1)}, u32[]{:S(2)}, u32[]{:S(2)}) collective-permute-start(s16[496,128]{1,0:T(8,128)(2,1)S(1)} %get-tuple-element.38), channel_id=1, source_target_pairs={{0,12},{4,0},{8,4},{12,8},{1,13},{5,1},{9,5},{13,9},{2,14},{6,2},{... | collective-permute-start | bytes 380936 | tf_op jit(solution)/shard_map/ppermute | solution.py:515
  28.3 0.0 collective-permute-start.7
  28.3 4.9 %collective-permute-done.7.refs_4_ = f32[8,128]{1,0:T(8,128)S(1)} collective-permute-done((f32[8,128]{1,0:T(8,128)S(1)}, f32[8,128]{1,0:T(8,128)S(1)}, u32[]{:S(2)}, u32[]{:S(2)}) %collective-permute-start.7) | collective-permute-done | bytes 4128 | tf_op jit(solution)/shard_map/ppermute | solution.py:533
  33.2 0.0 collective-permute-done.5.refs_1_.lo_ref
  33.2 0.0 collective-permute-done.6.refs_2_.hi_ref
  33.2 1.6 %collective-permute-start.8 = (f32[2,24,128]{2,1,0:T(8,128)S(1)}, f32[2,24,128]{2,1,0:T(8,128)S(1)}, u32[]{:S(2)}, u32[]{:S(2)}) collective-permute-start(f32[2,24,128]{2,1,0:T(8,128)S(1)} %shard_map.124.refs_4_.yp_ref), channel_id=1, source_target_pairs={{0,2},{2,0},{1,3},{3,1},{4,6},{6,4},{5,7},{7,5},{8,10},{10,8},{9,1... | collective-permute-start | bytes 73736 | tf_op jit(solution)/shard_map/ppermute | solution.py:497
  34.7 2.3 %collective-permute-done.8.refs_3_.yr_ref = f32[2,24,128]{2,1,0:T(8,128)S(1)} collective-permute-done((f32[2,24,128]{2,1,0:T(8,128)S(1)}, f32[2,24,128]{2,1,0:T(8,128)S(1)}, u32[]{:S(2)}, u32[]{:S(2)}) %collective-permute-start.8) | collective-permute-done | bytes 24608 | tf_op jit(solution)/shard_map/ppermute | solution.py:497
  37.1 0.2 shard_map.125
  37.3 0.1 collective-permute-start.9
  37.4 1.5 %collective-permute-done.9.zr_ref = f32[2,272,128]{2,1,0:T(8,128)S(1)} collective-permute-done((f32[2,272,128]{2,1,0:T(8,128)S(1)}, f32[2,272,128]{2,1,0:T(8,128)S(1)}, u32[]{:S(2)}, u32[]{:S(2)}) %collective-permute-start.9) | collective-permute-done | bytes 278560 | tf_op jit(solution)/shard_map/ppermute | solution.py:503
  38.9 0.6 %shard_map.127 = bf16[2,16,128]{2,1,0:T(8,128)(2,1)S(1)} custom-call(f32[4,240,128]{2,1,0:T(8,128)S(1)} %get-tuple-element.34.refs_0_.f_ref, f32[6,272,128]{2,1,0:T(8,128)S(1)} %get-tuple-element.35.a2_ref, f32[240,128]{1,0:T(8,128)S(1)} %get-tuple-element.36.ae2_ref, s16[496,128]{1,0:T(8,128)(2,1)S(1)} %collective-permute-done.5.refs_1_.lo_ref, ...), custom_call_target="tpu_custom_call" | custom-call | tf_op jit(solution)/shard_map/pallas_call | solution.py:73
  39.5 1.5 %collective-permute-start.10 = (bf16[2,16,128]{2,1,0:T(8,128)(2,1)S(1)}, bf16[2,16,128]{2,1,0:T(8,128)(2,1)S(1)}, u32[]{:S(2)}, u32[]{:S(2)}) collective-permute-start(bf16[2,16,128]{2,1,0:T(8,128)(2,1)S(1)} %shard_map.127), channel_id=1, source_target_pairs={{0,2},{2,0},{1,3},{3,1},{4,6},{6,4},{5,7},{7,5},{8,10},{10,8},{9,1... | collective-permute-start | bytes 24584 | tf_op jit(solution)/shard_map/ppermute | solution.py:497
  41.0 0.1 pad_add_fusion
  41.1 3.7 %shard_map.126 = (f32[4,240,128]{2,1,0:T(8,128)}, f32[4,240,128]{2,1,0:T(8,128)}, f32[4,240,128]{2,1,0:T(8,128)}, bf16[60,128]{1,0:T(8,128)(2,1)S(1)}) custom-call(f32[4,240,128]{2,1,0:T(8,128)S(1)} %get-tuple-element.34.refs_0_.f_ref, f32[6,272,128]{2,1,0:T(8,128)S(1)} %get-tuple-element.35.a2_ref, f32[240,128]{1,0:T(8,128)S(1)} %get-tuple-element.36.ae2_ref, ...), custom_call_target="tpu_custom_call" | custom-call | tf_op jit(solution)/shard_map/pallas_call | solution.py:73
  44.8 0.1 broadcast_in_dim.15.ids_ref.refs_0_
  44.9 2.0 %collective-permute-start.11 = (bf16[80,128]{1,0:T(8,128)(2,1)S(1)}, bf16[80,128]{1,0:T(8,128)(2,1)S(1)}, u32[]{:S(2)}, u32[]{:S(2)}) collective-permute-start(bf16[80,128]{1,0:T(8,128)(2,1)S(1)} %shard_map.128.plane_ref.refs_1_), channel_id=1, source_target_pairs={{0,4},{4,8},{8,12},{12,0},{1,5},{5,9},{9,13},{13,1},{2,6},{6,10},{... | collective-permute-start | bytes 61448 | tf_op jit(solution)/shard_map/ppermute | solution.py:781
  47.0 1.9 %collective-permute-start.12 = (bf16[80,128]{1,0:T(8,128)(2,1)S(1)}, bf16[80,128]{1,0:T(8,128)(2,1)S(1)}, u32[]{:S(2)}, u32[]{:S(2)}) collective-permute-start(bf16[80,128]{1,0:T(8,128)(2,1)S(1)} %shard_map.128.plane_ref.refs_1_), channel_id=1, source_target_pairs={{0,12},{4,0},{8,4},{12,8},{1,13},{5,1},{9,5},{13,9},{2,14},{6,2},{... | collective-permute-start | bytes 61448 | tf_op jit(solution)/shard_map/ppermute | solution.py:781
  48.8 0.1 collective-permute-start.13
  49.6 0.1 collective-permute-start.14
  49.7 0.7 %shard_map.129 = (bf16[3,512,640]{2,1,0:T(8,128)(2,1)S(1)}, bf16[3,512,128]{2,1,0:T(8,128)(2,1)S(1)}, bf16[3,640,128]{2,1,0:T(8,128)(2,1)S(1)}, f32[8,640]{1,0:T(8,128)S(1)}) custom-call(bf16[432,16]{1,0:T(8,128)(2,1)S(1)} %bitcast.19, bf16[432,16]{1,0:T(8,128)(2,1)S(1)} %bitcast.17, bf16[144,3]{1,0:T(8,128)(2,1)S(1)} %bitcast.21, f32[1,16]{1,0:T(1,128)S(1)} %bitcast.22, ...), custom_call_target="tpu_custom_call" | custom-call | tf_op jit(solution)/shard_map/pallas_call | solution.py:73
  50.4 0.2 collective-permute-done.11.refs_2_
  50.7 0.3 collective-permute-start.15
  51.0 0.2 collective-permute-start.16
  51.2 2.3 %collective-permute-done.13.refs_4_ = bf16[80,128]{1,0:T(8,128)(2,1)S(1)} collective-permute-done((bf16[80,128]{1,0:T(8,128)(2,1)S(1)}, bf16[80,128]{1,0:T(8,128)(2,1)S(1)}, u32[]{:S(2)}, u32[]{:S(2)}) %collective-permute-start.13) | collective-permute-done | bytes 20512 | tf_op jit(solution)/shard_map/ppermute | solution.py:781
  53.5 0.0 collective-permute-start.17
  53.5 0.0 collective-permute-done.14.refs_5_
  53.5 0.0 collective-permute-done.15.refs_6_
  53.5 0.0 collective-permute-done.16.refs_7_
  53.5 1.2 %collective-permute-done.17.refs_8_ = bf16[80,128]{1,0:T(8,128)(2,1)S(1)} collective-permute-done((bf16[80,128]{1,0:T(8,128)(2,1)S(1)}, bf16[80,128]{1,0:T(8,128)(2,1)S(1)}, u32[]{:S(2)}, u32[]{:S(2)}) %collective-permute-start.17) | collective-permute-done | bytes 20512 | tf_op jit(solution)/shard_map/ppermute | solution.py:503
  54.7 3.6 %shard_map.130 = f32[1,32,60]{2,1,0:T(8,128)} custom-call(s32[3,128]{1,0:T(4,128)S(1)} %broadcast_in_dim.15.ids_ref.refs_0_, bf16[80,128]{1,0:T(8,128)(2,1)S(1)} %shard_map.128.plane_ref.refs_1_, bf16[80,128]{1,0:T(8,128)(2,1)S(1)} %collective-permute-done.11.refs_2_, bf16[80,128]{1,0:T(8,128)(2,1)S(1)} %collective-permute-done.12.refs_3_, ...), custom_call_target="tpu_custom_call" | custom-call | tf_op jit(solution)/shard_map/pallas_call | solution.py:73
  (11 shorter events, 0.1 us)
Async XLA Ops:
  2.3 14.0 %collective-permute-start = (s16[736,128]{1,0:T(8,128)(2,1)S(1)}, s16[736,128]{1,0:T(8,128)(2,1)S(1)}, u32[]{:S(2)}, u32[]{:S(2)}) collective-permute-start(s16[736,128]{1,0:T(8,128)(2,1)S(1)} %get-tuple-element.31), channel_id=1, source_target_pairs={{0,4},{4,8},{8,12},{12,0},{1,5},{5,9},{9,13},{13,1},{2,6},{6,10},{... | collective-permute-start | bytes 565256 | tf_op jit(solution)/shard_map/ppermute | solution.py:515
  5.3 10.9 %collective-permute-start.1 = (s16[736,128]{1,0:T(8,128)(2,1)S(1)}, s16[736,128]{1,0:T(8,128)(2,1)S(1)}, u32[]{:S(2)}, u32[]{:S(2)}) collective-permute-start(s16[736,128]{1,0:T(8,128)(2,1)S(1)} %get-tuple-element.32), channel_id=1, source_target_pairs={{0,12},{4,0},{8,4},{12,8},{1,13},{5,1},{9,5},{13,9},{2,14},{6,2},{... | collective-permute-start | bytes 565256 | tf_op jit(solution)/shard_map/ppermute | solution.py:515
  7.4 8.8 %collective-permute-start.2 = (f32[8,128]{1,0:T(8,128)S(1)}, f32[8,128]{1,0:T(8,128)S(1)}, u32[]{:S(2)}, u32[]{:S(2)}) collective-permute-start(f32[8,128]{1,0:T(8,128)S(1)} %get-tuple-element.33.refs_4_), channel_id=1, source_target_pairs={{0,8},{4,12},{8,0},{12,4},{1,9},{5,13},{9,1},{13,5},{2,10},{6,14},... | collective-permute-start | bytes 12296 | tf_op jit(solution)/shard_map/ppermute | solution.py:533
  16.3 3.9 %collective-permute-start.3 = (f32[2,24,128]{2,1,0:T(8,128)S(1)}, f32[2,24,128]{2,1,0:T(8,128)S(1)}, u32[]{:S(2)}, u32[]{:S(2)}) collective-permute-start(f32[2,24,128]{2,1,0:T(8,128)S(1)} %shard_map.121.refs_5_.yp_ref), channel_id=1, source_target_pairs={{0,2},{2,0},{1,3},{3,1},{4,6},{6,4},{5,7},{7,5},{8,10},{10,8},{9,1... | collective-permute-start | bytes 73736 | tf_op jit(solution)/shard_map/ppermute | solution.py:497
  20.6 1.6 %collective-permute-start.4 = (f32[2,272,128]{2,1,0:T(8,128)S(1)}, f32[2,272,128]{2,1,0:T(8,128)S(1)}, u32[]{:S(2)}, u32[]{:S(2)}) collective-permute-start(f32[2,272,128]{2,1,0:T(8,128)S(1)} %shard_map.122), channel_id=1, source_target_pairs={{0,1},{1,0},{2,3},{3,2},{4,5},{5,4},{6,7},{7,6},{8,9},{9,8},{10,11... | collective-permute-start | bytes 835592 | tf_op jit(solution)/shard_map/ppermute | solution.py:503
  24.4 8.7 %collective-permute-start.5 = (s16[496,128]{1,0:T(8,128)(2,1)S(1)}, s16[496,128]{1,0:T(8,128)(2,1)S(1)}, u32[]{:S(2)}, u32[]{:S(2)}) collective-permute-start(s16[496,128]{1,0:T(8,128)(2,1)S(1)} %get-tuple-element.37), channel_id=1, source_target_pairs={{0,4},{4,8},{8,12},{12,0},{1,5},{5,9},{9,13},{13,1},{2,6},{6,10},{... | collective-permute-start | bytes 380936 | tf_op jit(solution)/shard_map/ppermute | solution.py:515
  25.1 8.1 %collective-permute-start.6 = (s16[496,128]{1,0:T(8,128)(2,1)S(1)}, s16[496,128]{1,0:T(8,128)(2,1)S(1)}, u32[]{:S(2)}, u32[]{:S(2)}) collective-permute-start(s16[496,128]{1,0:T(8,128)(2,1)S(1)} %get-tuple-element.38), channel_id=1, source_target_pairs={{0,12},{4,0},{8,4},{12,8},{1,13},{5,1},{9,5},{13,9},{2,14},{6,2},{... | collective-permute-start | bytes 380936 | tf_op jit(solution)/shard_map/ppermute | solution.py:515
  28.3 4.9 %collective-permute-start.7 = (f32[8,128]{1,0:T(8,128)S(1)}, f32[8,128]{1,0:T(8,128)S(1)}, u32[]{:S(2)}, u32[]{:S(2)}) collective-permute-start(f32[8,128]{1,0:T(8,128)S(1)} %get-tuple-element.39.refs_3_), channel_id=1, source_target_pairs={{0,8},{4,12},{8,0},{12,4},{1,9},{5,13},{9,1},{13,5},{2,10},{6,14},... | collective-permute-start | bytes 12296 | tf_op jit(solution)/shard_map/ppermute | solution.py:533
  33.2 3.9 %collective-permute-start.8 = (f32[2,24,128]{2,1,0:T(8,128)S(1)}, f32[2,24,128]{2,1,0:T(8,128)S(1)}, u32[]{:S(2)}, u32[]{:S(2)}) collective-permute-start(f32[2,24,128]{2,1,0:T(8,128)S(1)} %shard_map.124.refs_4_.yp_ref), channel_id=1, source_target_pairs={{0,2},{2,0},{1,3},{3,1},{4,6},{6,4},{5,7},{7,5},{8,10},{10,8},{9,1... | collective-permute-start | bytes 73736 | tf_op jit(solution)/shard_map/ppermute | solution.py:497
  37.3 1.6 %collective-permute-start.9 = (f32[2,272,128]{2,1,0:T(8,128)S(1)}, f32[2,272,128]{2,1,0:T(8,128)S(1)}, u32[]{:S(2)}, u32[]{:S(2)}) collective-permute-start(f32[2,272,128]{2,1,0:T(8,128)S(1)} %shard_map.125), channel_id=1, source_target_pairs={{0,1},{1,0},{2,3},{3,2},{4,5},{5,4},{6,7},{7,6},{8,9},{9,8},{10,11... | collective-permute-start | bytes 835592 | tf_op jit(solution)/shard_map/ppermute | solution.py:503
  38.9 10.8 %copy-start = (f32[16]{0:T(128)S(1)}, f32[16]{0:T(128)}, u32[]{:S(2)}) copy-start(f32[16]{0:T(128)} %param.13) | copy-start | bytes 196
  38.9 10.8 %copy-start.1 = (f32[16]{0:T(128)S(1)}, f32[16]{0:T(128)}, u32[]{:S(2)}) copy-start(f32[16]{0:T(128)} %param.15) | copy-start | bytes 196
  39.5 5.3 %collective-permute-start.10 = (bf16[2,16,128]{2,1,0:T(8,128)(2,1)S(1)}, bf16[2,16,128]{2,1,0:T(8,128)(2,1)S(1)}, u32[]{:S(2)}, u32[]{:S(2)}) collective-permute-start(bf16[2,16,128]{2,1,0:T(8,128)(2,1)S(1)} %shard_map.127), channel_id=1, source_target_pairs={{0,2},{2,0},{1,3},{3,1},{4,6},{6,4},{5,7},{7,5},{8,10},{10,8},{9,1... | collective-permute-start | bytes 24584 | tf_op jit(solution)/shard_map/ppermute | solution.py:497
  44.9 5.7 %collective-permute-start.11 = (bf16[80,128]{1,0:T(8,128)(2,1)S(1)}, bf16[80,128]{1,0:T(8,128)(2,1)S(1)}, u32[]{:S(2)}, u32[]{:S(2)}) collective-permute-start(bf16[80,128]{1,0:T(8,128)(2,1)S(1)} %shard_map.128.plane_ref.refs_1_), channel_id=1, source_target_pairs={{0,4},{4,8},{8,12},{12,0},{1,5},{5,9},{9,13},{13,1},{2,6},{6,10},{... | collective-permute-start | bytes 61448 | tf_op jit(solution)/shard_map/ppermute | solution.py:781
  47.0 4.0 %collective-permute-start.12 = (bf16[80,128]{1,0:T(8,128)(2,1)S(1)}, bf16[80,128]{1,0:T(8,128)(2,1)S(1)}, u32[]{:S(2)}, u32[]{:S(2)}) collective-permute-start(bf16[80,128]{1,0:T(8,128)(2,1)S(1)} %shard_map.128.plane_ref.refs_1_), channel_id=1, source_target_pairs={{0,12},{4,0},{8,4},{12,8},{1,13},{5,1},{9,5},{13,9},{2,14},{6,2},{... | collective-permute-start | bytes 61448 | tf_op jit(solution)/shard_map/ppermute | solution.py:781
  48.8 4.7 %collective-permute-start.13 = (bf16[80,128]{1,0:T(8,128)(2,1)S(1)}, bf16[80,128]{1,0:T(8,128)(2,1)S(1)}, u32[]{:S(2)}, u32[]{:S(2)}) collective-permute-start(bf16[80,128]{1,0:T(8,128)(2,1)S(1)} %shard_map.128.plane_ref.refs_1_), channel_id=1, source_target_pairs={{0,8},{4,12},{8,0},{12,4},{1,9},{5,13},{9,1},{13,5},{2,10},{6,14},... | collective-permute-start | bytes 61448 | tf_op jit(solution)/shard_map/ppermute | solution.py:781
  49.6 3.9 %collective-permute-start.14 = (bf16[80,128]{1,0:T(8,128)(2,1)S(1)}, bf16[80,128]{1,0:T(8,128)(2,1)S(1)}, u32[]{:S(2)}, u32[]{:S(2)}) collective-permute-start(bf16[80,128]{1,0:T(8,128)(2,1)S(1)} %shard_map.128.plane_ref.refs_1_), channel_id=1, source_target_pairs={{0,1},{1,0},{2,3},{3,2},{4,5},{5,4},{6,7},{7,6},{8,9},{9,8},{10,11... | collective-permute-start | bytes 61448 | tf_op jit(solution)/shard_map/ppermute | solution.py:503
  50.7 2.8 %collective-permute-start.15 = (bf16[80,128]{1,0:T(8,128)(2,1)S(1)}, bf16[80,128]{1,0:T(8,128)(2,1)S(1)}, u32[]{:S(2)}, u32[]{:S(2)}) collective-permute-start(bf16[80,128]{1,0:T(8,128)(2,1)S(1)} %collective-permute-done.11.refs_2_), channel_id=1, source_target_pairs={{0,1},{1,0},{2,3},{3,2},{4,5},{5,4},{6,7},{7,6},{8,9},{9,8},{10,11... | collective-permute-start | bytes 61448 | tf_op jit(solution)/shard_map/ppermute | solution.py:503
  51.0 2.5 %collective-permute-start.16 = (bf16[80,128]{1,0:T(8,128)(2,1)S(1)}, bf16[80,128]{1,0:T(8,128)(2,1)S(1)}, u32[]{:S(2)}, u32[]{:S(2)}) collective-permute-start(bf16[80,128]{1,0:T(8,128)(2,1)S(1)} %collective-permute-done.12.refs_3_), channel_id=1, source_target_pairs={{0,1},{1,0},{2,3},{3,2},{4,5},{5,4},{6,7},{7,6},{8,9},{9,8},{10,11... | collective-permute-start | bytes 61448 | tf_op jit(solution)/shard_map/ppermute | solution.py:503
  53.5 1.2 %collective-permute-start.17 = (bf16[80,128]{1,0:T(8,128)(2,1)S(1)}, bf16[80,128]{1,0:T(8,128)(2,1)S(1)}, u32[]{:S(2)}, u32[]{:S(2)}) collective-permute-start(bf16[80,128]{1,0:T(8,128)(2,1)S(1)} %collective-permute-done.13.refs_4_), channel_id=1, source_target_pairs={{0,1},{1,0},{2,3},{3,2},{4,5},{5,4},{6,7},{7,6},{8,9},{9,8},{10,11... | collective-permute-start | bytes 61448 | tf_op jit(solution)/shard_map/ppermute | solution.py:503

commit v13 on v12

--- a/solution.py
+++ b/solution.py
@@ -547,7 +547,7 @@
         concentration, damage, labels,
         in_specs=[HBM] * 3,
         scratch=[pltpu.VMEM(block, F32), pltpu.VMEM(block, jnp.int32), pltpu.SemaphoreType.DMA((3, nx))])
-    weights = weight_rows(w_first, w_second, w_third)
+    weights = weight_rows(w_first, w_second, w_third) + (b_first[None], b_second[None], b_third[None])
     sums, far = start(sums)
     lo, hi = x_sides(lo, hi)
     (ypay,) = call(edge_rows(A_CODE, ride_x, True), [((2, 24, nz), F32)], f, amp, lo, hi, sums, far, *weights)
@@ -579,7 +579,7 @@
             pltpu.VMEM(block, F32), pltpu.VMEM(block, F32), pltpu.VMEM(block, F32),
             pltpu.SemaphoreType.DMA, pltpu.SemaphoreType.DMA((3, nx))])
     ids = jnp.broadcast_to(jnp.stack([lax.axis_index(a) for a in ("gx", "gy", "gz")])[:, None], (3, nz))
-    crack_score = detector(pooled, edge, ids, weights + (b_first[None], b_second[None], b_third[None]), ny // 4, nz // 4)
+    crack_score = detector(pooled, edge, ids, weights, ny // 4, nz // 4)
     return (fraction, damage_field, flux_sum, crack_score)
 
 
@@ -783,7 +783,7 @@
         weight_kernel,
         [((3, 512, width), BF16), ((3, 512, 128), BF16), ((3, width, 128), BF16), ((8, width), F32)],
         *weights, plane)
-    own[1], *matrices = lax.optimization_barrier((own[1], *matrices))
+    own[-1], *matrices = lax.optimization_barrier((own[-1], *matrices))
     other = [z_neighbour(v, "gz", False) for v in own]
     args = (ids, *own, *other, *matrices)
     (score,) = call(

time: 58.6 us -> 59.1 us (level)
  waiting for transfers between devices: 21.4 us -> 18.3 us
  starting transfers between devices: 19.3 us -> 21.6 us
  local copies, waits for them, and re-layouts: 2.93 us -> 4.23 us
    ppermute x3, waiting for transfers between devices: 2.54 us -> 0.42 us  [detector(): own = [plane] + [lax.ppermute(plane, 'gx', ring('gx', s)) for s in shifts]]
    ppermute x3, starting transfers between devices: 4 us -> 5.81 us  [detector(): own = [plane] + [lax.ppermute(plane, 'gx', ring('gx', s)) for s in shifts]]
    unnamed x5 -> x9, local copies, waits for them, and re-layouts: 0.79 us -> 2.1 us
    ppermute x2, waiting for transfers between devices: 9.93 us -> 9.28 us  [start(): return (sums, lax.ppermute(sums, 'gx', ring('gx', 2)))]
where the time goes in v13:
time: 59.1 us; the launch traced here: 58.8 us
  starting transfers between devices  21.6 us (37%)
  waiting for transfers between devices  18.3 us (31%)
  Pallas kernels  13.1 us (22%)
  local copies, waits for them, and re-layouts  4.23 us (7%)
  between operations  1.41 us (2%)
    pallas_call x11, Pallas kernels, call(): pl.pallas_call(kernel, in_specs=in_specs or [VMEM] * len(args), out_specs...  13.1 us
    ppermute x2, waiting for transfers between devices, start(): return (sums, lax.ppermute(sums, 'gx', ring('gx', 2)))  9.28 us
    ppermute x3, starting transfers between devices, detector(): own = [plane] + [lax.ppermute(plane, 'gx', ring('gx', s)) for s in shifts]  5.81 us
    ppermute x2, starting transfers between devices, x_sides(): lax.ppermute(lo, 'gx', ring('gx', -1))  5.32 us
    ppermute x3, waiting for transfers between devices, both_sides(): return lax.ppermute(pay, axis, ring(axis, 1))  4.67 us
    ppermute x3, starting transfers between devices, both_sides(): return lax.ppermute(pay, axis, ring(axis, 1))  4.62 us
    ppermute x6, waiting for transfers between devices, z_neighbour(): return lax.ppermute(pay, axis, ring(axis, 1))  3.93 us
    ppermute x2, starting transfers between devices, x_sides(): lax.ppermute(hi, 'gx', ring('gx', 1))  3.72 us
  transfers between devices with their start and end apart: 18, of which 9 were waited for; matrix products, arithmetic and copies ran while one was open for 5% of the time, Pallas kernels for 8%

profile of v13, /device:TPU:0, one launch (start us, length us, event | category | flops | bytes accessed | tf_op | source)
XLA Modules:
  0.0 58.8 jit_solution(5361991116359505048)
XLA Ops:
  0.6 1.6 %shard_map.120 = (f32[4,240,128]{2,1,0:T(8,128)S(1)}, f32[4,240,128]{2,1,0:T(8,128)S(1)}, s16[736,128]{1,0:T(8,128)(2,1)S(1)}, s16[736,128]{1,0:T(8,128)(2,1)S(1...) custom-call(f32[4,240,128]{2,1,0:T(8,128)} %c_hbm.1, f32[4,240,128]{2,1,0:T(8,128)} %d_hbm.1, s32[4,240,128]{2,1,0:T(8,128)} %l_hbm.3), custom_call_target="tpu_custom_call" | custom-call | tf_op jit(solution)/shard_map/pallas_call | solution.py:73
  2.3 3.1 %collective-permute-start = (s16[736,128]{1,0:T(8,128)(2,1)S(1)}, s16[736,128]{1,0:T(8,128)(2,1)S(1)}, u32[]{:S(2)}, u32[]{:S(2)}) collective-permute-start(s16[736,128]{1,0:T(8,128)(2,1)S(1)} %get-tuple-element.31), channel_id=1, source_target_pairs={{0,4},{4,8},{8,12},{12,0},{1,5},{5,9},{9,13},{13,1},{2,6},{6,10},{... | collective-permute-start | bytes 565256 | tf_op jit(solution)/shard_map/ppermute | solution.py:515
  5.3 2.1 %collective-permute-start.1 = (s16[736,128]{1,0:T(8,128)(2,1)S(1)}, s16[736,128]{1,0:T(8,128)(2,1)S(1)}, u32[]{:S(2)}, u32[]{:S(2)}) collective-permute-start(s16[736,128]{1,0:T(8,128)(2,1)S(1)} %get-tuple-element.32), channel_id=1, source_target_pairs={{0,12},{4,0},{8,4},{12,8},{1,13},{5,1},{9,5},{13,9},{2,14},{6,2},{... | collective-permute-start | bytes 565256 | tf_op jit(solution)/shard_map/ppermute | solution.py:515
  7.4 0.9 %collective-permute-start.2 = (f32[8,128]{1,0:T(8,128)S(1)}, f32[8,128]{1,0:T(8,128)S(1)}, u32[]{:S(2)}, u32[]{:S(2)}) collective-permute-start(f32[8,128]{1,0:T(8,128)S(1)} %get-tuple-element.33.refs_4_), channel_id=1, source_target_pairs={{0,8},{4,12},{8,0},{12,4},{1,9},{5,13},{9,1},{13,5},{2,10},{6,14},... | collective-permute-start | bytes 12296 | tf_op jit(solution)/shard_map/ppermute | solution.py:533
  8.4 0.8 %copy.16 = bf16[27,4,16]{2,1,0:T(4,128)(2,1)S(1)} copy(bf16[27,4,16]{0,1,2:T(4,128)(2,1)} %bitcast.30) | data formatting | bytes 6912 | tf_op jit(solution)/shard_map/transpose | solution.py:655
  9.2 1.0 %copy.17 = bf16[27,16,16]{2,1,0:T(8,128)(2,1)S(1)} copy(bf16[27,16,16]{0,1,2:T(8,128)(2,1)} %bitcast.27) | data formatting | bytes 27648 | tf_op jit(solution)/shard_map/transpose | solution.py:656
  10.2 0.8 %copy.18 = bf16[27,1,16]{2,0,1:T(8,128)(2,1)S(1)} copy(bf16[27,1,16]{0,2,1:T(8,128)(2,1)} %param.16) | data formatting | bytes 1728 | tf_op args[7]
  11.1 0.1 copy.19
  11.9 4.4 %collective-permute-done.2.refs_5_ = f32[8,128]{1,0:T(8,128)S(1)} collective-permute-done((f32[8,128]{1,0:T(8,128)S(1)}, f32[8,128]{1,0:T(8,128)S(1)}, u32[]{:S(2)}, u32[]{:S(2)}) %collective-permute-start.2) | collective-permute-done | bytes 4128 | tf_op jit(solution)/shard_map/ppermute | solution.py:533
  16.3 0.0 collective-permute-done.refs_2_.lo_ref
  16.3 0.0 collective-permute-done.1.refs_3_.hi_ref
  16.3 0.0 copy-start
  16.3 0.6 %copy-done = f32[16]{0:T(128)S(1)} copy-done((f32[16]{0:T(128)S(1)}, f32[16]{0:T(128)}, u32[]{:S(2)}) %copy-start) | copy-done | bytes 88
  17.0 0.7 %copy-done.2 = f32[16]{0:T(128)S(1)} copy-done((f32[16]{0:T(128)S(1)}, f32[16]{0:T(128)}, u32[]{:S(2)}) %copy-start.2) | copy-done | bytes 88
  17.6 1.6 %collective-permute-start.3 = (f32[2,24,128]{2,1,0:T(8,128)S(1)}, f32[2,24,128]{2,1,0:T(8,128)S(1)}, u32[]{:S(2)}, u32[]{:S(2)}) collective-permute-start(f32[2,24,128]{2,1,0:T(8,128)S(1)} %shard_map.121.refs_5_.yp_ref), channel_id=1, source_target_pairs={{0,2},{2,0},{1,3},{3,1},{4,6},{6,4},{5,7},{7,5},{8,10},{10,8},{9,1... | collective-permute-start | bytes 73736 | tf_op jit(solution)/shard_map/ppermute | solution.py:497
  19.2 2.3 %collective-permute-done.3.refs_4_.yr_ref = f32[2,24,128]{2,1,0:T(8,128)S(1)} collective-permute-done((f32[2,24,128]{2,1,0:T(8,128)S(1)}, f32[2,24,128]{2,1,0:T(8,128)S(1)}, u32[]{:S(2)}, u32[]{:S(2)}) %collective-permute-start.3) | collective-permute-done | bytes 24608 | tf_op jit(solution)/shard_map/ppermute | solution.py:497
  21.5 0.3 shard_map.122
  21.9 0.1 collective-permute-start.4
  21.9 1.5 %collective-permute-done.4.zr_ref = f32[2,272,128]{2,1,0:T(8,128)S(1)} collective-permute-done((f32[2,272,128]{2,1,0:T(8,128)S(1)}, f32[2,272,128]{2,1,0:T(8,128)S(1)}, u32[]{:S(2)}, u32[]{:S(2)}) %collective-permute-start.4) | collective-permute-done | bytes 278560 | tf_op jit(solution)/shard_map/ppermute | solution.py:503
  23.5 2.2 %shard_map.123 = (f32[4,240,128]{2,1,0:T(8,128)S(1)}, f32[6,272,128]{2,1,0:T(8,128)S(1)}, f32[240,128]{1,0:T(8,128)S(1)}, s16[496,128]{1,0:T(8,128)(2,1)S(1)}, s...) custom-call(f32[4,240,128]{2,1,0:T(8,128)S(1)} %get-tuple-element.29.refs_0_.f_ref, ...), custom_call_target="tpu_custom_call" | custom-call | tf_op jit(solution)/shard_map/pallas_call | solution.py:73
  25.7 0.6 %collective-permute-start.5 = (s16[496,128]{1,0:T(8,128)(2,1)S(1)}, s16[496,128]{1,0:T(8,128)(2,1)S(1)}, u32[]{:S(2)}, u32[]{:S(2)}) collective-permute-start(s16[496,128]{1,0:T(8,128)(2,1)S(1)} %get-tuple-element.37), channel_id=1, source_target_pairs={{0,4},{4,8},{8,12},{12,0},{1,5},{5,9},{9,13},{13,1},{2,6},{6,10},{... | collective-permute-start | bytes 380936 | tf_op jit(solution)/shard_map/ppermute | solution.py:515
  26.4 3.2 %collective-permute-start.6 = (s16[496,128]{1,0:T(8,128)(2,1)S(1)}, s16[496,128]{1,0:T(8,128)(2,1)S(1)}, u32[]{:S(2)}, u32[]{:S(2)}) collective-permute-start(s16[496,128]{1,0:T(8,128)(2,1)S(1)} %get-tuple-element.38), channel_id=1, source_target_pairs={{0,12},{4,0},{8,4},{12,8},{1,13},{5,1},{9,5},{13,9},{2,14},{6,2},{... | collective-permute-start | bytes 380936 | tf_op jit(solution)/shard_map/ppermute | solution.py:515
  29.6 4.9 %collective-permute-done.7.refs_4_ = f32[8,128]{1,0:T(8,128)S(1)} collective-permute-done((f32[8,128]{1,0:T(8,128)S(1)}, f32[8,128]{1,0:T(8,128)S(1)}, u32[]{:S(2)}, u32[]{:S(2)}) %collective-permute-start.7) | collective-permute-done | bytes 4128 | tf_op jit(solution)/shard_map/ppermute | solution.py:533
  34.5 0.0 collective-permute-done.5.refs_1_.lo_ref
  34.5 0.0 collective-permute-done.6.refs_2_.hi_ref
  34.5 1.6 %collective-permute-start.8 = (f32[2,24,128]{2,1,0:T(8,128)S(1)}, f32[2,24,128]{2,1,0:T(8,128)S(1)}, u32[]{:S(2)}, u32[]{:S(2)}) collective-permute-start(f32[2,24,128]{2,1,0:T(8,128)S(1)} %shard_map.124.refs_4_.yp_ref), channel_id=1, source_target_pairs={{0,2},{2,0},{1,3},{3,1},{4,6},{6,4},{5,7},{7,5},{8,10},{10,8},{9,1... | collective-permute-start | bytes 73736 | tf_op jit(solution)/shard_map/ppermute | solution.py:497
  36.0 2.3 %collective-permute-done.8.refs_3_.yr_ref = f32[2,24,128]{2,1,0:T(8,128)S(1)} collective-permute-done((f32[2,24,128]{2,1,0:T(8,128)S(1)}, f32[2,24,128]{2,1,0:T(8,128)S(1)}, u32[]{:S(2)}, u32[]{:S(2)}) %collective-permute-start.8) | collective-permute-done | bytes 24608 | tf_op jit(solution)/shard_map/ppermute | solution.py:497
  38.4 0.2 shard_map.125
  38.6 0.1 collective-permute-start.9
  38.7 1.5 %collective-permute-done.9.zr_ref = f32[2,272,128]{2,1,0:T(8,128)S(1)} collective-permute-done((f32[2,272,128]{2,1,0:T(8,128)S(1)}, f32[2,272,128]{2,1,0:T(8,128)S(1)}, u32[]{:S(2)}, u32[]{:S(2)}) %collective-permute-start.9) | collective-permute-done | bytes 278560 | tf_op jit(solution)/shard_map/ppermute | solution.py:503
  40.2 0.6 %shard_map.127 = bf16[2,16,128]{2,1,0:T(8,128)(2,1)S(1)} custom-call(f32[4,240,128]{2,1,0:T(8,128)S(1)} %get-tuple-element.34.refs_0_.f_ref, f32[6,272,128]{2,1,0:T(8,128)S(1)} %get-tuple-element.35.a2_ref, f32[240,128]{1,0:T(8,128)S(1)} %get-tuple-element.36.ae2_ref, s16[496,128]{1,0:T(8,128)(2,1)S(1)} %collective-permute-done.5.refs_1_.lo_ref, ...), custom_call_target="tpu_custom_call" | custom-call | tf_op jit(solution)/shard_map/pallas_call | solution.py:73
  40.8 1.5 %collective-permute-start.10 = (bf16[2,16,128]{2,1,0:T(8,128)(2,1)S(1)}, bf16[2,16,128]{2,1,0:T(8,128)(2,1)S(1)}, u32[]{:S(2)}, u32[]{:S(2)}) collective-permute-start(bf16[2,16,128]{2,1,0:T(8,128)(2,1)S(1)} %shard_map.127), channel_id=1, source_target_pairs={{0,2},{2,0},{1,3},{3,1},{4,6},{6,4},{5,7},{7,5},{8,10},{10,8},{9,1... | collective-permute-start | bytes 24584 | tf_op jit(solution)/shard_map/ppermute | solution.py:497
  42.4 0.1 pad_add_fusion
  42.4 3.7 %shard_map.126 = (f32[4,240,128]{2,1,0:T(8,128)}, f32[4,240,128]{2,1,0:T(8,128)}, f32[4,240,128]{2,1,0:T(8,128)}, bf16[60,128]{1,0:T(8,128)(2,1)S(1)}) custom-call(f32[4,240,128]{2,1,0:T(8,128)S(1)} %get-tuple-element.34.refs_0_.f_ref, f32[6,272,128]{2,1,0:T(8,128)S(1)} %get-tuple-element.35.a2_ref, f32[240,128]{1,0:T(8,128)S(1)} %get-tuple-element.36.ae2_ref, ...), custom_call_target="tpu_custom_call" | custom-call | tf_op jit(solution)/shard_map/pallas_call | solution.py:73
  46.1 0.0 collective-permute-done.10.yr_ref
  46.1 0.1 broadcast_in_dim.18.ids_ref.refs_0_
  46.2 2.0 %collective-permute-start.13 = (bf16[80,128]{1,0:T(8,128)(2,1)S(1)}, bf16[80,128]{1,0:T(8,128)(2,1)S(1)}, u32[]{:S(2)}, u32[]{:S(2)}) collective-permute-start(bf16[80,128]{1,0:T(8,128)(2,1)S(1)} %shard_map.128.plane_ref.refs_1_), channel_id=1, source_target_pairs={{0,8},{4,12},{8,0},{12,4},{1,9},{5,13},{9,1},{13,5},{2,10},{6,14},... | collective-permute-start | bytes 61448 | tf_op jit(solution)/shard_map/ppermute | solution.py:781
  48.2 0.8 %collective-permute-start.11 = (bf16[80,128]{1,0:T(8,128)(2,1)S(1)}, bf16[80,128]{1,0:T(8,128)(2,1)S(1)}, u32[]{:S(2)}, u32[]{:S(2)}) collective-permute-start(bf16[80,128]{1,0:T(8,128)(2,1)S(1)} %shard_map.128.plane_ref.refs_1_), channel_id=1, source_target_pairs={{0,4},{4,8},{8,12},{12,0},{1,5},{5,9},{9,13},{13,1},{2,6},{6,10},{... | collective-permute-start | bytes 61448 | tf_op jit(solution)/shard_map/ppermute | solution.py:781
  49.1 3.0 %collective-permute-start.12 = (bf16[80,128]{1,0:T(8,128)(2,1)S(1)}, bf16[80,128]{1,0:T(8,128)(2,1)S(1)}, u32[]{:S(2)}, u32[]{:S(2)}) collective-permute-start(bf16[80,128]{1,0:T(8,128)(2,1)S(1)} %shard_map.128.plane_ref.refs_1_), channel_id=1, source_target_pairs={{0,12},{4,0},{8,4},{12,8},{1,13},{5,1},{9,5},{13,9},{2,14},{6,2},{... | collective-permute-start | bytes 61448 | tf_op jit(solution)/shard_map/ppermute | solution.py:781
  52.1 0.7 %shard_map.129 = (bf16[3,512,640]{2,1,0:T(8,128)(2,1)S(1)}, bf16[3,512,128]{2,1,0:T(8,128)(2,1)S(1)}, bf16[3,640,128]{2,1,0:T(8,128)(2,1)S(1)}, f32[8,640]{1,0:T(8,128)S(1)}) custom-call(bf16[432,16]{1,0:T(8,128)(2,1)S(1)} %bitcast.20, bf16[432,16]{1,0:T(8,128)(2,1)S(1)} %bitcast.18, bf16[144,3]{1,0:T(8,128)(2,1)S(1)} %bitcast.22, f32[1,16]{1,0:T(1,128)S(1)} %bitcast.24, ...), custom_call_target="tpu_custom_call" | custom-call | tf_op jit(solution)/shard_map/pallas_call | solution.py:73
  52.8 0.6 collective-permute-start.17
  53.4 0.4 collective-permute-done.11.refs_2_
  53.8 0.0 collective-permute-start.15
  53.8 0.0 collective-permute-done.12.refs_3_
  53.8 0.5 collective-permute-start.16
  54.3 0.7 %collective-permute-done.15.refs_6_ = bf16[80,128]{1,0:T(8,128)(2,1)S(1)} collective-permute-done((bf16[80,128]{1,0:T(8,128)(2,1)S(1)}, bf16[80,128]{1,0:T(8,128)(2,1)S(1)}, u32[]{:S(2)}, u32[]{:S(2)}) %collective-permute-start.15) | collective-permute-done | bytes 20512 | tf_op jit(solution)/shard_map/ppermute | solution.py:503
  55.0 0.2 collective-permute-done.16.refs_7_
  55.2 3.6 %shard_map.130 = f32[1,32,60]{2,1,0:T(8,128)} custom-call(s32[3,128]{1,0:T(4,128)S(1)} %broadcast_in_dim.18.ids_ref.refs_0_, bf16[80,128]{1,0:T(8,128)(2,1)S(1)} %shard_map.128.plane_ref.refs_1_, bf16[80,128]{1,0:T(8,128)(2,1)S(1)} %collective-permute-done.11.refs_2_, bf16[80,128]{1,0:T(8,128)(2,1)S(1)} %collective-permute-done.12.refs_3_, ...), custom_call_target="tpu_custom_call" | custom-call | tf_op jit(solution)/shard_map/pallas_call | solution.py:73
  (15 shorter events, 0.2 us)
Async XLA Ops:
  2.3 14.0 %collective-permute-start = (s16[736,128]{1,0:T(8,128)(2,1)S(1)}, s16[736,128]{1,0:T(8,128)(2,1)S(1)}, u32[]{:S(2)}, u32[]{:S(2)}) collective-permute-start(s16[736,128]{1,0:T(8,128)(2,1)S(1)} %get-tuple-element.31), channel_id=1, source_target_pairs={{0,4},{4,8},{8,12},{12,0},{1,5},{5,9},{9,13},{13,1},{2,6},{6,10},{... | collective-permute-start | bytes 565256 | tf_op jit(solution)/shard_map/ppermute | solution.py:515
  5.3 10.9 %collective-permute-start.1 = (s16[736,128]{1,0:T(8,128)(2,1)S(1)}, s16[736,128]{1,0:T(8,128)(2,1)S(1)}, u32[]{:S(2)}, u32[]{:S(2)}) collective-permute-start(s16[736,128]{1,0:T(8,128)(2,1)S(1)} %get-tuple-element.32), channel_id=1, source_target_pairs={{0,12},{4,0},{8,4},{12,8},{1,13},{5,1},{9,5},{13,9},{2,14},{6,2},{... | collective-permute-start | bytes 565256 | tf_op jit(solution)/shard_map/ppermute | solution.py:515
  7.4 8.8 %collective-permute-start.2 = (f32[8,128]{1,0:T(8,128)S(1)}, f32[8,128]{1,0:T(8,128)S(1)}, u32[]{:S(2)}, u32[]{:S(2)}) collective-permute-start(f32[8,128]{1,0:T(8,128)S(1)} %get-tuple-element.33.refs_4_), channel_id=1, source_target_pairs={{0,8},{4,12},{8,0},{12,4},{1,9},{5,13},{9,1},{13,5},{2,10},{6,14},... | collective-permute-start | bytes 12296 | tf_op jit(solution)/shard_map/ppermute | solution.py:533
  16.3 0.7 %copy-start = (f32[16]{0:T(128)S(1)}, f32[16]{0:T(128)}, u32[]{:S(2)}) copy-start(f32[16]{0:T(128)} %param.13) | copy-start | bytes 196
  17.0 0.7 %copy-start.2 = (f32[16]{0:T(128)S(1)}, f32[16]{0:T(128)}, u32[]{:S(2)}) copy-start(f32[16]{0:T(128)} %param.15) | copy-start | bytes 196
  17.6 3.9 %collective-permute-start.3 = (f32[2,24,128]{2,1,0:T(8,128)S(1)}, f32[2,24,128]{2,1,0:T(8,128)S(1)}, u32[]{:S(2)}, u32[]{:S(2)}) collective-permute-start(f32[2,24,128]{2,1,0:T(8,128)S(1)} %shard_map.121.refs_5_.yp_ref), channel_id=1, source_target_pairs={{0,2},{2,0},{1,3},{3,1},{4,6},{6,4},{5,7},{7,5},{8,10},{10,8},{9,1... | collective-permute-start | bytes 73736 | tf_op jit(solution)/shard_map/ppermute | solution.py:497
  21.9 1.6 %collective-permute-start.4 = (f32[2,272,128]{2,1,0:T(8,128)S(1)}, f32[2,272,128]{2,1,0:T(8,128)S(1)}, u32[]{:S(2)}, u32[]{:S(2)}) collective-permute-start(f32[2,272,128]{2,1,0:T(8,128)S(1)} %shard_map.122), channel_id=1, source_target_pairs={{0,1},{1,0},{2,3},{3,2},{4,5},{5,4},{6,7},{7,6},{8,9},{9,8},{10,11... | collective-permute-start | bytes 835592 | tf_op jit(solution)/shard_map/ppermute | solution.py:503
  25.7 8.7 %collective-permute-start.5 = (s16[496,128]{1,0:T(8,128)(2,1)S(1)}, s16[496,128]{1,0:T(8,128)(2,1)S(1)}, u32[]{:S(2)}, u32[]{:S(2)}) collective-permute-start(s16[496,128]{1,0:T(8,128)(2,1)S(1)} %get-tuple-element.37), channel_id=1, source_target_pairs={{0,4},{4,8},{8,12},{12,0},{1,5},{5,9},{9,13},{13,1},{2,6},{6,10},{... | collective-permute-start | bytes 380936 | tf_op jit(solution)/shard_map/ppermute | solution.py:515
  26.4 8.1 %collective-permute-start.6 = (s16[496,128]{1,0:T(8,128)(2,1)S(1)}, s16[496,128]{1,0:T(8,128)(2,1)S(1)}, u32[]{:S(2)}, u32[]{:S(2)}) collective-permute-start(s16[496,128]{1,0:T(8,128)(2,1)S(1)} %get-tuple-element.38), channel_id=1, source_target_pairs={{0,12},{4,0},{8,4},{12,8},{1,13},{5,1},{9,5},{13,9},{2,14},{6,2},{... | collective-permute-start | bytes 380936 | tf_op jit(solution)/shard_map/ppermute | solution.py:515
  29.6 4.9 %collective-permute-start.7 = (f32[8,128]{1,0:T(8,128)S(1)}, f32[8,128]{1,0:T(8,128)S(1)}, u32[]{:S(2)}, u32[]{:S(2)}) collective-permute-start(f32[8,128]{1,0:T(8,128)S(1)} %get-tuple-element.39.refs_3_), channel_id=1, source_target_pairs={{0,8},{4,12},{8,0},{12,4},{1,9},{5,13},{9,1},{13,5},{2,10},{6,14},... | collective-permute-start | bytes 12296 | tf_op jit(solution)/shard_map/ppermute | solution.py:533
  34.5 3.9 %collective-permute-start.8 = (f32[2,24,128]{2,1,0:T(8,128)S(1)}, f32[2,24,128]{2,1,0:T(8,128)S(1)}, u32[]{:S(2)}, u32[]{:S(2)}) collective-permute-start(f32[2,24,128]{2,1,0:T(8,128)S(1)} %shard_map.124.refs_4_.yp_ref), channel_id=1, source_target_pairs={{0,2},{2,0},{1,3},{3,1},{4,6},{6,4},{5,7},{7,5},{8,10},{10,8},{9,1... | collective-permute-start | bytes 73736 | tf_op jit(solution)/shard_map/ppermute | solution.py:497
  38.6 1.6 %collective-permute-start.9 = (f32[2,272,128]{2,1,0:T(8,128)S(1)}, f32[2,272,128]{2,1,0:T(8,128)S(1)}, u32[]{:S(2)}, u32[]{:S(2)}) collective-permute-start(f32[2,272,128]{2,1,0:T(8,128)S(1)} %shard_map.125), channel_id=1, source_target_pairs={{0,1},{1,0},{2,3},{3,2},{4,5},{5,4},{6,7},{7,6},{8,9},{9,8},{10,11... | collective-permute-start | bytes 835592 | tf_op jit(solution)/shard_map/ppermute | solution.py:503
  40.2 11.9 %copy-start.1 = (f32[16]{0:T(128)S(1)}, f32[16]{0:T(128)}, u32[]{:S(2)}) copy-start(f32[16]{0:T(128)} %param.13) | copy-start | bytes 196
  40.2 11.9 %copy-start.3 = (f32[16]{0:T(128)S(1)}, f32[16]{0:T(128)}, u32[]{:S(2)}) copy-start(f32[16]{0:T(128)} %param.15) | copy-start | bytes 196
  40.8 5.3 %collective-permute-start.10 = (bf16[2,16,128]{2,1,0:T(8,128)(2,1)S(1)}, bf16[2,16,128]{2,1,0:T(8,128)(2,1)S(1)}, u32[]{:S(2)}, u32[]{:S(2)}) collective-permute-start(bf16[2,16,128]{2,1,0:T(8,128)(2,1)S(1)} %shard_map.127), channel_id=1, source_target_pairs={{0,2},{2,0},{1,3},{3,1},{4,6},{6,4},{5,7},{7,5},{8,10},{10,8},{9,1... | collective-permute-start | bytes 24584 | tf_op jit(solution)/shard_map/ppermute | solution.py:497
  46.2 6.6 %collective-permute-start.13 = (bf16[80,128]{1,0:T(8,128)(2,1)S(1)}, bf16[80,128]{1,0:T(8,128)(2,1)S(1)}, u32[]{:S(2)}, u32[]{:S(2)}) collective-permute-start(bf16[80,128]{1,0:T(8,128)(2,1)S(1)} %shard_map.128.plane_ref.refs_1_), channel_id=1, source_target_pairs={{0,8},{4,12},{8,0},{12,4},{1,9},{5,13},{9,1},{13,5},{2,10},{6,14},... | collective-permute-start | bytes 61448 | tf_op jit(solution)/shard_map/ppermute | solution.py:781
  48.2 5.6 %collective-permute-start.11 = (bf16[80,128]{1,0:T(8,128)(2,1)S(1)}, bf16[80,128]{1,0:T(8,128)(2,1)S(1)}, u32[]{:S(2)}, u32[]{:S(2)}) collective-permute-start(bf16[80,128]{1,0:T(8,128)(2,1)S(1)} %shard_map.128.plane_ref.refs_1_), channel_id=1, source_target_pairs={{0,4},{4,8},{8,12},{12,0},{1,5},{5,9},{9,13},{13,1},{2,6},{6,10},{... | collective-permute-start | bytes 61448 | tf_op jit(solution)/shard_map/ppermute | solution.py:781
  49.1 4.8 %collective-permute-start.12 = (bf16[80,128]{1,0:T(8,128)(2,1)S(1)}, bf16[80,128]{1,0:T(8,128)(2,1)S(1)}, u32[]{:S(2)}, u32[]{:S(2)}) collective-permute-start(bf16[80,128]{1,0:T(8,128)(2,1)S(1)} %shard_map.128.plane_ref.refs_1_), channel_id=1, source_target_pairs={{0,12},{4,0},{8,4},{12,8},{1,13},{5,1},{9,5},{13,9},{2,14},{6,2},{... | collective-permute-start | bytes 61448 | tf_op jit(solution)/shard_map/ppermute | solution.py:781
  52.1 2.3 %collective-permute-start.14 = (bf16[80,128]{1,0:T(8,128)(2,1)S(1)}, bf16[80,128]{1,0:T(8,128)(2,1)S(1)}, u32[]{:S(2)}, u32[]{:S(2)}) collective-permute-start(bf16[80,128]{1,0:T(8,128)(2,1)S(1)} %shard_map.128.plane_ref.refs_1_), channel_id=1, source_target_pairs={{0,1},{1,0},{2,3},{3,2},{4,5},{5,4},{6,7},{7,6},{8,9},{9,8},{10,11... | collective-permute-start | bytes 61448 | tf_op jit(solution)/shard_map/ppermute | solution.py:503
  52.8 1.5 %collective-permute-start.17 = (bf16[80,128]{1,0:T(8,128)(2,1)S(1)}, bf16[80,128]{1,0:T(8,128)(2,1)S(1)}, u32[]{:S(2)}, u32[]{:S(2)}) collective-permute-start(bf16[80,128]{1,0:T(8,128)(2,1)S(1)} %collective-permute-done.13.refs_4_), channel_id=1, source_target_pairs={{0,1},{1,0},{2,3},{3,2},{4,5},{5,4},{6,7},{7,6},{8,9},{9,8},{10,11... | collective-permute-start | bytes 61448 | tf_op jit(solution)/shard_map/ppermute | solution.py:503
  53.8 1.2 %collective-permute-start.15 = (bf16[80,128]{1,0:T(8,128)(2,1)S(1)}, bf16[80,128]{1,0:T(8,128)(2,1)S(1)}, u32[]{:S(2)}, u32[]{:S(2)}) collective-permute-start(bf16[80,128]{1,0:T(8,128)(2,1)S(1)} %collective-permute-done.11.refs_2_), channel_id=1, source_target_pairs={{0,1},{1,0},{2,3},{3,2},{4,5},{5,4},{6,7},{7,6},{8,9},{9,8},{10,11... | collective-permute-start | bytes 61448 | tf_op jit(solution)/shard_map/ppermute | solution.py:503
  53.8 1.4 %collective-permute-start.16 = (bf16[80,128]{1,0:T(8,128)(2,1)S(1)}, bf16[80,128]{1,0:T(8,128)(2,1)S(1)}, u32[]{:S(2)}, u32[]{:S(2)}) collective-permute-start(bf16[80,128]{1,0:T(8,128)(2,1)S(1)} %collective-permute-done.12.refs_3_), channel_id=1, source_target_pairs={{0,1},{1,0},{2,3},{3,2},{4,5},{5,4},{6,7},{7,6},{8,9},{9,8},{10,11... | collective-permute-start | bytes 61448 | tf_op jit(solution)/shard_map/ppermute | solution.py:503

commit v14 on v13

--- a/solution.py
+++ b/solution.py
@@ -547,7 +547,7 @@
         concentration, damage, labels,
         in_specs=[HBM] * 3,
         scratch=[pltpu.VMEM(block, F32), pltpu.VMEM(block, jnp.int32), pltpu.SemaphoreType.DMA((3, nx))])
-    weights = weight_rows(w_first, w_second, w_third) + (b_first[None], b_second[None], b_third[None])
+    weights = weight_rows(w_first, w_second, w_third) + (b_third[None],)
     sums, far = start(sums)
     lo, hi = x_sides(lo, hi)
     (ypay,) = call(edge_rows(A_CODE, ride_x, True), [((2, 24, nz), F32)], f, amp, lo, hi, sums, far, *weights)
@@ -579,7 +579,7 @@
             pltpu.VMEM(block, F32), pltpu.VMEM(block, F32), pltpu.VMEM(block, F32),
             pltpu.SemaphoreType.DMA, pltpu.SemaphoreType.DMA((3, nx))])
     ids = jnp.broadcast_to(jnp.stack([lax.axis_index(a) for a in ("gx", "gy", "gz")])[:, None], (3, nz))
-    crack_score = detector(pooled, edge, ids, weights, ny // 4, nz // 4)
+    crack_score = detector(pooled, edge, ids, weights + (b_first[None], b_second[None]), ny // 4, nz // 4)
     return (fraction, damage_field, flux_sum, crack_score)
 
 
@@ -607,7 +607,7 @@
 SHIFTS = tuple(k for k in range(-3, 10) if k % (16 // CIN) == 3)
 
 
-def weight_kernel(w1_ref, w2_ref, w3_ref, b1_ref, b2_ref, b3_ref, plane_ref, t1_ref, t2_ref, t3_ref, bias_ref):
+def weight_kernel(w1_ref, w2_ref, w3_ref, b3_ref, b1_ref, b2_ref, plane_ref, t1_ref, t2_ref, t3_ref, bias_ref):
     n1 = bias_ref.shape[1]
     pz = 128 // CIN
     spread = one_hot(iota((CH, 128), 1) % CH == iota((CH, 128), 0))

time: 59.1 us -> 57.8 us (0.978)
  local copies, waits for them, and re-layouts: 4.23 us -> 2.93 us
    unnamed x9 -> x5, local copies, waits for them, and re-layouts: 2.1 us -> 0.79 us
where the time goes in v14:
time: 57.8 us; the launch traced here: 57.5 us
  starting transfers between devices  21.6 us (37%)
  waiting for transfers between devices  18.3 us (32%)
  Pallas kernels  13.1 us (23%)
  local copies, waits for them, and re-layouts  2.93 us (5%)
  between operations  1.41 us (2%)
    pallas_call x11, Pallas kernels, call(): pl.pallas_call(kernel, in_specs=in_specs or [VMEM] * len(args), out_specs...  13.1 us
    ppermute x2, waiting for transfers between devices, start(): return (sums, lax.ppermute(sums, 'gx', ring('gx', 2)))  9.28 us
    ppermute x3, starting transfers between devices, detector(): own = [plane] + [lax.ppermute(plane, 'gx', ring('gx', s)) for s in shifts]  5.81 us
    ppermute x2, starting transfers between devices, x_sides(): lax.ppermute(lo, 'gx', ring('gx', -1))  5.32 us
    ppermute x3, waiting for transfers between devices, both_sides(): return lax.ppermute(pay, axis, ring(axis, 1))  4.67 us
    ppermute x3, starting transfers between devices, both_sides(): return lax.ppermute(pay, axis, ring(axis, 1))  4.62 us
    ppermute x6, waiting for transfers between devices, z_neighbour(): return lax.ppermute(pay, axis, ring(axis, 1))  3.93 us
    ppermute x2, starting transfers between devices, x_sides(): lax.ppermute(hi, 'gx', ring('gx', 1))  3.72 us
  transfers between devices with their start and end apart: 18, of which 9 were waited for; matrix products, arithmetic and copies ran while one was open for 5% of the time, Pallas kernels for 8%

profile of v14, /device:TPU:0, one launch (start us, length us, event | category | flops | bytes accessed | tf_op | source)
XLA Modules:
  0.0 57.5 jit_solution(61903779125224914)
XLA Ops:
  0.6 1.6 %shard_map.120 = (f32[4,240,128]{2,1,0:T(8,128)S(1)}, f32[4,240,128]{2,1,0:T(8,128)S(1)}, s16[736,128]{1,0:T(8,128)(2,1)S(1)}, s16[736,128]{1,0:T(8,128)(2,1)S(1...) custom-call(f32[4,240,128]{2,1,0:T(8,128)} %c_hbm.1, f32[4,240,128]{2,1,0:T(8,128)} %d_hbm.1, s32[4,240,128]{2,1,0:T(8,128)} %l_hbm.3), custom_call_target="tpu_custom_call" | custom-call | tf_op jit(solution)/shard_map/pallas_call | solution.py:73
  2.3 3.1 %collective-permute-start = (s16[736,128]{1,0:T(8,128)(2,1)S(1)}, s16[736,128]{1,0:T(8,128)(2,1)S(1)}, u32[]{:S(2)}, u32[]{:S(2)}) collective-permute-start(s16[736,128]{1,0:T(8,128)(2,1)S(1)} %get-tuple-element.31), channel_id=1, source_target_pairs={{0,4},{4,8},{8,12},{12,0},{1,5},{5,9},{9,13},{13,1},{2,6},{6,10},{... | collective-permute-start | bytes 565256 | tf_op jit(solution)/shard_map/ppermute | solution.py:515
  5.3 2.1 %collective-permute-start.1 = (s16[736,128]{1,0:T(8,128)(2,1)S(1)}, s16[736,128]{1,0:T(8,128)(2,1)S(1)}, u32[]{:S(2)}, u32[]{:S(2)}) collective-permute-start(s16[736,128]{1,0:T(8,128)(2,1)S(1)} %get-tuple-element.32), channel_id=1, source_target_pairs={{0,12},{4,0},{8,4},{12,8},{1,13},{5,1},{9,5},{13,9},{2,14},{6,2},{... | collective-permute-start | bytes 565256 | tf_op jit(solution)/shard_map/ppermute | solution.py:515
  7.4 0.9 %collective-permute-start.2 = (f32[8,128]{1,0:T(8,128)S(1)}, f32[8,128]{1,0:T(8,128)S(1)}, u32[]{:S(2)}, u32[]{:S(2)}) collective-permute-start(f32[8,128]{1,0:T(8,128)S(1)} %get-tuple-element.33.refs_4_), channel_id=1, source_target_pairs={{0,8},{4,12},{8,0},{12,4},{1,9},{5,13},{9,1},{13,5},{2,10},{6,14},... | collective-permute-start | bytes 12296 | tf_op jit(solution)/shard_map/ppermute | solution.py:533
  8.4 0.8 %copy.16 = bf16[27,4,16]{2,1,0:T(4,128)(2,1)S(1)} copy(bf16[27,4,16]{0,1,2:T(4,128)(2,1)} %bitcast.28) | data formatting | bytes 6912 | tf_op jit(solution)/shard_map/transpose | solution.py:655
  9.2 1.0 %copy.17 = bf16[27,16,16]{2,1,0:T(8,128)(2,1)S(1)} copy(bf16[27,16,16]{0,1,2:T(8,128)(2,1)} %bitcast.25) | data formatting | bytes 27648 | tf_op jit(solution)/shard_map/transpose | solution.py:656
  10.2 0.8 %copy.18 = bf16[27,1,16]{2,0,1:T(8,128)(2,1)S(1)} copy(bf16[27,1,16]{0,2,1:T(8,128)(2,1)} %param.16) | data formatting | bytes 1728 | tf_op args[7]
  11.1 0.1 copy.19
  11.9 4.4 %collective-permute-done.2.refs_5_ = f32[8,128]{1,0:T(8,128)S(1)} collective-permute-done((f32[8,128]{1,0:T(8,128)S(1)}, f32[8,128]{1,0:T(8,128)S(1)}, u32[]{:S(2)}, u32[]{:S(2)}) %collective-permute-start.2) | collective-permute-done | bytes 4128 | tf_op jit(solution)/shard_map/ppermute | solution.py:533
  16.3 0.0 collective-permute-done.refs_2_.lo_ref
  16.3 0.0 collective-permute-done.1.refs_3_.hi_ref
  16.3 1.6 %collective-permute-start.3 = (f32[2,24,128]{2,1,0:T(8,128)S(1)}, f32[2,24,128]{2,1,0:T(8,128)S(1)}, u32[]{:S(2)}, u32[]{:S(2)}) collective-permute-start(f32[2,24,128]{2,1,0:T(8,128)S(1)} %shard_map.121.refs_5_.yp_ref), channel_id=1, source_target_pairs={{0,2},{2,0},{1,3},{3,1},{4,6},{6,4},{5,7},{7,5},{8,10},{10,8},{9,1... | collective-permute-start | bytes 73736 | tf_op jit(solution)/shard_map/ppermute | solution.py:497
  17.9 2.3 %collective-permute-done.3.refs_4_.yr_ref = f32[2,24,128]{2,1,0:T(8,128)S(1)} collective-permute-done((f32[2,24,128]{2,1,0:T(8,128)S(1)}, f32[2,24,128]{2,1,0:T(8,128)S(1)}, u32[]{:S(2)}, u32[]{:S(2)}) %collective-permute-start.3) | collective-permute-done | bytes 24608 | tf_op jit(solution)/shard_map/ppermute | solution.py:497
  20.2 0.3 shard_map.122
  20.6 0.1 collective-permute-start.4
  20.6 1.5 %collective-permute-done.4.zr_ref = f32[2,272,128]{2,1,0:T(8,128)S(1)} collective-permute-done((f32[2,272,128]{2,1,0:T(8,128)S(1)}, f32[2,272,128]{2,1,0:T(8,128)S(1)}, u32[]{:S(2)}, u32[]{:S(2)}) %collective-permute-start.4) | collective-permute-done | bytes 278560 | tf_op jit(solution)/shard_map/ppermute | solution.py:503
  22.2 2.2 %shard_map.123 = (f32[4,240,128]{2,1,0:T(8,128)S(1)}, f32[6,272,128]{2,1,0:T(8,128)S(1)}, f32[240,128]{1,0:T(8,128)S(1)}, s16[496,128]{1,0:T(8,128)(2,1)S(1)}, s...) custom-call(f32[4,240,128]{2,1,0:T(8,128)S(1)} %get-tuple-element.29.refs_0_.f_ref, ...), custom_call_target="tpu_custom_call" | custom-call | tf_op jit(solution)/shard_map/pallas_call | solution.py:73
  24.4 0.6 %collective-permute-start.5 = (s16[496,128]{1,0:T(8,128)(2,1)S(1)}, s16[496,128]{1,0:T(8,128)(2,1)S(1)}, u32[]{:S(2)}, u32[]{:S(2)}) collective-permute-start(s16[496,128]{1,0:T(8,128)(2,1)S(1)} %get-tuple-element.37), channel_id=1, source_target_pairs={{0,4},{4,8},{8,12},{12,0},{1,5},{5,9},{9,13},{13,1},{2,6},{6,10},{... | collective-permute-start | bytes 380936 | tf_op jit(solution)/shard_map/ppermute | solution.py:515
  25.1 3.2 %collective-permute-start.6 = (s16[496,128]{1,0:T(8,128)(2,1)S(1)}, s16[496,128]{1,0:T(8,128)(2,1)S(1)}, u32[]{:S(2)}, u32[]{:S(2)}) collective-permute-start(s16[496,128]{1,0:T(8,128)(2,1)S(1)} %get-tuple-element.38), channel_id=1, source_target_pairs={{0,12},{4,0},{8,4},{12,8},{1,13},{5,1},{9,5},{13,9},{2,14},{6,2},{... | collective-permute-start | bytes 380936 | tf_op jit(solution)/shard_map/ppermute | solution.py:515
  28.3 0.0 collective-permute-start.7
  28.3 4.9 %collective-permute-done.7.refs_4_ = f32[8,128]{1,0:T(8,128)S(1)} collective-permute-done((f32[8,128]{1,0:T(8,128)S(1)}, f32[8,128]{1,0:T(8,128)S(1)}, u32[]{:S(2)}, u32[]{:S(2)}) %collective-permute-start.7) | collective-permute-done | bytes 4128 | tf_op jit(solution)/shard_map/ppermute | solution.py:533
  33.2 0.0 collective-permute-done.5.refs_1_.lo_ref
  33.2 0.0 collective-permute-done.6.refs_2_.hi_ref
  33.2 1.6 %collective-permute-start.8 = (f32[2,24,128]{2,1,0:T(8,128)S(1)}, f32[2,24,128]{2,1,0:T(8,128)S(1)}, u32[]{:S(2)}, u32[]{:S(2)}) collective-permute-start(f32[2,24,128]{2,1,0:T(8,128)S(1)} %shard_map.124.refs_4_.yp_ref), channel_id=1, source_target_pairs={{0,2},{2,0},{1,3},{3,1},{4,6},{6,4},{5,7},{7,5},{8,10},{10,8},{9,1... | collective-permute-start | bytes 73736 | tf_op jit(solution)/shard_map/ppermute | solution.py:497
  34.7 2.3 %collective-permute-done.8.refs_3_.yr_ref = f32[2,24,128]{2,1,0:T(8,128)S(1)} collective-permute-done((f32[2,24,128]{2,1,0:T(8,128)S(1)}, f32[2,24,128]{2,1,0:T(8,128)S(1)}, u32[]{:S(2)}, u32[]{:S(2)}) %collective-permute-start.8) | collective-permute-done | bytes 24608 | tf_op jit(solution)/shard_map/ppermute | solution.py:497
  37.1 0.2 shard_map.125
  37.3 0.1 collective-permute-start.9
  37.4 1.5 %collective-permute-done.9.zr_ref = f32[2,272,128]{2,1,0:T(8,128)S(1)} collective-permute-done((f32[2,272,128]{2,1,0:T(8,128)S(1)}, f32[2,272,128]{2,1,0:T(8,128)S(1)}, u32[]{:S(2)}, u32[]{:S(2)}) %collective-permute-start.9) | collective-permute-done | bytes 278560 | tf_op jit(solution)/shard_map/ppermute | solution.py:503
  38.9 0.6 %shard_map.127 = bf16[2,16,128]{2,1,0:T(8,128)(2,1)S(1)} custom-call(f32[4,240,128]{2,1,0:T(8,128)S(1)} %get-tuple-element.34.refs_0_.f_ref, f32[6,272,128]{2,1,0:T(8,128)S(1)} %get-tuple-element.35.a2_ref, f32[240,128]{1,0:T(8,128)S(1)} %get-tuple-element.36.ae2_ref, s16[496,128]{1,0:T(8,128)(2,1)S(1)} %collective-permute-done.5.refs_1_.lo_ref, ...), custom_call_target="tpu_custom_call" | custom-call | tf_op jit(solution)/shard_map/pallas_call | solution.py:73
  39.5 1.5 %collective-permute-start.10 = (bf16[2,16,128]{2,1,0:T(8,128)(2,1)S(1)}, bf16[2,16,128]{2,1,0:T(8,128)(2,1)S(1)}, u32[]{:S(2)}, u32[]{:S(2)}) collective-permute-start(bf16[2,16,128]{2,1,0:T(8,128)(2,1)S(1)} %shard_map.127), channel_id=1, source_target_pairs={{0,2},{2,0},{1,3},{3,1},{4,6},{6,4},{5,7},{7,5},{8,10},{10,8},{9,1... | collective-permute-start | bytes 24584 | tf_op jit(solution)/shard_map/ppermute | solution.py:497
  41.0 0.1 pad_add_fusion
  41.1 3.7 %shard_map.126 = (f32[4,240,128]{2,1,0:T(8,128)}, f32[4,240,128]{2,1,0:T(8,128)}, f32[4,240,128]{2,1,0:T(8,128)}, bf16[60,128]{1,0:T(8,128)(2,1)S(1)}) custom-call(f32[4,240,128]{2,1,0:T(8,128)S(1)} %get-tuple-element.34.refs_0_.f_ref, f32[6,272,128]{2,1,0:T(8,128)S(1)} %get-tuple-element.35.a2_ref, f32[240,128]{1,0:T(8,128)S(1)} %get-tuple-element.36.ae2_ref, ...), custom_call_target="tpu_custom_call" | custom-call | tf_op jit(solution)/shard_map/pallas_call | solution.py:73
  44.8 0.0 collective-permute-done.10.yr_ref
  44.8 0.1 broadcast_in_dim.16.ids_ref.refs_0_
  44.9 2.0 %collective-permute-start.13 = (bf16[80,128]{1,0:T(8,128)(2,1)S(1)}, bf16[80,128]{1,0:T(8,128)(2,1)S(1)}, u32[]{:S(2)}, u32[]{:S(2)}) collective-permute-start(bf16[80,128]{1,0:T(8,128)(2,1)S(1)} %shard_map.128.plane_ref.refs_1_), channel_id=1, source_target_pairs={{0,8},{4,12},{8,0},{12,4},{1,9},{5,13},{9,1},{13,5},{2,10},{6,14},... | collective-permute-start | bytes 61448 | tf_op jit(solution)/shard_map/ppermute | solution.py:781
  46.9 0.8 %collective-permute-start.11 = (bf16[80,128]{1,0:T(8,128)(2,1)S(1)}, bf16[80,128]{1,0:T(8,128)(2,1)S(1)}, u32[]{:S(2)}, u32[]{:S(2)}) collective-permute-start(bf16[80,128]{1,0:T(8,128)(2,1)S(1)} %shard_map.128.plane_ref.refs_1_), channel_id=1, source_target_pairs={{0,4},{4,8},{8,12},{12,0},{1,5},{5,9},{9,13},{13,1},{2,6},{6,10},{... | collective-permute-start | bytes 61448 | tf_op jit(solution)/shard_map/ppermute | solution.py:781
  47.8 3.0 %collective-permute-start.12 = (bf16[80,128]{1,0:T(8,128)(2,1)S(1)}, bf16[80,128]{1,0:T(8,128)(2,1)S(1)}, u32[]{:S(2)}, u32[]{:S(2)}) collective-permute-start(bf16[80,128]{1,0:T(8,128)(2,1)S(1)} %shard_map.128.plane_ref.refs_1_), channel_id=1, source_target_pairs={{0,12},{4,0},{8,4},{12,8},{1,13},{5,1},{9,5},{13,9},{2,14},{6,2},{... | collective-permute-start | bytes 61448 | tf_op jit(solution)/shard_map/ppermute | solution.py:781
  50.8 0.0 collective-permute-start.14
  50.8 0.7 %shard_map.129 = (bf16[3,512,640]{2,1,0:T(8,128)(2,1)S(1)}, bf16[3,512,128]{2,1,0:T(8,128)(2,1)S(1)}, bf16[3,640,128]{2,1,0:T(8,128)(2,1)S(1)}, f32[8,640]{1,0:T(8,128)S(1)}) custom-call(bf16[432,16]{1,0:T(8,128)(2,1)S(1)} %bitcast.20, bf16[432,16]{1,0:T(8,128)(2,1)S(1)} %bitcast.18, bf16[144,3]{1,0:T(8,128)(2,1)S(1)} %bitcast.22, f32[1,1]{1,0:T(1,128)} %bitcast.16.b3_ref, ...), custom_call_target="tpu_custom_call" | custom-call | tf_op jit(solution)/shard_map/pallas_call | solution.py:73
  51.5 0.0 collective-permute-done.13.refs_4_
  51.5 0.6 collective-permute-start.17
  52.1 0.4 collective-permute-done.11.refs_2_
  52.5 0.0 collective-permute-start.15
  52.5 0.0 collective-permute-done.12.refs_3_
  52.5 0.5 collective-permute-start.16
  53.0 0.7 %collective-permute-done.15.refs_6_ = bf16[80,128]{1,0:T(8,128)(2,1)S(1)} collective-permute-done((bf16[80,128]{1,0:T(8,128)(2,1)S(1)}, bf16[80,128]{1,0:T(8,128)(2,1)S(1)}, u32[]{:S(2)}, u32[]{:S(2)}) %collective-permute-start.15) | collective-permute-done | bytes 20512 | tf_op jit(solution)/shard_map/ppermute | solution.py:503
  53.7 0.2 collective-permute-done.16.refs_7_
  53.9 3.6 %shard_map.130 = f32[1,32,60]{2,1,0:T(8,128)} custom-call(s32[3,128]{1,0:T(4,128)S(1)} %broadcast_in_dim.16.ids_ref.refs_0_, bf16[80,128]{1,0:T(8,128)(2,1)S(1)} %shard_map.128.plane_ref.refs_1_, bf16[80,128]{1,0:T(8,128)(2,1)S(1)} %collective-permute-done.11.refs_2_, bf16[80,128]{1,0:T(8,128)(2,1)S(1)} %collective-permute-done.12.refs_3_, ...), custom_call_target="tpu_custom_call" | custom-call | tf_op jit(solution)/shard_map/pallas_call | solution.py:73
  (11 shorter events, 0.1 us)
Async XLA Ops:
  2.3 14.0 %collective-permute-start = (s16[736,128]{1,0:T(8,128)(2,1)S(1)}, s16[736,128]{1,0:T(8,128)(2,1)S(1)}, u32[]{:S(2)}, u32[]{:S(2)}) collective-permute-start(s16[736,128]{1,0:T(8,128)(2,1)S(1)} %get-tuple-element.31), channel_id=1, source_target_pairs={{0,4},{4,8},{8,12},{12,0},{1,5},{5,9},{9,13},{13,1},{2,6},{6,10},{... | collective-permute-start | bytes 565256 | tf_op jit(solution)/shard_map/ppermute | solution.py:515
  5.3 10.9 %collective-permute-start.1 = (s16[736,128]{1,0:T(8,128)(2,1)S(1)}, s16[736,128]{1,0:T(8,128)(2,1)S(1)}, u32[]{:S(2)}, u32[]{:S(2)}) collective-permute-start(s16[736,128]{1,0:T(8,128)(2,1)S(1)} %get-tuple-element.32), channel_id=1, source_target_pairs={{0,12},{4,0},{8,4},{12,8},{1,13},{5,1},{9,5},{13,9},{2,14},{6,2},{... | collective-permute-start | bytes 565256 | tf_op jit(solution)/shard_map/ppermute | solution.py:515
  7.4 8.8 %collective-permute-start.2 = (f32[8,128]{1,0:T(8,128)S(1)}, f32[8,128]{1,0:T(8,128)S(1)}, u32[]{:S(2)}, u32[]{:S(2)}) collective-permute-start(f32[8,128]{1,0:T(8,128)S(1)} %get-tuple-element.33.refs_4_), channel_id=1, source_target_pairs={{0,8},{4,12},{8,0},{12,4},{1,9},{5,13},{9,1},{13,5},{2,10},{6,14},... | collective-permute-start | bytes 12296 | tf_op jit(solution)/shard_map/ppermute | solution.py:533
  16.3 3.9 %collective-permute-start.3 = (f32[2,24,128]{2,1,0:T(8,128)S(1)}, f32[2,24,128]{2,1,0:T(8,128)S(1)}, u32[]{:S(2)}, u32[]{:S(2)}) collective-permute-start(f32[2,24,128]{2,1,0:T(8,128)S(1)} %shard_map.121.refs_5_.yp_ref), channel_id=1, source_target_pairs={{0,2},{2,0},{1,3},{3,1},{4,6},{6,4},{5,7},{7,5},{8,10},{10,8},{9,1... | collective-permute-start | bytes 73736 | tf_op jit(solution)/shard_map/ppermute | solution.py:497
  20.6 1.6 %collective-permute-start.4 = (f32[2,272,128]{2,1,0:T(8,128)S(1)}, f32[2,272,128]{2,1,0:T(8,128)S(1)}, u32[]{:S(2)}, u32[]{:S(2)}) collective-permute-start(f32[2,272,128]{2,1,0:T(8,128)S(1)} %shard_map.122), channel_id=1, source_target_pairs={{0,1},{1,0},{2,3},{3,2},{4,5},{5,4},{6,7},{7,6},{8,9},{9,8},{10,11... | collective-permute-start | bytes 835592 | tf_op jit(solution)/shard_map/ppermute | solution.py:503
  24.4 8.7 %collective-permute-start.5 = (s16[496,128]{1,0:T(8,128)(2,1)S(1)}, s16[496,128]{1,0:T(8,128)(2,1)S(1)}, u32[]{:S(2)}, u32[]{:S(2)}) collective-permute-start(s16[496,128]{1,0:T(8,128)(2,1)S(1)} %get-tuple-element.37), channel_id=1, source_target_pairs={{0,4},{4,8},{8,12},{12,0},{1,5},{5,9},{9,13},{13,1},{2,6},{6,10},{... | collective-permute-start | bytes 380936 | tf_op jit(solution)/shard_map/ppermute | solution.py:515
  25.1 8.1 %collective-permute-start.6 = (s16[496,128]{1,0:T(8,128)(2,1)S(1)}, s16[496,128]{1,0:T(8,128)(2,1)S(1)}, u32[]{:S(2)}, u32[]{:S(2)}) collective-permute-start(s16[496,128]{1,0:T(8,128)(2,1)S(1)} %get-tuple-element.38), channel_id=1, source_target_pairs={{0,12},{4,0},{8,4},{12,8},{1,13},{5,1},{9,5},{13,9},{2,14},{6,2},{... | collective-permute-start | bytes 380936 | tf_op jit(solution)/shard_map/ppermute | solution.py:515
  28.3 4.9 %collective-permute-start.7 = (f32[8,128]{1,0:T(8,128)S(1)}, f32[8,128]{1,0:T(8,128)S(1)}, u32[]{:S(2)}, u32[]{:S(2)}) collective-permute-start(f32[8,128]{1,0:T(8,128)S(1)} %get-tuple-element.39.refs_3_), channel_id=1, source_target_pairs={{0,8},{4,12},{8,0},{12,4},{1,9},{5,13},{9,1},{13,5},{2,10},{6,14},... | collective-permute-start | bytes 12296 | tf_op jit(solution)/shard_map/ppermute | solution.py:533
  33.2 3.9 %collective-permute-start.8 = (f32[2,24,128]{2,1,0:T(8,128)S(1)}, f32[2,24,128]{2,1,0:T(8,128)S(1)}, u32[]{:S(2)}, u32[]{:S(2)}) collective-permute-start(f32[2,24,128]{2,1,0:T(8,128)S(1)} %shard_map.124.refs_4_.yp_ref), channel_id=1, source_target_pairs={{0,2},{2,0},{1,3},{3,1},{4,6},{6,4},{5,7},{7,5},{8,10},{10,8},{9,1... | collective-permute-start | bytes 73736 | tf_op jit(solution)/shard_map/ppermute | solution.py:497
  37.3 1.6 %collective-permute-start.9 = (f32[2,272,128]{2,1,0:T(8,128)S(1)}, f32[2,272,128]{2,1,0:T(8,128)S(1)}, u32[]{:S(2)}, u32[]{:S(2)}) collective-permute-start(f32[2,272,128]{2,1,0:T(8,128)S(1)} %shard_map.125), channel_id=1, source_target_pairs={{0,1},{1,0},{2,3},{3,2},{4,5},{5,4},{6,7},{7,6},{8,9},{9,8},{10,11... | collective-permute-start | bytes 835592 | tf_op jit(solution)/shard_map/ppermute | solution.py:503
  38.9 11.9 %copy-start = (f32[16]{0:T(128)S(1)}, f32[16]{0:T(128)}, u32[]{:S(2)}) copy-start(f32[16]{0:T(128)} %param.13) | copy-start | bytes 196
  38.9 11.9 %copy-start.1 = (f32[16]{0:T(128)S(1)}, f32[16]{0:T(128)}, u32[]{:S(2)}) copy-start(f32[16]{0:T(128)} %param.15) | copy-start | bytes 196
  39.5 5.3 %collective-permute-start.10 = (bf16[2,16,128]{2,1,0:T(8,128)(2,1)S(1)}, bf16[2,16,128]{2,1,0:T(8,128)(2,1)S(1)}, u32[]{:S(2)}, u32[]{:S(2)}) collective-permute-start(bf16[2,16,128]{2,1,0:T(8,128)(2,1)S(1)} %shard_map.127), channel_id=1, source_target_pairs={{0,2},{2,0},{1,3},{3,1},{4,6},{6,4},{5,7},{7,5},{8,10},{10,8},{9,1... | collective-permute-start | bytes 24584 | tf_op jit(solution)/shard_map/ppermute | solution.py:497
  44.9 6.6 %collective-permute-start.13 = (bf16[80,128]{1,0:T(8,128)(2,1)S(1)}, bf16[80,128]{1,0:T(8,128)(2,1)S(1)}, u32[]{:S(2)}, u32[]{:S(2)}) collective-permute-start(bf16[80,128]{1,0:T(8,128)(2,1)S(1)} %shard_map.128.plane_ref.refs_1_), channel_id=1, source_target_pairs={{0,8},{4,12},{8,0},{12,4},{1,9},{5,13},{9,1},{13,5},{2,10},{6,14},... | collective-permute-start | bytes 61448 | tf_op jit(solution)/shard_map/ppermute | solution.py:781
  46.9 5.6 %collective-permute-start.11 = (bf16[80,128]{1,0:T(8,128)(2,1)S(1)}, bf16[80,128]{1,0:T(8,128)(2,1)S(1)}, u32[]{:S(2)}, u32[]{:S(2)}) collective-permute-start(bf16[80,128]{1,0:T(8,128)(2,1)S(1)} %shard_map.128.plane_ref.refs_1_), channel_id=1, source_target_pairs={{0,4},{4,8},{8,12},{12,0},{1,5},{5,9},{9,13},{13,1},{2,6},{6,10},{... | collective-permute-start | bytes 61448 | tf_op jit(solution)/shard_map/ppermute | solution.py:781
  47.8 4.8 %collective-permute-start.12 = (bf16[80,128]{1,0:T(8,128)(2,1)S(1)}, bf16[80,128]{1,0:T(8,128)(2,1)S(1)}, u32[]{:S(2)}, u32[]{:S(2)}) collective-permute-start(bf16[80,128]{1,0:T(8,128)(2,1)S(1)} %shard_map.128.plane_ref.refs_1_), channel_id=1, source_target_pairs={{0,12},{4,0},{8,4},{12,8},{1,13},{5,1},{9,5},{13,9},{2,14},{6,2},{... | collective-permute-start | bytes 61448 | tf_op jit(solution)/shard_map/ppermute | solution.py:781
  50.8 2.3 %collective-permute-start.14 = (bf16[80,128]{1,0:T(8,128)(2,1)S(1)}, bf16[80,128]{1,0:T(8,128)(2,1)S(1)}, u32[]{:S(2)}, u32[]{:S(2)}) collective-permute-start(bf16[80,128]{1,0:T(8,128)(2,1)S(1)} %shard_map.128.plane_ref.refs_1_), channel_id=1, source_target_pairs={{0,1},{1,0},{2,3},{3,2},{4,5},{5,4},{6,7},{7,6},{8,9},{9,8},{10,11... | collective-permute-start | bytes 61448 | tf_op jit(solution)/shard_map/ppermute | solution.py:503
  51.5 1.5 %collective-permute-start.17 = (bf16[80,128]{1,0:T(8,128)(2,1)S(1)}, bf16[80,128]{1,0:T(8,128)(2,1)S(1)}, u32[]{:S(2)}, u32[]{:S(2)}) collective-permute-start(bf16[80,128]{1,0:T(8,128)(2,1)S(1)} %collective-permute-done.13.refs_4_), channel_id=1, source_target_pairs={{0,1},{1,0},{2,3},{3,2},{4,5},{5,4},{6,7},{7,6},{8,9},{9,8},{10,11... | collective-permute-start | bytes 61448 | tf_op jit(solution)/shard_map/ppermute | solution.py:503
  52.5 1.2 %collective-permute-start.15 = (bf16[80,128]{1,0:T(8,128)(2,1)S(1)}, bf16[80,128]{1,0:T(8,128)(2,1)S(1)}, u32[]{:S(2)}, u32[]{:S(2)}) collective-permute-start(bf16[80,128]{1,0:T(8,128)(2,1)S(1)} %collective-permute-done.11.refs_2_), channel_id=1, source_target_pairs={{0,1},{1,0},{2,3},{3,2},{4,5},{5,4},{6,7},{7,6},{8,9},{9,8},{10,11... | collective-permute-start | bytes 61448 | tf_op jit(solution)/shard_map/ppermute | solution.py:503
  52.5 1.4 %collective-permute-start.16 = (bf16[80,128]{1,0:T(8,128)(2,1)S(1)}, bf16[80,128]{1,0:T(8,128)(2,1)S(1)}, u32[]{:S(2)}, u32[]{:S(2)}) collective-permute-start(bf16[80,128]{1,0:T(8,128)(2,1)S(1)} %collective-permute-done.12.refs_3_), channel_id=1, source_target_pairs={{0,1},{1,0},{2,3},{3,2},{4,5},{5,4},{6,7},{7,6},{8,9},{9,8},{10,11... | collective-permute-start | bytes 61448 | tf_op jit(solution)/shard_map/ppermute | solution.py:503

commit v15 on v14

--- a/solution.py
+++ b/solution.py
@@ -404,15 +404,16 @@
 
 
 def pool_rows(scr_ref, count, nz):
-    zin = lax.broadcasted_iota(jnp.int32, (nz, nz), 0)
-    out = lax.broadcasted_iota(jnp.int32, (nz, nz), 1)
-    total = jnp.zeros((count, nz), F32)
+    k = lax.broadcasted_iota(jnp.int32, (4 * nz, nz), 0)
+    out = lax.broadcasted_iota(jnp.int32, (4 * nz, nz), 1)
+    pick = jnp.where((k % nz // 4 == out // 4) & (out % 4 == k // nz), 1.0 / 64.0, 0.0).astype(BF16)
+    high, low = [], []
     for i in range(4):
         rows = (scr_ref[i, pl.ds(0, count, stride=4), :] + scr_ref[i, pl.ds(1, count, stride=4), :]
                 + scr_ref[i, pl.ds(2, count, stride=4), :] + scr_ref[i, pl.ds(3, count, stride=4), :])
-        pick = jnp.where((zin // 4 == out // 4) & (out % 4 == i), 1.0 / 64.0, 0.0).astype(F32)
-        total = total + jnp.dot(rows, pick, precision=lax.Precision.HIGHEST, preferred_element_type=F32)
-    return total
+        high.append(rows.astype(BF16))
+        low.append((rows - high[-1].astype(F32)).astype(BF16))
+    return sum(jnp.dot(jnp.concatenate(v, axis=1), pick, preferred_element_type=F32) for v in (high, low))
 
 
 def edge_b(ride_y, ride_z):

time: 57.8 us -> 57.7 us (level)
  no operation moved by 1% of the time
where the time goes in v15:
time: 57.7 us; the launch traced here: 57.4 us
  starting transfers between devices  21.6 us (37%)
  waiting for transfers between devices  18.3 us (32%)
  Pallas kernels  13 us (23%)
  local copies, waits for them, and re-layouts  2.93 us (5%)
  between operations  1.41 us (2%)
    pallas_call x11, Pallas kernels, call(): pl.pallas_call(kernel, in_specs=in_specs or [VMEM] * len(args), out_specs...  13 us
    ppermute x2, waiting for transfers between devices, start(): return (sums, lax.ppermute(sums, 'gx', ring('gx', 2)))  9.28 us
    ppermute x3, starting transfers between devices, detector(): own = [plane] + [lax.ppermute(plane, 'gx', ring('gx', s)) for s in shifts]  5.81 us
    ppermute x2, starting transfers between devices, x_sides(): lax.ppermute(lo, 'gx', ring('gx', -1))  5.32 us
    ppermute x3, waiting for transfers between devices, both_sides(): return lax.ppermute(pay, axis, ring(axis, 1))  4.67 us
    ppermute x3, starting transfers between devices, both_sides(): return lax.ppermute(pay, axis, ring(axis, 1))  4.61 us
    ppermute x6, waiting for transfers between devices, z_neighbour(): return lax.ppermute(pay, axis, ring(axis, 1))  3.93 us
    ppermute x2, starting transfers between devices, x_sides(): lax.ppermute(hi, 'gx', ring('gx', 1))  3.72 us
  transfers between devices with their start and end apart: 18, of which 9 were waited for; matrix products, arithmetic and copies ran while one was open for 5% of the time, Pallas kernels for 8%

profile of v15, /device:TPU:0, one launch (start us, length us, event | category | flops | bytes accessed | tf_op | source)
XLA Modules:
  0.0 57.4 jit_solution(4114771475514346742)
XLA Ops:
  0.6 1.6 %shard_map.120 = (f32[4,240,128]{2,1,0:T(8,128)S(1)}, f32[4,240,128]{2,1,0:T(8,128)S(1)}, s16[736,128]{1,0:T(8,128)(2,1)S(1)}, s16[736,128]{1,0:T(8,128)(2,1)S(1...) custom-call(f32[4,240,128]{2,1,0:T(8,128)} %c_hbm.1, f32[4,240,128]{2,1,0:T(8,128)} %d_hbm.1, s32[4,240,128]{2,1,0:T(8,128)} %l_hbm.3), custom_call_target="tpu_custom_call" | custom-call | tf_op jit(solution)/shard_map/pallas_call | solution.py:73
  2.3 3.1 %collective-permute-start = (s16[736,128]{1,0:T(8,128)(2,1)S(1)}, s16[736,128]{1,0:T(8,128)(2,1)S(1)}, u32[]{:S(2)}, u32[]{:S(2)}) collective-permute-start(s16[736,128]{1,0:T(8,128)(2,1)S(1)} %get-tuple-element.31), channel_id=1, source_target_pairs={{0,4},{4,8},{8,12},{12,0},{1,5},{5,9},{9,13},{13,1},{2,6},{6,10},{... | collective-permute-start | bytes 565256 | tf_op jit(solution)/shard_map/ppermute | solution.py:516
  5.3 2.1 %collective-permute-start.1 = (s16[736,128]{1,0:T(8,128)(2,1)S(1)}, s16[736,128]{1,0:T(8,128)(2,1)S(1)}, u32[]{:S(2)}, u32[]{:S(2)}) collective-permute-start(s16[736,128]{1,0:T(8,128)(2,1)S(1)} %get-tuple-element.32), channel_id=1, source_target_pairs={{0,12},{4,0},{8,4},{12,8},{1,13},{5,1},{9,5},{13,9},{2,14},{6,2},{... | collective-permute-start | bytes 565256 | tf_op jit(solution)/shard_map/ppermute | solution.py:516
  7.4 0.9 %collective-permute-start.2 = (f32[8,128]{1,0:T(8,128)S(1)}, f32[8,128]{1,0:T(8,128)S(1)}, u32[]{:S(2)}, u32[]{:S(2)}) collective-permute-start(f32[8,128]{1,0:T(8,128)S(1)} %get-tuple-element.33.refs_4_), channel_id=1, source_target_pairs={{0,8},{4,12},{8,0},{12,4},{1,9},{5,13},{9,1},{13,5},{2,10},{6,14},... | collective-permute-start | bytes 12296 | tf_op jit(solution)/shard_map/ppermute | solution.py:534
  8.4 0.8 %copy.16 = bf16[27,4,16]{2,1,0:T(4,128)(2,1)S(1)} copy(bf16[27,4,16]{0,1,2:T(4,128)(2,1)} %bitcast.28) | data formatting | bytes 6912 | tf_op jit(solution)/shard_map/transpose | solution.py:656
  9.2 1.0 %copy.17 = bf16[27,16,16]{2,1,0:T(8,128)(2,1)S(1)} copy(bf16[27,16,16]{0,1,2:T(8,128)(2,1)} %bitcast.25) | data formatting | bytes 27648 | tf_op jit(solution)/shard_map/transpose | solution.py:657
  10.2 0.8 %copy.18 = bf16[27,1,16]{2,0,1:T(8,128)(2,1)S(1)} copy(bf16[27,1,16]{0,2,1:T(8,128)(2,1)} %param.16) | data formatting | bytes 1728 | tf_op args[7]
  11.1 0.1 copy.19
  11.9 4.4 %collective-permute-done.2.refs_5_ = f32[8,128]{1,0:T(8,128)S(1)} collective-permute-done((f32[8,128]{1,0:T(8,128)S(1)}, f32[8,128]{1,0:T(8,128)S(1)}, u32[]{:S(2)}, u32[]{:S(2)}) %collective-permute-start.2) | collective-permute-done | bytes 4128 | tf_op jit(solution)/shard_map/ppermute | solution.py:534
  16.3 0.0 collective-permute-done.refs_2_.lo_ref
  16.3 0.0 collective-permute-done.1.refs_3_.hi_ref
  16.3 1.6 %collective-permute-start.3 = (f32[2,24,128]{2,1,0:T(8,128)S(1)}, f32[2,24,128]{2,1,0:T(8,128)S(1)}, u32[]{:S(2)}, u32[]{:S(2)}) collective-permute-start(f32[2,24,128]{2,1,0:T(8,128)S(1)} %shard_map.121.refs_5_.yp_ref), channel_id=1, source_target_pairs={{0,2},{2,0},{1,3},{3,1},{4,6},{6,4},{5,7},{7,5},{8,10},{10,8},{9,1... | collective-permute-start | bytes 73736 | tf_op jit(solution)/shard_map/ppermute | solution.py:498
  17.9 2.3 %collective-permute-done.3.refs_4_.yr_ref = f32[2,24,128]{2,1,0:T(8,128)S(1)} collective-permute-done((f32[2,24,128]{2,1,0:T(8,128)S(1)}, f32[2,24,128]{2,1,0:T(8,128)S(1)}, u32[]{:S(2)}, u32[]{:S(2)}) %collective-permute-start.3) | collective-permute-done | bytes 24608 | tf_op jit(solution)/shard_map/ppermute | solution.py:498
  20.2 0.3 shard_map.122
  20.6 0.1 collective-permute-start.4
  20.6 1.5 %collective-permute-done.4.zr_ref = f32[2,272,128]{2,1,0:T(8,128)S(1)} collective-permute-done((f32[2,272,128]{2,1,0:T(8,128)S(1)}, f32[2,272,128]{2,1,0:T(8,128)S(1)}, u32[]{:S(2)}, u32[]{:S(2)}) %collective-permute-start.4) | collective-permute-done | bytes 278560 | tf_op jit(solution)/shard_map/ppermute | solution.py:504
  22.2 2.2 %shard_map.123 = (f32[4,240,128]{2,1,0:T(8,128)S(1)}, f32[6,272,128]{2,1,0:T(8,128)S(1)}, f32[240,128]{1,0:T(8,128)S(1)}, s16[496,128]{1,0:T(8,128)(2,1)S(1)}, s...) custom-call(f32[4,240,128]{2,1,0:T(8,128)S(1)} %get-tuple-element.29.refs_0_.f_ref, ...), custom_call_target="tpu_custom_call" | custom-call | tf_op jit(solution)/shard_map/pallas_call | solution.py:73
  24.4 0.6 %collective-permute-start.5 = (s16[496,128]{1,0:T(8,128)(2,1)S(1)}, s16[496,128]{1,0:T(8,128)(2,1)S(1)}, u32[]{:S(2)}, u32[]{:S(2)}) collective-permute-start(s16[496,128]{1,0:T(8,128)(2,1)S(1)} %get-tuple-element.37), channel_id=1, source_target_pairs={{0,4},{4,8},{8,12},{12,0},{1,5},{5,9},{9,13},{13,1},{2,6},{6,10},{... | collective-permute-start | bytes 380936 | tf_op jit(solution)/shard_map/ppermute | solution.py:516
  25.1 3.2 %collective-permute-start.6 = (s16[496,128]{1,0:T(8,128)(2,1)S(1)}, s16[496,128]{1,0:T(8,128)(2,1)S(1)}, u32[]{:S(2)}, u32[]{:S(2)}) collective-permute-start(s16[496,128]{1,0:T(8,128)(2,1)S(1)} %get-tuple-element.38), channel_id=1, source_target_pairs={{0,12},{4,0},{8,4},{12,8},{1,13},{5,1},{9,5},{13,9},{2,14},{6,2},{... | collective-permute-start | bytes 380936 | tf_op jit(solution)/shard_map/ppermute | solution.py:516
  28.3 0.0 collective-permute-start.7
  28.3 4.9 %collective-permute-done.7.refs_4_ = f32[8,128]{1,0:T(8,128)S(1)} collective-permute-done((f32[8,128]{1,0:T(8,128)S(1)}, f32[8,128]{1,0:T(8,128)S(1)}, u32[]{:S(2)}, u32[]{:S(2)}) %collective-permute-start.7) | collective-permute-done | bytes 4128 | tf_op jit(solution)/shard_map/ppermute | solution.py:534
  33.2 0.0 collective-permute-done.5.refs_1_.lo_ref
  33.2 1.6 %collective-permute-start.8 = (f32[2,24,128]{2,1,0:T(8,128)S(1)}, f32[2,24,128]{2,1,0:T(8,128)S(1)}, u32[]{:S(2)}, u32[]{:S(2)}) collective-permute-start(f32[2,24,128]{2,1,0:T(8,128)S(1)} %shard_map.124.refs_4_.yp_ref), channel_id=1, source_target_pairs={{0,2},{2,0},{1,3},{3,1},{4,6},{6,4},{5,7},{7,5},{8,10},{10,8},{9,1... | collective-permute-start | bytes 73736 | tf_op jit(solution)/shard_map/ppermute | solution.py:498
  34.7 2.3 %collective-permute-done.8.refs_3_.yr_ref = f32[2,24,128]{2,1,0:T(8,128)S(1)} collective-permute-done((f32[2,24,128]{2,1,0:T(8,128)S(1)}, f32[2,24,128]{2,1,0:T(8,128)S(1)}, u32[]{:S(2)}, u32[]{:S(2)}) %collective-permute-start.8) | collective-permute-done | bytes 24608 | tf_op jit(solution)/shard_map/ppermute | solution.py:498
  37.1 0.2 shard_map.125
  37.3 0.1 collective-permute-start.9
  37.4 1.5 %collective-permute-done.9.zr_ref = f32[2,272,128]{2,1,0:T(8,128)S(1)} collective-permute-done((f32[2,272,128]{2,1,0:T(8,128)S(1)}, f32[2,272,128]{2,1,0:T(8,128)S(1)}, u32[]{:S(2)}, u32[]{:S(2)}) %collective-permute-start.9) | collective-permute-done | bytes 278560 | tf_op jit(solution)/shard_map/ppermute | solution.py:504
  38.9 0.6 shard_map.127
  39.5 1.5 %collective-permute-start.10 = (bf16[2,16,128]{2,1,0:T(8,128)(2,1)S(1)}, bf16[2,16,128]{2,1,0:T(8,128)(2,1)S(1)}, u32[]{:S(2)}, u32[]{:S(2)}) collective-permute-start(bf16[2,16,128]{2,1,0:T(8,128)(2,1)S(1)} %shard_map.127), channel_id=1, source_target_pairs={{0,2},{2,0},{1,3},{3,1},{4,6},{6,4},{5,7},{7,5},{8,10},{10,8},{9,1... | collective-permute-start | bytes 24584 | tf_op jit(solution)/shard_map/ppermute | solution.py:498
  41.0 0.1 pad_add_fusion
  41.0 3.7 %shard_map.126 = (f32[4,240,128]{2,1,0:T(8,128)}, f32[4,240,128]{2,1,0:T(8,128)}, f32[4,240,128]{2,1,0:T(8,128)}, bf16[60,128]{1,0:T(8,128)(2,1)S(1)}) custom-call(f32[4,240,128]{2,1,0:T(8,128)S(1)} %get-tuple-element.34.refs_0_.f_ref, f32[6,272,128]{2,1,0:T(8,128)S(1)} %get-tuple-element.35.a2_ref, f32[240,128]{1,0:T(8,128)S(1)} %get-tuple-element.36.ae2_ref, ...), custom_call_target="tpu_custom_call" | custom-call | tf_op jit(solution)/shard_map/pallas_call | solution.py:73
  44.7 0.0 collective-permute-done.10.yr_ref
  44.7 0.1 broadcast_in_dim.16.ids_ref.refs_0_
  44.9 2.0 %collective-permute-start.13 = (bf16[80,128]{1,0:T(8,128)(2,1)S(1)}, bf16[80,128]{1,0:T(8,128)(2,1)S(1)}, u32[]{:S(2)}, u32[]{:S(2)}) collective-permute-start(bf16[80,128]{1,0:T(8,128)(2,1)S(1)} %shard_map.128.plane_ref.refs_1_), channel_id=1, source_target_pairs={{0,8},{4,12},{8,0},{12,4},{1,9},{5,13},{9,1},{13,5},{2,10},{6,14},... | collective-permute-start | bytes 61448 | tf_op jit(solution)/shard_map/ppermute | solution.py:782
  46.8 0.8 %collective-permute-start.11 = (bf16[80,128]{1,0:T(8,128)(2,1)S(1)}, bf16[80,128]{1,0:T(8,128)(2,1)S(1)}, u32[]{:S(2)}, u32[]{:S(2)}) collective-permute-start(bf16[80,128]{1,0:T(8,128)(2,1)S(1)} %shard_map.128.plane_ref.refs_1_), channel_id=1, source_target_pairs={{0,4},{4,8},{8,12},{12,0},{1,5},{5,9},{9,13},{13,1},{2,6},{6,10},{... | collective-permute-start | bytes 61448 | tf_op jit(solution)/shard_map/ppermute | solution.py:782
  47.7 3.0 %collective-permute-start.12 = (bf16[80,128]{1,0:T(8,128)(2,1)S(1)}, bf16[80,128]{1,0:T(8,128)(2,1)S(1)}, u32[]{:S(2)}, u32[]{:S(2)}) collective-permute-start(bf16[80,128]{1,0:T(8,128)(2,1)S(1)} %shard_map.128.plane_ref.refs_1_), channel_id=1, source_target_pairs={{0,12},{4,0},{8,4},{12,8},{1,13},{5,1},{9,5},{13,9},{2,14},{6,2},{... | collective-permute-start | bytes 61448 | tf_op jit(solution)/shard_map/ppermute | solution.py:782
  50.7 0.8 %shard_map.129 = (bf16[3,512,640]{2,1,0:T(8,128)(2,1)S(1)}, bf16[3,512,128]{2,1,0:T(8,128)(2,1)S(1)}, bf16[3,640,128]{2,1,0:T(8,128)(2,1)S(1)}, f32[8,640]{1,0:T(8,128)S(1)}) custom-call(bf16[432,16]{1,0:T(8,128)(2,1)S(1)} %bitcast.20, bf16[432,16]{1,0:T(8,128)(2,1)S(1)} %bitcast.18, bf16[144,3]{1,0:T(8,128)(2,1)S(1)} %bitcast.22, f32[1,1]{1,0:T(1,128)} %bitcast.16.b3_ref, ...), custom_call_target="tpu_custom_call" | custom-call | tf_op jit(solution)/shard_map/pallas_call | solution.py:73
  51.4 0.0 collective-permute-done.13.refs_4_
  51.5 0.6 collective-permute-start.17
  52.0 0.4 collective-permute-done.11.refs_2_
  52.4 0.0 collective-permute-start.15
  52.4 0.0 collective-permute-done.12.refs_3_
  52.4 0.5 collective-permute-start.16
  52.9 0.0 collective-permute-done.14.refs_5_
  52.9 0.0 collective-permute-done.17.refs_8_
  52.9 0.7 %collective-permute-done.15.refs_6_ = bf16[80,128]{1,0:T(8,128)(2,1)S(1)} collective-permute-done((bf16[80,128]{1,0:T(8,128)(2,1)S(1)}, bf16[80,128]{1,0:T(8,128)(2,1)S(1)}, u32[]{:S(2)}, u32[]{:S(2)}) %collective-permute-start.15) | collective-permute-done | bytes 20512 | tf_op jit(solution)/shard_map/ppermute | solution.py:504
  53.6 0.2 collective-permute-done.16.refs_7_
  53.8 3.6 %shard_map.130 = f32[1,32,60]{2,1,0:T(8,128)} custom-call(s32[3,128]{1,0:T(4,128)S(1)} %broadcast_in_dim.16.ids_ref.refs_0_, bf16[80,128]{1,0:T(8,128)(2,1)S(1)} %shard_map.128.plane_ref.refs_1_, bf16[80,128]{1,0:T(8,128)(2,1)S(1)} %collective-permute-done.11.refs_2_, bf16[80,128]{1,0:T(8,128)(2,1)S(1)} %collective-permute-done.12.refs_3_, ...), custom_call_target="tpu_custom_call" | custom-call | tf_op jit(solution)/shard_map/pallas_call | solution.py:73
  (11 shorter events, 0.1 us)
Async XLA Ops:
  2.3 14.0 %collective-permute-start = (s16[736,128]{1,0:T(8,128)(2,1)S(1)}, s16[736,128]{1,0:T(8,128)(2,1)S(1)}, u32[]{:S(2)}, u32[]{:S(2)}) collective-permute-start(s16[736,128]{1,0:T(8,128)(2,1)S(1)} %get-tuple-element.31), channel_id=1, source_target_pairs={{0,4},{4,8},{8,12},{12,0},{1,5},{5,9},{9,13},{13,1},{2,6},{6,10},{... | collective-permute-start | bytes 565256 | tf_op jit(solution)/shard_map/ppermute | solution.py:516
  5.3 10.9 %collective-permute-start.1 = (s16[736,128]{1,0:T(8,128)(2,1)S(1)}, s16[736,128]{1,0:T(8,128)(2,1)S(1)}, u32[]{:S(2)}, u32[]{:S(2)}) collective-permute-start(s16[736,128]{1,0:T(8,128)(2,1)S(1)} %get-tuple-element.32), channel_id=1, source_target_pairs={{0,12},{4,0},{8,4},{12,8},{1,13},{5,1},{9,5},{13,9},{2,14},{6,2},{... | collective-permute-start | bytes 565256 | tf_op jit(solution)/shard_map/ppermute | solution.py:516
  7.4 8.8 %collective-permute-start.2 = (f32[8,128]{1,0:T(8,128)S(1)}, f32[8,128]{1,0:T(8,128)S(1)}, u32[]{:S(2)}, u32[]{:S(2)}) collective-permute-start(f32[8,128]{1,0:T(8,128)S(1)} %get-tuple-element.33.refs_4_), channel_id=1, source_target_pairs={{0,8},{4,12},{8,0},{12,4},{1,9},{5,13},{9,1},{13,5},{2,10},{6,14},... | collective-permute-start | bytes 12296 | tf_op jit(solution)/shard_map/ppermute | solution.py:534
  16.3 3.9 %collective-permute-start.3 = (f32[2,24,128]{2,1,0:T(8,128)S(1)}, f32[2,24,128]{2,1,0:T(8,128)S(1)}, u32[]{:S(2)}, u32[]{:S(2)}) collective-permute-start(f32[2,24,128]{2,1,0:T(8,128)S(1)} %shard_map.121.refs_5_.yp_ref), channel_id=1, source_target_pairs={{0,2},{2,0},{1,3},{3,1},{4,6},{6,4},{5,7},{7,5},{8,10},{10,8},{9,1... | collective-permute-start | bytes 73736 | tf_op jit(solution)/shard_map/ppermute | solution.py:498
  20.6 1.6 %collective-permute-start.4 = (f32[2,272,128]{2,1,0:T(8,128)S(1)}, f32[2,272,128]{2,1,0:T(8,128)S(1)}, u32[]{:S(2)}, u32[]{:S(2)}) collective-permute-start(f32[2,272,128]{2,1,0:T(8,128)S(1)} %shard_map.122), channel_id=1, source_target_pairs={{0,1},{1,0},{2,3},{3,2},{4,5},{5,4},{6,7},{7,6},{8,9},{9,8},{10,11... | collective-permute-start | bytes 835592 | tf_op jit(solution)/shard_map/ppermute | solution.py:504
  24.4 8.7 %collective-permute-start.5 = (s16[496,128]{1,0:T(8,128)(2,1)S(1)}, s16[496,128]{1,0:T(8,128)(2,1)S(1)}, u32[]{:S(2)}, u32[]{:S(2)}) collective-permute-start(s16[496,128]{1,0:T(8,128)(2,1)S(1)} %get-tuple-element.37), channel_id=1, source_target_pairs={{0,4},{4,8},{8,12},{12,0},{1,5},{5,9},{9,13},{13,1},{2,6},{6,10},{... | collective-permute-start | bytes 380936 | tf_op jit(solution)/shard_map/ppermute | solution.py:516
  25.1 8.1 %collective-permute-start.6 = (s16[496,128]{1,0:T(8,128)(2,1)S(1)}, s16[496,128]{1,0:T(8,128)(2,1)S(1)}, u32[]{:S(2)}, u32[]{:S(2)}) collective-permute-start(s16[496,128]{1,0:T(8,128)(2,1)S(1)} %get-tuple-element.38), channel_id=1, source_target_pairs={{0,12},{4,0},{8,4},{12,8},{1,13},{5,1},{9,5},{13,9},{2,14},{6,2},{... | collective-permute-start | bytes 380936 | tf_op jit(solution)/shard_map/ppermute | solution.py:516
  28.3 4.9 %collective-permute-start.7 = (f32[8,128]{1,0:T(8,128)S(1)}, f32[8,128]{1,0:T(8,128)S(1)}, u32[]{:S(2)}, u32[]{:S(2)}) collective-permute-start(f32[8,128]{1,0:T(8,128)S(1)} %get-tuple-element.39.refs_3_), channel_id=1, source_target_pairs={{0,8},{4,12},{8,0},{12,4},{1,9},{5,13},{9,1},{13,5},{2,10},{6,14},... | collective-permute-start | bytes 12296 | tf_op jit(solution)/shard_map/ppermute | solution.py:534
  33.2 3.9 %collective-permute-start.8 = (f32[2,24,128]{2,1,0:T(8,128)S(1)}, f32[2,24,128]{2,1,0:T(8,128)S(1)}, u32[]{:S(2)}, u32[]{:S(2)}) collective-permute-start(f32[2,24,128]{2,1,0:T(8,128)S(1)} %shard_map.124.refs_4_.yp_ref), channel_id=1, source_target_pairs={{0,2},{2,0},{1,3},{3,1},{4,6},{6,4},{5,7},{7,5},{8,10},{10,8},{9,1... | collective-permute-start | bytes 73736 | tf_op jit(solution)/shard_map/ppermute | solution.py:498
  37.3 1.6 %collective-permute-start.9 = (f32[2,272,128]{2,1,0:T(8,128)S(1)}, f32[2,272,128]{2,1,0:T(8,128)S(1)}, u32[]{:S(2)}, u32[]{:S(2)}) collective-permute-start(f32[2,272,128]{2,1,0:T(8,128)S(1)} %shard_map.125), channel_id=1, source_target_pairs={{0,1},{1,0},{2,3},{3,2},{4,5},{5,4},{6,7},{7,6},{8,9},{9,8},{10,11... | collective-permute-start | bytes 835592 | tf_op jit(solution)/shard_map/ppermute | solution.py:504
  38.9 11.8 %copy-start = (f32[16]{0:T(128)S(1)}, f32[16]{0:T(128)}, u32[]{:S(2)}) copy-start(f32[16]{0:T(128)} %param.13) | copy-start | bytes 196
  38.9 11.8 %copy-start.1 = (f32[16]{0:T(128)S(1)}, f32[16]{0:T(128)}, u32[]{:S(2)}) copy-start(f32[16]{0:T(128)} %param.15) | copy-start | bytes 196
  39.5 5.3 %collective-permute-start.10 = (bf16[2,16,128]{2,1,0:T(8,128)(2,1)S(1)}, bf16[2,16,128]{2,1,0:T(8,128)(2,1)S(1)}, u32[]{:S(2)}, u32[]{:S(2)}) collective-permute-start(bf16[2,16,128]{2,1,0:T(8,128)(2,1)S(1)} %shard_map.127), channel_id=1, source_target_pairs={{0,2},{2,0},{1,3},{3,1},{4,6},{6,4},{5,7},{7,5},{8,10},{10,8},{9,1... | collective-permute-start | bytes 24584 | tf_op jit(solution)/shard_map/ppermute | solution.py:498
  44.9 6.6 %collective-permute-start.13 = (bf16[80,128]{1,0:T(8,128)(2,1)S(1)}, bf16[80,128]{1,0:T(8,128)(2,1)S(1)}, u32[]{:S(2)}, u32[]{:S(2)}) collective-permute-start(bf16[80,128]{1,0:T(8,128)(2,1)S(1)} %shard_map.128.plane_ref.refs_1_), channel_id=1, source_target_pairs={{0,8},{4,12},{8,0},{12,4},{1,9},{5,13},{9,1},{13,5},{2,10},{6,14},... | collective-permute-start | bytes 61448 | tf_op jit(solution)/shard_map/ppermute | solution.py:782
  46.8 5.6 %collective-permute-start.11 = (bf16[80,128]{1,0:T(8,128)(2,1)S(1)}, bf16[80,128]{1,0:T(8,128)(2,1)S(1)}, u32[]{:S(2)}, u32[]{:S(2)}) collective-permute-start(bf16[80,128]{1,0:T(8,128)(2,1)S(1)} %shard_map.128.plane_ref.refs_1_), channel_id=1, source_target_pairs={{0,4},{4,8},{8,12},{12,0},{1,5},{5,9},{9,13},{13,1},{2,6},{6,10},{... | collective-permute-start | bytes 61448 | tf_op jit(solution)/shard_map/ppermute | solution.py:782
  47.7 4.8 %collective-permute-start.12 = (bf16[80,128]{1,0:T(8,128)(2,1)S(1)}, bf16[80,128]{1,0:T(8,128)(2,1)S(1)}, u32[]{:S(2)}, u32[]{:S(2)}) collective-permute-start(bf16[80,128]{1,0:T(8,128)(2,1)S(1)} %shard_map.128.plane_ref.refs_1_), channel_id=1, source_target_pairs={{0,12},{4,0},{8,4},{12,8},{1,13},{5,1},{9,5},{13,9},{2,14},{6,2},{... | collective-permute-start | bytes 61448 | tf_op jit(solution)/shard_map/ppermute | solution.py:782
  50.7 2.3 %collective-permute-start.14 = (bf16[80,128]{1,0:T(8,128)(2,1)S(1)}, bf16[80,128]{1,0:T(8,128)(2,1)S(1)}, u32[]{:S(2)}, u32[]{:S(2)}) collective-permute-start(bf16[80,128]{1,0:T(8,128)(2,1)S(1)} %shard_map.128.plane_ref.refs_1_), channel_id=1, source_target_pairs={{0,1},{1,0},{2,3},{3,2},{4,5},{5,4},{6,7},{7,6},{8,9},{9,8},{10,11... | collective-permute-start | bytes 61448 | tf_op jit(solution)/shard_map/ppermute | solution.py:504
  51.5 1.5 %collective-permute-start.17 = (bf16[80,128]{1,0:T(8,128)(2,1)S(1)}, bf16[80,128]{1,0:T(8,128)(2,1)S(1)}, u32[]{:S(2)}, u32[]{:S(2)}) collective-permute-start(bf16[80,128]{1,0:T(8,128)(2,1)S(1)} %collective-permute-done.13.refs_4_), channel_id=1, source_target_pairs={{0,1},{1,0},{2,3},{3,2},{4,5},{5,4},{6,7},{7,6},{8,9},{9,8},{10,11... | collective-permute-start | bytes 61448 | tf_op jit(solution)/shard_map/ppermute | solution.py:504
  52.4 1.2 %collective-permute-start.15 = (bf16[80,128]{1,0:T(8,128)(2,1)S(1)}, bf16[80,128]{1,0:T(8,128)(2,1)S(1)}, u32[]{:S(2)}, u32[]{:S(2)}) collective-permute-start(bf16[80,128]{1,0:T(8,128)(2,1)S(1)} %collective-permute-done.11.refs_2_), channel_id=1, source_target_pairs={{0,1},{1,0},{2,3},{3,2},{4,5},{5,4},{6,7},{7,6},{8,9},{9,8},{10,11... | collective-permute-start | bytes 61448 | tf_op jit(solution)/shard_map/ppermute | solution.py:504
  52.4 1.4 %collective-permute-start.16 = (bf16[80,128]{1,0:T(8,128)(2,1)S(1)}, bf16[80,128]{1,0:T(8,128)(2,1)S(1)}, u32[]{:S(2)}, u32[]{:S(2)}) collective-permute-start(bf16[80,128]{1,0:T(8,128)(2,1)S(1)} %collective-permute-done.12.refs_3_), channel_id=1, source_target_pairs={{0,1},{1,0},{2,3},{3,2},{4,5},{5,4},{6,7},{7,6},{8,9},{9,8},{10,11... | collective-permute-start | bytes 61448 | tf_op jit(solution)/shard_map/ppermute | solution.py:504

commit v16 on v15

--- a/solution.py
+++ b/solution.py
@@ -450,30 +450,24 @@
         mean = weighted_mean(yp_ref, yr_ref, zr_ref, ride_y, ride_z)
         potentials_b(g, mean, a2_ref, ae2_ref, (f_ref, lo_ref, hi_ref, yr_ref, zr_ref), scratch, [(0, ny)], True)
         labels_in.wait()
-        outs = ((f3_ref, f3_hbm), (dmg_ref, dmg_hbm), (flux_ref, flux_hbm))
-
-        def out_copy(i, x):
-            return pltpu.make_async_copy(outs[i][0].at[x], outs[i][1].at[x], sems.at[i, x])
-
-        pool_scr[...] = jnp.zeros(pool_scr.shape, F32)
-
-        @functools.partial(each, nx, True)
-        def _(x):
-            for r, n in chunks(OFF, OFF + ny, 48):
-                s = slice(r - OFF, r - OFF + n)
+        copies = []
+        for k, (r, n) in enumerate(chunks(OFF, OFF + ny, 48)):
+            s = slice(r - OFF, r - OFF + n)
+            pooled = [None] * 4
+            for x in range(nx):
                 flux, values = finish_b(g, mean, x, r, n, l_ref[x, s, :], a2_ref, scratch)
                 f3_ref[x, s, :] = values[0]
                 dmg_ref[x, s, :] = values[1]
                 flux_ref[x, s, :] = flux
-                for i in range(4):
-                    pool_scr[i, s, :] = pool_scr[i, s, :] + values[i]
-            for i in range(3):
-                out_copy(i, x).start()
-
+                pooled = [v if p is None else p + v for p, v in zip(pooled, values)]
+            for i in range(4):
+                pool_scr[i, s, :] = pooled[i]
+            for i, (src, dst) in enumerate(((f3_ref, f3_hbm), (dmg_ref, dmg_hbm), (flux_ref, flux_hbm))):
+                copies.append(pltpu.make_async_copy(src.at[:, s, :], dst.at[:, s, :], sems.at[i, k]))
+                copies[-1].start()
         pool_ref[...] = pool_rows(pool_scr, ny // 4, nz).astype(BF16)
-        for x in range(nx):
-            for i in range(3):
-                out_copy(i, x).wait()
+        for c in copies:
+            c.wait()
     return kernel
 
 
@@ -578,7 +572,7 @@
         scratch=scratch + [
             pltpu.VMEM((4, ny, nz), F32), pltpu.VMEM(block, jnp.int32),
             pltpu.VMEM(block, F32), pltpu.VMEM(block, F32), pltpu.VMEM(block, F32),
-            pltpu.SemaphoreType.DMA, pltpu.SemaphoreType.DMA((3, nx))])
+            pltpu.SemaphoreType.DMA, pltpu.SemaphoreType.DMA((3, len(chunks(OFF, OFF + ny, 48))))])
     ids = jnp.broadcast_to(jnp.stack([lax.axis_index(a) for a in ("gx", "gy", "gz")])[:, None], (3, nz))
     crack_score = detector(pooled, edge, ids, weights + (b_first[None], b_second[None]), ny // 4, nz // 4)
     return (fraction, damage_field, flux_sum, crack_score)

time: 57.7 us -> 57.7 us (level)
  no operation moved by 1% of the time
where the time goes in v16:
time: 57.7 us; the launch traced here: 57.4 us
  starting transfers between devices  21.6 us (37%)
  waiting for transfers between devices  18.3 us (32%)
  Pallas kernels  13.1 us (23%)
  local copies, waits for them, and re-layouts  2.93 us (5%)
  between operations  1.41 us (2%)
    pallas_call x11, Pallas kernels, call(): pl.pallas_call(kernel, in_specs=in_specs or [VMEM] * len(args), out_specs...  13.1 us
    ppermute x2, waiting for transfers between devices, start(): return (sums, lax.ppermute(sums, 'gx', ring('gx', 2)))  9.28 us
    ppermute x3, starting transfers between devices, detector(): own = [plane] + [lax.ppermute(plane, 'gx', ring('gx', s)) for s in shifts]  5.81 us
    ppermute x2, starting transfers between devices, x_sides(): lax.ppermute(lo, 'gx', ring('gx', -1))  5.32 us
    ppermute x3, waiting for transfers between devices, both_sides(): return lax.ppermute(pay, axis, ring(axis, 1))  4.67 us
    ppermute x3, starting transfers between devices, both_sides(): return lax.ppermute(pay, axis, ring(axis, 1))  4.61 us
    ppermute x6, waiting for transfers between devices, z_neighbour(): return lax.ppermute(pay, axis, ring(axis, 1))  3.93 us
    ppermute x2, starting transfers between devices, x_sides(): lax.ppermute(hi, 'gx', ring('gx', 1))  3.72 us
  transfers between devices with their start and end apart: 18, of which 9 were waited for; matrix products, arithmetic and copies ran while one was open for 5% of the time, Pallas kernels for 8%

profile of v16, /device:TPU:0, one launch (start us, length us, event | category | flops | bytes accessed | tf_op | source)
XLA Modules:
  0.0 57.4 jit_solution(10849101299831923805)
XLA Ops:
  0.6 1.6 %shard_map.120 = (f32[4,240,128]{2,1,0:T(8,128)S(1)}, f32[4,240,128]{2,1,0:T(8,128)S(1)}, s16[736,128]{1,0:T(8,128)(2,1)S(1)}, s16[736,128]{1,0:T(8,128)(2,1)S(1...) custom-call(f32[4,240,128]{2,1,0:T(8,128)} %c_hbm.1, f32[4,240,128]{2,1,0:T(8,128)} %d_hbm.1, s32[4,240,128]{2,1,0:T(8,128)} %l_hbm.3), custom_call_target="tpu_custom_call" | custom-call | tf_op jit(solution)/shard_map/pallas_call | solution.py:73
  2.3 3.1 %collective-permute-start = (s16[736,128]{1,0:T(8,128)(2,1)S(1)}, s16[736,128]{1,0:T(8,128)(2,1)S(1)}, u32[]{:S(2)}, u32[]{:S(2)}) collective-permute-start(s16[736,128]{1,0:T(8,128)(2,1)S(1)} %get-tuple-element.31), channel_id=1, source_target_pairs={{0,4},{4,8},{8,12},{12,0},{1,5},{5,9},{9,13},{13,1},{2,6},{6,10},{... | collective-permute-start | bytes 565256 | tf_op jit(solution)/shard_map/ppermute | solution.py:510
  5.3 2.1 %collective-permute-start.1 = (s16[736,128]{1,0:T(8,128)(2,1)S(1)}, s16[736,128]{1,0:T(8,128)(2,1)S(1)}, u32[]{:S(2)}, u32[]{:S(2)}) collective-permute-start(s16[736,128]{1,0:T(8,128)(2,1)S(1)} %get-tuple-element.32), channel_id=1, source_target_pairs={{0,12},{4,0},{8,4},{12,8},{1,13},{5,1},{9,5},{13,9},{2,14},{6,2},{... | collective-permute-start | bytes 565256 | tf_op jit(solution)/shard_map/ppermute | solution.py:510
  7.4 0.9 %collective-permute-start.2 = (f32[8,128]{1,0:T(8,128)S(1)}, f32[8,128]{1,0:T(8,128)S(1)}, u32[]{:S(2)}, u32[]{:S(2)}) collective-permute-start(f32[8,128]{1,0:T(8,128)S(1)} %get-tuple-element.33.refs_4_), channel_id=1, source_target_pairs={{0,8},{4,12},{8,0},{12,4},{1,9},{5,13},{9,1},{13,5},{2,10},{6,14},... | collective-permute-start | bytes 12296 | tf_op jit(solution)/shard_map/ppermute | solution.py:528
  8.4 0.8 %copy.16 = bf16[27,4,16]{2,1,0:T(4,128)(2,1)S(1)} copy(bf16[27,4,16]{0,1,2:T(4,128)(2,1)} %bitcast.28) | data formatting | bytes 6912 | tf_op jit(solution)/shard_map/transpose | solution.py:650
  9.2 1.0 %copy.17 = bf16[27,16,16]{2,1,0:T(8,128)(2,1)S(1)} copy(bf16[27,16,16]{0,1,2:T(8,128)(2,1)} %bitcast.25) | data formatting | bytes 27648 | tf_op jit(solution)/shard_map/transpose | solution.py:651
  10.2 0.8 %copy.18 = bf16[27,1,16]{2,0,1:T(8,128)(2,1)S(1)} copy(bf16[27,1,16]{0,2,1:T(8,128)(2,1)} %param.16) | data formatting | bytes 1728 | tf_op args[7]
  11.1 0.1 copy.19
  11.9 4.4 %collective-permute-done.2.refs_5_ = f32[8,128]{1,0:T(8,128)S(1)} collective-permute-done((f32[8,128]{1,0:T(8,128)S(1)}, f32[8,128]{1,0:T(8,128)S(1)}, u32[]{:S(2)}, u32[]{:S(2)}) %collective-permute-start.2) | collective-permute-done | bytes 4128 | tf_op jit(solution)/shard_map/ppermute | solution.py:528
  16.3 0.0 collective-permute-done.refs_2_.lo_ref
  16.3 0.0 collective-permute-done.1.refs_3_.hi_ref
  16.3 1.6 %collective-permute-start.3 = (f32[2,24,128]{2,1,0:T(8,128)S(1)}, f32[2,24,128]{2,1,0:T(8,128)S(1)}, u32[]{:S(2)}, u32[]{:S(2)}) collective-permute-start(f32[2,24,128]{2,1,0:T(8,128)S(1)} %shard_map.121.refs_5_.yp_ref), channel_id=1, source_target_pairs={{0,2},{2,0},{1,3},{3,1},{4,6},{6,4},{5,7},{7,5},{8,10},{10,8},{9,1... | collective-permute-start | bytes 73736 | tf_op jit(solution)/shard_map/ppermute | solution.py:492
  17.9 2.3 %collective-permute-done.3.refs_4_.yr_ref = f32[2,24,128]{2,1,0:T(8,128)S(1)} collective-permute-done((f32[2,24,128]{2,1,0:T(8,128)S(1)}, f32[2,24,128]{2,1,0:T(8,128)S(1)}, u32[]{:S(2)}, u32[]{:S(2)}) %collective-permute-start.3) | collective-permute-done | bytes 24608 | tf_op jit(solution)/shard_map/ppermute | solution.py:492
  20.2 0.3 shard_map.122
  20.6 0.1 collective-permute-start.4
  20.6 1.5 %collective-permute-done.4.zr_ref = f32[2,272,128]{2,1,0:T(8,128)S(1)} collective-permute-done((f32[2,272,128]{2,1,0:T(8,128)S(1)}, f32[2,272,128]{2,1,0:T(8,128)S(1)}, u32[]{:S(2)}, u32[]{:S(2)}) %collective-permute-start.4) | collective-permute-done | bytes 278560 | tf_op jit(solution)/shard_map/ppermute | solution.py:498
  22.2 2.2 %shard_map.123 = (f32[4,240,128]{2,1,0:T(8,128)S(1)}, f32[6,272,128]{2,1,0:T(8,128)S(1)}, f32[240,128]{1,0:T(8,128)S(1)}, s16[496,128]{1,0:T(8,128)(2,1)S(1)}, s...) custom-call(f32[4,240,128]{2,1,0:T(8,128)S(1)} %get-tuple-element.29.refs_0_.f_ref, ...), custom_call_target="tpu_custom_call" | custom-call | tf_op jit(solution)/shard_map/pallas_call | solution.py:73
  24.4 0.6 %collective-permute-start.5 = (s16[496,128]{1,0:T(8,128)(2,1)S(1)}, s16[496,128]{1,0:T(8,128)(2,1)S(1)}, u32[]{:S(2)}, u32[]{:S(2)}) collective-permute-start(s16[496,128]{1,0:T(8,128)(2,1)S(1)} %get-tuple-element.37), channel_id=1, source_target_pairs={{0,4},{4,8},{8,12},{12,0},{1,5},{5,9},{9,13},{13,1},{2,6},{6,10},{... | collective-permute-start | bytes 380936 | tf_op jit(solution)/shard_map/ppermute | solution.py:510
  25.1 3.2 %collective-permute-start.6 = (s16[496,128]{1,0:T(8,128)(2,1)S(1)}, s16[496,128]{1,0:T(8,128)(2,1)S(1)}, u32[]{:S(2)}, u32[]{:S(2)}) collective-permute-start(s16[496,128]{1,0:T(8,128)(2,1)S(1)} %get-tuple-element.38), channel_id=1, source_target_pairs={{0,12},{4,0},{8,4},{12,8},{1,13},{5,1},{9,5},{13,9},{2,14},{6,2},{... | collective-permute-start | bytes 380936 | tf_op jit(solution)/shard_map/ppermute | solution.py:510
  28.3 0.0 collective-permute-start.7
  28.3 4.9 %collective-permute-done.7.refs_4_ = f32[8,128]{1,0:T(8,128)S(1)} collective-permute-done((f32[8,128]{1,0:T(8,128)S(1)}, f32[8,128]{1,0:T(8,128)S(1)}, u32[]{:S(2)}, u32[]{:S(2)}) %collective-permute-start.7) | collective-permute-done | bytes 4128 | tf_op jit(solution)/shard_map/ppermute | solution.py:528
  33.2 0.0 collective-permute-done.5.refs_1_.lo_ref
  33.2 0.0 collective-permute-done.6.refs_2_.hi_ref
  33.2 1.6 %collective-permute-start.8 = (f32[2,24,128]{2,1,0:T(8,128)S(1)}, f32[2,24,128]{2,1,0:T(8,128)S(1)}, u32[]{:S(2)}, u32[]{:S(2)}) collective-permute-start(f32[2,24,128]{2,1,0:T(8,128)S(1)} %shard_map.124.refs_4_.yp_ref), channel_id=1, source_target_pairs={{0,2},{2,0},{1,3},{3,1},{4,6},{6,4},{5,7},{7,5},{8,10},{10,8},{9,1... | collective-permute-start | bytes 73736 | tf_op jit(solution)/shard_map/ppermute | solution.py:492
  34.7 2.3 %collective-permute-done.8.refs_3_.yr_ref = f32[2,24,128]{2,1,0:T(8,128)S(1)} collective-permute-done((f32[2,24,128]{2,1,0:T(8,128)S(1)}, f32[2,24,128]{2,1,0:T(8,128)S(1)}, u32[]{:S(2)}, u32[]{:S(2)}) %collective-permute-start.8) | collective-permute-done | bytes 24608 | tf_op jit(solution)/shard_map/ppermute | solution.py:492
  37.1 0.2 shard_map.125
  37.3 0.1 collective-permute-start.9
  37.4 1.5 %collective-permute-done.9.zr_ref = f32[2,272,128]{2,1,0:T(8,128)S(1)} collective-permute-done((f32[2,272,128]{2,1,0:T(8,128)S(1)}, f32[2,272,128]{2,1,0:T(8,128)S(1)}, u32[]{:S(2)}, u32[]{:S(2)}) %collective-permute-start.9) | collective-permute-done | bytes 278560 | tf_op jit(solution)/shard_map/ppermute | solution.py:498
  38.9 0.6 shard_map.127
  39.5 1.5 %collective-permute-start.10 = (bf16[2,16,128]{2,1,0:T(8,128)(2,1)S(1)}, bf16[2,16,128]{2,1,0:T(8,128)(2,1)S(1)}, u32[]{:S(2)}, u32[]{:S(2)}) collective-permute-start(bf16[2,16,128]{2,1,0:T(8,128)(2,1)S(1)} %shard_map.127), channel_id=1, source_target_pairs={{0,2},{2,0},{1,3},{3,1},{4,6},{6,4},{5,7},{7,5},{8,10},{10,8},{9,1... | collective-permute-start | bytes 24584 | tf_op jit(solution)/shard_map/ppermute | solution.py:492
  41.0 0.1 pad_add_fusion
  41.0 3.7 %shard_map.126 = (f32[4,240,128]{2,1,0:T(8,128)}, f32[4,240,128]{2,1,0:T(8,128)}, f32[4,240,128]{2,1,0:T(8,128)}, bf16[60,128]{1,0:T(8,128)(2,1)S(1)}) custom-call(f32[4,240,128]{2,1,0:T(8,128)S(1)} %get-tuple-element.34.refs_0_.f_ref, f32[6,272,128]{2,1,0:T(8,128)S(1)} %get-tuple-element.35.a2_ref, f32[240,128]{1,0:T(8,128)S(1)} %get-tuple-element.36.ae2_ref, ...), custom_call_target="tpu_custom_call" | custom-call | tf_op jit(solution)/shard_map/pallas_call | solution.py:73
  44.8 0.0 collective-permute-done.10.yr_ref
  44.8 0.1 broadcast_in_dim.16.ids_ref.refs_0_
  44.9 2.0 %collective-permute-start.13 = (bf16[80,128]{1,0:T(8,128)(2,1)S(1)}, bf16[80,128]{1,0:T(8,128)(2,1)S(1)}, u32[]{:S(2)}, u32[]{:S(2)}) collective-permute-start(bf16[80,128]{1,0:T(8,128)(2,1)S(1)} %shard_map.128.plane_ref.refs_1_), channel_id=1, source_target_pairs={{0,8},{4,12},{8,0},{12,4},{1,9},{5,13},{9,1},{13,5},{2,10},{6,14},... | collective-permute-start | bytes 61448 | tf_op jit(solution)/shard_map/ppermute | solution.py:776
  46.9 0.8 %collective-permute-start.11 = (bf16[80,128]{1,0:T(8,128)(2,1)S(1)}, bf16[80,128]{1,0:T(8,128)(2,1)S(1)}, u32[]{:S(2)}, u32[]{:S(2)}) collective-permute-start(bf16[80,128]{1,0:T(8,128)(2,1)S(1)} %shard_map.128.plane_ref.refs_1_), channel_id=1, source_target_pairs={{0,4},{4,8},{8,12},{12,0},{1,5},{5,9},{9,13},{13,1},{2,6},{6,10},{... | collective-permute-start | bytes 61448 | tf_op jit(solution)/shard_map/ppermute | solution.py:776
  47.7 3.0 %collective-permute-start.12 = (bf16[80,128]{1,0:T(8,128)(2,1)S(1)}, bf16[80,128]{1,0:T(8,128)(2,1)S(1)}, u32[]{:S(2)}, u32[]{:S(2)}) collective-permute-start(bf16[80,128]{1,0:T(8,128)(2,1)S(1)} %shard_map.128.plane_ref.refs_1_), channel_id=1, source_target_pairs={{0,12},{4,0},{8,4},{12,8},{1,13},{5,1},{9,5},{13,9},{2,14},{6,2},{... | collective-permute-start | bytes 61448 | tf_op jit(solution)/shard_map/ppermute | solution.py:776
  50.7 0.0 collective-permute-start.14
  50.7 0.8 %shard_map.129 = (bf16[3,512,640]{2,1,0:T(8,128)(2,1)S(1)}, bf16[3,512,128]{2,1,0:T(8,128)(2,1)S(1)}, bf16[3,640,128]{2,1,0:T(8,128)(2,1)S(1)}, f32[8,640]{1,0:T(8,128)S(1)}) custom-call(bf16[432,16]{1,0:T(8,128)(2,1)S(1)} %bitcast.20, bf16[432,16]{1,0:T(8,128)(2,1)S(1)} %bitcast.18, bf16[144,3]{1,0:T(8,128)(2,1)S(1)} %bitcast.22, f32[1,1]{1,0:T(1,128)} %bitcast.16.b3_ref, ...), custom_call_target="tpu_custom_call" | custom-call | tf_op jit(solution)/shard_map/pallas_call | solution.py:73
  51.5 0.0 collective-permute-done.13.refs_4_
  51.5 0.6 collective-permute-start.17
  52.1 0.4 collective-permute-done.11.refs_2_
  52.5 0.0 collective-permute-start.15
  52.5 0.5 collective-permute-start.16
  53.0 0.0 collective-permute-done.17.refs_8_
  53.0 0.7 %collective-permute-done.15.refs_6_ = bf16[80,128]{1,0:T(8,128)(2,1)S(1)} collective-permute-done((bf16[80,128]{1,0:T(8,128)(2,1)S(1)}, bf16[80,128]{1,0:T(8,128)(2,1)S(1)}, u32[]{:S(2)}, u32[]{:S(2)}) %collective-permute-start.15) | collective-permute-done | bytes 20512 | tf_op jit(solution)/shard_map/ppermute | solution.py:498
  53.6 0.2 collective-permute-done.16.refs_7_
  53.8 3.6 %shard_map.130 = f32[1,32,60]{2,1,0:T(8,128)} custom-call(s32[3,128]{1,0:T(4,128)S(1)} %broadcast_in_dim.16.ids_ref.refs_0_, bf16[80,128]{1,0:T(8,128)(2,1)S(1)} %shard_map.128.plane_ref.refs_1_, bf16[80,128]{1,0:T(8,128)(2,1)S(1)} %collective-permute-done.11.refs_2_, bf16[80,128]{1,0:T(8,128)(2,1)S(1)} %collective-permute-done.12.refs_3_, ...), custom_call_target="tpu_custom_call" | custom-call | tf_op jit(solution)/shard_map/pallas_call | solution.py:73
  (11 shorter events, 0.1 us)
Async XLA Ops:
  2.3 14.0 %collective-permute-start = (s16[736,128]{1,0:T(8,128)(2,1)S(1)}, s16[736,128]{1,0:T(8,128)(2,1)S(1)}, u32[]{:S(2)}, u32[]{:S(2)}) collective-permute-start(s16[736,128]{1,0:T(8,128)(2,1)S(1)} %get-tuple-element.31), channel_id=1, source_target_pairs={{0,4},{4,8},{8,12},{12,0},{1,5},{5,9},{9,13},{13,1},{2,6},{6,10},{... | collective-permute-start | bytes 565256 | tf_op jit(solution)/shard_map/ppermute | solution.py:510
  5.3 10.9 %collective-permute-start.1 = (s16[736,128]{1,0:T(8,128)(2,1)S(1)}, s16[736,128]{1,0:T(8,128)(2,1)S(1)}, u32[]{:S(2)}, u32[]{:S(2)}) collective-permute-start(s16[736,128]{1,0:T(8,128)(2,1)S(1)} %get-tuple-element.32), channel_id=1, source_target_pairs={{0,12},{4,0},{8,4},{12,8},{1,13},{5,1},{9,5},{13,9},{2,14},{6,2},{... | collective-permute-start | bytes 565256 | tf_op jit(solution)/shard_map/ppermute | solution.py:510
  7.4 8.8 %collective-permute-start.2 = (f32[8,128]{1,0:T(8,128)S(1)}, f32[8,128]{1,0:T(8,128)S(1)}, u32[]{:S(2)}, u32[]{:S(2)}) collective-permute-start(f32[8,128]{1,0:T(8,128)S(1)} %get-tuple-element.33.refs_4_), channel_id=1, source_target_pairs={{0,8},{4,12},{8,0},{12,4},{1,9},{5,13},{9,1},{13,5},{2,10},{6,14},... | collective-permute-start | bytes 12296 | tf_op jit(solution)/shard_map/ppermute | solution.py:528
  16.3 3.9 %collective-permute-start.3 = (f32[2,24,128]{2,1,0:T(8,128)S(1)}, f32[2,24,128]{2,1,0:T(8,128)S(1)}, u32[]{:S(2)}, u32[]{:S(2)}) collective-permute-start(f32[2,24,128]{2,1,0:T(8,128)S(1)} %shard_map.121.refs_5_.yp_ref), channel_id=1, source_target_pairs={{0,2},{2,0},{1,3},{3,1},{4,6},{6,4},{5,7},{7,5},{8,10},{10,8},{9,1... | collective-permute-start | bytes 73736 | tf_op jit(solution)/shard_map/ppermute | solution.py:492
  20.6 1.6 %collective-permute-start.4 = (f32[2,272,128]{2,1,0:T(8,128)S(1)}, f32[2,272,128]{2,1,0:T(8,128)S(1)}, u32[]{:S(2)}, u32[]{:S(2)}) collective-permute-start(f32[2,272,128]{2,1,0:T(8,128)S(1)} %shard_map.122), channel_id=1, source_target_pairs={{0,1},{1,0},{2,3},{3,2},{4,5},{5,4},{6,7},{7,6},{8,9},{9,8},{10,11... | collective-permute-start | bytes 835592 | tf_op jit(solution)/shard_map/ppermute | solution.py:498
  24.4 8.7 %collective-permute-start.5 = (s16[496,128]{1,0:T(8,128)(2,1)S(1)}, s16[496,128]{1,0:T(8,128)(2,1)S(1)}, u32[]{:S(2)}, u32[]{:S(2)}) collective-permute-start(s16[496,128]{1,0:T(8,128)(2,1)S(1)} %get-tuple-element.37), channel_id=1, source_target_pairs={{0,4},{4,8},{8,12},{12,0},{1,5},{5,9},{9,13},{13,1},{2,6},{6,10},{... | collective-permute-start | bytes 380936 | tf_op jit(solution)/shard_map/ppermute | solution.py:510
  25.1 8.1 %collective-permute-start.6 = (s16[496,128]{1,0:T(8,128)(2,1)S(1)}, s16[496,128]{1,0:T(8,128)(2,1)S(1)}, u32[]{:S(2)}, u32[]{:S(2)}) collective-permute-start(s16[496,128]{1,0:T(8,128)(2,1)S(1)} %get-tuple-element.38), channel_id=1, source_target_pairs={{0,12},{4,0},{8,4},{12,8},{1,13},{5,1},{9,5},{13,9},{2,14},{6,2},{... | collective-permute-start | bytes 380936 | tf_op jit(solution)/shard_map/ppermute | solution.py:510
  28.3 4.9 %collective-permute-start.7 = (f32[8,128]{1,0:T(8,128)S(1)}, f32[8,128]{1,0:T(8,128)S(1)}, u32[]{:S(2)}, u32[]{:S(2)}) collective-permute-start(f32[8,128]{1,0:T(8,128)S(1)} %get-tuple-element.39.refs_3_), channel_id=1, source_target_pairs={{0,8},{4,12},{8,0},{12,4},{1,9},{5,13},{9,1},{13,5},{2,10},{6,14},... | collective-permute-start | bytes 12296 | tf_op jit(solution)/shard_map/ppermute | solution.py:528
  33.2 3.9 %collective-permute-start.8 = (f32[2,24,128]{2,1,0:T(8,128)S(1)}, f32[2,24,128]{2,1,0:T(8,128)S(1)}, u32[]{:S(2)}, u32[]{:S(2)}) collective-permute-start(f32[2,24,128]{2,1,0:T(8,128)S(1)} %shard_map.124.refs_4_.yp_ref), channel_id=1, source_target_pairs={{0,2},{2,0},{1,3},{3,1},{4,6},{6,4},{5,7},{7,5},{8,10},{10,8},{9,1... | collective-permute-start | bytes 73736 | tf_op jit(solution)/shard_map/ppermute | solution.py:492
  37.3 1.6 %collective-permute-start.9 = (f32[2,272,128]{2,1,0:T(8,128)S(1)}, f32[2,272,128]{2,1,0:T(8,128)S(1)}, u32[]{:S(2)}, u32[]{:S(2)}) collective-permute-start(f32[2,272,128]{2,1,0:T(8,128)S(1)} %shard_map.125), channel_id=1, source_target_pairs={{0,1},{1,0},{2,3},{3,2},{4,5},{5,4},{6,7},{7,6},{8,9},{9,8},{10,11... | collective-permute-start | bytes 835592 | tf_op jit(solution)/shard_map/ppermute | solution.py:498
  38.9 11.8 %copy-start = (f32[16]{0:T(128)S(1)}, f32[16]{0:T(128)}, u32[]{:S(2)}) copy-start(f32[16]{0:T(128)} %param.13) | copy-start | bytes 196
  38.9 11.8 %copy-start.1 = (f32[16]{0:T(128)S(1)}, f32[16]{0:T(128)}, u32[]{:S(2)}) copy-start(f32[16]{0:T(128)} %param.15) | copy-start | bytes 196
  39.5 5.3 %collective-permute-start.10 = (bf16[2,16,128]{2,1,0:T(8,128)(2,1)S(1)}, bf16[2,16,128]{2,1,0:T(8,128)(2,1)S(1)}, u32[]{:S(2)}, u32[]{:S(2)}) collective-permute-start(bf16[2,16,128]{2,1,0:T(8,128)(2,1)S(1)} %shard_map.127), channel_id=1, source_target_pairs={{0,2},{2,0},{1,3},{3,1},{4,6},{6,4},{5,7},{7,5},{8,10},{10,8},{9,1... | collective-permute-start | bytes 24584 | tf_op jit(solution)/shard_map/ppermute | solution.py:492
  44.9 6.6 %collective-permute-start.13 = (bf16[80,128]{1,0:T(8,128)(2,1)S(1)}, bf16[80,128]{1,0:T(8,128)(2,1)S(1)}, u32[]{:S(2)}, u32[]{:S(2)}) collective-permute-start(bf16[80,128]{1,0:T(8,128)(2,1)S(1)} %shard_map.128.plane_ref.refs_1_), channel_id=1, source_target_pairs={{0,8},{4,12},{8,0},{12,4},{1,9},{5,13},{9,1},{13,5},{2,10},{6,14},... | collective-permute-start | bytes 61448 | tf_op jit(solution)/shard_map/ppermute | solution.py:776
  46.9 5.6 %collective-permute-start.11 = (bf16[80,128]{1,0:T(8,128)(2,1)S(1)}, bf16[80,128]{1,0:T(8,128)(2,1)S(1)}, u32[]{:S(2)}, u32[]{:S(2)}) collective-permute-start(bf16[80,128]{1,0:T(8,128)(2,1)S(1)} %shard_map.128.plane_ref.refs_1_), channel_id=1, source_target_pairs={{0,4},{4,8},{8,12},{12,0},{1,5},{5,9},{9,13},{13,1},{2,6},{6,10},{... | collective-permute-start | bytes 61448 | tf_op jit(solution)/shard_map/ppermute | solution.py:776
  47.7 4.8 %collective-permute-start.12 = (bf16[80,128]{1,0:T(8,128)(2,1)S(1)}, bf16[80,128]{1,0:T(8,128)(2,1)S(1)}, u32[]{:S(2)}, u32[]{:S(2)}) collective-permute-start(bf16[80,128]{1,0:T(8,128)(2,1)S(1)} %shard_map.128.plane_ref.refs_1_), channel_id=1, source_target_pairs={{0,12},{4,0},{8,4},{12,8},{1,13},{5,1},{9,5},{13,9},{2,14},{6,2},{... | collective-permute-start | bytes 61448 | tf_op jit(solution)/shard_map/ppermute | solution.py:776
  50.7 2.3 %collective-permute-start.14 = (bf16[80,128]{1,0:T(8,128)(2,1)S(1)}, bf16[80,128]{1,0:T(8,128)(2,1)S(1)}, u32[]{:S(2)}, u32[]{:S(2)}) collective-permute-start(bf16[80,128]{1,0:T(8,128)(2,1)S(1)} %shard_map.128.plane_ref.refs_1_), channel_id=1, source_target_pairs={{0,1},{1,0},{2,3},{3,2},{4,5},{5,4},{6,7},{7,6},{8,9},{9,8},{10,11... | collective-permute-start | bytes 61448 | tf_op jit(solution)/shard_map/ppermute | solution.py:498
  51.5 1.5 %collective-permute-start.17 = (bf16[80,128]{1,0:T(8,128)(2,1)S(1)}, bf16[80,128]{1,0:T(8,128)(2,1)S(1)}, u32[]{:S(2)}, u32[]{:S(2)}) collective-permute-start(bf16[80,128]{1,0:T(8,128)(2,1)S(1)} %collective-permute-done.13.refs_4_), channel_id=1, source_target_pairs={{0,1},{1,0},{2,3},{3,2},{4,5},{5,4},{6,7},{7,6},{8,9},{9,8},{10,11... | collective-permute-start | bytes 61448 | tf_op jit(solution)/shard_map/ppermute | solution.py:498
  52.5 1.2 %collective-permute-start.15 = (bf16[80,128]{1,0:T(8,128)(2,1)S(1)}, bf16[80,128]{1,0:T(8,128)(2,1)S(1)}, u32[]{:S(2)}, u32[]{:S(2)}) collective-permute-start(bf16[80,128]{1,0:T(8,128)(2,1)S(1)} %collective-permute-done.11.refs_2_), channel_id=1, source_target_pairs={{0,1},{1,0},{2,3},{3,2},{4,5},{5,4},{6,7},{7,6},{8,9},{9,8},{10,11... | collective-permute-start | bytes 61448 | tf_op jit(solution)/shard_map/ppermute | solution.py:498
  52.5 1.4 %collective-permute-start.16 = (bf16[80,128]{1,0:T(8,128)(2,1)S(1)}, bf16[80,128]{1,0:T(8,128)(2,1)S(1)}, u32[]{:S(2)}, u32[]{:S(2)}) collective-permute-start(bf16[80,128]{1,0:T(8,128)(2,1)S(1)} %collective-permute-done.12.refs_3_), channel_id=1, source_target_pairs={{0,1},{1,0},{2,3},{3,2},{4,5},{5,4},{6,7},{7,6},{8,9},{9,8},{10,11... | collective-permute-start | bytes 61448 | tf_op jit(solution)/shard_map/ppermute | solution.py:498

commit v17 on v16

--- a/solution.py
+++ b/solution.py
@@ -441,8 +441,8 @@
 
 def step_b(ride_y, ride_z):
     def kernel(f_ref, a2_ref, ae2_ref, lo_ref, hi_ref, yr_ref, zr_ref, yp_ref, l_hbm,
-               f3_hbm, dmg_hbm, flux_hbm, pool_ref, *rest):
-        *scratch, pool_scr, l_ref, f3_ref, dmg_ref, flux_ref, l_sem, sems = rest
+               f3_ref, dmg_ref, flux_ref, pool_ref, *rest):
+        *scratch, pool_scr, l_ref, l_sem = rest
         nx, ny, nz = f_ref.shape
         labels_in = pltpu.make_async_copy(l_hbm, l_ref, l_sem)
         labels_in.start()
@@ -450,8 +450,7 @@
         mean = weighted_mean(yp_ref, yr_ref, zr_ref, ride_y, ride_z)
         potentials_b(g, mean, a2_ref, ae2_ref, (f_ref, lo_ref, hi_ref, yr_ref, zr_ref), scratch, [(0, ny)], True)
         labels_in.wait()
-        copies = []
-        for k, (r, n) in enumerate(chunks(OFF, OFF + ny, 48)):
+        for r, n in chunks(OFF, OFF + ny, 48):
             s = slice(r - OFF, r - OFF + n)
             pooled = [None] * 4
             for x in range(nx):
@@ -462,12 +461,7 @@
                 pooled = [v if p is None else p + v for p, v in zip(pooled, values)]
             for i in range(4):
                 pool_scr[i, s, :] = pooled[i]
-            for i, (src, dst) in enumerate(((f3_ref, f3_hbm), (dmg_ref, dmg_hbm), (flux_ref, flux_hbm))):
-                copies.append(pltpu.make_async_copy(src.at[:, s, :], dst.at[:, s, :], sems.at[i, k]))
-                copies[-1].start()
         pool_ref[...] = pool_rows(pool_scr, ny // 4, nz).astype(BF16)
-        for c in copies:
-            c.wait()
     return kernel
 
 
@@ -565,17 +559,18 @@
     (edge,) = call(
         edge_b(ride_y, ride_z), [((2, 16, nz), BF16)], *last, edge_labels,
         scratch=scratch + [pltpu.VMEM((4, 32, nz), F32)])
-    fraction, damage_field, flux_sum, pooled = call(
+    fraction, damage_field, flux_sum, pooled = pl.pallas_call(
         step_b(ride_y, ride_z),
-        [(block, F32), (block, F32), (block, F32), ((ny // 4, nz), BF16)], *last, labels,
-        in_specs=[VMEM] * 8 + [HBM], out_specs=[HBM] * 3 + [VMEM],
-        scratch=scratch + [
-            pltpu.VMEM((4, ny, nz), F32), pltpu.VMEM(block, jnp.int32),
-            pltpu.VMEM(block, F32), pltpu.VMEM(block, F32), pltpu.VMEM(block, F32),
-            pltpu.SemaphoreType.DMA, pltpu.SemaphoreType.DMA((3, len(chunks(OFF, OFF + ny, 48))))])
+        in_specs=[VMEM] * 8 + [HBM],
+        out_specs=[VMEM] * 4,
+        out_shape=[pltpu.VMEM(block, F32)] * 3 + [jax.ShapeDtypeStruct((ny // 4, nz), BF16)],
+        scratch_shapes=scratch + [
+            pltpu.VMEM((4, ny, nz), F32), pltpu.VMEM(block, jnp.int32), pltpu.SemaphoreType.DMA],
+        compiler_params=pltpu.CompilerParams(vmem_limit_bytes=16 * 1024 * 1024),
+    )(*last, labels)
     ids = jnp.broadcast_to(jnp.stack([lax.axis_index(a) for a in ("gx", "gy", "gz")])[:, None], (3, nz))
-    crack_score = detector(pooled, edge, ids, weights + (b_first[None], b_second[None]), ny // 4, nz // 4)
-    return (fraction, damage_field, flux_sum, crack_score)
+    return detector(
+        pooled, edge, ids, weights + (b_first[None], b_second[None]), (fraction, damage_field, flux_sum), ny // 4, nz // 4)
 
 
 CH = 16
@@ -677,8 +672,14 @@
         ids_ref = refs[0]
         own = refs[1:2 + n]
         other = refs[2 + n:3 + 2 * n]
-        t1_ref, t2_ref, t3_ref, bias_ref, out_ref = refs[3 + 2 * n:8 + 2 * n]
-        in_ref, beside_ref, lhs1_ref, act1_ref, lhs2_ref, act2_ref, tail_ref = refs[8 + 2 * n:]
+        t1_ref, t2_ref, t3_ref, bias_ref = refs[3 + 2 * n:7 + 2 * n]
+        fields = refs[7 + 2 * n:10 + 2 * n]
+        out_ref = refs[10 + 2 * n]
+        fields_hbm = refs[11 + 2 * n:14 + 2 * n]
+        in_ref, beside_ref, lhs1_ref, act1_ref, lhs2_ref, act2_ref, tail_ref, sems = refs[14 + 2 * n:]
+        copies = [pltpu.make_async_copy(src, dst, sems.at[k]) for k, (src, dst) in enumerate(zip(fields, fields_hbm))]
+        for c in copies:
+            c.start()
         ix, iy, iz = ids_ref[0:1, 0:1], ids_ref[1:2, 0:1], ids_ref[2:3, 0:1]
         half = own[0].shape[1]
         pz = half // CIN
@@ -754,10 +755,12 @@
         for j in (1, 2):
             score = score + pltpu.roll(tail_ref[j:j + py, :], 128 - j * pz, 1)
         out_ref[0] = jnp.transpose(score)[0:pz, :] + bias_ref[2:3, 0:1]
+        for c in copies:
+            c.wait()
     return kernel
 
 
-def detector(pooled, edge, ids, weights, py, pz):
+def detector(pooled, edge, ids, weights, fields, py, pz):
     counts = tuple(lax.axis_size(a) for a in ("gx", "gy", "gz"))
     half = pooled.shape[1]
     assert half == 128 and pz * CIN == half and pz * 3 <= 128
@@ -780,9 +783,10 @@
         *weights, plane)
     own[-1], *matrices = lax.optimization_barrier((own[-1], *matrices))
     other = [z_neighbour(v, "gz", False) for v in own]
-    args = (ids, *own, *other, *matrices)
-    (score,) = call(
-        conv_kernel(py, counts, shifts), [((1, pz, py), F32)], *args,
+    args = (ids, *own, *other, *matrices, *fields)
+    score, *fields = call(
+        conv_kernel(py, counts, shifts), [((1, pz, py), F32)] + [(v.shape, F32) for v in fields], *args,
+        out_specs=[VMEM] + [HBM] * 3,
         scratch=[
             pltpu.VMEM((7, tall, half), F32),
             pltpu.VMEM((7, tall, half), F32),
@@ -791,8 +795,9 @@
             pltpu.VMEM((5, blocks, rows, 512), BF16),
             pltpu.VMEM((3, rows, width), BF16),
             pltpu.VMEM((rows + 8, 128), F32),
+            pltpu.SemaphoreType.DMA((3,)),
         ], mib=32)
-    return jnp.swapaxes(score, 1, 2)
+    return *fields, jnp.swapaxes(score, 1, 2)
 
 
 def solution(mesh):

time: 57.7 us -> 59.5 us (1.031)
  waiting for transfers between devices: 18.3 us -> 22.7 us
  starting transfers between devices: 21.6 us -> 19.7 us
  Pallas kernels: 13.1 us -> 12.4 us
    ppermute x3, waiting for transfers between devices: 0.41 us -> 4.79 us  [detector(): own = [plane] + [lax.ppermute(plane, 'gx', ring('gx', s)) for s in shifts]]
    pallas_call x11 -> x10, Pallas kernels: 13.1 us -> 9.4 us  [call(): pl.pallas_call(kernel, in_specs=in_specs or [VMEM] * len(args), out_specs...]
    pallas_call x0 -> x1, Pallas kernels: none -> 3.01 us  [body(): pl.pallas_call(step_b(ride_y, ride_z), in_specs=[VMEM] * 8 + [HBM], out_s...]
    ppermute x3, starting transfers between devices: 5.81 us -> 4.4 us  [detector(): own = [plane] + [lax.ppermute(plane, 'gx', ring('gx', s)) for s in shifts]]
  transfers between devices with their start and end apart: 18 -> 18, of which waited for: 9 -> 10; matrix products, arithmetic and copies ran while one was open for 5% -> 5% of each run, Pallas kernels for 8% -> 6%
where the time goes in v17:
time: 59.5 us; the launch traced here: 59.2 us
  waiting for transfers between devices  22.7 us (38%)
  starting transfers between devices  19.7 us (33%)
  Pallas kernels  12.4 us (21%)
  local copies, waits for them, and re-layouts  2.93 us (5%)
  between operations  1.41 us (2%)
    pallas_call x10, Pallas kernels, call(): pl.pallas_call(kernel, in_specs=in_specs or [VMEM] * len(args), out_specs...  9.4 us
    ppermute x2, waiting for transfers between devices, start(): return (sums, lax.ppermute(sums, 'gx', ring('gx', 2)))  9.28 us
    ppermute x2, starting transfers between devices, x_sides(): lax.ppermute(lo, 'gx', ring('gx', -1))  5.32 us
    ppermute x3, waiting for transfers between devices, detector(): own = [plane] + [lax.ppermute(plane, 'gx', ring('gx', s)) for s in shifts]  4.79 us
    ppermute x3, waiting for transfers between devices, both_sides(): return lax.ppermute(pay, axis, ring(axis, 1))  4.67 us
    ppermute x3, starting transfers between devices, both_sides(): return lax.ppermute(pay, axis, ring(axis, 1))  4.61 us
    ppermute x3, starting transfers between devices, detector(): own = [plane] + [lax.ppermute(plane, 'gx', ring('gx', s)) for s in shifts]  4.4 us
    ppermute x6, waiting for transfers between devices, z_neighbour(): return lax.ppermute(pay, axis, ring(axis, 1))  3.93 us
  transfers between devices with their start and end apart: 18, of which 10 were waited for; matrix products, arithmetic and copies ran while one was open for 5% of the time, Pallas kernels for 6%

profile of v17, /device:TPU:0, one launch (start us, length us, event | category | flops | bytes accessed | tf_op | source)
XLA Modules:
  0.0 59.2 jit_solution(7087788107822178724)
XLA Ops:
  0.6 1.6 %shard_map.120 = (f32[4,240,128]{2,1,0:T(8,128)S(1)}, f32[4,240,128]{2,1,0:T(8,128)S(1)}, s16[736,128]{1,0:T(8,128)(2,1)S(1)}, s16[736,128]{1,0:T(8,128)(2,1)S(1...) custom-call(f32[4,240,128]{2,1,0:T(8,128)} %c_hbm.1, f32[4,240,128]{2,1,0:T(8,128)} %d_hbm.1, s32[4,240,128]{2,1,0:T(8,128)} %l_hbm.3), custom_call_target="tpu_custom_call" | custom-call | tf_op jit(solution)/shard_map/pallas_call | solution.py:73
  2.3 3.1 %collective-permute-start = (s16[736,128]{1,0:T(8,128)(2,1)S(1)}, s16[736,128]{1,0:T(8,128)(2,1)S(1)}, u32[]{:S(2)}, u32[]{:S(2)}) collective-permute-start(s16[736,128]{1,0:T(8,128)(2,1)S(1)} %get-tuple-element.35), channel_id=1, source_target_pairs={{0,4},{4,8},{8,12},{12,0},{1,5},{5,9},{9,13},{13,1},{2,6},{6,10},{... | collective-permute-start | bytes 565256 | tf_op jit(solution)/shard_map/ppermute | solution.py:504
  5.3 2.1 %collective-permute-start.1 = (s16[736,128]{1,0:T(8,128)(2,1)S(1)}, s16[736,128]{1,0:T(8,128)(2,1)S(1)}, u32[]{:S(2)}, u32[]{:S(2)}) collective-permute-start(s16[736,128]{1,0:T(8,128)(2,1)S(1)} %get-tuple-element.36), channel_id=1, source_target_pairs={{0,12},{4,0},{8,4},{12,8},{1,13},{5,1},{9,5},{13,9},{2,14},{6,2},{... | collective-permute-start | bytes 565256 | tf_op jit(solution)/shard_map/ppermute | solution.py:504
  7.4 0.9 %collective-permute-start.2 = (f32[8,128]{1,0:T(8,128)S(1)}, f32[8,128]{1,0:T(8,128)S(1)}, u32[]{:S(2)}, u32[]{:S(2)}) collective-permute-start(f32[8,128]{1,0:T(8,128)S(1)} %get-tuple-element.37.refs_4_), channel_id=1, source_target_pairs={{0,8},{4,12},{8,0},{12,4},{1,9},{5,13},{9,1},{13,5},{2,10},{6,14},... | collective-permute-start | bytes 12296 | tf_op jit(solution)/shard_map/ppermute | solution.py:522
  9.0 0.8 %copy.18 = bf16[27,1,16]{2,0,1:T(8,128)(2,1)S(1)} copy(bf16[27,1,16]{0,2,1:T(8,128)(2,1)} %param.16) | data formatting | bytes 1728 | tf_op args[7]
  9.8 0.1 copy.19
  10.0 0.8 %copy.16 = bf16[27,4,16]{2,1,0:T(4,128)(2,1)S(1)} copy(bf16[27,4,16]{0,1,2:T(4,128)(2,1)} %bitcast.27) | data formatting | bytes 6912 | tf_op jit(solution)/shard_map/transpose | solution.py:645
  10.8 1.0 %copy.17 = bf16[27,16,16]{2,1,0:T(8,128)(2,1)S(1)} copy(bf16[27,16,16]{0,1,2:T(8,128)(2,1)} %bitcast.25) | data formatting | bytes 27648 | tf_op jit(solution)/shard_map/transpose | solution.py:646
  11.8 4.4 %collective-permute-done.2.refs_5_ = f32[8,128]{1,0:T(8,128)S(1)} collective-permute-done((f32[8,128]{1,0:T(8,128)S(1)}, f32[8,128]{1,0:T(8,128)S(1)}, u32[]{:S(2)}, u32[]{:S(2)}) %collective-permute-start.2) | collective-permute-done | bytes 4128 | tf_op jit(solution)/shard_map/ppermute | solution.py:522
  16.3 0.0 collective-permute-done.refs_2_.lo_ref
  16.3 0.0 collective-permute-done.1.refs_3_.hi_ref
  16.3 1.6 %collective-permute-start.3 = (f32[2,24,128]{2,1,0:T(8,128)S(1)}, f32[2,24,128]{2,1,0:T(8,128)S(1)}, u32[]{:S(2)}, u32[]{:S(2)}) collective-permute-start(f32[2,24,128]{2,1,0:T(8,128)S(1)} %shard_map.121.refs_5_.yp_ref), channel_id=1, source_target_pairs={{0,2},{2,0},{1,3},{3,1},{4,6},{6,4},{5,7},{7,5},{8,10},{10,8},{9,1... | collective-permute-start | bytes 73736 | tf_op jit(solution)/shard_map/ppermute | solution.py:486
  17.9 2.3 %collective-permute-done.3.refs_4_.yr_ref = f32[2,24,128]{2,1,0:T(8,128)S(1)} collective-permute-done((f32[2,24,128]{2,1,0:T(8,128)S(1)}, f32[2,24,128]{2,1,0:T(8,128)S(1)}, u32[]{:S(2)}, u32[]{:S(2)}) %collective-permute-start.3) | collective-permute-done | bytes 24608 | tf_op jit(solution)/shard_map/ppermute | solution.py:486
  20.2 0.3 shard_map.122
  20.6 0.1 collective-permute-start.4
  20.6 1.5 %collective-permute-done.4.zr_ref = f32[2,272,128]{2,1,0:T(8,128)S(1)} collective-permute-done((f32[2,272,128]{2,1,0:T(8,128)S(1)}, f32[2,272,128]{2,1,0:T(8,128)S(1)}, u32[]{:S(2)}, u32[]{:S(2)}) %collective-permute-start.4) | collective-permute-done | bytes 278560 | tf_op jit(solution)/shard_map/ppermute | solution.py:492
  22.2 2.2 %shard_map.123 = (f32[4,240,128]{2,1,0:T(8,128)S(1)}, f32[6,272,128]{2,1,0:T(8,128)S(1)}, f32[240,128]{1,0:T(8,128)S(1)}, s16[496,128]{1,0:T(8,128)(2,1)S(1)}, s...) custom-call(f32[4,240,128]{2,1,0:T(8,128)S(1)} %get-tuple-element.33.refs_0_.f_ref, ...), custom_call_target="tpu_custom_call" | custom-call | tf_op jit(solution)/shard_map/pallas_call | solution.py:73
  24.4 0.6 %collective-permute-start.5 = (s16[496,128]{1,0:T(8,128)(2,1)S(1)}, s16[496,128]{1,0:T(8,128)(2,1)S(1)}, u32[]{:S(2)}, u32[]{:S(2)}) collective-permute-start(s16[496,128]{1,0:T(8,128)(2,1)S(1)} %get-tuple-element.41), channel_id=1, source_target_pairs={{0,4},{4,8},{8,12},{12,0},{1,5},{5,9},{9,13},{13,1},{2,6},{6,10},{... | collective-permute-start | bytes 380936 | tf_op jit(solution)/shard_map/ppermute | solution.py:504
  25.1 3.2 %collective-permute-start.6 = (s16[496,128]{1,0:T(8,128)(2,1)S(1)}, s16[496,128]{1,0:T(8,128)(2,1)S(1)}, u32[]{:S(2)}, u32[]{:S(2)}) collective-permute-start(s16[496,128]{1,0:T(8,128)(2,1)S(1)} %get-tuple-element.42), channel_id=1, source_target_pairs={{0,12},{4,0},{8,4},{12,8},{1,13},{5,1},{9,5},{13,9},{2,14},{6,2},{... | collective-permute-start | bytes 380936 | tf_op jit(solution)/shard_map/ppermute | solution.py:504
  28.3 0.0 collective-permute-start.7
  28.3 4.9 %collective-permute-done.7.refs_4_ = f32[8,128]{1,0:T(8,128)S(1)} collective-permute-done((f32[8,128]{1,0:T(8,128)S(1)}, f32[8,128]{1,0:T(8,128)S(1)}, u32[]{:S(2)}, u32[]{:S(2)}) %collective-permute-start.7) | collective-permute-done | bytes 4128 | tf_op jit(solution)/shard_map/ppermute | solution.py:522
  33.2 0.0 collective-permute-done.5.refs_1_.lo_ref
  33.2 0.0 collective-permute-done.6.refs_2_.hi_ref
  33.2 1.6 %collective-permute-start.8 = (f32[2,24,128]{2,1,0:T(8,128)S(1)}, f32[2,24,128]{2,1,0:T(8,128)S(1)}, u32[]{:S(2)}, u32[]{:S(2)}) collective-permute-start(f32[2,24,128]{2,1,0:T(8,128)S(1)} %shard_map.124.refs_4_.yp_ref), channel_id=1, source_target_pairs={{0,2},{2,0},{1,3},{3,1},{4,6},{6,4},{5,7},{7,5},{8,10},{10,8},{9,1... | collective-permute-start | bytes 73736 | tf_op jit(solution)/shard_map/ppermute | solution.py:486
  34.7 2.3 %collective-permute-done.8.refs_3_.yr_ref = f32[2,24,128]{2,1,0:T(8,128)S(1)} collective-permute-done((f32[2,24,128]{2,1,0:T(8,128)S(1)}, f32[2,24,128]{2,1,0:T(8,128)S(1)}, u32[]{:S(2)}, u32[]{:S(2)}) %collective-permute-start.8) | collective-permute-done | bytes 24608 | tf_op jit(solution)/shard_map/ppermute | solution.py:486
  37.1 0.2 shard_map.125
  37.3 0.1 collective-permute-start.9
  37.4 1.5 %collective-permute-done.9.zr_ref = f32[2,272,128]{2,1,0:T(8,128)S(1)} collective-permute-done((f32[2,272,128]{2,1,0:T(8,128)S(1)}, f32[2,272,128]{2,1,0:T(8,128)S(1)}, u32[]{:S(2)}, u32[]{:S(2)}) %collective-permute-start.9) | collective-permute-done | bytes 278560 | tf_op jit(solution)/shard_map/ppermute | solution.py:492
  38.9 0.6 shard_map.127
  39.5 1.5 %collective-permute-start.10 = (bf16[2,16,128]{2,1,0:T(8,128)(2,1)S(1)}, bf16[2,16,128]{2,1,0:T(8,128)(2,1)S(1)}, u32[]{:S(2)}, u32[]{:S(2)}) collective-permute-start(bf16[2,16,128]{2,1,0:T(8,128)(2,1)S(1)} %shard_map.127), channel_id=1, source_target_pairs={{0,2},{2,0},{1,3},{3,1},{4,6},{6,4},{5,7},{7,5},{8,10},{10,8},{9,1... | collective-permute-start | bytes 24584 | tf_op jit(solution)/shard_map/ppermute | solution.py:486
  41.0 0.1 pad_add_fusion
  41.0 3.0 %shard_map.126 = (f32[4,240,128]{2,1,0:T(8,128)S(1)}, f32[4,240,128]{2,1,0:T(8,128)S(1)}, f32[4,240,128]{2,1,0:T(8,128)S(1)}, bf16[60,128]{1,0:T(8,128)(2,1)S(1)}) custom-call(f32[4,240,128]{2,1,0:T(8,128)S(1)} %get-tuple-element.38.refs_0_.f_ref, f32[6,272,128]{2,1,0:T(8,128)S(1)} %get-tuple-element.39.a2_ref, f32[240,128]{1,0:T(8,128)S(1)} %get-tuple-element.40.ae2_ref, ...), custom_call_target="tpu_custom_call" | custom-call | tf_op jit(solution)/shard_map/pallas_call | solution.py:562
  44.1 0.0 collective-permute-done.10.yr_ref
  44.1 0.1 broadcast_in_dim.15.ids_ref.refs_0_
  44.2 2.0 %collective-permute-start.13 = (bf16[80,128]{1,0:T(8,128)(2,1)S(1)}, bf16[80,128]{1,0:T(8,128)(2,1)S(1)}, u32[]{:S(2)}, u32[]{:S(2)}) collective-permute-start(bf16[80,128]{1,0:T(8,128)(2,1)S(1)} %shard_map.128.plane_ref.refs_1_), channel_id=1, source_target_pairs={{0,8},{4,12},{8,0},{12,4},{1,9},{5,13},{9,1},{13,5},{2,10},{6,14},... | collective-permute-start | bytes 61448 | tf_op jit(solution)/shard_map/ppermute | solution.py:779
  46.2 2.4 %collective-permute-start.12 = (bf16[80,128]{1,0:T(8,128)(2,1)S(1)}, bf16[80,128]{1,0:T(8,128)(2,1)S(1)}, u32[]{:S(2)}, u32[]{:S(2)}) collective-permute-start(bf16[80,128]{1,0:T(8,128)(2,1)S(1)} %shard_map.128.plane_ref.refs_1_), channel_id=1, source_target_pairs={{0,12},{4,0},{8,4},{12,8},{1,13},{5,1},{9,5},{13,9},{2,14},{6,2},{... | collective-permute-start | bytes 61448 | tf_op jit(solution)/shard_map/ppermute | solution.py:779
  48.6 0.0 collective-permute-start.11
  48.6 0.8 %shard_map.129 = (bf16[3,512,640]{2,1,0:T(8,128)(2,1)S(1)}, bf16[3,512,128]{2,1,0:T(8,128)(2,1)S(1)}, bf16[3,640,128]{2,1,0:T(8,128)(2,1)S(1)}, f32[8,640]{1,0:T(8,128)S(1)}) custom-call(bf16[432,16]{1,0:T(8,128)(2,1)S(1)} %bitcast.20, bf16[432,16]{1,0:T(8,128)(2,1)S(1)} %bitcast.18, bf16[144,3]{1,0:T(8,128)(2,1)S(1)} %bitcast.22, f32[1,1]{1,0:T(1,128)} %bitcast.16.b3_ref, ...), custom_call_target="tpu_custom_call" | custom-call | tf_op jit(solution)/shard_map/pallas_call | solution.py:73
  49.4 0.0 collective-permute-done.13.refs_4_
  49.4 0.7 %collective-permute-done.12.refs_3_ = bf16[80,128]{1,0:T(8,128)(2,1)S(1)} collective-permute-done((bf16[80,128]{1,0:T(8,128)(2,1)S(1)}, bf16[80,128]{1,0:T(8,128)(2,1)S(1)}, u32[]{:S(2)}, u32[]{:S(2)}) %collective-permute-start.12) | collective-permute-done | bytes 20512 | tf_op jit(solution)/shard_map/ppermute | solution.py:779
  50.1 0.0 collective-permute-start.16
  50.1 4.1 %collective-permute-done.11.refs_2_ = bf16[80,128]{1,0:T(8,128)(2,1)S(1)} collective-permute-done((bf16[80,128]{1,0:T(8,128)(2,1)S(1)}, bf16[80,128]{1,0:T(8,128)(2,1)S(1)}, u32[]{:S(2)}, u32[]{:S(2)}) %collective-permute-start.11) | collective-permute-done | bytes 20512 | tf_op jit(solution)/shard_map/ppermute | solution.py:779
  54.2 0.5 collective-permute-start.17
  54.7 0.0 collective-permute-done.14.refs_5_
  54.7 0.0 collective-permute-done.16.refs_7_
  54.7 0.7 %collective-permute-done.15.refs_6_ = bf16[80,128]{1,0:T(8,128)(2,1)S(1)} collective-permute-done((bf16[80,128]{1,0:T(8,128)(2,1)S(1)}, bf16[80,128]{1,0:T(8,128)(2,1)S(1)}, u32[]{:S(2)}, u32[]{:S(2)}) %collective-permute-start.15) | collective-permute-done | bytes 20512 | tf_op jit(solution)/shard_map/ppermute | solution.py:492
  55.4 0.2 collective-permute-done.17.refs_8_
  55.5 3.6 %shard_map.130 = (f32[1,32,60]{2,1,0:T(8,128)}, f32[4,240,128]{2,1,0:T(8,128)}, f32[4,240,128]{2,1,0:T(8,128)}, f32[4,240,128]{2,1,0:T(8,128)}) custom-call(s32[3,128]{1,0:T(4,128)S(1)} %broadcast_in_dim.15.ids_ref.refs_0_, bf16[80,128]{1,0:T(8,128)(2,1)S(1)} %shard_map.128.plane_ref.refs_1_, bf16[80,128]{1,0:T(8,128)(2,1)S(1)} %collective-permute-done.11.refs_2_, ...), custom_call_target="tpu_custom_call" | custom-call | tf_op jit(solution)/shard_map/pallas_call | solution.py:73
  (11 shorter events, 0.1 us)
Async XLA Ops:
  2.3 14.0 %collective-permute-start = (s16[736,128]{1,0:T(8,128)(2,1)S(1)}, s16[736,128]{1,0:T(8,128)(2,1)S(1)}, u32[]{:S(2)}, u32[]{:S(2)}) collective-permute-start(s16[736,128]{1,0:T(8,128)(2,1)S(1)} %get-tuple-element.35), channel_id=1, source_target_pairs={{0,4},{4,8},{8,12},{12,0},{1,5},{5,9},{9,13},{13,1},{2,6},{6,10},{... | collective-permute-start | bytes 565256 | tf_op jit(solution)/shard_map/ppermute | solution.py:504
  5.3 10.9 %collective-permute-start.1 = (s16[736,128]{1,0:T(8,128)(2,1)S(1)}, s16[736,128]{1,0:T(8,128)(2,1)S(1)}, u32[]{:S(2)}, u32[]{:S(2)}) collective-permute-start(s16[736,128]{1,0:T(8,128)(2,1)S(1)} %get-tuple-element.36), channel_id=1, source_target_pairs={{0,12},{4,0},{8,4},{12,8},{1,13},{5,1},{9,5},{13,9},{2,14},{6,2},{... | collective-permute-start | bytes 565256 | tf_op jit(solution)/shard_map/ppermute | solution.py:504
  7.4 8.8 %collective-permute-start.2 = (f32[8,128]{1,0:T(8,128)S(1)}, f32[8,128]{1,0:T(8,128)S(1)}, u32[]{:S(2)}, u32[]{:S(2)}) collective-permute-start(f32[8,128]{1,0:T(8,128)S(1)} %get-tuple-element.37.refs_4_), channel_id=1, source_target_pairs={{0,8},{4,12},{8,0},{12,4},{1,9},{5,13},{9,1},{13,5},{2,10},{6,14},... | collective-permute-start | bytes 12296 | tf_op jit(solution)/shard_map/ppermute | solution.py:522
  16.3 3.9 %collective-permute-start.3 = (f32[2,24,128]{2,1,0:T(8,128)S(1)}, f32[2,24,128]{2,1,0:T(8,128)S(1)}, u32[]{:S(2)}, u32[]{:S(2)}) collective-permute-start(f32[2,24,128]{2,1,0:T(8,128)S(1)} %shard_map.121.refs_5_.yp_ref), channel_id=1, source_target_pairs={{0,2},{2,0},{1,3},{3,1},{4,6},{6,4},{5,7},{7,5},{8,10},{10,8},{9,1... | collective-permute-start | bytes 73736 | tf_op jit(solution)/shard_map/ppermute | solution.py:486
  20.6 1.6 %collective-permute-start.4 = (f32[2,272,128]{2,1,0:T(8,128)S(1)}, f32[2,272,128]{2,1,0:T(8,128)S(1)}, u32[]{:S(2)}, u32[]{:S(2)}) collective-permute-start(f32[2,272,128]{2,1,0:T(8,128)S(1)} %shard_map.122), channel_id=1, source_target_pairs={{0,1},{1,0},{2,3},{3,2},{4,5},{5,4},{6,7},{7,6},{8,9},{9,8},{10,11... | collective-permute-start | bytes 835592 | tf_op jit(solution)/shard_map/ppermute | solution.py:492
  24.4 8.7 %collective-permute-start.5 = (s16[496,128]{1,0:T(8,128)(2,1)S(1)}, s16[496,128]{1,0:T(8,128)(2,1)S(1)}, u32[]{:S(2)}, u32[]{:S(2)}) collective-permute-start(s16[496,128]{1,0:T(8,128)(2,1)S(1)} %get-tuple-element.41), channel_id=1, source_target_pairs={{0,4},{4,8},{8,12},{12,0},{1,5},{5,9},{9,13},{13,1},{2,6},{6,10},{... | collective-permute-start | bytes 380936 | tf_op jit(solution)/shard_map/ppermute | solution.py:504
  25.1 8.1 %collective-permute-start.6 = (s16[496,128]{1,0:T(8,128)(2,1)S(1)}, s16[496,128]{1,0:T(8,128)(2,1)S(1)}, u32[]{:S(2)}, u32[]{:S(2)}) collective-permute-start(s16[496,128]{1,0:T(8,128)(2,1)S(1)} %get-tuple-element.42), channel_id=1, source_target_pairs={{0,12},{4,0},{8,4},{12,8},{1,13},{5,1},{9,5},{13,9},{2,14},{6,2},{... | collective-permute-start | bytes 380936 | tf_op jit(solution)/shard_map/ppermute | solution.py:504
  28.3 4.9 %collective-permute-start.7 = (f32[8,128]{1,0:T(8,128)S(1)}, f32[8,128]{1,0:T(8,128)S(1)}, u32[]{:S(2)}, u32[]{:S(2)}) collective-permute-start(f32[8,128]{1,0:T(8,128)S(1)} %get-tuple-element.43.refs_3_), channel_id=1, source_target_pairs={{0,8},{4,12},{8,0},{12,4},{1,9},{5,13},{9,1},{13,5},{2,10},{6,14},... | collective-permute-start | bytes 12296 | tf_op jit(solution)/shard_map/ppermute | solution.py:522
  33.2 3.9 %collective-permute-start.8 = (f32[2,24,128]{2,1,0:T(8,128)S(1)}, f32[2,24,128]{2,1,0:T(8,128)S(1)}, u32[]{:S(2)}, u32[]{:S(2)}) collective-permute-start(f32[2,24,128]{2,1,0:T(8,128)S(1)} %shard_map.124.refs_4_.yp_ref), channel_id=1, source_target_pairs={{0,2},{2,0},{1,3},{3,1},{4,6},{6,4},{5,7},{7,5},{8,10},{10,8},{9,1... | collective-permute-start | bytes 73736 | tf_op jit(solution)/shard_map/ppermute | solution.py:486
  37.3 1.6 %collective-permute-start.9 = (f32[2,272,128]{2,1,0:T(8,128)S(1)}, f32[2,272,128]{2,1,0:T(8,128)S(1)}, u32[]{:S(2)}, u32[]{:S(2)}) collective-permute-start(f32[2,272,128]{2,1,0:T(8,128)S(1)} %shard_map.125), channel_id=1, source_target_pairs={{0,1},{1,0},{2,3},{3,2},{4,5},{5,4},{6,7},{7,6},{8,9},{9,8},{10,11... | collective-permute-start | bytes 835592 | tf_op jit(solution)/shard_map/ppermute | solution.py:492
  38.9 9.7 %copy-start = (f32[16]{0:T(128)S(1)}, f32[16]{0:T(128)}, u32[]{:S(2)}) copy-start(f32[16]{0:T(128)} %param.13) | copy-start | bytes 196
  38.9 9.7 %copy-start.1 = (f32[16]{0:T(128)S(1)}, f32[16]{0:T(128)}, u32[]{:S(2)}) copy-start(f32[16]{0:T(128)} %param.15) | copy-start | bytes 196
  39.5 4.6 %collective-permute-start.10 = (bf16[2,16,128]{2,1,0:T(8,128)(2,1)S(1)}, bf16[2,16,128]{2,1,0:T(8,128)(2,1)S(1)}, u32[]{:S(2)}, u32[]{:S(2)}) collective-permute-start(bf16[2,16,128]{2,1,0:T(8,128)(2,1)S(1)} %shard_map.127), channel_id=1, source_target_pairs={{0,2},{2,0},{1,3},{3,1},{4,6},{6,4},{5,7},{7,5},{8,10},{10,8},{9,1... | collective-permute-start | bytes 24584 | tf_op jit(solution)/shard_map/ppermute | solution.py:486
  44.2 5.2 %collective-permute-start.13 = (bf16[80,128]{1,0:T(8,128)(2,1)S(1)}, bf16[80,128]{1,0:T(8,128)(2,1)S(1)}, u32[]{:S(2)}, u32[]{:S(2)}) collective-permute-start(bf16[80,128]{1,0:T(8,128)(2,1)S(1)} %shard_map.128.plane_ref.refs_1_), channel_id=1, source_target_pairs={{0,8},{4,12},{8,0},{12,4},{1,9},{5,13},{9,1},{13,5},{2,10},{6,14},... | collective-permute-start | bytes 61448 | tf_op jit(solution)/shard_map/ppermute | solution.py:779
  46.2 3.9 %collective-permute-start.12 = (bf16[80,128]{1,0:T(8,128)(2,1)S(1)}, bf16[80,128]{1,0:T(8,128)(2,1)S(1)}, u32[]{:S(2)}, u32[]{:S(2)}) collective-permute-start(bf16[80,128]{1,0:T(8,128)(2,1)S(1)} %shard_map.128.plane_ref.refs_1_), channel_id=1, source_target_pairs={{0,12},{4,0},{8,4},{12,8},{1,13},{5,1},{9,5},{13,9},{2,14},{6,2},{... | collective-permute-start | bytes 61448 | tf_op jit(solution)/shard_map/ppermute | solution.py:779
  48.6 5.6 %collective-permute-start.11 = (bf16[80,128]{1,0:T(8,128)(2,1)S(1)}, bf16[80,128]{1,0:T(8,128)(2,1)S(1)}, u32[]{:S(2)}, u32[]{:S(2)}) collective-permute-start(bf16[80,128]{1,0:T(8,128)(2,1)S(1)} %shard_map.128.plane_ref.refs_1_), channel_id=1, source_target_pairs={{0,4},{4,8},{8,12},{12,0},{1,5},{5,9},{9,13},{13,1},{2,6},{6,10},{... | collective-permute-start | bytes 61448 | tf_op jit(solution)/shard_map/ppermute | solution.py:779
  48.6 6.1 %collective-permute-start.14 = (bf16[80,128]{1,0:T(8,128)(2,1)S(1)}, bf16[80,128]{1,0:T(8,128)(2,1)S(1)}, u32[]{:S(2)}, u32[]{:S(2)}) collective-permute-start(bf16[80,128]{1,0:T(8,128)(2,1)S(1)} %shard_map.128.plane_ref.refs_1_), channel_id=1, source_target_pairs={{0,1},{1,0},{2,3},{3,2},{4,5},{5,4},{6,7},{7,6},{8,9},{9,8},{10,11... | collective-permute-start | bytes 61448 | tf_op jit(solution)/shard_map/ppermute | solution.py:492
  50.1 4.6 %collective-permute-start.16 = (bf16[80,128]{1,0:T(8,128)(2,1)S(1)}, bf16[80,128]{1,0:T(8,128)(2,1)S(1)}, u32[]{:S(2)}, u32[]{:S(2)}) collective-permute-start(bf16[80,128]{1,0:T(8,128)(2,1)S(1)} %collective-permute-done.12.refs_3_), channel_id=1, source_target_pairs={{0,1},{1,0},{2,3},{3,2},{4,5},{5,4},{6,7},{7,6},{8,9},{9,8},{10,11... | collective-permute-start | bytes 61448 | tf_op jit(solution)/shard_map/ppermute | solution.py:492
  54.2 1.2 %collective-permute-start.15 = (bf16[80,128]{1,0:T(8,128)(2,1)S(1)}, bf16[80,128]{1,0:T(8,128)(2,1)S(1)}, u32[]{:S(2)}, u32[]{:S(2)}) collective-permute-start(bf16[80,128]{1,0:T(8,128)(2,1)S(1)} %collective-permute-done.11.refs_2_), channel_id=1, source_target_pairs={{0,1},{1,0},{2,3},{3,2},{4,5},{5,4},{6,7},{7,6},{8,9},{9,8},{10,11... | collective-permute-start | bytes 61448 | tf_op jit(solution)/shard_map/ppermute | solution.py:492
  54.2 1.4 %collective-permute-start.17 = (bf16[80,128]{1,0:T(8,128)(2,1)S(1)}, bf16[80,128]{1,0:T(8,128)(2,1)S(1)}, u32[]{:S(2)}, u32[]{:S(2)}) collective-permute-start(bf16[80,128]{1,0:T(8,128)(2,1)S(1)} %collective-permute-done.13.refs_4_), channel_id=1, source_target_pairs={{0,1},{1,0},{2,3},{3,2},{4,5},{5,4},{6,7},{7,6},{8,9},{9,8},{10,11... | collective-permute-start | bytes 61448 | tf_op jit(solution)/shard_map/ppermute | solution.py:492

commit v18 on v17

--- a/solution.py
+++ b/solution.py
@@ -773,7 +773,7 @@
         plane_kernel(py, counts[1]), [((tall, half), BF16)], ids, pooled, yr,
         scratch=[pltpu.VMEM((tall, half), F32)])
     shifts = []
-    for s in (1, -1, 2, -2, 3, -3):
+    for s in (-1, 1, 2, -2, 3, -3):
         if s % counts[0] and s % counts[0] not in shifts:
             shifts.append(s % counts[0])
     own = [plane] + [lax.ppermute(plane, "gx", ring("gx", s)) for s in shifts]

time: 59.5 us -> 57.4 us (0.965)
  waiting for transfers between devices: 22.7 us -> 19.2 us
  starting transfers between devices: 19.7 us -> 21.1 us
    ppermute x3, waiting for transfers between devices: 4.79 us -> 0.99 us  [detector(): own = [plane] + [lax.ppermute(plane, 'gx', ring('gx', s)) for s in shifts]]
    ppermute x3, starting transfers between devices: 4.4 us -> 5.81 us  [detector(): own = [plane] + [lax.ppermute(plane, 'gx', ring('gx', s)) for s in shifts]]
  transfers between devices with their start and end apart: 18 -> 18, of which waited for: 10 -> 10; matrix products, arithmetic and copies ran while one was open for 5% -> 5% of each run, Pallas kernels for 6% -> 7%
where the time goes in v18:
time: 57.4 us; the launch traced here: 57.1 us
  starting transfers between devices  21.1 us (37%)
  waiting for transfers between devices  19.2 us (33%)
  Pallas kernels  12.4 us (22%)
  local copies, waits for them, and re-layouts  2.93 us (5%)
  between operations  1.4 us (2%)
    pallas_call x10, Pallas kernels, call(): pl.pallas_call(kernel, in_specs=in_specs or [VMEM] * len(args), out_specs...  9.39 us
    ppermute x2, waiting for transfers between devices, start(): return (sums, lax.ppermute(sums, 'gx', ring('gx', 2)))  9.28 us
    ppermute x3, starting transfers between devices, detector(): own = [plane] + [lax.ppermute(plane, 'gx', ring('gx', s)) for s in shifts]  5.81 us
    ppermute x2, starting transfers between devices, x_sides(): lax.ppermute(lo, 'gx', ring('gx', -1))  5.32 us
    ppermute x3, waiting for transfers between devices, both_sides(): return lax.ppermute(pay, axis, ring(axis, 1))  4.67 us
    ppermute x3, starting transfers between devices, both_sides(): return lax.ppermute(pay, axis, ring(axis, 1))  4.61 us
    ppermute x6, waiting for transfers between devices, z_neighbour(): return lax.ppermute(pay, axis, ring(axis, 1))  4.27 us
    ppermute x2, starting transfers between devices, x_sides(): lax.ppermute(hi, 'gx', ring('gx', 1))  3.72 us
  transfers between devices with their start and end apart: 18, of which 10 were waited for; matrix products, arithmetic and copies ran while one was open for 5% of the time, Pallas kernels for 7%

profile of v18, /device:TPU:0, one launch (start us, length us, event | category | flops | bytes accessed | tf_op | source)
XLA Modules:
  0.0 57.1 jit_solution(13406883634980978774)
XLA Ops:
  0.6 1.6 %shard_map.120 = (f32[4,240,128]{2,1,0:T(8,128)S(1)}, f32[4,240,128]{2,1,0:T(8,128)S(1)}, s16[736,128]{1,0:T(8,128)(2,1)S(1)}, s16[736,128]{1,0:T(8,128)(2,1)S(1...) custom-call(f32[4,240,128]{2,1,0:T(8,128)} %c_hbm.1, f32[4,240,128]{2,1,0:T(8,128)} %d_hbm.1, s32[4,240,128]{2,1,0:T(8,128)} %l_hbm.3), custom_call_target="tpu_custom_call" | custom-call | tf_op jit(solution)/shard_map/pallas_call | solution.py:73
  2.3 3.1 %collective-permute-start = (s16[736,128]{1,0:T(8,128)(2,1)S(1)}, s16[736,128]{1,0:T(8,128)(2,1)S(1)}, u32[]{:S(2)}, u32[]{:S(2)}) collective-permute-start(s16[736,128]{1,0:T(8,128)(2,1)S(1)} %get-tuple-element.35), channel_id=1, source_target_pairs={{0,4},{4,8},{8,12},{12,0},{1,5},{5,9},{9,13},{13,1},{2,6},{6,10},{... | collective-permute-start | bytes 565256 | tf_op jit(solution)/shard_map/ppermute | solution.py:504
  5.3 2.1 %collective-permute-start.1 = (s16[736,128]{1,0:T(8,128)(2,1)S(1)}, s16[736,128]{1,0:T(8,128)(2,1)S(1)}, u32[]{:S(2)}, u32[]{:S(2)}) collective-permute-start(s16[736,128]{1,0:T(8,128)(2,1)S(1)} %get-tuple-element.36), channel_id=1, source_target_pairs={{0,12},{4,0},{8,4},{12,8},{1,13},{5,1},{9,5},{13,9},{2,14},{6,2},{... | collective-permute-start | bytes 565256 | tf_op jit(solution)/shard_map/ppermute | solution.py:504
  7.4 0.9 %collective-permute-start.2 = (f32[8,128]{1,0:T(8,128)S(1)}, f32[8,128]{1,0:T(8,128)S(1)}, u32[]{:S(2)}, u32[]{:S(2)}) collective-permute-start(f32[8,128]{1,0:T(8,128)S(1)} %get-tuple-element.37.refs_4_), channel_id=1, source_target_pairs={{0,8},{4,12},{8,0},{12,4},{1,9},{5,13},{9,1},{13,5},{2,10},{6,14},... | collective-permute-start | bytes 12296 | tf_op jit(solution)/shard_map/ppermute | solution.py:522
  9.0 0.8 %copy.18 = bf16[27,1,16]{2,0,1:T(8,128)(2,1)S(1)} copy(bf16[27,1,16]{0,2,1:T(8,128)(2,1)} %param.16) | data formatting | bytes 1728 | tf_op args[7]
  9.8 0.1 copy.19
  10.0 0.8 %copy.16 = bf16[27,4,16]{2,1,0:T(4,128)(2,1)S(1)} copy(bf16[27,4,16]{0,1,2:T(4,128)(2,1)} %bitcast.27) | data formatting | bytes 6912 | tf_op jit(solution)/shard_map/transpose | solution.py:645
  10.8 1.0 %copy.17 = bf16[27,16,16]{2,1,0:T(8,128)(2,1)S(1)} copy(bf16[27,16,16]{0,1,2:T(8,128)(2,1)} %bitcast.25) | data formatting | bytes 27648 | tf_op jit(solution)/shard_map/transpose | solution.py:646
  11.8 4.4 %collective-permute-done.2.refs_5_ = f32[8,128]{1,0:T(8,128)S(1)} collective-permute-done((f32[8,128]{1,0:T(8,128)S(1)}, f32[8,128]{1,0:T(8,128)S(1)}, u32[]{:S(2)}, u32[]{:S(2)}) %collective-permute-start.2) | collective-permute-done | bytes 4128 | tf_op jit(solution)/shard_map/ppermute | solution.py:522
  16.3 0.0 collective-permute-done.refs_2_.lo_ref
  16.3 0.0 collective-permute-done.1.refs_3_.hi_ref
  16.3 1.6 %collective-permute-start.3 = (f32[2,24,128]{2,1,0:T(8,128)S(1)}, f32[2,24,128]{2,1,0:T(8,128)S(1)}, u32[]{:S(2)}, u32[]{:S(2)}) collective-permute-start(f32[2,24,128]{2,1,0:T(8,128)S(1)} %shard_map.121.refs_5_.yp_ref), channel_id=1, source_target_pairs={{0,2},{2,0},{1,3},{3,1},{4,6},{6,4},{5,7},{7,5},{8,10},{10,8},{9,1... | collective-permute-start | bytes 73736 | tf_op jit(solution)/shard_map/ppermute | solution.py:486
  17.9 2.3 %collective-permute-done.3.refs_4_.yr_ref = f32[2,24,128]{2,1,0:T(8,128)S(1)} collective-permute-done((f32[2,24,128]{2,1,0:T(8,128)S(1)}, f32[2,24,128]{2,1,0:T(8,128)S(1)}, u32[]{:S(2)}, u32[]{:S(2)}) %collective-permute-start.3) | collective-permute-done | bytes 24608 | tf_op jit(solution)/shard_map/ppermute | solution.py:486
  20.2 0.3 shard_map.122
  20.6 0.1 collective-permute-start.4
  20.6 1.5 %collective-permute-done.4.zr_ref = f32[2,272,128]{2,1,0:T(8,128)S(1)} collective-permute-done((f32[2,272,128]{2,1,0:T(8,128)S(1)}, f32[2,272,128]{2,1,0:T(8,128)S(1)}, u32[]{:S(2)}, u32[]{:S(2)}) %collective-permute-start.4) | collective-permute-done | bytes 278560 | tf_op jit(solution)/shard_map/ppermute | solution.py:492
  22.2 2.2 %shard_map.123 = (f32[4,240,128]{2,1,0:T(8,128)S(1)}, f32[6,272,128]{2,1,0:T(8,128)S(1)}, f32[240,128]{1,0:T(8,128)S(1)}, s16[496,128]{1,0:T(8,128)(2,1)S(1)}, s...) custom-call(f32[4,240,128]{2,1,0:T(8,128)S(1)} %get-tuple-element.33.refs_0_.f_ref, ...), custom_call_target="tpu_custom_call" | custom-call | tf_op jit(solution)/shard_map/pallas_call | solution.py:73
  24.4 0.6 %collective-permute-start.5 = (s16[496,128]{1,0:T(8,128)(2,1)S(1)}, s16[496,128]{1,0:T(8,128)(2,1)S(1)}, u32[]{:S(2)}, u32[]{:S(2)}) collective-permute-start(s16[496,128]{1,0:T(8,128)(2,1)S(1)} %get-tuple-element.41), channel_id=1, source_target_pairs={{0,4},{4,8},{8,12},{12,0},{1,5},{5,9},{9,13},{13,1},{2,6},{6,10},{... | collective-permute-start | bytes 380936 | tf_op jit(solution)/shard_map/ppermute | solution.py:504
  25.1 3.2 %collective-permute-start.6 = (s16[496,128]{1,0:T(8,128)(2,1)S(1)}, s16[496,128]{1,0:T(8,128)(2,1)S(1)}, u32[]{:S(2)}, u32[]{:S(2)}) collective-permute-start(s16[496,128]{1,0:T(8,128)(2,1)S(1)} %get-tuple-element.42), channel_id=1, source_target_pairs={{0,12},{4,0},{8,4},{12,8},{1,13},{5,1},{9,5},{13,9},{2,14},{6,2},{... | collective-permute-start | bytes 380936 | tf_op jit(solution)/shard_map/ppermute | solution.py:504
  28.3 4.9 %collective-permute-done.7.refs_4_ = f32[8,128]{1,0:T(8,128)S(1)} collective-permute-done((f32[8,128]{1,0:T(8,128)S(1)}, f32[8,128]{1,0:T(8,128)S(1)}, u32[]{:S(2)}, u32[]{:S(2)}) %collective-permute-start.7) | collective-permute-done | bytes 4128 | tf_op jit(solution)/shard_map/ppermute | solution.py:522
  33.2 0.0 collective-permute-done.5.refs_1_.lo_ref
  33.2 0.0 collective-permute-done.6.refs_2_.hi_ref
  33.2 1.6 %collective-permute-start.8 = (f32[2,24,128]{2,1,0:T(8,128)S(1)}, f32[2,24,128]{2,1,0:T(8,128)S(1)}, u32[]{:S(2)}, u32[]{:S(2)}) collective-permute-start(f32[2,24,128]{2,1,0:T(8,128)S(1)} %shard_map.124.refs_4_.yp_ref), channel_id=1, source_target_pairs={{0,2},{2,0},{1,3},{3,1},{4,6},{6,4},{5,7},{7,5},{8,10},{10,8},{9,1... | collective-permute-start | bytes 73736 | tf_op jit(solution)/shard_map/ppermute | solution.py:486
  34.7 2.3 %collective-permute-done.8.refs_3_.yr_ref = f32[2,24,128]{2,1,0:T(8,128)S(1)} collective-permute-done((f32[2,24,128]{2,1,0:T(8,128)S(1)}, f32[2,24,128]{2,1,0:T(8,128)S(1)}, u32[]{:S(2)}, u32[]{:S(2)}) %collective-permute-start.8) | collective-permute-done | bytes 24608 | tf_op jit(solution)/shard_map/ppermute | solution.py:486
  37.1 0.2 shard_map.125
  37.3 0.1 collective-permute-start.9
  37.4 1.5 %collective-permute-done.9.zr_ref = f32[2,272,128]{2,1,0:T(8,128)S(1)} collective-permute-done((f32[2,272,128]{2,1,0:T(8,128)S(1)}, f32[2,272,128]{2,1,0:T(8,128)S(1)}, u32[]{:S(2)}, u32[]{:S(2)}) %collective-permute-start.9) | collective-permute-done | bytes 278560 | tf_op jit(solution)/shard_map/ppermute | solution.py:492
  38.9 0.6 shard_map.127
  39.5 1.5 %collective-permute-start.10 = (bf16[2,16,128]{2,1,0:T(8,128)(2,1)S(1)}, bf16[2,16,128]{2,1,0:T(8,128)(2,1)S(1)}, u32[]{:S(2)}, u32[]{:S(2)}) collective-permute-start(bf16[2,16,128]{2,1,0:T(8,128)(2,1)S(1)} %shard_map.127), channel_id=1, source_target_pairs={{0,2},{2,0},{1,3},{3,1},{4,6},{6,4},{5,7},{7,5},{8,10},{10,8},{9,1... | collective-permute-start | bytes 24584 | tf_op jit(solution)/shard_map/ppermute | solution.py:486
  41.0 0.1 pad_add_fusion
  41.0 3.0 %shard_map.126 = (f32[4,240,128]{2,1,0:T(8,128)S(1)}, f32[4,240,128]{2,1,0:T(8,128)S(1)}, f32[4,240,128]{2,1,0:T(8,128)S(1)}, bf16[60,128]{1,0:T(8,128)(2,1)S(1)}) custom-call(f32[4,240,128]{2,1,0:T(8,128)S(1)} %get-tuple-element.38.refs_0_.f_ref, f32[6,272,128]{2,1,0:T(8,128)S(1)} %get-tuple-element.39.a2_ref, f32[240,128]{1,0:T(8,128)S(1)} %get-tuple-element.40.ae2_ref, ...), custom_call_target="tpu_custom_call" | custom-call | tf_op jit(solution)/shard_map/pallas_call | solution.py:562
  44.1 0.0 collective-permute-done.10.yr_ref
  44.1 0.1 broadcast_in_dim.15.ids_ref.refs_0_
  44.2 2.0 %collective-permute-start.13 = (bf16[80,128]{1,0:T(8,128)(2,1)S(1)}, bf16[80,128]{1,0:T(8,128)(2,1)S(1)}, u32[]{:S(2)}, u32[]{:S(2)}) collective-permute-start(bf16[80,128]{1,0:T(8,128)(2,1)S(1)} %shard_map.128.plane_ref.refs_1_), channel_id=1, source_target_pairs={{0,8},{4,12},{8,0},{12,4},{1,9},{5,13},{9,1},{13,5},{2,10},{6,14},... | collective-permute-start | bytes 61448 | tf_op jit(solution)/shard_map/ppermute | solution.py:779
  46.2 0.8 %collective-permute-start.12 = (bf16[80,128]{1,0:T(8,128)(2,1)S(1)}, bf16[80,128]{1,0:T(8,128)(2,1)S(1)}, u32[]{:S(2)}, u32[]{:S(2)}) collective-permute-start(bf16[80,128]{1,0:T(8,128)(2,1)S(1)} %shard_map.128.plane_ref.refs_1_), channel_id=1, source_target_pairs={{0,4},{4,8},{8,12},{12,0},{1,5},{5,9},{9,13},{13,1},{2,6},{6,10},{... | collective-permute-start | bytes 61448 | tf_op jit(solution)/shard_map/ppermute | solution.py:779
  47.0 3.0 %collective-permute-start.11 = (bf16[80,128]{1,0:T(8,128)(2,1)S(1)}, bf16[80,128]{1,0:T(8,128)(2,1)S(1)}, u32[]{:S(2)}, u32[]{:S(2)}) collective-permute-start(bf16[80,128]{1,0:T(8,128)(2,1)S(1)} %shard_map.128.plane_ref.refs_1_), channel_id=1, source_target_pairs={{0,12},{4,0},{8,4},{12,8},{1,13},{5,1},{9,5},{13,9},{2,14},{6,2},{... | collective-permute-start | bytes 61448 | tf_op jit(solution)/shard_map/ppermute | solution.py:779
  50.0 0.0 collective-permute-start.14
  50.0 0.7 %shard_map.129 = (bf16[3,512,640]{2,1,0:T(8,128)(2,1)S(1)}, bf16[3,512,128]{2,1,0:T(8,128)(2,1)S(1)}, bf16[3,640,128]{2,1,0:T(8,128)(2,1)S(1)}, f32[8,640]{1,0:T(8,128)S(1)}) custom-call(bf16[432,16]{1,0:T(8,128)(2,1)S(1)} %bitcast.20, bf16[432,16]{1,0:T(8,128)(2,1)S(1)} %bitcast.18, bf16[144,3]{1,0:T(8,128)(2,1)S(1)} %bitcast.22, f32[1,1]{1,0:T(1,128)} %bitcast.16.b3_ref, ...), custom_call_target="tpu_custom_call" | custom-call | tf_op jit(solution)/shard_map/pallas_call | solution.py:73
  50.8 0.0 collective-permute-done.13.refs_4_
  50.8 1.0 %collective-permute-done.12.refs_3_ = bf16[80,128]{1,0:T(8,128)(2,1)S(1)} collective-permute-done((bf16[80,128]{1,0:T(8,128)(2,1)S(1)}, bf16[80,128]{1,0:T(8,128)(2,1)S(1)}, u32[]{:S(2)}, u32[]{:S(2)}) %collective-permute-start.12) | collective-permute-done | bytes 20512 | tf_op jit(solution)/shard_map/ppermute | solution.py:779
  51.8 0.0 collective-permute-start.16
  51.8 0.0 collective-permute-done.11.refs_2_
  51.8 0.5 collective-permute-start.15
  52.3 0.0 collective-permute-start.17
  52.3 0.7 %collective-permute-done.16.refs_7_ = bf16[80,128]{1,0:T(8,128)(2,1)S(1)} collective-permute-done((bf16[80,128]{1,0:T(8,128)(2,1)S(1)}, bf16[80,128]{1,0:T(8,128)(2,1)S(1)}, u32[]{:S(2)}, u32[]{:S(2)}) %collective-permute-start.16) | collective-permute-done | bytes 20512 | tf_op jit(solution)/shard_map/ppermute | solution.py:492
  52.9 0.2 collective-permute-done.15.refs_6_
  53.1 0.3 collective-permute-done.17.refs_8_
  53.5 3.6 %shard_map.130 = (f32[1,32,60]{2,1,0:T(8,128)}, f32[4,240,128]{2,1,0:T(8,128)}, f32[4,240,128]{2,1,0:T(8,128)}, f32[4,240,128]{2,1,0:T(8,128)}) custom-call(s32[3,128]{1,0:T(4,128)S(1)} %broadcast_in_dim.15.ids_ref.refs_0_, bf16[80,128]{1,0:T(8,128)(2,1)S(1)} %shard_map.128.plane_ref.refs_1_, bf16[80,128]{1,0:T(8,128)(2,1)S(1)} %collective-permute-done.11.refs_2_, ...), custom_call_target="tpu_custom_call" | custom-call | tf_op jit(solution)/shard_map/pallas_call | solution.py:73
  (11 shorter events, 0.1 us)
Async XLA Ops:
  2.3 14.0 %collective-permute-start = (s16[736,128]{1,0:T(8,128)(2,1)S(1)}, s16[736,128]{1,0:T(8,128)(2,1)S(1)}, u32[]{:S(2)}, u32[]{:S(2)}) collective-permute-start(s16[736,128]{1,0:T(8,128)(2,1)S(1)} %get-tuple-element.35), channel_id=1, source_target_pairs={{0,4},{4,8},{8,12},{12,0},{1,5},{5,9},{9,13},{13,1},{2,6},{6,10},{... | collective-permute-start | bytes 565256 | tf_op jit(solution)/shard_map/ppermute | solution.py:504
  5.3 10.9 %collective-permute-start.1 = (s16[736,128]{1,0:T(8,128)(2,1)S(1)}, s16[736,128]{1,0:T(8,128)(2,1)S(1)}, u32[]{:S(2)}, u32[]{:S(2)}) collective-permute-start(s16[736,128]{1,0:T(8,128)(2,1)S(1)} %get-tuple-element.36), channel_id=1, source_target_pairs={{0,12},{4,0},{8,4},{12,8},{1,13},{5,1},{9,5},{13,9},{2,14},{6,2},{... | collective-permute-start | bytes 565256 | tf_op jit(solution)/shard_map/ppermute | solution.py:504
  7.4 8.8 %collective-permute-start.2 = (f32[8,128]{1,0:T(8,128)S(1)}, f32[8,128]{1,0:T(8,128)S(1)}, u32[]{:S(2)}, u32[]{:S(2)}) collective-permute-start(f32[8,128]{1,0:T(8,128)S(1)} %get-tuple-element.37.refs_4_), channel_id=1, source_target_pairs={{0,8},{4,12},{8,0},{12,4},{1,9},{5,13},{9,1},{13,5},{2,10},{6,14},... | collective-permute-start | bytes 12296 | tf_op jit(solution)/shard_map/ppermute | solution.py:522
  16.3 3.9 %collective-permute-start.3 = (f32[2,24,128]{2,1,0:T(8,128)S(1)}, f32[2,24,128]{2,1,0:T(8,128)S(1)}, u32[]{:S(2)}, u32[]{:S(2)}) collective-permute-start(f32[2,24,128]{2,1,0:T(8,128)S(1)} %shard_map.121.refs_5_.yp_ref), channel_id=1, source_target_pairs={{0,2},{2,0},{1,3},{3,1},{4,6},{6,4},{5,7},{7,5},{8,10},{10,8},{9,1... | collective-permute-start | bytes 73736 | tf_op jit(solution)/shard_map/ppermute | solution.py:486
  20.6 1.6 %collective-permute-start.4 = (f32[2,272,128]{2,1,0:T(8,128)S(1)}, f32[2,272,128]{2,1,0:T(8,128)S(1)}, u32[]{:S(2)}, u32[]{:S(2)}) collective-permute-start(f32[2,272,128]{2,1,0:T(8,128)S(1)} %shard_map.122), channel_id=1, source_target_pairs={{0,1},{1,0},{2,3},{3,2},{4,5},{5,4},{6,7},{7,6},{8,9},{9,8},{10,11... | collective-permute-start | bytes 835592 | tf_op jit(solution)/shard_map/ppermute | solution.py:492
  24.4 8.7 %collective-permute-start.5 = (s16[496,128]{1,0:T(8,128)(2,1)S(1)}, s16[496,128]{1,0:T(8,128)(2,1)S(1)}, u32[]{:S(2)}, u32[]{:S(2)}) collective-permute-start(s16[496,128]{1,0:T(8,128)(2,1)S(1)} %get-tuple-element.41), channel_id=1, source_target_pairs={{0,4},{4,8},{8,12},{12,0},{1,5},{5,9},{9,13},{13,1},{2,6},{6,10},{... | collective-permute-start | bytes 380936 | tf_op jit(solution)/shard_map/ppermute | solution.py:504
  25.1 8.1 %collective-permute-start.6 = (s16[496,128]{1,0:T(8,128)(2,1)S(1)}, s16[496,128]{1,0:T(8,128)(2,1)S(1)}, u32[]{:S(2)}, u32[]{:S(2)}) collective-permute-start(s16[496,128]{1,0:T(8,128)(2,1)S(1)} %get-tuple-element.42), channel_id=1, source_target_pairs={{0,12},{4,0},{8,4},{12,8},{1,13},{5,1},{9,5},{13,9},{2,14},{6,2},{... | collective-permute-start | bytes 380936 | tf_op jit(solution)/shard_map/ppermute | solution.py:504
  28.3 4.9 %collective-permute-start.7 = (f32[8,128]{1,0:T(8,128)S(1)}, f32[8,128]{1,0:T(8,128)S(1)}, u32[]{:S(2)}, u32[]{:S(2)}) collective-permute-start(f32[8,128]{1,0:T(8,128)S(1)} %get-tuple-element.43.refs_3_), channel_id=1, source_target_pairs={{0,8},{4,12},{8,0},{12,4},{1,9},{5,13},{9,1},{13,5},{2,10},{6,14},... | collective-permute-start | bytes 12296 | tf_op jit(solution)/shard_map/ppermute | solution.py:522
  33.2 3.9 %collective-permute-start.8 = (f32[2,24,128]{2,1,0:T(8,128)S(1)}, f32[2,24,128]{2,1,0:T(8,128)S(1)}, u32[]{:S(2)}, u32[]{:S(2)}) collective-permute-start(f32[2,24,128]{2,1,0:T(8,128)S(1)} %shard_map.124.refs_4_.yp_ref), channel_id=1, source_target_pairs={{0,2},{2,0},{1,3},{3,1},{4,6},{6,4},{5,7},{7,5},{8,10},{10,8},{9,1... | collective-permute-start | bytes 73736 | tf_op jit(solution)/shard_map/ppermute | solution.py:486
  37.3 1.6 %collective-permute-start.9 = (f32[2,272,128]{2,1,0:T(8,128)S(1)}, f32[2,272,128]{2,1,0:T(8,128)S(1)}, u32[]{:S(2)}, u32[]{:S(2)}) collective-permute-start(f32[2,272,128]{2,1,0:T(8,128)S(1)} %shard_map.125), channel_id=1, source_target_pairs={{0,1},{1,0},{2,3},{3,2},{4,5},{5,4},{6,7},{7,6},{8,9},{9,8},{10,11... | collective-permute-start | bytes 835592 | tf_op jit(solution)/shard_map/ppermute | solution.py:492
  38.9 11.1 %copy-start = (f32[16]{0:T(128)S(1)}, f32[16]{0:T(128)}, u32[]{:S(2)}) copy-start(f32[16]{0:T(128)} %param.13) | copy-start | bytes 196
  38.9 11.1 %copy-start.1 = (f32[16]{0:T(128)S(1)}, f32[16]{0:T(128)}, u32[]{:S(2)}) copy-start(f32[16]{0:T(128)} %param.15) | copy-start | bytes 196
  39.5 4.6 %collective-permute-start.10 = (bf16[2,16,128]{2,1,0:T(8,128)(2,1)S(1)}, bf16[2,16,128]{2,1,0:T(8,128)(2,1)S(1)}, u32[]{:S(2)}, u32[]{:S(2)}) collective-permute-start(bf16[2,16,128]{2,1,0:T(8,128)(2,1)S(1)} %shard_map.127), channel_id=1, source_target_pairs={{0,2},{2,0},{1,3},{3,1},{4,6},{6,4},{5,7},{7,5},{8,10},{10,8},{9,1... | collective-permute-start | bytes 24584 | tf_op jit(solution)/shard_map/ppermute | solution.py:486
  44.2 6.6 %collective-permute-start.13 = (bf16[80,128]{1,0:T(8,128)(2,1)S(1)}, bf16[80,128]{1,0:T(8,128)(2,1)S(1)}, u32[]{:S(2)}, u32[]{:S(2)}) collective-permute-start(bf16[80,128]{1,0:T(8,128)(2,1)S(1)} %shard_map.128.plane_ref.refs_1_), channel_id=1, source_target_pairs={{0,8},{4,12},{8,0},{12,4},{1,9},{5,13},{9,1},{13,5},{2,10},{6,14},... | collective-permute-start | bytes 61448 | tf_op jit(solution)/shard_map/ppermute | solution.py:779
  46.2 5.6 %collective-permute-start.12 = (bf16[80,128]{1,0:T(8,128)(2,1)S(1)}, bf16[80,128]{1,0:T(8,128)(2,1)S(1)}, u32[]{:S(2)}, u32[]{:S(2)}) collective-permute-start(bf16[80,128]{1,0:T(8,128)(2,1)S(1)} %shard_map.128.plane_ref.refs_1_), channel_id=1, source_target_pairs={{0,4},{4,8},{8,12},{12,0},{1,5},{5,9},{9,13},{13,1},{2,6},{6,10},{... | collective-permute-start | bytes 61448 | tf_op jit(solution)/shard_map/ppermute | solution.py:779
  47.0 4.8 %collective-permute-start.11 = (bf16[80,128]{1,0:T(8,128)(2,1)S(1)}, bf16[80,128]{1,0:T(8,128)(2,1)S(1)}, u32[]{:S(2)}, u32[]{:S(2)}) collective-permute-start(bf16[80,128]{1,0:T(8,128)(2,1)S(1)} %shard_map.128.plane_ref.refs_1_), channel_id=1, source_target_pairs={{0,12},{4,0},{8,4},{12,8},{1,13},{5,1},{9,5},{13,9},{2,14},{6,2},{... | collective-permute-start | bytes 61448 | tf_op jit(solution)/shard_map/ppermute | solution.py:779
  50.0 2.3 %collective-permute-start.14 = (bf16[80,128]{1,0:T(8,128)(2,1)S(1)}, bf16[80,128]{1,0:T(8,128)(2,1)S(1)}, u32[]{:S(2)}, u32[]{:S(2)}) collective-permute-start(bf16[80,128]{1,0:T(8,128)(2,1)S(1)} %shard_map.128.plane_ref.refs_1_), channel_id=1, source_target_pairs={{0,1},{1,0},{2,3},{3,2},{4,5},{5,4},{6,7},{7,6},{8,9},{9,8},{10,11... | collective-permute-start | bytes 61448 | tf_op jit(solution)/shard_map/ppermute | solution.py:492
  51.8 1.2 %collective-permute-start.16 = (bf16[80,128]{1,0:T(8,128)(2,1)S(1)}, bf16[80,128]{1,0:T(8,128)(2,1)S(1)}, u32[]{:S(2)}, u32[]{:S(2)}) collective-permute-start(bf16[80,128]{1,0:T(8,128)(2,1)S(1)} %collective-permute-done.12.refs_3_), channel_id=1, source_target_pairs={{0,1},{1,0},{2,3},{3,2},{4,5},{5,4},{6,7},{7,6},{8,9},{9,8},{10,11... | collective-permute-start | bytes 61448 | tf_op jit(solution)/shard_map/ppermute | solution.py:492
  51.8 1.4 %collective-permute-start.15 = (bf16[80,128]{1,0:T(8,128)(2,1)S(1)}, bf16[80,128]{1,0:T(8,128)(2,1)S(1)}, u32[]{:S(2)}, u32[]{:S(2)}) collective-permute-start(bf16[80,128]{1,0:T(8,128)(2,1)S(1)} %collective-permute-done.11.refs_2_), channel_id=1, source_target_pairs={{0,1},{1,0},{2,3},{3,2},{4,5},{5,4},{6,7},{7,6},{8,9},{9,8},{10,11... | collective-permute-start | bytes 61448 | tf_op jit(solution)/shard_map/ppermute | solution.py:492
  52.3 1.2 %collective-permute-start.17 = (bf16[80,128]{1,0:T(8,128)(2,1)S(1)}, bf16[80,128]{1,0:T(8,128)(2,1)S(1)}, u32[]{:S(2)}, u32[]{:S(2)}) collective-permute-start(bf16[80,128]{1,0:T(8,128)(2,1)S(1)} %collective-permute-done.13.refs_4_), channel_id=1, source_target_pairs={{0,1},{1,0},{2,3},{3,2},{4,5},{5,4},{6,7},{7,6},{8,9},{9,8},{10,11... | collective-permute-start | bytes 61448 | tf_op jit(solution)/shard_map/ppermute | solution.py:492

commit v19 on v18

--- a/solution.py
+++ b/solution.py
@@ -448,7 +448,7 @@
         labels_in.start()
         g = Geometry(nx, ny, nz)
         mean = weighted_mean(yp_ref, yr_ref, zr_ref, ride_y, ride_z)
-        potentials_b(g, mean, a2_ref, ae2_ref, (f_ref, lo_ref, hi_ref, yr_ref, zr_ref), scratch, [(0, ny)], True)
+        potentials_b(g, mean, a2_ref, ae2_ref, (f_ref, lo_ref, hi_ref, yr_ref, zr_ref), scratch, [(0, ny)], False)
         labels_in.wait()
         for r, n in chunks(OFF, OFF + ny, 48):
             s = slice(r - OFF, r - OFF + n)

time: 57.4 us -> 57.3 us (level)
  transfers between devices with their start and end apart: 18 -> 18, of which waited for: 10 -> 10; matrix products, arithmetic and copies ran while one was open for 5% -> 5% of each run, Pallas kernels for 7% -> 6%
where the time goes in v19:
time: 57.3 us; the launch traced here: 57 us
  starting transfers between devices  21.1 us (37%)
  waiting for transfers between devices  19.2 us (34%)
  Pallas kernels  12.3 us (21%)
  local copies, waits for them, and re-layouts  2.93 us (5%)
  between operations  1.4 us (2%)
    pallas_call x10, Pallas kernels, call(): pl.pallas_call(kernel, in_specs=in_specs or [VMEM] * len(args), out_specs...  9.4 us
    ppermute x2, waiting for transfers between devices, start(): return (sums, lax.ppermute(sums, 'gx', ring('gx', 2)))  9.28 us
    ppermute x3, starting transfers between devices, detector(): own = [plane] + [lax.ppermute(plane, 'gx', ring('gx', s)) for s in shifts]  5.81 us
    ppermute x2, starting transfers between devices, x_sides(): lax.ppermute(lo, 'gx', ring('gx', -1))  5.32 us
    ppermute x3, waiting for transfers between devices, both_sides(): return lax.ppermute(pay, axis, ring(axis, 1))  4.67 us
    ppermute x3, starting transfers between devices, both_sides(): return lax.ppermute(pay, axis, ring(axis, 1))  4.61 us
    ppermute x6, waiting for transfers between devices, z_neighbour(): return lax.ppermute(pay, axis, ring(axis, 1))  4.27 us
    ppermute x2, starting transfers between devices, x_sides(): lax.ppermute(hi, 'gx', ring('gx', 1))  3.72 us
  transfers between devices with their start and end apart: 18, of which 10 were waited for; matrix products, arithmetic and copies ran while one was open for 5% of the time, Pallas kernels for 6%

profile of v19, /device:TPU:0, one launch (start us, length us, event | category | flops | bytes accessed | tf_op | source)
XLA Modules:
  0.0 57.0 jit_solution(12738447347862117532)
XLA Ops:
  0.6 1.6 %shard_map.120 = (f32[4,240,128]{2,1,0:T(8,128)S(1)}, f32[4,240,128]{2,1,0:T(8,128)S(1)}, s16[736,128]{1,0:T(8,128)(2,1)S(1)}, s16[736,128]{1,0:T(8,128)(2,1)S(1...) custom-call(f32[4,240,128]{2,1,0:T(8,128)} %c_hbm.1, f32[4,240,128]{2,1,0:T(8,128)} %d_hbm.1, s32[4,240,128]{2,1,0:T(8,128)} %l_hbm.3), custom_call_target="tpu_custom_call" | custom-call | tf_op jit(solution)/shard_map/pallas_call | solution.py:73
  2.3 3.1 %collective-permute-start = (s16[736,128]{1,0:T(8,128)(2,1)S(1)}, s16[736,128]{1,0:T(8,128)(2,1)S(1)}, u32[]{:S(2)}, u32[]{:S(2)}) collective-permute-start(s16[736,128]{1,0:T(8,128)(2,1)S(1)} %get-tuple-element.35), channel_id=1, source_target_pairs={{0,4},{4,8},{8,12},{12,0},{1,5},{5,9},{9,13},{13,1},{2,6},{6,10},{... | collective-permute-start | bytes 565256 | tf_op jit(solution)/shard_map/ppermute | solution.py:504
  5.3 2.1 %collective-permute-start.1 = (s16[736,128]{1,0:T(8,128)(2,1)S(1)}, s16[736,128]{1,0:T(8,128)(2,1)S(1)}, u32[]{:S(2)}, u32[]{:S(2)}) collective-permute-start(s16[736,128]{1,0:T(8,128)(2,1)S(1)} %get-tuple-element.36), channel_id=1, source_target_pairs={{0,12},{4,0},{8,4},{12,8},{1,13},{5,1},{9,5},{13,9},{2,14},{6,2},{... | collective-permute-start | bytes 565256 | tf_op jit(solution)/shard_map/ppermute | solution.py:504
  7.4 0.9 %collective-permute-start.2 = (f32[8,128]{1,0:T(8,128)S(1)}, f32[8,128]{1,0:T(8,128)S(1)}, u32[]{:S(2)}, u32[]{:S(2)}) collective-permute-start(f32[8,128]{1,0:T(8,128)S(1)} %get-tuple-element.37.refs_4_), channel_id=1, source_target_pairs={{0,8},{4,12},{8,0},{12,4},{1,9},{5,13},{9,1},{13,5},{2,10},{6,14},... | collective-permute-start | bytes 12296 | tf_op jit(solution)/shard_map/ppermute | solution.py:522
  9.0 0.8 %copy.18 = bf16[27,1,16]{2,0,1:T(8,128)(2,1)S(1)} copy(bf16[27,1,16]{0,2,1:T(8,128)(2,1)} %param.16) | data formatting | bytes 1728 | tf_op args[7]
  9.8 0.1 copy.19
  10.0 0.8 %copy.16 = bf16[27,4,16]{2,1,0:T(4,128)(2,1)S(1)} copy(bf16[27,4,16]{0,1,2:T(4,128)(2,1)} %bitcast.27) | data formatting | bytes 6912 | tf_op jit(solution)/shard_map/transpose | solution.py:645
  10.8 1.0 %copy.17 = bf16[27,16,16]{2,1,0:T(8,128)(2,1)S(1)} copy(bf16[27,16,16]{0,1,2:T(8,128)(2,1)} %bitcast.25) | data formatting | bytes 27648 | tf_op jit(solution)/shard_map/transpose | solution.py:646
  11.8 4.4 %collective-permute-done.2.refs_5_ = f32[8,128]{1,0:T(8,128)S(1)} collective-permute-done((f32[8,128]{1,0:T(8,128)S(1)}, f32[8,128]{1,0:T(8,128)S(1)}, u32[]{:S(2)}, u32[]{:S(2)}) %collective-permute-start.2) | collective-permute-done | bytes 4128 | tf_op jit(solution)/shard_map/ppermute | solution.py:522
  16.3 0.0 collective-permute-done.refs_2_.lo_ref
  16.3 0.0 collective-permute-done.1.refs_3_.hi_ref
  16.3 1.6 %collective-permute-start.3 = (f32[2,24,128]{2,1,0:T(8,128)S(1)}, f32[2,24,128]{2,1,0:T(8,128)S(1)}, u32[]{:S(2)}, u32[]{:S(2)}) collective-permute-start(f32[2,24,128]{2,1,0:T(8,128)S(1)} %shard_map.121.refs_5_.yp_ref), channel_id=1, source_target_pairs={{0,2},{2,0},{1,3},{3,1},{4,6},{6,4},{5,7},{7,5},{8,10},{10,8},{9,1... | collective-permute-start | bytes 73736 | tf_op jit(solution)/shard_map/ppermute | solution.py:486
  17.9 2.3 %collective-permute-done.3.refs_4_.yr_ref = f32[2,24,128]{2,1,0:T(8,128)S(1)} collective-permute-done((f32[2,24,128]{2,1,0:T(8,128)S(1)}, f32[2,24,128]{2,1,0:T(8,128)S(1)}, u32[]{:S(2)}, u32[]{:S(2)}) %collective-permute-start.3) | collective-permute-done | bytes 24608 | tf_op jit(solution)/shard_map/ppermute | solution.py:486
  20.2 0.3 shard_map.122
  20.6 0.1 collective-permute-start.4
  20.6 1.5 %collective-permute-done.4.zr_ref = f32[2,272,128]{2,1,0:T(8,128)S(1)} collective-permute-done((f32[2,272,128]{2,1,0:T(8,128)S(1)}, f32[2,272,128]{2,1,0:T(8,128)S(1)}, u32[]{:S(2)}, u32[]{:S(2)}) %collective-permute-start.4) | collective-permute-done | bytes 278560 | tf_op jit(solution)/shard_map/ppermute | solution.py:492
  22.2 2.2 %shard_map.123 = (f32[4,240,128]{2,1,0:T(8,128)S(1)}, f32[6,272,128]{2,1,0:T(8,128)S(1)}, f32[240,128]{1,0:T(8,128)S(1)}, s16[496,128]{1,0:T(8,128)(2,1)S(1)}, s...) custom-call(f32[4,240,128]{2,1,0:T(8,128)S(1)} %get-tuple-element.33.refs_0_.f_ref, ...), custom_call_target="tpu_custom_call" | custom-call | tf_op jit(solution)/shard_map/pallas_call | solution.py:73
  24.4 0.6 %collective-permute-start.5 = (s16[496,128]{1,0:T(8,128)(2,1)S(1)}, s16[496,128]{1,0:T(8,128)(2,1)S(1)}, u32[]{:S(2)}, u32[]{:S(2)}) collective-permute-start(s16[496,128]{1,0:T(8,128)(2,1)S(1)} %get-tuple-element.41), channel_id=1, source_target_pairs={{0,4},{4,8},{8,12},{12,0},{1,5},{5,9},{9,13},{13,1},{2,6},{6,10},{... | collective-permute-start | bytes 380936 | tf_op jit(solution)/shard_map/ppermute | solution.py:504
  25.1 3.2 %collective-permute-start.6 = (s16[496,128]{1,0:T(8,128)(2,1)S(1)}, s16[496,128]{1,0:T(8,128)(2,1)S(1)}, u32[]{:S(2)}, u32[]{:S(2)}) collective-permute-start(s16[496,128]{1,0:T(8,128)(2,1)S(1)} %get-tuple-element.42), channel_id=1, source_target_pairs={{0,12},{4,0},{8,4},{12,8},{1,13},{5,1},{9,5},{13,9},{2,14},{6,2},{... | collective-permute-start | bytes 380936 | tf_op jit(solution)/shard_map/ppermute | solution.py:504
  28.3 0.0 collective-permute-start.7
  28.3 4.9 %collective-permute-done.7.refs_4_ = f32[8,128]{1,0:T(8,128)S(1)} collective-permute-done((f32[8,128]{1,0:T(8,128)S(1)}, f32[8,128]{1,0:T(8,128)S(1)}, u32[]{:S(2)}, u32[]{:S(2)}) %collective-permute-start.7) | collective-permute-done | bytes 4128 | tf_op jit(solution)/shard_map/ppermute | solution.py:522
  33.2 0.0 collective-permute-done.5.refs_1_.lo_ref
  33.2 0.0 collective-permute-done.6.refs_2_.hi_ref
  33.2 1.6 %collective-permute-start.8 = (f32[2,24,128]{2,1,0:T(8,128)S(1)}, f32[2,24,128]{2,1,0:T(8,128)S(1)}, u32[]{:S(2)}, u32[]{:S(2)}) collective-permute-start(f32[2,24,128]{2,1,0:T(8,128)S(1)} %shard_map.124.refs_4_.yp_ref), channel_id=1, source_target_pairs={{0,2},{2,0},{1,3},{3,1},{4,6},{6,4},{5,7},{7,5},{8,10},{10,8},{9,1... | collective-permute-start | bytes 73736 | tf_op jit(solution)/shard_map/ppermute | solution.py:486
  34.7 2.3 %collective-permute-done.8.refs_3_.yr_ref = f32[2,24,128]{2,1,0:T(8,128)S(1)} collective-permute-done((f32[2,24,128]{2,1,0:T(8,128)S(1)}, f32[2,24,128]{2,1,0:T(8,128)S(1)}, u32[]{:S(2)}, u32[]{:S(2)}) %collective-permute-start.8) | collective-permute-done | bytes 24608 | tf_op jit(solution)/shard_map/ppermute | solution.py:486
  37.1 0.2 shard_map.125
  37.3 0.1 collective-permute-start.9
  37.4 1.5 %collective-permute-done.9.zr_ref = f32[2,272,128]{2,1,0:T(8,128)S(1)} collective-permute-done((f32[2,272,128]{2,1,0:T(8,128)S(1)}, f32[2,272,128]{2,1,0:T(8,128)S(1)}, u32[]{:S(2)}, u32[]{:S(2)}) %collective-permute-start.9) | collective-permute-done | bytes 278560 | tf_op jit(solution)/shard_map/ppermute | solution.py:492
  38.9 0.6 shard_map.127
  39.5 1.5 %collective-permute-start.10 = (bf16[2,16,128]{2,1,0:T(8,128)(2,1)S(1)}, bf16[2,16,128]{2,1,0:T(8,128)(2,1)S(1)}, u32[]{:S(2)}, u32[]{:S(2)}) collective-permute-start(bf16[2,16,128]{2,1,0:T(8,128)(2,1)S(1)} %shard_map.127), channel_id=1, source_target_pairs={{0,2},{2,0},{1,3},{3,1},{4,6},{6,4},{5,7},{7,5},{8,10},{10,8},{9,1... | collective-permute-start | bytes 24584 | tf_op jit(solution)/shard_map/ppermute | solution.py:486
  41.0 0.1 pad_add_fusion
  41.0 2.9 %shard_map.126 = (f32[4,240,128]{2,1,0:T(8,128)S(1)}, f32[4,240,128]{2,1,0:T(8,128)S(1)}, f32[4,240,128]{2,1,0:T(8,128)S(1)}, bf16[60,128]{1,0:T(8,128)(2,1)S(1)}) custom-call(f32[4,240,128]{2,1,0:T(8,128)S(1)} %get-tuple-element.38.refs_0_.f_ref, f32[6,272,128]{2,1,0:T(8,128)S(1)} %get-tuple-element.39.a2_ref, f32[240,128]{1,0:T(8,128)S(1)} %get-tuple-element.40.ae2_ref, ...), custom_call_target="tpu_custom_call" | custom-call | tf_op jit(solution)/shard_map/pallas_call | solution.py:562
  44.0 0.0 collective-permute-done.10.yr_ref
  44.0 0.1 broadcast_in_dim.15.ids_ref.refs_0_
  44.1 2.0 %collective-permute-start.13 = (bf16[80,128]{1,0:T(8,128)(2,1)S(1)}, bf16[80,128]{1,0:T(8,128)(2,1)S(1)}, u32[]{:S(2)}, u32[]{:S(2)}) collective-permute-start(bf16[80,128]{1,0:T(8,128)(2,1)S(1)} %shard_map.128.plane_ref.refs_1_), channel_id=1, source_target_pairs={{0,8},{4,12},{8,0},{12,4},{1,9},{5,13},{9,1},{13,5},{2,10},{6,14},... | collective-permute-start | bytes 61448 | tf_op jit(solution)/shard_map/ppermute | solution.py:779
  46.1 0.8 %collective-permute-start.12 = (bf16[80,128]{1,0:T(8,128)(2,1)S(1)}, bf16[80,128]{1,0:T(8,128)(2,1)S(1)}, u32[]{:S(2)}, u32[]{:S(2)}) collective-permute-start(bf16[80,128]{1,0:T(8,128)(2,1)S(1)} %shard_map.128.plane_ref.refs_1_), channel_id=1, source_target_pairs={{0,4},{4,8},{8,12},{12,0},{1,5},{5,9},{9,13},{13,1},{2,6},{6,10},{... | collective-permute-start | bytes 61448 | tf_op jit(solution)/shard_map/ppermute | solution.py:779
  46.9 3.0 %collective-permute-start.11 = (bf16[80,128]{1,0:T(8,128)(2,1)S(1)}, bf16[80,128]{1,0:T(8,128)(2,1)S(1)}, u32[]{:S(2)}, u32[]{:S(2)}) collective-permute-start(bf16[80,128]{1,0:T(8,128)(2,1)S(1)} %shard_map.128.plane_ref.refs_1_), channel_id=1, source_target_pairs={{0,12},{4,0},{8,4},{12,8},{1,13},{5,1},{9,5},{13,9},{2,14},{6,2},{... | collective-permute-start | bytes 61448 | tf_op jit(solution)/shard_map/ppermute | solution.py:779
  49.9 0.0 collective-permute-start.14
  49.9 0.8 %shard_map.129 = (bf16[3,512,640]{2,1,0:T(8,128)(2,1)S(1)}, bf16[3,512,128]{2,1,0:T(8,128)(2,1)S(1)}, bf16[3,640,128]{2,1,0:T(8,128)(2,1)S(1)}, f32[8,640]{1,0:T(8,128)S(1)}) custom-call(bf16[432,16]{1,0:T(8,128)(2,1)S(1)} %bitcast.20, bf16[432,16]{1,0:T(8,128)(2,1)S(1)} %bitcast.18, bf16[144,3]{1,0:T(8,128)(2,1)S(1)} %bitcast.22, f32[1,1]{1,0:T(1,128)} %bitcast.16.b3_ref, ...), custom_call_target="tpu_custom_call" | custom-call | tf_op jit(solution)/shard_map/pallas_call | solution.py:73
  50.7 0.0 collective-permute-done.13.refs_4_
  50.7 1.0 %collective-permute-done.12.refs_3_ = bf16[80,128]{1,0:T(8,128)(2,1)S(1)} collective-permute-done((bf16[80,128]{1,0:T(8,128)(2,1)S(1)}, bf16[80,128]{1,0:T(8,128)(2,1)S(1)}, u32[]{:S(2)}, u32[]{:S(2)}) %collective-permute-start.12) | collective-permute-done | bytes 20512 | tf_op jit(solution)/shard_map/ppermute | solution.py:779
  51.7 0.5 collective-permute-start.15
  52.2 0.0 collective-permute-start.17
  52.2 0.0 collective-permute-done.14.refs_5_
  52.2 0.7 %collective-permute-done.16.refs_7_ = bf16[80,128]{1,0:T(8,128)(2,1)S(1)} collective-permute-done((bf16[80,128]{1,0:T(8,128)(2,1)S(1)}, bf16[80,128]{1,0:T(8,128)(2,1)S(1)}, u32[]{:S(2)}, u32[]{:S(2)}) %collective-permute-start.16) | collective-permute-done | bytes 20512 | tf_op jit(solution)/shard_map/ppermute | solution.py:492
  52.8 0.2 collective-permute-done.15.refs_6_
  53.0 0.3 collective-permute-done.17.refs_8_
  53.4 3.6 %shard_map.130 = (f32[1,32,60]{2,1,0:T(8,128)}, f32[4,240,128]{2,1,0:T(8,128)}, f32[4,240,128]{2,1,0:T(8,128)}, f32[4,240,128]{2,1,0:T(8,128)}) custom-call(s32[3,128]{1,0:T(4,128)S(1)} %broadcast_in_dim.15.ids_ref.refs_0_, bf16[80,128]{1,0:T(8,128)(2,1)S(1)} %shard_map.128.plane_ref.refs_1_, bf16[80,128]{1,0:T(8,128)(2,1)S(1)} %collective-permute-done.11.refs_2_, ...), custom_call_target="tpu_custom_call" | custom-call | tf_op jit(solution)/shard_map/pallas_call | solution.py:73
  (11 shorter events, 0.1 us)
Async XLA Ops:
  2.3 14.0 %collective-permute-start = (s16[736,128]{1,0:T(8,128)(2,1)S(1)}, s16[736,128]{1,0:T(8,128)(2,1)S(1)}, u32[]{:S(2)}, u32[]{:S(2)}) collective-permute-start(s16[736,128]{1,0:T(8,128)(2,1)S(1)} %get-tuple-element.35), channel_id=1, source_target_pairs={{0,4},{4,8},{8,12},{12,0},{1,5},{5,9},{9,13},{13,1},{2,6},{6,10},{... | collective-permute-start | bytes 565256 | tf_op jit(solution)/shard_map/ppermute | solution.py:504
  5.3 10.9 %collective-permute-start.1 = (s16[736,128]{1,0:T(8,128)(2,1)S(1)}, s16[736,128]{1,0:T(8,128)(2,1)S(1)}, u32[]{:S(2)}, u32[]{:S(2)}) collective-permute-start(s16[736,128]{1,0:T(8,128)(2,1)S(1)} %get-tuple-element.36), channel_id=1, source_target_pairs={{0,12},{4,0},{8,4},{12,8},{1,13},{5,1},{9,5},{13,9},{2,14},{6,2},{... | collective-permute-start | bytes 565256 | tf_op jit(solution)/shard_map/ppermute | solution.py:504
  7.4 8.8 %collective-permute-start.2 = (f32[8,128]{1,0:T(8,128)S(1)}, f32[8,128]{1,0:T(8,128)S(1)}, u32[]{:S(2)}, u32[]{:S(2)}) collective-permute-start(f32[8,128]{1,0:T(8,128)S(1)} %get-tuple-element.37.refs_4_), channel_id=1, source_target_pairs={{0,8},{4,12},{8,0},{12,4},{1,9},{5,13},{9,1},{13,5},{2,10},{6,14},... | collective-permute-start | bytes 12296 | tf_op jit(solution)/shard_map/ppermute | solution.py:522
  16.3 3.9 %collective-permute-start.3 = (f32[2,24,128]{2,1,0:T(8,128)S(1)}, f32[2,24,128]{2,1,0:T(8,128)S(1)}, u32[]{:S(2)}, u32[]{:S(2)}) collective-permute-start(f32[2,24,128]{2,1,0:T(8,128)S(1)} %shard_map.121.refs_5_.yp_ref), channel_id=1, source_target_pairs={{0,2},{2,0},{1,3},{3,1},{4,6},{6,4},{5,7},{7,5},{8,10},{10,8},{9,1... | collective-permute-start | bytes 73736 | tf_op jit(solution)/shard_map/ppermute | solution.py:486
  20.6 1.6 %collective-permute-start.4 = (f32[2,272,128]{2,1,0:T(8,128)S(1)}, f32[2,272,128]{2,1,0:T(8,128)S(1)}, u32[]{:S(2)}, u32[]{:S(2)}) collective-permute-start(f32[2,272,128]{2,1,0:T(8,128)S(1)} %shard_map.122), channel_id=1, source_target_pairs={{0,1},{1,0},{2,3},{3,2},{4,5},{5,4},{6,7},{7,6},{8,9},{9,8},{10,11... | collective-permute-start | bytes 835592 | tf_op jit(solution)/shard_map/ppermute | solution.py:492
  24.4 8.7 %collective-permute-start.5 = (s16[496,128]{1,0:T(8,128)(2,1)S(1)}, s16[496,128]{1,0:T(8,128)(2,1)S(1)}, u32[]{:S(2)}, u32[]{:S(2)}) collective-permute-start(s16[496,128]{1,0:T(8,128)(2,1)S(1)} %get-tuple-element.41), channel_id=1, source_target_pairs={{0,4},{4,8},{8,12},{12,0},{1,5},{5,9},{9,13},{13,1},{2,6},{6,10},{... | collective-permute-start | bytes 380936 | tf_op jit(solution)/shard_map/ppermute | solution.py:504
  25.1 8.1 %collective-permute-start.6 = (s16[496,128]{1,0:T(8,128)(2,1)S(1)}, s16[496,128]{1,0:T(8,128)(2,1)S(1)}, u32[]{:S(2)}, u32[]{:S(2)}) collective-permute-start(s16[496,128]{1,0:T(8,128)(2,1)S(1)} %get-tuple-element.42), channel_id=1, source_target_pairs={{0,12},{4,0},{8,4},{12,8},{1,13},{5,1},{9,5},{13,9},{2,14},{6,2},{... | collective-permute-start | bytes 380936 | tf_op jit(solution)/shard_map/ppermute | solution.py:504
  28.3 4.9 %collective-permute-start.7 = (f32[8,128]{1,0:T(8,128)S(1)}, f32[8,128]{1,0:T(8,128)S(1)}, u32[]{:S(2)}, u32[]{:S(2)}) collective-permute-start(f32[8,128]{1,0:T(8,128)S(1)} %get-tuple-element.43.refs_3_), channel_id=1, source_target_pairs={{0,8},{4,12},{8,0},{12,4},{1,9},{5,13},{9,1},{13,5},{2,10},{6,14},... | collective-permute-start | bytes 12296 | tf_op jit(solution)/shard_map/ppermute | solution.py:522
  33.2 3.9 %collective-permute-start.8 = (f32[2,24,128]{2,1,0:T(8,128)S(1)}, f32[2,24,128]{2,1,0:T(8,128)S(1)}, u32[]{:S(2)}, u32[]{:S(2)}) collective-permute-start(f32[2,24,128]{2,1,0:T(8,128)S(1)} %shard_map.124.refs_4_.yp_ref), channel_id=1, source_target_pairs={{0,2},{2,0},{1,3},{3,1},{4,6},{6,4},{5,7},{7,5},{8,10},{10,8},{9,1... | collective-permute-start | bytes 73736 | tf_op jit(solution)/shard_map/ppermute | solution.py:486
  37.3 1.6 %collective-permute-start.9 = (f32[2,272,128]{2,1,0:T(8,128)S(1)}, f32[2,272,128]{2,1,0:T(8,128)S(1)}, u32[]{:S(2)}, u32[]{:S(2)}) collective-permute-start(f32[2,272,128]{2,1,0:T(8,128)S(1)} %shard_map.125), channel_id=1, source_target_pairs={{0,1},{1,0},{2,3},{3,2},{4,5},{5,4},{6,7},{7,6},{8,9},{9,8},{10,11... | collective-permute-start | bytes 835592 | tf_op jit(solution)/shard_map/ppermute | solution.py:492
  38.9 11.0 %copy-start = (f32[16]{0:T(128)S(1)}, f32[16]{0:T(128)}, u32[]{:S(2)}) copy-start(f32[16]{0:T(128)} %param.13) | copy-start | bytes 196
  38.9 11.0 %copy-start.1 = (f32[16]{0:T(128)S(1)}, f32[16]{0:T(128)}, u32[]{:S(2)}) copy-start(f32[16]{0:T(128)} %param.15) | copy-start | bytes 196
  39.5 4.5 %collective-permute-start.10 = (bf16[2,16,128]{2,1,0:T(8,128)(2,1)S(1)}, bf16[2,16,128]{2,1,0:T(8,128)(2,1)S(1)}, u32[]{:S(2)}, u32[]{:S(2)}) collective-permute-start(bf16[2,16,128]{2,1,0:T(8,128)(2,1)S(1)} %shard_map.127), channel_id=1, source_target_pairs={{0,2},{2,0},{1,3},{3,1},{4,6},{6,4},{5,7},{7,5},{8,10},{10,8},{9,1... | collective-permute-start | bytes 24584 | tf_op jit(solution)/shard_map/ppermute | solution.py:486
  44.1 6.6 %collective-permute-start.13 = (bf16[80,128]{1,0:T(8,128)(2,1)S(1)}, bf16[80,128]{1,0:T(8,128)(2,1)S(1)}, u32[]{:S(2)}, u32[]{:S(2)}) collective-permute-start(bf16[80,128]{1,0:T(8,128)(2,1)S(1)} %shard_map.128.plane_ref.refs_1_), channel_id=1, source_target_pairs={{0,8},{4,12},{8,0},{12,4},{1,9},{5,13},{9,1},{13,5},{2,10},{6,14},... | collective-permute-start | bytes 61448 | tf_op jit(solution)/shard_map/ppermute | solution.py:779
  46.1 5.6 %collective-permute-start.12 = (bf16[80,128]{1,0:T(8,128)(2,1)S(1)}, bf16[80,128]{1,0:T(8,128)(2,1)S(1)}, u32[]{:S(2)}, u32[]{:S(2)}) collective-permute-start(bf16[80,128]{1,0:T(8,128)(2,1)S(1)} %shard_map.128.plane_ref.refs_1_), channel_id=1, source_target_pairs={{0,4},{4,8},{8,12},{12,0},{1,5},{5,9},{9,13},{13,1},{2,6},{6,10},{... | collective-permute-start | bytes 61448 | tf_op jit(solution)/shard_map/ppermute | solution.py:779
  46.9 4.8 %collective-permute-start.11 = (bf16[80,128]{1,0:T(8,128)(2,1)S(1)}, bf16[80,128]{1,0:T(8,128)(2,1)S(1)}, u32[]{:S(2)}, u32[]{:S(2)}) collective-permute-start(bf16[80,128]{1,0:T(8,128)(2,1)S(1)} %shard_map.128.plane_ref.refs_1_), channel_id=1, source_target_pairs={{0,12},{4,0},{8,4},{12,8},{1,13},{5,1},{9,5},{13,9},{2,14},{6,2},{... | collective-permute-start | bytes 61448 | tf_op jit(solution)/shard_map/ppermute | solution.py:779
  49.9 2.3 %collective-permute-start.14 = (bf16[80,128]{1,0:T(8,128)(2,1)S(1)}, bf16[80,128]{1,0:T(8,128)(2,1)S(1)}, u32[]{:S(2)}, u32[]{:S(2)}) collective-permute-start(bf16[80,128]{1,0:T(8,128)(2,1)S(1)} %shard_map.128.plane_ref.refs_1_), channel_id=1, source_target_pairs={{0,1},{1,0},{2,3},{3,2},{4,5},{5,4},{6,7},{7,6},{8,9},{9,8},{10,11... | collective-permute-start | bytes 61448 | tf_op jit(solution)/shard_map/ppermute | solution.py:492
  51.7 1.2 %collective-permute-start.16 = (bf16[80,128]{1,0:T(8,128)(2,1)S(1)}, bf16[80,128]{1,0:T(8,128)(2,1)S(1)}, u32[]{:S(2)}, u32[]{:S(2)}) collective-permute-start(bf16[80,128]{1,0:T(8,128)(2,1)S(1)} %collective-permute-done.12.refs_3_), channel_id=1, source_target_pairs={{0,1},{1,0},{2,3},{3,2},{4,5},{5,4},{6,7},{7,6},{8,9},{9,8},{10,11... | collective-permute-start | bytes 61448 | tf_op jit(solution)/shard_map/ppermute | solution.py:492
  51.7 1.4 %collective-permute-start.15 = (bf16[80,128]{1,0:T(8,128)(2,1)S(1)}, bf16[80,128]{1,0:T(8,128)(2,1)S(1)}, u32[]{:S(2)}, u32[]{:S(2)}) collective-permute-start(bf16[80,128]{1,0:T(8,128)(2,1)S(1)} %collective-permute-done.11.refs_2_), channel_id=1, source_target_pairs={{0,1},{1,0},{2,3},{3,2},{4,5},{5,4},{6,7},{7,6},{8,9},{9,8},{10,11... | collective-permute-start | bytes 61448 | tf_op jit(solution)/shard_map/ppermute | solution.py:492
  52.2 1.2 %collective-permute-start.17 = (bf16[80,128]{1,0:T(8,128)(2,1)S(1)}, bf16[80,128]{1,0:T(8,128)(2,1)S(1)}, u32[]{:S(2)}, u32[]{:S(2)}) collective-permute-start(bf16[80,128]{1,0:T(8,128)(2,1)S(1)} %collective-permute-done.13.refs_4_), channel_id=1, source_target_pairs={{0,1},{1,0},{2,3},{3,2},{4,5},{5,4},{6,7},{7,6},{8,9},{9,8},{10,11... | collective-permute-start | bytes 61448 | tf_op jit(solution)/shard_map/ppermute | solution.py:492
